TPU v7x, 32 devices: a whole 2x2x4 slice. The times are simulated.
32 devices in a mesh: dp: 8 (over z, x), tensor: 4 (over y, core).
Axes of the slice: x: 2, y: 2, z: 4, core: 2. Of those that a mesh axis runs over, the one named last changes fastest.
Arguments:
- hidden: bfloat16 [8192, 2048], P(('dp', 'tensor')), may hold values from -6 to 6
- teacher: bfloat16 [8192, 2048], P(('dp', 'tensor')), may hold values from -6 to 6
- valid_mask: int32 [8192], P(('dp', 'tensor')), may hold values from 0 to 1, as said below
- prefix_len: int32 [8], P('dp'), may hold values from 128 to 256
- ln1_gain: bfloat16 [2048], replicated, may hold values from 0.5 to 1.5
- ln1_bias: bfloat16 [2048], replicated, may hold values from -1.75 to 1.75
- ln2_gain: bfloat16 [2048], replicated, may hold values from 0.5 to 1.5
- ln2_bias: bfloat16 [2048], replicated, may hold values from -1.75 to 1.75
- qkv_weight: bfloat16 [2048, 6144], P(None, 'tensor'), may hold values from -0.1875 to 0.1875
- qkv_bias: bfloat16 [6144], P('tensor'), may hold values from -1.75 to 1.75
- out_weight: bfloat16 [2048, 2048], P('tensor'), may hold values from -0.5 to 0.5
- out_bias: bfloat16 [2048], replicated, may hold values from -1.75 to 1.75
- fc1_weight: bfloat16 [2048, 8192], P(None, 'tensor'), may hold values from -0.125 to 0.125
- fc1_bias: bfloat16 [8192], P('tensor'), may hold values from -1.75 to 1.75
- fc2_weight: bfloat16 [8192, 2048], P('tensor'), may hold values from -0.0625 to 0.0625
- fc2_bias: bfloat16 [2048], replicated, may hold values from -1.75 to 1.75
Outputs:
- output: bfloat16 [8192, 2048], P(('dp', 'tensor'))
- loss: float32 [], replicated
- input_grad: float32 [8192, 2048], P(('dp', 'tensor'))
- ln1_gain_grad: float32 [2048], replicated
- ln1_bias_grad: float32 [2048], replicated
- ln2_gain_grad: float32 [2048], replicated
- ln2_bias_grad: float32 [2048], replicated
- qkv_weight_grad: float32 [2048, 6144], P(None, 'tensor')
- qkv_bias_grad: float32 [6144], P('tensor')
- out_weight_grad: float32 [2048, 2048], P('tensor')
- out_bias_grad: float32 [2048], replicated
- fc1_weight_grad: float32 [2048, 8192], P(None, 'tensor')
- fc1_bias_grad: float32 [8192], P('tensor')
- fc2_weight_grad: float32 [8192, 2048], P('tensor')
- fc2_bias_grad: float32 [2048], replicated
Inputs may be any that keep to these rules, and one draw needn't show every extreme that they name: `valid_mask`: 1 marks a token that counts in the loss, 0 one that does not; the first token of all counts.
All inputs are finite; a program needn't handle non-finite values.
Results may differ from a plain program's by a relative error of at most 0.006.
The roundings to bfloat16 on the way count: a program that leaves them out, or rounds other values in their place, can miss the bound.
Values may be sent and summed in bfloat16 or wider, within the bound.
No kernel may reach another device: no remote copies, remote signals or barrier semaphores. Data moves between devices by JAX's collectives and lax.ppermute only.
A program may use at most 256 MiB of HBM per device.

v0:
```python
import jax
import jax.numpy as jnp
from jax import lax
from jax.sharding import PartitionSpec as P

D = 2048
HD = 256
ROT = 64
LEN = 1024
SEQ_DEV = 1


EPSILON = 1e-05


def layer_norm(features, gain, shift):
    average = jnp.mean(features, axis=-1, keepdims=True)
    centered = features - average
    spread = jnp.mean(centered * centered, axis=-1, keepdims=True)
    return centered * lax.rsqrt(spread + EPSILON) * gain + shift


def norm_pair(features, gain_one, shift_one, gain_two, shift_two):
    return (layer_norm(features, gain_one, shift_one), layer_norm(features, gain_two, shift_two))


def rotary_tables(length, rot_dims):
    half_dims = rot_dims // 2
    frequency = 10000.0 ** (-2.0 * jnp.arange(half_dims, dtype=jnp.float32) / rot_dims)
    angles = jnp.arange(length, dtype=jnp.float32)[:, None] * frequency[None, :]
    return (jnp.cos(angles)[:, None, :], jnp.sin(angles)[:, None, :])


def rotate_block(block, cosine_table, sine_table):
    half_dims = cosine_table.shape[-1]
    first_half = block[..., :half_dims]
    second_half = block[..., half_dims : 2 * half_dims]
    return jnp.concatenate(
        [
            first_half * cosine_table - second_half * sine_table,
            second_half * cosine_table + first_half * sine_table,
            block[..., 2 * half_dims :],
        ],
        axis=-1,
    )


def unrotate_block(grad_block, cosine_table, sine_table):
    half_dims = cosine_table.shape[-1]
    first_half = grad_block[..., :half_dims]
    second_half = grad_block[..., half_dims : 2 * half_dims]
    return jnp.concatenate(
        [
            first_half * cosine_table + second_half * sine_table,
            second_half * cosine_table - first_half * sine_table,
            grad_block[..., 2 * half_dims :],
        ],
        axis=-1,
    )


def contract(left_side, right_side, left_dim, right_dim):
    return lax.dot_general(
        left_side,
        right_side,
        (((left_dim,), (right_dim,)), ((), ())),
        preferred_element_type=jnp.float32,
    )


def exact_gelu(pre_act):
    return jax.nn.gelu(pre_act, approximate=False)


def on_device(
    hidden,
    teacher,
    valid_mask,
    prefix_len,
    ln1_gain,
    ln1_bias,
    ln2_gain,
    ln2_bias,
    qkv_weight,
    qkv_bias,
    out_weight,
    out_bias,
    fc1_weight,
    fc1_bias,
    fc2_weight,
    fc2_bias,
):
    own_rows = hidden.shape[0]
    total_tokens = lax.axis_size("dp") * lax.axis_size("tensor") * own_rows
    heads_here = qkv_weight.shape[1] // (3 * HD)
    block_rows = SEQ_DEV * LEN
    hidden_own = hidden.astype(jnp.float32)
    gain_attn = ln1_gain.astype(jnp.float32)
    shift_attn = ln1_bias.astype(jnp.float32)
    gain_mlp = ln2_gain.astype(jnp.float32)
    shift_mlp = ln2_bias.astype(jnp.float32)
    mask_f = valid_mask.astype(jnp.float32)
    mask_total = jnp.sum(mask_f)
    hidden_all = lax.all_gather(hidden, "tensor", axis=0, tiled=True).astype(jnp.float32)
    norm_attn = layer_norm(hidden_all, gain_attn, shift_attn).astype(jnp.bfloat16)
    norm_mlp = layer_norm(hidden_all, gain_mlp, shift_mlp).astype(jnp.bfloat16)
    qkv_all = jnp.dot(norm_attn, qkv_weight, preferred_element_type=jnp.float32) + qkv_bias.astype(
        jnp.float32
    )
    cosine_table, sine_table = rotary_tables(LEN, ROT)
    scale_factor = HD ** (-0.5)
    places = jnp.arange(LEN, dtype=jnp.int32)

    def visible(prefix_end):
        return (places[None, :] <= places[:, None]) | (places[None, :] < prefix_end)

    def attend_forward(packed):
        qkv_rows, prefix_end = packed
        split_qkv = qkv_rows.reshape(LEN, heads_here, 3, HD)
        queries = rotate_block(split_qkv[:, :, 0], cosine_table, sine_table).astype(jnp.bfloat16)
        keys_rot = rotate_block(split_qkv[:, :, 1], cosine_table, sine_table).astype(jnp.bfloat16)
        values = split_qkv[:, :, 2].astype(jnp.bfloat16)
        scores = (
            jnp.einsum("qhd,khd->hqk", queries, keys_rot, preferred_element_type=jnp.float32)
            * scale_factor
        )
        scores = jnp.where(visible(prefix_end)[None], scores, -jnp.inf)
        top_score = jnp.max(scores, axis=-1, keepdims=True)
        log_total = top_score + jnp.log(
            jnp.sum(jnp.exp(scores - top_score), axis=-1, keepdims=True)
        )
        attention = jnp.exp(scores - log_total).astype(jnp.bfloat16)
        context_seq = jnp.einsum(
            "hqk,khd->qhd", attention, values, preferred_element_type=jnp.float32
        ).astype(jnp.bfloat16)
        return (context_seq.reshape(LEN, heads_here * HD), log_total, queries, keys_rot, values)

    context, log_totals, queries_all, keys_all, values_all = lax.map(
        attend_forward, (qkv_all.reshape(SEQ_DEV, LEN, heads_here * 3 * HD), prefix_len)
    )
    context = context.reshape(block_rows, heads_here * HD)
    hidden_pre = jnp.dot(
        norm_mlp, fc1_weight, preferred_element_type=jnp.float32
    ) + fc1_bias.astype(jnp.float32)
    active = exact_gelu(hidden_pre).astype(jnp.bfloat16)
    branch = lax.psum_scatter(
        jnp.dot(context, out_weight, preferred_element_type=jnp.float32)
        + jnp.dot(active, fc2_weight, preferred_element_type=jnp.float32),
        "tensor",
        scatter_dimension=0,
        tiled=True,
    )
    output_f = hidden_own + branch + out_bias.astype(jnp.float32) + fc2_bias.astype(jnp.float32)
    mismatch = output_f - teacher.astype(jnp.float32)
    error_part = jnp.sum(mask_f[:, None] * mismatch * mismatch)
    count_all, error_all = lax.psum((mask_total, error_part), ("dp", "tensor"))
    grad_out = mask_f[:, None] * mismatch * (2.0 * total_tokens / count_all)
    bias_part = jnp.sum(grad_out, axis=0)
    grad_rows = lax.all_gather(grad_out.astype(jnp.bfloat16), "tensor", axis=0, tiled=True)
    out_weight_part = contract(context, grad_rows, 0, 0)
    fc2_weight_part = contract(active, grad_rows, 0, 0)
    grad_context = contract(grad_rows, out_weight, 1, 1).astype(jnp.bfloat16)
    grad_active = contract(grad_rows, fc2_weight, 1, 1)
    gelu_back = jax.vjp(exact_gelu, hidden_pre)[1]
    grad_inner = gelu_back(grad_active)[0].astype(jnp.bfloat16)
    fc1_weight_part = contract(norm_mlp, grad_inner, 0, 0)
    fc1_bias_part = jnp.sum(grad_inner, axis=0, dtype=jnp.float32)
    grad_norm_mlp = contract(grad_inner, fc1_weight, 1, 1)

    def attend_backward(packed):
        queries, keys_rot, values, log_total, grad_ctx, prefix_end = packed
        scores = (
            jnp.einsum("qhd,khd->hqk", queries, keys_rot, preferred_element_type=jnp.float32)
            * scale_factor
        )
        scores = jnp.where(visible(prefix_end)[None], scores, -jnp.inf)
        attention = jnp.exp(scores - log_total)
        grad_attention = jnp.einsum(
            "qhd,khd->hqk", grad_ctx, values, preferred_element_type=jnp.float32
        )
        row_dots = jnp.sum(attention * grad_attention, axis=-1, keepdims=True)
        grad_scores = (attention * (grad_attention - row_dots)).astype(jnp.bfloat16)
        grad_queries = (
            jnp.einsum("hqk,khd->qhd", grad_scores, keys_rot, preferred_element_type=jnp.float32)
            * scale_factor
        )
        grad_keys = (
            jnp.einsum("hqk,qhd->khd", grad_scores, queries, preferred_element_type=jnp.float32)
            * scale_factor
        )
        grad_values = jnp.einsum(
            "hqk,qhd->khd",
            attention.astype(jnp.bfloat16),
            grad_ctx,
            preferred_element_type=jnp.float32,
        )
        grad_split = jnp.stack(
            [
                unrotate_block(grad_queries, cosine_table, sine_table),
                unrotate_block(grad_keys, cosine_table, sine_table),
                grad_values,
            ],
            axis=2,
        )
        return grad_split.reshape(LEN, heads_here * 3 * HD).astype(jnp.bfloat16)

    grad_qkv = lax.map(
        attend_backward,
        (
            queries_all,
            keys_all,
            values_all,
            log_totals,
            grad_context.reshape(SEQ_DEV, LEN, heads_here, HD),
            prefix_len,
        ),
    )
    grad_qkv = grad_qkv.reshape(block_rows, heads_here * 3 * HD)
    qkv_weight_part = contract(norm_attn, grad_qkv, 0, 0)
    qkv_bias_part = jnp.sum(grad_qkv, axis=0, dtype=jnp.float32)
    grad_norm_attn = contract(grad_qkv, qkv_weight, 1, 1)
    (
        qkv_weight_grad,
        qkv_bias_grad,
        out_weight_grad,
        fc1_weight_grad,
        fc1_bias_grad,
        fc2_weight_grad,
    ) = lax.psum(
        (
            qkv_weight_part,
            qkv_bias_part,
            out_weight_part,
            fc1_weight_part,
            fc1_bias_part,
            fc2_weight_part,
        ),
        "dp",
    )
    norm_back = jax.vjp(norm_pair, hidden_all, gain_attn, shift_attn, gain_mlp, shift_mlp)[1]
    grad_hidden, gain_attn_part, shift_attn_part, gain_mlp_part, shift_mlp_part = norm_back(
        (grad_norm_attn, grad_norm_mlp)
    )
    input_grad = grad_out + lax.psum_scatter(grad_hidden, "tensor", scatter_dimension=0, tiled=True)
    ln1_gain_grad, ln1_bias_grad, ln2_gain_grad, ln2_bias_grad, out_bias_grad = lax.psum(
        (gain_attn_part, shift_attn_part, gain_mlp_part, shift_mlp_part, bias_part),
        ("dp", "tensor"),
    )
    loss_value = error_all / (count_all * D)
    return (
        output_f.astype(jnp.bfloat16),
        loss_value,
        input_grad,
        ln1_gain_grad,
        ln1_bias_grad,
        ln2_gain_grad,
        ln2_bias_grad,
        qkv_weight_grad,
        qkv_bias_grad,
        out_weight_grad,
        out_bias_grad,
        fc1_weight_grad,
        fc1_bias_grad,
        fc2_weight_grad,
        out_bias_grad,
    )


def solution(mesh):
    in_specs = (
        P(("dp", "tensor"), None),
        P(("dp", "tensor"), None),
        P(("dp", "tensor")),
        P("dp"),
        P(),
        P(),
        P(),
        P(),
        P(None, "tensor"),
        P("tensor"),
        P("tensor", None),
        P(),
        P(None, "tensor"),
        P("tensor"),
        P("tensor", None),
        P(),
    )
    out_specs = (
        P(("dp", "tensor"), None),
        P(),
        P(("dp", "tensor"), None),
        P(),
        P(),
        P(),
        P(),
        P(None, "tensor"),
        P("tensor"),
        P("tensor", None),
        P(),
        P(None, "tensor"),
        P("tensor"),
        P("tensor", None),
        P(),
    )
    return jax.shard_map(
        on_device, mesh=mesh, in_specs=in_specs, out_specs=out_specs, check_vma=False
    )
```

profile of v0, /device:TPU:0, one launch (start us, length us, event | category | flops | bytes accessed | tf_op | source)
XLA Modules:
  0.0 1973.6 jit_solution(10650041223242711046)
XLA Ops:
  7.2 0.7 all-gather.3.cloned.1.call-update
  8.0 0.7 convert_element_type.111
  8.7 0.7 convert_element_type.109
  9.4 0.7 convert_element_type.108
  10.7 0.7 convert_element_type.103
  11.4 0.7 convert_element_type.101
  12.1 0.7 convert_element_type.100
  12.8 2.8 fusion.35
  16.0 30.8 %all-gather.3.cloned.1.call-done = bf16[1024,2048]{1,0:T(8,128)(2,1)} async-done(((bf16[256,2048]{1,0:T(8,128)(2,1)}), bf16[1024,2048]{1,0:T(8,128)(2,1)}) %all-gather.3.cloned.1.call-update) | async-done | bytes 4194320 | tf_op jit(solution)/shard_map/all_gather | solution.py:104
  46.8 3.0 convert_reduce_fusion
  49.8 3.4 fusion.16
  53.2 0.6 copy-done.28
  53.8 11.5 convolution_add_fusion
  65.3 6.6 copy.61
  72.0 4.8 fusion.55
  76.8 2.9 copy.90
  79.7 3.0 slice.111
  82.6 2.9 copy.89
  85.5 2.1 slice.112
  87.6 3.6 subtract_convert_fusion.1
  91.3 3.0 fusion.25
  94.3 13.4 exponential_reduce_fusion
  107.7 4.5 convolution_convert_fusion
  112.3 34.2 %multiply_convert_fusion.1 = (bf16[1024,2048]{1,0:T(8,128)(2,1)S(1)}, f32[1024,2048]{1,0:T(8,128)}, f32[1024,2048]{1,0:T(8,128)}) fusion(f32[2048]{0:T(1024)S(1)} %convert_element_type.111, bf16[2048,2048]{1,0:T(8,128)(2,1)} %param.28, bf16[1024,2048]{1,0:T(8,128)(2,1)S(1)} %copy-done.4, f32[2048]{0:T(1024)S(1)} %convert_element_type.109, ...), kind=kOutput, calls=%fused_computation.30 | convolution fusion | flops 8740929536 | bytes 33587200 | tf_op jit(solution)/shard_map/dot_general | solution.py:142
  146.5 8.8 fusion.56
  155.4 6.1 convolution_add_fusion.1
  161.6 0.6 copy-done.39
  162.2 0.6 convert_reduce_fusion.3
  162.8 39.8 %psum.92 = f32[]{:T(128)} all-reduce(f32[]{:T(128)} %convert_reduce_fusion.3), channel_id=1, replica_groups=mesh['dp'=8,'tensor'=4] {'dp','tensor'}, use_global_device_ids=true, to_apply=%region_8.9 | all-reduce | flops 1 | bytes 8 | tf_op jit(solution)/shard_map/psum | solution.py:156
  203.3 30.8 %reduce-scatter.3.cloned.1.call-done = f32[256,2048]{1,0:T(8,128)} async-done(((f32[1024,2048]{1,0:T(8,128)}), f32[256,2048]{1,0:T(8,128)}) %reduce-scatter.3.cloned.1.call-update) | async-done | bytes 2097168 | tf_op jit(solution)/shard_map/reduce_scatter | solution.py:146
  234.1 4.9 fusion.31
  239.2 34.4 %all-gather.5.cloned.1.call-done = bf16[1024,2048]{1,0:T(8,128)(2,1)} async-done(((bf16[256,2048]{1,0:T(8,128)(2,1)}), bf16[1024,2048]{1,0:T(8,128)(2,1)}) %all-gather.5.cloned.1.call-update) | async-done | bytes 4194320 | tf_op jit(solution)/shard_map/all_gather | solution.py:159
  273.7 4.7 convolution_convert_fusion.1
  278.4 5.5 convolution_bitcast_fusion
  283.9 4.3 multiply_reduce_fusion
  288.3 2.6 multiply_convert_fusion
  291.0 2.3 multiply_bitcast_fusion.1
  293.4 1.5 multiply_bitcast_fusion
  294.9 0.4 slice.89
  295.3 0.8 multiply_add_fusion.1
  296.0 0.4 slice.92
  296.4 20.3 %convert_reduce_fusion.1 = (f32[2048]{0:T(1024)S(1)}, bf16[1024,2048]{1,0:T(8,128)(2,1)}) fusion(f32[1024,2048]{1,0:T(8,128)} %get-tuple-element.112, f32[1024,2048]{1,0:T(8,128)} %get-tuple-element.135, f32[2048]{0:T(1024)S(1)} %convert_element_type.111, bf16[1024,2048]{1,0:T(8,128)(2,1)} %all-gather.5.cloned.1.call-done, bf16[2048,2048]{1,0:T(8,128)(2,1)} %param.30), kind=kOutput, calls=%fused_computation.25 | convolution fusion | flops 8625584128 | bytes 33570816 | tf_op jit(solution)/shard_map/dot_general | solution.py:63
  316.7 14.6 fusion.57
  331.2 1.9 maximum_bitcast_fusion
  333.1 2.0 convert_reduce_fusion.2
  335.2 4.7 copy.76
  339.8 15.0 fusion.53
  354.9 8.7 fusion.15
  363.6 9.9 add_add_fusion.2
  373.5 1.1 copy-done.13
  374.7 6.7 fusion.58
  381.4 11.8 fusion.59
  393.2 12.3 fusion.43
  405.5 11.7 fusion.47
  418.1 37.6 %all-reduce.1 = (f32[1536]{0:T(1024)}, f32[2048]{0:T(1024)}) all-reduce(f32[1536]{0:T(1024)S(1)} %reduce_sum.184, f32[2048]{0:T(1024)S(1)} %get-tuple-element.105), channel_id=1, replica_groups=mesh['dp'=8,'tensor'=4] {'dp'}, use_global_device_ids=true, to_apply=%region_25.26 | all-reduce | flops 3584 | bytes 28672 | tf_op jit(solution)/shard_map/psum | solution.py:229
  455.7 4.8 fusion.29
  460.5 44.1 %all-reduce = (f32[]{:T(128)}, f32[2048]{0:T(1024)}, f32[2048]{0:T(1024)}, f32[2048]{0:T(1024)}, f32[2048]{0:T(1024)}, /*index=5*/f32[2048]{0:T(1024)S(1)}) all-reduce(f32[]{:T(128)} %get-tuple-element.92, f32[2048]{0:T(1024)S(1)} %get-tuple-element.90, ...), channel_id=1, replica_groups=mesh['dp'=8,'tensor'=4] {'dp','tensor'}, use_global_device_ids=true, to_apply=%region_6.7 | all-reduce | flops 10241 | bytes 81928 | tf_op jit(solution)/shard_map/psum | solution.py:156
  505.3 1424.6 %all-reduce.5.cloned.1.call-done = (f32[2048,1536]{1,0:T(8,128)}, f32[512,2048]{1,0:T(8,128)}, f32[2048,2048]{1,0:T(8,128)}, f32[2048,2048]{1,0:T(8,128)}) async-done(((f32[2048,1536]{1,0:T(8,128)}, f32[512,2048]{1,0:T(8,128)}, f32[2048,2048]{1,0:T(8,128)}, f32[2048,2048]{1,0:T(8,128)}), (f32[2048,1536]{1,0:T(8,128)}, f32[512,2048]{1,0:T(8,128)}, f32[2048,2048]{1,0:T(8,128)}, ...) | async-done | bytes 50331664 | tf_op jit(solution)/shard_map/psum | solution.py:229
  1929.9 0.6 copy.105
  1930.5 10.8 copy.106
  1941.3 2.1 copy.107
  1943.4 14.0 copy.108
  1957.4 2.0 slice-done.5
  1959.4 6.3 copy.109
  (127 shorter events, 1.1 us)
Async XLA Ops:
  7.2 148.2 %copy-start = (bf16[512,2048]{1,0:T(8,128)(2,1)S(1)}, bf16[512,2048]{1,0:T(8,128)(2,1)}, u32[]{:S(2)}) copy-start(bf16[512,2048]{1,0:T(8,128)(2,1)} %param.26) | copy-start | bytes 6291460
  7.2 39.6 %all-gather.3.cloned.1.call-start = ((), (), s32[]{:S(2)}) async-start(), calls=%async_computation.2 | async-start | bytes 5242880 | tf_op jit(solution)/shard_map/all_gather | solution.py:104
  7.9 226.2 %reduce-scatter.3.cloned.1.call-start = ((), (), s32[]{:S(2)}) async-start(), calls=%async_computation.3 | async-start | bytes 10485760 | tf_op jit(solution)/shard_map/reduce_scatter | solution.py:146
  9.4 102.9 %copy-start.34 = (f32[2048]{0:T(1024)}, f32[2048]{0:T(1024)S(1)}, u32[]{:S(2)}) copy-start(f32[2048]{0:T(1024)S(1)} %convert_element_type.109) | copy-start | bytes 24580
  12.1 53.2 %copy-start.32 = (f32[2048]{0:T(1024)}, f32[2048]{0:T(1024)S(1)}, u32[]{:S(2)}) copy-start(f32[2048]{0:T(1024)S(1)} %convert_element_type.101) | copy-start | bytes 24580
  12.8 52.5 %copy-start.26 = (f32[2048]{0:T(1024)}, f32[2048]{0:T(1024)S(1)}, u32[]{:S(2)}) copy-start(f32[2048]{0:T(1024)S(1)} %convert_element_type.100) | copy-start | bytes 24580
  46.8 7.0 copy-start.3
  53.2 0.6 copy-start.28
  85.5 5.7 copy-start.14
  87.6 6.7 copy-start.16
  91.2 3.1 copy-start.18
  91.2 3.1 copy-start.20
  91.2 3.1 copy-start.22
  91.2 3.1 copy-start.24
  94.3 18.0 copy-start.2
  107.7 4.6 copy-start.4
  107.7 38.8 %slice-start.6 = ((s8[8388608]{0:T(1024)(128)(4,1)}), s8[4194304]{0:T(1024)(128)(4,1)S(1)}, s32[]{:S(2)}) async-start(s8[8388608]{0:T(1024)(128)(4,1)} %bitcast.69), calls=%async_computation.13 | async-start | bytes 8388608
  112.3 43.1 %copy-start.12 = (bf16[2,256,1024]{2,1,0:T(8,128)(2,1)}, bf16[2,256,1024]{2,1,0:T(8,128)(2,1)S(1)}, u32[]{:S(2)}) copy-start(bf16[2,256,1024]{2,1,0:T(8,128)(2,1)S(1)} %convolution_convert_fusion) | copy-start | bytes 3145732
  112.3 34.2 %slice-start.7 = ((s8[8388608]{0:T(1024)(128)(4,1)}), s8[4194304]{0:T(1024)(128)(4,1)S(1)}, s32[]{:S(2)}) async-start(s8[8388608]{0:T(1024)(128)(4,1)} %bitcast.69), calls=%async_computation.14 | async-start | bytes 8388608
  146.5 8.9 copy-start.41
  161.5 0.7 copy-start.39
  161.5 41.1 %copy-start.37 = (bf16[2048]{0:T(1024)(128)(2,1)S(1)}, bf16[2048]{0:T(1024)(128)(2,1)}, u32[]{:S(2)}) copy-start(bf16[2048]{0:T(1024)(128)(2,1)} %param.31) | copy-start | bytes 12292
  161.5 41.1 %copy-start.38 = (bf16[2048]{0:T(1024)(128)(2,1)S(1)}, bf16[2048]{0:T(1024)(128)(2,1)}, u32[]{:S(2)}) copy-start(bf16[2048]{0:T(1024)(128)(2,1)} %param.27) | copy-start | bytes 12292
  161.5 112.2 %all-gather.5.cloned.1.call-start = ((), (), s32[]{:S(2)}) async-start(), calls=%async_computation.4 | async-start | bytes 5242880 | tf_op jit(solution)/shard_map/all_gather | solution.py:159
  202.6 75.8 %copy-start.30 = (f32[256]{0:T(256)}, f32[256]{0:T(256)S(1)}, u32[]{:S(2)}) copy-start(f32[256]{0:T(256)S(1)} %convert_element_type.116) | copy-start | bytes 3076
  239.0 216.7 %reduce-scatter.5.cloned.1.call-start = ((), (), s32[]{:S(2)}) async-start(), calls=%async_computation.5 | async-start | bytes 10485760 | tf_op jit(solution)/shard_map/reduce_scatter | solution.py:244
  273.7 10.3 slice-start
  278.4 5.5 slice-start.1
  288.2 2.7 copy-start.15
  288.3 2.7 copy-start.23
  288.3 2.7 copy-start.25
  290.9 2.4 copy-start.17
  291.0 2.4 copy-start.19
  291.0 2.4 copy-start.21
  291.0 4.3 copy-start.8
  291.0 4.3 copy-start.9
  331.2 8.6 copy-start.27
  339.8 15.0 copy-start.29
  339.8 15.0 copy-start.5
  373.4 1.2 copy-start.13
  373.5 1556.4 %all-reduce.5.cloned.1.call-start = ((), (), s32[]{:S(2)}) async-start(), calls=%async_computation.6 | async-start | bytes 100663296 | tf_op jit(solution)/shard_map/psum | solution.py:229
  374.7 6.7 copy-start.40
  374.7 6.7 copy-start.42
  381.3 11.8 copy-start.6
  381.3 11.8 copy-start.35
  381.3 11.8 copy-start.43
  393.2 12.3 copy-start.11
  393.2 12.3 copy-start.33
  417.2 38.5 %copy-start.7 = (f32[256,2048]{1,0:T(8,128)S(1)}, f32[256,2048]{1,0:T(8,128)}, u32[]{:S(2)}) copy-start(f32[256,2048]{1,0:T(8,128)} %get-tuple-element.110) | copy-start | bytes 6291460
  417.2 38.5 %copy-start.31 = (f32[256]{0:T(256)S(1)}, f32[256]{0:T(256)}, u32[]{:S(2)}) copy-start(f32[256]{0:T(256)} %copy-done.30) | copy-start | bytes 3076
  504.6 1436.7 %copy-start.36 = (f32[2048]{0:T(1024)}, f32[2048]{0:T(1024)S(1)}, u32[]{:S(2)}) copy-start(f32[2048]{0:T(1024)S(1)} %get-tuple-element.183) | copy-start | bytes 24580
  1930.5 10.8 copy-start.10
  1941.3 16.2 slice-start.2
  1943.4 14.0 slice-start.3
  1943.4 14.0 slice-start.4
  1943.4 16.0 slice-start.5
  1959.4 6.3 copy-start.1
Sparse Core Ops, SparseCore 0:
  9.6 37.1 all-gather.2
  161.6 72.4 reduce-scatter.2
  239.1 34.4 all-gather.4
  373.6 71.6 reduce-scatter.4
  451.2 1478.6 all-reduce.4
where the time goes:
time: 1980 us; the launch traced here: 1970 us
  waiting for transfers between devices  1520 us (77%)
  matrix products  179 us (9%)
  blocking collectives  122 us (6%)
  other arithmetic  66.9 us (3%)
  local copies, waits for them, and re-layouts  66 us (3%)
    psum x1, waiting for transfers between devices, on_device(): lax.psum((qkv_weight_part, qkv_bias_part, out_weight_part, fc1_weight_par...  1420 us
    dot_general x8, matrix products, contract(): lax.dot_general(left_side, right_side, (((left_dim,), (right_dim,)), ((),...  97 us
    psum x2, blocking collectives, on_device(): count_all, error_all = lax.psum((mask_total, error_part), ('dp', 'tensor'))  84 us
    unnamed x111, local copies, waits for them, and re-layouts  44.1 us
  transfers between devices with their start and end apart: 5, of which 4 were waited for; matrix products, arithmetic and copies ran while one was open for 3% of the time, Pallas kernels for 0%

commit v1 on v0

v1 whole, which is shorter than its diff:
```python
import jax
import jax.numpy as jnp
from jax import lax
from jax.sharding import PartitionSpec as P

D = 2048
HD = 256
ROT = 64
LEN = 1024
EPSILON = 1e-05
BF = jnp.bfloat16
F32 = jnp.float32


def rotary_tables(length, rot_dims):
    half_dims = rot_dims // 2
    frequency = 10000.0 ** (-2.0 * jnp.arange(half_dims, dtype=F32) / rot_dims)
    angles = jnp.arange(length, dtype=F32)[:, None] * frequency[None, :]
    return jnp.cos(angles), jnp.sin(angles)


def rotate_block(block, cosine_table, sine_table):
    half_dims = cosine_table.shape[-1]
    first_half = block[..., :half_dims]
    second_half = block[..., half_dims : 2 * half_dims]
    return jnp.concatenate(
        [
            first_half * cosine_table - second_half * sine_table,
            second_half * cosine_table + first_half * sine_table,
            block[..., 2 * half_dims :],
        ],
        axis=-1,
    )


def contract(left_side, right_side, left_dim, right_dim):
    return lax.dot_general(
        left_side,
        right_side,
        (((left_dim,), (right_dim,)), ((), ())),
        preferred_element_type=F32,
    )


def exact_gelu(pre_act):
    return jax.nn.gelu(pre_act, approximate=False)


def after(value, *earlier):
    return lax.optimization_barrier((value,) + earlier)[0]


def on_device(
    hidden,
    teacher,
    valid_mask,
    prefix_len,
    ln1_gain,
    ln1_bias,
    ln2_gain,
    ln2_bias,
    qkv_weight,
    qkv_bias,
    out_weight,
    out_bias,
    fc1_weight,
    fc1_bias,
    fc2_weight,
    fc2_bias,
):
    rows = hidden.shape[0]
    dp = lax.axis_size("dp")
    tp = lax.axis_size("tensor")
    ways = tp // 2
    line = dp // 2
    total_tokens = dp * tp * rows
    heads = qkv_weight.shape[1] // (3 * HD)
    dp_index = lax.axis_index("dp")
    tp_index = lax.axis_index("tensor")
    core, y = tp_index % 2, tp_index // 2
    side, place = dp_index % 2, dp_index // 2

    def to_core(v):
        return lax.ppermute(v, "tensor", [(t, t ^ 1) for t in range(tp)])

    def from_y(v, step):
        pairs = [(t, ((t // 2 - step) % ways) * 2 + t % 2) for t in range(tp)]
        return lax.ppermute(v, "tensor", pairs)

    def to_y(v, step):
        pairs = [(t, ((t // 2 + step) % ways) * 2 + t % 2) for t in range(tp)]
        return lax.ppermute(v, "tensor", pairs)

    def to_side(v):
        return lax.ppermute(v, "dp", [(d, d ^ 1) for d in range(dp)])

    def along(v, hops):
        return lax.ppermute(v, "dp", [(a * 2 + s, b * 2 + s) for a, b in hops for s in (0, 1)])

    def tensor_sum(v):
        v = v + to_core(v)
        bit = 2
        while bit < tp:
            v = v + lax.ppermute(v, "tensor", [(t, t ^ bit) for t in range(tp)])
            bit *= 2
        return v

    def dp_sum(v):
        bit = 1
        while bit < dp:
            v = v + lax.ppermute(v, "dp", [(d, d ^ bit) for d in range(dp)])
            bit *= 2
        return v

    block_ids = [
        ((y + step) % ways) * 2 + (core if mate == 0 else 1 - core)
        for step in range(ways)
        for mate in (0, 1)
    ]

    def gather_rows(own):
        parts = [own, to_core(own)]
        for step in range(1, ways):
            far = from_y(own, step)
            parts += [far, to_core(far)]
        return parts

    def own_side(v, axis):
        half = v.shape[axis] // 2
        return lax.dynamic_slice_in_dim(v, side * half, half, axis)

    def other_side(v, axis):
        half = v.shape[axis] // 2
        return lax.dynamic_slice_in_dim(v, (1 - side) * half, half, axis)

    gain_attn = ln1_gain.astype(F32)
    shift_attn = ln1_bias.astype(F32)
    gain_mlp = ln2_gain.astype(F32)
    shift_mlp = ln2_bias.astype(F32)
    mask_f = valid_mask.astype(F32)
    count_all = dp_sum(tensor_sum(jnp.full((8, 128), jnp.sum(mask_f), F32)))[0, 0]

    def normalize(features):
        average = jnp.mean(features, axis=-1, keepdims=True)
        centered = features - average
        spread = jnp.mean(centered * centered, axis=-1, keepdims=True)
        inverse = lax.rsqrt(spread + EPSILON)
        return centered * inverse, inverse

    hidden_near = jnp.concatenate(gather_rows(hidden), axis=0)
    hidden_far = jnp.concatenate(gather_rows(to_side(hidden)), axis=0)
    xhat, inverse = normalize(hidden_near.astype(F32))
    norm_attn = (xhat * gain_attn + shift_attn).astype(BF)
    norm_mlp = (xhat * gain_mlp + shift_mlp).astype(BF)
    qkv_all = jnp.dot(norm_attn, qkv_weight, preferred_element_type=F32) + qkv_bias.astype(F32)

    cosine_all, sine_all = rotary_tables(LEN, ROT)

    def in_order(table):
        return jnp.concatenate(
            [lax.dynamic_slice_in_dim(table, b * rows, rows, 0) for b in block_ids], axis=0
        )

    cosine_table = in_order(cosine_all)[:, None, :]
    sine_table = in_order(sine_all)[:, None, :]
    spots = jnp.concatenate([b * rows + jnp.arange(rows, dtype=jnp.int32) for b in block_ids])
    scale_factor = HD ** (-0.5)
    visible = (spots[None, :] <= spots[:, None]) | (spots[None, :] < prefix_len[0])

    split_qkv = qkv_all.reshape(LEN, heads, 3, HD)
    queries = rotate_block(split_qkv[:, :, 0], cosine_table, sine_table).astype(BF)
    keys_rot = rotate_block(split_qkv[:, :, 1], cosine_table, sine_table).astype(BF)
    values = split_qkv[:, :, 2].astype(BF)

    def masked_scores():
        scores = (
            jnp.einsum("qhd,khd->hqk", queries, keys_rot, preferred_element_type=F32)
            * scale_factor
        )
        return jnp.where(visible[None], scores, -jnp.inf)

    scores = masked_scores()
    top_score = jnp.max(scores, axis=-1, keepdims=True)
    log_total = top_score + jnp.log(jnp.sum(jnp.exp(scores - top_score), axis=-1, keepdims=True))
    attention_low = jnp.exp(scores - log_total).astype(BF)
    context = (
        jnp.einsum("hqk,khd->qhd", attention_low, values, preferred_element_type=F32)
        .astype(BF)
        .reshape(LEN, heads * HD)
    )
    hidden_pre = jnp.dot(norm_mlp, fc1_weight, preferred_element_type=F32) + fc1_bias.astype(F32)
    active = exact_gelu(hidden_pre).astype(BF)
    branch_part = jnp.dot(context, out_weight, preferred_element_type=F32) + jnp.dot(
        active, fc2_weight, preferred_element_type=F32
    )

    def scatter_rows(part):
        blocks = part.reshape(ways, 2, rows, D)
        mine = blocks[:, 0] + to_core(blocks[:, 1].astype(BF)).astype(F32)
        total = mine[0]
        for step in range(1, ways):
            total = total + to_y(mine[step].astype(BF), step).astype(F32)
        return total

    branch = scatter_rows(branch_part)
    output_f = hidden.astype(F32) + branch + out_bias.astype(F32) + fc2_bias.astype(F32)
    mismatch = output_f - teacher.astype(F32)
    error_part = jnp.sum(mask_f[:, None] * mismatch * mismatch)
    grad_out = mask_f[:, None] * mismatch * (2.0 * total_tokens / count_all)
    bias_part = jnp.sum(grad_out, axis=0)
    grad_low = grad_out.astype(BF)
    grad_near = jnp.concatenate(gather_rows(grad_low), axis=0)
    grad_far = jnp.concatenate(gather_rows(to_side(grad_low)), axis=0)

    xhat_far, _ = normalize(hidden_far.astype(F32))
    norm_attn_far = (xhat_far * gain_attn + shift_attn).astype(BF)
    norm_mlp_far = (xhat_far * gain_mlp + shift_mlp).astype(BF)
    fc1_half = own_side(fc1_weight, 1)
    fc2_half = own_side(fc2_weight, 0)
    pre_far = jnp.dot(norm_mlp_far, fc1_half, preferred_element_type=F32) + own_side(
        fc1_bias, 0
    ).astype(F32)
    active_far = exact_gelu(pre_far).astype(BF)
    context_far = to_side(other_side(context, 1))

    flight = {"in": [], "mid": [], "out": [], "side": []}

    def send(kind, value, move):
        past = flight[kind]
        if len(past) >= 2:
            value = after(value, past[-2])
        result = move(value)
        past.append(result)
        return result

    middle = (place == line // 2 - 1) | (place == line // 2)

    def line_total(part):
        held = part
        low = part.astype(BF)
        for hop in range(line // 2 - 1):
            got = send(
                "in",
                low,
                lambda v, h=hop: along(v, [(h, h + 1), (line - 1 - h, line - 2 - h)]),
            )
            low = (held + got.astype(F32)).astype(BF)
        got = send(
            "mid",
            low,
            lambda v: along(v, [(line // 2 - 1, line // 2), (line // 2, line // 2 - 1)]),
        )
        low = (low.astype(F32) + got.astype(F32)).astype(BF)
        for hop in reversed(range(line // 2 - 1)):
            got = send(
                "out",
                low,
                lambda v, h=hop: along(v, [(h + 1, h), (line - 2 - h, line - 1 - h)]),
            )
            low = jnp.where((place == hop) | (place == line - 1 - hop), got, low)
        return low

    def summed(part, chunks, axis):
        size = part.shape[0] // chunks
        mine, theirs = [], []
        for i in range(chunks):
            low = line_total(lax.slice_in_dim(part, i * size, (i + 1) * size, axis=0))
            mine.append(low)
            theirs.append(send("side", low, to_side))
        mine = jnp.concatenate(mine, axis=0)
        theirs = jnp.concatenate(theirs, axis=0)
        first = jnp.where(side == 0, mine, theirs).astype(F32)
        second = jnp.where(side == 0, theirs, mine).astype(F32)
        return jnp.concatenate([first, second], axis=axis)

    fc2_part = contract(own_side(active, 1), grad_near, 0, 0) + contract(
        active_far, grad_far, 0, 0
    )
    fc2_weight_grad = summed(fc2_part, 4, 0)
    out_part = contract(own_side(context, 1), grad_near, 0, 0) + contract(
        context_far, grad_far, 0, 0
    )
    out_weight_grad = summed(out_part, 1, 0)

    grad_inner = jax.vjp(exact_gelu, hidden_pre)[1](contract(grad_near, fc2_weight, 1, 1))[
        0
    ].astype(BF)
    grad_inner_far = jax.vjp(exact_gelu, pre_far)[1](contract(grad_far, fc2_half, 1, 1))[
        0
    ].astype(BF)
    fc1_part = contract(norm_mlp, own_side(grad_inner, 1), 0, 0) + contract(
        norm_mlp_far, grad_inner_far, 0, 0
    )
    fc1_weight_grad = summed(fc1_part, 4, 1)
    fc1_bias_part = jnp.sum(grad_inner, axis=0, dtype=F32)

    grad_context = contract(grad_near, out_weight, 1, 1).astype(BF).reshape(LEN, heads, HD)
    attention = jnp.exp(masked_scores() - log_total)
    grad_attention = jnp.einsum("qhd,khd->hqk", grad_context, values, preferred_element_type=F32)
    row_dots = jnp.sum(attention * grad_attention, axis=-1, keepdims=True)
    grad_scores = (attention * (grad_attention - row_dots)).astype(BF)
    grad_queries = (
        jnp.einsum("hqk,khd->qhd", grad_scores, keys_rot, preferred_element_type=F32)
        * scale_factor
    )
    grad_keys = (
        jnp.einsum("hqk,qhd->khd", grad_scores, queries, preferred_element_type=F32)
        * scale_factor
    )
    grad_values = jnp.einsum(
        "hqk,qhd->khd", attention.astype(BF), grad_context, preferred_element_type=F32
    )
    grad_qkv = (
        jnp.stack(
            [
                rotate_block(grad_queries, cosine_table, -sine_table),
                rotate_block(grad_keys, cosine_table, -sine_table),
                grad_values,
            ],
            axis=2,
        )
        .reshape(LEN, heads * 3 * HD)
        .astype(BF)
    )
    grad_qkv_far = to_side(other_side(grad_qkv, 1))
    qkv_part = contract(norm_attn, own_side(grad_qkv, 1), 0, 0) + contract(
        norm_attn_far, grad_qkv_far, 0, 0
    )
    qkv_weight_grad = summed(qkv_part, 4, 1)
    qkv_bias_part = jnp.sum(grad_qkv, axis=0, dtype=F32)

    grad_norm_mlp = contract(grad_inner, fc1_weight, 1, 1)
    grad_norm_attn = contract(grad_qkv, qkv_weight, 1, 1)

    def norm_back(gained):
        return inverse * (
            gained
            - jnp.mean(gained, axis=-1, keepdims=True)
            - xhat * jnp.mean(gained * xhat, axis=-1, keepdims=True)
        )

    grad_hidden = norm_back(grad_norm_attn * gain_attn + grad_norm_mlp * gain_mlp)
    input_grad = grad_out + scatter_rows(grad_hidden)
    tensor_parts = jnp.stack(
        [
            jnp.sum(grad_norm_attn * xhat, axis=0),
            jnp.sum(grad_norm_attn, axis=0),
            jnp.sum(grad_norm_mlp * xhat, axis=0),
            jnp.sum(grad_norm_mlp, axis=0),
            bias_part,
            jnp.full((D,), error_part, F32),
        ]
    ).reshape(-1)
    small = jnp.concatenate([tensor_sum(tensor_parts), fc1_bias_part, qkv_bias_part])
    small = dp_sum(small)
    vectors = small[: 6 * D].reshape(6, D)
    fc1_bias_grad = small[6 * D : 6 * D + fc1_bias_part.shape[0]]
    qkv_bias_grad = small[6 * D + fc1_bias_part.shape[0] :]
    loss_value = vectors[5, 0] / (count_all * D)
    return (
        output_f.astype(BF),
        loss_value,
        input_grad,
        vectors[0],
        vectors[1],
        vectors[2],
        vectors[3],
        qkv_weight_grad,
        qkv_bias_grad,
        out_weight_grad,
        vectors[4],
        fc1_weight_grad,
        fc1_bias_grad,
        fc2_weight_grad,
        vectors[4],
    )


def solution(mesh):
    tokens = P(("dp", "tensor"), None)
    columns, lanes, down, whole = P(None, "tensor"), P("tensor"), P("tensor", None), P()
    in_specs = (
        tokens,
        tokens,
        P(("dp", "tensor")),
        P("dp"),
        whole,
        whole,
        whole,
        whole,
        columns,
        lanes,
        down,
        whole,
        columns,
        lanes,
        down,
        whole,
    )
    out_specs = (
        tokens,
        whole,
        tokens,
        whole,
        whole,
        whole,
        whole,
        columns,
        lanes,
        down,
        whole,
        columns,
        lanes,
        down,
        whole,
    )
    return jax.shard_map(
        on_device, mesh=mesh, in_specs=in_specs, out_specs=out_specs, check_vma=False
    )
```

time: 1980 us -> 957 us (0.48)
  waiting for transfers between devices: 1520 us -> 377 us
  blocking collectives: 122 us -> 0 us
  starting transfers between devices: 0.37 us -> 117 us
  other arithmetic: 66.9 us -> 130 us
  matrix products: 179 us -> 231 us
    psum x1 -> x0, waiting for transfers between devices: 1420 us -> none  [on_device(): lax.psum((qkv_weight_part, qkv_bias_part, out_weight_part, fc1_weight_par...]
    ppermute x0 -> x82, waiting for transfers between devices: none -> 377 us  [the longest x39 234 us: along(): lax.ppermute(v, 'dp', [(a * 2 + s, b * 2 + s) for a, b in hops for s in (...]
    psum x3 -> x0, blocking collectives: 122 us -> none  [the longest x2 84 us: on_device(): count_all, error_all = lax.psum((mask_total, error_part), ('dp', 'tensor'))]
    ppermute x0 -> x82, starting transfers between devices: none -> 117 us  [the longest x39 78.5 us: along(): lax.ppermute(v, 'dp', [(a * 2 + s, b * 2 + s) for a, b in hops for s in (...]
    all_gather x2 -> x0, waiting for transfers between devices: 65.2 us -> none  [the longest x1 34.4 us: on_device(): lax.all_gather(grad_out.astype(jnp.bfloat16), 'tensor', axis=0, tiled=True)]
    dot_general x8 -> x13, matrix products: 97 us -> 140 us  [contract(): lax.dot_general(left_side, right_side, (((left_dim,), (right_dim,)), ((),...]
    concatenate x0 -> x7, other arithmetic: none -> 32.7 us  [the longest x4 32.7 us: summed(): return jnp.concatenate([first, second], axis=axis)]
    reduce_scatter x2 -> x0, waiting for transfers between devices: 30.8 us -> none  [the longest x1 30.8 us: on_device(): lax.psum_scatter(jnp.dot(context, out_weight, preferred_element_type=jnp....]
  transfers between devices with their start and end apart: 5 -> 82, of which waited for: 4 -> 32; matrix products, arithmetic and copies ran while one was open for 3% -> 44% of each run, Pallas kernels for 0% -> 0%
where the time goes in v1:
time: 957 us; the launch traced here: 946 us
  waiting for transfers between devices  377 us (39%)
  matrix products  231 us (24%)
  other arithmetic  130 us (14%)
  starting transfers between devices  117 us (12%)
  local copies, waits for them, and re-layouts  83.9 us (9%)
    ppermute x39, waiting for transfers between devices, along(): lax.ppermute(v, 'dp', [(a * 2 + s, b * 2 + s) for a, b in hops for s in (...  234 us
    dot_general x13, matrix products, contract(): lax.dot_general(left_side, right_side, (((left_dim,), (right_dim,)), ((),...  140 us
    ppermute x39, starting transfers between devices, along(): lax.ppermute(v, 'dp', [(a * 2 + s, b * 2 + s) for a, b in hops for s in (...  78.5 us
    ppermute x4, waiting for transfers between devices, from_y(): return lax.ppermute(v, 'tensor', pairs)  59.8 us
    ppermute x17, waiting for transfers between devices, to_side(): return lax.ppermute(v, 'dp', [(d, d ^ 1) for d in range(dp)])  53 us
    unnamed x203, local copies, waits for them, and re-layouts  36.5 us
    dot_general x1, matrix products, on_device(): jnp.dot(norm_mlp, fc1_weight, preferred_element_type=F32)  35.2 us
    concatenate x4, other arithmetic, summed(): return jnp.concatenate([first, second], axis=axis)  32.7 us
  transfers between devices with their start and end apart: 82, of which 32 were waited for; matrix products, arithmetic and copies ran while one was open for 44% of the time, Pallas kernels for 0%

profile of v1, /device:TPU:0, one launch (start us, length us, event | category | flops | bytes accessed | tf_op | source)
XLA Modules:
  0.0 946.2 jit_solution(9349642774608341777)
XLA Ops:
  5.8 21.4 %collective-permute-done.1 = bf16[256,2048]{1,0:T(8,128)(2,1)} collective-permute-done((bf16[256,2048]{1,0:T(8,128)(2,1)}, bf16[256,2048]{1,0:T(8,128)(2,1)}, u32[]{:S(2)}, u32[]{:S(2)}) %collective-permute-start.1) | collective-permute-done | bytes 1048608 | tf_op jit(solution)/shard_map/ppermute | solution.py:88
  40.9 12.1 %convolution_add_fusion = f32[1024,1536]{1,0:T(8,128)} fusion(bf16[2048,1536]{1,0:T(8,128)(2,1)S(1)} %copy-done.70, f32[1536]{0:T(1024)S(1)} %convert_element_type.383, f32[2048]{0:T(1024)S(1)} %convert_element_type.381, f32[2048]{0:T(1024)S(1)} %convert_element_type.380, f32[1024]{0:T(1024)S(1)} %add_rsqrt_fusion.1, ...), kind=kOutput, calls=%fused_computation.63 | convolution fusion | flops 6471286784 | bytes 16807936 | tf_op jit(solution)/shard_map/dot_general | solution.py:155
  53.1 6.6 copy.69
  59.7 4.8 fusion.115
  75.2 3.6 subtract_convert_fusion.1
  86.2 4.5 convolution_convert_fusion
  90.7 35.2 %multiply_convert_fusion.1 = (bf16[1024,2048]{1,0:T(8,128)(2,1)S(1)}, f32[1024,2048]{1,0:T(8,128)}, f32[1024,2048]{1,0:T(8,128)}) fusion(f32[2048]{0:T(1024)S(1)} %convert_element_type.391, bf16[2048,2048]{1,0:T(8,128)(2,1)S(1)} %bitcast.125, f32[2048]{0:T(1024)S(1)} %convert_element_type.389, f32[2048]{0:T(1024)S(1)} %convert_element_type.388, ...), kind=kOutput, calls=%fused_computation.40 | convolution fusion | flops 8755609600 | bytes 33587200 | tf_op jit(solution)/shard_map/dot_general | solution.py:191
  125.9 13.2 %fusion.118 = f32[1024,2048]{1,0:T(8,128)S(1)} fusion(bf16[1024,2048]{1,0:T(8,128)(2,1)S(1)} %get-tuple-element.115, bf16[2048,2048]{1,0:T(8,128)(2,1)} %param.30), kind=kOutput, calls=%fused_computation.289 | convolution fusion | flops 8589934592 | bytes 20971520 | tf_op jit(solution)/shard_map/dot_general | solution.py:193
  146.2 21.9 %collective-permute-done.22 = bf16[256,2048]{1,0:T(8,128)(2,1)} collective-permute-done((bf16[256,2048]{1,0:T(8,128)(2,1)}, bf16[256,2048]{1,0:T(8,128)(2,1)}, u32[]{:S(2)}, u32[]{:S(2)}) %collective-permute-start.22) | collective-permute-done | bytes 1048608 | tf_op jit(solution)/shard_map/ppermute | solution.py:88
  174.8 23.2 %collective-permute-done.6 = f32[8,128]{1,0:T(8,128)S(1)} collective-permute-done((f32[8,128]{1,0:T(8,128)S(1)}, f32[8,128]{1,0:T(8,128)S(1)}, u32[]{:S(2)}, u32[]{:S(2)}) %collective-permute-start.6) | collective-permute-done | bytes 4128 | tf_op jit(solution)/shard_map/ppermute | solution.py:104
  218.8 4.2 fusion.55
  229.9 16.6 %collective-permute-done.11 = bf16[256,2048]{1,0:T(8,128)(2,1)S(1)} collective-permute-done((bf16[256,2048]{1,0:T(8,128)(2,1)S(1)}, bf16[256,2048]{1,0:T(8,128)(2,1)S(1)}, u32[]{:S(2)}, u32[]{:S(2)}) %collective-permute-start.11) | collective-permute-done | bytes 1048608 | tf_op jit(solution)/shard_map/ppermute | solution.py:88
  246.4 10.5 %fusion.47 = f32[1024,1024]{1,0:T(8,128)} fusion(bf16[2048,2048]{1,0:T(8,128)(2,1)S(1)} %bitcast.127, s32[]{:T(128)S(6)} %select_n.195, f32[1024]{0:T(1024)S(1)} %add_rsqrt_fusion, f32[1024]{0:T(1024)S(1)} %broadcast_multiply_fusion, f32[2048]{0:T(1024)S(1)} %convert_element_type.389, f32[2048]{0:T(1024)S(1)} %convert_element_type.388, ...), kind=kOutput, calls=%fused_computation.93 | convolution fusion | flops 4322230272 | bytes 12607492 | tf_op jit(solution)/shard_map/dot_general | solution.py:220
  261.2 5.5 convolution_convert_fusion.1
  268.7 4.3 multiply_reduce_fusion
  285.7 4.7 copy.89
  290.4 12.0 %fusion.119 = f32[1024,2048]{1,0:T(8,128)} fusion(bf16[1024,1536]{0,1:T(8,128)(2,1)} %bitcast.111, bf16[2048,1536]{1,0:T(8,128)(2,1)} %param.24), kind=kOutput, calls=%fused_computation.290 | convolution fusion | flops 6442450944 | bytes 17825792 | tf_op jit(solution)/shard_map/dot_general | solution.py:37
  302.4 21.0 %convert_reduce_fusion.2 = (f32[2048]{0:T(1024)S(1)}, bf16[1024,2048]{1,0:T(8,128)(2,1)}) fusion(f32[1024,2048]{1,0:T(8,128)} %get-tuple-element.116, bf16[2048,2048]{1,0:T(8,128)(2,1)} %param.30, bf16[256,2048]{1,0:T(8,128)(2,1)} %copy-done.78, bf16[256,2048]{1,0:T(8,128)(2,1)S(1)} %copy-done.72, bf16[256,2048]{1,0:T(8,128)(2,1)} %copy-done.75, ...), kind=kOutput, calls=%fused_computation.36 | convolution fusion | flops 8642361344 | bytes 33570816 | tf_op jit(solution)/shard_map/dot_general | solution.py:37
  323.4 18.6 %fusion.108 = (f32[1024]{0:T(1024)S(1)}, f32[1024]{0:T(1024)S(1)}, f32[1024,2048]{1,0:T(8,128)}, f32[2048]{0:T(1024)S(1)}, f32[2048]{0:T(1024)S(1)}, /*index=5*/f32[2048]{0:T(1024)S(1)}, f32[2048]{0:T(1024)S(1)}) fusion(f32[1024]{0:T(1024)S(1)} %add_rsqrt_fusion.1, f32[1024]{0:T(1024)S(1)} %broadcast_multiply_fusion.3, ...), kind=kOutput, calls=%fused_computation.280 | convolution fusion | flops 8636061696 | bytes 33619968 | tf_op jit(solution)/shard_map/dot_general | solution.py:37
  342.9 7.0 fusion.25
  355.2 9.4 fusion.68
  365.2 6.9 fusion.64
  391.5 19.5 %add_convert_fusion.1 = bf16[1024,1024]{1,0:T(8,128)(2,1)} fusion(f32[1024,1024]{1,0:T(8,128)} %fusion.47, bf16[1024,2048]{1,0:T(8,128)(2,1)} %constant_dynamic-update-slice_fusion, bf16[2048,2048]{1,0:T(8,128)(2,1)} %param.30, s32[]{:T(128)S(6)} %select_n.195, f32[1024]{0:T(1024)S(1)} %copy-done.68), kind=kOutput, calls=%fused_computation.78 | convolution fusion | flops 4371513344 | bytes 14684164 | tf_op jit(solution)/shard_map/dot_general | solution.py:37
  411.1 14.7 %convolution_add_fusion.2 = f32[1024,2048]{1,0:T(8,128)S(1)} fusion(f32[1024,2048]{1,0:T(8,128)S(1)} %bitcast.129, bf16[1024,2048]{1,0:T(8,128)(2,1)S(1)} %copy-done.53, f32[1024,1024]{1,0:T(8,128)} %fusion.47, f32[1024]{0:T(1024)S(1)} %copy-done.68), kind=kOutput, calls=%fused_computation.106 | convolution fusion | flops 4366270464 | bytes 25169920 | tf_op jit(solution)/shard_map/dot_general | solution.py:37
  431.8 9.6 %convolution_add_fusion.3 = f32[2048,1024]{1,0:T(8,128)S(1)} fusion(f32[2048,1024]{1,0:T(8,128)} %fusion.68, bf16[1024,1024]{1,0:T(8,128)(2,1)} %add_convert_fusion.1, f32[1024]{0:T(1024)S(1)} %copy-done.67, f32[1024]{0:T(1024)S(1)} %copy-done.56, f32[2048]{0:T(1024)S(1)} %convert_element_type.389, f32[2048]{0:T(1024)S(1)} %convert_element_type.388, ...), kind=kOutput, calls=%fused_computation.107 | convolution fusion | flops 4324327424 | bytes 23093248 | tf_op jit(solution)/shard_map/dot_general | solution.py:37
  441.4 3.7 fusion.120
  450.2 9.0 fusion.36
  460.6 16.1 %collective-permute-done.29 = bf16[256,2048]{1,0:T(8,128)(2,1)S(1)} collective-permute-done((bf16[256,2048]{1,0:T(8,128)(2,1)}, bf16[256,2048]{1,0:T(8,128)(2,1)S(1)}, u32[]{:S(2)}, u32[]{:S(2)}) %collective-permute-start.29) | collective-permute-done | bytes 1048608 | tf_op jit(solution)/shard_map/ppermute | solution.py:98
  476.7 4.3 collective-permute-start.30
  481.1 4.3 fusion.38
  489.6 9.5 %collective-permute-done.46 = bf16[256,2048]{1,0:T(8,128)(2,1)S(1)} collective-permute-done((bf16[256,2048]{1,0:T(8,128)(2,1)S(1)}, bf16[256,2048]{1,0:T(8,128)(2,1)S(1)}, u32[]{:S(2)}, u32[]{:S(2)}) %collective-permute-start.46) | collective-permute-done | bytes 1048608 | tf_op jit(solution)/shard_map/ppermute | solution.py:98
  499.1 5.3 collective-permute-start.47
  504.4 17.1 %collective-permute-done.30 = bf16[256,2048]{1,0:T(8,128)(2,1)S(1)} collective-permute-done((bf16[256,2048]{1,0:T(8,128)(2,1)S(1)}, bf16[256,2048]{1,0:T(8,128)(2,1)S(1)}, u32[]{:S(2)}, u32[]{:S(2)}) %collective-permute-start.30) | collective-permute-done | bytes 1048608 | tf_op jit(solution)/shard_map/ppermute | solution.py:98
  522.5 5.4 collective-permute-start.31
  527.9 5.0 add_convert_fusion.7
  533.6 7.7 fusion.74
  552.7 13.9 %collective-permute-done.31 = bf16[512,1024]{1,0:T(8,128)(2,1)} collective-permute-done((bf16[512,1024]{1,0:T(8,128)(2,1)}, bf16[512,1024]{1,0:T(8,128)(2,1)}, u32[]{:S(2)}, u32[]{:S(2)}) %collective-permute-start.31) | collective-permute-done | bytes 1048608 | tf_op jit(solution)/shard_map/ppermute | solution.py:98
  566.6 4.4 collective-permute-start.32
  577.6 11.4 %collective-permute-done.48 = bf16[512,1024]{1,0:T(8,128)(2,1)S(1)} collective-permute-done((bf16[512,1024]{1,0:T(8,128)(2,1)S(1)}, bf16[512,1024]{1,0:T(8,128)(2,1)S(1)}, u32[]{:S(2)}, u32[]{:S(2)}) %collective-permute-start.48) | collective-permute-done | bytes 1048608 | tf_op jit(solution)/shard_map/ppermute | solution.py:98
  590.2 18.9 %collective-permute-done.32 = bf16[512,1024]{1,0:T(8,128)(2,1)S(1)} collective-permute-done((bf16[512,1024]{1,0:T(8,128)(2,1)S(1)}, bf16[512,1024]{1,0:T(8,128)(2,1)S(1)}, u32[]{:S(2)}, u32[]{:S(2)}) %collective-permute-start.32) | collective-permute-done | bytes 1048608 | tf_op jit(solution)/shard_map/ppermute | solution.py:98
  609.1 4.4 collective-permute-start.49
  622.7 28.1 %collective-permute-done.33 = bf16[512,768]{1,0:T(8,128)(2,1)S(1)} collective-permute-done((bf16[512,768]{1,0:T(8,128)(2,1)S(1)}, bf16[512,768]{1,0:T(8,128)(2,1)S(1)}, u32[]{:S(2)}, u32[]{:S(2)}) %collective-permute-start.33) | collective-permute-done | bytes 786464 | tf_op jit(solution)/shard_map/ppermute | solution.py:98
  657.6 6.4 collective-permute-done.58
  670.6 5.7 collective-permute-done.69
  676.3 6.0 collective-permute-start.50
  688.0 9.8 %collective-permute-done.50 = bf16[512,768]{1,0:T(8,128)(2,1)} collective-permute-done((bf16[512,768]{1,0:T(8,128)(2,1)S(1)}, bf16[512,768]{1,0:T(8,128)(2,1)}, u32[]{:S(2)}, u32[]{:S(2)}) %collective-permute-start.50) | collective-permute-done | bytes 786464 | tf_op jit(solution)/shard_map/ppermute | solution.py:98
  699.9 9.6 %collective-permute-start.66 = (bf16[512,768]{1,0:T(8,128)(2,1)}, bf16[512,768]{1,0:T(8,128)(2,1)}, u32[]{:S(2)}, u32[]{:S(2)}) collective-permute-start(bf16[512,768]{1,0:T(8,128)(2,1)} %get-tuple-element.89), channel_id=1, source_target_pairs={{0,8},{4,12},{24,16},{28,20},{1,9},{5,13},{25,17},{29,21},{2,10},{... | collective-permute-start | bytes 2359304 | tf_op jit(solution)/shard_map/ppermute | solution.py:98
  709.6 8.0 collective-permute-done.70
  719.4 4.8 broadcast_select_fusion.1
  728.0 11.8 %maximum_convert_fusion.1 = f32[2048,2048]{1,0:T(8,128)} fusion(bf16[1024,2048]{1,0:T(8,128)(2,1)} %get-tuple-element.122, bf16[1024,2048]{1,0:T(8,128)(2,1)} %get-tuple-element.121), kind=kLoop, calls=%fused_computation.34 | loop fusion | flops 16777216 | bytes 25165824 | tf_op jit(solution)/shard_map/concatenate | solution.py:274
  745.6 4.2 add_convert_fusion.21
  752.2 6.1 collective-permute-done.41
  761.9 18.7 %collective-permute-done.60 = bf16[512,1024]{1,0:T(8,128)(2,1)S(1)} collective-permute-done((bf16[512,1024]{1,0:T(8,128)(2,1)S(1)}, bf16[512,1024]{1,0:T(8,128)(2,1)S(1)}, u32[]{:S(2)}, u32[]{:S(2)}) %collective-permute-start.60) | collective-permute-done | bytes 1048608 | tf_op jit(solution)/shard_map/ppermute | solution.py:98
  787.1 16.0 %collective-permute-done.42 = bf16[512,1024]{1,0:T(8,128)(2,1)S(1)} collective-permute-done((bf16[512,1024]{1,0:T(8,128)(2,1)S(1)}, bf16[512,1024]{1,0:T(8,128)(2,1)S(1)}, u32[]{:S(2)}, u32[]{:S(2)}) %collective-permute-start.42) | collective-permute-done | bytes 1048608 | tf_op jit(solution)/shard_map/ppermute | solution.py:98
  805.2 20.3 %collective-permute-done.61 = bf16[512,1024]{1,0:T(8,128)(2,1)S(1)} collective-permute-done((bf16[512,1024]{1,0:T(8,128)(2,1)S(1)}, bf16[512,1024]{1,0:T(8,128)(2,1)S(1)}, u32[]{:S(2)}, u32[]{:S(2)}) %collective-permute-start.61) | collective-permute-done | bytes 1048608 | tf_op jit(solution)/shard_map/ppermute | solution.py:98
  829.7 12.7 %collective-permute-done.43 = bf16[512,768]{1,0:T(8,128)(2,1)S(1)} collective-permute-done((bf16[512,768]{1,0:T(8,128)(2,1)S(1)}, bf16[512,768]{1,0:T(8,128)(2,1)S(1)}, u32[]{:S(2)}, u32[]{:S(2)}) %collective-permute-start.43) | collective-permute-done | bytes 786464 | tf_op jit(solution)/shard_map/ppermute | solution.py:98
  843.7 15.6 %collective-permute-done.62 = bf16[512,768]{1,0:T(8,128)(2,1)S(1)} collective-permute-done((bf16[512,768]{1,0:T(8,128)(2,1)S(1)}, bf16[512,768]{1,0:T(8,128)(2,1)S(1)}, u32[]{:S(2)}, u32[]{:S(2)}) %collective-permute-start.62) | collective-permute-done | bytes 786464 | tf_op jit(solution)/shard_map/ppermute | solution.py:98
  861.4 12.7 %collective-permute-done.78 = bf16[512,1024]{1,0:T(8,128)(2,1)S(1)} collective-permute-done((bf16[512,1024]{1,0:T(8,128)(2,1)S(1)}, bf16[512,1024]{1,0:T(8,128)(2,1)S(1)}, u32[]{:S(2)}, u32[]{:S(2)}) %collective-permute-start.78) | collective-permute-done | bytes 1048608 | tf_op jit(solution)/shard_map/ppermute | solution.py:95
  874.8 4.9 broadcast_select_fusion.3
  879.8 9.7 %collective-permute-done.68 = bf16[512,768]{1,0:T(8,128)(2,1)S(1)} collective-permute-done((bf16[512,768]{1,0:T(8,128)(2,1)S(1)}, bf16[512,768]{1,0:T(8,128)(2,1)S(1)}, u32[]{:S(2)}, u32[]{:S(2)}) %collective-permute-start.68) | collective-permute-done | bytes 786464 | tf_op jit(solution)/shard_map/ppermute | solution.py:98
  891.5 16.3 %collective-permute-done.79 = bf16[512,768]{1,0:T(8,128)(2,1)S(1)} collective-permute-done((bf16[512,768]{1,0:T(8,128)(2,1)S(1)}, bf16[512,768]{1,0:T(8,128)(2,1)S(1)}, u32[]{:S(2)}, u32[]{:S(2)}) %collective-permute-start.79) | collective-permute-done | bytes 786464 | tf_op jit(solution)/shard_map/ppermute | solution.py:95
  908.7 11.7 %maximum_convert_fusion = f32[2048,2048]{1,0:T(8,128)} fusion(bf16[2048,1024]{1,0:T(8,128)(2,1)} %get-tuple-element.124, bf16[2048,1024]{1,0:T(8,128)(2,1)} %get-tuple-element.123), kind=kLoop, calls=%fused_computation.33 | loop fusion | flops 16777216 | bytes 25165824 | tf_op jit(solution)/shard_map/concatenate | solution.py:274
  926.0 7.9 collective-permute-done.81
  937.5 6.6 maximum_convert_fusion.3
  (461 shorter events, 233.9 us)
Async XLA Ops:
  0.7 26.5 %collective-permute-start.1 = (bf16[256,2048]{1,0:T(8,128)(2,1)}, bf16[256,2048]{1,0:T(8,128)(2,1)}, u32[]{:S(2)}, u32[]{:S(2)}) collective-permute-start(bf16[256,2048]{1,0:T(8,128)(2,1)} %param.16), channel_id=1, source_target_pairs={{0,2},{1,3},{2,0},{3,1},{4,6},{5,7},{6,4},{7,5},{8,10},{9,11},{10,... | collective-permute-start | bytes 3145736 | tf_op jit(solution)/shard_map/ppermute | solution.py:88
  3.7 31.4 %collective-permute-start = (bf16[256,2048]{1,0:T(8,128)(2,1)}, bf16[256,2048]{1,0:T(8,128)(2,1)}, u32[]{:S(2)}, u32[]{:S(2)}) collective-permute-start(bf16[256,2048]{1,0:T(8,128)(2,1)} %param.16), channel_id=1, source_target_pairs={{0,1},{1,0},{2,3},{3,2},{4,5},{5,4},{6,7},{7,6},{8,9},{9,8},{10,11... | collective-permute-start | bytes 3145736 | tf_op jit(solution)/shard_map/ppermute | solution.py:84
  3.7 138.8 %collective-permute-start.20 = (bf16[256,2048]{1,0:T(8,128)(2,1)}, bf16[256,2048]{1,0:T(8,128)(2,1)}, u32[]{:S(2)}, u32[]{:S(2)}) collective-permute-start(bf16[256,2048]{1,0:T(8,128)(2,1)} %param.16), channel_id=1, source_target_pairs={{0,4},{4,0},{8,12},{12,8},{16,20},{20,16},{24,28},{28,24},{1,5},{5... | collective-permute-start | bytes 3145736 | tf_op jit(solution)/shard_map/ppermute | solution.py:95
  142.0 26.1 %collective-permute-start.3 = (bf16[2,256,2048]{2,1,0:T(8,128)(2,1)S(1)}, bf16[2,256,2048]{2,1,0:T(8,128)(2,1)S(1)}, u32[]{:S(2)}, u32[]{:S(2)}) collective-permute-start(bf16[2,256,2048]{2,1,0:T(8,128)(2,1)S(1)} %fusion.56), channel_id=1, source_target_pairs={{0,1},{1,0},{2,3},{3,2},{4,5},{5,4},{6,7},{7,6},{8,9},{9,8},{10,11... | collective-permute-start | bytes 6291464 | tf_op jit(solution)/shard_map/ppermute | solution.py:84
  145.6 28.2 %collective-permute-start.5 = (f32[8,128]{1,0:T(8,128)S(1)}, f32[8,128]{1,0:T(8,128)S(1)}, u32[]{:S(2)}, u32[]{:S(2)}) collective-permute-start(f32[8,128]{1,0:T(8,128)S(1)} %broadcast_in_dim.16), channel_id=1, source_target_pairs={{0,1},{1,0},{2,3},{3,2},{4,5},{5,4},{6,7},{7,6},{8,9},{9,8},{10,11... | collective-permute-start | bytes 12296 | tf_op jit(solution)/shard_map/ppermute | solution.py:84
  145.7 70.6 %collective-permute-start.21 = (bf16[256,2048]{1,0:T(8,128)(2,1)}, bf16[256,2048]{1,0:T(8,128)(2,1)}, u32[]{:S(2)}, u32[]{:S(2)}) collective-permute-start(bf16[256,2048]{1,0:T(8,128)(2,1)} %collective-permute-done.20), channel_id=1, source_target_pairs={{0,1},{1,0},{2,3},{3,2},{4,5},{5,4},{6,7},{7,6},{8,9},{9,8},{10,11... | collective-permute-start | bytes 3145736 | tf_op jit(solution)/shard_map/ppermute | solution.py:84
  168.0 48.2 %collective-permute-start.23 = (bf16[256,2048]{1,0:T(8,128)(2,1)}, bf16[256,2048]{1,0:T(8,128)(2,1)}, u32[]{:S(2)}, u32[]{:S(2)}) collective-permute-start(bf16[256,2048]{1,0:T(8,128)(2,1)} %collective-permute-done.22), channel_id=1, source_target_pairs={{0,1},{1,0},{2,3},{3,2},{4,5},{5,4},{6,7},{7,6},{8,9},{9,8},{10,11... | collective-permute-start | bytes 3145736 | tf_op jit(solution)/shard_map/ppermute | solution.py:84
  172.0 46.7 %collective-permute-start.4 = (bf16[256,2048]{1,0:T(8,128)(2,1)}, bf16[256,2048]{1,0:T(8,128)(2,1)}, u32[]{:S(2)}, u32[]{:S(2)}) collective-permute-start(bf16[256,2048]{1,0:T(8,128)(2,1)} %fusion.77), channel_id=1, source_target_pairs={{0,2},{1,3},{2,0},{3,1},{4,6},{5,7},{6,4},{7,5},{8,10},{9,11},{10,... | collective-permute-start | bytes 3145736 | tf_op jit(solution)/shard_map/ppermute | solution.py:92
  214.5 226.9 %collective-permute-start.44 = (bf16[1024,256]{0,1:T(8,128)(2,1)}, bf16[1024,256]{0,1:T(8,128)(2,1)}, u32[]{:S(2)}, u32[]{:S(2)}) collective-permute-start(bf16[1024,256]{0,1:T(8,128)(2,1)} %constant_dynamic-slice_fusion), channel_id=1, source_target_pairs={{0,4},{4,0},{8,12},{12,8},{16,20},{20,16},{24,28},{28,24},{1,5},{5... | collective-permute-start | bytes 1572872 | tf_op jit(solution)/shard_map/ppermute | solution.py:95
  229.2 32.0 %collective-permute-start.10 = (bf16[256,2048]{1,0:T(8,128)(2,1)S(1)}, bf16[256,2048]{1,0:T(8,128)(2,1)S(1)}, u32[]{:S(2)}, u32[]{:S(2)}) collective-permute-start(bf16[256,2048]{1,0:T(8,128)(2,1)S(1)} %fusion.71), channel_id=1, source_target_pairs={{0,1},{1,0},{2,3},{3,2},{4,5},{5,4},{6,7},{7,6},{8,9},{9,8},{10,11... | collective-permute-start | bytes 3145736 | tf_op jit(solution)/shard_map/ppermute | solution.py:84
  229.2 27.7 %collective-permute-start.25 = (bf16[256,2048]{1,0:T(8,128)(2,1)S(1)}, bf16[256,2048]{1,0:T(8,128)(2,1)}, u32[]{:S(2)}, u32[]{:S(2)}) collective-permute-start(bf16[256,2048]{1,0:T(8,128)(2,1)S(1)} %fusion.71), channel_id=1, source_target_pairs={{0,4},{4,0},{8,12},{12,8},{16,20},{20,16},{24,28},{28,24},{1,5},{5... | collective-permute-start | bytes 3145736 | tf_op jit(solution)/shard_map/ppermute | solution.py:95
  256.9 120.0 %collective-permute-start.26 = (bf16[256,2048]{1,0:T(8,128)(2,1)}, bf16[256,2048]{1,0:T(8,128)(2,1)}, u32[]{:S(2)}, u32[]{:S(2)}) collective-permute-start(bf16[256,2048]{1,0:T(8,128)(2,1)} %collective-permute-done.25), channel_id=1, source_target_pairs={{0,1},{1,0},{2,3},{3,2},{4,5},{5,4},{6,7},{7,6},{8,9},{9,8},{10,11... | collective-permute-start | bytes 3145736 | tf_op jit(solution)/shard_map/ppermute | solution.py:84
  257.1 118.3 %collective-permute-start.27 = (bf16[256,2048]{1,0:T(8,128)(2,1)}, bf16[256,2048]{1,0:T(8,128)(2,1)}, u32[]{:S(2)}, u32[]{:S(2)}) collective-permute-start(bf16[256,2048]{1,0:T(8,128)(2,1)} %collective-permute-done.25), channel_id=1, source_target_pairs={{0,2},{1,3},{2,0},{3,1},{4,6},{5,7},{6,4},{7,5},{8,10},{9,11},{10,... | collective-permute-start | bytes 3145736 | tf_op jit(solution)/shard_map/ppermute | solution.py:88
  351.6 129.5 %collective-permute-start.18 = (bf16[2,256,2048]{2,1,0:T(8,128)(2,1)}, bf16[2,256,2048]{2,1,0:T(8,128)(2,1)}, u32[]{:S(2)}, u32[]{:S(2)}) collective-permute-start(bf16[2,256,2048]{2,1,0:T(8,128)(2,1)} %fusion.57), channel_id=1, source_target_pairs={{0,1},{1,0},{2,3},{3,2},{4,5},{5,4},{6,7},{7,6},{8,9},{9,8},{10,11... | collective-permute-start | bytes 6291464 | tf_op jit(solution)/shard_map/ppermute | solution.py:84
  375.4 74.8 %collective-permute-start.24 = (bf16[1024,768]{0,1:T(8,128)(2,1)}, bf16[1024,768]{0,1:T(8,128)(2,1)}, u32[]{:S(2)}, u32[]{:S(2)}) collective-permute-start(bf16[1024,768]{0,1:T(8,128)(2,1)} %constant_dynamic-slice_fusion.1), channel_id=1, source_target_pairs={{0,4},{4,0},{8,12},{12,8},{16,20},{20,16},{24,28},{28,24},{1,5},{5... | collective-permute-start | bytes 4718600 | tf_op jit(solution)/shard_map/ppermute | solution.py:95
  428.1 31.1 %collective-permute-start.45 = (bf16[256,2048]{1,0:T(8,128)(2,1)}, bf16[256,2048]{1,0:T(8,128)(2,1)S(1)}, u32[]{:S(2)}, u32[]{:S(2)}) collective-permute-start(bf16[256,2048]{1,0:T(8,128)(2,1)} %get-tuple-element.133), channel_id=1, source_target_pairs={{0,8},{4,12},{24,16},{28,20},{1,9},{5,13},{25,17},{29,21},{2,10},{... | collective-permute-start | bytes 3145736 | tf_op jit(solution)/shard_map/ppermute | solution.py:98
  430.4 46.3 %collective-permute-start.29 = (bf16[256,2048]{1,0:T(8,128)(2,1)}, bf16[256,2048]{1,0:T(8,128)(2,1)S(1)}, u32[]{:S(2)}, u32[]{:S(2)}) collective-permute-start(bf16[256,2048]{1,0:T(8,128)(2,1)} %get-tuple-element.135), channel_id=1, source_target_pairs={{0,8},{4,12},{24,16},{28,20},{1,9},{5,13},{25,17},{29,21},{2,10},{... | collective-permute-start | bytes 3145736 | tf_op jit(solution)/shard_map/ppermute | solution.py:98
  459.2 39.8 %collective-permute-start.46 = (bf16[256,2048]{1,0:T(8,128)(2,1)S(1)}, bf16[256,2048]{1,0:T(8,128)(2,1)S(1)}, u32[]{:S(2)}, u32[]{:S(2)}) collective-permute-start(bf16[256,2048]{1,0:T(8,128)(2,1)S(1)} %copy-done.39), channel_id=1, source_target_pairs={{0,8},{4,12},{24,16},{28,20},{1,9},{5,13},{25,17},{29,21},{2,10},{... | collective-permute-start | bytes 3145736 | tf_op jit(solution)/shard_map/ppermute | solution.py:98
  476.7 44.8 %collective-permute-start.30 = (bf16[256,2048]{1,0:T(8,128)(2,1)S(1)}, bf16[256,2048]{1,0:T(8,128)(2,1)S(1)}, u32[]{:S(2)}, u32[]{:S(2)}) collective-permute-start(bf16[256,2048]{1,0:T(8,128)(2,1)S(1)} %copy-done.38), channel_id=1, source_target_pairs={{0,8},{4,12},{24,16},{28,20},{1,9},{5,13},{25,17},{29,21},{2,10},{... | collective-permute-start | bytes 3145736 | tf_op jit(solution)/shard_map/ppermute | solution.py:98
  488.1 55.7 %collective-permute-start.19 = (bf16[256,2048]{1,0:T(8,128)(2,1)}, bf16[256,2048]{1,0:T(8,128)(2,1)}, u32[]{:S(2)}, u32[]{:S(2)}) collective-permute-start(bf16[256,2048]{1,0:T(8,128)(2,1)} %fusion.78), channel_id=1, source_target_pairs={{0,2},{1,3},{2,0},{3,1},{4,6},{5,7},{6,4},{7,5},{8,10},{9,11},{10,... | collective-permute-start | bytes 3145736 | tf_op jit(solution)/shard_map/ppermute | solution.py:92
  499.1 51.5 %collective-permute-start.47 = (bf16[256,2048]{1,0:T(8,128)(2,1)}, bf16[256,2048]{1,0:T(8,128)(2,1)}, u32[]{:S(2)}, u32[]{:S(2)}) collective-permute-start(bf16[256,2048]{1,0:T(8,128)(2,1)} %get-tuple-element.72), channel_id=1, source_target_pairs={{0,8},{4,12},{24,16},{28,20},{1,9},{5,13},{25,17},{29,21},{2,10},{... | collective-permute-start | bytes 3145736 | tf_op jit(solution)/shard_map/ppermute | solution.py:98
  522.5 44.1 %collective-permute-start.31 = (bf16[512,1024]{1,0:T(8,128)(2,1)}, bf16[512,1024]{1,0:T(8,128)(2,1)}, u32[]{:S(2)}, u32[]{:S(2)}) collective-permute-start(bf16[512,1024]{1,0:T(8,128)(2,1)} %get-tuple-element.60), channel_id=1, source_target_pairs={{0,8},{4,12},{24,16},{28,20},{1,9},{5,13},{25,17},{29,21},{2,10},{... | collective-permute-start | bytes 3145736 | tf_op jit(solution)/shard_map/ppermute | solution.py:98
  532.9 38.2 %collective-permute-start.34 = (bf16[256,2048]{1,0:T(8,128)(2,1)}, bf16[256,2048]{1,0:T(8,128)(2,1)S(1)}, u32[]{:S(2)}, u32[]{:S(2)}) collective-permute-start(bf16[256,2048]{1,0:T(8,128)(2,1)} %get-tuple-element.127), channel_id=1, source_target_pairs={{8,16},{12,20},{16,8},{20,12},{9,17},{13,21},{17,9},{21,13},{10,18... | collective-permute-start | bytes 3145736 | tf_op jit(solution)/shard_map/ppermute | solution.py:98
  542.9 32.0 %collective-permute-start.51 = (bf16[256,2048]{1,0:T(8,128)(2,1)S(1)}, bf16[256,2048]{1,0:T(8,128)(2,1)S(1)}, u32[]{:S(2)}, u32[]{:S(2)}) collective-permute-start(bf16[256,2048]{1,0:T(8,128)(2,1)S(1)} %copy-done.17), channel_id=1, source_target_pairs={{8,16},{12,20},{16,8},{20,12},{9,17},{13,21},{17,9},{21,13},{10,18... | collective-permute-start | bytes 3145736 | tf_op jit(solution)/shard_map/ppermute | solution.py:98
  550.6 38.4 %collective-permute-start.48 = (bf16[512,1024]{1,0:T(8,128)(2,1)S(1)}, bf16[512,1024]{1,0:T(8,128)(2,1)S(1)}, u32[]{:S(2)}, u32[]{:S(2)}) collective-permute-start(bf16[512,1024]{1,0:T(8,128)(2,1)S(1)} %copy-done.37), channel_id=1, source_target_pairs={{0,8},{4,12},{24,16},{28,20},{1,9},{5,13},{25,17},{29,21},{2,10},{... | collective-permute-start | bytes 3145736 | tf_op jit(solution)/shard_map/ppermute | solution.py:98
  566.6 42.5 %collective-permute-start.32 = (bf16[512,1024]{1,0:T(8,128)(2,1)S(1)}, bf16[512,1024]{1,0:T(8,128)(2,1)S(1)}, u32[]{:S(2)}, u32[]{:S(2)}) collective-permute-start(bf16[512,1024]{1,0:T(8,128)(2,1)S(1)} %copy-done.36), channel_id=1, source_target_pairs={{0,8},{4,12},{24,16},{28,20},{1,9},{5,13},{25,17},{29,21},{2,10},{... | collective-permute-start | bytes 3145736 | tf_op jit(solution)/shard_map/ppermute | solution.py:98
  571.1 42.5 %collective-permute-start.35 = (bf16[256,2048]{1,0:T(8,128)(2,1)S(1)}, bf16[256,2048]{1,0:T(8,128)(2,1)S(1)}, u32[]{:S(2)}, u32[]{:S(2)}) collective-permute-start(bf16[256,2048]{1,0:T(8,128)(2,1)S(1)} %get-tuple-element.63), channel_id=1, source_target_pairs={{8,16},{12,20},{16,8},{20,12},{9,17},{13,21},{17,9},{21,13},{10,18... | collective-permute-start | bytes 3145736 | tf_op jit(solution)/shard_map/ppermute | solution.py:98
  573.4 41.9 %collective-permute-start.39 = (bf16[256,2048]{1,0:T(8,128)(2,1)S(1)}, bf16[256,2048]{1,0:T(8,128)(2,1)S(1)}, u32[]{:S(2)}, u32[]{:S(2)}) collective-permute-start(bf16[256,2048]{1,0:T(8,128)(2,1)S(1)} %add_convert_fusion.12), channel_id=1, source_target_pairs={{8,0},{12,4},{16,24},{20,28},{9,1},{13,5},{17,25},{21,29},{10,2},{... | collective-permute-start | bytes 3145736 | tf_op jit(solution)/shard_map/ppermute | solution.py:98
  574.9 41.8 %collective-permute-start.52 = (bf16[256,2048]{1,0:T(8,128)(2,1)S(1)}, bf16[256,2048]{1,0:T(8,128)(2,1)S(1)}, u32[]{:S(2)}, u32[]{:S(2)}) collective-permute-start(bf16[256,2048]{1,0:T(8,128)(2,1)S(1)} %get-tuple-element.76), channel_id=1, source_target_pairs={{8,16},{12,20},{16,8},{20,12},{9,17},{13,21},{17,9},{21,13},{10,18... | collective-permute-start | bytes 3145736 | tf_op jit(solution)/shard_map/ppermute | solution.py:98
  589.0 31.6 %collective-permute-start.57 = (bf16[256,2048]{1,0:T(8,128)(2,1)S(1)}, bf16[256,2048]{1,0:T(8,128)(2,1)S(1)}, u32[]{:S(2)}, u32[]{:S(2)}) collective-permute-start(bf16[256,2048]{1,0:T(8,128)(2,1)S(1)} %add_convert_fusion.2), channel_id=1, source_target_pairs={{8,0},{12,4},{16,24},{20,28},{9,1},{13,5},{17,25},{21,29},{10,2},{... | collective-permute-start | bytes 3145736 | tf_op jit(solution)/shard_map/ppermute | solution.py:98
  609.1 42.2 %collective-permute-start.49 = (bf16[512,1024]{1,0:T(8,128)(2,1)S(1)}, bf16[512,1024]{1,0:T(8,128)(2,1)S(1)}, u32[]{:S(2)}, u32[]{:S(2)}) collective-permute-start(bf16[512,1024]{1,0:T(8,128)(2,1)S(1)} %copy-done.35), channel_id=1, source_target_pairs={{0,8},{4,12},{24,16},{28,20},{1,9},{5,13},{25,17},{29,21},{2,10},{... | collective-permute-start | bytes 3145736 | tf_op jit(solution)/shard_map/ppermute | solution.py:98
  613.6 37.2 %collective-permute-start.33 = (bf16[512,768]{1,0:T(8,128)(2,1)S(1)}, bf16[512,768]{1,0:T(8,128)(2,1)S(1)}, u32[]{:S(2)}, u32[]{:S(2)}) collective-permute-start(bf16[512,768]{1,0:T(8,128)(2,1)S(1)} %get-tuple-element.62), channel_id=1, source_target_pairs={{0,8},{4,12},{24,16},{28,20},{1,9},{5,13},{25,17},{29,21},{2,10},{... | collective-permute-start | bytes 2359304 | tf_op jit(solution)/shard_map/ppermute | solution.py:98
  615.4 53.0 %collective-permute-start.40 = (bf16[256,2048]{1,0:T(8,128)(2,1)S(1)}, bf16[256,2048]{1,0:T(8,128)(2,1)}, u32[]{:S(2)}, u32[]{:S(2)}) collective-permute-start(bf16[256,2048]{1,0:T(8,128)(2,1)S(1)} %add_convert_fusion.13), channel_id=1, source_target_pairs={{8,0},{12,4},{16,24},{20,28},{9,1},{13,5},{17,25},{21,29},{10,2},{... | collective-permute-start | bytes 3145736 | tf_op jit(solution)/shard_map/ppermute | solution.py:98
  620.5 43.5 %collective-permute-start.58 = (bf16[256,2048]{1,0:T(8,128)(2,1)S(1)}, bf16[256,2048]{1,0:T(8,128)(2,1)}, u32[]{:S(2)}, u32[]{:S(2)}) collective-permute-start(bf16[256,2048]{1,0:T(8,128)(2,1)S(1)} %add_convert_fusion.3), channel_id=1, source_target_pairs={{8,0},{12,4},{16,24},{20,28},{9,1},{13,5},{17,25},{21,29},{10,2},{... | collective-permute-start | bytes 3145736 | tf_op jit(solution)/shard_map/ppermute | solution.py:98
  622.0 45.7 %collective-permute-start.74 = (bf16[256,2048]{1,0:T(8,128)(2,1)S(1)}, bf16[256,2048]{1,0:T(8,128)(2,1)}, u32[]{:S(2)}, u32[]{:S(2)}) collective-permute-start(bf16[256,2048]{1,0:T(8,128)(2,1)S(1)} %broadcast_select_fusion.8), channel_id=1, source_target_pairs={{0,4},{4,0},{8,12},{12,8},{16,20},{20,16},{24,28},{28,24},{1,5},{5... | collective-permute-start | bytes 3145736 | tf_op jit(solution)/shard_map/ppermute | solution.py:95
  652.7 29.5 %collective-permute-start.53 = (bf16[256,2048]{1,0:T(8,128)(2,1)S(1)}, bf16[256,2048]{1,0:T(8,128)(2,1)}, u32[]{:S(2)}, u32[]{:S(2)}) collective-permute-start(bf16[256,2048]{1,0:T(8,128)(2,1)S(1)} %add_convert_fusion.9), channel_id=1, source_target_pairs={{8,16},{12,20},{16,8},{20,12},{9,17},{13,21},{17,9},{21,13},{10,18... | collective-permute-start | bytes 3145736 | tf_op jit(solution)/shard_map/ppermute | solution.py:98
  664.0 79.6 %collective-permute-start.63 = (bf16[512,768]{1,0:T(8,128)(2,1)}, bf16[512,768]{1,0:T(8,128)(2,1)}, u32[]{:S(2)}, u32[]{:S(2)}) collective-permute-start(bf16[512,768]{1,0:T(8,128)(2,1)} %get-tuple-element.86), channel_id=1, source_target_pairs={{0,8},{4,12},{24,16},{28,20},{1,9},{5,13},{25,17},{29,21},{2,10},{... | collective-permute-start | bytes 2359304 | tf_op jit(solution)/shard_map/ppermute | solution.py:98
  667.6 30.9 %collective-permute-start.36 = (bf16[512,1024]{1,0:T(8,128)(2,1)S(1)}, bf16[512,1024]{1,0:T(8,128)(2,1)S(1)}, u32[]{:S(2)}, u32[]{:S(2)}) collective-permute-start(bf16[512,1024]{1,0:T(8,128)(2,1)S(1)} %get-tuple-element.64), channel_id=1, source_target_pairs={{8,16},{12,20},{16,8},{20,12},{9,17},{13,21},{17,9},{21,13},{10,18... | collective-permute-start | bytes 3145736 | tf_op jit(solution)/shard_map/ppermute | solution.py:98
  668.4 31.5 %collective-permute-start.75 = (bf16[256,2048]{1,0:T(8,128)(2,1)S(1)}, bf16[256,2048]{1,0:T(8,128)(2,1)S(1)}, u32[]{:S(2)}, u32[]{:S(2)}) collective-permute-start(bf16[256,2048]{1,0:T(8,128)(2,1)S(1)} %broadcast_select_fusion.9), channel_id=1, source_target_pairs={{0,4},{4,0},{8,12},{12,8},{16,20},{20,16},{24,28},{28,24},{1,5},{5... | collective-permute-start | bytes 3145736 | tf_op jit(solution)/shard_map/ppermute | solution.py:95
  682.2 35.4 %collective-permute-start.70 = (bf16[256,2048]{1,0:T(8,128)(2,1)S(1)}, bf16[256,2048]{1,0:T(8,128)(2,1)S(1)}, u32[]{:S(2)}, u32[]{:S(2)}) collective-permute-start(bf16[256,2048]{1,0:T(8,128)(2,1)S(1)} %broadcast_select_fusion.12), channel_id=1, source_target_pairs={{0,4},{4,0},{8,12},{12,8},{16,20},{20,16},{24,28},{28,24},{1,5},{5... | collective-permute-start | bytes 3145736 | tf_op jit(solution)/shard_map/ppermute | solution.py:95
  697.8 27.8 %collective-permute-start.54 = (bf16[512,1024]{1,0:T(8,128)(2,1)S(1)}, bf16[512,1024]{1,0:T(8,128)(2,1)S(1)}, u32[]{:S(2)}, u32[]{:S(2)}) collective-permute-start(bf16[512,1024]{1,0:T(8,128)(2,1)S(1)} %get-tuple-element.78), channel_id=1, source_target_pairs={{8,16},{12,20},{16,8},{20,12},{9,17},{13,21},{17,9},{21,13},{10,18... | collective-permute-start | bytes 3145736 | tf_op jit(solution)/shard_map/ppermute | solution.py:98
  698.6 41.2 %collective-permute-start.59 = (bf16[256,2048]{1,0:T(8,128)(2,1)}, bf16[256,2048]{1,0:T(8,128)(2,1)}, u32[]{:S(2)}, u32[]{:S(2)}) collective-permute-start(bf16[256,2048]{1,0:T(8,128)(2,1)} %add_convert_fusion.4), channel_id=1, source_target_pairs={{8,0},{12,4},{16,24},{20,28},{9,1},{13,5},{17,25},{21,29},{10,2},{... | collective-permute-start | bytes 3145736 | tf_op jit(solution)/shard_map/ppermute | solution.py:98
  699.9 45.1 %collective-permute-start.66 = (bf16[512,768]{1,0:T(8,128)(2,1)}, bf16[512,768]{1,0:T(8,128)(2,1)}, u32[]{:S(2)}, u32[]{:S(2)}) collective-permute-start(bf16[512,768]{1,0:T(8,128)(2,1)} %get-tuple-element.89), channel_id=1, source_target_pairs={{0,8},{4,12},{24,16},{28,20},{1,9},{5,13},{25,17},{29,21},{2,10},{... | collective-permute-start | bytes 2359304 | tf_op jit(solution)/shard_map/ppermute | solution.py:98
  717.7 32.1 %collective-permute-start.37 = (bf16[512,1024]{1,0:T(8,128)(2,1)S(1)}, bf16[512,1024]{1,0:T(8,128)(2,1)}, u32[]{:S(2)}, u32[]{:S(2)}) collective-permute-start(bf16[512,1024]{1,0:T(8,128)(2,1)S(1)} %get-tuple-element.65), channel_id=1, source_target_pairs={{8,16},{12,20},{16,8},{20,12},{9,17},{13,21},{17,9},{21,13},{10,18... | collective-permute-start | bytes 3145736 | tf_op jit(solution)/shard_map/ppermute | solution.py:98
  726.7 31.6 %collective-permute-start.41 = (bf16[512,1024]{1,0:T(8,128)(2,1)}, bf16[512,1024]{1,0:T(8,128)(2,1)}, u32[]{:S(2)}, u32[]{:S(2)}) collective-permute-start(bf16[512,1024]{1,0:T(8,128)(2,1)} %add_convert_fusion.14), channel_id=1, source_target_pairs={{8,0},{12,4},{16,24},{20,28},{9,1},{13,5},{17,25},{21,29},{10,2},{... | collective-permute-start | bytes 3145736 | tf_op jit(solution)/shard_map/ppermute | solution.py:98
  743.7 36.9 %collective-permute-start.60 = (bf16[512,1024]{1,0:T(8,128)(2,1)S(1)}, bf16[512,1024]{1,0:T(8,128)(2,1)S(1)}, u32[]{:S(2)}, u32[]{:S(2)}) collective-permute-start(bf16[512,1024]{1,0:T(8,128)(2,1)S(1)} %add_convert_fusion.5), channel_id=1, source_target_pairs={{8,0},{12,4},{16,24},{20,28},{9,1},{13,5},{17,25},{21,29},{10,2},{... | collective-permute-start | bytes 3145736 | tf_op jit(solution)/shard_map/ppermute | solution.py:98
  745.0 36.3 %collective-permute-start.76 = (bf16[256,2048]{1,0:T(8,128)(2,1)S(1)}, bf16[256,2048]{1,0:T(8,128)(2,1)S(1)}, u32[]{:S(2)}, u32[]{:S(2)}) collective-permute-start(bf16[256,2048]{1,0:T(8,128)(2,1)S(1)} %broadcast_select_fusion.10), channel_id=1, source_target_pairs={{0,4},{4,0},{8,12},{12,8},{16,20},{20,16},{24,28},{28,24},{1,5},{5... | collective-permute-start | bytes 3145736 | tf_op jit(solution)/shard_map/ppermute | solution.py:95
  749.8 35.6 %collective-permute-start.38 = (bf16[512,768]{1,0:T(8,128)(2,1)S(1)}, bf16[512,768]{1,0:T(8,128)(2,1)S(1)}, u32[]{:S(2)}, u32[]{:S(2)}) collective-permute-start(bf16[512,768]{1,0:T(8,128)(2,1)S(1)} %get-tuple-element.66), channel_id=1, source_target_pairs={{8,16},{12,20},{16,8},{20,12},{9,17},{13,21},{17,9},{21,13},{10,18... | collective-permute-start | bytes 2359304 | tf_op jit(solution)/shard_map/ppermute | solution.py:98
  758.2 44.8 %collective-permute-start.42 = (bf16[512,1024]{1,0:T(8,128)(2,1)S(1)}, bf16[512,1024]{1,0:T(8,128)(2,1)S(1)}, u32[]{:S(2)}, u32[]{:S(2)}) collective-permute-start(bf16[512,1024]{1,0:T(8,128)(2,1)S(1)} %add_convert_fusion.15), channel_id=1, source_target_pairs={{8,0},{12,4},{16,24},{20,28},{9,1},{13,5},{17,25},{21,29},{10,2},{... | collective-permute-start | bytes 3145736 | tf_op jit(solution)/shard_map/ppermute | solution.py:98
  760.9 43.0 %collective-permute-start.71 = (bf16[512,1024]{1,0:T(8,128)(2,1)S(1)}, bf16[512,1024]{1,0:T(8,128)(2,1)S(1)}, u32[]{:S(2)}, u32[]{:S(2)}) collective-permute-start(bf16[512,1024]{1,0:T(8,128)(2,1)S(1)} %broadcast_select_fusion.15), channel_id=1, source_target_pairs={{0,4},{4,0},{8,12},{12,8},{16,20},{20,16},{24,28},{28,24},{1,5},{5... | collective-permute-start | bytes 3145736 | tf_op jit(solution)/shard_map/ppermute | solution.py:95
  781.3 44.2 %collective-permute-start.61 = (bf16[512,1024]{1,0:T(8,128)(2,1)S(1)}, bf16[512,1024]{1,0:T(8,128)(2,1)S(1)}, u32[]{:S(2)}, u32[]{:S(2)}) collective-permute-start(bf16[512,1024]{1,0:T(8,128)(2,1)S(1)} %add_convert_fusion.6), channel_id=1, source_target_pairs={{8,0},{12,4},{16,24},{20,28},{9,1},{13,5},{17,25},{21,29},{10,2},{... | collective-permute-start | bytes 3145736 | tf_op jit(solution)/shard_map/ppermute | solution.py:98
  785.5 40.7 %collective-permute-start.77 = (bf16[512,1024]{1,0:T(8,128)(2,1)S(1)}, bf16[512,1024]{1,0:T(8,128)(2,1)S(1)}, u32[]{:S(2)}, u32[]{:S(2)}) collective-permute-start(bf16[512,1024]{1,0:T(8,128)(2,1)S(1)} %broadcast_select_fusion.13), channel_id=1, source_target_pairs={{0,4},{4,0},{8,12},{12,8},{16,20},{20,16},{24,28},{28,24},{1,5},{5... | collective-permute-start | bytes 3145736 | tf_op jit(solution)/shard_map/ppermute | solution.py:95
  786.0 41.7 %collective-permute-start.64 = (bf16[512,768]{1,0:T(8,128)(2,1)S(1)}, bf16[512,768]{1,0:T(8,128)(2,1)S(1)}, u32[]{:S(2)}, u32[]{:S(2)}) collective-permute-start(bf16[512,768]{1,0:T(8,128)(2,1)S(1)} %get-tuple-element.87), channel_id=1, source_target_pairs={{8,16},{12,20},{16,8},{20,12},{9,17},{13,21},{17,9},{21,13},{10,18... | collective-permute-start | bytes 2359304 | tf_op jit(solution)/shard_map/ppermute | solution.py:98
  803.1 26.4 %collective-permute-start.67 = (bf16[512,768]{1,0:T(8,128)(2,1)S(1)}, bf16[512,768]{1,0:T(8,128)(2,1)S(1)}, u32[]{:S(2)}, u32[]{:S(2)}) collective-permute-start(bf16[512,768]{1,0:T(8,128)(2,1)S(1)} %get-tuple-element.90), channel_id=1, source_target_pairs={{8,16},{12,20},{16,8},{20,12},{9,17},{13,21},{17,9},{21,13},{10,18... | collective-permute-start | bytes 2359304 | tf_op jit(solution)/shard_map/ppermute | solution.py:98
  803.9 38.5 %collective-permute-start.43 = (bf16[512,768]{1,0:T(8,128)(2,1)S(1)}, bf16[512,768]{1,0:T(8,128)(2,1)S(1)}, u32[]{:S(2)}, u32[]{:S(2)}) collective-permute-start(bf16[512,768]{1,0:T(8,128)(2,1)S(1)} %add_convert_fusion.26), channel_id=1, source_target_pairs={{8,0},{12,4},{16,24},{20,28},{9,1},{13,5},{17,25},{21,29},{10,2},{... | collective-permute-start | bytes 2359304 | tf_op jit(solution)/shard_map/ppermute | solution.py:98
  825.5 35.2 %collective-permute-start.72 = (bf16[512,1024]{1,0:T(8,128)(2,1)S(1)}, bf16[512,1024]{1,0:T(8,128)(2,1)S(1)}, u32[]{:S(2)}, u32[]{:S(2)}) collective-permute-start(bf16[512,1024]{1,0:T(8,128)(2,1)S(1)} %broadcast_select_fusion.16), channel_id=1, source_target_pairs={{0,4},{4,0},{8,12},{12,8},{16,20},{20,16},{24,28},{28,24},{1,5},{5... | collective-permute-start | bytes 3145736 | tf_op jit(solution)/shard_map/ppermute | solution.py:95
  826.2 33.0 %collective-permute-start.62 = (bf16[512,768]{1,0:T(8,128)(2,1)S(1)}, bf16[512,768]{1,0:T(8,128)(2,1)S(1)}, u32[]{:S(2)}, u32[]{:S(2)}) collective-permute-start(bf16[512,768]{1,0:T(8,128)(2,1)S(1)} %add_convert_fusion.24), channel_id=1, source_target_pairs={{8,0},{12,4},{16,24},{20,28},{9,1},{13,5},{17,25},{21,29},{10,2},{... | collective-permute-start | bytes 2359304 | tf_op jit(solution)/shard_map/ppermute | solution.py:98
  827.7 46.4 %collective-permute-start.78 = (bf16[512,1024]{1,0:T(8,128)(2,1)S(1)}, bf16[512,1024]{1,0:T(8,128)(2,1)S(1)}, u32[]{:S(2)}, u32[]{:S(2)}) collective-permute-start(bf16[512,1024]{1,0:T(8,128)(2,1)S(1)} %broadcast_select_fusion.14), channel_id=1, source_target_pairs={{0,4},{4,0},{8,12},{12,8},{16,20},{20,16},{24,28},{28,24},{1,5},{5... | collective-permute-start | bytes 3145736 | tf_op jit(solution)/shard_map/ppermute | solution.py:95
  842.4 37.3 %collective-permute-start.65 = (bf16[512,768]{1,0:T(8,128)(2,1)S(1)}, bf16[512,768]{1,0:T(8,128)(2,1)S(1)}, u32[]{:S(2)}, u32[]{:S(2)}) collective-permute-start(bf16[512,768]{1,0:T(8,128)(2,1)S(1)} %add_convert_fusion.22), channel_id=1, source_target_pairs={{8,0},{12,4},{16,24},{20,28},{9,1},{13,5},{17,25},{21,29},{10,2},{... | collective-permute-start | bytes 2359304 | tf_op jit(solution)/shard_map/ppermute | solution.py:98
  859.2 30.3 %collective-permute-start.68 = (bf16[512,768]{1,0:T(8,128)(2,1)S(1)}, bf16[512,768]{1,0:T(8,128)(2,1)S(1)}, u32[]{:S(2)}, u32[]{:S(2)}) collective-permute-start(bf16[512,768]{1,0:T(8,128)(2,1)S(1)} %add_convert_fusion.20), channel_id=1, source_target_pairs={{8,0},{12,4},{16,24},{20,28},{9,1},{13,5},{17,25},{21,29},{10,2},{... | collective-permute-start | bytes 2359304 | tf_op jit(solution)/shard_map/ppermute | solution.py:98
  860.8 30.2 %collective-permute-start.73 = (bf16[512,768]{1,0:T(8,128)(2,1)S(1)}, bf16[512,768]{1,0:T(8,128)(2,1)S(1)}, u32[]{:S(2)}, u32[]{:S(2)}) collective-permute-start(bf16[512,768]{1,0:T(8,128)(2,1)S(1)} %broadcast_select_fusion.20), channel_id=1, source_target_pairs={{0,4},{4,0},{8,12},{12,8},{16,20},{20,16},{24,28},{28,24},{1,5},{5... | collective-permute-start | bytes 2359304 | tf_op jit(solution)/shard_map/ppermute | solution.py:95
  874.1 33.7 %collective-permute-start.79 = (bf16[512,768]{1,0:T(8,128)(2,1)S(1)}, bf16[512,768]{1,0:T(8,128)(2,1)S(1)}, u32[]{:S(2)}, u32[]{:S(2)}) collective-permute-start(bf16[512,768]{1,0:T(8,128)(2,1)S(1)} %broadcast_select_fusion.19), channel_id=1, source_target_pairs={{0,4},{4,0},{8,12},{12,8},{16,20},{20,16},{24,28},{28,24},{1,5},{5... | collective-permute-start | bytes 2359304 | tf_op jit(solution)/shard_map/ppermute | solution.py:95
  891.0 33.8 %collective-permute-start.80 = (bf16[512,768]{1,0:T(8,128)(2,1)S(1)}, bf16[512,768]{1,0:T(8,128)(2,1)}, u32[]{:S(2)}, u32[]{:S(2)}) collective-permute-start(bf16[512,768]{1,0:T(8,128)(2,1)S(1)} %broadcast_select_fusion.18), channel_id=1, source_target_pairs={{0,4},{4,0},{8,12},{12,8},{16,20},{20,16},{24,28},{28,24},{1,5},{5... | collective-permute-start | bytes 2359304 | tf_op jit(solution)/shard_map/ppermute | solution.py:95
  907.8 26.0 %collective-permute-start.81 = (bf16[512,768]{1,0:T(8,128)(2,1)}, bf16[512,768]{1,0:T(8,128)(2,1)}, u32[]{:S(2)}, u32[]{:S(2)}) collective-permute-start(bf16[512,768]{1,0:T(8,128)(2,1)} %broadcast_select_fusion.17), channel_id=1, source_target_pairs={{0,4},{4,0},{8,12},{12,8},{16,20},{20,16},{24,28},{28,24},{1,5},{5... | collective-permute-start | bytes 2359304 | tf_op jit(solution)/shard_map/ppermute | solution.py:95
  (112 other events, 1593.4 us)

commit v2 on v1

v2 whole, which is shorter than its diff:
```python
import jax
import jax.numpy as jnp
from jax import lax
from jax.sharding import PartitionSpec as P

D = 2048
HD = 256
ROT = 64
LEN = 1024
EPSILON = 1e-05
BF = jnp.bfloat16
F32 = jnp.float32


def rotary_tables(length, rot_dims):
    half_dims = rot_dims // 2
    frequency = 10000.0 ** (-2.0 * jnp.arange(half_dims, dtype=F32) / rot_dims)
    angles = jnp.arange(length, dtype=F32)[:, None] * frequency[None, :]
    return jnp.cos(angles), jnp.sin(angles)


def rotate_block(block, cosine_table, sine_table):
    half_dims = cosine_table.shape[-1]
    first_half = block[..., :half_dims]
    second_half = block[..., half_dims : 2 * half_dims]
    return jnp.concatenate(
        [
            first_half * cosine_table - second_half * sine_table,
            second_half * cosine_table + first_half * sine_table,
            block[..., 2 * half_dims :],
        ],
        axis=-1,
    )


def contract(left_side, right_side, left_dim, right_dim):
    return lax.dot_general(
        left_side,
        right_side,
        (((left_dim,), (right_dim,)), ((), ())),
        preferred_element_type=F32,
    )


def exact_gelu(pre_act):
    below = 0.5 + 0.5 * lax.erf(pre_act * 0.5**0.5)
    density = jnp.exp(-0.5 * pre_act * pre_act) * (2.0 * jnp.pi) ** -0.5
    return pre_act * below, below + pre_act * density


def after(value, *earlier):
    return lax.optimization_barrier((value,) + earlier)[0]


def on_device(
    hidden,
    teacher,
    valid_mask,
    prefix_len,
    ln1_gain,
    ln1_bias,
    ln2_gain,
    ln2_bias,
    qkv_weight,
    qkv_bias,
    out_weight,
    out_bias,
    fc1_weight,
    fc1_bias,
    fc2_weight,
    fc2_bias,
):
    rows = hidden.shape[0]
    dp = lax.axis_size("dp")
    tp = lax.axis_size("tensor")
    ways = tp // 2
    squares = dp // 4
    total_tokens = dp * tp * rows
    heads = qkv_weight.shape[1] // (3 * HD)
    dp_index = lax.axis_index("dp")
    tp_index = lax.axis_index("tensor")
    core, y = tp_index % 2, tp_index // 2
    quarter = dp_index % 4

    def to_core(v):
        return lax.ppermute(v, "tensor", [(t, t ^ 1) for t in range(tp)])

    def from_y(v, step):
        pairs = [(t, ((t // 2 - step) % ways) * 2 + t % 2) for t in range(tp)]
        return lax.ppermute(v, "tensor", pairs)

    def to_y(v, step):
        pairs = [(t, ((t // 2 + step) % ways) * 2 + t % 2) for t in range(tp)]
        return lax.ppermute(v, "tensor", pairs)

    def flip(v, mask):
        return lax.ppermute(v, "dp", [(d, d ^ mask) for d in range(dp)])

    def tensor_sum(v):
        v = v + to_core(v)
        bit = 2
        while bit < tp:
            v = v + lax.ppermute(v, "tensor", [(t, t ^ bit) for t in range(tp)])
            bit *= 2
        return v

    def dp_sum(v):
        bit = 1
        while bit < dp:
            v = v + flip(v, bit)
            bit *= 2
        return v

    block_ids = [
        ((y + step) % ways) * 2 + (core if mate == 0 else 1 - core)
        for step in range(ways)
        for mate in (0, 1)
    ]

    def gather_near(own):
        parts, over_y = [own, to_core(own)], []
        for step in range(1, ways):
            over_y.append(from_y(own, step))
            parts += [over_y[-1], to_core(over_y[-1])]
        return jnp.concatenate(parts, axis=0), over_y

    def gather_far(own, over_y):
        first = [flip(own, 1), flip(own, 2)]
        first.append(flip(first[1], 1))
        rounds_y = [first]
        for step in range(1, ways):
            rounds_y.append(
                [from_y(first[0], step), flip(over_y[step - 1], 2), from_y(first[2], step)]
            )
        parts = [[], [], []]
        for blocks in rounds_y:
            mates = to_core(jnp.concatenate(blocks, axis=0))
            for i in range(3):
                parts[i] += [blocks[i], lax.slice_in_dim(mates, i * rows, (i + 1) * rows, axis=0)]
        return jnp.concatenate(parts[0] + parts[1] + parts[2], axis=0)

    def quarter_of(v, axis, index):
        size = v.shape[axis] // 4
        return lax.dynamic_slice_in_dim(v, index * size, size, axis)

    def swap_quarters(v):
        return [flip(quarter_of(v, 1, quarter ^ mask), mask) for mask in (1, 2, 3)]

    gain_attn = ln1_gain.astype(F32)
    shift_attn = ln1_bias.astype(F32)
    gain_mlp = ln2_gain.astype(F32)
    shift_mlp = ln2_bias.astype(F32)
    mask_f = valid_mask.astype(F32)
    count_all = dp_sum(tensor_sum(jnp.full((8, 128), jnp.sum(mask_f), F32)))[0, 0]

    def normalize(features):
        average = jnp.mean(features, axis=-1, keepdims=True)
        centered = features - average
        spread = jnp.mean(centered * centered, axis=-1, keepdims=True)
        inverse = lax.rsqrt(spread + EPSILON)
        return centered * inverse, inverse

    hidden_near, hidden_y = gather_near(hidden)
    hidden_far = gather_far(hidden, hidden_y)
    xhat, inverse = normalize(hidden_near.astype(F32))
    norm_attn = (xhat * gain_attn + shift_attn).astype(BF)
    norm_mlp = (xhat * gain_mlp + shift_mlp).astype(BF)
    qkv_all = jnp.dot(norm_attn, qkv_weight, preferred_element_type=F32) + qkv_bias.astype(F32)

    cosine_all, sine_all = rotary_tables(LEN, ROT)

    def in_order(table):
        return jnp.concatenate(
            [lax.dynamic_slice_in_dim(table, b * rows, rows, 0) for b in block_ids], axis=0
        )

    cosine_table = in_order(cosine_all)[:, None, :]
    sine_table = in_order(sine_all)[:, None, :]
    spots = jnp.concatenate([b * rows + jnp.arange(rows, dtype=jnp.int32) for b in block_ids])
    scale_factor = HD ** (-0.5)
    visible = (spots[None, :] <= spots[:, None]) | (spots[None, :] < prefix_len[0])

    split_qkv = qkv_all.reshape(LEN, heads, 3, HD)
    queries = rotate_block(split_qkv[:, :, 0], cosine_table, sine_table).astype(BF)
    keys_rot = rotate_block(split_qkv[:, :, 1], cosine_table, sine_table).astype(BF)
    values = split_qkv[:, :, 2].astype(BF)

    def masked_scores(rotated):
        scores = (
            jnp.einsum("qhd,khd->hqk", rotated, keys_rot, preferred_element_type=F32)
            * scale_factor
        )
        return jnp.where(visible[None], scores, -jnp.inf)

    scores = masked_scores(queries)
    top_score = jnp.max(scores, axis=-1, keepdims=True)
    log_total = top_score + jnp.log(jnp.sum(jnp.exp(scores - top_score), axis=-1, keepdims=True))
    attention_low = jnp.exp(scores - log_total).astype(BF)
    context = (
        jnp.einsum("hqk,khd->qhd", attention_low, values, preferred_element_type=F32)
        .astype(BF)
        .reshape(LEN, heads * HD)
    )
    hidden_pre = jnp.dot(norm_mlp, fc1_weight, preferred_element_type=F32) + fc1_bias.astype(F32)
    active, slope = exact_gelu(hidden_pre)
    active = active.astype(BF)
    branch_part = jnp.dot(context, out_weight, preferred_element_type=F32) + jnp.dot(
        active, fc2_weight, preferred_element_type=F32
    )

    def scatter_rows(part):
        blocks = part.reshape(ways, 2, rows, D)
        mine = blocks[:, 0] + to_core(blocks[:, 1].astype(BF)).astype(F32)
        total = mine[0]
        for step in range(1, ways):
            total = total + to_y(mine[step].astype(BF), step).astype(F32)
        return total

    branch = scatter_rows(branch_part)
    output_f = hidden.astype(F32) + branch + out_bias.astype(F32) + fc2_bias.astype(F32)
    mismatch = output_f - teacher.astype(F32)
    error_part = jnp.sum(mask_f[:, None] * mismatch * mismatch)
    grad_out = mask_f[:, None] * mismatch * (2.0 * total_tokens / count_all)
    bias_part = jnp.sum(grad_out, axis=0)
    grad_low = grad_out.astype(BF)
    grad_near, grad_y = gather_near(grad_low)
    grad_far = gather_far(grad_low, grad_y)

    xhat_far, _ = normalize(after(hidden_far, branch_part).astype(F32))
    norm_attn_far = (xhat_far * gain_attn + shift_attn).astype(BF)
    norm_mlp_far = (xhat_far * gain_mlp + shift_mlp).astype(BF)
    fc1_quarter = quarter_of(fc1_weight, 1, quarter)
    fc2_quarter = quarter_of(fc2_weight, 0, quarter)
    pre_far = jnp.dot(
        after(norm_mlp_far, grad_low), fc1_quarter, preferred_element_type=F32
    ) + quarter_of(fc1_bias, 0, quarter).astype(F32)
    active_far, slope_far = exact_gelu(pre_far)
    active_far = active_far.astype(BF)
    context_far = jnp.concatenate(swap_quarters(context), axis=0)

    queue = []
    due = {}
    clock = [0]
    results = {}
    token = [grad_near]

    def gate(v):
        return after(v, token[0])

    def travel(name, low):
        mask = 4
        while mask < dp:
            (got,) = yield [(low, mask)], 2
            low = (low.astype(F32) + got.astype(F32)).astype(BF)
            mask *= 2
        beside, across = yield [(low, 1), (low, 2)], 1
        (corner,) = yield [(across, 1)], 1
        results.setdefault(name, []).append((low, beside, across, corner))

    def enqueue(name, part, count):
        size = part.shape[0] // count
        for i in range(count):
            queue.append((name, lax.slice_in_dim(part, i * size, (i + 1) * size, axis=0)))

    def turn(*others):
        now = clock[0]
        clock[0] = now + 1
        arrived = due.pop(now, [])
        values = [got for _, gots in arrived for got in gots]
        if queue:
            name, held = queue.pop(0)
            values.append(held.astype(BF))
        tied = list(lax.optimization_barrier(tuple(values) + others))
        token[0] = tied[0]
        asked = []
        for walker, gots in arrived:
            gots = [tied.pop(0) for _ in gots]
            try:
                asked.append((walker, walker.send(gots)))
            except StopIteration:
                pass
        if len(values) > sum(len(gots) for _, gots in arrived):
            walker = travel(name, tied.pop(0))
            asked.append((walker, next(walker)))
        for walker, (sends, wait) in asked:
            due.setdefault(now + wait, []).append((walker, [flip(v, mask) for v, mask in sends]))
        return tied

    def joined(name, axis):
        pieces = [jnp.concatenate(piece, axis=0) for piece in zip(*results[name])]
        odd, high = quarter % 2 == 1, quarter >= 2
        a, b = jnp.where(odd, pieces[1], pieces[0]), jnp.where(odd, pieces[0], pieces[1])
        c, d = jnp.where(odd, pieces[3], pieces[2]), jnp.where(odd, pieces[2], pieces[3])
        order = [
            jnp.where(high, c, a),
            jnp.where(high, d, b),
            jnp.where(high, a, c),
            jnp.where(high, b, d),
        ]
        return jnp.concatenate([v.astype(F32) for v in order], axis=axis)

    grad_context = contract(grad_near, out_weight, 1, 1).astype(BF).reshape(LEN, heads, HD)
    grad_inner = (contract(grad_near, fc2_weight, 1, 1) * slope).astype(BF)
    attention = jnp.exp(masked_scores(queries) - log_total)
    grad_attention = jnp.einsum("qhd,khd->hqk", grad_context, values, preferred_element_type=F32)
    row_dots = jnp.sum(attention * grad_attention, axis=-1, keepdims=True)
    grad_scores = (attention * (grad_attention - row_dots)).astype(BF)
    attention_low = attention.astype(BF)
    fc2_part = contract(quarter_of(active, 1, quarter), grad_near, 0, 0) + contract(
        active_far, grad_far, 0, 0
    )
    enqueue("fc2", fc2_part, 4)
    grad_inner, grad_scores, attention_low = turn(grad_inner, grad_scores, attention_low)

    out_part = contract(quarter_of(context, 1, quarter), gate(grad_near), 0, 0) + contract(
        context_far, grad_far, 0, 0
    )
    enqueue("out", out_part, 1)
    grad_queries = (
        jnp.einsum("hqk,khd->qhd", grad_scores, keys_rot, preferred_element_type=F32)
        * scale_factor
    )
    grad_keys = (
        jnp.einsum("hqk,qhd->khd", grad_scores, queries, preferred_element_type=F32)
        * scale_factor
    )
    grad_values = jnp.einsum(
        "hqk,qhd->khd", attention_low, grad_context, preferred_element_type=F32
    )
    grad_qkv = (
        jnp.stack(
            [
                rotate_block(grad_queries, cosine_table, -sine_table),
                rotate_block(grad_keys, cosine_table, -sine_table),
                grad_values,
            ],
            axis=2,
        )
        .reshape(LEN, heads * 3 * HD)
        .astype(BF)
    )
    (grad_qkv,) = turn(grad_qkv)
    grad_qkv_far = jnp.concatenate(swap_quarters(grad_qkv), axis=0)
    grad_inner_far = (contract(gate(grad_far), fc2_quarter, 1, 1) * slope_far).astype(BF)
    (grad_inner_far,) = turn(grad_inner_far)
    fc1_part = contract(norm_mlp, gate(quarter_of(grad_inner, 1, quarter)), 0, 0) + contract(
        norm_mlp_far, grad_inner_far, 0, 0
    )
    enqueue("fc1", fc1_part, 4)
    (grad_qkv_far,) = turn(grad_qkv_far)
    qkv_part = contract(norm_attn, gate(quarter_of(grad_qkv, 1, quarter)), 0, 0) + contract(
        norm_attn_far, grad_qkv_far, 0, 0
    )
    (qkv_part,) = turn(qkv_part)
    enqueue("qkv", qkv_part, 4)
    grad_norm_mlp = contract(gate(grad_inner), fc1_weight, 1, 1)
    (grad_norm_mlp,) = turn(grad_norm_mlp)
    grad_norm_attn = contract(gate(grad_qkv), qkv_weight, 1, 1)
    (grad_norm_attn,) = turn(grad_norm_attn)

    def norm_back(gained):
        return inverse * (
            gained
            - jnp.mean(gained, axis=-1, keepdims=True)
            - xhat * jnp.mean(gained * xhat, axis=-1, keepdims=True)
        )

    xhat = gate(xhat)
    grad_hidden = norm_back(grad_norm_attn * gain_attn + grad_norm_mlp * gain_mlp)
    tensor_parts = jnp.stack(
        [
            jnp.sum(grad_norm_attn * xhat, axis=0),
            jnp.sum(grad_norm_attn, axis=0),
            jnp.sum(grad_norm_mlp * xhat, axis=0),
            jnp.sum(grad_norm_mlp, axis=0),
            bias_part,
            jnp.full((D,), error_part, F32),
        ]
    ).reshape(-1)
    fc1_bias_part = jnp.sum(grad_inner, axis=0, dtype=F32)
    qkv_bias_part = jnp.sum(grad_qkv, axis=0, dtype=F32)
    grad_hidden, tensor_parts = turn(grad_hidden, tensor_parts)
    input_grad = grad_out + scatter_rows(grad_hidden)
    (input_grad,) = turn(input_grad)
    small = jnp.concatenate([tensor_sum(tensor_parts), fc1_bias_part, qkv_bias_part])
    small = dp_sum(small)
    (small,) = turn(small)
    vectors = small[: 6 * D].reshape(6, D)
    fc1_bias_grad = small[6 * D : 6 * D + fc1_bias_part.shape[0]]
    qkv_bias_grad = small[6 * D + fc1_bias_part.shape[0] :]
    loss_value = vectors[5, 0] / (count_all * D)
    turn()
    turn()
    fc2_weight_grad = joined("fc2", 0)
    out_weight_grad = joined("out", 0)
    fc2_weight_grad, out_weight_grad = turn(fc2_weight_grad, out_weight_grad)
    while queue or due:
        turn()
    fc1_weight_grad = joined("fc1", 1)
    qkv_weight_grad = joined("qkv", 1)
    return (
        output_f.astype(BF),
        loss_value,
        input_grad,
        vectors[0],
        vectors[1],
        vectors[2],
        vectors[3],
        qkv_weight_grad,
        qkv_bias_grad,
        out_weight_grad,
        vectors[4],
        fc1_weight_grad,
        fc1_bias_grad,
        fc2_weight_grad,
        vectors[4],
    )


def solution(mesh):
    tokens = P(("dp", "tensor"), None)
    columns, lanes, down, whole = P(None, "tensor"), P("tensor"), P("tensor", None), P()
    in_specs = (
        tokens,
        tokens,
        P(("dp", "tensor")),
        P("dp"),
        whole,
        whole,
        whole,
        whole,
        columns,
        lanes,
        down,
        whole,
        columns,
        lanes,
        down,
        whole,
    )
    out_specs = (
        tokens,
        whole,
        tokens,
        whole,
        whole,
        whole,
        whole,
        columns,
        lanes,
        down,
        whole,
        columns,
        lanes,
        down,
        whole,
    )
    return jax.shard_map(
        on_device, mesh=mesh, in_specs=in_specs, out_specs=out_specs, check_vma=False
    )
```

time: 957 us -> 890 us (0.930)
  waiting for transfers between devices: 377 us -> 262 us
  local copies, waits for them, and re-layouts: 83.9 us -> 133 us
  other arithmetic: 130 us -> 165 us
  starting transfers between devices: 117 us -> 94.1 us
  matrix products: 231 us -> 219 us
    ppermute x62 -> x72, waiting for transfers between devices: 294 us -> 164 us  [flip(): return lax.ppermute(v, 'dp', [(d, d ^ mask) for d in range(dp)])]
    unnamed x203 -> x281, local copies, waits for them, and re-layouts: 36.5 us -> 75.6 us
    ppermute x4 -> x6, waiting for transfers between devices: 59.8 us -> 31.8 us  [from_y(): return lax.ppermute(v, 'tensor', pairs)]
    ppermute x62 -> x72, starting transfers between devices: 103 us -> 77.2 us  [flip(): return lax.ppermute(v, 'dp', [(d, d ^ mask) for d in range(dp)])]
    ppermute x2, waiting for transfers between devices: 0.01 us -> 21.3 us  [to_y(): return lax.ppermute(v, 'tensor', pairs)]
    ppermute x2, waiting for transfers between devices: 23.2 us -> 42.5 us  [tensor_sum(): v = v + lax.ppermute(v, 'tensor', [(t, t ^ bit) for t in range(tp)])]
    select_n x17 -> x9, other arithmetic: 19.5 us -> 36.8 us  [the longest x4 15.1 us: joined(): jnp.where(high, c, a)]
    sub x0 -> x1, matrix products: none -> 17.3 us  [on_device(): grad_scores = (attention * (grad_attention - row_dots)).astype(BF)]
  transfers between devices with their start and end apart: 82 -> 94, of which waited for: 32 -> 35; matrix products, arithmetic and copies ran while one was open for 44% -> 54% of each run, Pallas kernels for 0% -> 0%
where the time goes in v2:
time: 890 us; the launch traced here: 879 us
  waiting for transfers between devices  262 us (29%)
  matrix products  219 us (25%)
  other arithmetic  165 us (19%)
  local copies, waits for them, and re-layouts  133 us (15%)
  starting transfers between devices  94.1 us (11%)
    ppermute x72, waiting for transfers between devices, flip(): return lax.ppermute(v, 'dp', [(d, d ^ mask) for d in range(dp)])  164 us
    dot_general x13, matrix products, contract(): lax.dot_general(left_side, right_side, (((left_dim,), (right_dim,)), ((),...  128 us
    ppermute x72, starting transfers between devices, flip(): return lax.ppermute(v, 'dp', [(d, d ^ mask) for d in range(dp)])  77.2 us
    unnamed x281, local copies, waits for them, and re-layouts  75.6 us
    ppermute x2, waiting for transfers between devices, tensor_sum(): v = v + lax.ppermute(v, 'tensor', [(t, t ^ bit) for t in range(tp)])  42.5 us
    ppermute x6, waiting for transfers between devices, from_y(): return lax.ppermute(v, 'tensor', pairs)  31.8 us
    ppermute x2, waiting for transfers between devices, to_y(): return lax.ppermute(v, 'tensor', pairs)  21.3 us
    concatenate x4, other arithmetic, joined(): return jnp.concatenate([v.astype(F32) for v in order], axis=axis)  21 us
  transfers between devices with their start and end apart: 94, of which 35 were waited for; matrix products, arithmetic and copies ran while one was open for 54% of the time, Pallas kernels for 0%

profile of v2, /device:TPU:0, one launch (start us, length us, event | category | flops | bytes accessed | tf_op | source)
XLA Modules:
  0.0 878.9 jit_solution(4544535854912620552)
XLA Ops:
  7.3 19.8 %collective-permute-done.1 = bf16[256,2048]{1,0:T(8,128)(2,1)} collective-permute-done((bf16[256,2048]{1,0:T(8,128)(2,1)}, bf16[256,2048]{1,0:T(8,128)(2,1)}, u32[]{:S(2)}, u32[]{:S(2)}) %collective-permute-start.1) | collective-permute-done | bytes 1048608 | tf_op jit(solution)/shard_map/ppermute | solution.py:90
  45.1 14.0 %convolution_add_fusion = f32[1024,1536]{1,0:T(8,128)} fusion(bf16[2048,1536]{1,0:T(8,128)(2,1)} %param.24, f32[1536]{0:T(1024)S(1)} %copy-done.98, f32[2048]{0:T(1024)S(1)} %copy-done.95, f32[2048]{0:T(1024)S(1)} %convert_element_type.282, f32[1024]{0:T(1024)S(1)} %add_rsqrt_fusion.1, f32[1024]{0:T(1024)S(1)} %broadcast_multiply_fusion.3, ...), kind=kOutput, calls=%fused_computation.56 | convolution fusion | flops 6471286784 | bytes 16807936 | tf_op jit(solution)/shard_map/dot_general | solution.py:168
  59.1 6.5 copy.69
  65.6 4.8 fusion.95
  81.2 3.6 subtract_convert_fusion.3
  94.1 3.1 convolution_convert_fusion.1
  97.2 18.7 %multiply_convert_fusion.1 = (bf16[1024,2048]{1,0:T(8,128)(2,1)S(1)}, f32[1024,2048]{1,0:T(8,128)}) fusion(f32[2048]{0:T(1024)S(1)} %copy-done.97, bf16[2048,2048]{1,0:T(8,128)(2,1)} %param.28, f32[2048]{0:T(1024)S(1)} %copy-done.91, f32[2048]{0:T(1024)S(1)} %convert_element_type.290, f32[1024]{0:T(1024)S(1)} %add_rsqrt_fusion.1, ...), kind=kOutput, calls=%fused_computation.37 | convolution fusion | flops 8629780480 | bytes 25198592 | tf_op jit(solution)/shard_map/dot_general | solution.py:204
  116.0 8.8 %fusion.100 = f32[1024,2048]{1,0:T(8,128)S(1)} fusion(bf16[1024,2048]{1,0:T(8,128)(2,1)S(1)} %get-tuple-element.263, bf16[2048,2048]{1,0:T(8,128)(2,1)S(1)} %bitcast.131), kind=kOutput, calls=%fused_computation.307 | convolution fusion | flops 8589934592 | bytes 20971520 | tf_op jit(solution)/shard_map/dot_general | solution.py:207
  127.5 3.4 copy-done.2
  141.0 41.1 %collective-permute-done.6 = f32[8,128]{1,0:T(8,128)S(1)} collective-permute-done((f32[8,128]{1,0:T(8,128)S(1)}, f32[8,128]{1,0:T(8,128)S(1)}, u32[]{:S(2)}, u32[]{:S(2)}) %collective-permute-start.6) | collective-permute-done | bytes 4128 | tf_op jit(solution)/shard_map/ppermute | solution.py:103
  186.9 3.1 collective-permute-done.8
  209.7 9.2 %fusion.12 = f32[1024,2048]{1,0:T(8,128)} fusion(f32[1024]{0:T(1024)S(1)} %add_rsqrt_fusion.1, f32[1024]{0:T(1024)S(1)} %broadcast_multiply_fusion.3, bf16[256,2048]{1,0:T(8,128)(2,1)} %collective-permute-done.2, bf16[256,2048]{1,0:T(8,128)(2,1)} %collective-permute-done.1, bf16[256,2048]{1,0:T(8,128)(2,1)} %collective-permute-done, ...), kind=kLoop, calls=%fused_computation.16 | loop fusion | flops 20971520 | bytes 12591104 | tf_op jit(solution)/shard_map/mul | solution.py:161
  218.8 10.6 %collective-permute-done.4 = bf16[256,2048]{1,0:T(8,128)(2,1)S(1)} collective-permute-done((bf16[256,2048]{1,0:T(8,128)(2,1)S(1)}, bf16[256,2048]{1,0:T(8,128)(2,1)S(1)}, u32[]{:S(2)}, u32[]{:S(2)}) %collective-permute-start.4) | collective-permute-done | bytes 1048608 | tf_op jit(solution)/shard_map/ppermute | solution.py:94
  254.1 6.3 convert_reduce_fusion
  260.4 8.0 fusion.9
  268.4 8.5 fusion.6
  277.5 11.4 %fusion.51 = f32[3072,512]{1,0:T(8,128)} fusion(bf16[3072,2048]{1,0:T(8,128)(2,1)S(1)} %fusion.6, bf16[2048,2048]{1,0:T(8,128)(2,1)} %param.28, s32[]{:T(128)S(6)} %select_n.251), kind=kOutput, calls=%fused_computation.109 | convolution fusion | flops 6442450944 | bytes 20971524 | tf_op jit(solution)/shard_map/dot_general | solution.py:234
  294.8 4.6 convolution_convert_fusion.2
  300.4 6.5 fusion.73
  306.9 17.3 %multiply_convert_fusion = bf16[2,1024,1024]{1,2,0:T(8,128)(2,1)} fusion(f32[2,1024,1024]{1,2,0:T(8,128)} %fusion.73, f32[2,1024]{1,0:T(2,128)S(1)} %log_add_fusion, pred[1024,1024]{0,1:T(8,128)(4,1)S(1)} %copy-done.19, bf16[1024,2,192]{2,0,1:T(8,128)(2,1)} %copy-done.43, bf16[1024,2,32]{2,0,1:T(8,128)(2,1)} %copy-done.51, ...), kind=kOutput, calls=%fused_computation.34 | convolution fusion | flops 2181041152 | bytes 15736832 | tf_op jit(solution)/shard_map/sub | solution.py:307
  328.1 6.6 fusion.63
  334.7 3.6 pad_maximum_fusion.1
  340.3 12.0 %collective-permute-done.27 = bf16[256,2048]{1,0:T(8,128)(2,1)S(1)} collective-permute-done((bf16[256,2048]{1,0:T(8,128)(2,1)}, bf16[256,2048]{1,0:T(8,128)(2,1)S(1)}, u32[]{:S(2)}, u32[]{:S(2)}) %collective-permute-start.27) | collective-permute-done | bytes 1048608 | tf_op jit(solution)/shard_map/ppermute | solution.py:90
  355.3 19.3 %fusion.20 = bf16[1024,2048]{1,0:T(8,128)(2,1)} fusion(f32[1024,2048]{1,0:T(8,128)} %get-tuple-element.264, bf16[2048,2048]{1,0:T(8,128)(2,1)} %param.30, f32[2048]{0:T(1024)S(1)} %copy-done.97, bf16[256,2048]{1,0:T(8,128)(2,1)S(1)} %copy-done.49, bf16[256,2048]{1,0:T(8,128)(2,1)} %collective-permute-done.11, ...), kind=kOutput, calls=%fused_computation.25 | convolution fusion | flops 8629780480 | bytes 25174016 | tf_op jit(solution)/shard_map/dot_general | solution.py:37
  398.4 12.3 %add_convert_fusion.3 = bf16[512,2048]{1,0:T(8,128)(2,1)S(1)} fusion(f32[512,2048]{1,0:T(8,128)S(1)} %copy-done.103, bf16[3072,2048]{1,0:T(8,128)(2,1)} %slice_dynamic-update-slice_fusion, f32[3072,512]{1,0:T(8,128)S(1)} %bitcast.133, f32[512]{0:T(512)S(1)} %dynamic-slice_convert_fusion), kind=kOutput, calls=%fused_computation.66 | convolution fusion | flops 6453985280 | bytes 25167872 | tf_op jit(solution)/shard_map/dot_general | solution.py:37
  423.6 4.7 copy.89
  431.2 15.2 %fusion.28 = bf16[3072,512]{1,0:T(8,128)(2,1)} fusion(f32[3072,512]{1,0:T(8,128)} %fusion.51, bf16[3072,2048]{1,0:T(8,128)(2,1)} %slice_dynamic-update-slice_fusion, f32[512]{0:T(512)S(1)} %dynamic-slice_convert_fusion, bf16[2048,2048]{1,0:T(8,128)(2,1)} %param.30, s32[]{:T(128)S(6)} %select_n.251), kind=kOutput, calls=%fused_computation.50 | convolution fusion | flops 6459752448 | bytes 24119300 | tf_op jit(solution)/shard_map/dot_general | solution.py:37
  453.1 8.2 fusion.40
  463.0 14.4 %collective-permute-done.30 = bf16[128,2048]{1,0:T(8,128)(2,1)S(1)} collective-permute-done((bf16[128,2048]{1,0:T(8,128)(2,1)S(1)}, bf16[128,2048]{1,0:T(8,128)(2,1)S(1)}, u32[]{:S(2)}, u32[]{:S(2)}) %collective-permute-start.30) | collective-permute-done | bytes 524320 | tf_op jit(solution)/shard_map/ppermute | solution.py:97
  477.4 10.7 %fusion.101 = f32[2048,512]{1,0:T(8,128)} fusion(bf16[3072,2048]{1,0:T(8,128)(2,1)S(1)} %bitcast.122, bf16[3072,512]{1,0:T(8,128)(2,1)} %fusion.28), kind=kOutput, calls=%fused_computation.308 | convolution fusion | flops 6442450944 | bytes 19922944 | tf_op jit(solution)/shard_map/dot_general | solution.py:37
  488.4 5.4 add_convert_fusion.2
  495.8 13.4 %collective-permute-done.34 = bf16[1024,384]{0,1:T(8,128)(2,1)S(1)} collective-permute-done((bf16[1024,384]{0,1:T(8,128)(2,1)S(1)}, bf16[1024,384]{0,1:T(8,128)(2,1)S(1)}, u32[]{:S(2)}, u32[]{:S(2)}) %collective-permute-start.34) | collective-permute-done | bytes 786464 | tf_op jit(solution)/shard_map/ppermute | solution.py:97
  509.4 10.1 %collective-permute-done.32 = bf16[128,2048]{1,0:T(8,128)(2,1)S(1)} collective-permute-done((bf16[128,2048]{1,0:T(8,128)(2,1)S(1)}, bf16[128,2048]{1,0:T(8,128)(2,1)S(1)}, u32[]{:S(2)}, u32[]{:S(2)}) %collective-permute-start.32) | collective-permute-done | bytes 524320 | tf_op jit(solution)/shard_map/ppermute | solution.py:97
  524.2 14.2 %fusion.10 = f32[2048,384]{1,0:T(8,128)} fusion(bf16[3072,384]{0,1:T(8,128)(2,1)S(1)} %pad_maximum_fusion.7, bf16[3072,2048]{1,0:T(8,128)(2,1)} %slice_dynamic-update-slice_fusion.6, f32[2048]{0:T(1024)S(1)} %copy-done.96, f32[2048]{0:T(1024)S(1)} %copy-done.89, f32[3072]{0:T(1024)S(1)} %copy-done.81, f32[3072]{0:T(1024)S(1)} %copy-done.78), kind=kOutput, calls=%fused_computation.13 | convolution fusion | flops 4869586944 | bytes 18128896 | tf_op jit(solution)/shard_map/dot_general | solution.py:37
  540.9 5.3 fusion.57
  547.8 4.6 collective-permute-done.40
  558.6 13.5 %fusion.102 = f32[1024,2048]{1,0:T(8,128)} fusion(bf16[1024,2048]{1,0:T(8,128)(2,1)S(1)} %copy-done.20, bf16[2048,2048]{1,0:T(8,128)(2,1)} %param.28), kind=kOutput, calls=%fused_computation.309 | convolution fusion | flops 8589934592 | bytes 20971520 | tf_op jit(solution)/shard_map/dot_general | solution.py:37
  584.4 10.9 %fusion.103 = f32[1024,2048]{1,0:T(8,128)} fusion(bf16[1024,1536]{0,1:T(8,128)(2,1)S(1)} %bitcast.109, bf16[2048,1536]{1,0:T(8,128)(2,1)} %param.24), kind=kOutput, calls=%fused_computation.310 | convolution fusion | flops 6442450944 | bytes 17825792 | tf_op jit(solution)/shard_map/dot_general | solution.py:37
  595.4 7.4 collective-permute-done.50
  606.1 8.9 %fusion.94 = (f32[2048]{0:T(1024)}, f32[2048]{0:T(1024)}, f32[2048]{0:T(1024)}, f32[2048]{0:T(1024)}, f32[1024]{0:T(1024)S(1)}, /*index=5*/f32[1024]{0:T(1024)S(1)}, f32[1024,2048]{1,0:T(8,128)S(1)}) fusion(f32[1024,2048]{1,0:T(8,128)} %fusion.102, f32[1024,2048]{1,0:T(8,128)S(1)} %bitcast.101, f32[1024,2048]{1,0:T(8,128)} %fusion.103, ...), kind=kLoop, calls=%fused_computation.301 | loop fusion | flops 25155584 | bytes 33611776 | tf_op jit(solution)/shard_map/reduce_sum | solution.py:375
  617.9 4.6 subtract_multiply_fusion
  642.4 3.9 broadcast_select_fusion.15
  646.3 4.4 collective-permute-done.67
  658.3 6.5 maximum_convert_fusion
  666.5 10.7 %collective-permute-done.61 = bf16[256,2048]{1,0:T(8,128)(2,1)S(1)} collective-permute-done((bf16[256,2048]{1,0:T(8,128)(2,1)S(1)}, bf16[256,2048]{1,0:T(8,128)(2,1)S(1)}, u32[]{:S(2)}, u32[]{:S(2)}) %collective-permute-start.61) | collective-permute-done | bytes 1048608 | tf_op jit(solution)/shard_map/ppermute | solution.py:94
  679.6 9.2 %collective-permute-done.59 = bf16[128,2048]{1,0:T(8,128)(2,1)S(1)} collective-permute-done((bf16[128,2048]{1,0:T(8,128)(2,1)}, bf16[128,2048]{1,0:T(8,128)(2,1)S(1)}, u32[]{:S(2)}, u32[]{:S(2)}) %collective-permute-start.59) | collective-permute-done | bytes 524320 | tf_op jit(solution)/shard_map/ppermute | solution.py:97
  696.8 12.7 %collective-permute-done.63 = bf16[512,512]{1,0:T(8,128)(2,1)S(1)} collective-permute-done((bf16[512,512]{1,0:T(8,128)(2,1)S(1)}, bf16[512,512]{1,0:T(8,128)(2,1)S(1)}, u32[]{:S(2)}, u32[]{:S(2)}) %collective-permute-start.63) | collective-permute-done | bytes 524320 | tf_op jit(solution)/shard_map/ppermute | solution.py:97
  721.6 9.4 %collective-permute-done.73 = bf16[512,512]{1,0:T(8,128)(2,1)} collective-permute-done((bf16[512,512]{1,0:T(8,128)(2,1)S(1)}, bf16[512,512]{1,0:T(8,128)(2,1)}, u32[]{:S(2)}, u32[]{:S(2)}) %collective-permute-start.73) | collective-permute-done | bytes 524320 | tf_op jit(solution)/shard_map/ppermute | solution.py:97
  731.0 3.7 collective-permute-done.74
  752.6 9.2 %collective-permute-done.77 = bf16[512,512]{1,0:T(8,128)(2,1)} collective-permute-done((bf16[512,512]{1,0:T(8,128)(2,1)}, bf16[512,512]{1,0:T(8,128)(2,1)}, u32[]{:S(2)}, u32[]{:S(2)}) %collective-permute-start.77) | collective-permute-done | bytes 524320 | tf_op jit(solution)/shard_map/ppermute | solution.py:97
  771.1 12.8 %collective-permute-done.81 = bf16[512,384]{1,0:T(8,128)(2,1)S(1)} collective-permute-done((bf16[512,384]{1,0:T(8,128)(2,1)S(1)}, bf16[512,384]{1,0:T(8,128)(2,1)S(1)}, u32[]{:S(2)}, u32[]{:S(2)}) %collective-permute-start.81) | collective-permute-done | bytes 393248 | tf_op jit(solution)/shard_map/ppermute | solution.py:97
  787.0 3.5 broadcast_select_fusion.7
  792.7 7.4 collective-permute-done.84
  800.1 3.6 collective-permute-done.85
  808.6 6.6 maximum_convert_fusion.1
  818.6 7.2 collective-permute-done.89
  828.6 5.2 collective-permute-done.91
  835.7 4.2 collective-permute-done.92
  840.5 7.2 collective-permute-done.93
  847.7 5.9 broadcast_select_fusion.20
  853.6 6.0 broadcast_select_fusion.21
  859.5 5.9 broadcast_select_fusion.22
  865.5 6.2 broadcast_select_fusion.23
  871.7 5.2 maximum_convert_fusion.2
  (568 shorter events, 301.0 us)
Async XLA Ops:
  0.7 26.5 %collective-permute-start.1 = (bf16[256,2048]{1,0:T(8,128)(2,1)}, bf16[256,2048]{1,0:T(8,128)(2,1)}, u32[]{:S(2)}, u32[]{:S(2)}) collective-permute-start(bf16[256,2048]{1,0:T(8,128)(2,1)} %param.16), channel_id=1, source_target_pairs={{0,2},{1,3},{2,0},{3,1},{4,6},{5,7},{6,4},{7,5},{8,10},{9,11},{10,... | collective-permute-start | bytes 3145736 | tf_op jit(solution)/shard_map/ppermute | solution.py:90
  3.7 36.3 %collective-permute-start = (bf16[256,2048]{1,0:T(8,128)(2,1)}, bf16[256,2048]{1,0:T(8,128)(2,1)}, u32[]{:S(2)}, u32[]{:S(2)}) collective-permute-start(bf16[256,2048]{1,0:T(8,128)(2,1)} %param.16), channel_id=1, source_target_pairs={{0,1},{1,0},{2,3},{3,2},{4,5},{5,4},{6,7},{7,6},{8,9},{9,8},{10,11... | collective-permute-start | bytes 3145736 | tf_op jit(solution)/shard_map/ppermute | solution.py:86
  3.7 34.5 %collective-permute-start.14 = (bf16[256,2048]{1,0:T(8,128)(2,1)}, bf16[256,2048]{1,0:T(8,128)(2,1)}, u32[]{:S(2)}, u32[]{:S(2)}) collective-permute-start(bf16[256,2048]{1,0:T(8,128)(2,1)} %param.16), channel_id=1, source_target_pairs={{0,8},{4,12},{8,0},{12,4},{16,24},{20,28},{24,16},{28,20},{1,9},{5... | collective-permute-start | bytes 3145736 | tf_op jit(solution)/shard_map/ppermute | solution.py:97
  5.3 128.9 %collective-permute-start.13 = (bf16[256,2048]{1,0:T(8,128)(2,1)}, bf16[256,2048]{1,0:T(8,128)(2,1)}, u32[]{:S(2)}, u32[]{:S(2)}) collective-permute-start(bf16[256,2048]{1,0:T(8,128)(2,1)} %param.16), channel_id=1, source_target_pairs={{0,4},{4,0},{8,12},{12,8},{16,20},{20,16},{24,28},{28,24},{1,5},{5... | collective-permute-start | bytes 3145736 | tf_op jit(solution)/shard_map/ppermute | solution.py:97
  38.3 97.5 %collective-permute-start.15 = (bf16[256,2048]{1,0:T(8,128)(2,1)}, bf16[256,2048]{1,0:T(8,128)(2,1)}, u32[]{:S(2)}, u32[]{:S(2)}) collective-permute-start(bf16[256,2048]{1,0:T(8,128)(2,1)} %collective-permute-done.14), channel_id=1, source_target_pairs={{0,4},{4,0},{8,12},{12,8},{16,20},{20,16},{24,28},{28,24},{1,5},{5... | collective-permute-start | bytes 3145736 | tf_op jit(solution)/shard_map/ppermute | solution.py:97
  132.4 68.9 %collective-permute-start.3 = (bf16[2,256,2048]{2,1,0:T(8,128)(2,1)}, bf16[2,256,2048]{2,1,0:T(8,128)(2,1)}, u32[]{:S(2)}, u32[]{:S(2)}) collective-permute-start(bf16[2,256,2048]{2,1,0:T(8,128)(2,1)} %fusion.42), channel_id=1, source_target_pairs={{0,1},{1,0},{2,3},{3,2},{4,5},{5,4},{6,7},{7,6},{8,9},{9,8},{10,11... | collective-permute-start | bytes 6291464 | tf_op jit(solution)/shard_map/ppermute | solution.py:86
  132.6 66.0 %collective-permute-start.18 = (bf16[256,2048]{1,0:T(8,128)(2,1)}, bf16[256,2048]{1,0:T(8,128)(2,1)}, u32[]{:S(2)}, u32[]{:S(2)}) collective-permute-start(bf16[256,2048]{1,0:T(8,128)(2,1)} %collective-permute-done.1), channel_id=1, source_target_pairs={{0,8},{4,12},{8,0},{12,4},{16,24},{20,28},{24,16},{28,20},{1,9},{5... | collective-permute-start | bytes 3145736 | tf_op jit(solution)/shard_map/ppermute | solution.py:97
  134.2 64.5 %collective-permute-start.17 = (bf16[256,2048]{1,0:T(8,128)(2,1)}, bf16[256,2048]{1,0:T(8,128)(2,1)}, u32[]{:S(2)}, u32[]{:S(2)}) collective-permute-start(bf16[256,2048]{1,0:T(8,128)(2,1)} %collective-permute-done.13), channel_id=1, source_target_pairs={{0,2},{1,3},{2,0},{3,1},{4,6},{5,7},{6,4},{7,5},{8,10},{9,11},{10,... | collective-permute-start | bytes 3145736 | tf_op jit(solution)/shard_map/ppermute | solution.py:90
  135.7 63.0 %collective-permute-start.19 = (bf16[256,2048]{1,0:T(8,128)(2,1)}, bf16[256,2048]{1,0:T(8,128)(2,1)}, u32[]{:S(2)}, u32[]{:S(2)}) collective-permute-start(bf16[256,2048]{1,0:T(8,128)(2,1)} %collective-permute-done.15), channel_id=1, source_target_pairs={{0,2},{1,3},{2,0},{3,1},{4,6},{5,7},{6,4},{7,5},{8,10},{9,11},{10,... | collective-permute-start | bytes 3145736 | tf_op jit(solution)/shard_map/ppermute | solution.py:90
  139.4 42.7 %collective-permute-start.6 = (f32[8,128]{1,0:T(8,128)S(1)}, f32[8,128]{1,0:T(8,128)S(1)}, u32[]{:S(2)}, u32[]{:S(2)}) collective-permute-start(f32[8,128]{1,0:T(8,128)S(1)} %broadcast_add_fusion), channel_id=1, source_target_pairs={{0,2},{1,3},{2,0},{3,1},{4,6},{5,7},{6,4},{7,5},{8,10},{9,11},{10,... | collective-permute-start | bytes 12296 | tf_op jit(solution)/shard_map/ppermute | solution.py:103
  198.6 35.8 %collective-permute-start.16 = (bf16[768,2048]{1,0:T(8,128)(2,1)S(1)}, bf16[768,2048]{1,0:T(8,128)(2,1)S(1)}, u32[]{:S(2)}, u32[]{:S(2)}) collective-permute-start(bf16[768,2048]{1,0:T(8,128)(2,1)S(1)} %pad_maximum_fusion.2), channel_id=1, source_target_pairs={{0,1},{1,0},{2,3},{3,2},{4,5},{5,4},{6,7},{7,6},{8,9},{9,8},{10,11... | collective-permute-start | bytes 9437192 | tf_op jit(solution)/shard_map/ppermute | solution.py:86
  201.1 38.4 %collective-permute-start.20 = (bf16[768,2048]{1,0:T(8,128)(2,1)S(1)}, bf16[768,2048]{1,0:T(8,128)(2,1)S(1)}, u32[]{:S(2)}, u32[]{:S(2)}) collective-permute-start(bf16[768,2048]{1,0:T(8,128)(2,1)S(1)} %pad_maximum_fusion.3), channel_id=1, source_target_pairs={{0,1},{1,0},{2,3},{3,2},{4,5},{5,4},{6,7},{7,6},{8,9},{9,8},{10,11... | collective-permute-start | bytes 9437192 | tf_op jit(solution)/shard_map/ppermute | solution.py:86
  204.4 25.1 %collective-permute-start.4 = (bf16[256,2048]{1,0:T(8,128)(2,1)S(1)}, bf16[256,2048]{1,0:T(8,128)(2,1)S(1)}, u32[]{:S(2)}, u32[]{:S(2)}) collective-permute-start(bf16[256,2048]{1,0:T(8,128)(2,1)S(1)} %fusion.60), channel_id=1, source_target_pairs={{0,2},{1,3},{2,0},{3,1},{4,6},{5,7},{6,4},{7,5},{8,10},{9,11},{10,... | collective-permute-start | bytes 3145736 | tf_op jit(solution)/shard_map/ppermute | solution.py:94
  209.1 240.5 %collective-permute-start.41 = (bf16[1024,128]{0,1:T(8,128)(2,1)}, bf16[1024,128]{0,1:T(8,128)(2,1)}, u32[]{:S(2)}, u32[]{:S(2)}) collective-permute-start(bf16[1024,128]{0,1:T(8,128)(2,1)} %get-tuple-element.238), channel_id=1, source_target_pairs={{0,4},{4,0},{8,12},{12,8},{16,20},{20,16},{24,28},{28,24},{1,5},{5... | collective-permute-start | bytes 786440 | tf_op jit(solution)/shard_map/ppermute | solution.py:97
  233.6 58.1 %collective-permute-start.22 = (bf16[256,2048]{1,0:T(8,128)(2,1)}, bf16[256,2048]{1,0:T(8,128)(2,1)S(1)}, u32[]{:S(2)}, u32[]{:S(2)}) collective-permute-start(bf16[256,2048]{1,0:T(8,128)(2,1)} %fusion.54), channel_id=1, source_target_pairs={{0,8},{4,12},{8,0},{12,4},{16,24},{20,28},{24,16},{28,20},{1,9},{5... | collective-permute-start | bytes 3145736 | tf_op jit(solution)/shard_map/ppermute | solution.py:97
  234.0 54.9 %collective-permute-start.21 = (bf16[256,2048]{1,0:T(8,128)(2,1)}, bf16[256,2048]{1,0:T(8,128)(2,1)}, u32[]{:S(2)}, u32[]{:S(2)}) collective-permute-start(bf16[256,2048]{1,0:T(8,128)(2,1)} %fusion.54), channel_id=1, source_target_pairs={{0,4},{4,0},{8,12},{12,8},{16,20},{20,16},{24,28},{28,24},{1,5},{5... | collective-permute-start | bytes 3145736 | tf_op jit(solution)/shard_map/ppermute | solution.py:97
  234.4 42.5 %collective-permute-start.11 = (bf16[256,2048]{1,0:T(8,128)(2,1)}, bf16[256,2048]{1,0:T(8,128)(2,1)}, u32[]{:S(2)}, u32[]{:S(2)}) collective-permute-start(bf16[256,2048]{1,0:T(8,128)(2,1)} %fusion.54), channel_id=1, source_target_pairs={{0,2},{1,3},{2,0},{3,1},{4,6},{5,7},{6,4},{7,5},{8,10},{9,11},{10,... | collective-permute-start | bytes 3145736 | tf_op jit(solution)/shard_map/ppermute | solution.py:90
  239.5 53.9 %collective-permute-start.10 = (bf16[256,2048]{1,0:T(8,128)(2,1)}, bf16[256,2048]{1,0:T(8,128)(2,1)}, u32[]{:S(2)}, u32[]{:S(2)}) collective-permute-start(bf16[256,2048]{1,0:T(8,128)(2,1)} %fusion.54), channel_id=1, source_target_pairs={{0,1},{1,0},{2,3},{3,2},{4,5},{5,4},{6,7},{7,6},{8,9},{9,8},{10,11... | collective-permute-start | bytes 3145736 | tf_op jit(solution)/shard_map/ppermute | solution.py:86
  288.9 49.4 %collective-permute-start.25 = (bf16[256,2048]{1,0:T(8,128)(2,1)}, bf16[256,2048]{1,0:T(8,128)(2,1)}, u32[]{:S(2)}, u32[]{:S(2)}) collective-permute-start(bf16[256,2048]{1,0:T(8,128)(2,1)} %collective-permute-done.21), channel_id=1, source_target_pairs={{0,2},{1,3},{2,0},{3,1},{4,6},{5,7},{6,4},{7,5},{8,10},{9,11},{10,... | collective-permute-start | bytes 3145736 | tf_op jit(solution)/shard_map/ppermute | solution.py:90
  291.6 47.0 %collective-permute-start.26 = (bf16[256,2048]{1,0:T(8,128)(2,1)}, bf16[256,2048]{1,0:T(8,128)(2,1)}, u32[]{:S(2)}, u32[]{:S(2)}) collective-permute-start(bf16[256,2048]{1,0:T(8,128)(2,1)} %collective-permute-done.11), channel_id=1, source_target_pairs={{0,8},{4,12},{8,0},{12,4},{16,24},{20,28},{24,16},{28,20},{1,9},{5... | collective-permute-start | bytes 3145736 | tf_op jit(solution)/shard_map/ppermute | solution.py:97
  293.3 30.9 %collective-permute-start.23 = (bf16[256,2048]{1,0:T(8,128)(2,1)S(1)}, bf16[256,2048]{1,0:T(8,128)(2,1)}, u32[]{:S(2)}, u32[]{:S(2)}) collective-permute-start(bf16[256,2048]{1,0:T(8,128)(2,1)S(1)} %collective-permute-done.22), channel_id=1, source_target_pairs={{0,4},{4,0},{8,12},{12,8},{16,20},{20,16},{24,28},{28,24},{1,5},{5... | collective-permute-start | bytes 3145736 | tf_op jit(solution)/shard_map/ppermute | solution.py:97
  326.4 48.3 %collective-permute-start.24 = (bf16[768,2048]{1,0:T(8,128)(2,1)S(1)}, bf16[768,2048]{1,0:T(8,128)(2,1)}, u32[]{:S(2)}, u32[]{:S(2)}) collective-permute-start(bf16[768,2048]{1,0:T(8,128)(2,1)S(1)} %pad_maximum_fusion.4), channel_id=1, source_target_pairs={{0,1},{1,0},{2,3},{3,2},{4,5},{5,4},{6,7},{7,6},{8,9},{9,8},{10,11... | collective-permute-start | bytes 9437192 | tf_op jit(solution)/shard_map/ppermute | solution.py:86
  326.5 25.8 %collective-permute-start.27 = (bf16[256,2048]{1,0:T(8,128)(2,1)}, bf16[256,2048]{1,0:T(8,128)(2,1)S(1)}, u32[]{:S(2)}, u32[]{:S(2)}) collective-permute-start(bf16[256,2048]{1,0:T(8,128)(2,1)} %collective-permute-done.23), channel_id=1, source_target_pairs={{0,2},{1,3},{2,0},{3,1},{4,6},{5,7},{6,4},{7,5},{8,10},{9,11},{10,... | collective-permute-start | bytes 3145736 | tf_op jit(solution)/shard_map/ppermute | solution.py:90
  338.3 111.7 %collective-permute-start.43 = (bf16[1024,128]{0,1:T(8,128)(2,1)}, bf16[1024,128]{0,1:T(8,128)(2,1)}, u32[]{:S(2)}, u32[]{:S(2)}) collective-permute-start(bf16[1024,128]{0,1:T(8,128)(2,1)} %get-tuple-element.239), channel_id=1, source_target_pairs={{0,12},{4,8},{8,4},{12,0},{16,28},{20,24},{24,20},{28,16},{1,13},{... | collective-permute-start | bytes 786440 | tf_op jit(solution)/shard_map/ppermute | solution.py:97
  338.7 113.0 %collective-permute-start.42 = (bf16[1024,128]{0,1:T(8,128)(2,1)S(1)}, bf16[1024,128]{0,1:T(8,128)(2,1)}, u32[]{:S(2)}, u32[]{:S(2)}) collective-permute-start(bf16[1024,128]{0,1:T(8,128)(2,1)S(1)} %get-tuple-element.240), channel_id=1, source_target_pairs={{0,8},{4,12},{8,0},{12,4},{16,24},{20,28},{24,16},{28,20},{1,9},{5... | collective-permute-start | bytes 786440 | tf_op jit(solution)/shard_map/ppermute | solution.py:97
  355.3 24.0 %collective-permute-start.28 = (bf16[768,2048]{1,0:T(8,128)(2,1)}, bf16[768,2048]{1,0:T(8,128)(2,1)}, u32[]{:S(2)}, u32[]{:S(2)}) collective-permute-start(bf16[768,2048]{1,0:T(8,128)(2,1)} %pad_maximum_fusion.5), channel_id=1, source_target_pairs={{0,1},{1,0},{2,3},{3,2},{4,5},{5,4},{6,7},{7,6},{8,9},{9,8},{10,11... | collective-permute-start | bytes 9437192 | tf_op jit(solution)/shard_map/ppermute | solution.py:86
  428.3 81.2 %collective-permute-start.29 = (bf16[128,2048]{1,0:T(8,128)(2,1)}, bf16[128,2048]{1,0:T(8,128)(2,1)}, u32[]{:S(2)}, u32[]{:S(2)}) collective-permute-start(bf16[128,2048]{1,0:T(8,128)(2,1)} %get-tuple-element.107), channel_id=1, source_target_pairs={{0,16},{4,20},{8,24},{12,28},{16,0},{20,4},{24,8},{28,12},{1,17},{... | collective-permute-start | bytes 1572872 | tf_op jit(solution)/shard_map/ppermute | solution.py:97
  430.9 46.5 %collective-permute-start.30 = (bf16[128,2048]{1,0:T(8,128)(2,1)S(1)}, bf16[128,2048]{1,0:T(8,128)(2,1)S(1)}, u32[]{:S(2)}, u32[]{:S(2)}) collective-permute-start(bf16[128,2048]{1,0:T(8,128)(2,1)S(1)} %get-tuple-element.108), channel_id=1, source_target_pairs={{0,16},{4,20},{8,24},{12,28},{16,0},{20,4},{24,8},{28,12},{1,17},{... | collective-permute-start | bytes 1572872 | tf_op jit(solution)/shard_map/ppermute | solution.py:97
  449.6 44.2 %collective-permute-start.35 = (bf16[1024,384]{0,1:T(8,128)(2,1)S(1)}, bf16[1024,384]{0,1:T(8,128)(2,1)S(1)}, u32[]{:S(2)}, u32[]{:S(2)}) collective-permute-start(bf16[1024,384]{0,1:T(8,128)(2,1)S(1)} %get-tuple-element.211), channel_id=1, source_target_pairs={{0,12},{4,8},{8,4},{12,0},{16,28},{20,24},{24,20},{28,16},{1,13},{... | collective-permute-start | bytes 2359304 | tf_op jit(solution)/shard_map/ppermute | solution.py:97
  449.9 59.3 %collective-permute-start.34 = (bf16[1024,384]{0,1:T(8,128)(2,1)S(1)}, bf16[1024,384]{0,1:T(8,128)(2,1)S(1)}, u32[]{:S(2)}, u32[]{:S(2)}) collective-permute-start(bf16[1024,384]{0,1:T(8,128)(2,1)S(1)} %get-tuple-element.212), channel_id=1, source_target_pairs={{0,8},{4,12},{8,0},{12,4},{16,24},{20,28},{24,16},{28,20},{1,9},{5... | collective-permute-start | bytes 2359304 | tf_op jit(solution)/shard_map/ppermute | solution.py:97
  451.7 57.6 %collective-permute-start.33 = (bf16[1024,384]{0,1:T(8,128)(2,1)S(1)}, bf16[1024,384]{0,1:T(8,128)(2,1)S(1)}, u32[]{:S(2)}, u32[]{:S(2)}) collective-permute-start(bf16[1024,384]{0,1:T(8,128)(2,1)S(1)} %get-tuple-element.213), channel_id=1, source_target_pairs={{0,4},{4,0},{8,12},{12,8},{16,20},{20,16},{24,28},{28,24},{1,5},{5... | collective-permute-start | bytes 2359304 | tf_op jit(solution)/shard_map/ppermute | solution.py:97
  488.3 31.2 %collective-permute-start.32 = (bf16[128,2048]{1,0:T(8,128)(2,1)S(1)}, bf16[128,2048]{1,0:T(8,128)(2,1)S(1)}, u32[]{:S(2)}, u32[]{:S(2)}) collective-permute-start(bf16[128,2048]{1,0:T(8,128)(2,1)S(1)} %add_convert_fusion.20), channel_id=1, source_target_pairs={{0,8},{4,12},{8,0},{12,4},{16,24},{20,28},{24,16},{28,20},{1,9},{5... | collective-permute-start | bytes 1572872 | tf_op jit(solution)/shard_map/ppermute | solution.py:97
  493.8 25.7 %collective-permute-start.31 = (bf16[128,2048]{1,0:T(8,128)(2,1)S(1)}, bf16[128,2048]{1,0:T(8,128)(2,1)S(1)}, u32[]{:S(2)}, u32[]{:S(2)}) collective-permute-start(bf16[128,2048]{1,0:T(8,128)(2,1)S(1)} %add_convert_fusion.20), channel_id=1, source_target_pairs={{0,4},{4,0},{8,12},{12,8},{16,20},{20,16},{24,28},{28,24},{1,5},{5... | collective-permute-start | bytes 1572872 | tf_op jit(solution)/shard_map/ppermute | solution.py:97
  509.3 37.8 %collective-permute-start.37 = (bf16[128,2048]{1,0:T(8,128)(2,1)S(1)}, bf16[128,2048]{1,0:T(8,128)(2,1)S(1)}, u32[]{:S(2)}, u32[]{:S(2)}) collective-permute-start(bf16[128,2048]{1,0:T(8,128)(2,1)S(1)} %copy-done.35), channel_id=1, source_target_pairs={{0,16},{4,20},{8,24},{12,28},{16,0},{20,4},{24,8},{28,12},{1,17},{... | collective-permute-start | bytes 1572872 | tf_op jit(solution)/shard_map/ppermute | solution.py:97
  522.5 24.6 %collective-permute-start.39 = (bf16[128,2048]{1,0:T(8,128)(2,1)S(1)}, bf16[128,2048]{1,0:T(8,128)(2,1)S(1)}, u32[]{:S(2)}, u32[]{:S(2)}) collective-permute-start(bf16[128,2048]{1,0:T(8,128)(2,1)S(1)} %add_convert_fusion.19), channel_id=1, source_target_pairs={{0,8},{4,12},{8,0},{12,4},{16,24},{20,28},{24,16},{28,20},{1,9},{5... | collective-permute-start | bytes 1572872 | tf_op jit(solution)/shard_map/ppermute | solution.py:97
  522.6 24.5 %collective-permute-start.38 = (bf16[128,2048]{1,0:T(8,128)(2,1)S(1)}, bf16[128,2048]{1,0:T(8,128)(2,1)}, u32[]{:S(2)}, u32[]{:S(2)}) collective-permute-start(bf16[128,2048]{1,0:T(8,128)(2,1)S(1)} %add_convert_fusion.19), channel_id=1, source_target_pairs={{0,4},{4,0},{8,12},{12,8},{16,20},{20,16},{24,28},{28,24},{1,5},{5... | collective-permute-start | bytes 1572872 | tf_op jit(solution)/shard_map/ppermute | solution.py:97
  538.4 36.8 %collective-permute-start.36 = (bf16[128,2048]{1,0:T(8,128)(2,1)S(1)}, bf16[128,2048]{1,0:T(8,128)(2,1)S(1)}, u32[]{:S(2)}, u32[]{:S(2)}) collective-permute-start(bf16[128,2048]{1,0:T(8,128)(2,1)S(1)} %get-tuple-element.112), channel_id=1, source_target_pairs={{0,16},{4,20},{8,24},{12,28},{16,0},{20,4},{24,8},{28,12},{1,17},{... | collective-permute-start | bytes 1572872 | tf_op jit(solution)/shard_map/ppermute | solution.py:97
  553.6 23.6 %collective-permute-start.45 = (bf16[128,2048]{1,0:T(8,128)(2,1)S(1)}, bf16[128,2048]{1,0:T(8,128)(2,1)}, u32[]{:S(2)}, u32[]{:S(2)}) collective-permute-start(bf16[128,2048]{1,0:T(8,128)(2,1)S(1)} %add_convert_fusion.18), channel_id=1, source_target_pairs={{0,8},{4,12},{8,0},{12,4},{16,24},{20,28},{24,16},{28,20},{1,9},{5... | collective-permute-start | bytes 1572872 | tf_op jit(solution)/shard_map/ppermute | solution.py:97
  554.0 23.2 %collective-permute-start.44 = (bf16[128,2048]{1,0:T(8,128)(2,1)S(1)}, bf16[128,2048]{1,0:T(8,128)(2,1)S(1)}, u32[]{:S(2)}, u32[]{:S(2)}) collective-permute-start(bf16[128,2048]{1,0:T(8,128)(2,1)S(1)} %add_convert_fusion.18), channel_id=1, source_target_pairs={{0,4},{4,0},{8,12},{12,8},{16,20},{20,16},{24,28},{28,24},{1,5},{5... | collective-permute-start | bytes 1572872 | tf_op jit(solution)/shard_map/ppermute | solution.py:97
  554.7 22.5 %collective-permute-start.46 = (bf16[128,2048]{1,0:T(8,128)(2,1)S(1)}, bf16[128,2048]{1,0:T(8,128)(2,1)S(1)}, u32[]{:S(2)}, u32[]{:S(2)}) collective-permute-start(bf16[128,2048]{1,0:T(8,128)(2,1)S(1)} %collective-permute-done.39), channel_id=1, source_target_pairs={{0,4},{4,0},{8,12},{12,8},{16,20},{20,16},{24,28},{28,24},{1,5},{5... | collective-permute-start | bytes 1572872 | tf_op jit(solution)/shard_map/ppermute | solution.py:97
  556.0 39.4 %collective-permute-start.48 = (bf16[128,2048]{1,0:T(8,128)(2,1)S(1)}, bf16[128,2048]{1,0:T(8,128)(2,1)S(1)}, u32[]{:S(2)}, u32[]{:S(2)}) collective-permute-start(bf16[128,2048]{1,0:T(8,128)(2,1)S(1)} %copy-done.59), channel_id=1, source_target_pairs={{0,16},{4,20},{8,24},{12,28},{16,0},{20,4},{24,8},{28,12},{1,17},{... | collective-permute-start | bytes 1572872 | tf_op jit(solution)/shard_map/ppermute | solution.py:97
  578.2 24.7 %collective-permute-start.50 = (bf16[128,2048]{1,0:T(8,128)(2,1)S(1)}, bf16[128,2048]{1,0:T(8,128)(2,1)}, u32[]{:S(2)}, u32[]{:S(2)}) collective-permute-start(bf16[128,2048]{1,0:T(8,128)(2,1)S(1)} %add_convert_fusion.17), channel_id=1, source_target_pairs={{0,8},{4,12},{8,0},{12,4},{16,24},{20,28},{24,16},{28,20},{1,9},{5... | collective-permute-start | bytes 1572872 | tf_op jit(solution)/shard_map/ppermute | solution.py:97
  578.8 24.0 %collective-permute-start.49 = (bf16[128,2048]{1,0:T(8,128)(2,1)S(1)}, bf16[128,2048]{1,0:T(8,128)(2,1)S(1)}, u32[]{:S(2)}, u32[]{:S(2)}) collective-permute-start(bf16[128,2048]{1,0:T(8,128)(2,1)S(1)} %add_convert_fusion.17), channel_id=1, source_target_pairs={{0,4},{4,0},{8,12},{12,8},{16,20},{20,16},{24,28},{28,24},{1,5},{5... | collective-permute-start | bytes 1572872 | tf_op jit(solution)/shard_map/ppermute | solution.py:97
  579.6 24.2 %collective-permute-start.51 = (bf16[128,2048]{1,0:T(8,128)(2,1)}, bf16[128,2048]{1,0:T(8,128)(2,1)S(1)}, u32[]{:S(2)}, u32[]{:S(2)}) collective-permute-start(bf16[128,2048]{1,0:T(8,128)(2,1)} %collective-permute-done.45), channel_id=1, source_target_pairs={{0,4},{4,0},{8,12},{12,8},{16,20},{20,16},{24,28},{28,24},{1,5},{5... | collective-permute-start | bytes 1572872 | tf_op jit(solution)/shard_map/ppermute | solution.py:97
  582.9 47.6 %collective-permute-start.47 = (bf16[512,512]{1,0:T(8,128)(2,1)}, bf16[512,512]{1,0:T(8,128)(2,1)}, u32[]{:S(2)}, u32[]{:S(2)}) collective-permute-start(bf16[512,512]{1,0:T(8,128)(2,1)} %get-tuple-element.125), channel_id=1, source_target_pairs={{0,16},{4,20},{8,24},{12,28},{16,0},{20,4},{24,8},{28,12},{1,17},{... | collective-permute-start | bytes 1572872 | tf_op jit(solution)/shard_map/ppermute | solution.py:97
  604.0 26.5 %collective-permute-start.53 = (bf16[128,2048]{1,0:T(8,128)(2,1)S(1)}, bf16[128,2048]{1,0:T(8,128)(2,1)}, u32[]{:S(2)}, u32[]{:S(2)}) collective-permute-start(bf16[128,2048]{1,0:T(8,128)(2,1)S(1)} %add_convert_fusion.16), channel_id=1, source_target_pairs={{0,8},{4,12},{8,0},{12,4},{16,24},{20,28},{24,16},{28,20},{1,9},{5... | collective-permute-start | bytes 1572872 | tf_op jit(solution)/shard_map/ppermute | solution.py:97
  605.3 25.2 %collective-permute-start.52 = (bf16[128,2048]{1,0:T(8,128)(2,1)S(1)}, bf16[128,2048]{1,0:T(8,128)(2,1)}, u32[]{:S(2)}, u32[]{:S(2)}) collective-permute-start(bf16[128,2048]{1,0:T(8,128)(2,1)S(1)} %add_convert_fusion.16), channel_id=1, source_target_pairs={{0,4},{4,0},{8,12},{12,8},{16,20},{20,16},{24,28},{28,24},{1,5},{5... | collective-permute-start | bytes 1572872 | tf_op jit(solution)/shard_map/ppermute | solution.py:97
  616.3 63.3 %collective-permute-start.56 = (bf16[512,512]{1,0:T(8,128)(2,1)}, bf16[512,512]{1,0:T(8,128)(2,1)}, u32[]{:S(2)}, u32[]{:S(2)}) collective-permute-start(bf16[512,512]{1,0:T(8,128)(2,1)} %get-tuple-element.136), channel_id=1, source_target_pairs={{0,16},{4,20},{8,24},{12,28},{16,0},{20,4},{24,8},{28,12},{1,17},{... | collective-permute-start | bytes 1572872 | tf_op jit(solution)/shard_map/ppermute | solution.py:97
  633.2 19.2 %collective-permute-start.60 = (bf16[2,256,2048]{2,1,0:T(8,128)(2,1)S(1)}, bf16[2,256,2048]{2,1,0:T(8,128)(2,1)S(1)}, u32[]{:S(2)}, u32[]{:S(2)}) collective-permute-start(bf16[2,256,2048]{2,1,0:T(8,128)(2,1)S(1)} %fusion.43), channel_id=1, source_target_pairs={{0,1},{1,0},{2,3},{3,2},{4,5},{5,4},{6,7},{7,6},{8,9},{9,8},{10,11... | collective-permute-start | bytes 6291464 | tf_op jit(solution)/shard_map/ppermute | solution.py:86
  635.2 44.4 %collective-permute-start.58 = (bf16[512,512]{1,0:T(8,128)(2,1)S(1)}, bf16[512,512]{1,0:T(8,128)(2,1)S(1)}, u32[]{:S(2)}, u32[]{:S(2)}) collective-permute-start(bf16[512,512]{1,0:T(8,128)(2,1)S(1)} %add_convert_fusion.15), channel_id=1, source_target_pairs={{0,8},{4,12},{8,0},{12,4},{16,24},{20,28},{24,16},{28,20},{1,9},{5... | collective-permute-start | bytes 1572872 | tf_op jit(solution)/shard_map/ppermute | solution.py:97
  635.8 43.9 %collective-permute-start.57 = (bf16[512,512]{1,0:T(8,128)(2,1)S(1)}, bf16[512,512]{1,0:T(8,128)(2,1)S(1)}, u32[]{:S(2)}, u32[]{:S(2)}) collective-permute-start(bf16[512,512]{1,0:T(8,128)(2,1)S(1)} %add_convert_fusion.15), channel_id=1, source_target_pairs={{0,4},{4,0},{8,12},{12,8},{16,20},{20,16},{24,28},{28,24},{1,5},{5... | collective-permute-start | bytes 1572872 | tf_op jit(solution)/shard_map/ppermute | solution.py:97
  653.4 23.7 %collective-permute-start.61 = (bf16[256,2048]{1,0:T(8,128)(2,1)S(1)}, bf16[256,2048]{1,0:T(8,128)(2,1)S(1)}, u32[]{:S(2)}, u32[]{:S(2)}) collective-permute-start(bf16[256,2048]{1,0:T(8,128)(2,1)S(1)} %fusion.61), channel_id=1, source_target_pairs={{0,2},{1,3},{2,0},{3,1},{4,6},{5,7},{6,4},{7,5},{8,10},{9,11},{10,... | collective-permute-start | bytes 3145736 | tf_op jit(solution)/shard_map/ppermute | solution.py:94
  664.9 31.9 %collective-permute-start.55 = (bf16[512,512]{1,0:T(8,128)(2,1)S(1)}, bf16[512,512]{1,0:T(8,128)(2,1)S(1)}, u32[]{:S(2)}, u32[]{:S(2)}) collective-permute-start(bf16[512,512]{1,0:T(8,128)(2,1)S(1)} %copy-done.34), channel_id=1, source_target_pairs={{0,16},{4,20},{8,24},{12,28},{16,0},{20,4},{24,8},{28,12},{1,17},{... | collective-permute-start | bytes 1572872 | tf_op jit(solution)/shard_map/ppermute | solution.py:97
  690.2 19.4 %collective-permute-start.63 = (bf16[512,512]{1,0:T(8,128)(2,1)S(1)}, bf16[512,512]{1,0:T(8,128)(2,1)S(1)}, u32[]{:S(2)}, u32[]{:S(2)}) collective-permute-start(bf16[512,512]{1,0:T(8,128)(2,1)S(1)} %add_convert_fusion.14), channel_id=1, source_target_pairs={{0,8},{4,12},{8,0},{12,4},{16,24},{20,28},{24,16},{28,20},{1,9},{5... | collective-permute-start | bytes 1572872 | tf_op jit(solution)/shard_map/ppermute | solution.py:97
  691.5 21.0 %collective-permute-start.64 = (bf16[512,512]{1,0:T(8,128)(2,1)S(1)}, bf16[512,512]{1,0:T(8,128)(2,1)S(1)}, u32[]{:S(2)}, u32[]{:S(2)}) collective-permute-start(bf16[512,512]{1,0:T(8,128)(2,1)S(1)} %collective-permute-done.58), channel_id=1, source_target_pairs={{0,4},{4,0},{8,12},{12,8},{16,20},{20,16},{24,28},{28,24},{1,5},{5... | collective-permute-start | bytes 1572872 | tf_op jit(solution)/shard_map/ppermute | solution.py:97
  693.6 28.0 %collective-permute-start.71 = (bf16[512,512]{1,0:T(8,128)(2,1)S(1)}, bf16[512,512]{1,0:T(8,128)(2,1)S(1)}, u32[]{:S(2)}, u32[]{:S(2)}) collective-permute-start(bf16[512,512]{1,0:T(8,128)(2,1)S(1)} %copy-done.33), channel_id=1, source_target_pairs={{0,16},{4,20},{8,24},{12,28},{16,0},{20,4},{24,8},{28,12},{1,17},{... | collective-permute-start | bytes 1572872 | tf_op jit(solution)/shard_map/ppermute | solution.py:97
  720.0 32.6 %collective-permute-start.70 = (bf16[512,384]{1,0:T(8,128)(2,1)}, bf16[512,384]{1,0:T(8,128)(2,1)}, u32[]{:S(2)}, u32[]{:S(2)}) collective-permute-start(bf16[512,384]{1,0:T(8,128)(2,1)} %get-tuple-element.146), channel_id=1, source_target_pairs={{0,16},{4,20},{8,24},{12,28},{16,0},{20,4},{24,8},{28,12},{1,17},{... | collective-permute-start | bytes 1179656 | tf_op jit(solution)/shard_map/ppermute | solution.py:97
  738.8 23.0 %collective-permute-start.77 = (bf16[512,512]{1,0:T(8,128)(2,1)}, bf16[512,512]{1,0:T(8,128)(2,1)}, u32[]{:S(2)}, u32[]{:S(2)}) collective-permute-start(bf16[512,512]{1,0:T(8,128)(2,1)} %collective-permute-done.73), channel_id=1, source_target_pairs={{0,4},{4,0},{8,12},{12,8},{16,20},{20,16},{24,28},{28,24},{1,5},{5... | collective-permute-start | bytes 1572872 | tf_op jit(solution)/shard_map/ppermute | solution.py:97
  747.9 23.2 %collective-permute-start.79 = (bf16[512,384]{1,0:T(8,128)(2,1)}, bf16[512,384]{1,0:T(8,128)(2,1)S(1)}, u32[]{:S(2)}, u32[]{:S(2)}) collective-permute-start(bf16[512,384]{1,0:T(8,128)(2,1)} %get-tuple-element.153), channel_id=1, source_target_pairs={{0,16},{4,20},{8,24},{12,28},{16,0},{20,4},{24,8},{28,12},{1,17},{... | collective-permute-start | bytes 1179656 | tf_op jit(solution)/shard_map/ppermute | solution.py:97
  761.8 22.1 %collective-permute-start.82 = (bf16[512,512]{1,0:T(8,128)(2,1)}, bf16[512,512]{1,0:T(8,128)(2,1)S(1)}, u32[]{:S(2)}, u32[]{:S(2)}) collective-permute-start(bf16[512,512]{1,0:T(8,128)(2,1)} %collective-permute-done.76), channel_id=1, source_target_pairs={{0,4},{4,0},{8,12},{12,8},{16,20},{20,16},{24,28},{28,24},{1,5},{5... | collective-permute-start | bytes 1572872 | tf_op jit(solution)/shard_map/ppermute | solution.py:97
  763.4 20.5 %collective-permute-start.81 = (bf16[512,384]{1,0:T(8,128)(2,1)S(1)}, bf16[512,384]{1,0:T(8,128)(2,1)S(1)}, u32[]{:S(2)}, u32[]{:S(2)}) collective-permute-start(bf16[512,384]{1,0:T(8,128)(2,1)S(1)} %add_convert_fusion.28), channel_id=1, source_target_pairs={{0,8},{4,12},{8,0},{12,4},{16,24},{20,28},{24,16},{28,20},{1,9},{5... | collective-permute-start | bytes 1179656 | tf_op jit(solution)/shard_map/ppermute | solution.py:97
  763.5 20.4 %collective-permute-start.80 = (bf16[512,384]{1,0:T(8,128)(2,1)S(1)}, bf16[512,384]{1,0:T(8,128)(2,1)S(1)}, u32[]{:S(2)}, u32[]{:S(2)}) collective-permute-start(bf16[512,384]{1,0:T(8,128)(2,1)S(1)} %add_convert_fusion.28), channel_id=1, source_target_pairs={{0,4},{4,0},{8,12},{12,8},{16,20},{20,16},{24,28},{28,24},{1,5},{5... | collective-permute-start | bytes 1179656 | tf_op jit(solution)/shard_map/ppermute | solution.py:97
  765.3 27.4 %collective-permute-start.78 = (bf16[512,384]{1,0:T(8,128)(2,1)S(1)}, bf16[512,384]{1,0:T(8,128)(2,1)S(1)}, u32[]{:S(2)}, u32[]{:S(2)}) collective-permute-start(bf16[512,384]{1,0:T(8,128)(2,1)S(1)} %copy-done.38), channel_id=1, source_target_pairs={{0,16},{4,20},{8,24},{12,28},{16,0},{20,4},{24,8},{28,12},{1,17},{... | collective-permute-start | bytes 1179656 | tf_op jit(solution)/shard_map/ppermute | solution.py:97
  786.2 29.1 %collective-permute-start.86 = (bf16[512,384]{1,0:T(8,128)(2,1)S(1)}, bf16[512,384]{1,0:T(8,128)(2,1)S(1)}, u32[]{:S(2)}, u32[]{:S(2)}) collective-permute-start(bf16[512,384]{1,0:T(8,128)(2,1)S(1)} %get-tuple-element.169), channel_id=1, source_target_pairs={{0,16},{4,20},{8,24},{12,28},{16,0},{20,4},{24,8},{28,12},{1,17},{... | collective-permute-start | bytes 1179656 | tf_op jit(solution)/shard_map/ppermute | solution.py:97
  (146 other events, 2425.9 us)

commit v3 on v2

v3 whole, which is shorter than its diff:
```python
import functools

import jax
import jax.numpy as jnp
from jax import lax
from jax.experimental import pallas as pl
from jax.experimental.pallas import tpu as pltpu
from jax.sharding import PartitionSpec as P

D = 2048
HD = 256
ROT = 64
LEN = 1024
EPSILON = 1e-05
BF = jnp.bfloat16
F32 = jnp.float32


def rotary_tables(length, rot_dims):
    half_dims = rot_dims // 2
    frequency = 10000.0 ** (-2.0 * jnp.arange(half_dims, dtype=F32) / rot_dims)
    angles = jnp.arange(length, dtype=F32)[:, None] * frequency[None, :]
    return jnp.cos(angles), jnp.sin(angles)


def contract(left_side, right_side, left_dim, right_dim):
    return lax.dot_general(
        left_side,
        right_side,
        (((left_dim,), (right_dim,)), ((), ())),
        preferred_element_type=F32,
    )


def exact_gelu(pre_act):
    below = 0.5 + 0.5 * lax.erf(pre_act * 0.5**0.5)
    density = jnp.exp(-0.5 * pre_act * pre_act) * (2.0 * jnp.pi) ** -0.5
    return pre_act * below, below + pre_act * density


def after(value, *earlier):
    return lax.optimization_barrier((value,) + earlier)[0]


def rotary_lanes(cosine, sine):
    ones = jnp.ones((cosine.shape[0], 128 - ROT), F32)
    none = jnp.zeros_like(sine)
    rest = jnp.zeros_like(ones)
    keep = jnp.concatenate([cosine, cosine, ones], axis=1)
    up = jnp.concatenate([-sine, none, rest], axis=1)
    down = jnp.concatenate([none, sine, rest], axis=1)
    return keep, up, down


def turned(block, keep, up, down, sign):
    head = block[:, :128]
    half = ROT // 2
    moved = head * keep + sign * (
        pltpu.roll(head, 128 - half, 1) * up + pltpu.roll(head, half, 1) * down
    )
    return jnp.concatenate([moved, block[:, 128:]], axis=1)


def qkv_kernel(x_ref, w_ref, b_ref, keep_ref, up_ref, down_ref, o_ref):
    kind = pl.program_id(0) % 3
    tile = o_ref.shape[0] // 4

    def rows_at(i):
        return pl.ds(pl.multiple_of(i * tile, tile), tile)

    def project(i):
        return (
            jnp.dot(x_ref[rows_at(i), :], w_ref[...], preferred_element_type=F32) + b_ref[...]
        )

    @pl.when(kind == 2)
    def _():
        @pl.loop(0, 4)
        def _(i):
            o_ref[rows_at(i), :] = project(i).astype(BF)

    @pl.when(kind != 2)
    def _():
        @pl.loop(0, 4)
        def _(i):
            at = rows_at(i)
            o_ref[at, :] = turned(
                project(i), keep_ref[at, :], up_ref[at, :], down_ref[at, :], 1.0
            ).astype(BF)


def project_qkv(normed, weight, bias, tables):
    length, width = normed.shape
    columns = weight.shape[1]
    table = pl.BlockSpec((length, 128), lambda j: (0, 0))
    return pl.pallas_call(
        qkv_kernel,
        grid=(columns // HD,),
        in_specs=[
            pl.BlockSpec((length, width), lambda j: (0, 0)),
            pl.BlockSpec((width, HD), lambda j: (0, j)),
            pl.BlockSpec((1, HD), lambda j: (0, j)),
            table,
            table,
            table,
        ],
        out_specs=pl.BlockSpec((length, HD), lambda j: (0, j)),
        out_shape=jax.ShapeDtypeStruct((length, columns), BF),
        compiler_params=pltpu.CompilerParams(vmem_limit_bytes=40 << 20),
        cost_estimate=pl.CostEstimate(
            flops=2 * length * width * columns,
            bytes_accessed=2 * (length * width + width * columns + length * columns),
            transcendentals=0,
        ),
        name="qkv_rotary",
    )(normed, weight, bias.astype(F32)[None, :], *tables)


def visible_scores(queries, keys, row_spots, key_spots, prefix):
    scores = lax.dot_general(
        queries, keys, (((1,), (1,)), ((), ())), preferred_element_type=F32
    ) * (HD**-0.5)
    allowed = (key_spots <= row_spots) | (key_spots < prefix)
    return jnp.where(allowed, scores, -jnp.inf)


def attend_kernel(prefix_ref, q_ref, k_ref, v_ref, rows_ref, keys_ref, o_ref, log_ref):
    scores = visible_scores(
        q_ref[...], k_ref[...], rows_ref[...], keys_ref[...], prefix_ref[0]
    )
    top = jnp.max(scores, axis=-1, keepdims=True)
    weights = jnp.exp(scores - top)
    total = jnp.sum(weights, axis=-1, keepdims=True)
    probs = (weights * (1.0 / total)).astype(BF)
    o_ref[...] = jnp.dot(probs, v_ref[...], preferred_element_type=F32).astype(BF)
    log_ref[0] = top + jnp.log(total)


def attend(qkv, prefix, spots):
    length = qkv.shape[0]
    heads = qkv.shape[1] // (3 * HD)
    tile = length // 4
    whole = lambda part: pl.BlockSpec((length, HD), lambda h, i, p: (0, 3 * h + part))
    return pl.pallas_call(
        attend_kernel,
        grid_spec=pltpu.PrefetchScalarGridSpec(
            num_scalar_prefetch=1,
            grid=(heads, 4),
            in_specs=[
                pl.BlockSpec((tile, HD), lambda h, i, p: (i, 3 * h)),
                whole(1),
                whole(2),
                pl.BlockSpec((tile, 1), lambda h, i, p: (i, 0)),
                pl.BlockSpec((1, length), lambda h, i, p: (0, 0)),
            ],
            out_specs=[
                pl.BlockSpec((tile, HD), lambda h, i, p: (i, h)),
                pl.BlockSpec((1, tile, 1), lambda h, i, p: (h, i, 0)),
            ],
        ),
        out_shape=[
            jax.ShapeDtypeStruct((length, heads * HD), BF),
            jax.ShapeDtypeStruct((heads, length, 1), F32),
        ],
        compiler_params=pltpu.CompilerParams(vmem_limit_bytes=32 << 20),
        cost_estimate=pl.CostEstimate(
            flops=4 * heads * length * length * HD,
            bytes_accessed=8 * length * heads * HD,
            transcendentals=heads * length * length,
        ),
        name="attend",
    )(prefix, qkv, qkv, qkv, spots[:, None], spots[None, :])


def attend_back_kernel(
    prefix_ref, q_ref, k_ref, v_ref, g_ref, log_ref, rows_ref, keys_ref, keep_ref, up_ref,
    down_ref, o_ref, dk_ref, dv_ref,
):
    length = q_ref.shape[0]
    tile = length // 4
    scale = HD**-0.5
    for i in range(4):
        at = pl.ds(i * tile, tile)
        q, g = q_ref[at, :], g_ref[at, :]
        scores = visible_scores(q, k_ref[...], rows_ref[at, :], keys_ref[...], prefix_ref[0])
        probs = jnp.exp(scores - log_ref[0, at, :])
        grad_probs = lax.dot_general(
            g, v_ref[...], (((1,), (1,)), ((), ())), preferred_element_type=F32
        )
        dots = jnp.sum(probs * grad_probs, axis=-1, keepdims=True)
        grad_scores = (probs * (grad_probs - dots)).astype(BF)
        dq = jnp.dot(grad_scores, k_ref[...], preferred_element_type=F32) * scale
        o_ref[at, :HD] = turned(
            dq, keep_ref[at, :], up_ref[at, :], down_ref[at, :], -1.0
        ).astype(BF)
        dk = contract(grad_scores, q, 0, 0)
        dv = contract(probs.astype(BF), g, 0, 0)
        if i == 0:
            dk_ref[...] = dk
            dv_ref[...] = dv
        else:
            dk_ref[...] += dk
            dv_ref[...] += dv
    o_ref[:, HD : 2 * HD] = turned(
        dk_ref[...] * scale, keep_ref[...], up_ref[...], down_ref[...], -1.0
    ).astype(BF)
    o_ref[:, 2 * HD :] = dv_ref[...].astype(BF)


def attend_back(qkv, grad_context, log_total, prefix, spots, tables):
    length = qkv.shape[0]
    heads = qkv.shape[1] // (3 * HD)
    part = lambda n: pl.BlockSpec((length, HD), lambda h, p: (0, 3 * h + n))
    table = pl.BlockSpec((length, 128), lambda h, p: (0, 0))
    return pl.pallas_call(
        attend_back_kernel,
        grid_spec=pltpu.PrefetchScalarGridSpec(
            num_scalar_prefetch=1,
            grid=(heads,),
            in_specs=[
                part(0),
                part(1),
                part(2),
                pl.BlockSpec((length, HD), lambda h, p: (0, h)),
                pl.BlockSpec((1, length, 1), lambda h, p: (h, 0, 0)),
                pl.BlockSpec((length, 1), lambda h, p: (0, 0)),
                pl.BlockSpec((1, length), lambda h, p: (0, 0)),
                table,
                table,
                table,
            ],
            out_specs=pl.BlockSpec((length, 3 * HD), lambda h, p: (0, h)),
            scratch_shapes=[pltpu.VMEM((length, HD), F32), pltpu.VMEM((length, HD), F32)],
        ),
        out_shape=jax.ShapeDtypeStruct((length, heads * 3 * HD), BF),
        compiler_params=pltpu.CompilerParams(vmem_limit_bytes=48 << 20),
        cost_estimate=pl.CostEstimate(
            flops=10 * heads * length * length * HD,
            bytes_accessed=14 * length * heads * HD,
            transcendentals=heads * length * length,
        ),
        name="attend_back",
    )(prefix, qkv, qkv, qkv, grad_context, log_total, spots[:, None], spots[None, :], *tables)


def place_kernel(quarter_ref, *refs):
    pieces, out_ref = refs[-5:-1], refs[-1]
    for index, piece in enumerate(pieces):

        @pl.when(pl.program_id(0) == index)
        def _(piece=piece):
            out_ref[...] = piece[...].astype(F32)


def place_quarters(whole, pieces, shape, axis, chunk, chunks, quarter):
    rows, columns = pieces[0].shape
    if axis == 0:
        spot = lambda k, q: ((q[0] ^ k) * chunks + chunk, 0)
    else:
        spot = lambda k, q: (chunk, q[0] ^ k)
    first = whole is None
    operands = ([] if first else [whole]) + list(pieces)
    return pl.pallas_call(
        place_kernel,
        grid_spec=pltpu.PrefetchScalarGridSpec(
            num_scalar_prefetch=1,
            grid=(4,),
            in_specs=([] if first else [pl.BlockSpec(memory_space=pl.ANY)])
            + [pl.BlockSpec((rows, columns), lambda k, q: (0, 0))] * 4,
            out_specs=pl.BlockSpec((rows, columns), spot),
        ),
        out_shape=jax.ShapeDtypeStruct(shape, F32),
        input_output_aliases={} if first else {1: 0},
        compiler_params=pltpu.CompilerParams(vmem_limit_bytes=24 << 20),
        cost_estimate=pl.CostEstimate(
            flops=0, bytes_accessed=24 * rows * columns, transcendentals=0
        ),
        name="place_quarters",
    )(quarter.reshape(1), *operands)


def norms_kernel(count, gains_ref, *refs):
    blocks, (attn_ref, mlp_ref) = refs[:count], refs[count:]
    for index, block in enumerate(blocks):

        @pl.when(pl.program_id(0) == index)
        def _(block=block):
            features = block[...].astype(F32)
            average = jnp.mean(features, axis=-1, keepdims=True)
            centered = features - average
            spread = jnp.mean(centered * centered, axis=-1, keepdims=True)
            xhat = centered * lax.rsqrt(spread + EPSILON)
            attn_ref[...] = (xhat * gains_ref[0:1, :] + gains_ref[1:2, :]).astype(BF)
            mlp_ref[...] = (xhat * gains_ref[2:3, :] + gains_ref[3:4, :]).astype(BF)


def both_norms(blocks, gains):
    count = len(blocks)
    rows, width = blocks[0].shape
    shape = jax.ShapeDtypeStruct((count * rows, width), BF)
    return pl.pallas_call(
        functools.partial(norms_kernel, count),
        grid=(count,),
        in_specs=[pl.BlockSpec((8, width), lambda i: (0, 0))]
        + [pl.BlockSpec((rows, width), lambda i: (0, 0))] * count,
        out_specs=[pl.BlockSpec((rows, width), lambda i: (i, 0))] * 2,
        out_shape=[shape, shape],
        compiler_params=pltpu.CompilerParams(vmem_limit_bytes=48 << 20),
        cost_estimate=pl.CostEstimate(
            flops=12 * count * rows * width,
            bytes_accessed=6 * count * rows * width,
            transcendentals=0,
        ),
        name="both_norms",
    )(gains, *blocks)


def outer_kernel(near_ref, far_ref, right_ref, *refs):
    rights, o_ref = refs[:-1], refs[-1]
    total = contract(near_ref[...], right_ref[...], 0, 0)
    rows = rights[0].shape[0]
    for index, right in enumerate(rights):
        total += contract(far_ref[pl.ds(index * rows, rows), :], right[...], 0, 0)
    o_ref[...] = total.astype(BF)


def outer_blocks(near, far, near_right, far_blocks):
    length, left = near.shape
    width = near_right.shape[1]
    rows = far_blocks[0].shape[0]
    tile = 512
    return pl.pallas_call(
        outer_kernel,
        grid=(width // tile,),
        in_specs=[
            pl.BlockSpec((length, left), lambda j: (0, 0)),
            pl.BlockSpec(far.shape, lambda j: (0, 0)),
            pl.BlockSpec((length, tile), lambda j: (0, j)),
        ]
        + [pl.BlockSpec((rows, tile), lambda j: (0, j))] * len(far_blocks),
        out_specs=pl.BlockSpec((left, tile), lambda j: (0, j)),
        out_shape=jax.ShapeDtypeStruct((left, width), BF),
        compiler_params=pltpu.CompilerParams(vmem_limit_bytes=56 << 20),
        cost_estimate=pl.CostEstimate(
            flops=2 * (length + far.shape[0]) * left * width,
            bytes_accessed=2 * (length + far.shape[0]) * (left + width),
            transcendentals=0,
        ),
        name="outer_blocks",
    )(near, far, near_right, *far_blocks)


def back_kernel(weight_ref, slope_ref, *refs):
    blocks, o_ref = refs[:-1], refs[-1]
    for index, block in enumerate(blocks):

        @pl.when(pl.program_id(0) == index)
        def _(block=block):
            o_ref[...] = (contract(block[...], weight_ref[...], 1, 1) * slope_ref[...]).astype(BF)


def back_blocks(blocks, weight, slope):
    rows, width = blocks[0].shape
    units = weight.shape[0]
    count = len(blocks)
    return pl.pallas_call(
        back_kernel,
        grid=(count,),
        in_specs=[
            pl.BlockSpec((units, width), lambda i: (0, 0)),
            pl.BlockSpec((rows, units), lambda i: (i, 0)),
        ]
        + [pl.BlockSpec((rows, width), lambda i: (0, 0))] * count,
        out_specs=pl.BlockSpec((rows, units), lambda i: (i, 0)),
        out_shape=jax.ShapeDtypeStruct((count * rows, units), BF),
        compiler_params=pltpu.CompilerParams(vmem_limit_bytes=56 << 20),
        cost_estimate=pl.CostEstimate(
            flops=2 * count * rows * units * width,
            bytes_accessed=2 * count * rows * (width + 3 * units),
            transcendentals=0,
        ),
        name="back_blocks",
    )(weight, slope, *blocks)


def on_device(
    hidden,
    teacher,
    valid_mask,
    prefix_len,
    ln1_gain,
    ln1_bias,
    ln2_gain,
    ln2_bias,
    qkv_weight,
    qkv_bias,
    out_weight,
    out_bias,
    fc1_weight,
    fc1_bias,
    fc2_weight,
    fc2_bias,
):
    rows = hidden.shape[0]
    dp = lax.axis_size("dp")
    tp = lax.axis_size("tensor")
    ways = tp // 2
    squares = dp // 4
    total_tokens = dp * tp * rows
    heads = qkv_weight.shape[1] // (3 * HD)
    dp_index = lax.axis_index("dp")
    tp_index = lax.axis_index("tensor")
    core, y = tp_index % 2, tp_index // 2
    quarter = dp_index % 4

    def to_core(v):
        return lax.ppermute(v, "tensor", [(t, t ^ 1) for t in range(tp)])

    def from_y(v, step):
        pairs = [(t, ((t // 2 - step) % ways) * 2 + t % 2) for t in range(tp)]
        return lax.ppermute(v, "tensor", pairs)

    def to_y(v, step):
        pairs = [(t, ((t // 2 + step) % ways) * 2 + t % 2) for t in range(tp)]
        return lax.ppermute(v, "tensor", pairs)

    def flip(v, mask):
        return lax.ppermute(v, "dp", [(d, d ^ mask) for d in range(dp)])

    def tensor_sum(v):
        v = v + to_core(v)
        bit = 2
        while bit < tp:
            v = v + lax.ppermute(v, "tensor", [(t, t ^ bit) for t in range(tp)])
            bit *= 2
        return v

    def dp_sum(v):
        bit = 1
        while bit < dp:
            v = v + flip(v, bit)
            bit *= 2
        return v

    block_ids = [
        ((y + step) % ways) * 2 + (core if mate == 0 else 1 - core)
        for step in range(ways)
        for mate in (0, 1)
    ]

    def gather_near(own):
        parts, over_y = [own, to_core(own)], []
        for step in range(1, ways):
            over_y.append(from_y(own, step))
            parts += [over_y[-1], to_core(over_y[-1])]
        return parts, over_y

    def gather_far(own, over_y):
        first = [flip(own, 1), flip(own, 2)]
        first.append(flip(first[1], 1))
        rounds_y = [first]
        for step in range(1, ways):
            rounds_y.append(
                [from_y(first[0], step), flip(over_y[step - 1], 2), from_y(first[2], step)]
            )
        parts = [[], [], []]
        for blocks in rounds_y:
            for i in range(3):
                parts[i] += [blocks[i], to_core(blocks[i])]
        return parts[0] + parts[1] + parts[2]

    def quarter_of(v, axis, index):
        size = v.shape[axis] // 4
        return lax.dynamic_slice_in_dim(v, index * size, size, axis)

    def swap_quarters(v):
        return [flip(quarter_of(v, 1, quarter ^ mask), mask) for mask in (1, 2, 3)]

    gain_attn = ln1_gain.astype(F32)
    shift_attn = ln1_bias.astype(F32)
    gain_mlp = ln2_gain.astype(F32)
    shift_mlp = ln2_bias.astype(F32)
    mask_f = valid_mask.astype(F32)
    count_all = dp_sum(tensor_sum(jnp.full((8, 128), jnp.sum(mask_f), F32)))[0, 0]

    gains = jnp.pad(
        jnp.stack([gain_attn, shift_attn, gain_mlp, shift_mlp]), ((0, 4), (0, 0))
    )
    near_blocks, hidden_y = gather_near(hidden)
    far_blocks = gather_far(hidden, hidden_y)
    norm_attn, norm_mlp = both_norms(near_blocks, gains)

    cosine_all, sine_all = rotary_tables(LEN, ROT)

    def in_order(table):
        return jnp.concatenate(
            [lax.dynamic_slice_in_dim(table, b * rows, rows, 0) for b in block_ids], axis=0
        )

    tables = rotary_lanes(in_order(cosine_all), in_order(sine_all))
    spots = jnp.concatenate([b * rows + jnp.arange(rows, dtype=jnp.int32) for b in block_ids])
    qkv_low = project_qkv(norm_attn, qkv_weight, qkv_bias, tables)
    context, log_total = attend(qkv_low, prefix_len, spots)
    hidden_pre = jnp.dot(norm_mlp, fc1_weight, preferred_element_type=F32) + fc1_bias.astype(F32)
    active, slope = exact_gelu(hidden_pre)
    active = active.astype(BF)
    active, *far_blocks = lax.optimization_barrier((active, *far_blocks))
    branch_part = jnp.dot(context, out_weight, preferred_element_type=F32) + jnp.dot(
        active, fc2_weight, preferred_element_type=F32
    )

    def scatter_rows(part, meanwhile=None):
        blocks = part.reshape(ways, 2, rows, D)
        mine = blocks[:, 0] + to_core(blocks[:, 1].astype(BF)).astype(F32)
        total = mine[0]
        side_work = None
        for step in range(1, ways):
            low = mine[step].astype(BF)
            got = to_y(low, step)
            if meanwhile is not None and step == 1:
                side_work = meanwhile(low)
                got = after(got, *side_work)
            total = total + got.astype(F32)
        return total, side_work

    branch, (norm_attn_far, norm_mlp_far) = scatter_rows(
        branch_part,
        lambda sent: both_norms([after(far_blocks[0], sent)] + far_blocks[1:], gains),
    )
    output_f = hidden.astype(F32) + branch + out_bias.astype(F32) + fc2_bias.astype(F32)
    mismatch = output_f - teacher.astype(F32)
    error_part = jnp.sum(mask_f[:, None] * mismatch * mismatch)
    grad_out = mask_f[:, None] * mismatch * (2.0 * total_tokens / count_all)
    bias_part = jnp.sum(grad_out, axis=0)
    grad_low = grad_out.astype(BF)
    grad_blocks, grad_y = gather_near(grad_low)
    grad_near = jnp.concatenate(grad_blocks, axis=0)
    grad_far = gather_far(grad_low, grad_y)

    fc1_quarter = quarter_of(fc1_weight, 1, quarter)
    fc2_quarter = quarter_of(fc2_weight, 0, quarter)
    pre_far = jnp.dot(
        after(norm_mlp_far, grad_low), fc1_quarter, preferred_element_type=F32
    ) + quarter_of(fc1_bias, 0, quarter).astype(F32)
    active_far, slope_far = exact_gelu(pre_far)
    active_far = active_far.astype(BF)
    context_far = jnp.concatenate(swap_quarters(context), axis=0)

    queue = []
    due = {}
    clock = [0]
    results = {}
    token = [grad_near]

    def gate(v):
        return after(v, token[0])

    def travel(name, low):
        mask = 4
        while mask < dp:
            (got,) = yield [(low, mask)], 2
            low = (low.astype(F32) + got.astype(F32)).astype(BF)
            mask *= 2
        beside, across = yield [(low, 1), (low, 2)], 1
        (corner,) = yield [(across, 1)], 1
        results.setdefault(name, []).append((low, beside, across, corner))

    def enqueue(name, part, count):
        size = part.shape[0] // count
        for i in range(count):
            queue.append((name, lax.slice_in_dim(part, i * size, (i + 1) * size, axis=0)))

    def turn(*others):
        now = clock[0]
        clock[0] = now + 1
        arrived = due.pop(now, [])
        values = [got for _, gots in arrived for got in gots]
        if queue:
            name, held = queue.pop(0)
            values.append(held)
        tied = list(lax.optimization_barrier(tuple(values) + others))
        token[0] = tied[0]
        asked = []
        for walker, gots in arrived:
            gots = [tied.pop(0) for _ in gots]
            try:
                asked.append((walker, walker.send(gots)))
            except StopIteration:
                pass
        if len(values) > sum(len(gots) for _, gots in arrived):
            walker = travel(name, tied.pop(0))
            asked.append((walker, next(walker)))
        for walker, (sends, wait) in asked:
            due.setdefault(now + wait, []).append((walker, [flip(v, mask) for v, mask in sends]))
        return tied

    placed = {}

    def place(name, axis, chunks):
        whole, done = placed.get(name, (None, 0))
        pieces = results.get(name, [])
        while done < len(pieces):
            whole = place_one(whole, pieces[done], axis, done, chunks)
            done += 1
        placed[name] = (whole, done)
        return whole

    def place_one(whole, pieces, axis, chunk, chunks):
        rows_here, columns = pieces[0].shape
        shape = (
            (4 * rows_here * chunks, columns) if axis == 0 else (rows_here * chunks, 4 * columns)
        )
        if columns % 128 == 0:
            return place_quarters(whole, pieces, shape, axis, chunk, chunks, quarter)
        if whole is None:
            whole = jnp.zeros(shape, F32)
        for index, piece in enumerate(pieces):
            spot = quarter ^ index
            start = (
                ((spot * chunks + chunk) * rows_here, 0)
                if axis == 0
                else (chunk * rows_here, spot * columns)
            )
            whole = lax.dynamic_update_slice(whole, piece.astype(F32), start)
        return whole

    grad_inner = (contract(grad_near, fc2_weight, 1, 1) * slope).astype(BF)
    grad_context = contract(grad_near, out_weight, 1, 1).astype(BF)
    grad_qkv = attend_back(qkv_low, grad_context, log_total, prefix_len, spots, tables)
    grad_qkv_far = swap_quarters(grad_qkv)
    left_near = jnp.concatenate(
        [quarter_of(active, 1, quarter), quarter_of(context, 1, quarter)], axis=1
    )
    left_far = jnp.concatenate([active_far, context_far], axis=1)
    part = outer_blocks(left_near, left_far, grad_near, grad_far)
    units = active_far.shape[1]
    enqueue("fc2", part[:units], 4)
    enqueue("out", part[units:], 1)
    grad_inner, *grad_qkv_far = turn(grad_inner, *grad_qkv_far)

    grad_inner_far = back_blocks([gate(grad_far[0])] + grad_far[1:], fc2_quarter, slope_far)
    fc1_part = contract(norm_mlp, quarter_of(grad_inner, 1, quarter), 0, 0) + contract(
        norm_mlp_far, grad_inner_far, 0, 0
    )
    (fc1_part,) = turn(fc1_part.astype(BF))
    enqueue("fc1", fc1_part, 4)
    qkv_part = contract(norm_attn, gate(quarter_of(grad_qkv, 1, quarter)), 0, 0) + contract(
        norm_attn_far, jnp.concatenate(grad_qkv_far, axis=0), 0, 0
    )
    (qkv_part,) = turn(qkv_part.astype(BF))
    enqueue("qkv", qkv_part, 8)
    grad_norm_mlp = contract(gate(grad_inner), fc1_weight, 1, 1)
    (grad_norm_mlp,) = turn(grad_norm_mlp)
    grad_norm_attn = contract(gate(grad_qkv), qkv_weight, 1, 1)
    (grad_norm_attn,) = turn(grad_norm_attn)

    features = jnp.concatenate(near_blocks, axis=0)
    features = gate(features).astype(F32)
    centered = features - jnp.mean(features, axis=-1, keepdims=True)
    inverse = lax.rsqrt(jnp.mean(centered * centered, axis=-1, keepdims=True) + EPSILON)
    xhat = centered * inverse

    def norm_back(gained):
        return inverse * (
            gained
            - jnp.mean(gained, axis=-1, keepdims=True)
            - xhat * jnp.mean(gained * xhat, axis=-1, keepdims=True)
        )

    grad_hidden = norm_back(grad_norm_attn * gain_attn + grad_norm_mlp * gain_mlp)
    tensor_parts = jnp.stack(
        [
            jnp.sum(grad_norm_attn * xhat, axis=0),
            jnp.sum(grad_norm_attn, axis=0),
            jnp.sum(grad_norm_mlp * xhat, axis=0),
            jnp.sum(grad_norm_mlp, axis=0),
            bias_part,
            jnp.full((D,), error_part, F32),
        ]
    ).reshape(-1)
    fc1_bias_part = jnp.sum(grad_inner, axis=0, dtype=F32)
    qkv_bias_part = jnp.sum(grad_qkv, axis=0, dtype=F32)
    grad_hidden, tensor_parts = turn(grad_hidden, tensor_parts)
    input_grad = grad_out + scatter_rows(grad_hidden)[0]
    (input_grad,) = turn(input_grad)
    small = jnp.concatenate([tensor_sum(tensor_parts), fc1_bias_part, qkv_bias_part])
    small = dp_sum(small)
    (small,) = turn(small)
    vectors = small[: 6 * D].reshape(6, D)
    fc1_bias_grad = small[6 * D : 6 * D + fc1_bias_part.shape[0]]
    qkv_bias_grad = small[6 * D + fc1_bias_part.shape[0] :]
    loss_value = vectors[5, 0] / (count_all * D)
    layout = {"fc2": (0, 4), "out": (0, 1), "fc1": (1, 4), "qkv": (1, 8)}
    while queue or due:
        for name, (axis, chunks) in layout.items():
            if len(results.get(name, [])) > placed.get(name, (None, 0))[1]:
                whole, done = placed.get(name, (None, 0))
                whole = place_one(whole, results[name][done], axis, done, chunks)
                placed[name] = (whole, done + 1)
                (whole,) = turn(whole)
                placed[name] = (whole, done + 1)
                break
        else:
            turn()
    fc2_weight_grad = place("fc2", 0, 4)
    out_weight_grad = place("out", 0, 1)
    fc1_weight_grad = place("fc1", 1, 4)
    qkv_weight_grad = place("qkv", 1, 8)
    return (
        output_f.astype(BF),
        loss_value,
        input_grad,
        vectors[0],
        vectors[1],
        vectors[2],
        vectors[3],
        qkv_weight_grad,
        qkv_bias_grad,
        out_weight_grad,
        vectors[4],
        fc1_weight_grad,
        fc1_bias_grad,
        fc2_weight_grad,
        vectors[4],
    )


def solution(mesh):
    tokens = P(("dp", "tensor"), None)
    columns, lanes, down, whole = P(None, "tensor"), P("tensor"), P("tensor", None), P()
    in_specs = (
        tokens,
        tokens,
        P(("dp", "tensor")),
        P("dp"),
        whole,
        whole,
        whole,
        whole,
        columns,
        lanes,
        down,
        whole,
        columns,
        lanes,
        down,
        whole,
    )
    out_specs = (
        tokens,
        whole,
        tokens,
        whole,
        whole,
        whole,
        whole,
        columns,
        lanes,
        down,
        whole,
        columns,
        lanes,
        down,
        whole,
    )
    return jax.shard_map(
        on_device, mesh=mesh, in_specs=in_specs, out_specs=out_specs, check_vma=False
    )
```

time: 890 us -> 788 us (0.89)
  Pallas kernels: 0 us -> 135 us
  other arithmetic: 165 us -> 56.7 us
  local copies, waits for them, and re-layouts: 133 us -> 34.4 us
  matrix products: 219 us -> 130 us
  starting transfers between devices: 94.1 us -> 135 us
  waiting for transfers between devices: 262 us -> 281 us
    pallas_call x0 -> x24, Pallas kernels: none -> 135 us  [the longest x17 38.8 us: place_quarters(): pl.pallas_call(place_kernel, grid_spec=pltpu.PrefetchScalarGridSpec(num_s...]
    unnamed x281 -> x163, local copies, waits for them, and re-layouts: 75.6 us -> 10.4 us
    ppermute x72 -> x88, waiting for transfers between devices: 164 us -> 215 us  [flip(): return lax.ppermute(v, 'dp', [(d, d ^ mask) for d in range(dp)])]
    dot_general x13 -> x8, matrix products: 128 us -> 80.7 us  [contract(): lax.dot_general(left_side, right_side, (((left_dim,), (right_dim,)), ((),...]
    ppermute x72 -> x88, starting transfers between devices: 77.2 us -> 121 us  [flip(): return lax.ppermute(v, 'dp', [(d, d ^ mask) for d in range(dp)])]
    select_n x9 -> x0, other arithmetic: 36.8 us -> none  [the longest x4 15.1 us: joined(): jnp.where(high, c, a)]
    dot_general x7 -> x0, matrix products: 31.9 us -> none  [the longest x1 14 us: on_device(): jnp.dot(norm_attn, qkv_weight, preferred_element_type=F32)]
    ppermute x2, waiting for transfers between devices: 21.3 us -> 0.01 us  [to_y(): return lax.ppermute(v, 'tensor', pairs)]
  transfers between devices with their start and end apart: 94 -> 118, of which waited for: 35 -> 52; matrix products, arithmetic and copies ran while one was open for 54% -> 24% of each run, Pallas kernels for 0% -> 16%
where the time goes in v3:
time: 788 us; the launch traced here: 779 us
  waiting for transfers between devices  281 us (36%)
  starting transfers between devices  135 us (17%)
  Pallas kernels  135 us (17%)
  matrix products  130 us (16%)
  other arithmetic  56.7 us (7%)
  local copies, waits for them, and re-layouts  34.4 us (4%)
    ppermute x88, waiting for transfers between devices, flip(): return lax.ppermute(v, 'dp', [(d, d ^ mask) for d in range(dp)])  215 us
    ppermute x88, starting transfers between devices, flip(): return lax.ppermute(v, 'dp', [(d, d ^ mask) for d in range(dp)])  121 us
    dot_general x8, matrix products, contract(): lax.dot_general(left_side, right_side, (((left_dim,), (right_dim,)), ((),...  80.7 us
    pallas_call x17, Pallas kernels, place_quarters(): pl.pallas_call(place_kernel, grid_spec=pltpu.PrefetchScalarGridSpec(num_s...  38.8 us
    ppermute x2, waiting for transfers between devices, tensor_sum(): v = v + lax.ppermute(v, 'tensor', [(t, t ^ bit) for t in range(tp)])  36.8 us
    pallas_call x2, Pallas kernels, both_norms(): pl.pallas_call(functools.partial(norms_kernel, count), grid=(count,), in_...  27.1 us
    ppermute x6, waiting for transfers between devices, from_y(): return lax.ppermute(v, 'tensor', pairs)  19.8 us
    pallas_call x1, Pallas kernels, back_blocks(): pl.pallas_call(back_kernel, grid=(count,), in_specs=[pl.BlockSpec((units,...  17.4 us
  transfers between devices with their start and end apart: 118, of which 52 were waited for; matrix products, arithmetic and copies ran while one was open for 24% of the time, Pallas kernels for 16%

profile of v3, /device:TPU:0, one launch (start us, length us, event | category | flops | bytes accessed | tf_op | source)
XLA Modules:
  0.0 778.7 jit_solution(15705452445407664793)
XLA Ops:
  0.7 3.0 collective-permute-start.1
  14.0 13.1 %collective-permute-done.1.refs_2_ = bf16[256,2048]{1,0:T(8,128)(2,1)} collective-permute-done((bf16[256,2048]{1,0:T(8,128)(2,1)}, bf16[256,2048]{1,0:T(8,128)(2,1)}, u32[]{:S(2)}, u32[]{:S(2)}) %collective-permute-start.1) | collective-permute-done | bytes 1048608 | tf_op jit(solution)/shard_map/ppermute | solution.py:421
  38.4 15.2 %collective-permute-done.11.refs_8_ = bf16[256,2048]{1,0:T(8,128)(2,1)} collective-permute-done((bf16[256,2048]{1,0:T(8,128)(2,1)}, bf16[256,2048]{1,0:T(8,128)(2,1)}, u32[]{:S(2)}, u32[]{:S(2)}) %collective-permute-start.11) | collective-permute-done | bytes 1048608 | tf_op jit(solution)/shard_map/ppermute | solution.py:428
  54.8 7.9 %both_norms.2 = (bf16[1024,2048]{1,0:T(8,128)(2,1)}, bf16[1024,2048]{1,0:T(8,128)(2,1)}) custom-call(f32[8,2048]{1,0:T(8,128)S(1)} %select_maximum_fusion.gains_ref, bf16[256,2048]{1,0:T(8,128)(2,1)S(1)} %copy-done.3, bf16[256,2048]{1,0:T(8,128)(2,1)} %collective-permute-done.refs_1_, bf16[256,2048]{1,0:T(8,128)(2,1)} %collective-permute-done.1.refs_2_, ...), custom_call_target="tpu_custom_call" | custom-call | flops 25165824 | bytes 12582912 | tf_op jit(solution)/shard_map/both_norms/pallas_call | solution.py:301
  62.7 16.0 %multiply_convert_fusion = (bf16[1024,2048]{1,0:T(8,128)(2,1)}, f32[1024,2048]{1,0:T(8,128)}) fusion(f32[2048]{0:T(1024)S(1)} %convert_element_type.249, bf16[1024,2048]{1,0:T(8,128)(2,1)} %get-tuple-element.154, bf16[2048,2048]{1,0:T(8,128)(2,1)} %param.28), kind=kOutput, calls=%fused_computation.24 | convolution fusion | flops 8602517504 | bytes 25174016 | tf_op jit(solution)/shard_map/dot_general | solution.py:504
  80.4 3.5 collective-permute-done.13.refs_10_
  83.9 13.8 %qkv_rotary.1.q_ref.k_ref.v_ref = bf16[1024,1536]{1,0:T(8,128)(2,1)S(1)} custom-call(bf16[1024,2048]{1,0:T(8,128)(2,1)S(1)} %copy-done.30, bf16[2048,1536]{1,0:T(8,128)(2,1)} %w_ref.1, f32[1,1536]{1,0:T(1,128)S(1)} %reshape.119.b_ref, f32[1024,128]{1,0:T(8,128)S(1)} %maximum_maximum_fusion.1.keep_ref, f32[1024,128]{1,0:T(8,128)S(1)} %get-tuple-element.333.up_ref, ...), custom_call_target="tpu_custom_call" | custom-call | flops 6442450944 | bytes 13631488 | tf_op jit(solution)/shard_map/qkv_rotary/pallas_call | solution.py:96
  97.8 9.4 %attend.1 = (bf16[1024,512]{1,0:T(8,128)(2,1)S(1)}, f32[2,1024,1]{2,1,0:T(8,128)S(1)}) custom-call(s32[1]{0:T(128)S(6)} %copy.105.prefix_ref, bf16[1024,1536]{1,0:T(8,128)(2,1)S(1)} %qkv_rotary.1.q_ref.k_ref.v_ref, bf16[1024,1536]{1,0:T(8,128)(2,1)S(1)} %qkv_rotary.1.q_ref.k_ref.v_ref, bf16[1024,1536]{1,0:T(8,128)(2,1)S(1)} %qkv_rotary.1.q_ref.k_ref.v_ref, ...), custom_call_target="tpu_custom_call" | custom-call | flops 2147483648 | bytes 4194304 | tf_op jit(solution)/shard_map/attend/pallas_call | solution.py:144
  107.2 5.7 fusion.62
  113.1 15.4 %convolution_add_fusion = f32[1024,2048]{1,0:T(8,128)S(1)} fusion(f32[1024,2048]{1,0:T(8,128)} %fusion.62, bf16[1024,2048]{1,0:T(8,128)(2,1)} %get-tuple-element.155, bf16[2048,2048]{1,0:T(8,128)(2,1)} %param.30), kind=kOutput, calls=%fused_computation.43 | convolution fusion | flops 8592031744 | bytes 29360128 | tf_op jit(solution)/shard_map/dot_general | solution.py:508
  129.1 4.0 collective-permute-done.15
  142.0 20.4 %collective-permute-done.18 = f32[8,128]{1,0:T(8,128)S(1)} collective-permute-done((f32[8,128]{1,0:T(8,128)S(1)}, f32[8,128]{1,0:T(8,128)S(1)}, u32[]{:S(2)}, u32[]{:S(2)}) %collective-permute-start.18) | collective-permute-done | bytes 4128 | tf_op jit(solution)/shard_map/ppermute | solution.py:434
  163.6 3.1 collective-permute-done.19
  167.2 3.2 collective-permute-done.20
  179.7 19.2 %both_norms.3 = (bf16[3072,2048]{1,0:T(8,128)(2,1)}, bf16[3072,2048]{1,0:T(8,128)(2,1)}) custom-call(f32[8,2048]{1,0:T(8,128)S(1)} %select_maximum_fusion.gains_ref, bf16[256,2048]{1,0:T(8,128)(2,1)} %collective-permute-done.3.refs_0_, bf16[256,2048]{1,0:T(8,128)(2,1)S(1)} %copy-done.9, bf16[256,2048]{1,0:T(8,128)(2,1)S(1)} %copy-done.7, ...), custom_call_target="tpu_custom_call" | custom-call | flops 75497472 | bytes 37748736 | tf_op jit(solution)/shard_map/both_norms/pallas_call | solution.py:301
  199.0 4.0 fusion.30
  205.3 3.3 constant_dynamic-slice_fusion.1.weight_ref
  217.6 16.3 %collective-permute-done.23 = bf16[1024,128]{1,0:T(8,128)(2,1)S(1)} collective-permute-done((bf16[1024,128]{1,0:T(8,128)(2,1)S(1)}, bf16[1024,128]{1,0:T(8,128)(2,1)S(1)}, u32[]{:S(2)}, u32[]{:S(2)}) %collective-permute-start.23) | collective-permute-done | bytes 262176 | tf_op jit(solution)/shard_map/ppermute | solution.py:428
  236.1 12.7 %fusion.21 = (f32[3072,512]{1,0:T(8,128)}, bf16[3072,512]{1,0:T(8,128)(2,1)S(1)}) fusion(f32[512]{0:T(512)S(1)} %dynamic-slice_convert_fusion, bf16[3072,2048]{1,0:T(8,128)(2,1)S(1)} %bitcast.89, bf16[2048,2048]{1,0:T(8,128)(2,1)} %param.28, s32[]{:T(128)S(6)} %select_n.83), kind=kOutput, calls=%fused_computation.29 | convolution fusion | flops 6459752448 | bytes 24119300 | tf_op jit(solution)/shard_map/dot_general | solution.py:542
  248.8 9.0 %maximum_maximum_fusion.far_ref = bf16[3072,640]{1,0:T(8,128)(2,1)} fusion(bf16[1024,128]{1,0:T(8,128)(2,1)S(1)} %collective-permute-done.24, bf16[1024,128]{1,0:T(8,128)(2,1)S(1)} %collective-permute-done.23, bf16[1024,128]{1,0:T(8,128)(2,1)S(1)} %collective-permute-done.22, bf16[3072,512]{1,0:T(8,128)(2,1)S(1)} %get-tuple-element.306), kind=kLoop, calls=%fused_computation.42 | loop fusion | flops 15728640 | bytes 7864320 | tf_op jit(solution)/shard_map/concatenate | solution.py:634
  262.2 15.7 %collective-permute-done.36.refs_8_ = bf16[256,2048]{1,0:T(8,128)(2,1)} collective-permute-done((bf16[256,2048]{1,0:T(8,128)(2,1)}, bf16[256,2048]{1,0:T(8,128)(2,1)}, u32[]{:S(2)}, u32[]{:S(2)}) %collective-permute-start.36) | collective-permute-done | bytes 1048608 | tf_op jit(solution)/shard_map/ppermute | solution.py:428
  278.4 19.1 %fusion.17 = bf16[1024,2048]{1,0:T(8,128)(2,1)} fusion(f32[1024,2048]{1,0:T(8,128)} %get-tuple-element.353, bf16[2048,2048]{1,0:T(8,128)(2,1)} %param.30, f32[2048]{0:T(1024)S(1)} %convert_element_type.249, bf16[256,2048]{1,0:T(8,128)(2,1)} %collective-permute-done.27, bf16[256,2048]{1,0:T(8,128)(2,1)} %collective-permute-done.26, ...), kind=kOutput, calls=%fused_computation.21 | convolution fusion | flops 8629780480 | bytes 25174016 | tf_op jit(solution)/shard_map/dot_general | solution.py:27
  297.5 4.7 convolution_convert_fusion.g_ref
  302.9 3.2 collective-permute-done.38.refs_10_
  306.1 12.1 %attend_back.1 = bf16[1024,1536]{1,0:T(8,128)(2,1)} custom-call(s32[1]{0:T(128)S(6)} %copy.105.prefix_ref, bf16[1024,1536]{1,0:T(8,128)(2,1)} %copy-done.2, bf16[1024,1536]{1,0:T(8,128)(2,1)} %copy-done.2, bf16[1024,1536]{1,0:T(8,128)(2,1)} %copy-done.2, bf16[1024,512]{1,0:T(8,128)(2,1)S(1)} %convolution_convert_fusion.g_ref, f32[2,1024,1]{2,1,0:T(8,128)S(1)} %copy-done.33, ...), custom_call_target="tpu_custom_call" | custom-call | flops 5368709120 | bytes 7340032 | tf_op jit(solution)/shard_map/attend_back/pallas_call | solution.py:215
  318.2 3.5 constant_dynamic-slice_fusion
  321.7 6.8 pad_maximum_fusion.right_ref
  333.0 16.7 %outer_blocks.1 = bf16[640,2048]{1,0:T(8,128)(2,1)} custom-call(bf16[1024,640]{1,0:T(8,128)(2,1)} %pad_maximum_fusion.2.near_ref, bf16[3072,640]{1,0:T(8,128)(2,1)} %maximum_maximum_fusion.far_ref, bf16[1024,2048]{1,0:T(8,128)(2,1)} %pad_maximum_fusion.right_ref, bf16[256,2048]{1,0:T(8,128)(2,1)} %collective-permute-done.28.refs_0_, ...), custom_call_target="tpu_custom_call" | custom-call | flops 10737418240 | bytes 22020096 | tf_op jit(solution)/shard_map/outer_blocks/pallas_call | solution.py:332
  352.7 14.2 %collective-permute-done.42 = bf16[1024,384]{1,0:T(8,128)(2,1)} collective-permute-done((bf16[1024,384]{1,0:T(8,128)(2,1)S(1)}, bf16[1024,384]{1,0:T(8,128)(2,1)}, u32[]{:S(2)}, u32[]{:S(2)}) %collective-permute-start.42) | collective-permute-done | bytes 786464 | tf_op jit(solution)/shard_map/ppermute | solution.py:428
  369.4 6.9 fusion.45
  376.3 17.4 %back_blocks.1 = bf16[3072,512]{1,0:T(8,128)(2,1)} custom-call(bf16[512,2048]{1,0:T(8,128)(2,1)} %constant_dynamic-slice_fusion.1.weight_ref, f32[3072,512]{1,0:T(8,128)} %get-tuple-element.305.slope_ref, bf16[256,2048]{1,0:T(8,128)(2,1)} %collective-permute-done.28.refs_0_, bf16[256,2048]{1,0:T(8,128)(2,1)} %collective-permute-done.29.refs_1_, ...), custom_call_target="tpu_custom_call" | custom-call | flops 6442450944 | bytes 22020096 | tf_op jit(solution)/shard_map/back_blocks/pallas_call | solution.py:366
  393.7 13.6 %add_convert_fusion = bf16[2048,512]{1,0:T(8,128)(2,1)S(1)} fusion(f32[2048,512]{1,0:T(8,128)} %fusion.45, bf16[3072,2048]{1,0:T(8,128)(2,1)} %get-tuple-element.172, bf16[3072,512]{1,0:T(8,128)(2,1)} %back_blocks.1), kind=kOutput, calls=%fused_computation.41 | convolution fusion | flops 6444548096 | bytes 22020096 | tf_op jit(solution)/shard_map/dot_general | solution.py:27
  409.1 10.2 %fusion.24 = f32[2048,384]{1,0:T(8,128)S(1)} fusion(bf16[3072,2048]{1,0:T(8,128)(2,1)} %get-tuple-element.169, bf16[1024,384]{1,0:T(8,128)(2,1)} %collective-permute-done.42, bf16[1024,384]{1,0:T(8,128)(2,1)} %collective-permute-done.41, bf16[1024,384]{1,0:T(8,128)(2,1)S(1)} %copy-done.77), kind=kOutput, calls=%fused_computation.47 | convolution fusion | flops 4838916096 | bytes 18087936 | tf_op jit(solution)/shard_map/dot_general | solution.py:27
  419.4 3.7 add_convert_fusion.1
  425.4 11.7 %fusion.63 = f32[1024,2048]{1,0:T(8,128)S(1)} fusion(bf16[1024,2048]{1,0:T(8,128)(2,1)S(1)} %copy-done.42, bf16[2048,2048]{1,0:T(8,128)(2,1)} %param.28), kind=kOutput, calls=%fused_computation.152 | convolution fusion | flops 8589934592 | bytes 20971520 | tf_op jit(solution)/shard_map/dot_general | solution.py:27
  439.7 4.1 collective-permute-done.46.refs_2_
  446.1 10.8 %fusion.64 = f32[1024,2048]{1,0:T(8,128)} fusion(bf16[1024,1536]{1,0:T(8,128)(2,1)S(1)} %copy-done.39, bf16[2048,1536]{1,0:T(8,128)(2,1)} %w_ref.1), kind=kOutput, calls=%fused_computation.153 | convolution fusion | flops 6442450944 | bytes 17825792 | tf_op jit(solution)/shard_map/dot_general | solution.py:27
  461.9 7.5 collective-permute-done.50.refs_3_
  474.9 7.3 fusion.55
  483.5 6.0 fusion.8
  489.5 5.8 collective-permute-done.53.refs_3_
  496.1 4.1 collective-permute-done.60
  503.1 3.5 collective-permute-start.56
  511.1 16.5 %collective-permute-done.66 = f32[12288]{0:T(1024)S(1)} collective-permute-done((f32[12288]{0:T(1024)S(1)}, f32[12288]{0:T(1024)S(1)}, u32[]{:S(2)}, u32[]{:S(2)}) %collective-permute-start.66) | collective-permute-done | bytes 49184 | tf_op jit(solution)/shard_map/ppermute | solution.py:434
  529.1 3.5 collective-permute-start.55
  535.5 6.2 collective-permute-done.59.refs_4_
  546.0 21.1 %collective-permute-done.68 = f32[15872]{0:T(1024)S(1)} collective-permute-done((f32[15872]{0:T(1024)S(1)}, f32[15872]{0:T(1024)S(1)}, u32[]{:S(2)}, u32[]{:S(2)}) %collective-permute-start.68) | collective-permute-done | bytes 63520 | tf_op jit(solution)/shard_map/ppermute | solution.py:428
  567.1 5.5 collective-permute-done.69
  580.5 18.1 %collective-permute-done.70 = bf16[512,512]{1,0:T(8,128)(2,1)S(1)} collective-permute-done((bf16[512,512]{1,0:T(8,128)(2,1)S(1)}, bf16[512,512]{1,0:T(8,128)(2,1)S(1)}, u32[]{:S(2)}, u32[]{:S(2)}) %collective-permute-start.70) | collective-permute-done | bytes 524320 | tf_op jit(solution)/shard_map/ppermute | solution.py:428
  598.7 7.7 collective-permute-start.76
  606.8 6.7 collective-permute-start.74
  615.9 7.7 collective-permute-done.75
  627.2 3.5 place_quarters.19.refs_0_
  630.7 10.6 %collective-permute-done.74 = bf16[512,512]{1,0:T(8,128)(2,1)S(1)} collective-permute-done((bf16[512,512]{1,0:T(8,128)(2,1)S(1)}, bf16[512,512]{1,0:T(8,128)(2,1)S(1)}, u32[]{:S(2)}, u32[]{:S(2)}) %collective-permute-start.74) | collective-permute-done | bytes 524320 | tf_op jit(solution)/shard_map/ppermute | solution.py:428
  641.3 6.9 collective-permute-done.80.refs_3_
  656.1 7.4 collective-permute-done.83
  665.7 6.0 collective-permute-done.86.refs_4_
  679.6 7.0 collective-permute-done.82
  692.1 3.1 collective-permute-start.90
  700.3 4.1 collective-permute-start.99
  710.8 5.6 collective-permute-start.98
  720.1 3.4 collective-permute-start.103
  723.7 3.9 collective-permute-start.107
  747.7 4.0 collective-permute-done.111.refs_2_
  (471 shorter events, 207.5 us)
Async XLA Ops:
  0.7 26.5 %collective-permute-start.1 = (bf16[256,2048]{1,0:T(8,128)(2,1)}, bf16[256,2048]{1,0:T(8,128)(2,1)}, u32[]{:S(2)}, u32[]{:S(2)}) collective-permute-start(bf16[256,2048]{1,0:T(8,128)(2,1)} %refs_0_.1), channel_id=1, source_target_pairs={{0,2},{1,3},{2,0},{3,1},{4,6},{5,7},{6,4},{7,5},{8,10},{9,11},{10,... | collective-permute-start | bytes 3145736 | tf_op jit(solution)/shard_map/ppermute | solution.py:421
  3.7 24.9 %collective-permute-start.7 = (bf16[256,2048]{1,0:T(8,128)(2,1)}, bf16[256,2048]{1,0:T(8,128)(2,1)}, u32[]{:S(2)}, u32[]{:S(2)}) collective-permute-start(bf16[256,2048]{1,0:T(8,128)(2,1)} %refs_0_.1), channel_id=1, source_target_pairs={{0,8},{4,12},{8,0},{12,4},{16,24},{20,28},{24,16},{28,20},{1,9},{5... | collective-permute-start | bytes 3145736 | tf_op jit(solution)/shard_map/ppermute | solution.py:428
  5.3 32.6 %collective-permute-start = (bf16[256,2048]{1,0:T(8,128)(2,1)}, bf16[256,2048]{1,0:T(8,128)(2,1)}, u32[]{:S(2)}, u32[]{:S(2)}) collective-permute-start(bf16[256,2048]{1,0:T(8,128)(2,1)} %refs_0_.1), channel_id=1, source_target_pairs={{0,1},{1,0},{2,3},{3,2},{4,5},{5,4},{6,7},{7,6},{8,9},{9,8},{10,11... | collective-permute-start | bytes 3145736 | tf_op jit(solution)/shard_map/ppermute | solution.py:417
  5.3 32.1 %collective-permute-start.3 = (bf16[256,2048]{1,0:T(8,128)(2,1)}, bf16[256,2048]{1,0:T(8,128)(2,1)}, u32[]{:S(2)}, u32[]{:S(2)}) collective-permute-start(bf16[256,2048]{1,0:T(8,128)(2,1)} %refs_0_.1), channel_id=1, source_target_pairs={{0,4},{4,0},{8,12},{12,8},{16,20},{20,16},{24,28},{28,24},{1,5},{5... | collective-permute-start | bytes 3145736 | tf_op jit(solution)/shard_map/ppermute | solution.py:428
  28.6 25.0 %collective-permute-start.11 = (bf16[256,2048]{1,0:T(8,128)(2,1)}, bf16[256,2048]{1,0:T(8,128)(2,1)}, u32[]{:S(2)}, u32[]{:S(2)}) collective-permute-start(bf16[256,2048]{1,0:T(8,128)(2,1)} %collective-permute-done.7.refs_4_), channel_id=1, source_target_pairs={{0,4},{4,0},{8,12},{12,8},{16,20},{20,16},{24,28},{28,24},{1,5},{5... | collective-permute-start | bytes 3145736 | tf_op jit(solution)/shard_map/ppermute | solution.py:428
  35.8 42.9 %collective-permute-start.9 = (bf16[256,2048]{1,0:T(8,128)(2,1)}, bf16[256,2048]{1,0:T(8,128)(2,1)S(1)}, u32[]{:S(2)}, u32[]{:S(2)}) collective-permute-start(bf16[256,2048]{1,0:T(8,128)(2,1)} %collective-permute-done.1.refs_2_), channel_id=1, source_target_pairs={{0,8},{4,12},{8,0},{12,4},{16,24},{20,28},{24,16},{28,20},{1,9},{5... | collective-permute-start | bytes 3145736 | tf_op jit(solution)/shard_map/ppermute | solution.py:428
  37.4 41.4 %collective-permute-start.5 = (bf16[256,2048]{1,0:T(8,128)(2,1)}, bf16[256,2048]{1,0:T(8,128)(2,1)S(1)}, u32[]{:S(2)}, u32[]{:S(2)}) collective-permute-start(bf16[256,2048]{1,0:T(8,128)(2,1)} %collective-permute-done.3.refs_0_), channel_id=1, source_target_pairs={{0,2},{1,3},{2,0},{3,1},{4,6},{5,7},{6,4},{7,5},{8,10},{9,11},{10,... | collective-permute-start | bytes 3145736 | tf_op jit(solution)/shard_map/ppermute | solution.py:421
  37.9 41.4 %collective-permute-start.4 = (bf16[256,2048]{1,0:T(8,128)(2,1)}, bf16[256,2048]{1,0:T(8,128)(2,1)S(1)}, u32[]{:S(2)}, u32[]{:S(2)}) collective-permute-start(bf16[256,2048]{1,0:T(8,128)(2,1)} %collective-permute-done.3.refs_0_), channel_id=1, source_target_pairs={{0,1},{1,0},{2,3},{3,2},{4,5},{5,4},{6,7},{7,6},{8,9},{9,8},{10,11... | collective-permute-start | bytes 3145736 | tf_op jit(solution)/shard_map/ppermute | solution.py:417
  37.9 75.0 %collective-permute-start.8 = (bf16[256,2048]{1,0:T(8,128)(2,1)}, bf16[256,2048]{1,0:T(8,128)(2,1)S(1)}, u32[]{:S(2)}, u32[]{:S(2)}) collective-permute-start(bf16[256,2048]{1,0:T(8,128)(2,1)} %collective-permute-done.7.refs_4_), channel_id=1, source_target_pairs={{0,1},{1,0},{2,3},{3,2},{4,5},{5,4},{6,7},{7,6},{8,9},{9,8},{10,11... | collective-permute-start | bytes 3145736 | tf_op jit(solution)/shard_map/ppermute | solution.py:417
  53.6 30.2 %collective-permute-start.13 = (bf16[256,2048]{1,0:T(8,128)(2,1)}, bf16[256,2048]{1,0:T(8,128)(2,1)S(1)}, u32[]{:S(2)}, u32[]{:S(2)}) collective-permute-start(bf16[256,2048]{1,0:T(8,128)(2,1)} %collective-permute-done.11.refs_8_), channel_id=1, source_target_pairs={{0,2},{1,3},{2,0},{3,1},{4,6},{5,7},{6,4},{7,5},{8,10},{9,11},{10,... | collective-permute-start | bytes 3145736 | tf_op jit(solution)/shard_map/ppermute | solution.py:421
  78.7 34.3 %collective-permute-start.12 = (bf16[256,2048]{1,0:T(8,128)(2,1)}, bf16[256,2048]{1,0:T(8,128)(2,1)S(1)}, u32[]{:S(2)}, u32[]{:S(2)}) collective-permute-start(bf16[256,2048]{1,0:T(8,128)(2,1)} %collective-permute-done.11.refs_8_), channel_id=1, source_target_pairs={{0,1},{1,0},{2,3},{3,2},{4,5},{5,4},{6,7},{7,6},{8,9},{9,8},{10,11... | collective-permute-start | bytes 3145736 | tf_op jit(solution)/shard_map/ppermute | solution.py:417
  78.8 34.2 %collective-permute-start.10 = (bf16[256,2048]{1,0:T(8,128)(2,1)S(1)}, bf16[256,2048]{1,0:T(8,128)(2,1)S(1)}, u32[]{:S(2)}, u32[]{:S(2)}) collective-permute-start(bf16[256,2048]{1,0:T(8,128)(2,1)S(1)} %collective-permute-done.9.refs_6_), channel_id=1, source_target_pairs={{0,1},{1,0},{2,3},{3,2},{4,5},{5,4},{6,7},{7,6},{8,9},{9,8},{10,11... | collective-permute-start | bytes 3145736 | tf_op jit(solution)/shard_map/ppermute | solution.py:417
  80.3 32.7 %collective-permute-start.6 = (bf16[256,2048]{1,0:T(8,128)(2,1)S(1)}, bf16[256,2048]{1,0:T(8,128)(2,1)S(1)}, u32[]{:S(2)}, u32[]{:S(2)}) collective-permute-start(bf16[256,2048]{1,0:T(8,128)(2,1)S(1)} %collective-permute-done.5.refs_2_), channel_id=1, source_target_pairs={{0,1},{1,0},{2,3},{3,2},{4,5},{5,4},{6,7},{7,6},{8,9},{9,8},{10,11... | collective-permute-start | bytes 3145736 | tf_op jit(solution)/shard_map/ppermute | solution.py:417
  83.9 29.2 %collective-permute-start.14 = (bf16[256,2048]{1,0:T(8,128)(2,1)S(1)}, bf16[256,2048]{1,0:T(8,128)(2,1)S(1)}, u32[]{:S(2)}, u32[]{:S(2)}) collective-permute-start(bf16[256,2048]{1,0:T(8,128)(2,1)S(1)} %collective-permute-done.13.refs_10_), channel_id=1, source_target_pairs={{0,1},{1,0},{2,3},{3,2},{4,5},{5,4},{6,7},{7,6},{8,9},{9,8},{10,11... | collective-permute-start | bytes 3145736 | tf_op jit(solution)/shard_map/ppermute | solution.py:417
  136.8 62.1 %collective-permute-start.16 = (bf16[256,2048]{1,0:T(8,128)(2,1)}, bf16[256,2048]{1,0:T(8,128)(2,1)}, u32[]{:S(2)}, u32[]{:S(2)}) collective-permute-start(bf16[256,2048]{1,0:T(8,128)(2,1)} %fusion.43), channel_id=1, source_target_pairs={{0,2},{1,3},{2,0},{3,1},{4,6},{5,7},{6,4},{7,5},{8,10},{9,11},{10,... | collective-permute-start | bytes 3145736 | tf_op jit(solution)/shard_map/ppermute | solution.py:425
  141.4 20.9 %collective-permute-start.18 = (f32[8,128]{1,0:T(8,128)S(1)}, f32[8,128]{1,0:T(8,128)S(1)}, u32[]{:S(2)}, u32[]{:S(2)}) collective-permute-start(f32[8,128]{1,0:T(8,128)S(1)} %broadcast_add_fusion), channel_id=1, source_target_pairs={{0,2},{1,3},{2,0},{3,1},{4,6},{5,7},{6,4},{7,5},{8,10},{9,11},{10,... | collective-permute-start | bytes 12296 | tf_op jit(solution)/shard_map/ppermute | solution.py:434
  203.3 31.3 %collective-permute-start.26 = (bf16[256,2048]{1,0:T(8,128)(2,1)S(1)}, bf16[256,2048]{1,0:T(8,128)(2,1)}, u32[]{:S(2)}, u32[]{:S(2)}) collective-permute-start(bf16[256,2048]{1,0:T(8,128)(2,1)S(1)} %fusion.42), channel_id=1, source_target_pairs={{0,2},{1,3},{2,0},{3,1},{4,6},{5,7},{6,4},{7,5},{8,10},{9,11},{10,... | collective-permute-start | bytes 3145736 | tf_op jit(solution)/shard_map/ppermute | solution.py:421
  204.8 29.7 %collective-permute-start.32 = (bf16[256,2048]{1,0:T(8,128)(2,1)S(1)}, bf16[256,2048]{1,0:T(8,128)(2,1)}, u32[]{:S(2)}, u32[]{:S(2)}) collective-permute-start(bf16[256,2048]{1,0:T(8,128)(2,1)S(1)} %fusion.42), channel_id=1, source_target_pairs={{0,8},{4,12},{8,0},{12,4},{16,24},{20,28},{24,16},{28,20},{1,9},{5... | collective-permute-start | bytes 3145736 | tf_op jit(solution)/shard_map/ppermute | solution.py:428
  209.3 24.6 %collective-permute-start.23 = (bf16[1024,128]{1,0:T(8,128)(2,1)S(1)}, bf16[1024,128]{1,0:T(8,128)(2,1)S(1)}, u32[]{:S(2)}, u32[]{:S(2)}) collective-permute-start(bf16[1024,128]{1,0:T(8,128)(2,1)S(1)} %get-tuple-element.330), channel_id=1, source_target_pairs={{0,8},{4,12},{8,0},{12,4},{16,24},{20,28},{24,16},{28,20},{1,9},{5... | collective-permute-start | bytes 786440 | tf_op jit(solution)/shard_map/ppermute | solution.py:428
  210.8 38.0 %collective-permute-start.24 = (bf16[1024,128]{1,0:T(8,128)(2,1)S(1)}, bf16[1024,128]{1,0:T(8,128)(2,1)S(1)}, u32[]{:S(2)}, u32[]{:S(2)}) collective-permute-start(bf16[1024,128]{1,0:T(8,128)(2,1)S(1)} %get-tuple-element.329), channel_id=1, source_target_pairs={{0,12},{4,8},{8,4},{12,0},{16,28},{20,24},{24,20},{28,16},{1,13},{... | collective-permute-start | bytes 786440 | tf_op jit(solution)/shard_map/ppermute | solution.py:428
  217.6 43.1 %collective-permute-start.25 = (bf16[256,2048]{1,0:T(8,128)(2,1)S(1)}, bf16[256,2048]{1,0:T(8,128)(2,1)S(1)}, u32[]{:S(2)}, u32[]{:S(2)}) collective-permute-start(bf16[256,2048]{1,0:T(8,128)(2,1)S(1)} %fusion.42), channel_id=1, source_target_pairs={{0,1},{1,0},{2,3},{3,2},{4,5},{5,4},{6,7},{7,6},{8,9},{9,8},{10,11... | collective-permute-start | bytes 3145736 | tf_op jit(solution)/shard_map/ppermute | solution.py:417
  234.0 26.2 %collective-permute-start.28 = (bf16[256,2048]{1,0:T(8,128)(2,1)S(1)}, bf16[256,2048]{1,0:T(8,128)(2,1)}, u32[]{:S(2)}, u32[]{:S(2)}) collective-permute-start(bf16[256,2048]{1,0:T(8,128)(2,1)S(1)} %fusion.42), channel_id=1, source_target_pairs={{0,4},{4,0},{8,12},{12,8},{16,20},{20,16},{24,28},{28,24},{1,5},{5... | collective-permute-start | bytes 3145736 | tf_op jit(solution)/shard_map/ppermute | solution.py:428
  234.5 27.1 %collective-permute-start.27 = (bf16[256,2048]{1,0:T(8,128)(2,1)}, bf16[256,2048]{1,0:T(8,128)(2,1)}, u32[]{:S(2)}, u32[]{:S(2)}) collective-permute-start(bf16[256,2048]{1,0:T(8,128)(2,1)} %collective-permute-done.26), channel_id=1, source_target_pairs={{0,1},{1,0},{2,3},{3,2},{4,5},{5,4},{6,7},{7,6},{8,9},{9,8},{10,11... | collective-permute-start | bytes 3145736 | tf_op jit(solution)/shard_map/ppermute | solution.py:417
  234.5 43.3 %collective-permute-start.36 = (bf16[256,2048]{1,0:T(8,128)(2,1)}, bf16[256,2048]{1,0:T(8,128)(2,1)}, u32[]{:S(2)}, u32[]{:S(2)}) collective-permute-start(bf16[256,2048]{1,0:T(8,128)(2,1)} %collective-permute-done.32.refs_4_), channel_id=1, source_target_pairs={{0,4},{4,0},{8,12},{12,8},{16,20},{20,16},{24,28},{28,24},{1,5},{5... | collective-permute-start | bytes 3145736 | tf_op jit(solution)/shard_map/ppermute | solution.py:428
  257.9 44.4 %collective-permute-start.34 = (bf16[256,2048]{1,0:T(8,128)(2,1)}, bf16[256,2048]{1,0:T(8,128)(2,1)}, u32[]{:S(2)}, u32[]{:S(2)}) collective-permute-start(bf16[256,2048]{1,0:T(8,128)(2,1)} %collective-permute-done.26), channel_id=1, source_target_pairs={{0,8},{4,12},{8,0},{12,4},{16,24},{20,28},{24,16},{28,20},{1,9},{5... | collective-permute-start | bytes 3145736 | tf_op jit(solution)/shard_map/ppermute | solution.py:428
  260.2 42.0 %collective-permute-start.30 = (bf16[256,2048]{1,0:T(8,128)(2,1)}, bf16[256,2048]{1,0:T(8,128)(2,1)}, u32[]{:S(2)}, u32[]{:S(2)}) collective-permute-start(bf16[256,2048]{1,0:T(8,128)(2,1)} %collective-permute-done.28.refs_0_), channel_id=1, source_target_pairs={{0,2},{1,3},{2,0},{3,1},{4,6},{5,7},{6,4},{7,5},{8,10},{9,11},{10,... | collective-permute-start | bytes 3145736 | tf_op jit(solution)/shard_map/ppermute | solution.py:421
  261.7 41.1 %collective-permute-start.29 = (bf16[256,2048]{1,0:T(8,128)(2,1)}, bf16[256,2048]{1,0:T(8,128)(2,1)}, u32[]{:S(2)}, u32[]{:S(2)}) collective-permute-start(bf16[256,2048]{1,0:T(8,128)(2,1)} %collective-permute-done.28.refs_0_), channel_id=1, source_target_pairs={{0,1},{1,0},{2,3},{3,2},{4,5},{5,4},{6,7},{7,6},{8,9},{9,8},{10,11... | collective-permute-start | bytes 3145736 | tf_op jit(solution)/shard_map/ppermute | solution.py:417
  261.7 66.9 %collective-permute-start.33 = (bf16[256,2048]{1,0:T(8,128)(2,1)}, bf16[256,2048]{1,0:T(8,128)(2,1)}, u32[]{:S(2)}, u32[]{:S(2)}) collective-permute-start(bf16[256,2048]{1,0:T(8,128)(2,1)} %collective-permute-done.32.refs_4_), channel_id=1, source_target_pairs={{0,1},{1,0},{2,3},{3,2},{4,5},{5,4},{6,7},{7,6},{8,9},{9,8},{10,11... | collective-permute-start | bytes 3145736 | tf_op jit(solution)/shard_map/ppermute | solution.py:417
  277.9 28.2 %collective-permute-start.38 = (bf16[256,2048]{1,0:T(8,128)(2,1)}, bf16[256,2048]{1,0:T(8,128)(2,1)}, u32[]{:S(2)}, u32[]{:S(2)}) collective-permute-start(bf16[256,2048]{1,0:T(8,128)(2,1)} %collective-permute-done.36.refs_8_), channel_id=1, source_target_pairs={{0,2},{1,3},{2,0},{3,1},{4,6},{5,7},{6,4},{7,5},{8,10},{9,11},{10,... | collective-permute-start | bytes 3145736 | tf_op jit(solution)/shard_map/ppermute | solution.py:421
  302.2 29.8 %collective-permute-start.37 = (bf16[256,2048]{1,0:T(8,128)(2,1)}, bf16[256,2048]{1,0:T(8,128)(2,1)S(1)}, u32[]{:S(2)}, u32[]{:S(2)}) collective-permute-start(bf16[256,2048]{1,0:T(8,128)(2,1)} %collective-permute-done.36.refs_8_), channel_id=1, source_target_pairs={{0,1},{1,0},{2,3},{3,2},{4,5},{5,4},{6,7},{7,6},{8,9},{9,8},{10,11... | collective-permute-start | bytes 3145736 | tf_op jit(solution)/shard_map/ppermute | solution.py:417
  302.3 26.8 %collective-permute-start.31 = (bf16[256,2048]{1,0:T(8,128)(2,1)}, bf16[256,2048]{1,0:T(8,128)(2,1)S(1)}, u32[]{:S(2)}, u32[]{:S(2)}) collective-permute-start(bf16[256,2048]{1,0:T(8,128)(2,1)} %collective-permute-done.30.refs_2_), channel_id=1, source_target_pairs={{0,1},{1,0},{2,3},{3,2},{4,5},{5,4},{6,7},{7,6},{8,9},{9,8},{10,11... | collective-permute-start | bytes 3145736 | tf_op jit(solution)/shard_map/ppermute | solution.py:417
  302.8 27.9 %collective-permute-start.35 = (bf16[256,2048]{1,0:T(8,128)(2,1)}, bf16[256,2048]{1,0:T(8,128)(2,1)S(1)}, u32[]{:S(2)}, u32[]{:S(2)}) collective-permute-start(bf16[256,2048]{1,0:T(8,128)(2,1)} %collective-permute-done.34.refs_6_), channel_id=1, source_target_pairs={{0,1},{1,0},{2,3},{3,2},{4,5},{5,4},{6,7},{7,6},{8,9},{9,8},{10,11... | collective-permute-start | bytes 3145736 | tf_op jit(solution)/shard_map/ppermute | solution.py:417
  306.1 26.0 %collective-permute-start.39 = (bf16[256,2048]{1,0:T(8,128)(2,1)}, bf16[256,2048]{1,0:T(8,128)(2,1)}, u32[]{:S(2)}, u32[]{:S(2)}) collective-permute-start(bf16[256,2048]{1,0:T(8,128)(2,1)} %collective-permute-done.38.refs_10_), channel_id=1, source_target_pairs={{0,1},{1,0},{2,3},{3,2},{4,5},{5,4},{6,7},{7,6},{8,9},{9,8},{10,11... | collective-permute-start | bytes 3145736 | tf_op jit(solution)/shard_map/ppermute | solution.py:417
  328.5 24.1 %collective-permute-start.40 = (bf16[1024,384]{1,0:T(8,128)(2,1)}, bf16[1024,384]{1,0:T(8,128)(2,1)S(1)}, u32[]{:S(2)}, u32[]{:S(2)}) collective-permute-start(bf16[1024,384]{1,0:T(8,128)(2,1)} %get-tuple-element.310), channel_id=1, source_target_pairs={{0,4},{4,0},{8,12},{12,8},{16,20},{20,16},{24,28},{28,24},{1,5},{5... | collective-permute-start | bytes 2359304 | tf_op jit(solution)/shard_map/ppermute | solution.py:428
  329.1 23.6 %collective-permute-start.41 = (bf16[1024,384]{1,0:T(8,128)(2,1)}, bf16[1024,384]{1,0:T(8,128)(2,1)}, u32[]{:S(2)}, u32[]{:S(2)}) collective-permute-start(bf16[1024,384]{1,0:T(8,128)(2,1)} %get-tuple-element.309), channel_id=1, source_target_pairs={{0,8},{4,12},{8,0},{12,4},{16,24},{20,28},{24,16},{28,20},{1,9},{5... | collective-permute-start | bytes 2359304 | tf_op jit(solution)/shard_map/ppermute | solution.py:428
  330.6 36.2 %collective-permute-start.42 = (bf16[1024,384]{1,0:T(8,128)(2,1)S(1)}, bf16[1024,384]{1,0:T(8,128)(2,1)}, u32[]{:S(2)}, u32[]{:S(2)}) collective-permute-start(bf16[1024,384]{1,0:T(8,128)(2,1)S(1)} %get-tuple-element.308), channel_id=1, source_target_pairs={{0,12},{4,8},{8,4},{12,0},{16,28},{20,24},{24,20},{28,16},{1,13},{... | collective-permute-start | bytes 2359304 | tf_op jit(solution)/shard_map/ppermute | solution.py:428
  366.8 56.3 %collective-permute-start.44 = (bf16[128,2048]{1,0:T(8,128)(2,1)S(1)}, bf16[128,2048]{1,0:T(8,128)(2,1)S(1)}, u32[]{:S(2)}, u32[]{:S(2)}) collective-permute-start(bf16[128,2048]{1,0:T(8,128)(2,1)S(1)} %get-tuple-element.175), channel_id=1, source_target_pairs={{0,16},{4,20},{8,24},{12,28},{16,0},{20,4},{24,8},{28,12},{1,17},{... | collective-permute-start | bytes 1572872 | tf_op jit(solution)/shard_map/ppermute | solution.py:428
  407.4 32.4 %collective-permute-start.43 = (bf16[128,2048]{1,0:T(8,128)(2,1)S(1)}, bf16[128,2048]{1,0:T(8,128)(2,1)S(1)}, u32[]{:S(2)}, u32[]{:S(2)}) collective-permute-start(bf16[128,2048]{1,0:T(8,128)(2,1)S(1)} %get-tuple-element.177), channel_id=1, source_target_pairs={{0,16},{4,20},{8,24},{12,28},{16,0},{20,4},{24,8},{28,12},{1,17},{... | collective-permute-start | bytes 1572872 | tf_op jit(solution)/shard_map/ppermute | solution.py:428
  423.8 20.0 %collective-permute-start.46 = (bf16[128,2048]{1,0:T(8,128)(2,1)S(1)}, bf16[128,2048]{1,0:T(8,128)(2,1)S(1)}, u32[]{:S(2)}, u32[]{:S(2)}) collective-permute-start(bf16[128,2048]{1,0:T(8,128)(2,1)S(1)} %add_convert_fusion.10.refs_0_), channel_id=1, source_target_pairs={{0,8},{4,12},{8,0},{12,4},{16,24},{20,28},{24,16},{28,20},{1,9},{5... | collective-permute-start | bytes 1572872 | tf_op jit(solution)/shard_map/ppermute | solution.py:428
  437.1 24.8 %collective-permute-start.48 = (bf16[128,2048]{1,0:T(8,128)(2,1)}, bf16[128,2048]{1,0:T(8,128)(2,1)S(1)}, u32[]{:S(2)}, u32[]{:S(2)}) collective-permute-start(bf16[128,2048]{1,0:T(8,128)(2,1)} %get-tuple-element.185), channel_id=1, source_target_pairs={{0,16},{4,20},{8,24},{12,28},{16,0},{20,4},{24,8},{28,12},{1,17},{... | collective-permute-start | bytes 1572872 | tf_op jit(solution)/shard_map/ppermute | solution.py:428
  444.6 24.8 %collective-permute-start.50 = (bf16[128,2048]{1,0:T(8,128)(2,1)S(1)}, bf16[128,2048]{1,0:T(8,128)(2,1)S(1)}, u32[]{:S(2)}, u32[]{:S(2)}) collective-permute-start(bf16[128,2048]{1,0:T(8,128)(2,1)S(1)} %add_convert_fusion.9.refs_1_), channel_id=1, source_target_pairs={{0,8},{4,12},{8,0},{12,4},{16,24},{20,28},{24,16},{28,20},{1,9},{5... | collective-permute-start | bytes 1572872 | tf_op jit(solution)/shard_map/ppermute | solution.py:428
  444.6 24.8 %collective-permute-start.51 = (bf16[128,2048]{1,0:T(8,128)(2,1)S(1)}, bf16[128,2048]{1,0:T(8,128)(2,1)S(1)}, u32[]{:S(2)}, u32[]{:S(2)}) collective-permute-start(bf16[128,2048]{1,0:T(8,128)(2,1)S(1)} %collective-permute-done.46.refs_2_), channel_id=1, source_target_pairs={{0,4},{4,0},{8,12},{12,8},{16,20},{20,16},{24,28},{28,24},{1,5},{5... | collective-permute-start | bytes 1572872 | tf_op jit(solution)/shard_map/ppermute | solution.py:428
  456.9 32.6 %collective-permute-start.47 = (bf16[128,2048]{1,0:T(8,128)(2,1)}, bf16[128,2048]{1,0:T(8,128)(2,1)}, u32[]{:S(2)}, u32[]{:S(2)}) collective-permute-start(bf16[128,2048]{1,0:T(8,128)(2,1)} %get-tuple-element.184), channel_id=1, source_target_pairs={{0,16},{4,20},{8,24},{12,28},{16,0},{20,4},{24,8},{28,12},{1,17},{... | collective-permute-start | bytes 1572872 | tf_op jit(solution)/shard_map/ppermute | solution.py:428
  472.9 22.4 %collective-permute-start.53 = (bf16[128,2048]{1,0:T(8,128)(2,1)S(1)}, bf16[128,2048]{1,0:T(8,128)(2,1)}, u32[]{:S(2)}, u32[]{:S(2)}) collective-permute-start(bf16[128,2048]{1,0:T(8,128)(2,1)S(1)} %add_convert_fusion.8.refs_1_), channel_id=1, source_target_pairs={{0,8},{4,12},{8,0},{12,4},{16,24},{20,28},{24,16},{28,20},{1,9},{5... | collective-permute-start | bytes 1572872 | tf_op jit(solution)/shard_map/ppermute | solution.py:428
  501.3 27.8 %collective-permute-start.61 = (bf16[256,2048]{1,0:T(8,128)(2,1)S(1)}, bf16[256,2048]{1,0:T(8,128)(2,1)S(1)}, u32[]{:S(2)}, u32[]{:S(2)}) collective-permute-start(bf16[256,2048]{1,0:T(8,128)(2,1)S(1)} %fusion.44), channel_id=1, source_target_pairs={{0,2},{1,3},{2,0},{3,1},{4,6},{5,7},{6,4},{7,5},{8,10},{9,11},{10,... | collective-permute-start | bytes 3145736 | tf_op jit(solution)/shard_map/ppermute | solution.py:425
  503.1 31.4 %collective-permute-start.56 = (bf16[128,2048]{1,0:T(8,128)(2,1)S(1)}, bf16[128,2048]{1,0:T(8,128)(2,1)S(1)}, u32[]{:S(2)}, u32[]{:S(2)}) collective-permute-start(bf16[128,2048]{1,0:T(8,128)(2,1)S(1)} %copy-done.47), channel_id=1, source_target_pairs={{0,16},{4,20},{8,24},{12,28},{16,0},{20,4},{24,8},{28,12},{1,17},{... | collective-permute-start | bytes 1572872 | tf_op jit(solution)/shard_map/ppermute | solution.py:428
  506.7 20.9 %collective-permute-start.66 = (f32[12288]{0:T(1024)S(1)}, f32[12288]{0:T(1024)S(1)}, u32[]{:S(2)}, u32[]{:S(2)}) collective-permute-start(f32[12288]{0:T(1024)S(1)} %add.335), channel_id=1, source_target_pairs={{0,2},{1,3},{2,0},{3,1},{4,6},{5,7},{6,4},{7,5},{8,10},{9,11},{10,... | collective-permute-start | bytes 147464 | tf_op jit(solution)/shard_map/ppermute | solution.py:434
  509.6 25.5 %collective-permute-start.57 = (bf16[128,2048]{1,0:T(8,128)(2,1)S(1)}, bf16[128,2048]{1,0:T(8,128)(2,1)S(1)}, u32[]{:S(2)}, u32[]{:S(2)}) collective-permute-start(bf16[128,2048]{1,0:T(8,128)(2,1)S(1)} %add_convert_fusion.7.refs_1_), channel_id=1, source_target_pairs={{0,4},{4,0},{8,12},{12,8},{16,20},{20,16},{24,28},{28,24},{1,5},{5... | collective-permute-start | bytes 1572872 | tf_op jit(solution)/shard_map/ppermute | solution.py:428
  511.1 24.4 %collective-permute-start.58 = (bf16[128,2048]{1,0:T(8,128)(2,1)S(1)}, bf16[128,2048]{1,0:T(8,128)(2,1)S(1)}, u32[]{:S(2)}, u32[]{:S(2)}) collective-permute-start(bf16[128,2048]{1,0:T(8,128)(2,1)S(1)} %add_convert_fusion.7.refs_1_), channel_id=1, source_target_pairs={{0,8},{4,12},{8,0},{12,4},{16,24},{20,28},{24,16},{28,20},{1,9},{5... | collective-permute-start | bytes 1572872 | tf_op jit(solution)/shard_map/ppermute | solution.py:428
  529.1 43.7 %collective-permute-start.55 = (bf16[512,512]{1,0:T(8,128)(2,1)S(1)}, bf16[512,512]{1,0:T(8,128)(2,1)S(1)}, u32[]{:S(2)}, u32[]{:S(2)}) collective-permute-start(bf16[512,512]{1,0:T(8,128)(2,1)S(1)} %copy-done.51), channel_id=1, source_target_pairs={{0,16},{4,20},{8,24},{12,28},{16,0},{20,4},{24,8},{28,12},{1,17},{... | collective-permute-start | bytes 1572872 | tf_op jit(solution)/shard_map/ppermute | solution.py:428
  541.8 31.0 %collective-permute-start.62 = (bf16[128,2048]{1,0:T(8,128)(2,1)S(1)}, bf16[128,2048]{1,0:T(8,128)(2,1)S(1)}, u32[]{:S(2)}, u32[]{:S(2)}) collective-permute-start(bf16[128,2048]{1,0:T(8,128)(2,1)S(1)} %add_convert_fusion.6.refs_0_), channel_id=1, source_target_pairs={{0,4},{4,0},{8,12},{12,8},{16,20},{20,16},{24,28},{28,24},{1,5},{5... | collective-permute-start | bytes 1572872 | tf_op jit(solution)/shard_map/ppermute | solution.py:428
  543.3 29.5 %collective-permute-start.63 = (bf16[128,2048]{1,0:T(8,128)(2,1)S(1)}, bf16[128,2048]{1,0:T(8,128)(2,1)S(1)}, u32[]{:S(2)}, u32[]{:S(2)}) collective-permute-start(bf16[128,2048]{1,0:T(8,128)(2,1)S(1)} %add_convert_fusion.6.refs_0_), channel_id=1, source_target_pairs={{0,8},{4,12},{8,0},{12,4},{16,24},{20,28},{24,16},{28,20},{1,9},{5... | collective-permute-start | bytes 1572872 | tf_op jit(solution)/shard_map/ppermute | solution.py:428
  544.1 28.7 %collective-permute-start.64 = (bf16[128,2048]{1,0:T(8,128)(2,1)S(1)}, bf16[128,2048]{1,0:T(8,128)(2,1)S(1)}, u32[]{:S(2)}, u32[]{:S(2)}) collective-permute-start(bf16[128,2048]{1,0:T(8,128)(2,1)S(1)} %collective-permute-done.58.refs_3_), channel_id=1, source_target_pairs={{0,4},{4,0},{8,12},{12,8},{16,20},{20,16},{24,28},{28,24},{1,5},{5... | collective-permute-start | bytes 1572872 | tf_op jit(solution)/shard_map/ppermute | solution.py:428
  545.6 21.4 %collective-permute-start.68 = (f32[15872]{0:T(1024)S(1)}, f32[15872]{0:T(1024)S(1)}, u32[]{:S(2)}, u32[]{:S(2)}) collective-permute-start(f32[15872]{0:T(1024)S(1)} %fusion.53), channel_id=1, source_target_pairs={{0,8},{4,12},{8,0},{12,4},{16,24},{20,28},{24,16},{28,20},{1,9},{5... | collective-permute-start | bytes 190472 | tf_op jit(solution)/shard_map/ppermute | solution.py:428
  572.7 25.9 %collective-permute-start.70 = (bf16[512,512]{1,0:T(8,128)(2,1)S(1)}, bf16[512,512]{1,0:T(8,128)(2,1)S(1)}, u32[]{:S(2)}, u32[]{:S(2)}) collective-permute-start(bf16[512,512]{1,0:T(8,128)(2,1)S(1)} %copy-done.50), channel_id=1, source_target_pairs={{0,16},{4,20},{8,24},{12,28},{16,0},{20,4},{24,8},{28,12},{1,17},{... | collective-permute-start | bytes 1572872 | tf_op jit(solution)/shard_map/ppermute | solution.py:428
  572.9 25.6 %collective-permute-start.71 = (bf16[512,512]{1,0:T(8,128)(2,1)S(1)}, bf16[512,512]{1,0:T(8,128)(2,1)S(1)}, u32[]{:S(2)}, u32[]{:S(2)}) collective-permute-start(bf16[512,512]{1,0:T(8,128)(2,1)S(1)} %add_convert_fusion.5.refs_0_), channel_id=1, source_target_pairs={{0,4},{4,0},{8,12},{12,8},{16,20},{20,16},{24,28},{28,24},{1,5},{5... | collective-permute-start | bytes 1572872 | tf_op jit(solution)/shard_map/ppermute | solution.py:428
  574.0 24.6 %collective-permute-start.72 = (bf16[512,512]{1,0:T(8,128)(2,1)S(1)}, bf16[512,512]{1,0:T(8,128)(2,1)S(1)}, u32[]{:S(2)}, u32[]{:S(2)}) collective-permute-start(bf16[512,512]{1,0:T(8,128)(2,1)S(1)} %add_convert_fusion.5.refs_0_), channel_id=1, source_target_pairs={{0,8},{4,12},{8,0},{12,4},{16,24},{20,28},{24,16},{28,20},{1,9},{5... | collective-permute-start | bytes 1572872 | tf_op jit(solution)/shard_map/ppermute | solution.py:428
  576.4 22.2 %collective-permute-start.73 = (bf16[128,2048]{1,0:T(8,128)(2,1)S(1)}, bf16[128,2048]{1,0:T(8,128)(2,1)S(1)}, u32[]{:S(2)}, u32[]{:S(2)}) collective-permute-start(bf16[128,2048]{1,0:T(8,128)(2,1)S(1)} %collective-permute-done.63.refs_2_), channel_id=1, source_target_pairs={{0,4},{4,0},{8,12},{12,8},{16,20},{20,16},{24,28},{28,24},{1,5},{5... | collective-permute-start | bytes 1572872 | tf_op jit(solution)/shard_map/ppermute | solution.py:428
  579.3 44.3 %collective-permute-start.75 = (bf16[512,512]{1,0:T(8,128)(2,1)S(1)}, bf16[512,512]{1,0:T(8,128)(2,1)S(1)}, u32[]{:S(2)}, u32[]{:S(2)}) collective-permute-start(bf16[512,512]{1,0:T(8,128)(2,1)S(1)} %copy-done.49), channel_id=1, source_target_pairs={{0,16},{4,20},{8,24},{12,28},{16,0},{20,4},{24,8},{28,12},{1,17},{... | collective-permute-start | bytes 1572872 | tf_op jit(solution)/shard_map/ppermute | solution.py:428
  598.7 24.9 %collective-permute-start.76 = (bf16[512,512]{1,0:T(8,128)(2,1)S(1)}, bf16[512,512]{1,0:T(8,128)(2,1)S(1)}, u32[]{:S(2)}, u32[]{:S(2)}) collective-permute-start(bf16[512,512]{1,0:T(8,128)(2,1)S(1)} %add_convert_fusion.4.refs_1_), channel_id=1, source_target_pairs={{0,4},{4,0},{8,12},{12,8},{16,20},{20,16},{24,28},{28,24},{1,5},{5... | collective-permute-start | bytes 1572872 | tf_op jit(solution)/shard_map/ppermute | solution.py:428
  606.8 34.5 %collective-permute-start.74 = (bf16[512,512]{1,0:T(8,128)(2,1)S(1)}, bf16[512,512]{1,0:T(8,128)(2,1)S(1)}, u32[]{:S(2)}, u32[]{:S(2)}) collective-permute-start(bf16[512,512]{1,0:T(8,128)(2,1)S(1)} %copy-done.48), channel_id=1, source_target_pairs={{0,16},{4,20},{8,24},{12,28},{16,0},{20,4},{24,8},{28,12},{1,17},{... | collective-permute-start | bytes 1572872 | tf_op jit(solution)/shard_map/ppermute | solution.py:428
  627.1 21.1 %collective-permute-start.80 = (bf16[512,512]{1,0:T(8,128)(2,1)S(1)}, bf16[512,512]{1,0:T(8,128)(2,1)S(1)}, u32[]{:S(2)}, u32[]{:S(2)}) collective-permute-start(bf16[512,512]{1,0:T(8,128)(2,1)S(1)} %add_convert_fusion.3.refs_1_), channel_id=1, source_target_pairs={{0,8},{4,12},{8,0},{12,4},{16,24},{20,28},{24,16},{28,20},{1,9},{5... | collective-permute-start | bytes 1572872 | tf_op jit(solution)/shard_map/ppermute | solution.py:428
  627.1 21.6 %collective-permute-start.81 = (bf16[512,512]{1,0:T(8,128)(2,1)S(1)}, bf16[512,512]{1,0:T(8,128)(2,1)S(1)}, u32[]{:S(2)}, u32[]{:S(2)}) collective-permute-start(bf16[512,512]{1,0:T(8,128)(2,1)S(1)} %collective-permute-done.77.refs_3_), channel_id=1, source_target_pairs={{0,4},{4,0},{8,12},{12,8},{16,20},{20,16},{24,28},{28,24},{1,5},{5... | collective-permute-start | bytes 1572872 | tf_op jit(solution)/shard_map/ppermute | solution.py:428
  649.3 22.4 %collective-permute-start.86 = (bf16[512,512]{1,0:T(8,128)(2,1)S(1)}, bf16[512,512]{1,0:T(8,128)(2,1)S(1)}, u32[]{:S(2)}, u32[]{:S(2)}) collective-permute-start(bf16[512,512]{1,0:T(8,128)(2,1)S(1)} %collective-permute-done.80.refs_3_), channel_id=1, source_target_pairs={{0,4},{4,0},{8,12},{12,8},{16,20},{20,16},{24,28},{28,24},{1,5},{5... | collective-permute-start | bytes 1572872 | tf_op jit(solution)/shard_map/ppermute | solution.py:428
  (135 other events, 2517.3 us)

commit v4 on v3

--- a/solution.py
+++ b/solution.py
@@ -61,59 +61,62 @@
     return jnp.concatenate([moved, block[:, 128:]], axis=1)
 
 
-def qkv_kernel(x_ref, w_ref, b_ref, keep_ref, up_ref, down_ref, o_ref):
+def qkv_kernel(x_ref, w_ref, b_ref, keep_ref, up_ref, down_ref, *refs):
+    o_ref = refs[-1]
     kind = pl.program_id(0) % 3
-    tile = o_ref.shape[0] // 4
-
-    def rows_at(i):
-        return pl.ds(pl.multiple_of(i * tile, tile), tile)
-
-    def project(i):
+    rows = x_ref.shape[0]
+    tile = min(rows, 512)
+
+    def project(at):
         return (
-            jnp.dot(x_ref[rows_at(i), :], w_ref[...], preferred_element_type=F32) + b_ref[...]
+            jnp.dot(x_ref[at, :], w_ref[...], preferred_element_type=F32) + b_ref[...]
         )
 
-    @pl.when(kind == 2)
-    def _():
-        @pl.loop(0, 4)
-        def _(i):
-            o_ref[rows_at(i), :] = project(i).astype(BF)
-
-    @pl.when(kind != 2)
-    def _():
-        @pl.loop(0, 4)
-        def _(i):
-            at = rows_at(i)
+    for start in range(0, rows, tile):
+        at = pl.ds(start, min(tile, rows - start))
+
+        @pl.when(kind == 2)
+        def _(at=at):
+            o_ref[at, :] = project(at).astype(BF)
+
+        @pl.when(kind != 2)
+        def _(at=at):
             o_ref[at, :] = turned(
-                project(i), keep_ref[at, :], up_ref[at, :], down_ref[at, :], 1.0
+                project(at), keep_ref[at, :], up_ref[at, :], down_ref[at, :], 1.0
             ).astype(BF)
 
 
-def project_qkv(normed, weight, bias, tables):
-    length, width = normed.shape
+def project_qkv(normed, weight, bias, tables, length, whole=None):
+    rows, width = normed.shape
     columns = weight.shape[1]
-    table = pl.BlockSpec((length, 128), lambda j: (0, 0))
+    part = 0 if whole is None else 1
+    if part and rows * 2 != length:
+        rest = project_qkv(normed, weight, bias, tables, rows)
+        return jnp.concatenate([whole[: length - rows], rest], axis=0)
+    table = pl.BlockSpec((rows, 128), lambda j: (0, 0))
     return pl.pallas_call(
         qkv_kernel,
         grid=(columns // HD,),
         in_specs=[
-            pl.BlockSpec((length, width), lambda j: (0, 0)),
+            pl.BlockSpec((rows, width), lambda j: (0, 0)),
             pl.BlockSpec((width, HD), lambda j: (0, j)),
             pl.BlockSpec((1, HD), lambda j: (0, j)),
             table,
             table,
             table,
-        ],
-        out_specs=pl.BlockSpec((length, HD), lambda j: (0, j)),
+        ]
+        + [pl.BlockSpec(memory_space=pl.ANY)] * part,
+        out_specs=pl.BlockSpec((rows, HD), lambda j: (part, j)),
         out_shape=jax.ShapeDtypeStruct((length, columns), BF),
+        input_output_aliases={6: 0} if part else {},
         compiler_params=pltpu.CompilerParams(vmem_limit_bytes=40 << 20),
         cost_estimate=pl.CostEstimate(
-            flops=2 * length * width * columns,
-            bytes_accessed=2 * (length * width + width * columns + length * columns),
+            flops=2 * rows * width * columns,
+            bytes_accessed=2 * (rows * width + width * columns + rows * columns),
             transcendentals=0,
         ),
         name="qkv_rotary",
-    )(normed, weight, bias.astype(F32)[None, :], *tables)
+    )(normed, weight, bias.astype(F32)[None, :], *tables, *([whole] if part else []))
 
 
 def visible_scores(queries, keys, row_spots, key_spots, prefix):
@@ -316,18 +319,28 @@
 
 
 def outer_kernel(near_ref, far_ref, right_ref, *refs):
-    rights, o_ref = refs[:-1], refs[-1]
-    total = contract(near_ref[...], right_ref[...], 0, 0)
+    rights, (o_ref, left_ref, joined_ref) = refs[:-3], refs[-3:]
+    near = near_ref.shape[0]
     rows = rights[0].shape[0]
+
+    @pl.when(pl.program_id(0) == 0)
+    def _():
+        for start in range(0, near, rows):
+            left_ref[:, pl.ds(start, rows)] = near_ref[pl.ds(start, rows), :].T
+        for start in range(0, far_ref.shape[0], rows):
+            left_ref[:, pl.ds(near + start, rows)] = far_ref[pl.ds(start, rows), :].T
+
+    joined_ref[:near, :] = right_ref[...]
     for index, right in enumerate(rights):
-        total += contract(far_ref[pl.ds(index * rows, rows), :], right[...], 0, 0)
-    o_ref[...] = total.astype(BF)
+        joined_ref[pl.ds(near + index * rows, rows), :] = right[...]
+    o_ref[...] = jnp.dot(left_ref[...], joined_ref[...], preferred_element_type=F32).astype(BF)
 
 
 def outer_blocks(near, far, near_right, far_blocks):
     length, left = near.shape
     width = near_right.shape[1]
     rows = far_blocks[0].shape[0]
+    tokens = length + far.shape[0]
     tile = 512
     return pl.pallas_call(
         outer_kernel,
@@ -340,10 +353,11 @@
         + [pl.BlockSpec((rows, tile), lambda j: (0, j))] * len(far_blocks),
         out_specs=pl.BlockSpec((left, tile), lambda j: (0, j)),
         out_shape=jax.ShapeDtypeStruct((left, width), BF),
+        scratch_shapes=[pltpu.VMEM((left, tokens), BF), pltpu.VMEM((tokens, tile), BF)],
         compiler_params=pltpu.CompilerParams(vmem_limit_bytes=56 << 20),
         cost_estimate=pl.CostEstimate(
-            flops=2 * (length + far.shape[0]) * left * width,
-            bytes_accessed=2 * (length + far.shape[0]) * (left + width),
+            flops=2 * tokens * left * width,
+            bytes_accessed=2 * tokens * (left + width),
             transcendentals=0,
         ),
         name="outer_blocks",
@@ -427,21 +441,6 @@
     def flip(v, mask):
         return lax.ppermute(v, "dp", [(d, d ^ mask) for d in range(dp)])
 
-    def tensor_sum(v):
-        v = v + to_core(v)
-        bit = 2
-        while bit < tp:
-            v = v + lax.ppermute(v, "tensor", [(t, t ^ bit) for t in range(tp)])
-            bit *= 2
-        return v
-
-    def dp_sum(v):
-        bit = 1
-        while bit < dp:
-            v = v + flip(v, bit)
-            bit *= 2
-        return v
-
     block_ids = [
         ((y + step) % ways) * 2 + (core if mate == 0 else 1 - core)
         for step in range(ways)
@@ -449,25 +448,28 @@
     ]
 
     def gather_near(own):
-        parts, over_y = [own, to_core(own)], []
-        for step in range(1, ways):
-            over_y.append(from_y(own, step))
-            parts += [over_y[-1], to_core(over_y[-1])]
+        over_y = [from_y(own, step) for step in range(1, ways)]
+        parts = []
+        for block in [own] + over_y:
+            parts += [block, to_core(block)]
         return parts, over_y
 
-    def gather_far(own, over_y):
-        first = [flip(own, 1), flip(own, 2)]
-        first.append(flip(first[1], 1))
-        rounds_y = [first]
-        for step in range(1, ways):
-            rounds_y.append(
-                [from_y(first[0], step), flip(over_y[step - 1], 2), from_y(first[2], step)]
-            )
-        parts = [[], [], []]
-        for blocks in rounds_y:
-            for i in range(3):
-                parts[i] += [blocks[i], to_core(blocks[i])]
-        return parts[0] + parts[1] + parts[2]
+    def first_far(own):
+        return [flip(own, 1), flip(own, 2)]
+
+    def second_far(first, over_y):
+        corner = flip(first[1], 1)
+        beside = [from_y(first[0], step) for step in range(1, ways)]
+        across = [flip(block, 2) for block in over_y]
+        return corner, beside, across
+
+    def far_parts(first, second, last):
+        corner, beside, across = second
+        parts = []
+        for blocks in ([first[0]] + beside, [first[1]] + across, [corner] + last):
+            for block in blocks:
+                parts += [block, to_core(block)]
+        return parts
 
     def quarter_of(v, axis, index):
         size = v.shape[axis] // 4
@@ -481,14 +483,13 @@
     gain_mlp = ln2_gain.astype(F32)
     shift_mlp = ln2_bias.astype(F32)
     mask_f = valid_mask.astype(F32)
-    count_all = dp_sum(tensor_sum(jnp.full((8, 128), jnp.sum(mask_f), F32)))[0, 0]
-
     gains = jnp.pad(
         jnp.stack([gain_attn, shift_attn, gain_mlp, shift_mlp]), ((0, 4), (0, 0))
     )
+    count = jnp.full((8, 128), jnp.sum(mask_f), F32)
     near_blocks, hidden_y = gather_near(hidden)
-    far_blocks = gather_far(hidden, hidden_y)
-    norm_attn, norm_mlp = both_norms(near_blocks, gains)
+    first = first_far(hidden)
+    count = count + to_core(count)
 
     cosine_all, sine_all = rotary_tables(LEN, ROT)
 
@@ -499,52 +500,112 @@
 
     tables = rotary_lanes(in_order(cosine_all), in_order(sine_all))
     spots = jnp.concatenate([b * rows + jnp.arange(rows, dtype=jnp.int32) for b in block_ids])
-    qkv_low = project_qkv(norm_attn, qkv_weight, qkv_bias, tables)
+    close = 2 * rows
+
+    def units(normed):
+        return jnp.dot(normed, fc1_weight, preferred_element_type=F32) + fc1_bias.astype(F32)
+
+    norm_attn_own, norm_mlp_own = both_norms(near_blocks[:2], gains)
+    pre_own = units(norm_mlp_own)
+    active_own = exact_gelu(pre_own)[0].astype(BF)
+    qkv_own = project_qkv(norm_attn_own, qkv_weight, qkv_bias, [t[:close] for t in tables], LEN)
+
+    arrived = lax.optimization_barrier(
+        (active_own, qkv_own, count, *first, *near_blocks[2:])
+    )
+    active_own, qkv_own, count, *rest = arrived
+    first, rest_blocks = rest[:2], rest[2:]
+    count = count + flip(count, 1)
+    norm_attn_rest, norm_mlp_rest = both_norms(rest_blocks, gains)
+    count, norm_attn_rest = lax.optimization_barrier((count, norm_attn_rest))
+    count = count + flip(count, 2)
+    qkv_low = project_qkv(
+        norm_attn_rest, qkv_weight, qkv_bias, [t[close:] for t in tables], LEN, qkv_own
+    )
+    count, qkv_low = lax.optimization_barrier((count, qkv_low))
+    mask = 4
+    while mask < dp:
+        count = count + flip(count, mask)
+        mask *= 2
     context, log_total = attend(qkv_low, prefix_len, spots)
-    hidden_pre = jnp.dot(norm_mlp, fc1_weight, preferred_element_type=F32) + fc1_bias.astype(F32)
-    active, slope = exact_gelu(hidden_pre)
-    active = active.astype(BF)
-    active, *far_blocks = lax.optimization_barrier((active, *far_blocks))
-    branch_part = jnp.dot(context, out_weight, preferred_element_type=F32) + jnp.dot(
-        active, fc2_weight, preferred_element_type=F32
-    )
-
-    def scatter_rows(part, meanwhile=None):
-        blocks = part.reshape(ways, 2, rows, D)
-        mine = blocks[:, 0] + to_core(blocks[:, 1].astype(BF)).astype(F32)
-        total = mine[0]
-        side_work = None
-        for step in range(1, ways):
-            low = mine[step].astype(BF)
-            got = to_y(low, step)
-            if meanwhile is not None and step == 1:
-                side_work = meanwhile(low)
-                got = after(got, *side_work)
-            total = total + got.astype(F32)
-        return total, side_work
-
-    branch, (norm_attn_far, norm_mlp_far) = scatter_rows(
-        branch_part,
-        lambda sent: both_norms([after(far_blocks[0], sent)] + far_blocks[1:], gains),
-    )
+    count, context, *first = lax.optimization_barrier((count, context, *first))
+    second = second_far(first, hidden_y)
+    context_far = swap_quarters(context)
+    bit = 2
+    while bit < tp:
+        count = count + lax.ppermute(count, "tensor", [(t, t ^ bit) for t in range(tp)])
+        bit *= 2
+    pre_rest = units(norm_mlp_rest)
+    active_rest = exact_gelu(pre_rest)[0].astype(BF)
+    active_rest, count, *corner = lax.optimization_barrier((active_rest, count, second[0]))
+    count_all = count[0, 0]
+    last = [from_y(corner[0], step) for step in range(1, ways)]
+    far_blocks = far_parts(first, (corner[0], second[1], second[2]), last)
+
+    def branch_rows(context_rows, active_rows):
+        return jnp.dot(context_rows, out_weight, preferred_element_type=F32) + jnp.dot(
+            active_rows, fc2_weight, preferred_element_type=F32
+        )
+
+    def core_total(part):
+        blocks = part.reshape(-1, 2, rows, D)
+        return blocks[:, 0] + to_core(blocks[:, 1].astype(BF)).astype(F32)
+
+    sums = core_total(branch_rows(context[close:], active_rest))
+    leaving = [sums[step - 1].astype(BF) for step in range(1, ways)]
+    came = [to_y(low, step) for step, low in enumerate(leaving, 1)]
+    active_now, context_now, *far_blocks = lax.optimization_barrier(
+        (active_own, context[:close], *far_blocks, leaving[0])
+    )[:-1]
+    branch = core_total(branch_rows(context_now, active_now))[0]
+    far_blocks[0] = after(far_blocks[0], branch)
+    norm_attn_far, norm_mlp_far = both_norms(far_blocks, gains)
+    fc1_quarter = quarter_of(fc1_weight, 1, quarter)
+    fc2_quarter = quarter_of(fc2_weight, 0, quarter)
+    pre_far = jnp.dot(norm_mlp_far, fc1_quarter, preferred_element_type=F32) + quarter_of(
+        fc1_bias, 0, quarter
+    ).astype(F32)
+    active_far, slope_far = exact_gelu(pre_far)
+    active_far = active_far.astype(BF)
+    left_far = jnp.concatenate([active_far, jnp.concatenate(context_far, axis=0)], axis=1)
+    left_near = jnp.concatenate(
+        [
+            jnp.concatenate(
+                [quarter_of(active_own, 1, quarter), quarter_of(active_rest, 1, quarter)], axis=0
+            ),
+            quarter_of(context, 1, quarter),
+        ],
+        axis=1,
+    )
+    came = lax.optimization_barrier((*came, left_far, left_near))
+    (*came, left_far, left_near) = came
+    for got in came:
+        branch = branch + got.astype(F32)
+
     output_f = hidden.astype(F32) + branch + out_bias.astype(F32) + fc2_bias.astype(F32)
     mismatch = output_f - teacher.astype(F32)
     error_part = jnp.sum(mask_f[:, None] * mismatch * mismatch)
     grad_out = mask_f[:, None] * mismatch * (2.0 * total_tokens / count_all)
-    bias_part = jnp.sum(grad_out, axis=0)
     grad_low = grad_out.astype(BF)
     grad_blocks, grad_y = gather_near(grad_low)
+    grad_first = first_far(grad_low)
+    tied = lax.optimization_barrier((*grad_first, *grad_blocks, *grad_y))
+    grad_first, tied = list(tied[:2]), tied[2:]
+    grad_blocks, grad_y = list(tied[: 2 * ways]), list(tied[2 * ways :])
+    grad_second = second_far(grad_first, grad_y)
     grad_near = jnp.concatenate(grad_blocks, axis=0)
-    grad_far = gather_far(grad_low, grad_y)
-
-    fc1_quarter = quarter_of(fc1_weight, 1, quarter)
-    fc2_quarter = quarter_of(fc2_weight, 0, quarter)
-    pre_far = jnp.dot(
-        after(norm_mlp_far, grad_low), fc1_quarter, preferred_element_type=F32
-    ) + quarter_of(fc1_bias, 0, quarter).astype(F32)
-    active_far, slope_far = exact_gelu(pre_far)
-    active_far = active_far.astype(BF)
-    context_far = jnp.concatenate(swap_quarters(context), axis=0)
+    hidden_pre = jnp.concatenate([pre_own, pre_rest], axis=0)
+    grad_inner = (contract(grad_near, fc2_weight, 1, 1) * exact_gelu(hidden_pre)[1]).astype(BF)
+    grad_context = contract(grad_near, out_weight, 1, 1).astype(BF)
+    grad_inner, grad_context, corner, *tied = lax.optimization_barrier(
+        (grad_inner, grad_context, grad_second[0], *grad_second[1], *grad_second[2])
+    )
+    grad_second = (corner, list(tied[: ways - 1]), list(tied[ways - 1 :]))
+    grad_last = [from_y(corner, step) for step in range(1, ways)]
+    grad_far = far_parts(grad_first, grad_second, grad_last)
+    grad_qkv = attend_back(qkv_low, grad_context, log_total, prefix_len, spots, tables)
+    grad_qkv, *grad_far = lax.optimization_barrier((grad_qkv, *grad_far))
+    bias_part = jnp.sum(grad_out, axis=0)
 
     queue = []
     due = {}
@@ -555,15 +616,54 @@
     def gate(v):
         return after(v, token[0])
 
+    def flipped(v, mask):
+        return v, lambda value: flip(value, mask)
+
     def travel(name, low):
         mask = 4
         while mask < dp:
-            (got,) = yield [(low, mask)], 2
+            (got,) = yield [flipped(low, mask)], 2
             low = (low.astype(F32) + got.astype(F32)).astype(BF)
             mask *= 2
-        beside, across = yield [(low, 1), (low, 2)], 1
-        (corner,) = yield [(across, 1)], 1
+        beside, across = yield [flipped(low, 1), flipped(low, 2)], 1
+        (corner,) = yield [flipped(across, 1)], 1
         results.setdefault(name, []).append((low, beside, across, corner))
+
+    def swap_walk(v, into):
+        got = yield [flipped(quarter_of(v, 1, quarter ^ m), m) for m in (1, 2, 3)], 3
+        into.extend(got)
+
+    def scatter_walk(kept, mates, into):
+        (got,) = yield [(mates, to_core)], 1
+        sums = kept + got.astype(F32)
+        total = sums[0]
+        for step in range(1, ways):
+            (got,) = yield [(sums[step].astype(BF), lambda v, s=step: to_y(v, s))], 2
+            total = total + got.astype(F32)
+        into["input"] = grad_out + total
+
+    def small_walk(parts, others, into):
+        bit = 1
+        while bit < tp:
+            pairs = [(t, t ^ bit) for t in range(tp)]
+            (got,) = yield [(parts, lambda v, p=pairs: lax.ppermute(v, "tensor", p))], 1
+            parts = parts + got
+            bit *= 2
+        parts = jnp.concatenate([parts, others])
+        bit = 1
+        while bit < dp:
+            (got,) = yield [flipped(parts, bit)], 1
+            parts = parts + got
+            bit *= 2
+        into["small"] = parts
+
+    def walk(walker):
+        asked = next(walker)
+        start(walker, asked, clock[0] - 1)
+
+    def start(walker, asked, now):
+        sends, wait = asked
+        due.setdefault(now + wait, []).append((walker, [move(v) for v, move in sends]))
 
     def enqueue(name, part, count):
         size = part.shape[0] // count
@@ -590,8 +690,8 @@
         if len(values) > sum(len(gots) for _, gots in arrived):
             walker = travel(name, tied.pop(0))
             asked.append((walker, next(walker)))
-        for walker, (sends, wait) in asked:
-            due.setdefault(now + wait, []).append((walker, [flip(v, mask) for v, mask in sends]))
+        for walker, request in asked:
+            start(walker, request, now)
         return tied
 
     placed = {}
@@ -624,50 +724,51 @@
             whole = lax.dynamic_update_slice(whole, piece.astype(F32), start)
         return whole
 
-    grad_inner = (contract(grad_near, fc2_weight, 1, 1) * slope).astype(BF)
-    grad_context = contract(grad_near, out_weight, 1, 1).astype(BF)
-    grad_qkv = attend_back(qkv_low, grad_context, log_total, prefix_len, spots, tables)
-    grad_qkv_far = swap_quarters(grad_qkv)
-    left_near = jnp.concatenate(
-        [quarter_of(active, 1, quarter), quarter_of(context, 1, quarter)], axis=1
-    )
-    left_far = jnp.concatenate([active_far, context_far], axis=1)
     part = outer_blocks(left_near, left_far, grad_near, grad_far)
-    units = active_far.shape[1]
-    enqueue("fc2", part[:units], 4)
-    enqueue("out", part[units:], 1)
-    grad_inner, *grad_qkv_far = turn(grad_inner, *grad_qkv_far)
-
+    mine = active_far.shape[1]
+    enqueue("fc2", part[:mine], 4)
+    enqueue("out", part[mine:], 1)
+    turn()
+    grad_qkv_far = []
+    walk(swap_walk(grad_qkv, grad_qkv_far))
     grad_inner_far = back_blocks([gate(grad_far[0])] + grad_far[1:], fc2_quarter, slope_far)
-    fc1_part = contract(norm_mlp, quarter_of(grad_inner, 1, quarter), 0, 0) + contract(
-        norm_mlp_far, grad_inner_far, 0, 0
+    (grad_inner_far,) = turn(grad_inner_far)
+    inner_quarter = gate(quarter_of(grad_inner, 1, quarter))
+    fc1_part = (
+        contract(norm_mlp_own, inner_quarter[:close], 0, 0)
+        + contract(norm_mlp_rest, inner_quarter[close:], 0, 0)
+        + contract(norm_mlp_far, grad_inner_far, 0, 0)
     )
     (fc1_part,) = turn(fc1_part.astype(BF))
     enqueue("fc1", fc1_part, 4)
-    qkv_part = contract(norm_attn, gate(quarter_of(grad_qkv, 1, quarter)), 0, 0) + contract(
-        norm_attn_far, jnp.concatenate(grad_qkv_far, axis=0), 0, 0
+    grad_norm_attn = contract(gate(grad_qkv), qkv_weight, 1, 1)
+    (grad_norm_attn,) = turn(grad_norm_attn)
+    qkv_quarter = gate(quarter_of(grad_qkv, 1, quarter))
+    qkv_part = (
+        contract(norm_attn_own, qkv_quarter[:close], 0, 0)
+        + contract(norm_attn_rest, qkv_quarter[close:], 0, 0)
+        + contract(norm_attn_far, jnp.concatenate(grad_qkv_far, axis=0), 0, 0)
     )
     (qkv_part,) = turn(qkv_part.astype(BF))
     enqueue("qkv", qkv_part, 8)
     grad_norm_mlp = contract(gate(grad_inner), fc1_weight, 1, 1)
     (grad_norm_mlp,) = turn(grad_norm_mlp)
-    grad_norm_attn = contract(gate(grad_qkv), qkv_weight, 1, 1)
-    (grad_norm_attn,) = turn(grad_norm_attn)
-
-    features = jnp.concatenate(near_blocks, axis=0)
-    features = gate(features).astype(F32)
+
+    features = gate(jnp.concatenate(near_blocks, axis=0)).astype(F32)
     centered = features - jnp.mean(features, axis=-1, keepdims=True)
     inverse = lax.rsqrt(jnp.mean(centered * centered, axis=-1, keepdims=True) + EPSILON)
     xhat = centered * inverse
-
-    def norm_back(gained):
-        return inverse * (
-            gained
-            - jnp.mean(gained, axis=-1, keepdims=True)
-            - xhat * jnp.mean(gained * xhat, axis=-1, keepdims=True)
-        )
-
-    grad_hidden = norm_back(grad_norm_attn * gain_attn + grad_norm_mlp * gain_mlp)
+    gained = grad_norm_attn * gain_attn + grad_norm_mlp * gain_mlp
+    grad_hidden = inverse * (
+        gained
+        - jnp.mean(gained, axis=-1, keepdims=True)
+        - xhat * jnp.mean(gained * xhat, axis=-1, keepdims=True)
+    )
+    blocks = grad_hidden.reshape(ways, 2, rows, D)
+    mates = blocks[:, 1].astype(BF)
+    kept, mates = turn(blocks[:, 0], mates)
+    outcome = {}
+    walk(scatter_walk(kept, mates, outcome))
     tensor_parts = jnp.stack(
         [
             jnp.sum(grad_norm_attn * xhat, axis=0),
@@ -680,16 +781,8 @@
     ).reshape(-1)
     fc1_bias_part = jnp.sum(grad_inner, axis=0, dtype=F32)
     qkv_bias_part = jnp.sum(grad_qkv, axis=0, dtype=F32)
-    grad_hidden, tensor_parts = turn(grad_hidden, tensor_parts)
-    input_grad = grad_out + scatter_rows(grad_hidden)[0]
-    (input_grad,) = turn(input_grad)
-    small = jnp.concatenate([tensor_sum(tensor_parts), fc1_bias_part, qkv_bias_part])
-    small = dp_sum(small)
-    (small,) = turn(small)
-    vectors = small[: 6 * D].reshape(6, D)
-    fc1_bias_grad = small[6 * D : 6 * D + fc1_bias_part.shape[0]]
-    qkv_bias_grad = small[6 * D + fc1_bias_part.shape[0] :]
-    loss_value = vectors[5, 0] / (count_all * D)
+    tensor_parts, fc1_bias_part, qkv_bias_part = turn(tensor_parts, fc1_bias_part, qkv_bias_part)
+    walk(small_walk(tensor_parts, jnp.concatenate([fc1_bias_part, qkv_bias_part]), outcome))
     layout = {"fc2": (0, 4), "out": (0, 1), "fc1": (1, 4), "qkv": (1, 8)}
     while queue or due:
         for name, (axis, chunks) in layout.items():
@@ -702,6 +795,12 @@
                 break
         else:
             turn()
+    input_grad = outcome["input"]
+    small = outcome["small"]
+    vectors = small[: 6 * D].reshape(6, D)
+    fc1_bias_grad = small[6 * D : 6 * D + fc1_bias_part.shape[0]]
+    qkv_bias_grad = small[6 * D + fc1_bias_part.shape[0] :]
+    loss_value = vectors[5, 0] / (count_all * D)
     fc2_weight_grad = place("fc2", 0, 4)
     out_weight_grad = place("out", 0, 1)
     fc1_weight_grad = place("fc1", 1, 4)

time: 788 us -> 769 us (0.976)
  starting transfers between devices: 135 us -> 109 us
  local copies, waits for them, and re-layouts: 34.4 us -> 54.5 us
  matrix products: 130 us -> 117 us
    ppermute x6, waiting for transfers between devices: 19.8 us -> 70.6 us  [from_y(): return lax.ppermute(v, 'tensor', pairs)]
    ppermute x2 -> x3, waiting for transfers between devices: 36.8 us -> 1.59 us  [the longest x2 1.23 us: small_walk(): lax.ppermute(v, 'tensor', p)]
    ppermute x88, starting transfers between devices: 121 us -> 94.8 us  [flip(): return lax.ppermute(v, 'dp', [(d, d ^ mask) for d in range(dp)])]
    unnamed x163 -> x258, local copies, waits for them, and re-layouts: 10.4 us -> 21.8 us
    dot_general x8 -> x10, matrix products: 80.7 us -> 70.3 us  [contract(): lax.dot_general(left_side, right_side, (((left_dim,), (right_dim,)), ((),...]
    concatenate x5 -> x4, other arithmetic: 19.1 us -> 12 us  [the longest x1 8.83 us: on_device(): jnp.concatenate([active_far, jnp.concatenate(context_far, axis=0)], axis=1)]
    dot_general x4 -> x7, matrix products: 49.8 us -> 46.5 us  [the longest x2 20.7 us: units(): jnp.dot(normed, fc1_weight, preferred_element_type=F32)]
    pallas_call x2 -> x3, Pallas kernels: 27.1 us -> 28 us  [both_norms(): pl.pallas_call(functools.partial(norms_kernel, count), grid=(count,), in_...]
  transfers between devices with their start and end apart: 118 -> 119, of which waited for: 52 -> 50; matrix products, arithmetic and copies ran while one was open for 24% -> 25% of each run, Pallas kernels for 16% -> 14%
where the time goes in v4:
time: 769 us; the launch traced here: 765 us
  waiting for transfers between devices  288 us (37%)
  Pallas kernels  135 us (18%)
  matrix products  117 us (15%)
  starting transfers between devices  109 us (14%)
  other arithmetic  55.3 us (7%)
  local copies, waits for them, and re-layouts  54.5 us (7%)
    ppermute x88, waiting for transfers between devices, flip(): return lax.ppermute(v, 'dp', [(d, d ^ mask) for d in range(dp)])  213 us
    ppermute x88, starting transfers between devices, flip(): return lax.ppermute(v, 'dp', [(d, d ^ mask) for d in range(dp)])  94.8 us
    ppermute x6, waiting for transfers between devices, from_y(): return lax.ppermute(v, 'tensor', pairs)  70.6 us
    dot_general x10, matrix products, contract(): lax.dot_general(left_side, right_side, (((left_dim,), (right_dim,)), ((),...  70.3 us
    pallas_call x17, Pallas kernels, place_quarters(): pl.pallas_call(place_kernel, grid_spec=pltpu.PrefetchScalarGridSpec(num_s...  39.1 us
    pallas_call x3, Pallas kernels, both_norms(): pl.pallas_call(functools.partial(norms_kernel, count), grid=(count,), in_...  28 us
    unnamed x258, local copies, waits for them, and re-layouts  21.8 us
    dot_general x2, matrix products, units(): jnp.dot(normed, fc1_weight, preferred_element_type=F32)  20.7 us
  transfers between devices with their start and end apart: 119, of which 50 were waited for; matrix products, arithmetic and copies ran while one was open for 25% of the time, Pallas kernels for 14%

profile of v4, /device:TPU:0, one launch (start us, length us, event | category | flops | bytes accessed | tf_op | source)
XLA Modules:
  0.0 765.3 jit_solution(10224682315116286382)
XLA Ops:
  1.2 2.6 collective-permute-start.2
  27.6 4.5 both_norms.3
  33.3 5.3 qkv_rotary.2.refs_0_
  39.5 10.3 %multiply_convert_fusion.2 = (bf16[512,2048]{1,0:T(8,128)(2,1)}, f32[512,2048]{1,0:T(8,128)}) fusion(f32[2048]{0:T(1024)S(1)} %convert_element_type.279, bf16[512,2048]{1,0:T(8,128)(2,1)S(1)} %copy-done.95, bf16[2048,2048]{1,0:T(8,128)(2,1)} %param.28), kind=kOutput, calls=%fused_computation.38 | convolution fusion | flops 4301258752 | bytes 16785408 | tf_op jit(solution)/shard_map/dot_general | solution.py:506
  53.1 11.4 %collective-permute-done.13.refs_6_ = bf16[256,2048]{1,0:T(8,128)(2,1)} collective-permute-done((bf16[256,2048]{1,0:T(8,128)(2,1)}, bf16[256,2048]{1,0:T(8,128)(2,1)}, u32[]{:S(2)}, u32[]{:S(2)}) %collective-permute-start.13) | collective-permute-done | bytes 1048608 | tf_op jit(solution)/shard_map/ppermute | solution.py:442
  65.8 4.3 both_norms.4
  72.7 2.8 copy-done.6
  77.4 5.3 qkv_rotary.3.q_ref.k_ref.v_ref
  82.7 2.7 collective-permute-start.8
  85.4 9.8 %attend.1 = (bf16[1024,512]{1,0:T(8,128)(2,1)S(1)}, f32[2,1024,1]{2,1,0:T(8,128)S(1)}) custom-call(s32[1]{0:T(128)S(6)} %copy.94.prefix_ref, bf16[1024,1536]{1,0:T(8,128)(2,1)S(1)} %qkv_rotary.3.q_ref.k_ref.v_ref, bf16[1024,1536]{1,0:T(8,128)(2,1)S(1)} %qkv_rotary.3.q_ref.k_ref.v_ref, bf16[1024,1536]{1,0:T(8,128)(2,1)S(1)} %qkv_rotary.3.q_ref.k_ref.v_ref, ...), custom_call_target="tpu_custom_call" | custom-call | flops 2147483648 | bytes 4194304 | tf_op jit(solution)/shard_map/attend/pallas_call | solution.py:147
  95.9 10.5 %multiply_convert_fusion.1 = (bf16[512,2048]{1,0:T(8,128)(2,1)S(1)}, f32[512,2048]{1,0:T(8,128)}) fusion(f32[2048]{0:T(1024)S(1)} %convert_element_type.279, bf16[512,2048]{1,0:T(8,128)(2,1)S(1)} %copy-done.92, bf16[2048,2048]{1,0:T(8,128)(2,1)} %param.28), kind=kOutput, calls=%fused_computation.37 | convolution fusion | flops 4301258752 | bytes 16785408 | tf_op jit(solution)/shard_map/dot_general | solution.py:506
  110.0 10.9 %collective-permute-done.16.refs_8_ = bf16[256,2048]{1,0:T(8,128)(2,1)S(1)} collective-permute-done((bf16[256,2048]{1,0:T(8,128)(2,1)}, bf16[256,2048]{1,0:T(8,128)(2,1)S(1)}, u32[]{:S(2)}, u32[]{:S(2)}) %collective-permute-start.16) | collective-permute-done | bytes 1048608 | tf_op jit(solution)/shard_map/ppermute | solution.py:442
  121.4 4.5 convolution_add_fusion.1
  126.7 6.4 collective-permute-done.10.refs_2_
  133.1 21.5 %collective-permute-done.18.refs_10_ = bf16[256,2048]{1,0:T(8,128)(2,1)S(1)} collective-permute-done((bf16[256,2048]{1,0:T(8,128)(2,1)S(1)}, bf16[256,2048]{1,0:T(8,128)(2,1)S(1)}, u32[]{:S(2)}, u32[]{:S(2)}) %collective-permute-start.18) | collective-permute-done | bytes 1048608 | tf_op jit(solution)/shard_map/ppermute | solution.py:435
  158.8 4.5 fusion.69
  181.2 19.3 %both_norms.5 = (bf16[3072,2048]{1,0:T(8,128)(2,1)}, bf16[3072,2048]{1,0:T(8,128)(2,1)}) custom-call(f32[8,2048]{1,0:T(8,128)S(1)} %select_maximum_fusion.gains_ref, bf16[256,2048]{1,0:T(8,128)(2,1)} %collective-permute-done.2.refs_0_, bf16[256,2048]{1,0:T(8,128)(2,1)S(1)} %copy-done.35, bf16[256,2048]{1,0:T(8,128)(2,1)S(1)} %copy-done.33, ...), custom_call_target="tpu_custom_call" | custom-call | flops 75497472 | bytes 37748736 | tf_op jit(solution)/shard_map/both_norms/pallas_call | solution.py:304
  200.4 14.2 %fusion.21 = (f32[3072,512]{1,0:T(8,128)}, bf16[3072,512]{1,0:T(8,128)(2,1)S(1)}) fusion(f32[512]{0:T(512)S(1)} %dynamic-slice_convert_fusion, bf16[3072,2048]{1,0:T(8,128)(2,1)} %get-tuple-element.244, bf16[2048,2048]{1,0:T(8,128)(2,1)} %param.28, s32[]{:T(128)S(6)} %select_n.84), kind=kOutput, calls=%fused_computation.28 | convolution fusion | flops 6459752448 | bytes 24119300 | tf_op jit(solution)/shard_map/dot_general | solution.py:565
  214.7 8.8 %maximum_maximum_fusion.far_ref = bf16[3072,640]{1,0:T(8,128)(2,1)} fusion(bf16[1024,128]{1,0:T(8,128)(2,1)S(1)} %collective-permute-done.25, bf16[1024,128]{1,0:T(8,128)(2,1)S(1)} %collective-permute-done.24, bf16[1024,128]{1,0:T(8,128)(2,1)S(1)} %collective-permute-done.23, bf16[3072,512]{1,0:T(8,128)(2,1)S(1)} %get-tuple-element.415), kind=kLoop, calls=%fused_computation.39 | loop fusion | flops 15728640 | bytes 7864320 | tf_op jit(solution)/shard_map/concatenate | solution.py:570
  223.5 2.5 fusion.28
  229.2 21.5 %collective-permute-done.29 = bf16[256,2048]{1,0:T(8,128)(2,1)S(1)} collective-permute-done((bf16[256,2048]{1,0:T(8,128)(2,1)S(1)}, bf16[256,2048]{1,0:T(8,128)(2,1)S(1)}, u32[]{:S(2)}, u32[]{:S(2)}) %collective-permute-start.29) | collective-permute-done | bytes 1048608 | tf_op jit(solution)/shard_map/ppermute | solution.py:435
  256.6 17.3 %fusion.17 = bf16[1024,2048]{1,0:T(8,128)(2,1)} fusion(f32[512,2048]{1,0:T(8,128)} %get-tuple-element.471, f32[512,2048]{1,0:T(8,128)} %get-tuple-element.469, bf16[1024,2048]{1,0:T(8,128)(2,1)S(1)} %constant_dynamic-update-slice_fusion.right_ref, bf16[2048,2048]{1,0:T(8,128)(2,1)} %param.30), kind=kOutput, calls=%fused_computation.21 | convolution fusion | flops 8613003264 | bytes 25165824 | tf_op jit(solution)/shard_map/dot_general | solution.py:27
  273.9 3.3 convolution_convert_fusion.g_ref
  277.3 2.6 collective-permute-done.31.refs_8_
  284.2 21.2 %collective-permute-done.39.refs_10_ = bf16[256,2048]{1,0:T(8,128)(2,1)} collective-permute-done((bf16[256,2048]{1,0:T(8,128)(2,1)}, bf16[256,2048]{1,0:T(8,128)(2,1)}, u32[]{:S(2)}, u32[]{:S(2)}) %collective-permute-start.39) | collective-permute-done | bytes 1048608 | tf_op jit(solution)/shard_map/ppermute | solution.py:435
  305.4 3.1 constant_dynamic-slice_fusion.2.weight_ref
  311.9 11.9 %attend_back.1 = bf16[1024,1536]{1,0:T(8,128)(2,1)} custom-call(s32[1]{0:T(128)S(6)} %copy.94.prefix_ref, bf16[1024,1536]{1,0:T(8,128)(2,1)} %copy-done.4, bf16[1024,1536]{1,0:T(8,128)(2,1)} %copy-done.4, bf16[1024,1536]{1,0:T(8,128)(2,1)} %copy-done.4, bf16[1024,512]{1,0:T(8,128)(2,1)S(1)} %copy-done.82, f32[2,1024,1]{2,1,0:T(8,128)S(1)} %copy-done.81, ...), custom_call_target="tpu_custom_call" | custom-call | flops 5368709120 | bytes 7340032 | tf_op jit(solution)/shard_map/attend_back/pallas_call | solution.py:218
  323.8 17.9 %outer_blocks.1 = bf16[640,2048]{1,0:T(8,128)(2,1)} custom-call(bf16[1024,640]{1,0:T(8,128)(2,1)} %pad_maximum_fusion.2.near_ref, bf16[3072,640]{1,0:T(8,128)(2,1)} %maximum_maximum_fusion.far_ref, bf16[1024,2048]{1,0:T(8,128)(2,1)} %copy-done.110, bf16[256,2048]{1,0:T(8,128)(2,1)} %copy-done.103, bf16[256,2048]{1,0:T(8,128)(2,1)} %copy-done.106, ...), custom_call_target="tpu_custom_call" | custom-call | flops 10737418240 | bytes 22020096 | tf_op jit(solution)/shard_map/outer_blocks/pallas_call | solution.py:345
  341.7 3.0 fusion.62
  345.0 17.7 %back_blocks.1 = bf16[3072,512]{1,0:T(8,128)(2,1)} custom-call(bf16[512,2048]{1,0:T(8,128)(2,1)} %constant_dynamic-slice_fusion.2.weight_ref, f32[3072,512]{1,0:T(8,128)} %get-tuple-element.414.slope_ref, bf16[256,2048]{1,0:T(8,128)(2,1)} %copy-done.103, bf16[256,2048]{1,0:T(8,128)(2,1)} %copy-done.106, bf16[256,2048]{1,0:T(8,128)(2,1)} %collective-permute-done.32.refs_2_, ...), custom_call_target="tpu_custom_call" | custom-call | flops 6442450944 | bytes 22020096 | tf_op jit(solution)/shard_map/back_blocks/pallas_call | solution.py:380
  362.7 11.2 %fusion.70 = f32[2048,512]{1,0:T(8,128)S(1)} fusion(bf16[3072,2048]{1,0:T(8,128)(2,1)} %get-tuple-element.244, bf16[3072,512]{1,0:T(8,128)(2,1)} %back_blocks.1), kind=kOutput, calls=%fused_computation.170 | convolution fusion | flops 6442450944 | bytes 19922944 | tf_op jit(solution)/shard_map/dot_general | solution.py:27
  373.9 2.6 collective-permute-start.44
  386.6 13.8 %collective-permute-done.44 = bf16[128,2048]{1,0:T(8,128)(2,1)S(1)} collective-permute-done((bf16[128,2048]{1,0:T(8,128)(2,1)}, bf16[128,2048]{1,0:T(8,128)(2,1)S(1)}, u32[]{:S(2)}, u32[]{:S(2)}) %collective-permute-start.44) | collective-permute-done | bytes 524320 | tf_op jit(solution)/shard_map/ppermute | solution.py:442
  400.7 6.7 fusion.71
  408.8 3.3 collective-permute-start.49
  412.1 28.1 %collective-permute-done.43 = bf16[1024,384]{1,0:T(8,128)(2,1)} collective-permute-done((bf16[1024,384]{1,0:T(8,128)(2,1)}, bf16[1024,384]{1,0:T(8,128)(2,1)}, u32[]{:S(2)}, u32[]{:S(2)}) %collective-permute-start.43) | collective-permute-done | bytes 786464 | tf_op jit(solution)/shard_map/ppermute | solution.py:442
  440.3 9.1 %collective-permute-done.47.refs_2_ = bf16[128,2048]{1,0:T(8,128)(2,1)S(1)} collective-permute-done((bf16[128,2048]{1,0:T(8,128)(2,1)S(1)}, bf16[128,2048]{1,0:T(8,128)(2,1)S(1)}, u32[]{:S(2)}, u32[]{:S(2)}) %collective-permute-start.47) | collective-permute-done | bytes 524320 | tf_op jit(solution)/shard_map/ppermute | solution.py:442
  454.8 11.7 %fusion.22 = f32[2048,384]{1,0:T(8,128)} fusion(bf16[3072,2048]{1,0:T(8,128)(2,1)} %get-tuple-element.287, bf16[1024,384]{1,0:T(8,128)(2,1)} %collective-permute-done.43, bf16[1024,384]{1,0:T(8,128)(2,1)} %collective-permute-done.42, bf16[1024,384]{1,0:T(8,128)(2,1)} %collective-permute-done.41), kind=kOutput, calls=%fused_computation.47 | convolution fusion | flops 4838916096 | bytes 18087936 | tf_op jit(solution)/shard_map/dot_general | solution.py:27
  469.1 2.6 add_convert_fusion.1
  479.2 13.3 %fusion.72 = f32[1024,2048]{1,0:T(8,128)} fusion(bf16[1024,2048]{1,0:T(8,128)(2,1)S(1)} %copy-done.89, bf16[2048,2048]{1,0:T(8,128)(2,1)} %param.28), kind=kOutput, calls=%fused_computation.172 | convolution fusion | flops 8589934592 | bytes 20971520 | tf_op jit(solution)/shard_map/dot_general | solution.py:27
  493.2 5.8 collective-permute-done.54.refs_3_
  503.8 7.7 %fusion.59 = (f32[2048]{0:T(1024)S(1)}, f32[2048]{0:T(1024)S(1)}, f32[1024]{0:T(1024)S(1)}, f32[1024]{0:T(1024)S(1)}, f32[1024,2048]{1,0:T(8,128)S(1)}, /*index=5*/f32[2048]{0:T(1024)S(1)}, f32[2048]{0:T(1024)S(1)}) fusion(f32[1024,2048]{1,0:T(8,128)} %fusion.72, f32[1024]{0:T(1024)S(1)} %add_rsqrt_fusion, f32[1024]{0:T(1024)S(1)} %broadcast_multiply_fusion.2, ...), kind=kLoop, calls=%fused_computation.159 | loop fusion | flops 31447040 | bytes 29425664 | tf_op jit(solution)/shard_map/reduce_sum | solution.py:777
  511.5 2.7 fusion.8
  514.2 2.6 copy_bitcast_fusion
  519.3 5.6 collective-permute-done.60.refs_4_
  531.9 18.8 %collective-permute-done.56 = bf16[512,512]{1,0:T(8,128)(2,1)S(1)} collective-permute-done((bf16[512,512]{1,0:T(8,128)(2,1)}, bf16[512,512]{1,0:T(8,128)(2,1)S(1)}, u32[]{:S(2)}, u32[]{:S(2)}) %collective-permute-start.56) | collective-permute-done | bytes 524320 | tf_op jit(solution)/shard_map/ppermute | solution.py:442
  556.9 3.5 convert_add_fusion
  562.0 14.3 %collective-permute-done.65 = bf16[512,512]{1,0:T(8,128)(2,1)S(1)} collective-permute-done((bf16[512,512]{1,0:T(8,128)(2,1)}, bf16[512,512]{1,0:T(8,128)(2,1)S(1)}, u32[]{:S(2)}, u32[]{:S(2)}) %collective-permute-start.65) | collective-permute-done | bytes 524320 | tf_op jit(solution)/shard_map/ppermute | solution.py:442
  585.9 17.1 %collective-permute-done.71 = bf16[512,512]{1,0:T(8,128)(2,1)S(1)} collective-permute-done((bf16[512,512]{1,0:T(8,128)(2,1)S(1)}, bf16[512,512]{1,0:T(8,128)(2,1)S(1)}, u32[]{:S(2)}, u32[]{:S(2)}) %collective-permute-start.71) | collective-permute-done | bytes 524320 | tf_op jit(solution)/shard_map/ppermute | solution.py:442
  604.8 2.5 place_quarters.18.refs_0_
  615.9 16.1 %collective-permute-done.76 = bf16[512,512]{1,0:T(8,128)(2,1)S(1)} collective-permute-done((bf16[512,512]{1,0:T(8,128)(2,1)S(1)}, bf16[512,512]{1,0:T(8,128)(2,1)S(1)}, u32[]{:S(2)}, u32[]{:S(2)}) %collective-permute-start.76) | collective-permute-done | bytes 524320 | tf_op jit(solution)/shard_map/ppermute | solution.py:442
  643.1 8.3 %collective-permute-done.81 = bf16[256,384]{1,0:T(8,128)(2,1)S(1)} collective-permute-done((bf16[256,384]{1,0:T(8,128)(2,1)S(1)}, bf16[256,384]{1,0:T(8,128)(2,1)S(1)}, u32[]{:S(2)}, u32[]{:S(2)}) %collective-permute-start.81) | collective-permute-done | bytes 196640 | tf_op jit(solution)/shard_map/ppermute | solution.py:442
  652.8 4.4 collective-permute-done.84.refs_4_
  658.6 2.6 collective-permute-start.86
  664.4 3.6 place_quarters.21
  668.0 5.0 collective-permute-done.86
  681.7 3.4 collective-permute-done.92
  687.4 2.5 collective-permute-start.100
  693.5 5.8 collective-permute-done.97.refs_3_
  718.6 2.5 collective-permute-done.106.refs_4_
  735.3 3.1 collective-permute-done.112.refs_2_
  751.8 2.6 collective-permute-done.118.refs_4_
  757.9 2.7 place_quarters.32.refs_0_
  760.6 2.8 place_quarters.33
  (584 shorter events, 229.0 us)
Async XLA Ops:
  0.7 26.9 %collective-permute-start = (bf16[256,2048]{1,0:T(8,128)(2,1)}, bf16[256,2048]{1,0:T(8,128)(2,1)}, u32[]{:S(2)}, u32[]{:S(2)}) collective-permute-start(bf16[256,2048]{1,0:T(8,128)(2,1)} %refs_0_.1), channel_id=1, source_target_pairs={{0,1},{1,0},{2,3},{3,2},{4,5},{5,4},{6,7},{7,6},{8,9},{9,8},{10,11... | collective-permute-start | bytes 3145736 | tf_op jit(solution)/shard_map/ppermute | solution.py:431
  1.2 48.6 %collective-permute-start.2 = (bf16[256,2048]{1,0:T(8,128)(2,1)}, bf16[256,2048]{1,0:T(8,128)(2,1)}, u32[]{:S(2)}, u32[]{:S(2)}) collective-permute-start(bf16[256,2048]{1,0:T(8,128)(2,1)} %refs_0_.1), channel_id=1, source_target_pairs={{0,4},{4,0},{8,12},{12,8},{16,20},{20,16},{24,28},{28,24},{1,5},{5... | collective-permute-start | bytes 3145736 | tf_op jit(solution)/shard_map/ppermute | solution.py:442
  3.7 46.1 %collective-permute-start.3 = (bf16[256,2048]{1,0:T(8,128)(2,1)}, bf16[256,2048]{1,0:T(8,128)(2,1)}, u32[]{:S(2)}, u32[]{:S(2)}) collective-permute-start(bf16[256,2048]{1,0:T(8,128)(2,1)} %refs_0_.1), channel_id=1, source_target_pairs={{0,8},{4,12},{8,0},{12,4},{16,24},{20,28},{24,16},{28,20},{1,9},{5... | collective-permute-start | bytes 3145736 | tf_op jit(solution)/shard_map/ppermute | solution.py:442
  5.3 33.3 %collective-permute-start.4 = (bf16[256,2048]{1,0:T(8,128)(2,1)}, bf16[256,2048]{1,0:T(8,128)(2,1)}, u32[]{:S(2)}, u32[]{:S(2)}) collective-permute-start(bf16[256,2048]{1,0:T(8,128)(2,1)} %refs_0_.1), channel_id=1, source_target_pairs={{0,2},{1,3},{2,0},{3,1},{4,6},{5,7},{6,4},{7,5},{8,10},{9,11},{10,... | collective-permute-start | bytes 3145736 | tf_op jit(solution)/shard_map/ppermute | solution.py:435
  39.1 25.5 %collective-permute-start.13 = (bf16[256,2048]{1,0:T(8,128)(2,1)}, bf16[256,2048]{1,0:T(8,128)(2,1)}, u32[]{:S(2)}, u32[]{:S(2)}) collective-permute-start(bf16[256,2048]{1,0:T(8,128)(2,1)} %collective-permute-done.4.refs_0_), channel_id=1, source_target_pairs={{0,8},{4,12},{8,0},{12,4},{16,24},{20,28},{24,16},{28,20},{1,9},{5... | collective-permute-start | bytes 3145736 | tf_op jit(solution)/shard_map/ppermute | solution.py:442
  64.6 62.0 %collective-permute-start.14 = (bf16[256,2048]{1,0:T(8,128)(2,1)}, bf16[256,2048]{1,0:T(8,128)(2,1)S(1)}, u32[]{:S(2)}, u32[]{:S(2)}) collective-permute-start(bf16[256,2048]{1,0:T(8,128)(2,1)} %collective-permute-done.13.refs_6_), channel_id=1, source_target_pairs={{0,1},{1,0},{2,3},{3,2},{4,5},{5,4},{6,7},{7,6},{8,9},{9,8},{10,11... | collective-permute-start | bytes 3145736 | tf_op jit(solution)/shard_map/ppermute | solution.py:431
  95.2 25.6 %collective-permute-start.16 = (bf16[256,2048]{1,0:T(8,128)(2,1)}, bf16[256,2048]{1,0:T(8,128)(2,1)S(1)}, u32[]{:S(2)}, u32[]{:S(2)}) collective-permute-start(bf16[256,2048]{1,0:T(8,128)(2,1)} %collective-permute-done.3.refs_4_), channel_id=1, source_target_pairs={{0,4},{4,0},{8,12},{12,8},{16,20},{20,16},{24,28},{28,24},{1,5},{5... | collective-permute-start | bytes 3145736 | tf_op jit(solution)/shard_map/ppermute | solution.py:442
  106.8 26.2 %collective-permute-start.10 = (bf16[256,2048]{1,0:T(8,128)(2,1)}, bf16[256,2048]{1,0:T(8,128)(2,1)S(1)}, u32[]{:S(2)}, u32[]{:S(2)}) collective-permute-start(bf16[256,2048]{1,0:T(8,128)(2,1)} %collective-permute-done.2.refs_0_), channel_id=1, source_target_pairs={{0,2},{1,3},{2,0},{3,1},{4,6},{5,7},{6,4},{7,5},{8,10},{9,11},{10,... | collective-permute-start | bytes 3145736 | tf_op jit(solution)/shard_map/ppermute | solution.py:435
  120.8 33.7 %collective-permute-start.18 = (bf16[256,2048]{1,0:T(8,128)(2,1)S(1)}, bf16[256,2048]{1,0:T(8,128)(2,1)S(1)}, u32[]{:S(2)}, u32[]{:S(2)}) collective-permute-start(bf16[256,2048]{1,0:T(8,128)(2,1)S(1)} %collective-permute-done.16.refs_8_), channel_id=1, source_target_pairs={{0,2},{1,3},{2,0},{3,1},{4,6},{5,7},{6,4},{7,5},{8,10},{9,11},{10,... | collective-permute-start | bytes 3145736 | tf_op jit(solution)/shard_map/ppermute | solution.py:435
  126.0 28.6 %collective-permute-start.20 = (bf16[1,256,2048]{2,1,0:T(8,128)(2,1)S(1)}, bf16[1,256,2048]{2,1,0:T(8,128)(2,1)S(1)}, u32[]{:S(2)}, u32[]{:S(2)}) collective-permute-start(bf16[1,256,2048]{2,1,0:T(8,128)(2,1)S(1)} %fusion.41), channel_id=1, source_target_pairs={{0,1},{1,0},{2,3},{3,2},{4,5},{5,4},{6,7},{7,6},{8,9},{9,8},{10,11... | collective-permute-start | bytes 3145736 | tf_op jit(solution)/shard_map/ppermute | solution.py:431
  126.1 30.3 %collective-permute-start.9 = (bf16[256,2048]{1,0:T(8,128)(2,1)}, bf16[256,2048]{1,0:T(8,128)(2,1)S(1)}, u32[]{:S(2)}, u32[]{:S(2)}) collective-permute-start(bf16[256,2048]{1,0:T(8,128)(2,1)} %collective-permute-done.2.refs_0_), channel_id=1, source_target_pairs={{0,1},{1,0},{2,3},{3,2},{4,5},{5,4},{6,7},{7,6},{8,9},{9,8},{10,11... | collective-permute-start | bytes 3145736 | tf_op jit(solution)/shard_map/ppermute | solution.py:431
  126.6 29.8 %collective-permute-start.12 = (bf16[256,2048]{1,0:T(8,128)(2,1)}, bf16[256,2048]{1,0:T(8,128)(2,1)S(1)}, u32[]{:S(2)}, u32[]{:S(2)}) collective-permute-start(bf16[256,2048]{1,0:T(8,128)(2,1)} %collective-permute-done.3.refs_4_), channel_id=1, source_target_pairs={{0,1},{1,0},{2,3},{3,2},{4,5},{5,4},{6,7},{7,6},{8,9},{9,8},{10,11... | collective-permute-start | bytes 3145736 | tf_op jit(solution)/shard_map/ppermute | solution.py:431
  133.1 25.2 %collective-permute-start.17 = (bf16[256,2048]{1,0:T(8,128)(2,1)S(1)}, bf16[256,2048]{1,0:T(8,128)(2,1)S(1)}, u32[]{:S(2)}, u32[]{:S(2)}) collective-permute-start(bf16[256,2048]{1,0:T(8,128)(2,1)S(1)} %collective-permute-done.16.refs_8_), channel_id=1, source_target_pairs={{0,1},{1,0},{2,3},{3,2},{4,5},{5,4},{6,7},{7,6},{8,9},{9,8},{10,11... | collective-permute-start | bytes 3145736 | tf_op jit(solution)/shard_map/ppermute | solution.py:431
  171.1 43.6 %collective-permute-start.25 = (bf16[1024,128]{1,0:T(8,128)(2,1)S(1)}, bf16[1024,128]{1,0:T(8,128)(2,1)S(1)}, u32[]{:S(2)}, u32[]{:S(2)}) collective-permute-start(bf16[1024,128]{1,0:T(8,128)(2,1)S(1)} %get-tuple-element.439), channel_id=1, source_target_pairs={{0,12},{4,8},{8,4},{12,0},{16,28},{20,24},{24,20},{28,16},{1,13},{... | collective-permute-start | bytes 786440 | tf_op jit(solution)/shard_map/ppermute | solution.py:442
  172.9 41.8 %collective-permute-start.24 = (bf16[1024,128]{1,0:T(8,128)(2,1)S(1)}, bf16[1024,128]{1,0:T(8,128)(2,1)S(1)}, u32[]{:S(2)}, u32[]{:S(2)}) collective-permute-start(bf16[1024,128]{1,0:T(8,128)(2,1)S(1)} %get-tuple-element.440), channel_id=1, source_target_pairs={{0,8},{4,12},{8,0},{12,4},{16,24},{20,28},{24,16},{28,20},{1,9},{5... | collective-permute-start | bytes 786440 | tf_op jit(solution)/shard_map/ppermute | solution.py:442
  173.8 40.8 %collective-permute-start.23 = (bf16[1024,128]{1,0:T(8,128)(2,1)S(1)}, bf16[1024,128]{1,0:T(8,128)(2,1)S(1)}, u32[]{:S(2)}, u32[]{:S(2)}) collective-permute-start(bf16[1024,128]{1,0:T(8,128)(2,1)S(1)} %get-tuple-element.441), channel_id=1, source_target_pairs={{0,4},{4,0},{8,12},{12,8},{16,20},{20,16},{24,28},{28,24},{1,5},{5... | collective-permute-start | bytes 786440 | tf_op jit(solution)/shard_map/ppermute | solution.py:442
  178.1 45.4 %collective-permute-start.22 = (bf16[256,2048]{1,0:T(8,128)(2,1)S(1)}, bf16[256,2048]{1,0:T(8,128)(2,1)S(1)}, u32[]{:S(2)}, u32[]{:S(2)}) collective-permute-start(bf16[256,2048]{1,0:T(8,128)(2,1)S(1)} %copy-done.107), channel_id=1, source_target_pairs={{0,2},{1,3},{2,0},{3,1},{4,6},{5,7},{6,4},{7,5},{8,10},{9,11},{10,... | collective-permute-start | bytes 3145736 | tf_op jit(solution)/shard_map/ppermute | solution.py:439
  226.3 24.4 %collective-permute-start.29 = (bf16[256,2048]{1,0:T(8,128)(2,1)S(1)}, bf16[256,2048]{1,0:T(8,128)(2,1)S(1)}, u32[]{:S(2)}, u32[]{:S(2)}) collective-permute-start(bf16[256,2048]{1,0:T(8,128)(2,1)S(1)} %fusion.39), channel_id=1, source_target_pairs={{0,2},{1,3},{2,0},{3,1},{4,6},{5,7},{6,4},{7,5},{8,10},{9,11},{10,... | collective-permute-start | bytes 3145736 | tf_op jit(solution)/shard_map/ppermute | solution.py:435
  226.9 24.0 %collective-permute-start.26 = (bf16[256,2048]{1,0:T(8,128)(2,1)S(1)}, bf16[256,2048]{1,0:T(8,128)(2,1)S(1)}, u32[]{:S(2)}, u32[]{:S(2)}) collective-permute-start(bf16[256,2048]{1,0:T(8,128)(2,1)S(1)} %fusion.39), channel_id=1, source_target_pairs={{0,4},{4,0},{8,12},{12,8},{16,20},{20,16},{24,28},{28,24},{1,5},{5... | collective-permute-start | bytes 3145736 | tf_op jit(solution)/shard_map/ppermute | solution.py:442
  228.1 23.8 %collective-permute-start.27 = (bf16[256,2048]{1,0:T(8,128)(2,1)S(1)}, bf16[256,2048]{1,0:T(8,128)(2,1)}, u32[]{:S(2)}, u32[]{:S(2)}) collective-permute-start(bf16[256,2048]{1,0:T(8,128)(2,1)S(1)} %fusion.39), channel_id=1, source_target_pairs={{0,8},{4,12},{8,0},{12,4},{16,24},{20,28},{24,16},{28,20},{1,9},{5... | collective-permute-start | bytes 3145736 | tf_op jit(solution)/shard_map/ppermute | solution.py:442
  229.2 22.8 %collective-permute-start.28 = (bf16[256,2048]{1,0:T(8,128)(2,1)S(1)}, bf16[256,2048]{1,0:T(8,128)(2,1)S(1)}, u32[]{:S(2)}, u32[]{:S(2)}) collective-permute-start(bf16[256,2048]{1,0:T(8,128)(2,1)S(1)} %fusion.39), channel_id=1, source_target_pairs={{0,1},{1,0},{2,3},{3,2},{4,5},{5,4},{6,7},{7,6},{8,9},{9,8},{10,11... | collective-permute-start | bytes 3145736 | tf_op jit(solution)/shard_map/ppermute | solution.py:431
  253.3 26.6 %collective-permute-start.32 = (bf16[256,2048]{1,0:T(8,128)(2,1)S(1)}, bf16[256,2048]{1,0:T(8,128)(2,1)}, u32[]{:S(2)}, u32[]{:S(2)}) collective-permute-start(bf16[256,2048]{1,0:T(8,128)(2,1)S(1)} %collective-permute-done.26.refs_0_), channel_id=1, source_target_pairs={{0,2},{1,3},{2,0},{3,1},{4,6},{5,7},{6,4},{7,5},{8,10},{9,11},{10,... | collective-permute-start | bytes 3145736 | tf_op jit(solution)/shard_map/ppermute | solution.py:435
  253.9 28.7 %collective-permute-start.34 = (bf16[256,2048]{1,0:T(8,128)(2,1)S(1)}, bf16[256,2048]{1,0:T(8,128)(2,1)S(1)}, u32[]{:S(2)}, u32[]{:S(2)}) collective-permute-start(bf16[256,2048]{1,0:T(8,128)(2,1)S(1)} %collective-permute-done.26.refs_0_), channel_id=1, source_target_pairs={{0,1},{1,0},{2,3},{3,2},{4,5},{5,4},{6,7},{7,6},{8,9},{9,8},{10,11... | collective-permute-start | bytes 3145736 | tf_op jit(solution)/shard_map/ppermute | solution.py:431
  253.9 26.0 %collective-permute-start.31 = (bf16[256,2048]{1,0:T(8,128)(2,1)}, bf16[256,2048]{1,0:T(8,128)(2,1)}, u32[]{:S(2)}, u32[]{:S(2)}) collective-permute-start(bf16[256,2048]{1,0:T(8,128)(2,1)} %collective-permute-done.27.refs_4_), channel_id=1, source_target_pairs={{0,4},{4,0},{8,12},{12,8},{16,20},{20,16},{24,28},{28,24},{1,5},{5... | collective-permute-start | bytes 3145736 | tf_op jit(solution)/shard_map/ppermute | solution.py:442
  255.2 25.4 %collective-permute-start.33 = (bf16[256,2048]{1,0:T(8,128)(2,1)S(1)}, bf16[256,2048]{1,0:T(8,128)(2,1)}, u32[]{:S(2)}, u32[]{:S(2)}) collective-permute-start(bf16[256,2048]{1,0:T(8,128)(2,1)S(1)} %collective-permute-done.29), channel_id=1, source_target_pairs={{0,8},{4,12},{8,0},{12,4},{16,24},{20,28},{24,16},{28,20},{1,9},{5... | collective-permute-start | bytes 3145736 | tf_op jit(solution)/shard_map/ppermute | solution.py:442
  280.6 24.8 %collective-permute-start.39 = (bf16[256,2048]{1,0:T(8,128)(2,1)}, bf16[256,2048]{1,0:T(8,128)(2,1)}, u32[]{:S(2)}, u32[]{:S(2)}) collective-permute-start(bf16[256,2048]{1,0:T(8,128)(2,1)} %collective-permute-done.31.refs_8_), channel_id=1, source_target_pairs={{0,2},{1,3},{2,0},{3,1},{4,6},{5,7},{6,4},{7,5},{8,10},{9,11},{10,... | collective-permute-start | bytes 3145736 | tf_op jit(solution)/shard_map/ppermute | solution.py:435
  282.1 41.7 %collective-permute-start.36 = (bf16[256,2048]{1,0:T(8,128)(2,1)}, bf16[256,2048]{1,0:T(8,128)(2,1)}, u32[]{:S(2)}, u32[]{:S(2)}) collective-permute-start(bf16[256,2048]{1,0:T(8,128)(2,1)} %collective-permute-done.27.refs_4_), channel_id=1, source_target_pairs={{0,1},{1,0},{2,3},{3,2},{4,5},{5,4},{6,7},{7,6},{8,9},{9,8},{10,11... | collective-permute-start | bytes 3145736 | tf_op jit(solution)/shard_map/ppermute | solution.py:431
  282.1 41.7 %collective-permute-start.38 = (bf16[256,2048]{1,0:T(8,128)(2,1)}, bf16[256,2048]{1,0:T(8,128)(2,1)}, u32[]{:S(2)}, u32[]{:S(2)}) collective-permute-start(bf16[256,2048]{1,0:T(8,128)(2,1)} %collective-permute-done.31.refs_8_), channel_id=1, source_target_pairs={{0,1},{1,0},{2,3},{3,2},{4,5},{5,4},{6,7},{7,6},{8,9},{9,8},{10,11... | collective-permute-start | bytes 3145736 | tf_op jit(solution)/shard_map/ppermute | solution.py:431
  282.6 41.2 %collective-permute-start.35 = (bf16[256,2048]{1,0:T(8,128)(2,1)}, bf16[256,2048]{1,0:T(8,128)(2,1)}, u32[]{:S(2)}, u32[]{:S(2)}) collective-permute-start(bf16[256,2048]{1,0:T(8,128)(2,1)} %collective-permute-done.32.refs_2_), channel_id=1, source_target_pairs={{0,1},{1,0},{2,3},{3,2},{4,5},{5,4},{6,7},{7,6},{8,9},{9,8},{10,11... | collective-permute-start | bytes 3145736 | tf_op jit(solution)/shard_map/ppermute | solution.py:431
  283.7 40.1 %collective-permute-start.37 = (bf16[256,2048]{1,0:T(8,128)(2,1)}, bf16[256,2048]{1,0:T(8,128)(2,1)}, u32[]{:S(2)}, u32[]{:S(2)}) collective-permute-start(bf16[256,2048]{1,0:T(8,128)(2,1)} %collective-permute-done.33.refs_6_), channel_id=1, source_target_pairs={{0,1},{1,0},{2,3},{3,2},{4,5},{5,4},{6,7},{7,6},{8,9},{9,8},{10,11... | collective-permute-start | bytes 3145736 | tf_op jit(solution)/shard_map/ppermute | solution.py:431
  344.7 39.7 %collective-permute-start.45 = (bf16[128,2048]{1,0:T(8,128)(2,1)}, bf16[128,2048]{1,0:T(8,128)(2,1)}, u32[]{:S(2)}, u32[]{:S(2)}) collective-permute-start(bf16[128,2048]{1,0:T(8,128)(2,1)} %get-tuple-element.424), channel_id=1, source_target_pairs={{0,16},{4,20},{8,24},{12,28},{16,0},{20,4},{24,8},{28,12},{1,17},{... | collective-permute-start | bytes 1572872 | tf_op jit(solution)/shard_map/ppermute | solution.py:442
  373.9 26.6 %collective-permute-start.44 = (bf16[128,2048]{1,0:T(8,128)(2,1)}, bf16[128,2048]{1,0:T(8,128)(2,1)S(1)}, u32[]{:S(2)}, u32[]{:S(2)}) collective-permute-start(bf16[128,2048]{1,0:T(8,128)(2,1)} %get-tuple-element.275), channel_id=1, source_target_pairs={{0,16},{4,20},{8,24},{12,28},{16,0},{20,4},{24,8},{28,12},{1,17},{... | collective-permute-start | bytes 1572872 | tf_op jit(solution)/shard_map/ppermute | solution.py:442
  379.3 29.5 %collective-permute-start.41 = (bf16[1024,384]{1,0:T(8,128)(2,1)}, bf16[1024,384]{1,0:T(8,128)(2,1)}, u32[]{:S(2)}, u32[]{:S(2)}) collective-permute-start(bf16[1024,384]{1,0:T(8,128)(2,1)} %get-tuple-element.420), channel_id=1, source_target_pairs={{0,4},{4,0},{8,12},{12,8},{16,20},{20,16},{24,28},{28,24},{1,5},{5... | collective-permute-start | bytes 2359304 | tf_op jit(solution)/shard_map/ppermute | solution.py:442
  380.1 32.0 %collective-permute-start.42 = (bf16[1024,384]{1,0:T(8,128)(2,1)}, bf16[1024,384]{1,0:T(8,128)(2,1)}, u32[]{:S(2)}, u32[]{:S(2)}) collective-permute-start(bf16[1024,384]{1,0:T(8,128)(2,1)} %get-tuple-element.419), channel_id=1, source_target_pairs={{0,8},{4,12},{8,0},{12,4},{16,24},{20,28},{24,16},{28,20},{1,9},{5... | collective-permute-start | bytes 2359304 | tf_op jit(solution)/shard_map/ppermute | solution.py:442
  381.2 59.1 %collective-permute-start.43 = (bf16[1024,384]{1,0:T(8,128)(2,1)}, bf16[1024,384]{1,0:T(8,128)(2,1)}, u32[]{:S(2)}, u32[]{:S(2)}) collective-permute-start(bf16[1024,384]{1,0:T(8,128)(2,1)} %get-tuple-element.418), channel_id=1, source_target_pairs={{0,12},{4,8},{8,4},{12,0},{16,28},{20,24},{24,20},{28,16},{1,13},{... | collective-permute-start | bytes 2359304 | tf_op jit(solution)/shard_map/ppermute | solution.py:442
  385.7 54.5 %collective-permute-start.46 = (bf16[128,2048]{1,0:T(8,128)(2,1)S(1)}, bf16[128,2048]{1,0:T(8,128)(2,1)S(1)}, u32[]{:S(2)}, u32[]{:S(2)}) collective-permute-start(bf16[128,2048]{1,0:T(8,128)(2,1)S(1)} %add_convert_fusion.10.refs_0_), channel_id=1, source_target_pairs={{0,4},{4,0},{8,12},{12,8},{16,20},{20,16},{24,28},{28,24},{1,5},{5... | collective-permute-start | bytes 1572872 | tf_op jit(solution)/shard_map/ppermute | solution.py:442
  400.4 49.0 %collective-permute-start.47 = (bf16[128,2048]{1,0:T(8,128)(2,1)S(1)}, bf16[128,2048]{1,0:T(8,128)(2,1)S(1)}, u32[]{:S(2)}, u32[]{:S(2)}) collective-permute-start(bf16[128,2048]{1,0:T(8,128)(2,1)S(1)} %add_convert_fusion.10.refs_0_), channel_id=1, source_target_pairs={{0,8},{4,12},{8,0},{12,4},{16,24},{20,28},{24,16},{28,20},{1,9},{5... | collective-permute-start | bytes 1572872 | tf_op jit(solution)/shard_map/ppermute | solution.py:442
  408.8 63.0 %collective-permute-start.49 = (bf16[128,2048]{1,0:T(8,128)(2,1)S(1)}, bf16[128,2048]{1,0:T(8,128)(2,1)S(1)}, u32[]{:S(2)}, u32[]{:S(2)}) collective-permute-start(bf16[128,2048]{1,0:T(8,128)(2,1)S(1)} %get-tuple-element.282), channel_id=1, source_target_pairs={{0,16},{4,20},{8,24},{12,28},{16,0},{20,4},{24,8},{28,12},{1,17},{... | collective-permute-start | bytes 1572872 | tf_op jit(solution)/shard_map/ppermute | solution.py:442
  450.8 21.0 %collective-permute-start.50 = (bf16[128,2048]{1,0:T(8,128)(2,1)S(1)}, bf16[128,2048]{1,0:T(8,128)(2,1)S(1)}, u32[]{:S(2)}, u32[]{:S(2)}) collective-permute-start(bf16[128,2048]{1,0:T(8,128)(2,1)S(1)} %add_convert_fusion.9.refs_1_), channel_id=1, source_target_pairs={{0,4},{4,0},{8,12},{12,8},{16,20},{20,16},{24,28},{28,24},{1,5},{5... | collective-permute-start | bytes 1572872 | tf_op jit(solution)/shard_map/ppermute | solution.py:442
  452.1 22.1 %collective-permute-start.51 = (bf16[128,2048]{1,0:T(8,128)(2,1)S(1)}, bf16[128,2048]{1,0:T(8,128)(2,1)S(1)}, u32[]{:S(2)}, u32[]{:S(2)}) collective-permute-start(bf16[128,2048]{1,0:T(8,128)(2,1)S(1)} %add_convert_fusion.9.refs_1_), channel_id=1, source_target_pairs={{0,8},{4,12},{8,0},{12,4},{16,24},{20,28},{24,16},{28,20},{1,9},{5... | collective-permute-start | bytes 1572872 | tf_op jit(solution)/shard_map/ppermute | solution.py:442
  452.1 22.6 %collective-permute-start.52 = (bf16[128,2048]{1,0:T(8,128)(2,1)S(1)}, bf16[128,2048]{1,0:T(8,128)(2,1)S(1)}, u32[]{:S(2)}, u32[]{:S(2)}) collective-permute-start(bf16[128,2048]{1,0:T(8,128)(2,1)S(1)} %collective-permute-done.47.refs_2_), channel_id=1, source_target_pairs={{0,4},{4,0},{8,12},{12,8},{16,20},{20,16},{24,28},{28,24},{1,5},{5... | collective-permute-start | bytes 1572872 | tf_op jit(solution)/shard_map/ppermute | solution.py:442
  452.9 39.6 %collective-permute-start.48 = (bf16[128,2048]{1,0:T(8,128)(2,1)S(1)}, bf16[128,2048]{1,0:T(8,128)(2,1)S(1)}, u32[]{:S(2)}, u32[]{:S(2)}) collective-permute-start(bf16[128,2048]{1,0:T(8,128)(2,1)S(1)} %get-tuple-element.281), channel_id=1, source_target_pairs={{0,16},{4,20},{8,24},{12,28},{16,0},{20,4},{24,8},{28,12},{1,17},{... | collective-permute-start | bytes 1572872 | tf_op jit(solution)/shard_map/ppermute | solution.py:442
  476.1 22.9 %collective-permute-start.54 = (bf16[128,2048]{1,0:T(8,128)(2,1)S(1)}, bf16[128,2048]{1,0:T(8,128)(2,1)S(1)}, u32[]{:S(2)}, u32[]{:S(2)}) collective-permute-start(bf16[128,2048]{1,0:T(8,128)(2,1)S(1)} %add_convert_fusion.8.refs_1_), channel_id=1, source_target_pairs={{0,8},{4,12},{8,0},{12,4},{16,24},{20,28},{24,16},{28,20},{1,9},{5... | collective-permute-start | bytes 1572872 | tf_op jit(solution)/shard_map/ppermute | solution.py:442
  476.1 42.4 %collective-permute-start.57 = (bf16[128,2048]{1,0:T(8,128)(2,1)S(1)}, bf16[128,2048]{1,0:T(8,128)(2,1)S(1)}, u32[]{:S(2)}, u32[]{:S(2)}) collective-permute-start(bf16[128,2048]{1,0:T(8,128)(2,1)S(1)} %get-tuple-element.295), channel_id=1, source_target_pairs={{0,16},{4,20},{8,24},{12,28},{16,0},{20,4},{24,8},{28,12},{1,17},{... | collective-permute-start | bytes 1572872 | tf_op jit(solution)/shard_map/ppermute | solution.py:442
  501.0 23.9 %collective-permute-start.60 = (bf16[128,2048]{1,0:T(8,128)(2,1)S(1)}, bf16[128,2048]{1,0:T(8,128)(2,1)S(1)}, u32[]{:S(2)}, u32[]{:S(2)}) collective-permute-start(bf16[128,2048]{1,0:T(8,128)(2,1)S(1)} %collective-permute-done.54.refs_3_), channel_id=1, source_target_pairs={{0,4},{4,0},{8,12},{12,8},{16,20},{20,16},{24,28},{28,24},{1,5},{5... | collective-permute-start | bytes 1572872 | tf_op jit(solution)/shard_map/ppermute | solution.py:442
  524.9 27.7 %collective-permute-start.64 = (bf16[2,256,2048]{2,1,0:T(8,128)(2,1)}, bf16[2,256,2048]{2,1,0:T(8,128)(2,1)}, u32[]{:S(2)}, u32[]{:S(2)}) collective-permute-start(bf16[2,256,2048]{2,1,0:T(8,128)(2,1)} %fusion.29), channel_id=1, source_target_pairs={{0,1},{1,0},{2,3},{3,2},{4,5},{5,4},{6,7},{7,6},{8,9},{9,8},{10,11... | collective-permute-start | bytes 6291464 | tf_op jit(solution)/shard_map/ppermute | solution.py:431
  524.9 25.8 %collective-permute-start.56 = (bf16[512,512]{1,0:T(8,128)(2,1)}, bf16[512,512]{1,0:T(8,128)(2,1)S(1)}, u32[]{:S(2)}, u32[]{:S(2)}) collective-permute-start(bf16[512,512]{1,0:T(8,128)(2,1)} %get-tuple-element.294), channel_id=1, source_target_pairs={{0,16},{4,20},{8,24},{12,28},{16,0},{20,4},{24,8},{28,12},{1,17},{... | collective-permute-start | bytes 1572872 | tf_op jit(solution)/shard_map/ppermute | solution.py:442
  526.3 24.4 %collective-permute-start.61 = (bf16[128,2048]{1,0:T(8,128)(2,1)S(1)}, bf16[128,2048]{1,0:T(8,128)(2,1)}, u32[]{:S(2)}, u32[]{:S(2)}) collective-permute-start(bf16[128,2048]{1,0:T(8,128)(2,1)S(1)} %add_convert_fusion.6.refs_0_), channel_id=1, source_target_pairs={{0,4},{4,0},{8,12},{12,8},{16,20},{20,16},{24,28},{28,24},{1,5},{5... | collective-permute-start | bytes 1572872 | tf_op jit(solution)/shard_map/ppermute | solution.py:442
  527.5 25.1 %collective-permute-start.62 = (bf16[128,2048]{1,0:T(8,128)(2,1)S(1)}, bf16[128,2048]{1,0:T(8,128)(2,1)}, u32[]{:S(2)}, u32[]{:S(2)}) collective-permute-start(bf16[128,2048]{1,0:T(8,128)(2,1)S(1)} %add_convert_fusion.6.refs_0_), channel_id=1, source_target_pairs={{0,8},{4,12},{8,0},{12,4},{16,24},{20,28},{24,16},{28,20},{1,9},{5... | collective-permute-start | bytes 1572872 | tf_op jit(solution)/shard_map/ppermute | solution.py:442
  529.2 23.5 %collective-permute-start.63 = (bf16[128,2048]{1,0:T(8,128)(2,1)S(1)}, bf16[128,2048]{1,0:T(8,128)(2,1)S(1)}, u32[]{:S(2)}, u32[]{:S(2)}) collective-permute-start(bf16[128,2048]{1,0:T(8,128)(2,1)S(1)} %collective-permute-done.59.refs_3_), channel_id=1, source_target_pairs={{0,4},{4,0},{8,12},{12,8},{16,20},{20,16},{24,28},{28,24},{1,5},{5... | collective-permute-start | bytes 1572872 | tf_op jit(solution)/shard_map/ppermute | solution.py:442
  550.7 25.6 %collective-permute-start.65 = (bf16[512,512]{1,0:T(8,128)(2,1)}, bf16[512,512]{1,0:T(8,128)(2,1)S(1)}, u32[]{:S(2)}, u32[]{:S(2)}) collective-permute-start(bf16[512,512]{1,0:T(8,128)(2,1)} %get-tuple-element.305), channel_id=1, source_target_pairs={{0,16},{4,20},{8,24},{12,28},{16,0},{20,4},{24,8},{28,12},{1,17},{... | collective-permute-start | bytes 1572872 | tf_op jit(solution)/shard_map/ppermute | solution.py:442
  554.1 26.0 %collective-permute-start.66 = (bf16[512,512]{1,0:T(8,128)(2,1)S(1)}, bf16[512,512]{1,0:T(8,128)(2,1)S(1)}, u32[]{:S(2)}, u32[]{:S(2)}) collective-permute-start(bf16[512,512]{1,0:T(8,128)(2,1)S(1)} %add_convert_fusion.5.refs_0_), channel_id=1, source_target_pairs={{0,4},{4,0},{8,12},{12,8},{16,20},{20,16},{24,28},{28,24},{1,5},{5... | collective-permute-start | bytes 1572872 | tf_op jit(solution)/shard_map/ppermute | solution.py:442
  555.0 25.0 %collective-permute-start.67 = (bf16[512,512]{1,0:T(8,128)(2,1)S(1)}, bf16[512,512]{1,0:T(8,128)(2,1)S(1)}, u32[]{:S(2)}, u32[]{:S(2)}) collective-permute-start(bf16[512,512]{1,0:T(8,128)(2,1)S(1)} %add_convert_fusion.5.refs_0_), channel_id=1, source_target_pairs={{0,8},{4,12},{8,0},{12,4},{16,24},{20,28},{24,16},{28,20},{1,9},{5... | collective-permute-start | bytes 1572872 | tf_op jit(solution)/shard_map/ppermute | solution.py:442
  556.2 23.9 %collective-permute-start.68 = (bf16[128,2048]{1,0:T(8,128)(2,1)}, bf16[128,2048]{1,0:T(8,128)(2,1)S(1)}, u32[]{:S(2)}, u32[]{:S(2)}) collective-permute-start(bf16[128,2048]{1,0:T(8,128)(2,1)} %collective-permute-done.62.refs_2_), channel_id=1, source_target_pairs={{0,4},{4,0},{8,12},{12,8},{16,20},{20,16},{24,28},{28,24},{1,5},{5... | collective-permute-start | bytes 1572872 | tf_op jit(solution)/shard_map/ppermute | solution.py:442
  560.5 46.7 %collective-permute-start.70 = (bf16[256,2048]{1,0:T(8,128)(2,1)S(1)}, bf16[256,2048]{1,0:T(8,128)(2,1)S(1)}, u32[]{:S(2)}, u32[]{:S(2)}) collective-permute-start(bf16[256,2048]{1,0:T(8,128)(2,1)S(1)} %fusion.43), channel_id=1, source_target_pairs={{0,2},{1,3},{2,0},{3,1},{4,6},{5,7},{6,4},{7,5},{8,10},{9,11},{10,... | collective-permute-start | bytes 3145736 | tf_op jit(solution)/shard_map/ppermute | solution.py:439
  577.5 25.5 %collective-permute-start.71 = (bf16[512,512]{1,0:T(8,128)(2,1)S(1)}, bf16[512,512]{1,0:T(8,128)(2,1)S(1)}, u32[]{:S(2)}, u32[]{:S(2)}) collective-permute-start(bf16[512,512]{1,0:T(8,128)(2,1)S(1)} %copy-done.98), channel_id=1, source_target_pairs={{0,16},{4,20},{8,24},{12,28},{16,0},{20,4},{24,8},{28,12},{1,17},{... | collective-permute-start | bytes 1572872 | tf_op jit(solution)/shard_map/ppermute | solution.py:442
  581.4 25.8 %collective-permute-start.72 = (bf16[512,512]{1,0:T(8,128)(2,1)S(1)}, bf16[512,512]{1,0:T(8,128)(2,1)S(1)}, u32[]{:S(2)}, u32[]{:S(2)}) collective-permute-start(bf16[512,512]{1,0:T(8,128)(2,1)S(1)} %add_convert_fusion.4.refs_1_), channel_id=1, source_target_pairs={{0,4},{4,0},{8,12},{12,8},{16,20},{20,16},{24,28},{28,24},{1,5},{5... | collective-permute-start | bytes 1572872 | tf_op jit(solution)/shard_map/ppermute | solution.py:442
  582.9 25.0 %collective-permute-start.73 = (bf16[512,512]{1,0:T(8,128)(2,1)S(1)}, bf16[512,512]{1,0:T(8,128)(2,1)S(1)}, u32[]{:S(2)}, u32[]{:S(2)}) collective-permute-start(bf16[512,512]{1,0:T(8,128)(2,1)S(1)} %add_convert_fusion.4.refs_1_), channel_id=1, source_target_pairs={{0,8},{4,12},{8,0},{12,4},{16,24},{20,28},{24,16},{28,20},{1,9},{5... | collective-permute-start | bytes 1572872 | tf_op jit(solution)/shard_map/ppermute | solution.py:442
  585.1 22.8 %collective-permute-start.74 = (bf16[512,512]{1,0:T(8,128)(2,1)S(1)}, bf16[512,512]{1,0:T(8,128)(2,1)S(1)}, u32[]{:S(2)}, u32[]{:S(2)}) collective-permute-start(bf16[512,512]{1,0:T(8,128)(2,1)S(1)} %collective-permute-done.67.refs_2_), channel_id=1, source_target_pairs={{0,4},{4,0},{8,12},{12,8},{16,20},{20,16},{24,28},{28,24},{1,5},{5... | collective-permute-start | bytes 1572872 | tf_op jit(solution)/shard_map/ppermute | solution.py:442
  607.2 24.8 %collective-permute-start.76 = (bf16[512,512]{1,0:T(8,128)(2,1)S(1)}, bf16[512,512]{1,0:T(8,128)(2,1)S(1)}, u32[]{:S(2)}, u32[]{:S(2)}) collective-permute-start(bf16[512,512]{1,0:T(8,128)(2,1)S(1)} %copy-done.97), channel_id=1, source_target_pairs={{0,16},{4,20},{8,24},{12,28},{16,0},{20,4},{24,8},{28,12},{1,17},{... | collective-permute-start | bytes 1572872 | tf_op jit(solution)/shard_map/ppermute | solution.py:442
  608.0 25.6 %collective-permute-start.77 = (bf16[512,512]{1,0:T(8,128)(2,1)S(1)}, bf16[512,512]{1,0:T(8,128)(2,1)S(1)}, u32[]{:S(2)}, u32[]{:S(2)}) collective-permute-start(bf16[512,512]{1,0:T(8,128)(2,1)S(1)} %add_convert_fusion.3.refs_1_), channel_id=1, source_target_pairs={{0,4},{4,0},{8,12},{12,8},{16,20},{20,16},{24,28},{28,24},{1,5},{5... | collective-permute-start | bytes 1572872 | tf_op jit(solution)/shard_map/ppermute | solution.py:442
  608.9 24.7 %collective-permute-start.78 = (bf16[512,512]{1,0:T(8,128)(2,1)S(1)}, bf16[512,512]{1,0:T(8,128)(2,1)S(1)}, u32[]{:S(2)}, u32[]{:S(2)}) collective-permute-start(bf16[512,512]{1,0:T(8,128)(2,1)S(1)} %add_convert_fusion.3.refs_1_), channel_id=1, source_target_pairs={{0,8},{4,12},{8,0},{12,4},{16,24},{20,28},{24,16},{28,20},{1,9},{5... | collective-permute-start | bytes 1572872 | tf_op jit(solution)/shard_map/ppermute | solution.py:442
  611.3 22.4 %collective-permute-start.79 = (bf16[512,512]{1,0:T(8,128)(2,1)S(1)}, bf16[512,512]{1,0:T(8,128)(2,1)S(1)}, u32[]{:S(2)}, u32[]{:S(2)}) collective-permute-start(bf16[512,512]{1,0:T(8,128)(2,1)S(1)} %collective-permute-done.73.refs_3_), channel_id=1, source_target_pairs={{0,4},{4,0},{8,12},{12,8},{16,20},{20,16},{24,28},{28,24},{1,5},{5... | collective-permute-start | bytes 1572872 | tf_op jit(solution)/shard_map/ppermute | solution.py:442
  611.9 21.8 %collective-permute-start.80 = (f32[15872]{0:T(1024)S(1)}, f32[15872]{0:T(1024)S(1)}, u32[]{:S(2)}, u32[]{:S(2)}) collective-permute-start(f32[15872]{0:T(1024)S(1)} %pad_maximum_fusion.5), channel_id=1, source_target_pairs={{0,4},{4,0},{8,12},{12,8},{16,20},{20,16},{24,28},{28,24},{1,5},{5... | collective-permute-start | bytes 190472 | tf_op jit(solution)/shard_map/ppermute | solution.py:442
  (182 other events, 2153.2 us)

commit v5 on v4

--- a/solution.py
+++ b/solution.py
@@ -2,6 +2,7 @@
 
 import jax
 import jax.numpy as jnp
+import numpy as np
 from jax import lax
 from jax.experimental import pallas as pl
 from jax.experimental.pallas import tpu as pltpu
@@ -16,11 +17,17 @@
 F32 = jnp.float32
 
 
-def rotary_tables(length, rot_dims):
-    half_dims = rot_dims // 2
-    frequency = 10000.0 ** (-2.0 * jnp.arange(half_dims, dtype=F32) / rot_dims)
-    angles = jnp.arange(length, dtype=F32)[:, None] * frequency[None, :]
-    return jnp.cos(angles), jnp.sin(angles)
+def rotary_table(length):
+    half = ROT // 2
+    frequency = (10000.0 ** (-2.0 * np.arange(half, dtype=np.float32) / ROT)).astype(np.float32)
+    angles = np.arange(length, dtype=np.float32)[:, None] * frequency[None, :]
+    cosine, sine = np.cos(angles), np.sin(angles)
+    table = np.zeros((length, 3 * 128), np.float32)
+    table[:, ROT:128] = 1.0
+    table[:, :half] = table[:, half:ROT] = cosine
+    table[:, 128 : 128 + half] = -sine
+    table[:, 256 + half : 256 + ROT] = sine
+    return table
 
 
 def contract(left_side, right_side, left_dim, right_dim):
@@ -42,16 +49,6 @@
     return lax.optimization_barrier((value,) + earlier)[0]
 
 
-def rotary_lanes(cosine, sine):
-    ones = jnp.ones((cosine.shape[0], 128 - ROT), F32)
-    none = jnp.zeros_like(sine)
-    rest = jnp.zeros_like(ones)
-    keep = jnp.concatenate([cosine, cosine, ones], axis=1)
-    up = jnp.concatenate([-sine, none, rest], axis=1)
-    down = jnp.concatenate([none, sine, rest], axis=1)
-    return keep, up, down
-
-
 def turned(block, keep, up, down, sign):
     head = block[:, :128]
     half = ROT // 2
@@ -69,7 +66,8 @@
 
     def project(at):
         return (
-            jnp.dot(x_ref[at, :], w_ref[...], preferred_element_type=F32) + b_ref[...]
+            jnp.dot(x_ref[at, :], w_ref[...], preferred_element_type=F32)
+            + b_ref[...].astype(F32)
         )
 
     for start in range(0, rows, tile):
@@ -86,14 +84,13 @@
             ).astype(BF)
 
 
-def project_qkv(normed, weight, bias, tables, length, whole=None):
+def project_qkv(normed, weight, bias, table, length, whole=None):
     rows, width = normed.shape
     columns = weight.shape[1]
     part = 0 if whole is None else 1
     if part and rows * 2 != length:
-        rest = project_qkv(normed, weight, bias, tables, rows)
+        rest = project_qkv(normed, weight, bias, table[length - rows :], rows)
         return jnp.concatenate([whole[: length - rows], rest], axis=0)
-    table = pl.BlockSpec((rows, 128), lambda j: (0, 0))
     return pl.pallas_call(
         qkv_kernel,
         grid=(columns // HD,),
@@ -101,10 +98,8 @@
             pl.BlockSpec((rows, width), lambda j: (0, 0)),
             pl.BlockSpec((width, HD), lambda j: (0, j)),
             pl.BlockSpec((1, HD), lambda j: (0, j)),
-            table,
-            table,
-            table,
         ]
+        + [pl.BlockSpec((rows, 128), lambda j, k=k: (part, k)) for k in range(3)]
         + [pl.BlockSpec(memory_space=pl.ANY)] * part,
         out_specs=pl.BlockSpec((rows, HD), lambda j: (part, j)),
         out_shape=jax.ShapeDtypeStruct((length, columns), BF),
@@ -116,7 +111,7 @@
             transcendentals=0,
         ),
         name="qkv_rotary",
-    )(normed, weight, bias.astype(F32)[None, :], *tables, *([whole] if part else []))
+    )(normed, weight, bias[None, :], table, table, table, *([whole] if part else []))
 
 
 def visible_scores(queries, keys, row_spots, key_spots, prefix):
@@ -210,11 +205,10 @@
     o_ref[:, 2 * HD :] = dv_ref[...].astype(BF)
 
 
-def attend_back(qkv, grad_context, log_total, prefix, spots, tables):
+def attend_back(qkv, grad_context, log_total, prefix, spots, table):
     length = qkv.shape[0]
     heads = qkv.shape[1] // (3 * HD)
     part = lambda n: pl.BlockSpec((length, HD), lambda h, p: (0, 3 * h + n))
-    table = pl.BlockSpec((length, 128), lambda h, p: (0, 0))
     return pl.pallas_call(
         attend_back_kernel,
         grid_spec=pltpu.PrefetchScalarGridSpec(
@@ -228,10 +222,8 @@
                 pl.BlockSpec((1, length, 1), lambda h, p: (h, 0, 0)),
                 pl.BlockSpec((length, 1), lambda h, p: (0, 0)),
                 pl.BlockSpec((1, length), lambda h, p: (0, 0)),
-                table,
-                table,
-                table,
-            ],
+            ]
+            + [pl.BlockSpec((length, 128), lambda h, p, k=k: (0, k)) for k in range(3)],
             out_specs=pl.BlockSpec((length, 3 * HD), lambda h, p: (0, h)),
             scratch_shapes=[pltpu.VMEM((length, HD), F32), pltpu.VMEM((length, HD), F32)],
         ),
@@ -243,7 +235,7 @@
             transcendentals=heads * length * length,
         ),
         name="attend_back",
-    )(prefix, qkv, qkv, qkv, grad_context, log_total, spots[:, None], spots[None, :], *tables)
+    )(prefix, qkv, qkv, qkv, grad_context, log_total, spots[:, None], spots[None, :], table, table, table)
 
 
 def place_kernel(quarter_ref, *refs):
@@ -282,8 +274,8 @@
     )(quarter.reshape(1), *operands)
 
 
-def norms_kernel(count, gains_ref, *refs):
-    blocks, (attn_ref, mlp_ref) = refs[:count], refs[count:]
+def norms_kernel(count, *refs):
+    gains, blocks, (attn_ref, mlp_ref) = refs[:4], refs[4 : 4 + count], refs[4 + count :]
     for index, block in enumerate(blocks):
 
         @pl.when(pl.program_id(0) == index)
@@ -293,8 +285,9 @@
             centered = features - average
             spread = jnp.mean(centered * centered, axis=-1, keepdims=True)
             xhat = centered * lax.rsqrt(spread + EPSILON)
-            attn_ref[...] = (xhat * gains_ref[0:1, :] + gains_ref[1:2, :]).astype(BF)
-            mlp_ref[...] = (xhat * gains_ref[2:3, :] + gains_ref[3:4, :]).astype(BF)
+            gain_a, shift_a, gain_m, shift_m = (ref[...].astype(F32) for ref in gains)
+            attn_ref[...] = (xhat * gain_a + shift_a).astype(BF)
+            mlp_ref[...] = (xhat * gain_m + shift_m).astype(BF)
 
 
 def both_norms(blocks, gains):
@@ -304,7 +297,7 @@
     return pl.pallas_call(
         functools.partial(norms_kernel, count),
         grid=(count,),
-        in_specs=[pl.BlockSpec((8, width), lambda i: (0, 0))]
+        in_specs=[pl.BlockSpec((1, width), lambda i: (0, 0))] * 4
         + [pl.BlockSpec((rows, width), lambda i: (0, 0))] * count,
         out_specs=[pl.BlockSpec((rows, width), lambda i: (i, 0))] * 2,
         out_shape=[shape, shape],
@@ -315,45 +308,51 @@
             transcendentals=0,
         ),
         name="both_norms",
-    )(gains, *blocks)
-
-
-def outer_kernel(near_ref, far_ref, right_ref, *refs):
-    rights, (o_ref, left_ref, joined_ref) = refs[:-3], refs[-3:]
-    near = near_ref.shape[0]
-    rows = rights[0].shape[0]
+    )(*gains, *blocks)
+
+
+def outer_kernel(lefts, pieces, _, *refs):
+    left_refs, rights, (o_ref, left_ref, joined_ref) = refs[:lefts], refs[lefts:-3], refs[-3:]
 
     @pl.when(pl.program_id(0) == 0)
     def _():
-        for start in range(0, near, rows):
-            left_ref[:, pl.ds(start, rows)] = near_ref[pl.ds(start, rows), :].T
-        for start in range(0, far_ref.shape[0], rows):
-            left_ref[:, pl.ds(near + start, rows)] = far_ref[pl.ds(start, rows), :].T
-
-    joined_ref[:near, :] = right_ref[...]
-    for index, right in enumerate(rights):
-        joined_ref[pl.ds(near + index * rows, rows), :] = right[...]
+        for ref, (row, column) in zip(left_refs, pieces):
+            count, width = ref.shape
+            step = min(count, 256)
+            for start in range(0, count, step):
+                left_ref[pl.ds(row, width), pl.ds(column + start, step)] = ref[
+                    pl.ds(start, step), :
+                ].T
+
+    column = 0
+    for ref in rights:
+        joined_ref[pl.ds(column, ref.shape[0]), :] = ref[...]
+        column += ref.shape[0]
     o_ref[...] = jnp.dot(left_ref[...], joined_ref[...], preferred_element_type=F32).astype(BF)
 
 
-def outer_blocks(near, far, near_right, far_blocks):
-    length, left = near.shape
-    width = near_right.shape[1]
-    rows = far_blocks[0].shape[0]
-    tokens = length + far.shape[0]
+def outer_blocks(lefts, rights, quarter):
+    width = rights[0].shape[1]
+    tokens = sum(r.shape[0] for r in rights)
+    left = max(row + taken for _, taken, row, _ in lefts)
     tile = 512
+    specs = [
+        pl.BlockSpec((a.shape[0], taken), lambda j, q: (0, q[0]))
+        if taken < a.shape[1]
+        else pl.BlockSpec(a.shape, lambda j, q: (0, 0))
+        for a, taken, _, _ in lefts
+    ]
     return pl.pallas_call(
-        outer_kernel,
-        grid=(width // tile,),
-        in_specs=[
-            pl.BlockSpec((length, left), lambda j: (0, 0)),
-            pl.BlockSpec(far.shape, lambda j: (0, 0)),
-            pl.BlockSpec((length, tile), lambda j: (0, j)),
-        ]
-        + [pl.BlockSpec((rows, tile), lambda j: (0, j))] * len(far_blocks),
-        out_specs=pl.BlockSpec((left, tile), lambda j: (0, j)),
+        functools.partial(outer_kernel, len(lefts), [(r, t) for _, _, r, t in lefts]),
+        grid_spec=pltpu.PrefetchScalarGridSpec(
+            num_scalar_prefetch=1,
+            grid=(width // tile,),
+            in_specs=specs
+            + [pl.BlockSpec((r.shape[0], tile), lambda j, q: (0, j)) for r in rights],
+            out_specs=pl.BlockSpec((left, tile), lambda j, q: (0, j)),
+            scratch_shapes=[pltpu.VMEM((left, tokens), BF), pltpu.VMEM((tokens, tile), BF)],
+        ),
         out_shape=jax.ShapeDtypeStruct((left, width), BF),
-        scratch_shapes=[pltpu.VMEM((left, tokens), BF), pltpu.VMEM((tokens, tile), BF)],
         compiler_params=pltpu.CompilerParams(vmem_limit_bytes=56 << 20),
         cost_estimate=pl.CostEstimate(
             flops=2 * tokens * left * width,
@@ -361,7 +360,7 @@
             transcendentals=0,
         ),
         name="outer_blocks",
-    )(near, far, near_right, *far_blocks)
+    )(quarter.reshape(1), *[a for a, _, _, _ in lefts], *rights)
 
 
 def back_kernel(weight_ref, slope_ref, *refs):
@@ -463,6 +462,10 @@
         across = [flip(block, 2) for block in over_y]
         return corner, beside, across
 
+    def last_far(second):
+        half = rows // 2
+        return [(flip(v[:half], 1), flip(u[half:], 2)) for u, v in zip(second[1], second[2])]
+
     def far_parts(first, second, last):
         corner, beside, across = second
         parts = []
@@ -471,6 +474,10 @@
                 parts += [block, to_core(block)]
         return parts
 
+    def meet(*trees):
+        leaves, shape = jax.tree.flatten(trees)
+        return jax.tree.unflatten(shape, lax.optimization_barrier(tuple(leaves)))
+
     def quarter_of(v, axis, index):
         size = v.shape[axis] // 4
         return lax.dynamic_slice_in_dim(v, index * size, size, axis)
@@ -483,64 +490,51 @@
     gain_mlp = ln2_gain.astype(F32)
     shift_mlp = ln2_bias.astype(F32)
     mask_f = valid_mask.astype(F32)
-    gains = jnp.pad(
-        jnp.stack([gain_attn, shift_attn, gain_mlp, shift_mlp]), ((0, 4), (0, 0))
-    )
+    gains = [v[None, :] for v in (ln1_gain, ln1_bias, ln2_gain, ln2_bias)]
+    close = 2 * rows
+
+    def units(normed):
+        return jnp.dot(normed, fc1_weight, preferred_element_type=F32) + fc1_bias.astype(F32)
+
     count = jnp.full((8, 128), jnp.sum(mask_f), F32)
+    count = count + to_core(count)
+    counted = flip(count, 1)
     near_blocks, hidden_y = gather_near(hidden)
     first = first_far(hidden)
-    count = count + to_core(count)
-
-    cosine_all, sine_all = rotary_tables(LEN, ROT)
-
-    def in_order(table):
-        return jnp.concatenate(
-            [lax.dynamic_slice_in_dim(table, b * rows, rows, 0) for b in block_ids], axis=0
-        )
-
-    tables = rotary_lanes(in_order(cosine_all), in_order(sine_all))
-    spots = jnp.concatenate([b * rows + jnp.arange(rows, dtype=jnp.int32) for b in block_ids])
-    close = 2 * rows
-
-    def units(normed):
-        return jnp.dot(normed, fc1_weight, preferred_element_type=F32) + fc1_bias.astype(F32)
-
     norm_attn_own, norm_mlp_own = both_norms(near_blocks[:2], gains)
     pre_own = units(norm_mlp_own)
     active_own = exact_gelu(pre_own)[0].astype(BF)
-    qkv_own = project_qkv(norm_attn_own, qkv_weight, qkv_bias, [t[:close] for t in tables], LEN)
-
-    arrived = lax.optimization_barrier(
-        (active_own, qkv_own, count, *first, *near_blocks[2:])
-    )
-    active_own, qkv_own, count, *rest = arrived
-    first, rest_blocks = rest[:2], rest[2:]
-    count = count + flip(count, 1)
-    norm_attn_rest, norm_mlp_rest = both_norms(rest_blocks, gains)
-    count, norm_attn_rest = lax.optimization_barrier((count, norm_attn_rest))
-    count = count + flip(count, 2)
-    qkv_low = project_qkv(
-        norm_attn_rest, qkv_weight, qkv_bias, [t[close:] for t in tables], LEN, qkv_own
-    )
-    count, qkv_low = lax.optimization_barrier((count, qkv_low))
-    mask = 4
-    while mask < dp:
-        count = count + flip(count, mask)
-        mask *= 2
+    table = jnp.concatenate(
+        [
+            lax.dynamic_slice_in_dim(jnp.asarray(rotary_table(LEN)), b * rows, rows, 0)
+            for b in block_ids
+        ],
+        axis=0,
+    )
+    spots = jnp.concatenate([b * rows + jnp.arange(rows, dtype=jnp.int32) for b in block_ids])
+    active_own, table = after(active_own, table), after(table, active_own)
+    qkv_own = project_qkv(norm_attn_own, qkv_weight, qkv_bias, table, LEN)
+    active_own, qkv_own, counted, first, hidden_y = meet(
+        active_own, qkv_own, counted, first, hidden_y
+    )
+    count = count + counted
+
+    near_blocks = near_blocks[:2]
+    for block in hidden_y:
+        near_blocks += [block, to_core(block)]
+    second = second_far(first, hidden_y)
+    counted = flip(count, 2)
+    norm_attn_rest, norm_mlp_rest = both_norms(near_blocks[2:], gains)
+    qkv_low = project_qkv(norm_attn_rest, qkv_weight, qkv_bias, table, LEN, qkv_own)
     context, log_total = attend(qkv_low, prefix_len, spots)
-    count, context, *first = lax.optimization_barrier((count, context, *first))
-    second = second_far(first, hidden_y)
+    norm_mlp_rest = after(norm_mlp_rest, context)
     context_far = swap_quarters(context)
-    bit = 2
-    while bit < tp:
-        count = count + lax.ppermute(count, "tensor", [(t, t ^ bit) for t in range(tp)])
-        bit *= 2
     pre_rest = units(norm_mlp_rest)
     active_rest = exact_gelu(pre_rest)[0].astype(BF)
-    active_rest, count, *corner = lax.optimization_barrier((active_rest, count, second[0]))
-    count_all = count[0, 0]
-    last = [from_y(corner[0], step) for step in range(1, ways)]
-    far_blocks = far_parts(first, (corner[0], second[1], second[2]), last)
+    active_rest, context, counted, second, context_far = meet(
+        active_rest, context, counted, second, context_far
+    )
+    count = count + counted
 
     def branch_rows(context_rows, active_rows):
         return jnp.dot(context_rows, out_weight, preferred_element_type=F32) + jnp.dot(
@@ -551,15 +545,46 @@
         blocks = part.reshape(-1, 2, rows, D)
         return blocks[:, 0] + to_core(blocks[:, 1].astype(BF)).astype(F32)
 
-    sums = core_total(branch_rows(context[close:], active_rest))
-    leaving = [sums[step - 1].astype(BF) for step in range(1, ways)]
-    came = [to_y(low, step) for step, low in enumerate(leaving, 1)]
-    active_now, context_now, *far_blocks = lax.optimization_barrier(
-        (active_own, context[:close], *far_blocks, leaving[0])
-    )[:-1]
-    branch = core_total(branch_rows(context_now, active_now))[0]
-    far_blocks[0] = after(far_blocks[0], branch)
+    last = last_far(second)
+    counted = jnp.zeros_like(count)
+    bit = 2
+    while bit < tp:
+        counted = lax.ppermute(count, "tensor", [(t, t ^ bit) for t in range(tp)])
+        bit *= 2
+        if bit < tp:
+            count = count + counted
+    part_rest = branch_rows(context[close:], active_rest).reshape(-1, 2, rows, D)
+    mates_rest = to_core(part_rest[:, 1].astype(BF))
+    part_own = branch_rows(context[:close], after(active_own, part_rest)).reshape(2, rows, D)
+    part_own, mates_rest, last, counted = meet(part_own, mates_rest, last, counted)
+    count = count + counted
+
+    sums = part_rest[:, 0] + mates_rest.astype(F32)
+    came = [to_y(sums[step - 1].astype(BF), step) for step in range(1, ways)]
+    mates_own = to_core(part_own[1].astype(BF))
+    counted = flip(count, 4) if dp > 4 else jnp.zeros_like(count)
+    last = [jnp.concatenate(pair, axis=0) for pair in last]
+    far_blocks = far_parts(first, second, last)
     norm_attn_far, norm_mlp_far = both_norms(far_blocks, gains)
+    came, mates_own, counted, norm_mlp_far = meet(came, mates_own, counted, norm_mlp_far)
+    count = count + counted
+    mask = 8
+    while mask < dp:
+        count = count + flip(count, mask)
+        mask *= 2
+    branch = part_own[0] + mates_own.astype(F32)
+    for got in came:
+        branch = branch + got.astype(F32)
+    output_f = hidden.astype(F32) + branch + out_bias.astype(F32) + fc2_bias.astype(F32)
+    mismatch = output_f - teacher.astype(F32)
+    error_part = jnp.sum(mask_f[:, None] * mismatch * mismatch)
+    grad_out = mask_f[:, None] * mismatch * (2.0 * total_tokens / count[0, 0])
+    grad_low = grad_out.astype(BF)
+    grad_out, grad_low, norm_mlp_far = meet(grad_out, grad_low, norm_mlp_far)
+
+    grad_y = [from_y(grad_low, step) for step in range(1, ways)]
+    grad_first = first_far(grad_low)
+    grad_mate = to_core(grad_low)
     fc1_quarter = quarter_of(fc1_weight, 1, quarter)
     fc2_quarter = quarter_of(fc2_weight, 0, quarter)
     pre_far = jnp.dot(norm_mlp_far, fc1_quarter, preferred_element_type=F32) + quarter_of(
@@ -567,44 +592,31 @@
     ).astype(F32)
     active_far, slope_far = exact_gelu(pre_far)
     active_far = active_far.astype(BF)
-    left_far = jnp.concatenate([active_far, jnp.concatenate(context_far, axis=0)], axis=1)
-    left_near = jnp.concatenate(
-        [
-            jnp.concatenate(
-                [quarter_of(active_own, 1, quarter), quarter_of(active_rest, 1, quarter)], axis=0
-            ),
-            quarter_of(context, 1, quarter),
-        ],
-        axis=1,
-    )
-    came = lax.optimization_barrier((*came, left_far, left_near))
-    (*came, left_far, left_near) = came
-    for got in came:
-        branch = branch + got.astype(F32)
-
-    output_f = hidden.astype(F32) + branch + out_bias.astype(F32) + fc2_bias.astype(F32)
-    mismatch = output_f - teacher.astype(F32)
-    error_part = jnp.sum(mask_f[:, None] * mismatch * mismatch)
-    grad_out = mask_f[:, None] * mismatch * (2.0 * total_tokens / count_all)
-    grad_low = grad_out.astype(BF)
-    grad_blocks, grad_y = gather_near(grad_low)
-    grad_first = first_far(grad_low)
-    tied = lax.optimization_barrier((*grad_first, *grad_blocks, *grad_y))
-    grad_first, tied = list(tied[:2]), tied[2:]
-    grad_blocks, grad_y = list(tied[: 2 * ways]), list(tied[2 * ways :])
+    grad_y, grad_first, active_far, grad_mate = meet(grad_y, grad_first, active_far, grad_mate)
+
     grad_second = second_far(grad_first, grad_y)
+    grad_blocks = [grad_low, grad_mate]
+    for block in grad_y:
+        grad_blocks += [block, to_core(block)]
     grad_near = jnp.concatenate(grad_blocks, axis=0)
     hidden_pre = jnp.concatenate([pre_own, pre_rest], axis=0)
     grad_inner = (contract(grad_near, fc2_weight, 1, 1) * exact_gelu(hidden_pre)[1]).astype(BF)
     grad_context = contract(grad_near, out_weight, 1, 1).astype(BF)
-    grad_inner, grad_context, corner, *tied = lax.optimization_barrier(
-        (grad_inner, grad_context, grad_second[0], *grad_second[1], *grad_second[2])
-    )
-    grad_second = (corner, list(tied[: ways - 1]), list(tied[ways - 1 :]))
-    grad_last = [from_y(corner, step) for step in range(1, ways)]
-    grad_far = far_parts(grad_first, grad_second, grad_last)
-    grad_qkv = attend_back(qkv_low, grad_context, log_total, prefix_len, spots, tables)
-    grad_qkv, *grad_far = lax.optimization_barrier((grad_qkv, *grad_far))
+    grad_inner, grad_context, grad_near, grad_second = meet(
+        grad_inner, grad_context, grad_near, grad_second
+    )
+
+    grad_last = last_far(grad_second)
+    corner, beside, across = grad_second
+    ahead = [grad_first[0]] + beside + [grad_first[1]] + across + [corner]
+    mates = [to_core(block) for block in ahead]
+    grad_qkv = attend_back(qkv_low, grad_context, log_total, prefix_len, spots, table)
+    grad_qkv, grad_last, mates = meet(grad_qkv, grad_last, mates)
+
+    grad_last = [jnp.concatenate(pair, axis=0) for pair in grad_last]
+    ahead += grad_last
+    mates += [to_core(block) for block in grad_last]
+    grad_far = [block for pair in zip(ahead, mates) for block in pair]
     bias_part = jnp.sum(grad_out, axis=0)
 
     queue = []
@@ -724,8 +736,17 @@
             whole = lax.dynamic_update_slice(whole, piece.astype(F32), start)
         return whole
 
-    part = outer_blocks(left_near, left_far, grad_near, grad_far)
     mine = active_far.shape[1]
+    lefts = [
+        (active_own, mine, 0, 0),
+        (active_rest, mine, 0, close),
+        (active_far, mine, 0, LEN),
+    ]
+    kept_columns = context.shape[1] // 4
+    context_parts = [quarter_of(context, 1, quarter)] + context_far
+    for index, piece in enumerate(context_parts):
+        lefts.append((piece, kept_columns, mine, index * LEN))
+    part = outer_blocks(lefts, [grad_near] + grad_far, quarter)
     enqueue("fc2", part[:mine], 4)
     enqueue("out", part[mine:], 1)
     turn()
@@ -754,7 +775,8 @@
     grad_norm_mlp = contract(gate(grad_inner), fc1_weight, 1, 1)
     (grad_norm_mlp,) = turn(grad_norm_mlp)
 
-    features = gate(jnp.concatenate(near_blocks, axis=0)).astype(F32)
+    near_blocks = lax.optimization_barrier((token[0], *near_blocks))[1:]
+    features = jnp.concatenate(near_blocks, axis=0).astype(F32)
     centered = features - jnp.mean(features, axis=-1, keepdims=True)
     inverse = lax.rsqrt(jnp.mean(centered * centered, axis=-1, keepdims=True) + EPSILON)
     xhat = centered * inverse
@@ -800,7 +822,7 @@
     vectors = small[: 6 * D].reshape(6, D)
     fc1_bias_grad = small[6 * D : 6 * D + fc1_bias_part.shape[0]]
     qkv_bias_grad = small[6 * D + fc1_bias_part.shape[0] :]
-    loss_value = vectors[5, 0] / (count_all * D)
+    loss_value = vectors[5, 0] / (count[0, 0] * D)
     fc2_weight_grad = place("fc2", 0, 4)
     out_weight_grad = place("out", 0, 1)
     fc1_weight_grad = place("fc1", 1, 4)

time: 769 us -> 651 us (0.85)
  waiting for transfers between devices: 288 us -> 161 us
  Pallas kernels: 135 us -> 144 us
    ppermute x88 -> x92, waiting for transfers between devices: 213 us -> 148 us  [flip(): return lax.ppermute(v, 'dp', [(d, d ^ mask) for d in range(dp)])]
    ppermute x6 -> x4, waiting for transfers between devices: 70.6 us -> 9.7 us  [from_y(): return lax.ppermute(v, 'tensor', pairs)]
    concatenate x7 -> x1, other arithmetic: 14.6 us -> 0.1 us  [on_device(): jnp.concatenate([lax.dynamic_slice_in_dim(jnp.asarray(rotary_table(LEN)),...]
    pallas_call x3, Pallas kernels: 28 us -> 37.4 us  [both_norms(): pl.pallas_call(functools.partial(norms_kernel, count), grid=(count,), in_...]
    ppermute x88 -> x92, starting transfers between devices: 94.8 us -> 104 us  [flip(): return lax.ppermute(v, 'dp', [(d, d ^ mask) for d in range(dp)])]
    unnamed x258 -> x246, local copies, waits for them, and re-layouts: 21.8 us -> 24.3 us
  transfers between devices with their start and end apart: 119 -> 121, of which waited for: 50 -> 44; matrix products, arithmetic and copies ran while one was open for 25% -> 29% of each run, Pallas kernels for 14% -> 21%
where the time goes in v5:
time: 651 us; the launch traced here: 646 us
  waiting for transfers between devices  161 us (25%)
  Pallas kernels  144 us (22%)
  matrix products  120 us (18%)
  starting transfers between devices  115 us (18%)
  local copies, waits for them, and re-layouts  50.9 us (8%)
  other arithmetic  48.9 us (8%)
  between operations  6.58 us (1%)
    ppermute x92, waiting for transfers between devices, flip(): return lax.ppermute(v, 'dp', [(d, d ^ mask) for d in range(dp)])  148 us
    ppermute x92, starting transfers between devices, flip(): return lax.ppermute(v, 'dp', [(d, d ^ mask) for d in range(dp)])  104 us
    dot_general x10, matrix products, contract(): lax.dot_general(left_side, right_side, (((left_dim,), (right_dim,)), ((),...  74.6 us
    pallas_call x17, Pallas kernels, place_quarters(): pl.pallas_call(place_kernel, grid_spec=pltpu.PrefetchScalarGridSpec(num_s...  38.9 us
    pallas_call x3, Pallas kernels, both_norms(): pl.pallas_call(functools.partial(norms_kernel, count), grid=(count,), in_...  37.4 us
    unnamed x246, local copies, waits for them, and re-layouts  24.3 us
    dot_general x2, matrix products, units(): jnp.dot(normed, fc1_weight, preferred_element_type=F32)  20.7 us
    pallas_call x1, Pallas kernels, outer_blocks(): pl.pallas_call(functools.partial(outer_kernel, len(lefts), [(r, t) for _,...  17.8 us
  transfers between devices with their start and end apart: 121, of which 44 were waited for; matrix products, arithmetic and copies ran while one was open for 29% of the time, Pallas kernels for 21%

profile of v5, /device:TPU:0, one launch (start us, length us, event | category | flops | bytes accessed | tf_op | source)
XLA Modules:
  0.0 645.8 jit_solution(14304839823876104138)
XLA Ops:
  1.3 2.6 collective-permute-start.3
  12.1 4.3 both_norms.3
  16.4 10.4 %multiply_convert_fusion.2 = (bf16[512,2048]{1,0:T(8,128)(2,1)}, f32[512,2048]{1,0:T(8,128)}) fusion(f32[2048]{0:T(1024)S(1)} %convert_element_type.263, bf16[512,2048]{1,0:T(8,128)(2,1)} %get-tuple-element.199, bf16[2048,2048]{1,0:T(8,128)(2,1)} %param.32), kind=kOutput, calls=%fused_computation.38 | convolution fusion | flops 4301258752 | bytes 16785408 | tf_op jit(solution)/shard_map/dot_general | solution.py:497
  26.8 5.4 qkv_rotary.2.refs_0_
  40.7 4.6 both_norms.4
  45.3 2.6 copy-done.3
  49.3 2.8 copy-done.9
  52.1 5.4 qkv_rotary.3.q_ref.k_ref.v_ref
  57.6 9.7 %attend.1 = (bf16[1024,512]{1,0:T(8,128)(2,1)S(1)}, f32[2,1024,1]{2,1,0:T(8,128)S(1)}) custom-call(s32[1]{0:T(128)S(6)} %copy.79.prefix_ref, bf16[1024,1536]{1,0:T(8,128)(2,1)S(1)} %qkv_rotary.3.q_ref.k_ref.v_ref, bf16[1024,1536]{1,0:T(8,128)(2,1)S(1)} %qkv_rotary.3.q_ref.k_ref.v_ref, bf16[1024,1536]{1,0:T(8,128)(2,1)S(1)} %qkv_rotary.3.q_ref.k_ref.v_ref, ...), custom_call_target="tpu_custom_call" | custom-call | flops 2147483648 | bytes 4194304 | tf_op jit(solution)/shard_map/attend/pallas_call | solution.py:142
  68.2 2.7 collective-permute-start.13
  71.0 10.3 %multiply_convert_fusion.1 = (bf16[512,2048]{1,0:T(8,128)(2,1)S(1)}, f32[512,2048]{1,0:T(8,128)}) fusion(f32[2048]{0:T(1024)S(1)} %convert_element_type.263, bf16[512,2048]{1,0:T(8,128)(2,1)S(1)} %copy-done.77, bf16[2048,2048]{1,0:T(8,128)(2,1)} %param.32), kind=kOutput, calls=%fused_computation.37 | convolution fusion | flops 4301258752 | bytes 16785408 | tf_op jit(solution)/shard_map/dot_general | solution.py:497
  81.7 4.5 fusion.68
  90.5 4.5 fusion.69
  98.7 4.7 collective-permute-done.15
  111.8 2.6 collective-permute-start.20
  118.1 28.5 %both_norms.5 = (bf16[3072,2048]{1,0:T(8,128)(2,1)}, bf16[3072,2048]{1,0:T(8,128)(2,1)}) custom-call(bf16[1,2048]{1,0:T(2,128)(2,1)S(1)} %broadcast_in_dim.16.refs_0_, bf16[1,2048]{1,0:T(2,128)(2,1)S(1)} %broadcast_in_dim.17.refs_1_, bf16[1,2048]{1,0:T(2,128)(2,1)S(1)} %broadcast_in_dim.18.refs_2_, bf16[1,2048]{1,0:T(2,128)(2,1)S(1)} %broadcast_in_dim.19.refs_3_, ...), custom_call_target="tpu_custom_call" | custom-call | flops 75497472 | bytes 37748736 | tf_op jit(solution)/shard_map/both_norms/pallas_call | solution.py:297
  147.8 3.2 fusion.30
  155.8 13.1 %fusion.21 = (f32[3072,512]{1,0:T(8,128)}, bf16[3072,512]{1,0:T(8,128)(2,1)}) fusion(f32[512]{0:T(512)S(1)} %dynamic-slice_convert_fusion, bf16[3072,2048]{1,0:T(8,128)(2,1)S(1)} %copy-done.106, bf16[2048,2048]{1,0:T(8,128)(2,1)} %param.32, s32[]{:T(128)S(6)} %select_n.81), kind=kOutput, calls=%fused_computation.28 | convolution fusion | flops 6459752448 | bytes 24119300 | tf_op jit(solution)/shard_map/dot_general | solution.py:590
  168.8 9.7 %collective-permute-done.27 = bf16[256,2048]{1,0:T(8,128)(2,1)S(1)} collective-permute-done((bf16[256,2048]{1,0:T(8,128)(2,1)S(1)}, bf16[256,2048]{1,0:T(8,128)(2,1)S(1)}, u32[]{:S(2)}, u32[]{:S(2)}) %collective-permute-start.27) | collective-permute-done | bytes 1048608 | tf_op jit(solution)/shard_map/ppermute | solution.py:434
  185.1 17.2 %fusion.17 = bf16[1024,2048]{1,0:T(8,128)(2,1)} fusion(f32[512,2048]{1,0:T(8,128)} %get-tuple-element.439, f32[512,2048]{1,0:T(8,128)} %get-tuple-element.437, bf16[1024,2048]{1,0:T(8,128)(2,1)} %copy-done.95, bf16[2048,2048]{1,0:T(8,128)(2,1)} %param.34), kind=kOutput, calls=%fused_computation.21 | convolution fusion | flops 8613003264 | bytes 25165824 | tf_op jit(solution)/shard_map/dot_general | solution.py:34
  202.3 4.7 convolution_convert_fusion.g_ref
  210.9 11.7 %attend_back.1 = bf16[1024,1536]{1,0:T(8,128)(2,1)} custom-call(s32[1]{0:T(128)S(6)} %copy.79.prefix_ref, bf16[1024,1536]{1,0:T(8,128)(2,1)} %copy-done.4, bf16[1024,1536]{1,0:T(8,128)(2,1)} %copy-done.4, bf16[1024,1536]{1,0:T(8,128)(2,1)} %copy-done.4, bf16[1024,512]{1,0:T(8,128)(2,1)S(1)} %convolution_convert_fusion.g_ref, f32[2,1024,1]{2,1,0:T(8,128)S(1)} %copy-done.22, ...), custom_call_target="tpu_custom_call" | custom-call | flops 5368709120 | bytes 7340032 | tf_op jit(solution)/shard_map/attend_back/pallas_call | solution.py:212
  224.4 3.6 constant_dynamic-slice_fusion.2.weight_ref
  235.9 17.8 %outer_blocks.1 = bf16[640,2048]{1,0:T(8,128)(2,1)} custom-call(s32[1]{0:T(128)} %bitcast.10._.quarter_ref, bf16[512,2048]{1,0:T(8,128)(2,1)} %get-tuple-element.215.refs_0_, bf16[512,2048]{1,0:T(8,128)(2,1)} %copy-done.111, bf16[3072,512]{1,0:T(8,128)(2,1)} %get-tuple-element.242.refs_2_, bf16[1024,128]{1,0:T(8,128)(2,1)} %constant_dynamic-slice_fusion.3.refs_3_, ...), custom_call_target="tpu_custom_call" | custom-call | flops 10737418240 | bytes 22020096 | tf_op jit(solution)/shard_map/outer_blocks/pallas_call | solution.py:345
  253.7 3.0 fusion.64
  257.0 17.7 %back_blocks.1 = bf16[3072,512]{1,0:T(8,128)(2,1)} custom-call(bf16[512,2048]{1,0:T(8,128)(2,1)} %constant_dynamic-slice_fusion.2.weight_ref, f32[3072,512]{1,0:T(8,128)} %get-tuple-element.399.slope_ref, bf16[256,2048]{1,0:T(8,128)(2,1)} %copy-done.87, bf16[256,2048]{1,0:T(8,128)(2,1)} %copy-done.89, bf16[256,2048]{1,0:T(8,128)(2,1)} %copy-done.80, ...), custom_call_target="tpu_custom_call" | custom-call | flops 6442450944 | bytes 22020096 | tf_op jit(solution)/shard_map/back_blocks/pallas_call | solution.py:379
  274.7 3.0 fusion.48
  279.1 2.7 collective-permute-start.46
  281.7 11.6 %add_convert_fusion = bf16[2048,512]{1,0:T(8,128)(2,1)} fusion(f32[2048,512]{1,0:T(8,128)S(1)} %fusion.48, f32[2048,512]{1,0:T(8,128)S(1)} %fusion.46, bf16[3072,2048]{1,0:T(8,128)(2,1)} %get-tuple-element.231, bf16[3072,512]{1,0:T(8,128)(2,1)} %back_blocks.1), kind=kOutput, calls=%fused_computation.36 | convolution fusion | flops 6445596672 | bytes 26214400 | tf_op jit(solution)/shard_map/dot_general | solution.py:34
  296.8 9.3 %fusion.70 = f32[1024,2048]{1,0:T(8,128)} fusion(bf16[1024,1536]{1,0:T(8,128)(2,1)S(1)} %copy-done.69, bf16[2048,1536]{1,0:T(8,128)(2,1)S(1)} %bitcast.79), kind=kOutput, calls=%fused_computation.152 | convolution fusion | flops 6442450944 | bytes 17825792 | tf_op jit(solution)/shard_map/dot_general | solution.py:34
  308.0 8.1 %collective-permute-done.49.refs_2_ = bf16[128,2048]{1,0:T(8,128)(2,1)S(1)} collective-permute-done((bf16[128,2048]{1,0:T(8,128)(2,1)S(1)}, bf16[128,2048]{1,0:T(8,128)(2,1)S(1)}, u32[]{:S(2)}, u32[]{:S(2)}) %collective-permute-start.49) | collective-permute-done | bytes 524320 | tf_op jit(solution)/shard_map/ppermute | solution.py:441
  321.1 4.0 collective-permute-start.50
  325.1 11.4 %add_convert_fusion.1 = bf16[2048,384]{1,0:T(8,128)(2,1)} fusion(f32[2048,384]{1,0:T(8,128)S(1)} %fusion.54, f32[2048,384]{1,0:T(8,128)S(1)} %fusion.52, bf16[3072,2048]{1,0:T(8,128)(2,1)} %get-tuple-element.267, bf16[1024,384]{1,0:T(8,128)(2,1)} %collective-permute-done.44, bf16[1024,384]{1,0:T(8,128)(2,1)} %collective-permute-done.43, ...), kind=kOutput, calls=%fused_computation.41 | convolution fusion | flops 4841275392 | bytes 22806528 | tf_op jit(solution)/shard_map/dot_general | solution.py:34
  336.6 6.1 collective-permute-done.53.refs_3_
  345.8 2.9 collective-permute-start.59
  349.8 13.4 %fusion.71 = f32[1024,2048]{1,0:T(8,128)} fusion(bf16[1024,2048]{1,0:T(8,128)(2,1)S(1)} %copy-done.75, bf16[2048,2048]{1,0:T(8,128)(2,1)} %param.32), kind=kOutput, calls=%fused_computation.153 | convolution fusion | flops 8589934592 | bytes 20971520 | tf_op jit(solution)/shard_map/dot_general | solution.py:34
  364.0 7.1 %collective-permute-done.56.refs_3_ = bf16[128,2048]{1,0:T(8,128)(2,1)S(1)} collective-permute-done((bf16[128,2048]{1,0:T(8,128)(2,1)S(1)}, bf16[128,2048]{1,0:T(8,128)(2,1)S(1)}, u32[]{:S(2)}, u32[]{:S(2)}) %collective-permute-start.56) | collective-permute-done | bytes 524320 | tf_op jit(solution)/shard_map/ppermute | solution.py:441
  374.8 2.5 convert_reduce_fusion
  377.3 2.8 fusion.11
  380.1 9.4 %fusion.59 = (f32[2048]{0:T(1024)S(1)}, f32[2048]{0:T(1024)S(1)}, f32[1024]{0:T(1024)S(1)}, f32[1024]{0:T(1024)S(1)}, f32[1024,2048]{1,0:T(8,128)S(1)}, /*index=5*/f32[2048]{0:T(1024)S(1)}, f32[2048]{0:T(1024)S(1)}) fusion(f32[1024,2048]{1,0:T(8,128)S(1)} %copy-done.74, f32[1024]{0:T(1024)S(1)} %add_rsqrt_fusion, f32[1024]{0:T(1024)S(1)} %broadcast_multiply_fusion.2, ...), kind=kLoop, calls=%fused_computation.142 | loop fusion | flops 46127104 | bytes 29425664 | tf_op jit(solution)/shard_map/reduce_sum | solution.py:799
  389.6 6.6 %fusion.8 = f32[1024,2048]{1,0:T(8,128)S(1)} fusion(f32[1024,2048]{1,0:T(8,128)S(1)} %get-tuple-element.396, f32[1024]{0:T(1024)S(1)} %broadcast_multiply_fusion, f32[1024]{0:T(1024)S(1)} %broadcast_multiply_fusion.1, f32[1024]{0:T(1024)S(1)} %add_rsqrt_fusion, f32[1024]{0:T(1024)S(1)} %broadcast_multiply_fusion.2, ...), kind=kLoop, calls=%fused_computation.12 | loop fusion | flops 29360128 | bytes 20987904 | tf_op jit(solution)/shard_map/mul | solution.py:784
  408.9 2.8 convert_reduce_fusion.1
  413.0 17.5 %collective-permute-done.58 = bf16[512,512]{1,0:T(8,128)(2,1)} collective-permute-done((bf16[512,512]{1,0:T(8,128)(2,1)}, bf16[512,512]{1,0:T(8,128)(2,1)}, u32[]{:S(2)}, u32[]{:S(2)}) %collective-permute-start.58) | collective-permute-done | bytes 524320 | tf_op jit(solution)/shard_map/ppermute | solution.py:441
  437.5 3.5 convert_add_fusion
  441.7 13.7 %collective-permute-done.67 = bf16[512,512]{1,0:T(8,128)(2,1)S(1)} collective-permute-done((bf16[512,512]{1,0:T(8,128)(2,1)}, bf16[512,512]{1,0:T(8,128)(2,1)S(1)}, u32[]{:S(2)}, u32[]{:S(2)}) %collective-permute-start.67) | collective-permute-done | bytes 524320 | tf_op jit(solution)/shard_map/ppermute | solution.py:441
  456.7 2.5 place_quarters.17.refs_0_
  460.4 2.7 collective-permute-start.75
  464.1 18.2 %collective-permute-done.73 = bf16[512,512]{1,0:T(8,128)(2,1)S(1)} collective-permute-done((bf16[512,512]{1,0:T(8,128)(2,1)S(1)}, bf16[512,512]{1,0:T(8,128)(2,1)S(1)}, u32[]{:S(2)}, u32[]{:S(2)}) %collective-permute-start.73) | collective-permute-done | bytes 524320 | tf_op jit(solution)/shard_map/ppermute | solution.py:441
  483.1 2.5 place_quarters.18.refs_0_
  492.1 2.5 place_quarters.19.refs_0_
  494.6 16.1 %collective-permute-done.78 = bf16[512,512]{1,0:T(8,128)(2,1)S(1)} collective-permute-done((bf16[512,512]{1,0:T(8,128)(2,1)S(1)}, bf16[512,512]{1,0:T(8,128)(2,1)S(1)}, u32[]{:S(2)}, u32[]{:S(2)}) %collective-permute-start.78) | collective-permute-done | bytes 524320 | tf_op jit(solution)/shard_map/ppermute | solution.py:441
  519.3 2.5 place_quarters.20
  521.8 7.6 %collective-permute-done.83 = bf16[256,384]{1,0:T(8,128)(2,1)S(1)} collective-permute-done((bf16[256,384]{1,0:T(8,128)(2,1)S(1)}, bf16[256,384]{1,0:T(8,128)(2,1)S(1)}, u32[]{:S(2)}, u32[]{:S(2)}) %collective-permute-start.83) | collective-permute-done | bytes 196640 | tf_op jit(solution)/shard_map/ppermute | solution.py:441
  531.1 4.9 collective-permute-done.86.refs_4_
  536.9 2.5 collective-permute-start.88
  542.9 3.5 place_quarters.21
  546.4 5.0 collective-permute-done.88
  560.0 3.4 collective-permute-done.94
  566.7 2.6 collective-permute-start.102
  569.3 2.4 place_quarters.23.refs_0_
  572.0 5.8 collective-permute-done.99.refs_3_
  585.7 3.1 collective-permute-done.104.refs_3_
  638.3 2.6 place_quarters.32.refs_0_
  641.0 2.9 place_quarters.33
  (564 shorter events, 200.5 us)
Async XLA Ops:
  1.3 32.6 %collective-permute-start.3 = (bf16[256,2048]{1,0:T(8,128)(2,1)}, bf16[256,2048]{1,0:T(8,128)(2,1)}, u32[]{:S(2)}, u32[]{:S(2)}) collective-permute-start(bf16[256,2048]{1,0:T(8,128)(2,1)} %refs_4_.1), channel_id=1, source_target_pairs={{0,4},{4,0},{8,12},{12,8},{16,20},{20,16},{24,28},{28,24},{1,5},{5... | collective-permute-start | bytes 3145736 | tf_op jit(solution)/shard_map/ppermute | solution.py:441
  3.8 30.1 %collective-permute-start.4 = (bf16[256,2048]{1,0:T(8,128)(2,1)}, bf16[256,2048]{1,0:T(8,128)(2,1)}, u32[]{:S(2)}, u32[]{:S(2)}) collective-permute-start(bf16[256,2048]{1,0:T(8,128)(2,1)} %refs_4_.1), channel_id=1, source_target_pairs={{0,8},{4,12},{8,0},{12,4},{16,24},{20,28},{24,16},{28,20},{1,9},{5... | collective-permute-start | bytes 3145736 | tf_op jit(solution)/shard_map/ppermute | solution.py:441
  5.4 28.5 %collective-permute-start.5 = (bf16[256,2048]{1,0:T(8,128)(2,1)}, bf16[256,2048]{1,0:T(8,128)(2,1)}, u32[]{:S(2)}, u32[]{:S(2)}) collective-permute-start(bf16[256,2048]{1,0:T(8,128)(2,1)} %refs_4_.1), channel_id=1, source_target_pairs={{0,2},{1,3},{2,0},{3,1},{4,6},{5,7},{6,4},{7,5},{8,10},{9,11},{10,... | collective-permute-start | bytes 3145736 | tf_op jit(solution)/shard_map/ppermute | solution.py:434
  11.5 22.4 %collective-permute-start.2 = (f32[8,128]{1,0:T(8,128)S(1)}, f32[8,128]{1,0:T(8,128)S(1)}, u32[]{:S(2)}, u32[]{:S(2)}) collective-permute-start(f32[8,128]{1,0:T(8,128)S(1)} %broadcast_add_fusion), channel_id=1, source_target_pairs={{0,4},{4,0},{8,12},{12,8},{16,20},{20,16},{24,28},{28,24},{1,5},{5... | collective-permute-start | bytes 12296 | tf_op jit(solution)/shard_map/ppermute | solution.py:441
  34.8 33.5 %collective-permute-start.8 = (bf16[256,2048]{1,0:T(8,128)(2,1)}, bf16[256,2048]{1,0:T(8,128)(2,1)}, u32[]{:S(2)}, u32[]{:S(2)}) collective-permute-start(bf16[256,2048]{1,0:T(8,128)(2,1)} %collective-permute-done.4.refs_8_), channel_id=1, source_target_pairs={{0,4},{4,0},{8,12},{12,8},{16,20},{20,16},{24,28},{28,24},{1,5},{5... | collective-permute-start | bytes 3145736 | tf_op jit(solution)/shard_map/ppermute | solution.py:441
  37.4 44.0 %collective-permute-start.10 = (bf16[256,2048]{1,0:T(8,128)(2,1)}, bf16[256,2048]{1,0:T(8,128)(2,1)}, u32[]{:S(2)}, u32[]{:S(2)}) collective-permute-start(bf16[256,2048]{1,0:T(8,128)(2,1)} %collective-permute-done.5.refs_4_), channel_id=1, source_target_pairs={{0,8},{4,12},{8,0},{12,4},{16,24},{20,28},{24,16},{28,20},{1,9},{5... | collective-permute-start | bytes 3145736 | tf_op jit(solution)/shard_map/ppermute | solution.py:441
  38.5 29.5 %collective-permute-start.7 = (f32[8,128]{1,0:T(8,128)S(1)}, f32[8,128]{1,0:T(8,128)S(1)}, u32[]{:S(2)}, u32[]{:S(2)}) collective-permute-start(f32[8,128]{1,0:T(8,128)S(1)} %fusion.98), channel_id=1, source_target_pairs={{0,8},{4,12},{8,0},{12,4},{16,24},{20,28},{24,16},{28,20},{1,9},{5... | collective-permute-start | bytes 12296 | tf_op jit(solution)/shard_map/ppermute | solution.py:441
  40.2 41.1 %collective-permute-start.9 = (bf16[256,2048]{1,0:T(8,128)(2,1)}, bf16[256,2048]{1,0:T(8,128)(2,1)S(1)}, u32[]{:S(2)}, u32[]{:S(2)}) collective-permute-start(bf16[256,2048]{1,0:T(8,128)(2,1)} %collective-permute-done.3.refs_4_), channel_id=1, source_target_pairs={{0,2},{1,3},{2,0},{3,1},{4,6},{5,7},{6,4},{7,5},{8,10},{9,11},{10,... | collective-permute-start | bytes 3145736 | tf_op jit(solution)/shard_map/ppermute | solution.py:434
  81.3 26.4 %collective-permute-start.21 = (bf16[256,2048]{1,0:T(8,128)(2,1)}, bf16[256,2048]{1,0:T(8,128)(2,1)S(1)}, u32[]{:S(2)}, u32[]{:S(2)}) collective-permute-start(bf16[256,2048]{1,0:T(8,128)(2,1)} %collective-permute-done.3.refs_4_), channel_id=1, source_target_pairs={{0,1},{1,0},{2,3},{3,2},{4,5},{5,4},{6,7},{7,6},{8,9},{9,8},{10,11... | collective-permute-start | bytes 3145736 | tf_op jit(solution)/shard_map/ppermute | solution.py:430
  109.0 37.6 %collective-permute-start.18 = (bf16[256,2048]{1,0:T(8,128)(2,1)}, bf16[256,2048]{1,0:T(8,128)(2,1)}, u32[]{:S(2)}, u32[]{:S(2)}) collective-permute-start(bf16[256,2048]{1,0:T(8,128)(2,1)} %fusion.43), channel_id=1, source_target_pairs={{0,2},{1,3},{2,0},{3,1},{4,6},{5,7},{6,4},{7,5},{8,10},{9,11},{10,... | collective-permute-start | bytes 3145736 | tf_op jit(solution)/shard_map/ppermute | solution.py:438
  111.6 35.0 %collective-permute-start.19 = (bf16[256,2048]{1,0:T(8,128)(2,1)}, bf16[256,2048]{1,0:T(8,128)(2,1)}, u32[]{:S(2)}, u32[]{:S(2)}) collective-permute-start(bf16[256,2048]{1,0:T(8,128)(2,1)} %fusion.44), channel_id=1, source_target_pairs={{0,1},{1,0},{2,3},{3,2},{4,5},{5,4},{6,7},{7,6},{8,9},{9,8},{10,11... | collective-permute-start | bytes 3145736 | tf_op jit(solution)/shard_map/ppermute | solution.py:430
  111.8 34.8 %collective-permute-start.20 = (f32[8,128]{1,0:T(8,128)S(1)}, f32[8,128]{1,0:T(8,128)S(1)}, u32[]{:S(2)}, u32[]{:S(2)}) collective-permute-start(f32[8,128]{1,0:T(8,128)S(1)} %add.323), channel_id=1, source_target_pairs={{0,16},{4,20},{8,24},{12,28},{16,0},{20,4},{24,8},{28,12},{1,17},{... | collective-permute-start | bytes 12296 | tf_op jit(solution)/shard_map/ppermute | solution.py:441
  153.3 25.2 %collective-permute-start.27 = (bf16[256,2048]{1,0:T(8,128)(2,1)S(1)}, bf16[256,2048]{1,0:T(8,128)(2,1)S(1)}, u32[]{:S(2)}, u32[]{:S(2)}) collective-permute-start(bf16[256,2048]{1,0:T(8,128)(2,1)S(1)} %get-tuple-element.230), channel_id=1, source_target_pairs={{0,2},{1,3},{2,0},{3,1},{4,6},{5,7},{6,4},{7,5},{8,10},{9,11},{10,... | collective-permute-start | bytes 3145736 | tf_op jit(solution)/shard_map/ppermute | solution.py:434
  153.9 24.9 %collective-permute-start.28 = (bf16[256,2048]{1,0:T(8,128)(2,1)S(1)}, bf16[256,2048]{1,0:T(8,128)(2,1)S(1)}, u32[]{:S(2)}, u32[]{:S(2)}) collective-permute-start(bf16[256,2048]{1,0:T(8,128)(2,1)S(1)} %get-tuple-element.230), channel_id=1, source_target_pairs={{0,4},{4,0},{8,12},{12,8},{16,20},{20,16},{24,28},{28,24},{1,5},{5... | collective-permute-start | bytes 3145736 | tf_op jit(solution)/shard_map/ppermute | solution.py:441
  154.9 24.6 %collective-permute-start.29 = (bf16[256,2048]{1,0:T(8,128)(2,1)S(1)}, bf16[256,2048]{1,0:T(8,128)(2,1)S(1)}, u32[]{:S(2)}, u32[]{:S(2)}) collective-permute-start(bf16[256,2048]{1,0:T(8,128)(2,1)S(1)} %get-tuple-element.230), channel_id=1, source_target_pairs={{0,8},{4,12},{8,0},{12,4},{16,24},{20,28},{24,16},{28,20},{1,9},{5... | collective-permute-start | bytes 3145736 | tf_op jit(solution)/shard_map/ppermute | solution.py:441
  155.8 23.7 %collective-permute-start.30 = (bf16[256,2048]{1,0:T(8,128)(2,1)S(1)}, bf16[256,2048]{1,0:T(8,128)(2,1)S(1)}, u32[]{:S(2)}, u32[]{:S(2)}) collective-permute-start(bf16[256,2048]{1,0:T(8,128)(2,1)S(1)} %get-tuple-element.230), channel_id=1, source_target_pairs={{0,1},{1,0},{2,3},{3,2},{4,5},{5,4},{6,7},{7,6},{8,9},{9,8},{10,11... | collective-permute-start | bytes 3145736 | tf_op jit(solution)/shard_map/ppermute | solution.py:430
  179.6 28.0 %collective-permute-start.34 = (bf16[256,2048]{1,0:T(8,128)(2,1)S(1)}, bf16[256,2048]{1,0:T(8,128)(2,1)S(1)}, u32[]{:S(2)}, u32[]{:S(2)}) collective-permute-start(bf16[256,2048]{1,0:T(8,128)(2,1)S(1)} %collective-permute-done.27), channel_id=1, source_target_pairs={{0,8},{4,12},{8,0},{12,4},{16,24},{20,28},{24,16},{28,20},{1,9},{5... | collective-permute-start | bytes 3145736 | tf_op jit(solution)/shard_map/ppermute | solution.py:441
  180.5 27.1 %collective-permute-start.33 = (bf16[256,2048]{1,0:T(8,128)(2,1)S(1)}, bf16[256,2048]{1,0:T(8,128)(2,1)S(1)}, u32[]{:S(2)}, u32[]{:S(2)}) collective-permute-start(bf16[256,2048]{1,0:T(8,128)(2,1)S(1)} %collective-permute-done.28.refs_8_.refs_0_), channel_id=1, source_target_pairs={{0,2},{1,3},{2,0},{3,1},{4,6},{5,7},{6,4},{7,5},{8,10},{9,11},{10,... | collective-permute-start | bytes 3145736 | tf_op jit(solution)/shard_map/ppermute | solution.py:434
  182.0 26.4 %collective-permute-start.37 = (bf16[256,2048]{1,0:T(8,128)(2,1)S(1)}, bf16[256,2048]{1,0:T(8,128)(2,1)S(1)}, u32[]{:S(2)}, u32[]{:S(2)}) collective-permute-start(bf16[256,2048]{1,0:T(8,128)(2,1)S(1)} %collective-permute-done.28.refs_8_.refs_0_), channel_id=1, source_target_pairs={{0,1},{1,0},{2,3},{3,2},{4,5},{5,4},{6,7},{7,6},{8,9},{9,8},{10,11... | collective-permute-start | bytes 3145736 | tf_op jit(solution)/shard_map/ppermute | solution.py:430
  182.0 25.6 %collective-permute-start.32 = (bf16[256,2048]{1,0:T(8,128)(2,1)S(1)}, bf16[256,2048]{1,0:T(8,128)(2,1)S(1)}, u32[]{:S(2)}, u32[]{:S(2)}) collective-permute-start(bf16[256,2048]{1,0:T(8,128)(2,1)S(1)} %collective-permute-done.29.refs_12_.refs_4_), channel_id=1, source_target_pairs={{0,4},{4,0},{8,12},{12,8},{16,20},{20,16},{24,28},{28,24},{1,5},{5... | collective-permute-start | bytes 3145736 | tf_op jit(solution)/shard_map/ppermute | solution.py:441
  182.7 26.9 %collective-permute-start.39 = (bf16[256,2048]{1,0:T(8,128)(2,1)S(1)}, bf16[256,2048]{1,0:T(8,128)(2,1)S(1)}, u32[]{:S(2)}, u32[]{:S(2)}) collective-permute-start(bf16[256,2048]{1,0:T(8,128)(2,1)S(1)} %collective-permute-done.29.refs_12_.refs_4_), channel_id=1, source_target_pairs={{0,1},{1,0},{2,3},{3,2},{4,5},{5,4},{6,7},{7,6},{8,9},{9,8},{10,11... | collective-permute-start | bytes 3145736 | tf_op jit(solution)/shard_map/ppermute | solution.py:430
  232.4 63.2 %collective-permute-start.42 = (bf16[1024,384]{1,0:T(8,128)(2,1)}, bf16[1024,384]{1,0:T(8,128)(2,1)}, u32[]{:S(2)}, u32[]{:S(2)}) collective-permute-start(bf16[1024,384]{1,0:T(8,128)(2,1)} %get-tuple-element.404), channel_id=1, source_target_pairs={{0,4},{4,0},{8,12},{12,8},{16,20},{20,16},{24,28},{28,24},{1,5},{5... | collective-permute-start | bytes 2359304 | tf_op jit(solution)/shard_map/ppermute | solution.py:441
  233.5 74.0 %collective-permute-start.43 = (bf16[1024,384]{1,0:T(8,128)(2,1)}, bf16[1024,384]{1,0:T(8,128)(2,1)}, u32[]{:S(2)}, u32[]{:S(2)}) collective-permute-start(bf16[1024,384]{1,0:T(8,128)(2,1)} %get-tuple-element.403), channel_id=1, source_target_pairs={{0,8},{4,12},{8,0},{12,4},{16,24},{20,28},{24,16},{28,20},{1,9},{5... | collective-permute-start | bytes 2359304 | tf_op jit(solution)/shard_map/ppermute | solution.py:441
  234.7 73.3 %collective-permute-start.44 = (bf16[1024,384]{1,0:T(8,128)(2,1)S(1)}, bf16[1024,384]{1,0:T(8,128)(2,1)}, u32[]{:S(2)}, u32[]{:S(2)}) collective-permute-start(bf16[1024,384]{1,0:T(8,128)(2,1)S(1)} %get-tuple-element.402), channel_id=1, source_target_pairs={{0,12},{4,8},{8,4},{12,0},{16,28},{20,24},{24,20},{28,16},{1,13},{... | collective-permute-start | bytes 2359304 | tf_op jit(solution)/shard_map/ppermute | solution.py:441
  256.7 36.7 %collective-permute-start.47 = (bf16[128,2048]{1,0:T(8,128)(2,1)S(1)}, bf16[128,2048]{1,0:T(8,128)(2,1)}, u32[]{:S(2)}, u32[]{:S(2)}) collective-permute-start(bf16[128,2048]{1,0:T(8,128)(2,1)S(1)} %get-tuple-element.408), channel_id=1, source_target_pairs={{0,16},{4,20},{8,24},{12,28},{16,0},{20,4},{24,8},{28,12},{1,17},{... | collective-permute-start | bytes 1572872 | tf_op jit(solution)/shard_map/ppermute | solution.py:441
  279.1 28.9 %collective-permute-start.46 = (bf16[128,2048]{1,0:T(8,128)(2,1)S(1)}, bf16[128,2048]{1,0:T(8,128)(2,1)S(1)}, u32[]{:S(2)}, u32[]{:S(2)}) collective-permute-start(bf16[128,2048]{1,0:T(8,128)(2,1)S(1)} %get-tuple-element.255), channel_id=1, source_target_pairs={{0,16},{4,20},{8,24},{12,28},{16,0},{20,4},{24,8},{28,12},{1,17},{... | collective-permute-start | bytes 1572872 | tf_op jit(solution)/shard_map/ppermute | solution.py:441
  295.7 20.5 %collective-permute-start.49 = (bf16[128,2048]{1,0:T(8,128)(2,1)S(1)}, bf16[128,2048]{1,0:T(8,128)(2,1)S(1)}, u32[]{:S(2)}, u32[]{:S(2)}) collective-permute-start(bf16[128,2048]{1,0:T(8,128)(2,1)S(1)} %add_convert_fusion.10.refs_0_), channel_id=1, source_target_pairs={{0,8},{4,12},{8,0},{12,4},{16,24},{20,28},{24,16},{28,20},{1,9},{5... | collective-permute-start | bytes 1572872 | tf_op jit(solution)/shard_map/ppermute | solution.py:441
  307.5 29.0 %collective-permute-start.51 = (bf16[128,2048]{1,0:T(8,128)(2,1)}, bf16[128,2048]{1,0:T(8,128)(2,1)S(1)}, u32[]{:S(2)}, u32[]{:S(2)}) collective-permute-start(bf16[128,2048]{1,0:T(8,128)(2,1)} %get-tuple-element.262), channel_id=1, source_target_pairs={{0,16},{4,20},{8,24},{12,28},{16,0},{20,4},{24,8},{28,12},{1,17},{... | collective-permute-start | bytes 1572872 | tf_op jit(solution)/shard_map/ppermute | solution.py:441
  316.3 20.2 %collective-permute-start.52 = (bf16[128,2048]{1,0:T(8,128)(2,1)S(1)}, bf16[128,2048]{1,0:T(8,128)(2,1)S(1)}, u32[]{:S(2)}, u32[]{:S(2)}) collective-permute-start(bf16[128,2048]{1,0:T(8,128)(2,1)S(1)} %add_convert_fusion.9.refs_1_), channel_id=1, source_target_pairs={{0,4},{4,0},{8,12},{12,8},{16,20},{20,16},{24,28},{28,24},{1,5},{5... | collective-permute-start | bytes 1572872 | tf_op jit(solution)/shard_map/ppermute | solution.py:441
  317.4 25.2 %collective-permute-start.53 = (bf16[128,2048]{1,0:T(8,128)(2,1)S(1)}, bf16[128,2048]{1,0:T(8,128)(2,1)S(1)}, u32[]{:S(2)}, u32[]{:S(2)}) collective-permute-start(bf16[128,2048]{1,0:T(8,128)(2,1)S(1)} %add_convert_fusion.9.refs_1_), channel_id=1, source_target_pairs={{0,8},{4,12},{8,0},{12,4},{16,24},{20,28},{24,16},{28,20},{1,9},{5... | collective-permute-start | bytes 1572872 | tf_op jit(solution)/shard_map/ppermute | solution.py:441
  320.1 22.6 %collective-permute-start.54 = (bf16[128,2048]{1,0:T(8,128)(2,1)S(1)}, bf16[128,2048]{1,0:T(8,128)(2,1)S(1)}, u32[]{:S(2)}, u32[]{:S(2)}) collective-permute-start(bf16[128,2048]{1,0:T(8,128)(2,1)S(1)} %collective-permute-done.49.refs_2_), channel_id=1, source_target_pairs={{0,4},{4,0},{8,12},{12,8},{16,20},{20,16},{24,28},{28,24},{1,5},{5... | collective-permute-start | bytes 1572872 | tf_op jit(solution)/shard_map/ppermute | solution.py:441
  321.1 42.1 %collective-permute-start.50 = (bf16[128,2048]{1,0:T(8,128)(2,1)}, bf16[128,2048]{1,0:T(8,128)(2,1)S(1)}, u32[]{:S(2)}, u32[]{:S(2)}) collective-permute-start(bf16[128,2048]{1,0:T(8,128)(2,1)} %get-tuple-element.261), channel_id=1, source_target_pairs={{0,16},{4,20},{8,24},{12,28},{16,0},{20,4},{24,8},{28,12},{1,17},{... | collective-permute-start | bytes 1572872 | tf_op jit(solution)/shard_map/ppermute | solution.py:441
  344.8 18.4 %collective-permute-start.55 = (bf16[128,2048]{1,0:T(8,128)(2,1)S(1)}, bf16[128,2048]{1,0:T(8,128)(2,1)S(1)}, u32[]{:S(2)}, u32[]{:S(2)}) collective-permute-start(bf16[128,2048]{1,0:T(8,128)(2,1)S(1)} %add_convert_fusion.8.refs_1_), channel_id=1, source_target_pairs={{0,4},{4,0},{8,12},{12,8},{16,20},{20,16},{24,28},{28,24},{1,5},{5... | collective-permute-start | bytes 1572872 | tf_op jit(solution)/shard_map/ppermute | solution.py:441
  345.8 25.3 %collective-permute-start.56 = (bf16[128,2048]{1,0:T(8,128)(2,1)S(1)}, bf16[128,2048]{1,0:T(8,128)(2,1)S(1)}, u32[]{:S(2)}, u32[]{:S(2)}) collective-permute-start(bf16[128,2048]{1,0:T(8,128)(2,1)S(1)} %add_convert_fusion.8.refs_1_), channel_id=1, source_target_pairs={{0,8},{4,12},{8,0},{12,4},{16,24},{20,28},{24,16},{28,20},{1,9},{5... | collective-permute-start | bytes 1572872 | tf_op jit(solution)/shard_map/ppermute | solution.py:441
  345.8 54.2 %collective-permute-start.59 = (bf16[128,2048]{1,0:T(8,128)(2,1)}, bf16[128,2048]{1,0:T(8,128)(2,1)}, u32[]{:S(2)}, u32[]{:S(2)}) collective-permute-start(bf16[128,2048]{1,0:T(8,128)(2,1)} %get-tuple-element.275), channel_id=1, source_target_pairs={{0,16},{4,20},{8,24},{12,28},{16,0},{20,4},{24,8},{28,12},{1,17},{... | collective-permute-start | bytes 1572872 | tf_op jit(solution)/shard_map/ppermute | solution.py:441
  348.8 22.4 %collective-permute-start.57 = (bf16[128,2048]{1,0:T(8,128)(2,1)S(1)}, bf16[128,2048]{1,0:T(8,128)(2,1)S(1)}, u32[]{:S(2)}, u32[]{:S(2)}) collective-permute-start(bf16[128,2048]{1,0:T(8,128)(2,1)S(1)} %collective-permute-done.53.refs_3_), channel_id=1, source_target_pairs={{0,4},{4,0},{8,12},{12,8},{16,20},{20,16},{24,28},{28,24},{1,5},{5... | collective-permute-start | bytes 1572872 | tf_op jit(solution)/shard_map/ppermute | solution.py:441
  372.7 27.4 %collective-permute-start.60 = (bf16[128,2048]{1,0:T(8,128)(2,1)S(1)}, bf16[128,2048]{1,0:T(8,128)(2,1)S(1)}, u32[]{:S(2)}, u32[]{:S(2)}) collective-permute-start(bf16[128,2048]{1,0:T(8,128)(2,1)S(1)} %add_convert_fusion.7.refs_1_), channel_id=1, source_target_pairs={{0,4},{4,0},{8,12},{12,8},{16,20},{20,16},{24,28},{28,24},{1,5},{5... | collective-permute-start | bytes 1572872 | tf_op jit(solution)/shard_map/ppermute | solution.py:441
  373.8 26.3 %collective-permute-start.61 = (bf16[128,2048]{1,0:T(8,128)(2,1)S(1)}, bf16[128,2048]{1,0:T(8,128)(2,1)S(1)}, u32[]{:S(2)}, u32[]{:S(2)}) collective-permute-start(bf16[128,2048]{1,0:T(8,128)(2,1)S(1)} %add_convert_fusion.7.refs_1_), channel_id=1, source_target_pairs={{0,8},{4,12},{8,0},{12,4},{16,24},{20,28},{24,16},{28,20},{1,9},{5... | collective-permute-start | bytes 1572872 | tf_op jit(solution)/shard_map/ppermute | solution.py:441
  373.8 27.1 %collective-permute-start.62 = (bf16[128,2048]{1,0:T(8,128)(2,1)S(1)}, bf16[128,2048]{1,0:T(8,128)(2,1)S(1)}, u32[]{:S(2)}, u32[]{:S(2)}) collective-permute-start(bf16[128,2048]{1,0:T(8,128)(2,1)S(1)} %collective-permute-done.56.refs_3_), channel_id=1, source_target_pairs={{0,4},{4,0},{8,12},{12,8},{16,20},{20,16},{24,28},{28,24},{1,5},{5... | collective-permute-start | bytes 1572872 | tf_op jit(solution)/shard_map/ppermute | solution.py:441
  401.7 30.4 %collective-permute-start.66 = (bf16[2,256,2048]{2,1,0:T(8,128)(2,1)}, bf16[2,256,2048]{2,1,0:T(8,128)(2,1)}, u32[]{:S(2)}, u32[]{:S(2)}) collective-permute-start(bf16[2,256,2048]{2,1,0:T(8,128)(2,1)} %fusion.31), channel_id=1, source_target_pairs={{0,1},{1,0},{2,3},{3,2},{4,5},{5,4},{6,7},{7,6},{8,9},{9,8},{10,11... | collective-permute-start | bytes 6291464 | tf_op jit(solution)/shard_map/ppermute | solution.py:430
  403.4 27.0 %collective-permute-start.58 = (bf16[512,512]{1,0:T(8,128)(2,1)}, bf16[512,512]{1,0:T(8,128)(2,1)}, u32[]{:S(2)}, u32[]{:S(2)}) collective-permute-start(bf16[512,512]{1,0:T(8,128)(2,1)} %get-tuple-element.274), channel_id=1, source_target_pairs={{0,16},{4,20},{8,24},{12,28},{16,0},{20,4},{24,8},{28,12},{1,17},{... | collective-permute-start | bytes 1572872 | tf_op jit(solution)/shard_map/ppermute | solution.py:441
  405.9 24.5 %collective-permute-start.63 = (bf16[128,2048]{1,0:T(8,128)(2,1)S(1)}, bf16[128,2048]{1,0:T(8,128)(2,1)S(1)}, u32[]{:S(2)}, u32[]{:S(2)}) collective-permute-start(bf16[128,2048]{1,0:T(8,128)(2,1)S(1)} %add_convert_fusion.6.refs_0_), channel_id=1, source_target_pairs={{0,4},{4,0},{8,12},{12,8},{16,20},{20,16},{24,28},{28,24},{1,5},{5... | collective-permute-start | bytes 1572872 | tf_op jit(solution)/shard_map/ppermute | solution.py:441
  407.0 24.2 %collective-permute-start.64 = (bf16[128,2048]{1,0:T(8,128)(2,1)S(1)}, bf16[128,2048]{1,0:T(8,128)(2,1)}, u32[]{:S(2)}, u32[]{:S(2)}) collective-permute-start(bf16[128,2048]{1,0:T(8,128)(2,1)S(1)} %add_convert_fusion.6.refs_0_), channel_id=1, source_target_pairs={{0,8},{4,12},{8,0},{12,4},{16,24},{20,28},{24,16},{28,20},{1,9},{5... | collective-permute-start | bytes 1572872 | tf_op jit(solution)/shard_map/ppermute | solution.py:441
  407.8 23.5 %collective-permute-start.65 = (bf16[128,2048]{1,0:T(8,128)(2,1)}, bf16[128,2048]{1,0:T(8,128)(2,1)S(1)}, u32[]{:S(2)}, u32[]{:S(2)}) collective-permute-start(bf16[128,2048]{1,0:T(8,128)(2,1)} %copy-done.29), channel_id=1, source_target_pairs={{0,4},{4,0},{8,12},{12,8},{16,20},{20,16},{24,28},{28,24},{1,5},{5... | collective-permute-start | bytes 1572872 | tf_op jit(solution)/shard_map/ppermute | solution.py:441
  430.4 25.0 %collective-permute-start.67 = (bf16[512,512]{1,0:T(8,128)(2,1)}, bf16[512,512]{1,0:T(8,128)(2,1)S(1)}, u32[]{:S(2)}, u32[]{:S(2)}) collective-permute-start(bf16[512,512]{1,0:T(8,128)(2,1)} %get-tuple-element.289), channel_id=1, source_target_pairs={{0,16},{4,20},{8,24},{12,28},{16,0},{20,4},{24,8},{28,12},{1,17},{... | collective-permute-start | bytes 1572872 | tf_op jit(solution)/shard_map/ppermute | solution.py:441
  433.5 25.6 %collective-permute-start.68 = (bf16[512,512]{1,0:T(8,128)(2,1)S(1)}, bf16[512,512]{1,0:T(8,128)(2,1)S(1)}, u32[]{:S(2)}, u32[]{:S(2)}) collective-permute-start(bf16[512,512]{1,0:T(8,128)(2,1)S(1)} %add_convert_fusion.5.refs_0_), channel_id=1, source_target_pairs={{0,4},{4,0},{8,12},{12,8},{16,20},{20,16},{24,28},{28,24},{1,5},{5... | collective-permute-start | bytes 1572872 | tf_op jit(solution)/shard_map/ppermute | solution.py:441
  434.6 24.5 %collective-permute-start.69 = (bf16[512,512]{1,0:T(8,128)(2,1)S(1)}, bf16[512,512]{1,0:T(8,128)(2,1)S(1)}, u32[]{:S(2)}, u32[]{:S(2)}) collective-permute-start(bf16[512,512]{1,0:T(8,128)(2,1)S(1)} %add_convert_fusion.5.refs_0_), channel_id=1, source_target_pairs={{0,8},{4,12},{8,0},{12,4},{16,24},{20,28},{24,16},{28,20},{1,9},{5... | collective-permute-start | bytes 1572872 | tf_op jit(solution)/shard_map/ppermute | solution.py:441
  436.5 22.7 %collective-permute-start.70 = (bf16[128,2048]{1,0:T(8,128)(2,1)}, bf16[128,2048]{1,0:T(8,128)(2,1)S(1)}, u32[]{:S(2)}, u32[]{:S(2)}) collective-permute-start(bf16[128,2048]{1,0:T(8,128)(2,1)} %collective-permute-done.64.refs_2_), channel_id=1, source_target_pairs={{0,4},{4,0},{8,12},{12,8},{16,20},{20,16},{24,28},{28,24},{1,5},{5... | collective-permute-start | bytes 1572872 | tf_op jit(solution)/shard_map/ppermute | solution.py:441
  441.1 45.3 %collective-permute-start.72 = (bf16[256,2048]{1,0:T(8,128)(2,1)S(1)}, bf16[256,2048]{1,0:T(8,128)(2,1)S(1)}, u32[]{:S(2)}, u32[]{:S(2)}) collective-permute-start(bf16[256,2048]{1,0:T(8,128)(2,1)S(1)} %fusion.45), channel_id=1, source_target_pairs={{0,2},{1,3},{2,0},{3,1},{4,6},{5,7},{6,4},{7,5},{8,10},{9,11},{10,... | collective-permute-start | bytes 3145736 | tf_op jit(solution)/shard_map/ppermute | solution.py:438
  456.6 25.7 %collective-permute-start.73 = (bf16[512,512]{1,0:T(8,128)(2,1)S(1)}, bf16[512,512]{1,0:T(8,128)(2,1)S(1)}, u32[]{:S(2)}, u32[]{:S(2)}) collective-permute-start(bf16[512,512]{1,0:T(8,128)(2,1)S(1)} %copy-done.84), channel_id=1, source_target_pairs={{0,16},{4,20},{8,24},{12,28},{16,0},{20,4},{24,8},{28,12},{1,17},{... | collective-permute-start | bytes 1572872 | tf_op jit(solution)/shard_map/ppermute | solution.py:441
  459.3 27.1 %collective-permute-start.74 = (bf16[512,512]{1,0:T(8,128)(2,1)S(1)}, bf16[512,512]{1,0:T(8,128)(2,1)S(1)}, u32[]{:S(2)}, u32[]{:S(2)}) collective-permute-start(bf16[512,512]{1,0:T(8,128)(2,1)S(1)} %add_convert_fusion.4.refs_1_), channel_id=1, source_target_pairs={{0,4},{4,0},{8,12},{12,8},{16,20},{20,16},{24,28},{28,24},{1,5},{5... | collective-permute-start | bytes 1572872 | tf_op jit(solution)/shard_map/ppermute | solution.py:441
  460.4 26.1 %collective-permute-start.75 = (bf16[512,512]{1,0:T(8,128)(2,1)S(1)}, bf16[512,512]{1,0:T(8,128)(2,1)S(1)}, u32[]{:S(2)}, u32[]{:S(2)}) collective-permute-start(bf16[512,512]{1,0:T(8,128)(2,1)S(1)} %add_convert_fusion.4.refs_1_), channel_id=1, source_target_pairs={{0,8},{4,12},{8,0},{12,4},{16,24},{20,28},{24,16},{28,20},{1,9},{5... | collective-permute-start | bytes 1572872 | tf_op jit(solution)/shard_map/ppermute | solution.py:441
  463.1 23.4 %collective-permute-start.76 = (bf16[512,512]{1,0:T(8,128)(2,1)S(1)}, bf16[512,512]{1,0:T(8,128)(2,1)S(1)}, u32[]{:S(2)}, u32[]{:S(2)}) collective-permute-start(bf16[512,512]{1,0:T(8,128)(2,1)S(1)} %collective-permute-done.69.refs_2_), channel_id=1, source_target_pairs={{0,4},{4,0},{8,12},{12,8},{16,20},{20,16},{24,28},{28,24},{1,5},{5... | collective-permute-start | bytes 1572872 | tf_op jit(solution)/shard_map/ppermute | solution.py:441
  486.5 24.2 %collective-permute-start.78 = (bf16[512,512]{1,0:T(8,128)(2,1)S(1)}, bf16[512,512]{1,0:T(8,128)(2,1)S(1)}, u32[]{:S(2)}, u32[]{:S(2)}) collective-permute-start(bf16[512,512]{1,0:T(8,128)(2,1)S(1)} %copy-done.83), channel_id=1, source_target_pairs={{0,16},{4,20},{8,24},{12,28},{16,0},{20,4},{24,8},{28,12},{1,17},{... | collective-permute-start | bytes 1572872 | tf_op jit(solution)/shard_map/ppermute | solution.py:441
  486.6 25.7 %collective-permute-start.79 = (bf16[512,512]{1,0:T(8,128)(2,1)S(1)}, bf16[512,512]{1,0:T(8,128)(2,1)S(1)}, u32[]{:S(2)}, u32[]{:S(2)}) collective-permute-start(bf16[512,512]{1,0:T(8,128)(2,1)S(1)} %add_convert_fusion.3.refs_1_), channel_id=1, source_target_pairs={{0,4},{4,0},{8,12},{12,8},{16,20},{20,16},{24,28},{28,24},{1,5},{5... | collective-permute-start | bytes 1572872 | tf_op jit(solution)/shard_map/ppermute | solution.py:441
  487.7 24.6 %collective-permute-start.80 = (bf16[512,512]{1,0:T(8,128)(2,1)S(1)}, bf16[512,512]{1,0:T(8,128)(2,1)S(1)}, u32[]{:S(2)}, u32[]{:S(2)}) collective-permute-start(bf16[512,512]{1,0:T(8,128)(2,1)S(1)} %add_convert_fusion.3.refs_1_), channel_id=1, source_target_pairs={{0,8},{4,12},{8,0},{12,4},{16,24},{20,28},{24,16},{28,20},{1,9},{5... | collective-permute-start | bytes 1572872 | tf_op jit(solution)/shard_map/ppermute | solution.py:441
  489.9 22.4 %collective-permute-start.81 = (bf16[512,512]{1,0:T(8,128)(2,1)S(1)}, bf16[512,512]{1,0:T(8,128)(2,1)S(1)}, u32[]{:S(2)}, u32[]{:S(2)}) collective-permute-start(bf16[512,512]{1,0:T(8,128)(2,1)S(1)} %collective-permute-done.75.refs_3_), channel_id=1, source_target_pairs={{0,4},{4,0},{8,12},{12,8},{16,20},{20,16},{24,28},{28,24},{1,5},{5... | collective-permute-start | bytes 1572872 | tf_op jit(solution)/shard_map/ppermute | solution.py:441
  491.0 21.3 %collective-permute-start.82 = (f32[15872]{0:T(1024)S(1)}, f32[15872]{0:T(1024)S(1)}, u32[]{:S(2)}, u32[]{:S(2)}) collective-permute-start(f32[15872]{0:T(1024)S(1)} %pad_maximum_fusion.3), channel_id=1, source_target_pairs={{0,4},{4,0},{8,12},{12,8},{16,20},{20,16},{24,28},{28,24},{1,5},{5... | collective-permute-start | bytes 190472 | tf_op jit(solution)/shard_map/ppermute | solution.py:441
  512.5 18.6 %collective-permute-start.84 = (bf16[512,512]{1,0:T(8,128)(2,1)S(1)}, bf16[512,512]{1,0:T(8,128)(2,1)S(1)}, u32[]{:S(2)}, u32[]{:S(2)}) collective-permute-start(bf16[512,512]{1,0:T(8,128)(2,1)S(1)} %add_convert_fusion.2.refs_1_), channel_id=1, source_target_pairs={{0,4},{4,0},{8,12},{12,8},{16,20},{20,16},{24,28},{28,24},{1,5},{5... | collective-permute-start | bytes 1572872 | tf_op jit(solution)/shard_map/ppermute | solution.py:441
  513.5 17.5 %collective-permute-start.85 = (bf16[512,512]{1,0:T(8,128)(2,1)S(1)}, bf16[512,512]{1,0:T(8,128)(2,1)S(1)}, u32[]{:S(2)}, u32[]{:S(2)}) collective-permute-start(bf16[512,512]{1,0:T(8,128)(2,1)S(1)} %add_convert_fusion.2.refs_1_), channel_id=1, source_target_pairs={{0,8},{4,12},{8,0},{12,4},{16,24},{20,28},{24,16},{28,20},{1,9},{5... | collective-permute-start | bytes 1572872 | tf_op jit(solution)/shard_map/ppermute | solution.py:441
  515.5 20.4 %collective-permute-start.86 = (bf16[512,512]{1,0:T(8,128)(2,1)S(1)}, bf16[512,512]{1,0:T(8,128)(2,1)S(1)}, u32[]{:S(2)}, u32[]{:S(2)}) collective-permute-start(bf16[512,512]{1,0:T(8,128)(2,1)S(1)} %collective-permute-done.80.refs_3_), channel_id=1, source_target_pairs={{0,4},{4,0},{8,12},{12,8},{16,20},{20,16},{24,28},{28,24},{1,5},{5... | collective-permute-start | bytes 1572872 | tf_op jit(solution)/shard_map/ppermute | solution.py:441
  535.9 17.0 %collective-permute-start.91 = (bf16[512,512]{1,0:T(8,128)(2,1)S(1)}, bf16[512,512]{1,0:T(8,128)(2,1)S(1)}, u32[]{:S(2)}, u32[]{:S(2)}) collective-permute-start(bf16[512,512]{1,0:T(8,128)(2,1)S(1)} %collective-permute-done.85.refs_3_), channel_id=1, source_target_pairs={{0,4},{4,0},{8,12},{12,8},{16,20},{20,16},{24,28},{28,24},{1,5},{5... | collective-permute-start | bytes 1572872 | tf_op jit(solution)/shard_map/ppermute | solution.py:441
  566.7 18.0 %collective-permute-start.102 = (bf16[256,384]{1,0:T(8,128)(2,1)S(1)}, bf16[256,384]{1,0:T(8,128)(2,1)S(1)}, u32[]{:S(2)}, u32[]{:S(2)}) collective-permute-start(bf16[256,384]{1,0:T(8,128)(2,1)S(1)} %get-tuple-element.340), channel_id=1, source_target_pairs={{0,16},{4,20},{8,24},{12,28},{16,0},{20,4},{24,8},{28,12},{1,17},{... | collective-permute-start | bytes 589832 | tf_op jit(solution)/shard_map/ppermute | solution.py:441
  579.9 17.5 %collective-permute-start.101 = (bf16[256,384]{1,0:T(8,128)(2,1)S(1)}, bf16[256,384]{1,0:T(8,128)(2,1)S(1)}, u32[]{:S(2)}, u32[]{:S(2)}) collective-permute-start(bf16[256,384]{1,0:T(8,128)(2,1)S(1)} %get-tuple-element.339), channel_id=1, source_target_pairs={{0,16},{4,20},{8,24},{12,28},{16,0},{20,4},{24,8},{28,12},{1,17},{... | collective-permute-start | bytes 589832 | tf_op jit(solution)/shard_map/ppermute | solution.py:441
  (177 other events, 1940.2 us)

commit v6 on v5

--- a/solution.py
+++ b/solution.py
@@ -247,12 +247,13 @@
             out_ref[...] = piece[...].astype(F32)
 
 
-def place_quarters(whole, pieces, shape, axis, chunk, chunks, quarter):
+def place_quarters(whole, pieces, shape, axis, offset, quarter):
     rows, columns = pieces[0].shape
     if axis == 0:
-        spot = lambda k, q: ((q[0] ^ k) * chunks + chunk, 0)
+        each, first_row = shape[0] // 4 // rows, offset // rows
+        spot = lambda k, q: ((q[0] ^ k) * each + first_row, 0)
     else:
-        spot = lambda k, q: (chunk, q[0] ^ k)
+        spot = lambda k, q: (offset // rows, q[0] ^ k)
     first = whole is None
     operands = ([] if first else [whole]) + list(pieces)
     return pl.pallas_call(
@@ -311,8 +312,9 @@
     )(*gains, *blocks)
 
 
-def outer_kernel(lefts, pieces, _, *refs):
-    left_refs, rights, (o_ref, left_ref, joined_ref) = refs[:lefts], refs[lefts:-3], refs[-3:]
+def outer_kernel(lefts, pieces, outs, _, *refs):
+    left_refs, rights = refs[:lefts], refs[lefts : -2 - outs]
+    out_refs, (left_ref, joined_ref) = refs[-2 - outs : -2], refs[-2:]
 
     @pl.when(pl.program_id(0) == 0)
     def _():
@@ -328,31 +330,34 @@
     for ref in rights:
         joined_ref[pl.ds(column, ref.shape[0]), :] = ref[...]
         column += ref.shape[0]
-    o_ref[...] = jnp.dot(left_ref[...], joined_ref[...], preferred_element_type=F32).astype(BF)
-
-
-def outer_blocks(lefts, rights, quarter):
+    total = jnp.dot(left_ref[...], joined_ref[...], preferred_element_type=F32).astype(BF)
+    row = 0
+    for ref in out_refs:
+        ref[...] = total[row : row + ref.shape[0], :]
+        row += ref.shape[0]
+
+
+def outer_blocks(lefts, rights, sizes, quarter):
     width = rights[0].shape[1]
     tokens = sum(r.shape[0] for r in rights)
-    left = max(row + taken for _, taken, row, _ in lefts)
+    left = sum(sizes)
     tile = 512
     specs = [
-        pl.BlockSpec((a.shape[0], taken), lambda j, q: (0, q[0]))
-        if taken < a.shape[1]
-        else pl.BlockSpec(a.shape, lambda j, q: (0, 0))
-        for a, taken, _, _ in lefts
+        pl.BlockSpec((a.shape[0], taken), lambda j, q, m=times, o=offset: (0, q[0] * m + o))
+        for a, taken, times, offset, _, _ in lefts
     ]
+    pieces = [(row, token) for *_, row, token in lefts]
     return pl.pallas_call(
-        functools.partial(outer_kernel, len(lefts), [(r, t) for _, _, r, t in lefts]),
+        functools.partial(outer_kernel, len(lefts), pieces, len(sizes)),
         grid_spec=pltpu.PrefetchScalarGridSpec(
             num_scalar_prefetch=1,
             grid=(width // tile,),
             in_specs=specs
             + [pl.BlockSpec((r.shape[0], tile), lambda j, q: (0, j)) for r in rights],
-            out_specs=pl.BlockSpec((left, tile), lambda j, q: (0, j)),
+            out_specs=[pl.BlockSpec((size, tile), lambda j, q: (0, j)) for size in sizes],
             scratch_shapes=[pltpu.VMEM((left, tokens), BF), pltpu.VMEM((tokens, tile), BF)],
         ),
-        out_shape=jax.ShapeDtypeStruct((left, width), BF),
+        out_shape=[jax.ShapeDtypeStruct((size, width), BF) for size in sizes],
         compiler_params=pltpu.CompilerParams(vmem_limit_bytes=56 << 20),
         cost_estimate=pl.CostEstimate(
             flops=2 * tokens * left * width,
@@ -360,7 +365,7 @@
             transcendentals=0,
         ),
         name="outer_blocks",
-    )(quarter.reshape(1), *[a for a, _, _, _ in lefts], *rights)
+    )(quarter.reshape(1), *[a for a, *_ in lefts], *rights)
 
 
 def back_kernel(weight_ref, slope_ref, *refs):
@@ -489,25 +494,26 @@
     shift_attn = ln1_bias.astype(F32)
     gain_mlp = ln2_gain.astype(F32)
     shift_mlp = ln2_bias.astype(F32)
-    mask_f = valid_mask.astype(F32)
     gains = [v[None, :] for v in (ln1_gain, ln1_bias, ln2_gain, ln2_bias)]
     close = 2 * rows
 
     def units(normed):
         return jnp.dot(normed, fc1_weight, preferred_element_type=F32) + fc1_bias.astype(F32)
 
+    near_blocks, hidden_y = gather_near(hidden)
+    first = first_far(hidden)
+    norm_attn_own, norm_mlp_own = both_norms(near_blocks[:2], gains)
+    mask_f = after(valid_mask, norm_mlp_own).astype(F32)
     count = jnp.full((8, 128), jnp.sum(mask_f), F32)
     count = count + to_core(count)
     counted = flip(count, 1)
-    near_blocks, hidden_y = gather_near(hidden)
-    first = first_far(hidden)
-    norm_attn_own, norm_mlp_own = both_norms(near_blocks[:2], gains)
     pre_own = units(norm_mlp_own)
     active_own = exact_gelu(pre_own)[0].astype(BF)
+    start = after(jnp.asarray(block_ids) * rows, norm_mlp_own)
     table = jnp.concatenate(
         [
-            lax.dynamic_slice_in_dim(jnp.asarray(rotary_table(LEN)), b * rows, rows, 0)
-            for b in block_ids
+            lax.dynamic_slice_in_dim(jnp.asarray(rotary_table(LEN)), start[i], rows, 0)
+            for i in range(tp)
         ],
         axis=0,
     )
@@ -556,7 +562,7 @@
     part_rest = branch_rows(context[close:], active_rest).reshape(-1, 2, rows, D)
     mates_rest = to_core(part_rest[:, 1].astype(BF))
     part_own = branch_rows(context[:close], after(active_own, part_rest)).reshape(2, rows, D)
-    part_own, mates_rest, last, counted = meet(part_own, mates_rest, last, counted)
+    part_own, mates_rest, counted = meet(part_own, mates_rest, counted)
     count = count + counted
 
     sums = part_rest[:, 0] + mates_rest.astype(F32)
@@ -586,13 +592,16 @@
     grad_first = first_far(grad_low)
     grad_mate = to_core(grad_low)
     fc1_quarter = quarter_of(fc1_weight, 1, quarter)
-    fc2_quarter = quarter_of(fc2_weight, 0, quarter)
+    fc2_quarter = quarter_of(after(fc2_weight, norm_mlp_far), 0, quarter)
+    context_quarter = quarter_of(after(context, norm_mlp_far), 1, quarter)
     pre_far = jnp.dot(norm_mlp_far, fc1_quarter, preferred_element_type=F32) + quarter_of(
         fc1_bias, 0, quarter
     ).astype(F32)
     active_far, slope_far = exact_gelu(pre_far)
     active_far = active_far.astype(BF)
-    grad_y, grad_first, active_far, grad_mate = meet(grad_y, grad_first, active_far, grad_mate)
+    grad_y, grad_first, active_far, grad_mate, fc2_quarter, context_quarter = meet(
+        grad_y, grad_first, active_far, grad_mate, fc2_quarter, context_quarter
+    )
 
     grad_second = second_far(grad_first, grad_y)
     grad_blocks = [grad_low, grad_mate]
@@ -677,10 +686,19 @@
         sends, wait = asked
         due.setdefault(now + wait, []).append((walker, [move(v) for v, move in sends]))
 
-    def enqueue(name, part, count):
-        size = part.shape[0] // count
-        for i in range(count):
-            queue.append((name, lax.slice_in_dim(part, i * size, (i + 1) * size, axis=0)))
+    parts_of = {}
+
+    def cut(part, shares):
+        unit = part.shape[0] // 16
+        edges = [unit * sum(shares[:i]) for i in range(len(shares) + 1)]
+        return [lax.slice_in_dim(part, a, b, axis=0) for a, b in zip(edges, edges[1:])]
+
+    def enqueue(name, chunks):
+        rows_before, _ = parts_of.get(name, (0, 0))
+        for piece in chunks:
+            queue.append((name, piece))
+            rows_before += piece.shape[0]
+        parts_of[name] = (rows_before, chunks[0].shape[1])
 
     def turn(*others):
         now = clock[0]
@@ -706,52 +724,45 @@
             start(walker, request, now)
         return tied
 
-    placed = {}
-
-    def place(name, axis, chunks):
-        whole, done = placed.get(name, (None, 0))
-        pieces = results.get(name, [])
-        while done < len(pieces):
-            whole = place_one(whole, pieces[done], axis, done, chunks)
-            done += 1
-        placed[name] = (whole, done)
-        return whole
-
-    def place_one(whole, pieces, axis, chunk, chunks):
+    def place_one(whole, pieces, shape, axis, offset):
         rows_here, columns = pieces[0].shape
-        shape = (
-            (4 * rows_here * chunks, columns) if axis == 0 else (rows_here * chunks, 4 * columns)
-        )
         if columns % 128 == 0:
-            return place_quarters(whole, pieces, shape, axis, chunk, chunks, quarter)
+            return place_quarters(whole, pieces, shape, axis, offset, quarter)
         if whole is None:
             whole = jnp.zeros(shape, F32)
         for index, piece in enumerate(pieces):
             spot = quarter ^ index
             start = (
-                ((spot * chunks + chunk) * rows_here, 0)
-                if axis == 0
-                else (chunk * rows_here, spot * columns)
+                (spot * (shape[0] // 4) + offset, 0) if axis == 0 else (offset, spot * columns)
             )
             whole = lax.dynamic_update_slice(whole, piece.astype(F32), start)
         return whole
 
-    mine = active_far.shape[1]
-    lefts = [
-        (active_own, mine, 0, 0),
-        (active_rest, mine, 0, close),
-        (active_far, mine, 0, LEN),
-    ]
+    half = active_far.shape[1] // 2
+    rights = [grad_near] + grad_far
+
+    def hidden_lefts(part):
+        return [
+            (active_own, half, 2, part, 0, 0),
+            (active_rest, half, 2, part, 0, close),
+            (active_far, half, 0, part, 0, LEN),
+        ]
+
+    chunk = half // 2
     kept_columns = context.shape[1] // 4
-    context_parts = [quarter_of(context, 1, quarter)] + context_far
-    for index, piece in enumerate(context_parts):
-        lefts.append((piece, kept_columns, mine, index * LEN))
-    part = outer_blocks(lefts, [grad_near] + grad_far, quarter)
-    enqueue("fc2", part[:mine], 4)
-    enqueue("out", part[mine:], 1)
+    enqueue("fc2", outer_blocks(hidden_lefts(0), rights, [chunk] * 2, quarter))
     turn()
+    lefts = hidden_lefts(1)
+    for index, piece in enumerate([context_quarter] + context_far):
+        lefts.append((piece, kept_columns, 0, 0, half, index * LEN))
+    *parts, out_part = outer_blocks(
+        lefts, [gate(grad_near)] + grad_far, [chunk] * 2 + [kept_columns], quarter
+    )
+    enqueue("fc2", parts)
+    enqueue("out", [out_part])
     grad_qkv_far = []
-    walk(swap_walk(grad_qkv, grad_qkv_far))
+    walk(swap_walk(gate(grad_qkv), grad_qkv_far))
+    (out_part,) = turn(out_part)
     grad_inner_far = back_blocks([gate(grad_far[0])] + grad_far[1:], fc2_quarter, slope_far)
     (grad_inner_far,) = turn(grad_inner_far)
     inner_quarter = gate(quarter_of(grad_inner, 1, quarter))
@@ -761,9 +772,7 @@
         + contract(norm_mlp_far, grad_inner_far, 0, 0)
     )
     (fc1_part,) = turn(fc1_part.astype(BF))
-    enqueue("fc1", fc1_part, 4)
-    grad_norm_attn = contract(gate(grad_qkv), qkv_weight, 1, 1)
-    (grad_norm_attn,) = turn(grad_norm_attn)
+    enqueue("fc1", cut(fc1_part, [4, 4, 4, 4]))
     qkv_quarter = gate(quarter_of(grad_qkv, 1, quarter))
     qkv_part = (
         contract(norm_attn_own, qkv_quarter[:close], 0, 0)
@@ -771,7 +780,9 @@
         + contract(norm_attn_far, jnp.concatenate(grad_qkv_far, axis=0), 0, 0)
     )
     (qkv_part,) = turn(qkv_part.astype(BF))
-    enqueue("qkv", qkv_part, 8)
+    enqueue("qkv", cut(qkv_part, [4, 4, 4, 2, 1, 1]))
+    grad_norm_attn = contract(gate(grad_qkv), qkv_weight, 1, 1)
+    (grad_norm_attn,) = turn(grad_norm_attn)
     grad_norm_mlp = contract(gate(grad_inner), fc1_weight, 1, 1)
     (grad_norm_mlp,) = turn(grad_norm_mlp)
 
@@ -781,16 +792,8 @@
     inverse = lax.rsqrt(jnp.mean(centered * centered, axis=-1, keepdims=True) + EPSILON)
     xhat = centered * inverse
     gained = grad_norm_attn * gain_attn + grad_norm_mlp * gain_mlp
-    grad_hidden = inverse * (
-        gained
-        - jnp.mean(gained, axis=-1, keepdims=True)
-        - xhat * jnp.mean(gained * xhat, axis=-1, keepdims=True)
-    )
-    blocks = grad_hidden.reshape(ways, 2, rows, D)
-    mates = blocks[:, 1].astype(BF)
-    kept, mates = turn(blocks[:, 0], mates)
-    outcome = {}
-    walk(scatter_walk(kept, mates, outcome))
+    lift = jnp.mean(gained, axis=-1, keepdims=True)
+    pull = jnp.mean(gained * xhat, axis=-1, keepdims=True)
     tensor_parts = jnp.stack(
         [
             jnp.sum(grad_norm_attn * xhat, axis=0),
@@ -801,32 +804,47 @@
             jnp.full((D,), error_part, F32),
         ]
     ).reshape(-1)
-    fc1_bias_part = jnp.sum(grad_inner, axis=0, dtype=F32)
-    qkv_bias_part = jnp.sum(grad_qkv, axis=0, dtype=F32)
-    tensor_parts, fc1_bias_part, qkv_bias_part = turn(tensor_parts, fc1_bias_part, qkv_bias_part)
+    tensor_parts, lift, pull = turn(tensor_parts, lift, pull)
+    grad_hidden = inverse * (gained - lift - xhat * pull)
+    blocks = grad_hidden.reshape(ways, 2, rows, D)
+    kept, mates = turn(blocks[:, 0], blocks[:, 1].astype(BF))
+    outcome = {}
+    walk(scatter_walk(kept, mates, outcome))
+    fc1_bias_part = jnp.sum(gate(grad_inner), axis=0, dtype=F32)
+    qkv_bias_part = jnp.sum(gate(grad_qkv), axis=0, dtype=F32)
+    fc1_bias_part, qkv_bias_part = turn(fc1_bias_part, qkv_bias_part)
     walk(small_walk(tensor_parts, jnp.concatenate([fc1_bias_part, qkv_bias_part]), outcome))
-    layout = {"fc2": (0, 4), "out": (0, 1), "fc1": (1, 4), "qkv": (1, 8)}
+    axes = {"fc2": 0, "out": 0, "fc1": 1, "qkv": 1}
+    placed = {name: (None, 0, 0) for name in axes}
+
+    def place(name):
+        whole, done, offset = placed[name]
+        pieces = results[name][done]
+        lengths, columns = parts_of[name]
+        shape = (4 * lengths, columns) if axes[name] == 0 else (lengths, 4 * columns)
+        whole = place_one(whole, pieces, shape, axes[name], offset)
+        placed[name] = (whole, done + 1, offset + pieces[0].shape[0])
+
     while queue or due:
-        for name, (axis, chunks) in layout.items():
-            if len(results.get(name, [])) > placed.get(name, (None, 0))[1]:
-                whole, done = placed.get(name, (None, 0))
-                whole = place_one(whole, results[name][done], axis, done, chunks)
-                placed[name] = (whole, done + 1)
-                (whole,) = turn(whole)
-                placed[name] = (whole, done + 1)
-                break
-        else:
-            turn()
+        ready = []
+        for name in axes:
+            if len(ready) < 2 and len(results.get(name, [])) > placed[name][1]:
+                place(name)
+                ready.append(name)
+        wholes = turn(*[placed[name][0] for name in ready])
+        for name, whole in zip(ready, wholes):
+            placed[name] = (whole,) + placed[name][1:]
+    for name in axes:
+        while len(results[name]) > placed[name][1]:
+            place(name)
     input_grad = outcome["input"]
     small = outcome["small"]
     vectors = small[: 6 * D].reshape(6, D)
     fc1_bias_grad = small[6 * D : 6 * D + fc1_bias_part.shape[0]]
     qkv_bias_grad = small[6 * D + fc1_bias_part.shape[0] :]
     loss_value = vectors[5, 0] / (count[0, 0] * D)
-    fc2_weight_grad = place("fc2", 0, 4)
-    out_weight_grad = place("out", 0, 1)
-    fc1_weight_grad = place("fc1", 1, 4)
-    qkv_weight_grad = place("qkv", 1, 8)
+    fc2_weight_grad, out_weight_grad = placed["fc2"][0], placed["out"][0]
+    fc1_weight_grad, qkv_weight_grad = placed["fc1"][0], placed["qkv"][0]
     return (
         output_f.astype(BF),
         loss_value,

time: 651 us -> 672 us (1.032)
  waiting for transfers between devices: 161 us -> 188 us
  starting transfers between devices: 115 us -> 93.6 us
  between operations: 6.58 us -> 14.1 us
    ppermute x92 -> x84, waiting for transfers between devices: 148 us -> 184 us  [flip(): return lax.ppermute(v, 'dp', [(d, d ^ mask) for d in range(dp)])]
    ppermute x92 -> x84, starting transfers between devices: 104 us -> 81.6 us  [flip(): return lax.ppermute(v, 'dp', [(d, d ^ mask) for d in range(dp)])]
    pallas_call x1 -> x2, Pallas kernels: 17.8 us -> 23.3 us  [outer_blocks(): pl.pallas_call(functools.partial(outer_kernel, len(lefts), pieces, len(si...]
    pallas_call x17 -> x15, Pallas kernels: 38.9 us -> 35.8 us  [place_quarters(): pl.pallas_call(place_kernel, grid_spec=pltpu.PrefetchScalarGridSpec(num_s...]
    unnamed x246 -> x216, local copies, waits for them, and re-layouts: 24.3 us -> 25.2 us
  transfers between devices with their start and end apart: 121 -> 113, of which waited for: 44 -> 40; matrix products, arithmetic and copies ran while one was open for 29% -> 29% of each run, Pallas kernels for 21% -> 20%
where the time goes in v6:
time: 672 us; the launch traced here: 661 us
  waiting for transfers between devices  188 us (28%)
  Pallas kernels  145 us (22%)
  matrix products  118 us (18%)
  starting transfers between devices  93.6 us (14%)
  local copies, waits for them, and re-layouts  53.3 us (8%)
  other arithmetic  48.1 us (7%)
  between operations  14.1 us (2%)
    ppermute x84, waiting for transfers between devices, flip(): return lax.ppermute(v, 'dp', [(d, d ^ mask) for d in range(dp)])  184 us
    ppermute x84, starting transfers between devices, flip(): return lax.ppermute(v, 'dp', [(d, d ^ mask) for d in range(dp)])  81.6 us
    dot_general x10, matrix products, contract(): lax.dot_general(left_side, right_side, (((left_dim,), (right_dim,)), ((),...  71.3 us
    pallas_call x3, Pallas kernels, both_norms(): pl.pallas_call(functools.partial(norms_kernel, count), grid=(count,), in_...  36 us
    pallas_call x15, Pallas kernels, place_quarters(): pl.pallas_call(place_kernel, grid_spec=pltpu.PrefetchScalarGridSpec(num_s...  35.8 us
    unnamed x216, local copies, waits for them, and re-layouts  25.2 us
    pallas_call x2, Pallas kernels, outer_blocks(): pl.pallas_call(functools.partial(outer_kernel, len(lefts), pieces, len(si...  23.3 us
    dot_general x2, matrix products, units(): jnp.dot(normed, fc1_weight, preferred_element_type=F32)  20.1 us
  transfers between devices with their start and end apart: 113, of which 40 were waited for; matrix products, arithmetic and copies ran while one was open for 29% of the time, Pallas kernels for 20%

profile of v6, /device:TPU:0, one launch (start us, length us, event | category | flops | bytes accessed | tf_op | source)
XLA Modules:
  0.0 660.6 jit_solution(17610775007568297144)
XLA Ops:
  1.2 2.6 collective-permute-start.3
  12.3 3.1 both_norms.3
  17.4 9.7 %multiply_convert_fusion.2 = (bf16[512,2048]{1,0:T(8,128)(2,1)}, f32[512,2048]{1,0:T(8,128)}) fusion(f32[2048]{0:T(1024)S(1)} %convert_element_type.245, bf16[512,2048]{1,0:T(8,128)(2,1)} %get-tuple-element.205, bf16[2048,2048]{1,0:T(8,128)(2,1)} %param.32), kind=kOutput, calls=%fused_computation.38 | convolution fusion | flops 4301258752 | bytes 16785408 | tf_op jit(solution)/shard_map/dot_general | solution.py:501
  38.6 2.8 copy-done.14
  41.4 5.4 qkv_rotary.2.refs_0_
  55.4 4.7 both_norms.4
  60.1 2.6 copy-done.3
  64.2 2.8 copy-done.15
  66.9 5.5 qkv_rotary.3.q_ref.k_ref.v_ref
  72.5 9.7 %attend.1 = (bf16[1024,512]{1,0:T(8,128)(2,1)S(1)}, f32[2,1024,1]{2,1,0:T(8,128)S(1)}) custom-call(s32[1]{0:T(128)S(6)} %copy.75.prefix_ref, bf16[1024,1536]{1,0:T(8,128)(2,1)S(1)} %qkv_rotary.3.q_ref.k_ref.v_ref, bf16[1024,1536]{1,0:T(8,128)(2,1)S(1)} %qkv_rotary.3.q_ref.k_ref.v_ref, bf16[1024,1536]{1,0:T(8,128)(2,1)S(1)} %qkv_rotary.3.q_ref.k_ref.v_ref, ...), custom_call_target="tpu_custom_call" | custom-call | flops 2147483648 | bytes 4194304 | tf_op jit(solution)/shard_map/attend/pallas_call | solution.py:142
  83.2 2.7 collective-permute-start.13
  85.9 10.3 %multiply_convert_fusion.1 = (bf16[512,2048]{1,0:T(8,128)(2,1)S(1)}, f32[512,2048]{1,0:T(8,128)}) fusion(f32[2048]{0:T(1024)S(1)} %convert_element_type.245, bf16[512,2048]{1,0:T(8,128)(2,1)S(1)} %copy-done.80, bf16[2048,2048]{1,0:T(8,128)(2,1)} %param.32), kind=kOutput, calls=%fused_computation.37 | convolution fusion | flops 4301258752 | bytes 16785408 | tf_op jit(solution)/shard_map/dot_general | solution.py:501
  97.6 4.6 fusion.68
  106.2 4.6 fusion.69
  112.4 6.9 %collective-permute-done.24 = bf16[128,2048]{1,0:T(8,128)(2,1)S(1)} collective-permute-done((bf16[128,2048]{1,0:T(8,128)(2,1)S(1)}, bf16[128,2048]{1,0:T(8,128)(2,1)S(1)}, u32[]{:S(2)}, u32[]{:S(2)}) %collective-permute-start.24) | collective-permute-done | bytes 524320 | tf_op jit(solution)/shard_map/ppermute | solution.py:446
  120.2 4.8 collective-permute-done.25
  135.1 2.6 collective-permute-start.18
  141.5 28.3 %both_norms.5 = (bf16[3072,2048]{1,0:T(8,128)(2,1)}, bf16[3072,2048]{1,0:T(8,128)(2,1)}) custom-call(bf16[1,2048]{1,0:T(2,128)(2,1)S(1)} %broadcast_in_dim.24.refs_0_, bf16[1,2048]{1,0:T(2,128)(2,1)S(1)} %broadcast_in_dim.25.refs_1_, bf16[1,2048]{1,0:T(2,128)(2,1)S(1)} %broadcast_in_dim.26.refs_2_, bf16[1,2048]{1,0:T(2,128)(2,1)S(1)} %broadcast_in_dim.27.refs_3_, ...), custom_call_target="tpu_custom_call" | custom-call | flops 75497472 | bytes 37748736 | tf_op jit(solution)/shard_map/both_norms/pallas_call | solution.py:298
  171.0 3.0 fusion.30
  178.9 14.7 %fusion.21 = (f32[3072,512]{1,0:T(8,128)}, bf16[3072,512]{1,0:T(8,128)(2,1)}) fusion(f32[512]{0:T(512)S(1)} %dynamic-slice_convert_fusion, bf16[3072,2048]{1,0:T(8,128)(2,1)} %get-tuple-element.237, bf16[2048,2048]{1,0:T(8,128)(2,1)} %param.32, s32[]{:T(128)S(6)} %select_n.81), kind=kOutput, calls=%fused_computation.28 | convolution fusion | flops 6459752448 | bytes 24119300 | tf_op jit(solution)/shard_map/dot_general | solution.py:597
  195.2 3.2 constant_dynamic-slice_fusion.6.weight_ref
  198.4 3.3 collective-permute-done.27
  207.4 17.9 %fusion.17 = bf16[1024,2048]{1,0:T(8,128)(2,1)} fusion(f32[512,2048]{1,0:T(8,128)} %get-tuple-element.448, f32[512,2048]{1,0:T(8,128)} %get-tuple-element.446, bf16[1024,2048]{1,0:T(8,128)(2,1)S(1)} %constant_dynamic-update-slice_fusion.2.refs_3_.refs_7_, bf16[2048,2048]{1,0:T(8,128)(2,1)} %param.34), kind=kOutput, calls=%fused_computation.21 | convolution fusion | flops 8613003264 | bytes 25165824 | tf_op jit(solution)/shard_map/dot_general | solution.py:34
  227.7 3.1 collective-permute-done.32.refs_12_.refs_16_.refs_8_
  234.7 11.7 %attend_back.1 = bf16[1024,1536]{1,0:T(8,128)(2,1)} custom-call(s32[1]{0:T(128)S(6)} %copy.75.prefix_ref, bf16[1024,1536]{1,0:T(8,128)(2,1)} %copy-done.4, bf16[1024,1536]{1,0:T(8,128)(2,1)} %copy-done.4, bf16[1024,1536]{1,0:T(8,128)(2,1)} %copy-done.4, bf16[1024,512]{1,0:T(8,128)(2,1)S(1)} %convolution_convert_fusion.g_ref, f32[2,1024,1]{2,1,0:T(8,128)S(1)} %copy-done.35, ...), custom_call_target="tpu_custom_call" | custom-call | flops 5368709120 | bytes 7340032 | tf_op jit(solution)/shard_map/attend_back/pallas_call | solution.py:212
  254.7 10.6 %outer_blocks.2 = (bf16[128,2048]{1,0:T(8,128)(2,1)}, bf16[128,2048]{1,0:T(8,128)(2,1)}) custom-call(s32[1]{0:T(128)} %bitcast.18._.quarter_ref, bf16[512,2048]{1,0:T(8,128)(2,1)} %get-tuple-element.223.refs_0_, bf16[512,2048]{1,0:T(8,128)(2,1)} %copy-done.76, bf16[3072,512]{1,0:T(8,128)(2,1)} %get-tuple-element.250.refs_2_, bf16[1024,2048]{1,0:T(8,128)(2,1)} %copy-done.64, ...), custom_call_target="tpu_custom_call" | custom-call | flops 4294967296 | bytes 18874368 | tf_op jit(solution)/shard_map/outer_blocks/pallas_call | solution.py:350
  265.7 12.8 %outer_blocks.3 = (bf16[128,2048]{1,0:T(8,128)(2,1)}, bf16[128,2048]{1,0:T(8,128)(2,1)}, bf16[128,2048]{1,0:T(8,128)(2,1)}) custom-call(s32[1]{0:T(128)} %bitcast.18._.quarter_ref, bf16[512,2048]{1,0:T(8,128)(2,1)} %get-tuple-element.223.refs_0_, bf16[512,2048]{1,0:T(8,128)(2,1)} %copy-done.76, bf16[3072,512]{1,0:T(8,128)(2,1)} %get-tuple-element.250.refs_2_, ...), custom_call_target="tpu_custom_call" | custom-call | flops 6442450944 | bytes 19922944 | tf_op jit(solution)/shard_map/outer_blocks/pallas_call | solution.py:350
  285.9 17.7 %back_blocks.1 = bf16[3072,512]{1,0:T(8,128)(2,1)} custom-call(bf16[512,2048]{1,0:T(8,128)(2,1)} %constant_dynamic-slice_fusion.6.weight_ref, f32[3072,512]{1,0:T(8,128)} %get-tuple-element.413.slope_ref, bf16[256,2048]{1,0:T(8,128)(2,1)} %copy-done.69, bf16[256,2048]{1,0:T(8,128)(2,1)} %collective-permute-done.37.refs_5_.refs_9_.refs_1_, ...), custom_call_target="tpu_custom_call" | custom-call | flops 6442450944 | bytes 22020096 | tf_op jit(solution)/shard_map/back_blocks/pallas_call | solution.py:384
  309.4 5.3 collective-permute-done.46
  314.7 11.8 %add_convert_fusion = bf16[2048,512]{1,0:T(8,128)(2,1)} fusion(f32[2048,512]{1,0:T(8,128)S(1)} %fusion.48, f32[2048,512]{1,0:T(8,128)S(1)} %fusion.46, bf16[3072,2048]{1,0:T(8,128)(2,1)} %get-tuple-element.237, bf16[3072,512]{1,0:T(8,128)(2,1)} %back_blocks.1), kind=kOutput, calls=%fused_computation.36 | convolution fusion | flops 6445596672 | bytes 26214400 | tf_op jit(solution)/shard_map/dot_general | solution.py:34
  328.4 22.8 %collective-permute-done.45 = bf16[1024,384]{1,0:T(8,128)(2,1)} collective-permute-done((bf16[1024,384]{1,0:T(8,128)(2,1)}, bf16[1024,384]{1,0:T(8,128)(2,1)}, u32[]{:S(2)}, u32[]{:S(2)}) %collective-permute-start.45) | collective-permute-done | bytes 786464 | tf_op jit(solution)/shard_map/ppermute | solution.py:446
  352.0 10.3 %collective-permute-done.49.refs_2_ = bf16[128,2048]{1,0:T(8,128)(2,1)S(1)} collective-permute-done((bf16[128,2048]{1,0:T(8,128)(2,1)S(1)}, bf16[128,2048]{1,0:T(8,128)(2,1)S(1)}, u32[]{:S(2)}, u32[]{:S(2)}) %collective-permute-start.49) | collective-permute-done | bytes 524320 | tf_op jit(solution)/shard_map/ppermute | solution.py:446
  370.3 11.4 %add_convert_fusion.1 = bf16[2048,384]{1,0:T(8,128)(2,1)} fusion(f32[2048,384]{1,0:T(8,128)S(1)} %fusion.54, f32[2048,384]{1,0:T(8,128)S(1)} %fusion.52, bf16[3072,2048]{1,0:T(8,128)(2,1)} %get-tuple-element.283, bf16[1024,384]{1,0:T(8,128)(2,1)} %collective-permute-done.45, bf16[1024,384]{1,0:T(8,128)(2,1)} %collective-permute-done.44, ...), kind=kOutput, calls=%fused_computation.41 | convolution fusion | flops 4841275392 | bytes 22806528 | tf_op jit(solution)/shard_map/dot_general | solution.py:34
  383.1 4.6 collective-permute-done.54.refs_3_
  390.4 6.7 %fusion.70 = f32[1024,2048]{1,0:T(8,128)S(1)} fusion(bf16[1024,1536]{1,0:T(8,128)(2,1)S(1)} %copy-done.60, bf16[2048,1536]{1,0:T(8,128)(2,1)S(1)} %bitcast.89), kind=kOutput, calls=%fused_computation.151 | convolution fusion | flops 6442450944 | bytes 17825792 | tf_op jit(solution)/shard_map/dot_general | solution.py:34
  397.2 5.5 collective-permute-done.55.refs_2_
  402.7 6.7 %collective-permute-done.56.refs_3_ = bf16[128,2048]{1,0:T(8,128)(2,1)S(1)} collective-permute-done((bf16[128,2048]{1,0:T(8,128)(2,1)S(1)}, bf16[128,2048]{1,0:T(8,128)(2,1)S(1)}, u32[]{:S(2)}, u32[]{:S(2)}) %collective-permute-start.56) | collective-permute-done | bytes 524320 | tf_op jit(solution)/shard_map/ppermute | solution.py:446
  414.4 14.9 %fusion.71 = f32[1024,2048]{1,0:T(8,128)} fusion(bf16[1024,2048]{1,0:T(8,128)(2,1)} %fusion.17, bf16[2048,2048]{1,0:T(8,128)(2,1)} %param.32), kind=kOutput, calls=%fused_computation.152 | convolution fusion | flops 8589934592 | bytes 20971520 | tf_op jit(solution)/shard_map/dot_general | solution.py:34
  431.0 5.1 collective-permute-done.62.refs_4_
  440.0 2.7 convert_reduce_fusion
  442.7 3.7 fusion.11
  446.4 10.5 %fusion.59 = (f32[2048]{0:T(1024)S(1)}, f32[2048]{0:T(1024)S(1)}, f32[1024]{0:T(1024)S(1)}, f32[1024]{0:T(1024)S(1)}, f32[1024,2048]{1,0:T(8,128)}, /*index=5*/f32[2048]{0:T(1024)S(1)}, f32[2048]{0:T(1024)S(1)}) fusion(f32[1024,2048]{1,0:T(8,128)S(1)} %copy-done.74, f32[1024]{0:T(1024)S(1)} %add_rsqrt_fusion, f32[1024]{0:T(1024)S(1)} %broadcast_multiply_fusion.2, ...), kind=kLoop, calls=%fused_computation.141 | loop fusion | flops 46127104 | bytes 29425664 | tf_op jit(solution)/shard_map/reduce_sum | solution.py:802
  457.7 5.8 collective-permute-done.58
  467.0 7.7 %fusion.10 = f32[1024,2048]{1,0:T(8,128)S(1)} fusion(f32[1024,2048]{1,0:T(8,128)} %get-tuple-element.410, f32[1024]{0:T(1024)S(1)} %broadcast_multiply_fusion, f32[1024]{0:T(1024)S(1)} %broadcast_multiply_fusion.1, f32[1024]{0:T(1024)S(1)} %add_rsqrt_fusion, f32[1024]{0:T(1024)S(1)} %broadcast_multiply_fusion.2, bf16[256,2048]{1,0:T(8,128)(2,1)S(1)} %copy-done.13, ...), kind=kLoop, calls=%fused_computation.14 | loop fusion | flops 29360128 | bytes 20987904 | tf_op jit(solution)/shard_map/mul | solution.py:808
  476.4 3.3 collective-permute-done.67.refs_1_
  479.8 4.4 collective-permute-done.68.refs_2_
  490.9 20.1 %collective-permute-done.71 = bf16[512,512]{1,0:T(8,128)(2,1)S(1)} collective-permute-done((bf16[512,512]{1,0:T(8,128)(2,1)S(1)}, bf16[512,512]{1,0:T(8,128)(2,1)S(1)}, u32[]{:S(2)}, u32[]{:S(2)}) %collective-permute-start.71) | collective-permute-done | bytes 524320 | tf_op jit(solution)/shard_map/ppermute | solution.py:446
  517.1 2.5 place_quarters.15.refs_0_
  519.5 3.8 place_quarters.16
  523.3 12.9 %collective-permute-done.70 = bf16[512,512]{1,0:T(8,128)(2,1)S(1)} collective-permute-done((bf16[512,512]{1,0:T(8,128)(2,1)S(1)}, bf16[512,512]{1,0:T(8,128)(2,1)S(1)}, u32[]{:S(2)}, u32[]{:S(2)}) %collective-permute-start.70) | collective-permute-done | bytes 524320 | tf_op jit(solution)/shard_map/ppermute | solution.py:446
  543.1 15.2 %collective-permute-done.81 = bf16[512,384]{1,0:T(8,128)(2,1)S(1)} collective-permute-done((bf16[512,384]{1,0:T(8,128)(2,1)S(1)}, bf16[512,384]{1,0:T(8,128)(2,1)S(1)}, u32[]{:S(2)}, u32[]{:S(2)}) %collective-permute-start.81) | collective-permute-done | bytes 393248 | tf_op jit(solution)/shard_map/ppermute | solution.py:446
  561.7 2.5 place_quarters.17.refs_0_
  564.2 3.4 collective-permute-start.86
  571.0 2.5 place_quarters.19.refs_0_
  573.4 2.4 place_quarters.20.refs_0_
  575.9 8.5 %collective-permute-done.86 = bf16[512,384]{1,0:T(8,128)(2,1)S(1)} collective-permute-done((bf16[512,384]{1,0:T(8,128)(2,1)S(1)}, bf16[512,384]{1,0:T(8,128)(2,1)S(1)}, u32[]{:S(2)}, u32[]{:S(2)}) %collective-permute-start.86) | collective-permute-done | bytes 393248 | tf_op jit(solution)/shard_map/ppermute | solution.py:446
  584.3 5.1 collective-permute-done.90
  593.8 3.7 place_quarters.21
  597.4 2.4 place_quarters.22.refs_0_
  600.7 5.7 collective-permute-done.95
  614.1 2.4 place_quarters.23
  620.8 3.6 collective-permute-done.99.refs_4_
  632.4 5.6 collective-permute-done.103.refs_2_
  642.9 3.2 collective-permute-done.106.refs_2_
  (517 shorter events, 186.1 us)
Async XLA Ops:
  1.2 47.3 %collective-permute-start.3 = (bf16[256,2048]{1,0:T(8,128)(2,1)}, bf16[256,2048]{1,0:T(8,128)(2,1)}, u32[]{:S(2)}, u32[]{:S(2)}) collective-permute-start(bf16[256,2048]{1,0:T(8,128)(2,1)} %refs_4_.1), channel_id=1, source_target_pairs={{0,4},{4,0},{8,12},{12,8},{16,20},{20,16},{24,28},{28,24},{1,5},{5... | collective-permute-start | bytes 3145736 | tf_op jit(solution)/shard_map/ppermute | solution.py:446
  3.7 44.8 %collective-permute-start.4 = (bf16[256,2048]{1,0:T(8,128)(2,1)}, bf16[256,2048]{1,0:T(8,128)(2,1)}, u32[]{:S(2)}, u32[]{:S(2)}) collective-permute-start(bf16[256,2048]{1,0:T(8,128)(2,1)} %refs_4_.1), channel_id=1, source_target_pairs={{0,8},{4,12},{8,0},{12,4},{16,24},{20,28},{24,16},{28,20},{1,9},{5... | collective-permute-start | bytes 3145736 | tf_op jit(solution)/shard_map/ppermute | solution.py:446
  5.3 43.2 %collective-permute-start.5 = (bf16[256,2048]{1,0:T(8,128)(2,1)}, bf16[256,2048]{1,0:T(8,128)(2,1)}, u32[]{:S(2)}, u32[]{:S(2)}) collective-permute-start(bf16[256,2048]{1,0:T(8,128)(2,1)} %refs_4_.1), channel_id=1, source_target_pairs={{0,2},{1,3},{2,0},{3,1},{4,6},{5,7},{6,4},{7,5},{8,10},{9,11},{10,... | collective-permute-start | bytes 3145736 | tf_op jit(solution)/shard_map/ppermute | solution.py:439
  17.3 20.0 %collective-permute-start.1 = (f32[8,128]{1,0:T(8,128)S(1)}, f32[8,128]{1,0:T(8,128)S(1)}, u32[]{:S(2)}, u32[]{:S(2)}) collective-permute-start(f32[8,128]{1,0:T(8,128)S(1)} %broadcast_in_dim.61), channel_id=1, source_target_pairs={{0,1},{1,0},{2,3},{3,2},{4,5},{5,4},{6,7},{7,6},{8,9},{9,8},{10,11... | collective-permute-start | bytes 12296 | tf_op jit(solution)/shard_map/ppermute | solution.py:435
  49.5 33.7 %collective-permute-start.8 = (bf16[256,2048]{1,0:T(8,128)(2,1)}, bf16[256,2048]{1,0:T(8,128)(2,1)}, u32[]{:S(2)}, u32[]{:S(2)}) collective-permute-start(bf16[256,2048]{1,0:T(8,128)(2,1)} %collective-permute-done.4.refs_8_), channel_id=1, source_target_pairs={{0,4},{4,0},{8,12},{12,8},{16,20},{20,16},{24,28},{28,24},{1,5},{5... | collective-permute-start | bytes 3145736 | tf_op jit(solution)/shard_map/ppermute | solution.py:446
  52.1 44.2 %collective-permute-start.10 = (bf16[256,2048]{1,0:T(8,128)(2,1)}, bf16[256,2048]{1,0:T(8,128)(2,1)}, u32[]{:S(2)}, u32[]{:S(2)}) collective-permute-start(bf16[256,2048]{1,0:T(8,128)(2,1)} %collective-permute-done.5.refs_4_), channel_id=1, source_target_pairs={{0,8},{4,12},{8,0},{12,4},{16,24},{20,28},{24,16},{28,20},{1,9},{5... | collective-permute-start | bytes 3145736 | tf_op jit(solution)/shard_map/ppermute | solution.py:446
  53.3 29.7 %collective-permute-start.7 = (f32[8,128]{1,0:T(8,128)S(1)}, f32[8,128]{1,0:T(8,128)S(1)}, u32[]{:S(2)}, u32[]{:S(2)}) collective-permute-start(f32[8,128]{1,0:T(8,128)S(1)} %fusion.98), channel_id=1, source_target_pairs={{0,8},{4,12},{8,0},{12,4},{16,24},{20,28},{24,16},{28,20},{1,9},{5... | collective-permute-start | bytes 12296 | tf_op jit(solution)/shard_map/ppermute | solution.py:446
  54.9 41.3 %collective-permute-start.9 = (bf16[256,2048]{1,0:T(8,128)(2,1)}, bf16[256,2048]{1,0:T(8,128)(2,1)S(1)}, u32[]{:S(2)}, u32[]{:S(2)}) collective-permute-start(bf16[256,2048]{1,0:T(8,128)(2,1)} %collective-permute-done.3.refs_4_), channel_id=1, source_target_pairs={{0,2},{1,3},{2,0},{3,1},{4,6},{5,7},{6,4},{7,5},{8,10},{9,11},{10,... | collective-permute-start | bytes 3145736 | tf_op jit(solution)/shard_map/ppermute | solution.py:439
  96.2 34.1 %collective-permute-start.19 = (bf16[256,2048]{1,0:T(8,128)(2,1)}, bf16[256,2048]{1,0:T(8,128)(2,1)S(1)}, u32[]{:S(2)}, u32[]{:S(2)}) collective-permute-start(bf16[256,2048]{1,0:T(8,128)(2,1)} %collective-permute-done.3.refs_4_), channel_id=1, source_target_pairs={{0,1},{1,0},{2,3},{3,2},{4,5},{5,4},{6,7},{7,6},{8,9},{9,8},{10,11... | collective-permute-start | bytes 3145736 | tf_op jit(solution)/shard_map/ppermute | solution.py:435
  96.3 35.3 %collective-permute-start.21 = (bf16[256,2048]{1,0:T(8,128)(2,1)}, bf16[256,2048]{1,0:T(8,128)(2,1)S(1)}, u32[]{:S(2)}, u32[]{:S(2)}) collective-permute-start(bf16[256,2048]{1,0:T(8,128)(2,1)} %collective-permute-done.4.refs_8_), channel_id=1, source_target_pairs={{0,1},{1,0},{2,3},{3,2},{4,5},{5,4},{6,7},{7,6},{8,9},{9,8},{10,11... | collective-permute-start | bytes 3145736 | tf_op jit(solution)/shard_map/ppermute | solution.py:435
  103.8 24.8 %collective-permute-start.14 = (bf16[1,256,2048]{2,1,0:T(8,128)(2,1)S(1)}, bf16[1,256,2048]{2,1,0:T(8,128)(2,1)S(1)}, u32[]{:S(2)}, u32[]{:S(2)}) collective-permute-start(bf16[1,256,2048]{2,1,0:T(8,128)(2,1)S(1)} %fusion.42), channel_id=1, source_target_pairs={{0,1},{1,0},{2,3},{3,2},{4,5},{5,4},{6,7},{7,6},{8,9},{9,8},{10,11... | collective-permute-start | bytes 3145736 | tf_op jit(solution)/shard_map/ppermute | solution.py:435
  131.7 38.1 %collective-permute-start.16 = (bf16[256,2048]{1,0:T(8,128)(2,1)}, bf16[256,2048]{1,0:T(8,128)(2,1)}, u32[]{:S(2)}, u32[]{:S(2)}) collective-permute-start(bf16[256,2048]{1,0:T(8,128)(2,1)} %fusion.43), channel_id=1, source_target_pairs={{0,2},{1,3},{2,0},{3,1},{4,6},{5,7},{6,4},{7,5},{8,10},{9,11},{10,... | collective-permute-start | bytes 3145736 | tf_op jit(solution)/shard_map/ppermute | solution.py:443
  134.2 35.5 %collective-permute-start.17 = (bf16[256,2048]{1,0:T(8,128)(2,1)}, bf16[256,2048]{1,0:T(8,128)(2,1)}, u32[]{:S(2)}, u32[]{:S(2)}) collective-permute-start(bf16[256,2048]{1,0:T(8,128)(2,1)} %fusion.44), channel_id=1, source_target_pairs={{0,1},{1,0},{2,3},{3,2},{4,5},{5,4},{6,7},{7,6},{8,9},{9,8},{10,11... | collective-permute-start | bytes 3145736 | tf_op jit(solution)/shard_map/ppermute | solution.py:435
  135.1 34.6 %collective-permute-start.18 = (f32[8,128]{1,0:T(8,128)S(1)}, f32[8,128]{1,0:T(8,128)S(1)}, u32[]{:S(2)}, u32[]{:S(2)}) collective-permute-start(f32[8,128]{1,0:T(8,128)S(1)} %add.317), channel_id=1, source_target_pairs={{0,16},{4,20},{8,24},{12,28},{16,0},{20,4},{24,8},{28,12},{1,17},{... | collective-permute-start | bytes 12296 | tf_op jit(solution)/shard_map/ppermute | solution.py:446
  176.4 25.3 %collective-permute-start.27 = (bf16[256,2048]{1,0:T(8,128)(2,1)S(1)}, bf16[256,2048]{1,0:T(8,128)(2,1)}, u32[]{:S(2)}, u32[]{:S(2)}) collective-permute-start(bf16[256,2048]{1,0:T(8,128)(2,1)S(1)} %get-tuple-element.236), channel_id=1, source_target_pairs={{0,2},{1,3},{2,0},{3,1},{4,6},{5,7},{6,4},{7,5},{8,10},{9,11},{10,... | collective-permute-start | bytes 3145736 | tf_op jit(solution)/shard_map/ppermute | solution.py:439
  177.0 24.9 %collective-permute-start.28 = (bf16[256,2048]{1,0:T(8,128)(2,1)S(1)}, bf16[256,2048]{1,0:T(8,128)(2,1)S(1)}, u32[]{:S(2)}, u32[]{:S(2)}) collective-permute-start(bf16[256,2048]{1,0:T(8,128)(2,1)S(1)} %get-tuple-element.236), channel_id=1, source_target_pairs={{0,4},{4,0},{8,12},{12,8},{16,20},{20,16},{24,28},{28,24},{1,5},{5... | collective-permute-start | bytes 3145736 | tf_op jit(solution)/shard_map/ppermute | solution.py:446
  177.8 24.6 %collective-permute-start.29 = (bf16[256,2048]{1,0:T(8,128)(2,1)S(1)}, bf16[256,2048]{1,0:T(8,128)(2,1)S(1)}, u32[]{:S(2)}, u32[]{:S(2)}) collective-permute-start(bf16[256,2048]{1,0:T(8,128)(2,1)S(1)} %get-tuple-element.236), channel_id=1, source_target_pairs={{0,8},{4,12},{8,0},{12,4},{16,24},{20,28},{24,16},{28,20},{1,9},{5... | collective-permute-start | bytes 3145736 | tf_op jit(solution)/shard_map/ppermute | solution.py:446
  178.9 23.5 %collective-permute-start.30 = (bf16[256,2048]{1,0:T(8,128)(2,1)S(1)}, bf16[256,2048]{1,0:T(8,128)(2,1)S(1)}, u32[]{:S(2)}, u32[]{:S(2)}) collective-permute-start(bf16[256,2048]{1,0:T(8,128)(2,1)S(1)} %get-tuple-element.236), channel_id=1, source_target_pairs={{0,1},{1,0},{2,3},{3,2},{4,5},{5,4},{6,7},{7,6},{8,9},{9,8},{10,11... | collective-permute-start | bytes 3145736 | tf_op jit(solution)/shard_map/ppermute | solution.py:435
  202.5 28.4 %collective-permute-start.34 = (bf16[256,2048]{1,0:T(8,128)(2,1)}, bf16[256,2048]{1,0:T(8,128)(2,1)S(1)}, u32[]{:S(2)}, u32[]{:S(2)}) collective-permute-start(bf16[256,2048]{1,0:T(8,128)(2,1)} %collective-permute-done.27), channel_id=1, source_target_pairs={{0,8},{4,12},{8,0},{12,4},{16,24},{20,28},{24,16},{28,20},{1,9},{5... | collective-permute-start | bytes 3145736 | tf_op jit(solution)/shard_map/ppermute | solution.py:446
  203.6 27.2 %collective-permute-start.33 = (bf16[256,2048]{1,0:T(8,128)(2,1)S(1)}, bf16[256,2048]{1,0:T(8,128)(2,1)S(1)}, u32[]{:S(2)}, u32[]{:S(2)}) collective-permute-start(bf16[256,2048]{1,0:T(8,128)(2,1)S(1)} %collective-permute-done.28.refs_4_.refs_8_.refs_0_), channel_id=1, source_target_pairs={{0,2},{1,3},{2,0},{3,1},{4,6},{5,7},{6,4},{7,5},{8,10},{9,11},{10,... | collective-permute-start | bytes 3145736 | tf_op jit(solution)/shard_map/ppermute | solution.py:439
  205.1 27.3 %collective-permute-start.37 = (bf16[256,2048]{1,0:T(8,128)(2,1)S(1)}, bf16[256,2048]{1,0:T(8,128)(2,1)}, u32[]{:S(2)}, u32[]{:S(2)}) collective-permute-start(bf16[256,2048]{1,0:T(8,128)(2,1)S(1)} %collective-permute-done.28.refs_4_.refs_8_.refs_0_), channel_id=1, source_target_pairs={{0,1},{1,0},{2,3},{3,2},{4,5},{5,4},{6,7},{7,6},{8,9},{9,8},{10,11... | collective-permute-start | bytes 3145736 | tf_op jit(solution)/shard_map/ppermute | solution.py:435
  205.1 25.7 %collective-permute-start.32 = (bf16[256,2048]{1,0:T(8,128)(2,1)S(1)}, bf16[256,2048]{1,0:T(8,128)(2,1)}, u32[]{:S(2)}, u32[]{:S(2)}) collective-permute-start(bf16[256,2048]{1,0:T(8,128)(2,1)S(1)} %collective-permute-done.29.refs_8_.refs_12_.refs_4_), channel_id=1, source_target_pairs={{0,4},{4,0},{8,12},{12,8},{16,20},{20,16},{24,28},{28,24},{1,5},{5... | collective-permute-start | bytes 3145736 | tf_op jit(solution)/shard_map/ppermute | solution.py:446
  207.0 25.9 %collective-permute-start.39 = (bf16[256,2048]{1,0:T(8,128)(2,1)S(1)}, bf16[256,2048]{1,0:T(8,128)(2,1)}, u32[]{:S(2)}, u32[]{:S(2)}) collective-permute-start(bf16[256,2048]{1,0:T(8,128)(2,1)S(1)} %collective-permute-done.29.refs_8_.refs_12_.refs_4_), channel_id=1, source_target_pairs={{0,1},{1,0},{2,3},{3,2},{4,5},{5,4},{6,7},{7,6},{8,9},{9,8},{10,11... | collective-permute-start | bytes 3145736 | tf_op jit(solution)/shard_map/ppermute | solution.py:435
  265.3 38.6 %collective-permute-start.47 = (bf16[128,2048]{1,0:T(8,128)(2,1)}, bf16[128,2048]{1,0:T(8,128)(2,1)}, u32[]{:S(2)}, u32[]{:S(2)}) collective-permute-start(bf16[128,2048]{1,0:T(8,128)(2,1)} %get-tuple-element.259), channel_id=1, source_target_pairs={{0,16},{4,20},{8,24},{12,28},{16,0},{20,4},{24,8},{28,12},{1,17},{... | collective-permute-start | bytes 1572872 | tf_op jit(solution)/shard_map/ppermute | solution.py:446
  278.5 36.1 %collective-permute-start.46 = (bf16[128,2048]{1,0:T(8,128)(2,1)S(1)}, bf16[128,2048]{1,0:T(8,128)(2,1)}, u32[]{:S(2)}, u32[]{:S(2)}) collective-permute-start(bf16[128,2048]{1,0:T(8,128)(2,1)S(1)} %copy-done.91), channel_id=1, source_target_pairs={{0,16},{4,20},{8,24},{12,28},{16,0},{20,4},{24,8},{28,12},{1,17},{... | collective-permute-start | bytes 1572872 | tf_op jit(solution)/shard_map/ppermute | solution.py:446
  282.4 44.1 %collective-permute-start.43 = (bf16[1024,384]{1,0:T(8,128)(2,1)}, bf16[1024,384]{1,0:T(8,128)(2,1)}, u32[]{:S(2)}, u32[]{:S(2)}) collective-permute-start(bf16[1024,384]{1,0:T(8,128)(2,1)} %get-tuple-element.417), channel_id=1, source_target_pairs={{0,4},{4,0},{8,12},{12,8},{16,20},{20,16},{24,28},{28,24},{1,5},{5... | collective-permute-start | bytes 2359304 | tf_op jit(solution)/shard_map/ppermute | solution.py:446
  283.9 44.5 %collective-permute-start.44 = (bf16[1024,384]{1,0:T(8,128)(2,1)}, bf16[1024,384]{1,0:T(8,128)(2,1)}, u32[]{:S(2)}, u32[]{:S(2)}) collective-permute-start(bf16[1024,384]{1,0:T(8,128)(2,1)} %get-tuple-element.416), channel_id=1, source_target_pairs={{0,8},{4,12},{8,0},{12,4},{16,24},{20,28},{24,16},{28,20},{1,9},{5... | collective-permute-start | bytes 2359304 | tf_op jit(solution)/shard_map/ppermute | solution.py:446
  284.9 66.4 %collective-permute-start.45 = (bf16[1024,384]{1,0:T(8,128)(2,1)}, bf16[1024,384]{1,0:T(8,128)(2,1)}, u32[]{:S(2)}, u32[]{:S(2)}) collective-permute-start(bf16[1024,384]{1,0:T(8,128)(2,1)} %get-tuple-element.415), channel_id=1, source_target_pairs={{0,12},{4,8},{8,4},{12,0},{16,28},{20,24},{24,20},{28,16},{1,13},{... | collective-permute-start | bytes 2359304 | tf_op jit(solution)/shard_map/ppermute | solution.py:446
  305.2 46.0 %collective-permute-start.48 = (bf16[128,2048]{1,0:T(8,128)(2,1)S(1)}, bf16[128,2048]{1,0:T(8,128)(2,1)S(1)}, u32[]{:S(2)}, u32[]{:S(2)}) collective-permute-start(bf16[128,2048]{1,0:T(8,128)(2,1)S(1)} %add_convert_fusion.10.refs_0_), channel_id=1, source_target_pairs={{0,4},{4,0},{8,12},{12,8},{16,20},{20,16},{24,28},{28,24},{1,5},{5... | collective-permute-start | bytes 1572872 | tf_op jit(solution)/shard_map/ppermute | solution.py:446
  314.7 47.7 %collective-permute-start.49 = (bf16[128,2048]{1,0:T(8,128)(2,1)S(1)}, bf16[128,2048]{1,0:T(8,128)(2,1)S(1)}, u32[]{:S(2)}, u32[]{:S(2)}) collective-permute-start(bf16[128,2048]{1,0:T(8,128)(2,1)S(1)} %add_convert_fusion.10.refs_0_), channel_id=1, source_target_pairs={{0,8},{4,12},{8,0},{12,4},{16,24},{20,28},{24,16},{28,20},{1,9},{5... | collective-permute-start | bytes 1572872 | tf_op jit(solution)/shard_map/ppermute | solution.py:446
  326.5 56.6 %collective-permute-start.51 = (bf16[128,2048]{1,0:T(8,128)(2,1)S(1)}, bf16[128,2048]{1,0:T(8,128)(2,1)S(1)}, u32[]{:S(2)}, u32[]{:S(2)}) collective-permute-start(bf16[128,2048]{1,0:T(8,128)(2,1)S(1)} %copy-done.90), channel_id=1, source_target_pairs={{0,16},{4,20},{8,24},{12,28},{16,0},{20,4},{24,8},{28,12},{1,17},{... | collective-permute-start | bytes 1572872 | tf_op jit(solution)/shard_map/ppermute | solution.py:446
  363.8 19.3 %collective-permute-start.52 = (bf16[128,2048]{1,0:T(8,128)(2,1)S(1)}, bf16[128,2048]{1,0:T(8,128)(2,1)S(1)}, u32[]{:S(2)}, u32[]{:S(2)}) collective-permute-start(bf16[128,2048]{1,0:T(8,128)(2,1)S(1)} %add_convert_fusion.9.refs_1_), channel_id=1, source_target_pairs={{0,4},{4,0},{8,12},{12,8},{16,20},{20,16},{24,28},{28,24},{1,5},{5... | collective-permute-start | bytes 1572872 | tf_op jit(solution)/shard_map/ppermute | solution.py:446
  365.1 18.0 %collective-permute-start.53 = (bf16[128,2048]{1,0:T(8,128)(2,1)S(1)}, bf16[128,2048]{1,0:T(8,128)(2,1)S(1)}, u32[]{:S(2)}, u32[]{:S(2)}) collective-permute-start(bf16[128,2048]{1,0:T(8,128)(2,1)S(1)} %add_convert_fusion.9.refs_1_), channel_id=1, source_target_pairs={{0,8},{4,12},{8,0},{12,4},{16,24},{20,28},{24,16},{28,20},{1,9},{5... | collective-permute-start | bytes 1572872 | tf_op jit(solution)/shard_map/ppermute | solution.py:446
  368.8 18.9 %collective-permute-start.54 = (bf16[128,2048]{1,0:T(8,128)(2,1)S(1)}, bf16[128,2048]{1,0:T(8,128)(2,1)S(1)}, u32[]{:S(2)}, u32[]{:S(2)}) collective-permute-start(bf16[128,2048]{1,0:T(8,128)(2,1)S(1)} %collective-permute-done.49.refs_2_), channel_id=1, source_target_pairs={{0,4},{4,0},{8,12},{12,8},{16,20},{20,16},{24,28},{28,24},{1,5},{5... | collective-permute-start | bytes 1572872 | tf_op jit(solution)/shard_map/ppermute | solution.py:446
  369.8 27.5 %collective-permute-start.50 = (bf16[128,2048]{1,0:T(8,128)(2,1)S(1)}, bf16[128,2048]{1,0:T(8,128)(2,1)}, u32[]{:S(2)}, u32[]{:S(2)}) collective-permute-start(bf16[128,2048]{1,0:T(8,128)(2,1)S(1)} %copy-done.89), channel_id=1, source_target_pairs={{0,16},{4,20},{8,24},{12,28},{16,0},{20,4},{24,8},{28,12},{1,17},{... | collective-permute-start | bytes 1572872 | tf_op jit(solution)/shard_map/ppermute | solution.py:446
  389.1 20.3 %collective-permute-start.56 = (bf16[128,2048]{1,0:T(8,128)(2,1)S(1)}, bf16[128,2048]{1,0:T(8,128)(2,1)S(1)}, u32[]{:S(2)}, u32[]{:S(2)}) collective-permute-start(bf16[128,2048]{1,0:T(8,128)(2,1)S(1)} %add_convert_fusion.8.refs_1_), channel_id=1, source_target_pairs={{0,8},{4,12},{8,0},{12,4},{16,24},{20,28},{24,16},{28,20},{1,9},{5... | collective-permute-start | bytes 1572872 | tf_op jit(solution)/shard_map/ppermute | solution.py:446
  389.1 41.9 %collective-permute-start.59 = (bf16[128,2048]{1,0:T(8,128)(2,1)S(1)}, bf16[128,2048]{1,0:T(8,128)(2,1)S(1)}, u32[]{:S(2)}, u32[]{:S(2)}) collective-permute-start(bf16[128,2048]{1,0:T(8,128)(2,1)S(1)} %copy-done.88), channel_id=1, source_target_pairs={{0,16},{4,20},{8,24},{12,28},{16,0},{20,4},{24,8},{28,12},{1,17},{... | collective-permute-start | bytes 1572872 | tf_op jit(solution)/shard_map/ppermute | solution.py:446
  389.1 21.7 %collective-permute-start.57 = (bf16[128,2048]{1,0:T(8,128)(2,1)S(1)}, bf16[128,2048]{1,0:T(8,128)(2,1)S(1)}, u32[]{:S(2)}, u32[]{:S(2)}) collective-permute-start(bf16[128,2048]{1,0:T(8,128)(2,1)S(1)} %collective-permute-done.53.refs_3_), channel_id=1, source_target_pairs={{0,4},{4,0},{8,12},{12,8},{16,20},{20,16},{24,28},{28,24},{1,5},{5... | collective-permute-start | bytes 1572872 | tf_op jit(solution)/shard_map/ppermute | solution.py:446
  412.3 18.8 %collective-permute-start.60 = (bf16[128,2048]{1,0:T(8,128)(2,1)S(1)}, bf16[128,2048]{1,0:T(8,128)(2,1)S(1)}, u32[]{:S(2)}, u32[]{:S(2)}) collective-permute-start(bf16[128,2048]{1,0:T(8,128)(2,1)S(1)} %add_convert_fusion.7.refs_1_), channel_id=1, source_target_pairs={{0,4},{4,0},{8,12},{12,8},{16,20},{20,16},{24,28},{28,24},{1,5},{5... | collective-permute-start | bytes 1572872 | tf_op jit(solution)/shard_map/ppermute | solution.py:446
  413.6 22.6 %collective-permute-start.62 = (bf16[128,2048]{1,0:T(8,128)(2,1)S(1)}, bf16[128,2048]{1,0:T(8,128)(2,1)S(1)}, u32[]{:S(2)}, u32[]{:S(2)}) collective-permute-start(bf16[128,2048]{1,0:T(8,128)(2,1)S(1)} %collective-permute-done.56.refs_3_), channel_id=1, source_target_pairs={{0,4},{4,0},{8,12},{12,8},{16,20},{20,16},{24,28},{28,24},{1,5},{5... | collective-permute-start | bytes 1572872 | tf_op jit(solution)/shard_map/ppermute | solution.py:446
  429.3 34.2 %collective-permute-start.58 = (bf16[512,512]{1,0:T(8,128)(2,1)}, bf16[512,512]{1,0:T(8,128)(2,1)}, u32[]{:S(2)}, u32[]{:S(2)}) collective-permute-start(bf16[512,512]{1,0:T(8,128)(2,1)} %get-tuple-element.290), channel_id=1, source_target_pairs={{0,16},{4,20},{8,24},{12,28},{16,0},{20,4},{24,8},{28,12},{1,17},{... | collective-permute-start | bytes 1572872 | tf_op jit(solution)/shard_map/ppermute | solution.py:446
  437.1 26.4 %collective-permute-start.63 = (bf16[128,2048]{1,0:T(8,128)(2,1)}, bf16[128,2048]{1,0:T(8,128)(2,1)}, u32[]{:S(2)}, u32[]{:S(2)}) collective-permute-start(bf16[128,2048]{1,0:T(8,128)(2,1)} %add_convert_fusion.6.refs_0_), channel_id=1, source_target_pairs={{0,4},{4,0},{8,12},{12,8},{16,20},{20,16},{24,28},{28,24},{1,5},{5... | collective-permute-start | bytes 1572872 | tf_op jit(solution)/shard_map/ppermute | solution.py:446
  438.4 25.1 %collective-permute-start.64 = (bf16[128,2048]{1,0:T(8,128)(2,1)}, bf16[128,2048]{1,0:T(8,128)(2,1)}, u32[]{:S(2)}, u32[]{:S(2)}) collective-permute-start(bf16[128,2048]{1,0:T(8,128)(2,1)} %add_convert_fusion.6.refs_0_), channel_id=1, source_target_pairs={{0,8},{4,12},{8,0},{12,4},{16,24},{20,28},{24,16},{28,20},{1,9},{5... | collective-permute-start | bytes 1572872 | tf_op jit(solution)/shard_map/ppermute | solution.py:446
  438.4 38.0 %collective-permute-start.66 = (bf16[512,512]{1,0:T(8,128)(2,1)}, bf16[512,512]{1,0:T(8,128)(2,1)}, u32[]{:S(2)}, u32[]{:S(2)}) collective-permute-start(bf16[512,512]{1,0:T(8,128)(2,1)} %get-tuple-element.305), channel_id=1, source_target_pairs={{0,16},{4,20},{8,24},{12,28},{16,0},{20,4},{24,8},{28,12},{1,17},{... | collective-permute-start | bytes 1572872 | tf_op jit(solution)/shard_map/ppermute | solution.py:446
  439.7 23.8 %collective-permute-start.65 = (bf16[128,2048]{1,0:T(8,128)(2,1)}, bf16[128,2048]{1,0:T(8,128)(2,1)}, u32[]{:S(2)}, u32[]{:S(2)}) collective-permute-start(bf16[128,2048]{1,0:T(8,128)(2,1)} %collective-permute-done.61.refs_3_), channel_id=1, source_target_pairs={{0,4},{4,0},{8,12},{12,8},{16,20},{20,16},{24,28},{28,24},{1,5},{5... | collective-permute-start | bytes 1572872 | tf_op jit(solution)/shard_map/ppermute | solution.py:446
  466.3 19.1 %collective-permute-start.69 = (bf16[128,2048]{1,0:T(8,128)(2,1)}, bf16[128,2048]{1,0:T(8,128)(2,1)S(1)}, u32[]{:S(2)}, u32[]{:S(2)}) collective-permute-start(bf16[128,2048]{1,0:T(8,128)(2,1)} %collective-permute-done.64.refs_2_), channel_id=1, source_target_pairs={{0,4},{4,0},{8,12},{12,8},{16,20},{20,16},{24,28},{28,24},{1,5},{5... | collective-permute-start | bytes 1572872 | tf_op jit(solution)/shard_map/ppermute | solution.py:446
  485.4 27.4 %collective-permute-start.75 = (bf16[2,256,2048]{2,1,0:T(8,128)(2,1)S(1)}, bf16[2,256,2048]{2,1,0:T(8,128)(2,1)S(1)}, u32[]{:S(2)}, u32[]{:S(2)}) collective-permute-start(bf16[2,256,2048]{2,1,0:T(8,128)(2,1)S(1)} %fusion.31), channel_id=1, source_target_pairs={{0,1},{1,0},{2,3},{3,2},{4,5},{5,4},{6,7},{7,6},{8,9},{9,8},{10,11... | collective-permute-start | bytes 6291464 | tf_op jit(solution)/shard_map/ppermute | solution.py:435
  485.5 25.5 %collective-permute-start.71 = (bf16[512,512]{1,0:T(8,128)(2,1)S(1)}, bf16[512,512]{1,0:T(8,128)(2,1)S(1)}, u32[]{:S(2)}, u32[]{:S(2)}) collective-permute-start(bf16[512,512]{1,0:T(8,128)(2,1)S(1)} %copy-done.85), channel_id=1, source_target_pairs={{0,16},{4,20},{8,24},{12,28},{16,0},{20,4},{24,8},{28,12},{1,17},{... | collective-permute-start | bytes 1572872 | tf_op jit(solution)/shard_map/ppermute | solution.py:446
  487.0 24.0 %collective-permute-start.72 = (bf16[512,512]{1,0:T(8,128)(2,1)S(1)}, bf16[512,512]{1,0:T(8,128)(2,1)S(1)}, u32[]{:S(2)}, u32[]{:S(2)}) collective-permute-start(bf16[512,512]{1,0:T(8,128)(2,1)S(1)} %add_convert_fusion.4.refs_1_), channel_id=1, source_target_pairs={{0,4},{4,0},{8,12},{12,8},{16,20},{20,16},{24,28},{28,24},{1,5},{5... | collective-permute-start | bytes 1572872 | tf_op jit(solution)/shard_map/ppermute | solution.py:446
  487.5 25.2 %collective-permute-start.73 = (bf16[512,512]{1,0:T(8,128)(2,1)S(1)}, bf16[512,512]{1,0:T(8,128)(2,1)S(1)}, u32[]{:S(2)}, u32[]{:S(2)}) collective-permute-start(bf16[512,512]{1,0:T(8,128)(2,1)S(1)} %add_convert_fusion.4.refs_1_), channel_id=1, source_target_pairs={{0,8},{4,12},{8,0},{12,4},{16,24},{20,28},{24,16},{28,20},{1,9},{5... | collective-permute-start | bytes 1572872 | tf_op jit(solution)/shard_map/ppermute | solution.py:446
  488.6 24.2 %collective-permute-start.74 = (bf16[512,512]{1,0:T(8,128)(2,1)S(1)}, bf16[512,512]{1,0:T(8,128)(2,1)S(1)}, u32[]{:S(2)}, u32[]{:S(2)}) collective-permute-start(bf16[512,512]{1,0:T(8,128)(2,1)S(1)} %collective-permute-done.68.refs_2_), channel_id=1, source_target_pairs={{0,4},{4,0},{8,12},{12,8},{16,20},{20,16},{24,28},{28,24},{1,5},{5... | collective-permute-start | bytes 1572872 | tf_op jit(solution)/shard_map/ppermute | solution.py:446
  511.0 25.2 %collective-permute-start.70 = (bf16[512,512]{1,0:T(8,128)(2,1)S(1)}, bf16[512,512]{1,0:T(8,128)(2,1)S(1)}, u32[]{:S(2)}, u32[]{:S(2)}) collective-permute-start(bf16[512,512]{1,0:T(8,128)(2,1)S(1)} %copy-done.84), channel_id=1, source_target_pairs={{0,16},{4,20},{8,24},{12,28},{16,0},{20,4},{24,8},{28,12},{1,17},{... | collective-permute-start | bytes 1572872 | tf_op jit(solution)/shard_map/ppermute | solution.py:446
  512.9 23.3 %collective-permute-start.76 = (bf16[512,512]{1,0:T(8,128)(2,1)S(1)}, bf16[512,512]{1,0:T(8,128)(2,1)S(1)}, u32[]{:S(2)}, u32[]{:S(2)}) collective-permute-start(bf16[512,512]{1,0:T(8,128)(2,1)S(1)} %add_convert_fusion.3.refs_1_), channel_id=1, source_target_pairs={{0,4},{4,0},{8,12},{12,8},{16,20},{20,16},{24,28},{28,24},{1,5},{5... | collective-permute-start | bytes 1572872 | tf_op jit(solution)/shard_map/ppermute | solution.py:446
  514.5 24.1 %collective-permute-start.77 = (bf16[512,512]{1,0:T(8,128)(2,1)S(1)}, bf16[512,512]{1,0:T(8,128)(2,1)S(1)}, u32[]{:S(2)}, u32[]{:S(2)}) collective-permute-start(bf16[512,512]{1,0:T(8,128)(2,1)S(1)} %add_convert_fusion.3.refs_1_), channel_id=1, source_target_pairs={{0,8},{4,12},{8,0},{12,4},{16,24},{20,28},{24,16},{28,20},{1,9},{5... | collective-permute-start | bytes 1572872 | tf_op jit(solution)/shard_map/ppermute | solution.py:446
  514.5 24.1 %collective-permute-start.78 = (bf16[512,512]{1,0:T(8,128)(2,1)S(1)}, bf16[512,512]{1,0:T(8,128)(2,1)S(1)}, u32[]{:S(2)}, u32[]{:S(2)}) collective-permute-start(bf16[512,512]{1,0:T(8,128)(2,1)S(1)} %collective-permute-done.73.refs_3_), channel_id=1, source_target_pairs={{0,4},{4,0},{8,12},{12,8},{16,20},{20,16},{24,28},{28,24},{1,5},{5... | collective-permute-start | bytes 1572872 | tf_op jit(solution)/shard_map/ppermute | solution.py:446
  516.3 51.3 %collective-permute-start.80 = (bf16[256,2048]{1,0:T(8,128)(2,1)S(1)}, bf16[256,2048]{1,0:T(8,128)(2,1)S(1)}, u32[]{:S(2)}, u32[]{:S(2)}) collective-permute-start(bf16[256,2048]{1,0:T(8,128)(2,1)S(1)} %fusion.45), channel_id=1, source_target_pairs={{0,2},{1,3},{2,0},{3,1},{4,6},{5,7},{6,4},{7,5},{8,10},{9,11},{10,... | collective-permute-start | bytes 3145736 | tf_op jit(solution)/shard_map/ppermute | solution.py:443
  538.8 28.8 %collective-permute-start.82 = (bf16[512,512]{1,0:T(8,128)(2,1)S(1)}, bf16[512,512]{1,0:T(8,128)(2,1)S(1)}, u32[]{:S(2)}, u32[]{:S(2)}) collective-permute-start(bf16[512,512]{1,0:T(8,128)(2,1)S(1)} %add_convert_fusion.2.refs_1_), channel_id=1, source_target_pairs={{0,4},{4,0},{8,12},{12,8},{16,20},{20,16},{24,28},{28,24},{1,5},{5... | collective-permute-start | bytes 1572872 | tf_op jit(solution)/shard_map/ppermute | solution.py:446
  539.5 28.1 %collective-permute-start.83 = (bf16[512,512]{1,0:T(8,128)(2,1)S(1)}, bf16[512,512]{1,0:T(8,128)(2,1)S(1)}, u32[]{:S(2)}, u32[]{:S(2)}) collective-permute-start(bf16[512,512]{1,0:T(8,128)(2,1)S(1)} %add_convert_fusion.2.refs_1_), channel_id=1, source_target_pairs={{0,8},{4,12},{8,0},{12,4},{16,24},{20,28},{24,16},{28,20},{1,9},{5... | collective-permute-start | bytes 1572872 | tf_op jit(solution)/shard_map/ppermute | solution.py:446
  539.5 28.1 %collective-permute-start.84 = (bf16[512,512]{1,0:T(8,128)(2,1)S(1)}, bf16[512,512]{1,0:T(8,128)(2,1)S(1)}, u32[]{:S(2)}, u32[]{:S(2)}) collective-permute-start(bf16[512,512]{1,0:T(8,128)(2,1)S(1)} %collective-permute-done.77.refs_3_), channel_id=1, source_target_pairs={{0,4},{4,0},{8,12},{12,8},{16,20},{20,16},{24,28},{28,24},{1,5},{5... | collective-permute-start | bytes 1572872 | tf_op jit(solution)/shard_map/ppermute | solution.py:446
  564.2 20.1 %collective-permute-start.86 = (bf16[512,384]{1,0:T(8,128)(2,1)S(1)}, bf16[512,384]{1,0:T(8,128)(2,1)S(1)}, u32[]{:S(2)}, u32[]{:S(2)}) collective-permute-start(bf16[512,384]{1,0:T(8,128)(2,1)S(1)} %get-tuple-element.338), channel_id=1, source_target_pairs={{0,16},{4,20},{8,24},{12,28},{16,0},{20,4},{24,8},{28,12},{1,17},{... | collective-permute-start | bytes 1179656 | tf_op jit(solution)/shard_map/ppermute | solution.py:446
  567.6 21.8 %collective-permute-start.89 = (bf16[512,512]{1,0:T(8,128)(2,1)S(1)}, bf16[512,512]{1,0:T(8,128)(2,1)S(1)}, u32[]{:S(2)}, u32[]{:S(2)}) collective-permute-start(bf16[512,512]{1,0:T(8,128)(2,1)S(1)} %collective-permute-done.83.refs_3_), channel_id=1, source_target_pairs={{0,4},{4,0},{8,12},{12,8},{16,20},{20,16},{24,28},{28,24},{1,5},{5... | collective-permute-start | bytes 1572872 | tf_op jit(solution)/shard_map/ppermute | solution.py:446
  568.7 20.7 %collective-permute-start.87 = (bf16[512,384]{1,0:T(8,128)(2,1)S(1)}, bf16[512,384]{1,0:T(8,128)(2,1)S(1)}, u32[]{:S(2)}, u32[]{:S(2)}) collective-permute-start(bf16[512,384]{1,0:T(8,128)(2,1)S(1)} %add_convert_fusion.13.refs_0_), channel_id=1, source_target_pairs={{0,4},{4,0},{8,12},{12,8},{16,20},{20,16},{24,28},{28,24},{1,5},{5... | collective-permute-start | bytes 1179656 | tf_op jit(solution)/shard_map/ppermute | solution.py:446
  569.9 19.5 %collective-permute-start.88 = (bf16[512,384]{1,0:T(8,128)(2,1)S(1)}, bf16[512,384]{1,0:T(8,128)(2,1)S(1)}, u32[]{:S(2)}, u32[]{:S(2)}) collective-permute-start(bf16[512,384]{1,0:T(8,128)(2,1)S(1)} %add_convert_fusion.13.refs_0_), channel_id=1, source_target_pairs={{0,8},{4,12},{8,0},{12,4},{16,24},{20,28},{24,16},{28,20},{1,9},{5... | collective-permute-start | bytes 1179656 | tf_op jit(solution)/shard_map/ppermute | solution.py:446
  569.9 19.5 %collective-permute-start.90 = (f32[15872]{0:T(1024)S(1)}, f32[15872]{0:T(1024)S(1)}, u32[]{:S(2)}, u32[]{:S(2)}) collective-permute-start(f32[15872]{0:T(1024)S(1)} %pad_maximum_fusion.3), channel_id=1, source_target_pairs={{0,4},{4,0},{8,12},{12,8},{16,20},{20,16},{24,28},{28,24},{1,5},{5... | collective-permute-start | bytes 190472 | tf_op jit(solution)/shard_map/ppermute | solution.py:446
  (154 other events, 1875.4 us)

commit v7 on v6

--- a/solution.py
+++ b/solution.py
@@ -15,6 +15,7 @@
 EPSILON = 1e-05
 BF = jnp.bfloat16
 F32 = jnp.float32
+SMALL = pl.CostEstimate(flops=1 << 20, bytes_accessed=1 << 16, transcendentals=0)
 
 
 def rotary_table(length):
@@ -105,11 +106,7 @@
         out_shape=jax.ShapeDtypeStruct((length, columns), BF),
         input_output_aliases={6: 0} if part else {},
         compiler_params=pltpu.CompilerParams(vmem_limit_bytes=40 << 20),
-        cost_estimate=pl.CostEstimate(
-            flops=2 * rows * width * columns,
-            bytes_accessed=2 * (rows * width + width * columns + rows * columns),
-            transcendentals=0,
-        ),
+        cost_estimate=SMALL,
         name="qkv_rotary",
     )(normed, weight, bias[None, :], table, table, table, *([whole] if part else []))
 
@@ -161,11 +158,7 @@
             jax.ShapeDtypeStruct((heads, length, 1), F32),
         ],
         compiler_params=pltpu.CompilerParams(vmem_limit_bytes=32 << 20),
-        cost_estimate=pl.CostEstimate(
-            flops=4 * heads * length * length * HD,
-            bytes_accessed=8 * length * heads * HD,
-            transcendentals=heads * length * length,
-        ),
+        cost_estimate=SMALL,
         name="attend",
     )(prefix, qkv, qkv, qkv, spots[:, None], spots[None, :])
 
@@ -229,11 +222,7 @@
         ),
         out_shape=jax.ShapeDtypeStruct((length, heads * 3 * HD), BF),
         compiler_params=pltpu.CompilerParams(vmem_limit_bytes=48 << 20),
-        cost_estimate=pl.CostEstimate(
-            flops=10 * heads * length * length * HD,
-            bytes_accessed=14 * length * heads * HD,
-            transcendentals=heads * length * length,
-        ),
+        cost_estimate=SMALL,
         name="attend_back",
     )(prefix, qkv, qkv, qkv, grad_context, log_total, spots[:, None], spots[None, :], table, table, table)
 
@@ -247,36 +236,34 @@
             out_ref[...] = piece[...].astype(F32)
 
 
-def place_quarters(whole, pieces, shape, axis, offset, quarter):
-    rows, columns = pieces[0].shape
+def place_quarters(whole, near, far, shape, axis, offset, quarter):
+    rows, columns = near.shape[0] // 2, near.shape[1]
     if axis == 0:
         each, first_row = shape[0] // 4 // rows, offset // rows
         spot = lambda k, q: ((q[0] ^ k) * each + first_row, 0)
     else:
         spot = lambda k, q: (offset // rows, q[0] ^ k)
     first = whole is None
-    operands = ([] if first else [whole]) + list(pieces)
+    operands = ([] if first else [whole]) + [near, far, near, far]
     return pl.pallas_call(
         place_kernel,
         grid_spec=pltpu.PrefetchScalarGridSpec(
             num_scalar_prefetch=1,
             grid=(4,),
             in_specs=([] if first else [pl.BlockSpec(memory_space=pl.ANY)])
-            + [pl.BlockSpec((rows, columns), lambda k, q: (0, 0))] * 4,
+            + [pl.BlockSpec((rows, columns), lambda k, q, h=h: (h, 0)) for h in (0, 0, 1, 1)],
             out_specs=pl.BlockSpec((rows, columns), spot),
         ),
         out_shape=jax.ShapeDtypeStruct(shape, F32),
         input_output_aliases={} if first else {1: 0},
         compiler_params=pltpu.CompilerParams(vmem_limit_bytes=24 << 20),
-        cost_estimate=pl.CostEstimate(
-            flops=0, bytes_accessed=24 * rows * columns, transcendentals=0
-        ),
+        cost_estimate=SMALL,
         name="place_quarters",
     )(quarter.reshape(1), *operands)
 
 
 def norms_kernel(count, *refs):
-    gains, blocks, (attn_ref, mlp_ref) = refs[:4], refs[4 : 4 + count], refs[4 + count :]
+    gains, blocks, (attn_ref, mlp_ref) = refs[:4], refs[4 : 4 + count], refs[-2:]
     for index, block in enumerate(blocks):
 
         @pl.when(pl.program_id(0) == index)
@@ -291,25 +278,25 @@
             mlp_ref[...] = (xhat * gain_m + shift_m).astype(BF)
 
 
-def both_norms(blocks, gains):
+def both_norms(blocks, gains, total=None, into=()):
     count = len(blocks)
+    total = total or count
+    skip = total - count if into else 0
     rows, width = blocks[0].shape
-    shape = jax.ShapeDtypeStruct((count * rows, width), BF)
+    shape = jax.ShapeDtypeStruct((total * rows, width), BF)
     return pl.pallas_call(
         functools.partial(norms_kernel, count),
         grid=(count,),
         in_specs=[pl.BlockSpec((1, width), lambda i: (0, 0))] * 4
-        + [pl.BlockSpec((rows, width), lambda i: (0, 0))] * count,
-        out_specs=[pl.BlockSpec((rows, width), lambda i: (i, 0))] * 2,
+        + [pl.BlockSpec((rows, width), lambda i: (0, 0))] * count
+        + [pl.BlockSpec(memory_space=pl.ANY)] * len(into),
+        out_specs=[pl.BlockSpec((rows, width), lambda i: (i + skip, 0))] * 2,
         out_shape=[shape, shape],
+        input_output_aliases={4 + count: 0, 5 + count: 1} if into else {},
         compiler_params=pltpu.CompilerParams(vmem_limit_bytes=48 << 20),
-        cost_estimate=pl.CostEstimate(
-            flops=12 * count * rows * width,
-            bytes_accessed=6 * count * rows * width,
-            transcendentals=0,
-        ),
+        cost_estimate=SMALL,
         name="both_norms",
-    )(*gains, *blocks)
+    )(*gains, *blocks, *into)
 
 
 def outer_kernel(lefts, pieces, outs, _, *refs):
@@ -359,11 +346,7 @@
         ),
         out_shape=[jax.ShapeDtypeStruct((size, width), BF) for size in sizes],
         compiler_params=pltpu.CompilerParams(vmem_limit_bytes=56 << 20),
-        cost_estimate=pl.CostEstimate(
-            flops=2 * tokens * left * width,
-            bytes_accessed=2 * tokens * (left + width),
-            transcendentals=0,
-        ),
+        cost_estimate=SMALL,
         name="outer_blocks",
     )(quarter.reshape(1), *[a for a, *_ in lefts], *rights)
 
@@ -392,11 +375,7 @@
         out_specs=pl.BlockSpec((rows, units), lambda i: (i, 0)),
         out_shape=jax.ShapeDtypeStruct((count * rows, units), BF),
         compiler_params=pltpu.CompilerParams(vmem_limit_bytes=56 << 20),
-        cost_estimate=pl.CostEstimate(
-            flops=2 * count * rows * units * width,
-            bytes_accessed=2 * count * rows * (width + 3 * units),
-            transcendentals=0,
-        ),
+        cost_estimate=SMALL,
         name="back_blocks",
     )(weight, slope, *blocks)
 
@@ -471,14 +450,6 @@
         half = rows // 2
         return [(flip(v[:half], 1), flip(u[half:], 2)) for u, v in zip(second[1], second[2])]
 
-    def far_parts(first, second, last):
-        corner, beside, across = second
-        parts = []
-        for blocks in ([first[0]] + beside, [first[1]] + across, [corner] + last):
-            for block in blocks:
-                parts += [block, to_core(block)]
-        return parts
-
     def meet(*trees):
         leaves, shape = jax.tree.flatten(trees)
         return jax.tree.unflatten(shape, lax.optimization_barrier(tuple(leaves)))
@@ -509,11 +480,10 @@
     counted = flip(count, 1)
     pre_own = units(norm_mlp_own)
     active_own = exact_gelu(pre_own)[0].astype(BF)
-    start = after(jnp.asarray(block_ids) * rows, norm_mlp_own)
     table = jnp.concatenate(
         [
-            lax.dynamic_slice_in_dim(jnp.asarray(rotary_table(LEN)), start[i], rows, 0)
-            for i in range(tp)
+            lax.dynamic_slice_in_dim(jnp.asarray(rotary_table(LEN)), b * rows, rows, 0)
+            for b in block_ids
         ],
         axis=0,
     )
@@ -529,6 +499,7 @@
     for block in hidden_y:
         near_blocks += [block, to_core(block)]
     second = second_far(first, hidden_y)
+    first_mates = [to_core(block) for block in first]
     counted = flip(count, 2)
     norm_attn_rest, norm_mlp_rest = both_norms(near_blocks[2:], gains)
     qkv_low = project_qkv(norm_attn_rest, qkv_weight, qkv_bias, table, LEN, qkv_own)
@@ -537,8 +508,8 @@
     context_far = swap_quarters(context)
     pre_rest = units(norm_mlp_rest)
     active_rest = exact_gelu(pre_rest)[0].astype(BF)
-    active_rest, context, counted, second, context_far = meet(
-        active_rest, context, counted, second, context_far
+    active_rest, context, counted, second, context_far, first_mates = meet(
+        active_rest, context, counted, second, context_far, first_mates
     )
     count = count + counted
 
@@ -551,7 +522,8 @@
         blocks = part.reshape(-1, 2, rows, D)
         return blocks[:, 0] + to_core(blocks[:, 1].astype(BF)).astype(F32)
 
-    last = last_far(second)
+    corner, beside, across = second
+    second_mates = [to_core(block) for block in [corner] + beside + across]
     counted = jnp.zeros_like(count)
     bit = 2
     while bit < tp:
@@ -562,16 +534,30 @@
     part_rest = branch_rows(context[close:], active_rest).reshape(-1, 2, rows, D)
     mates_rest = to_core(part_rest[:, 1].astype(BF))
     part_own = branch_rows(context[:close], after(active_own, part_rest)).reshape(2, rows, D)
-    part_own, mates_rest, counted = meet(part_own, mates_rest, counted)
+    part_own, mates_rest, counted, second_mates = meet(
+        part_own, mates_rest, counted, second_mates
+    )
     count = count + counted
 
     sums = part_rest[:, 0] + mates_rest.astype(F32)
     came = [to_y(sums[step - 1].astype(BF), step) for step in range(1, ways)]
     mates_own = to_core(part_own[1].astype(BF))
     counted = flip(count, 4) if dp > 4 else jnp.zeros_like(count)
+    last = last_far(second)
+    ahead = [first[0]] + beside + [first[1]] + across + [corner]
+    mates = (
+        [first_mates[0]]
+        + second_mates[1:ways]
+        + [first_mates[1]]
+        + second_mates[ways:]
+        + [second_mates[0]]
+    )
+    far_blocks = [block for pair in zip(ahead, mates) for block in pair]
+    norms_far = both_norms(far_blocks, gains, 6 * ways)
+    last, norms_far = meet(last, norms_far)
     last = [jnp.concatenate(pair, axis=0) for pair in last]
-    far_blocks = far_parts(first, second, last)
-    norm_attn_far, norm_mlp_far = both_norms(far_blocks, gains)
+    far_blocks = [block for v in last for block in (v, to_core(v))]
+    norm_attn_far, norm_mlp_far = both_norms(far_blocks, gains, 6 * ways, norms_far)
     came, mates_own, counted, norm_mlp_far = meet(came, mates_own, counted, norm_mlp_far)
     count = count + counted
     mask = 8
@@ -630,7 +616,7 @@
 
     queue = []
     due = {}
-    clock = [0]
+    clock, launched = [0], [0]
     results = {}
     token = [grad_near]
 
@@ -640,30 +626,31 @@
     def flipped(v, mask):
         return v, lambda value: flip(value, mask)
 
-    def travel(name, low):
+    def travel(low, name, wait):
         mask = 4
         while mask < dp:
-            (got,) = yield [flipped(low, mask)], 2
+            (got,) = yield [flipped(low, mask)], wait
             low = (low.astype(F32) + got.astype(F32)).astype(BF)
-            mask *= 2
-        beside, across = yield [flipped(low, 1), flipped(low, 2)], 1
-        (corner,) = yield [flipped(across, 1)], 1
-        results.setdefault(name, []).append((low, beside, across, corner))
+            mask, wait = mask * 2, 1
+        (across,) = yield [flipped(low, 2)], 1
+        near = jnp.concatenate([low, across], axis=0)
+        (far,) = yield [flipped(near, 1)], 1
+        results.setdefault(name, []).append((near, far))
 
     def swap_walk(v, into):
-        got = yield [flipped(quarter_of(v, 1, quarter ^ m), m) for m in (1, 2, 3)], 3
+        got = yield [flipped(quarter_of(v, 1, quarter ^ m), m) for m in (1, 2)], 1
         into.extend(got)
-
-    def scatter_walk(kept, mates, into):
+        got = yield [flipped(quarter_of(v, 1, quarter ^ 3), 3)], 1
+        into.extend(got)
+
+    def last_walk(kept, mates, parts, others, into):
         (got,) = yield [(mates, to_core)], 1
         sums = kept + got.astype(F32)
         total = sums[0]
         for step in range(1, ways):
-            (got,) = yield [(sums[step].astype(BF), lambda v, s=step: to_y(v, s))], 2
+            (got,) = yield [(sums[step].astype(BF), lambda v, s=step: to_y(v, s))], 1
             total = total + got.astype(F32)
         into["input"] = grad_out + total
-
-    def small_walk(parts, others, into):
         bit = 1
         while bit < tp:
             pairs = [(t, t ^ bit) for t in range(tp)]
@@ -693,22 +680,23 @@
         edges = [unit * sum(shares[:i]) for i in range(len(shares) + 1)]
         return [lax.slice_in_dim(part, a, b, axis=0) for a, b in zip(edges, edges[1:])]
 
-    def enqueue(name, chunks):
-        rows_before, _ = parts_of.get(name, (0, 0))
-        for piece in chunks:
-            queue.append((name, piece))
-            rows_before += piece.shape[0]
-        parts_of[name] = (rows_before, chunks[0].shape[1])
+    def enqueue(name, *units):
+        before, _ = parts_of.get(name, (0, 0))
+        parts_of[name] = (before + sum(u.shape[0] for u in units), units[0].shape[1])
+        queue.extend((unit, name) for unit in units)
 
     def turn(*others):
         now = clock[0]
         clock[0] = now + 1
         arrived = due.pop(now, [])
         values = [got for _, gots in arrived for got in gots]
-        if queue:
-            name, held = queue.pop(0)
-            values.append(held)
-        tied = list(lax.optimization_barrier(tuple(values) + others))
+        fresh = []
+        while queue and launched[0] <= now + 1:
+            fresh.append(queue.pop(0) + (max(launched[0] - now, 0) + 1,))
+            launched[0] += 1
+        tied = list(
+            lax.optimization_barrier(tuple(values) + tuple(f[0] for f in fresh) + others)
+        )
         token[0] = tied[0]
         asked = []
         for walker, gots in arrived:
@@ -717,19 +705,20 @@
                 asked.append((walker, walker.send(gots)))
             except StopIteration:
                 pass
-        if len(values) > sum(len(gots) for _, gots in arrived):
-            walker = travel(name, tied.pop(0))
+        for _, name, wait in fresh:
+            walker = travel(tied.pop(0), name, wait)
             asked.append((walker, next(walker)))
         for walker, request in asked:
             start(walker, request, now)
         return tied
 
-    def place_one(whole, pieces, shape, axis, offset):
-        rows_here, columns = pieces[0].shape
+    def place_one(whole, near, far, shape, axis, offset):
+        rows_here, columns = near.shape[0] // 2, near.shape[1]
         if columns % 128 == 0:
-            return place_quarters(whole, pieces, shape, axis, offset, quarter)
+            return place_quarters(whole, near, far, shape, axis, offset, quarter)
         if whole is None:
             whole = jnp.zeros(shape, F32)
+        pieces = (near[:rows_here], far[:rows_here], near[rows_here:], far[rows_here:])
         for index, piece in enumerate(pieces):
             spot = quarter ^ index
             start = (
@@ -750,19 +739,19 @@
 
     chunk = half // 2
     kept_columns = context.shape[1] // 4
-    enqueue("fc2", outer_blocks(hidden_lefts(0), rights, [chunk] * 2, quarter))
+    enqueue("fc2", *outer_blocks(hidden_lefts(0), rights, [chunk] * 2, quarter))
     turn()
+    grad_qkv_far = []
+    walk(swap_walk(gate(grad_qkv), grad_qkv_far))
     lefts = hidden_lefts(1)
     for index, piece in enumerate([context_quarter] + context_far):
         lefts.append((piece, kept_columns, 0, 0, half, index * LEN))
     *parts, out_part = outer_blocks(
         lefts, [gate(grad_near)] + grad_far, [chunk] * 2 + [kept_columns], quarter
     )
-    enqueue("fc2", parts)
-    enqueue("out", [out_part])
-    grad_qkv_far = []
-    walk(swap_walk(gate(grad_qkv), grad_qkv_far))
-    (out_part,) = turn(out_part)
+    enqueue("fc2", *parts)
+    enqueue("out", out_part)
+    turn()
     grad_inner_far = back_blocks([gate(grad_far[0])] + grad_far[1:], fc2_quarter, slope_far)
     (grad_inner_far,) = turn(grad_inner_far)
     inner_quarter = gate(quarter_of(grad_inner, 1, quarter))
@@ -772,15 +761,7 @@
         + contract(norm_mlp_far, grad_inner_far, 0, 0)
     )
     (fc1_part,) = turn(fc1_part.astype(BF))
-    enqueue("fc1", cut(fc1_part, [4, 4, 4, 4]))
-    qkv_quarter = gate(quarter_of(grad_qkv, 1, quarter))
-    qkv_part = (
-        contract(norm_attn_own, qkv_quarter[:close], 0, 0)
-        + contract(norm_attn_rest, qkv_quarter[close:], 0, 0)
-        + contract(norm_attn_far, jnp.concatenate(grad_qkv_far, axis=0), 0, 0)
-    )
-    (qkv_part,) = turn(qkv_part.astype(BF))
-    enqueue("qkv", cut(qkv_part, [4, 4, 4, 2, 1, 1]))
+    enqueue("fc1", *cut(fc1_part, [4, 4, 4, 4]))
     grad_norm_attn = contract(gate(grad_qkv), qkv_weight, 1, 1)
     (grad_norm_attn,) = turn(grad_norm_attn)
     grad_norm_mlp = contract(gate(grad_inner), fc1_weight, 1, 1)
@@ -807,13 +788,22 @@
     tensor_parts, lift, pull = turn(tensor_parts, lift, pull)
     grad_hidden = inverse * (gained - lift - xhat * pull)
     blocks = grad_hidden.reshape(ways, 2, rows, D)
-    kept, mates = turn(blocks[:, 0], blocks[:, 1].astype(BF))
-    outcome = {}
-    walk(scatter_walk(kept, mates, outcome))
     fc1_bias_part = jnp.sum(gate(grad_inner), axis=0, dtype=F32)
     qkv_bias_part = jnp.sum(gate(grad_qkv), axis=0, dtype=F32)
-    fc1_bias_part, qkv_bias_part = turn(fc1_bias_part, qkv_bias_part)
-    walk(small_walk(tensor_parts, jnp.concatenate([fc1_bias_part, qkv_bias_part]), outcome))
+    kept, mates, fc1_bias_part, qkv_bias_part = turn(
+        blocks[:, 0], blocks[:, 1].astype(BF), fc1_bias_part, qkv_bias_part
+    )
+    outcome = {}
+    others = jnp.concatenate([fc1_bias_part, qkv_bias_part])
+    walk(last_walk(kept, mates, tensor_parts, others, outcome))
+    qkv_quarter = gate(quarter_of(grad_qkv, 1, quarter))
+    qkv_part = (
+        contract(norm_attn_own, qkv_quarter[:close], 0, 0)
+        + contract(norm_attn_rest, qkv_quarter[close:], 0, 0)
+        + contract(norm_attn_far, jnp.concatenate(grad_qkv_far, axis=0), 0, 0)
+    )
+    (qkv_part,) = turn(qkv_part.astype(BF))
+    enqueue("qkv", *cut(qkv_part, [4, 4, 4, 2, 1, 1]))
     axes = {"fc2": 0, "out": 0, "fc1": 1, "qkv": 1}
     placed = {name: (None, 0, 0) for name in axes}
 
@@ -822,8 +812,8 @@
         pieces = results[name][done]
         lengths, columns = parts_of[name]
         shape = (4 * lengths, columns) if axes[name] == 0 else (lengths, 4 * columns)
-        whole = place_one(whole, pieces, shape, axes[name], offset)
-        placed[name] = (whole, done + 1, offset + pieces[0].shape[0])
+        whole = place_one(whole, *pieces, shape, axes[name], offset)
+        placed[name] = (whole, done + 1, offset + pieces[0].shape[0] // 2)
 
     while queue or due:
         ready = []

time: 672 us -> 641 us (0.954)
  waiting for transfers between devices: 188 us -> 179 us
  other arithmetic: 48.1 us -> 56 us
  between operations: 14.1 us -> 6.52 us
  local copies, waits for them, and re-layouts: 53.3 us -> 46.2 us
  matrix products: 118 us -> 111 us
  Pallas kernels: 145 us -> 138 us
    ppermute x84 -> x69, waiting for transfers between devices: 184 us -> 175 us  [flip(): return lax.ppermute(v, 'dp', [(d, d ^ mask) for d in range(dp)])]
    pallas_call x3 -> x4, Pallas kernels: 36 us -> 29.2 us  [both_norms(): pl.pallas_call(functools.partial(norms_kernel, count), grid=(count,), in_...]
    unnamed x216 -> x180, local copies, waits for them, and re-layouts: 25.2 us -> 18.5 us
    ppermute x84 -> x69, starting transfers between devices: 81.6 us -> 82.2 us  [flip(): return lax.ppermute(v, 'dp', [(d, d ^ mask) for d in range(dp)])]
  transfers between devices with their start and end apart: 113 -> 98, of which waited for: 40 -> 44; matrix products, arithmetic and copies ran while one was open for 29% -> 29% of each run, Pallas kernels for 20% -> 20%
where the time goes in v7:
time: 641 us; the launch traced here: 631 us
  waiting for transfers between devices  179 us (28%)
  Pallas kernels  138 us (22%)
  matrix products  111 us (17%)
  starting transfers between devices  94.2 us (15%)
  other arithmetic  56 us (9%)
  local copies, waits for them, and re-layouts  46.2 us (7%)
  between operations  6.52 us (1%)
    ppermute x69, waiting for transfers between devices, flip(): return lax.ppermute(v, 'dp', [(d, d ^ mask) for d in range(dp)])  175 us
    ppermute x69, starting transfers between devices, flip(): return lax.ppermute(v, 'dp', [(d, d ^ mask) for d in range(dp)])  82.2 us
    dot_general x10, matrix products, contract(): lax.dot_general(left_side, right_side, (((left_dim,), (right_dim,)), ((),...  64.9 us
    pallas_call x15, Pallas kernels, place_quarters(): pl.pallas_call(place_kernel, grid_spec=pltpu.PrefetchScalarGridSpec(num_s...  35 us
    pallas_call x4, Pallas kernels, both_norms(): pl.pallas_call(functools.partial(norms_kernel, count), grid=(count,), in_...  29.2 us
    pallas_call x2, Pallas kernels, outer_blocks(): pl.pallas_call(functools.partial(outer_kernel, len(lefts), pieces, len(si...  23.3 us
    dot_general x2, matrix products, units(): jnp.dot(normed, fc1_weight, preferred_element_type=F32)  20.2 us
    unnamed x180, local copies, waits for them, and re-layouts  18.5 us
  transfers between devices with their start and end apart: 98, of which 44 were waited for; matrix products, arithmetic and copies ran while one was open for 29% of the time, Pallas kernels for 20%

profile of v7, /device:TPU:0, one launch (start us, length us, event | category | flops | bytes accessed | tf_op | source)
XLA Modules:
  0.0 631.4 jit_solution(12099984049954087340)
XLA Ops:
  1.2 2.6 collective-permute-start.3
  12.4 3.1 both_norms.4
  20.0 9.7 %multiply_convert_fusion.2 = (bf16[512,2048]{1,0:T(8,128)(2,1)}, f32[512,2048]{1,0:T(8,128)}) fusion(f32[2048]{0:T(1024)S(1)} %convert_element_type.245, bf16[512,2048]{1,0:T(8,128)(2,1)} %get-tuple-element.199, bf16[2048,2048]{1,0:T(8,128)(2,1)} %param.32), kind=kOutput, calls=%fused_computation.38 | convolution fusion | flops 4301258752 | bytes 16785408 | tf_op jit(solution)/shard_map/dot_general | solution.py:472
  29.7 5.4 qkv_rotary.2.refs_0_
  43.5 4.3 both_norms.5
  47.8 2.6 copy-done.3
  51.9 2.8 copy-done.14
  54.6 5.4 qkv_rotary.3.q_ref.k_ref.v_ref
  60.1 9.6 %attend.1 = (bf16[1024,512]{1,0:T(8,128)(2,1)S(1)}, f32[2,1024,1]{2,1,0:T(8,128)S(1)}) custom-call(s32[1]{0:T(128)S(6)} %copy.79.prefix_ref, bf16[1024,1536]{1,0:T(8,128)(2,1)S(1)} %qkv_rotary.3.q_ref.k_ref.v_ref, bf16[1024,1536]{1,0:T(8,128)(2,1)S(1)} %qkv_rotary.3.q_ref.k_ref.v_ref, bf16[1024,1536]{1,0:T(8,128)(2,1)S(1)} %qkv_rotary.3.q_ref.k_ref.v_ref, ...), custom_call_target="tpu_custom_call" | custom-call | flops 1048576 | bytes 65536 | tf_op jit(solution)/shard_map/attend/pallas_call | solution.py:139
  73.7 10.5 %multiply_convert_fusion.1 = (bf16[512,2048]{1,0:T(8,128)(2,1)S(1)}, f32[512,2048]{1,0:T(8,128)}) fusion(f32[2048]{0:T(1024)S(1)} %convert_element_type.245, bf16[512,2048]{1,0:T(8,128)(2,1)S(1)} %copy-done.57, bf16[2048,2048]{1,0:T(8,128)(2,1)} %param.32), kind=kOutput, calls=%fused_computation.37 | convolution fusion | flops 4301258752 | bytes 16785408 | tf_op jit(solution)/shard_map/dot_general | solution.py:472
  86.2 4.5 fusion.67
  93.2 4.5 fusion.68
  107.7 16.7 %both_norms.6 = (bf16[3072,2048]{1,0:T(8,128)(2,1)}, bf16[3072,2048]{1,0:T(8,128)(2,1)}) custom-call(bf16[1,2048]{1,0:T(2,128)(2,1)S(1)} %broadcast_in_dim.16.refs_0_, bf16[1,2048]{1,0:T(2,128)(2,1)S(1)} %broadcast_in_dim.17.refs_1_, bf16[1,2048]{1,0:T(2,128)(2,1)S(1)} %broadcast_in_dim.18.refs_2_, bf16[1,2048]{1,0:T(2,128)(2,1)S(1)} %broadcast_in_dim.19.refs_3_, ...), custom_call_target="tpu_custom_call" | custom-call | flops 1048576 | bytes 65536 | tf_op jit(solution)/shard_map/both_norms/pallas_call | solution.py:287
  129.8 2.6 collective-permute-start.23
  132.5 5.1 both_norms.7
  138.9 3.0 fusion.30
  148.6 14.7 %fusion.21 = (f32[3072,512]{1,0:T(8,128)}, bf16[3072,512]{1,0:T(8,128)(2,1)}) fusion(f32[512]{0:T(512)S(1)} %dynamic-slice_convert_fusion, bf16[3072,2048]{1,0:T(8,128)(2,1)} %get-tuple-element.241, bf16[2048,2048]{1,0:T(8,128)(2,1)} %param.32, s32[]{:T(128)S(6)} %select_n.81), kind=kOutput, calls=%fused_computation.28 | convolution fusion | flops 6459752448 | bytes 24119300 | tf_op jit(solution)/shard_map/dot_general | solution.py:583
  164.9 3.2 constant_dynamic-slice_fusion.6.weight_ref
  176.3 17.3 %fusion.17 = bf16[1024,2048]{1,0:T(8,128)(2,1)} fusion(f32[512,2048]{1,0:T(8,128)} %get-tuple-element.432, f32[512,2048]{1,0:T(8,128)} %get-tuple-element.430, bf16[1024,2048]{1,0:T(8,128)(2,1)S(1)} %constant_dynamic-update-slice_fusion.2.refs_3_.refs_7_, bf16[2048,2048]{1,0:T(8,128)(2,1)} %param.34), kind=kOutput, calls=%fused_computation.21 | convolution fusion | flops 8613003264 | bytes 25165824 | tf_op jit(solution)/shard_map/dot_general | solution.py:35
  196.1 3.1 collective-permute-done.32.refs_12_.refs_16_.refs_8_
  201.3 11.8 %attend_back.1 = bf16[1024,1536]{1,0:T(8,128)(2,1)} custom-call(s32[1]{0:T(128)S(6)} %copy.79.prefix_ref, bf16[1024,1536]{1,0:T(8,128)(2,1)} %copy-done.4, bf16[1024,1536]{1,0:T(8,128)(2,1)} %copy-done.4, bf16[1024,1536]{1,0:T(8,128)(2,1)} %copy-done.4, bf16[1024,512]{1,0:T(8,128)(2,1)S(1)} %convolution_convert_fusion.g_ref, f32[2,1024,1]{2,1,0:T(8,128)S(1)} %copy-done.35, ...), custom_call_target="tpu_custom_call" | custom-call | flops 1048576 | bytes 65536 | tf_op jit(solution)/shard_map/attend_back/pallas_call | solution.py:205
  217.1 2.8 collective-permute-done.42.refs_15_.refs_19_.refs_11_
  219.9 10.7 %outer_blocks.2 = (bf16[128,2048]{1,0:T(8,128)(2,1)}, bf16[128,2048]{1,0:T(8,128)(2,1)}) custom-call(s32[1]{0:T(128)} %bitcast.9._.quarter_ref, bf16[512,2048]{1,0:T(8,128)(2,1)} %get-tuple-element.216.refs_0_, bf16[512,2048]{1,0:T(8,128)(2,1)} %copy-done.53, bf16[3072,512]{1,0:T(8,128)(2,1)} %get-tuple-element.244.refs_2_, bf16[1024,2048]{1,0:T(8,128)(2,1)} %copy-done.41, ...), custom_call_target="tpu_custom_call" | custom-call | flops 1048576 | bytes 65536 | tf_op jit(solution)/shard_map/outer_blocks/pallas_call | solution.py:337
  238.1 12.6 %outer_blocks.3 = (bf16[128,2048]{1,0:T(8,128)(2,1)}, bf16[128,2048]{1,0:T(8,128)(2,1)}, bf16[128,2048]{1,0:T(8,128)(2,1)}) custom-call(s32[1]{0:T(128)} %bitcast.9._.quarter_ref, bf16[512,2048]{1,0:T(8,128)(2,1)} %get-tuple-element.216.refs_0_, bf16[512,2048]{1,0:T(8,128)(2,1)} %copy-done.53, bf16[3072,512]{1,0:T(8,128)(2,1)} %get-tuple-element.244.refs_2_, ...), custom_call_target="tpu_custom_call" | custom-call | flops 1048576 | bytes 65536 | tf_op jit(solution)/shard_map/outer_blocks/pallas_call | solution.py:337
  250.7 12.2 %collective-permute-done.44 = bf16[128,2048]{1,0:T(8,128)(2,1)S(1)} collective-permute-done((bf16[128,2048]{1,0:T(8,128)(2,1)}, bf16[128,2048]{1,0:T(8,128)(2,1)S(1)}, u32[]{:S(2)}, u32[]{:S(2)}) %collective-permute-start.44) | collective-permute-done | bytes 524320 | tf_op jit(solution)/shard_map/ppermute | solution.py:425
  262.9 6.8 %collective-permute-done.46 = bf16[1024,384]{1,0:T(8,128)(2,1)S(1)} collective-permute-done((bf16[1024,384]{1,0:T(8,128)(2,1)S(1)}, bf16[1024,384]{1,0:T(8,128)(2,1)S(1)}, u32[]{:S(2)}, u32[]{:S(2)}) %collective-permute-start.46) | collective-permute-done | bytes 786464 | tf_op jit(solution)/shard_map/ppermute | solution.py:425
  277.2 18.0 %back_blocks.1 = bf16[3072,512]{1,0:T(8,128)(2,1)} custom-call(bf16[512,2048]{1,0:T(8,128)(2,1)} %constant_dynamic-slice_fusion.6.weight_ref, f32[3072,512]{1,0:T(8,128)} %get-tuple-element.401.slope_ref, bf16[256,2048]{1,0:T(8,128)(2,1)} %copy-done.47, bf16[256,2048]{1,0:T(8,128)(2,1)} %collective-permute-done.37.refs_5_.refs_9_.refs_1_, ...), custom_call_target="tpu_custom_call" | custom-call | flops 1048576 | bytes 65536 | tf_op jit(solution)/shard_map/back_blocks/pallas_call | solution.py:367
  295.2 9.0 %collective-permute-done.48 = bf16[1024,384]{1,0:T(8,128)(2,1)} collective-permute-done((bf16[1024,384]{1,0:T(8,128)(2,1)}, bf16[1024,384]{1,0:T(8,128)(2,1)}, u32[]{:S(2)}, u32[]{:S(2)}) %collective-permute-start.48) | collective-permute-done | bytes 786464 | tf_op jit(solution)/shard_map/ppermute | solution.py:425
  304.3 9.6 %collective-permute-done.47 = bf16[128,2048]{1,0:T(8,128)(2,1)} collective-permute-done((bf16[128,2048]{1,0:T(8,128)(2,1)}, bf16[128,2048]{1,0:T(8,128)(2,1)}, u32[]{:S(2)}, u32[]{:S(2)}) %collective-permute-start.47) | collective-permute-done | bytes 524320 | tf_op jit(solution)/shard_map/ppermute | solution.py:425
  323.0 10.6 %add_convert_fusion = bf16[2048,512]{1,0:T(8,128)(2,1)S(1)} fusion(f32[2048,512]{1,0:T(8,128)S(1)} %fusion.48, f32[2048,512]{1,0:T(8,128)S(1)} %fusion.46, bf16[3072,2048]{1,0:T(8,128)(2,1)} %get-tuple-element.241, bf16[3072,512]{1,0:T(8,128)(2,1)} %back_blocks.1), kind=kOutput, calls=%fused_computation.36 | convolution fusion | flops 6445596672 | bytes 26214400 | tf_op jit(solution)/shard_map/dot_general | solution.py:35
  333.7 5.8 collective-permute-done.51
  339.5 4.3 collective-permute-done.52.refs_1_.refs_3_
  345.5 2.6 collective-permute-start.56
  350.1 6.7 %fusion.69 = f32[1024,2048]{1,0:T(8,128)S(1)} fusion(bf16[1024,1536]{1,0:T(8,128)(2,1)S(1)} %copy-done.37, bf16[2048,1536]{1,0:T(8,128)(2,1)S(1)} %bitcast.83), kind=kOutput, calls=%fused_computation.164 | convolution fusion | flops 6442450944 | bytes 17825792 | tf_op jit(solution)/shard_map/dot_general | solution.py:35
  358.1 10.6 %collective-permute-done.53 = bf16[128,2048]{1,0:T(8,128)(2,1)S(1)} collective-permute-done((bf16[128,2048]{1,0:T(8,128)(2,1)S(1)}, bf16[128,2048]{1,0:T(8,128)(2,1)S(1)}, u32[]{:S(2)}, u32[]{:S(2)}) %collective-permute-start.53) | collective-permute-done | bytes 524320 | tf_op jit(solution)/shard_map/ppermute | solution.py:425
  368.7 3.5 collective-permute-done.54.refs_2_.refs_4_
  376.1 12.7 %fusion.70 = f32[1024,2048]{1,0:T(8,128)S(1)} fusion(bf16[1024,2048]{1,0:T(8,128)(2,1)} %fusion.17, bf16[2048,2048]{1,0:T(8,128)(2,1)} %param.32), kind=kOutput, calls=%fused_computation.165 | convolution fusion | flops 8589934592 | bytes 20971520 | tf_op jit(solution)/shard_map/dot_general | solution.py:35
  390.2 6.4 %collective-permute-done.58.refs_2_.refs_4_ = bf16[256,2048]{1,0:T(8,128)(2,1)S(1)} collective-permute-done((bf16[256,2048]{1,0:T(8,128)(2,1)S(1)}, bf16[256,2048]{1,0:T(8,128)(2,1)S(1)}, u32[]{:S(2)}, u32[]{:S(2)}) %collective-permute-start.58) | collective-permute-done | bytes 1048608 | tf_op jit(solution)/shard_map/ppermute | solution.py:425
  402.9 2.7 convert_reduce_fusion
  405.6 3.7 fusion.11
  409.3 10.5 %fusion.59 = (f32[2048]{0:T(1024)S(1)}, f32[2048]{0:T(1024)S(1)}, f32[1024]{0:T(1024)S(1)}, f32[1024]{0:T(1024)S(1)}, f32[1024,2048]{1,0:T(8,128)}, /*index=5*/f32[2048]{0:T(1024)S(1)}, f32[2048]{0:T(1024)S(1)}) fusion(f32[1024,2048]{1,0:T(8,128)S(1)} %fusion.70, f32[1024]{0:T(1024)S(1)} %add_rsqrt_fusion, f32[1024]{0:T(1024)S(1)} %broadcast_multiply_fusion.2, ...), kind=kLoop, calls=%fused_computation.155 | loop fusion | flops 46127104 | bytes 29425664 | tf_op jit(solution)/shard_map/reduce_sum | solution.py:783
  427.2 7.8 %fusion.10 = f32[1024,2048]{1,0:T(8,128)S(1)} fusion(f32[1024,2048]{1,0:T(8,128)} %get-tuple-element.398, f32[1024]{0:T(1024)S(1)} %broadcast_multiply_fusion, f32[1024]{0:T(1024)S(1)} %broadcast_multiply_fusion.1, f32[1024]{0:T(1024)S(1)} %add_rsqrt_fusion, f32[1024]{0:T(1024)S(1)} %broadcast_multiply_fusion.2, bf16[256,2048]{1,0:T(8,128)(2,1)S(1)} %copy-done.13, ...), kind=kLoop, calls=%fused_computation.14 | loop fusion | flops 29360128 | bytes 20987904 | tf_op jit(solution)/shard_map/mul | solution.py:789
  440.5 5.3 collective-permute-done.62
  445.8 3.7 collective-permute-done.63.refs_1_.refs_3_
  456.8 9.9 %add_convert_fusion.1 = bf16[2048,384]{1,0:T(8,128)(2,1)S(1)} fusion(f32[2048,384]{1,0:T(8,128)S(1)} %fusion.54, f32[2048,384]{1,0:T(8,128)S(1)} %fusion.52, bf16[3072,2048]{1,0:T(8,128)(2,1)} %get-tuple-element.316, bf16[1024,384]{1,0:T(8,128)(2,1)} %collective-permute-done.48, bf16[1024,384]{1,0:T(8,128)(2,1)S(1)} %copy-done.80, ...), kind=kOutput, calls=%fused_computation.41 | convolution fusion | flops 4841275392 | bytes 22806528 | tf_op jit(solution)/shard_map/dot_general | solution.py:35
  466.7 5.5 collective-permute-done.66
  472.2 3.1 collective-permute-done.67.refs_1_.refs_3_
  482.1 2.4 place_quarters.15.refs_0_
  487.1 13.8 %collective-permute-done.64 = bf16[512,512]{1,0:T(8,128)(2,1)S(1)} collective-permute-done((bf16[512,512]{1,0:T(8,128)(2,1)S(1)}, bf16[512,512]{1,0:T(8,128)(2,1)S(1)}, u32[]{:S(2)}, u32[]{:S(2)}) %collective-permute-start.64) | collective-permute-done | bytes 524320 | tf_op jit(solution)/shard_map/ppermute | solution.py:425
  502.0 2.5 collective-permute-start.75
  506.9 2.4 place_quarters.17.refs_0_
  509.4 11.9 %collective-permute-done.75 = bf16[512,384]{1,0:T(8,128)(2,1)S(1)} collective-permute-done((bf16[512,384]{1,0:T(8,128)(2,1)S(1)}, bf16[512,384]{1,0:T(8,128)(2,1)S(1)}, u32[]{:S(2)}, u32[]{:S(2)}) %collective-permute-start.75) | collective-permute-done | bytes 393248 | tf_op jit(solution)/shard_map/ppermute | solution.py:425
  523.5 2.6 collective-permute-done.73.refs_2_.refs_4_
  526.7 2.6 collective-permute-start.79
  529.8 2.7 place_quarters.19.refs_0_
  535.0 9.8 %collective-permute-done.76 = bf16[512,384]{1,0:T(8,128)(2,1)S(1)} collective-permute-done((bf16[512,384]{1,0:T(8,128)(2,1)S(1)}, bf16[512,384]{1,0:T(8,128)(2,1)S(1)}, u32[]{:S(2)}, u32[]{:S(2)}) %collective-permute-start.76) | collective-permute-done | bytes 393248 | tf_op jit(solution)/shard_map/ppermute | solution.py:425
  545.2 4.8 collective-permute-done.77.refs_2_.refs_4_
  550.6 2.6 collective-permute-start.81
  555.0 4.0 place_quarters.21
  561.5 6.4 %collective-permute-done.80 = bf16[512,384]{1,0:T(8,128)(2,1)S(1)} collective-permute-done((bf16[512,384]{1,0:T(8,128)(2,1)S(1)}, bf16[512,384]{1,0:T(8,128)(2,1)S(1)}, u32[]{:S(2)}, u32[]{:S(2)}) %collective-permute-start.80) | collective-permute-done | bytes 393248 | tf_op jit(solution)/shard_map/ppermute | solution.py:425
  577.2 3.3 collective-permute-done.84
  580.5 6.0 collective-permute-done.87
  598.7 7.0 %collective-permute-done.90.refs_2_.refs_4_ = bf16[1024,384]{1,0:T(8,128)(2,1)S(1)} collective-permute-done((bf16[1024,384]{1,0:T(8,128)(2,1)S(1)}, bf16[1024,384]{1,0:T(8,128)(2,1)S(1)}, u32[]{:S(2)}, u32[]{:S(2)}) %collective-permute-start.90) | collective-permute-done | bytes 786464 | tf_op jit(solution)/shard_map/ppermute | solution.py:425
  621.6 2.5 collective-permute-start.97
  (466 shorter events, 197.8 us)
Async XLA Ops:
  1.2 35.6 %collective-permute-start.3 = (bf16[256,2048]{1,0:T(8,128)(2,1)}, bf16[256,2048]{1,0:T(8,128)(2,1)}, u32[]{:S(2)}, u32[]{:S(2)}) collective-permute-start(bf16[256,2048]{1,0:T(8,128)(2,1)} %refs_4_.1), channel_id=1, source_target_pairs={{0,4},{4,0},{8,12},{12,8},{16,20},{20,16},{24,28},{28,24},{1,5},{5... | collective-permute-start | bytes 3145736 | tf_op jit(solution)/shard_map/ppermute | solution.py:425
  3.8 33.1 %collective-permute-start.4 = (bf16[256,2048]{1,0:T(8,128)(2,1)}, bf16[256,2048]{1,0:T(8,128)(2,1)}, u32[]{:S(2)}, u32[]{:S(2)}) collective-permute-start(bf16[256,2048]{1,0:T(8,128)(2,1)} %refs_4_.1), channel_id=1, source_target_pairs={{0,8},{4,12},{8,0},{12,4},{16,24},{20,28},{24,16},{28,20},{1,9},{5... | collective-permute-start | bytes 3145736 | tf_op jit(solution)/shard_map/ppermute | solution.py:425
  5.3 31.5 %collective-permute-start.5 = (bf16[256,2048]{1,0:T(8,128)(2,1)}, bf16[256,2048]{1,0:T(8,128)(2,1)}, u32[]{:S(2)}, u32[]{:S(2)}) collective-permute-start(bf16[256,2048]{1,0:T(8,128)(2,1)} %refs_4_.1), channel_id=1, source_target_pairs={{0,2},{1,3},{2,0},{3,1},{4,6},{5,7},{6,4},{7,5},{8,10},{9,11},{10,... | collective-permute-start | bytes 3145736 | tf_op jit(solution)/shard_map/ppermute | solution.py:418
  19.4 17.5 %collective-permute-start.2 = (f32[8,128]{1,0:T(8,128)S(1)}, f32[8,128]{1,0:T(8,128)S(1)}, u32[]{:S(2)}, u32[]{:S(2)}) collective-permute-start(f32[8,128]{1,0:T(8,128)S(1)} %broadcast_add_fusion), channel_id=1, source_target_pairs={{0,4},{4,0},{8,12},{12,8},{16,20},{20,16},{24,28},{28,24},{1,5},{5... | collective-permute-start | bytes 12296 | tf_op jit(solution)/shard_map/ppermute | solution.py:425
  37.1 33.1 %collective-permute-start.8 = (bf16[256,2048]{1,0:T(8,128)(2,1)}, bf16[256,2048]{1,0:T(8,128)(2,1)}, u32[]{:S(2)}, u32[]{:S(2)}) collective-permute-start(bf16[256,2048]{1,0:T(8,128)(2,1)} %collective-permute-done.4.refs_8_), channel_id=1, source_target_pairs={{0,4},{4,0},{8,12},{12,8},{16,20},{20,16},{24,28},{28,24},{1,5},{5... | collective-permute-start | bytes 3145736 | tf_op jit(solution)/shard_map/ppermute | solution.py:425
  38.5 32.3 %collective-permute-start.9 = (bf16[256,2048]{1,0:T(8,128)(2,1)}, bf16[256,2048]{1,0:T(8,128)(2,1)}, u32[]{:S(2)}, u32[]{:S(2)}) collective-permute-start(bf16[256,2048]{1,0:T(8,128)(2,1)} %collective-permute-done.3.refs_4_), channel_id=1, source_target_pairs={{0,2},{1,3},{2,0},{3,1},{4,6},{5,7},{6,4},{7,5},{8,10},{9,11},{10,... | collective-permute-start | bytes 3145736 | tf_op jit(solution)/shard_map/ppermute | solution.py:418
  39.0 32.4 %collective-permute-start.10 = (bf16[256,2048]{1,0:T(8,128)(2,1)}, bf16[256,2048]{1,0:T(8,128)(2,1)}, u32[]{:S(2)}, u32[]{:S(2)}) collective-permute-start(bf16[256,2048]{1,0:T(8,128)(2,1)} %collective-permute-done.5.refs_4_), channel_id=1, source_target_pairs={{0,8},{4,12},{8,0},{12,4},{16,24},{20,28},{24,16},{28,20},{1,9},{5... | collective-permute-start | bytes 3145736 | tf_op jit(solution)/shard_map/ppermute | solution.py:425
  41.2 43.0 %collective-permute-start.14 = (bf16[256,2048]{1,0:T(8,128)(2,1)}, bf16[256,2048]{1,0:T(8,128)(2,1)S(1)}, u32[]{:S(2)}, u32[]{:S(2)}) collective-permute-start(bf16[256,2048]{1,0:T(8,128)(2,1)} %collective-permute-done.3.refs_4_), channel_id=1, source_target_pairs={{0,1},{1,0},{2,3},{3,2},{4,5},{5,4},{6,7},{7,6},{8,9},{9,8},{10,11... | collective-permute-start | bytes 3145736 | tf_op jit(solution)/shard_map/ppermute | solution.py:414
  41.9 28.0 %collective-permute-start.7 = (f32[8,128]{1,0:T(8,128)S(1)}, f32[8,128]{1,0:T(8,128)S(1)}, u32[]{:S(2)}, u32[]{:S(2)}) collective-permute-start(f32[8,128]{1,0:T(8,128)S(1)} %fusion.97), channel_id=1, source_target_pairs={{0,8},{4,12},{8,0},{12,4},{16,24},{20,28},{24,16},{28,20},{1,9},{5... | collective-permute-start | bytes 12296 | tf_op jit(solution)/shard_map/ppermute | solution.py:425
  104.2 20.2 %collective-permute-start.24 = (bf16[128,2048]{1,0:T(8,128)(2,1)}, bf16[128,2048]{1,0:T(8,128)(2,1)}, u32[]{:S(2)}, u32[]{:S(2)}) collective-permute-start(bf16[128,2048]{1,0:T(8,128)(2,1)} %slice.136), channel_id=1, source_target_pairs={{0,4},{4,0},{8,12},{12,8},{16,20},{20,16},{24,28},{28,24},{1,5},{5... | collective-permute-start | bytes 1572872 | tf_op jit(solution)/shard_map/ppermute | solution.py:425
  105.3 19.1 %collective-permute-start.25 = (bf16[128,2048]{1,0:T(8,128)(2,1)S(1)}, bf16[128,2048]{1,0:T(8,128)(2,1)}, u32[]{:S(2)}, u32[]{:S(2)}) collective-permute-start(bf16[128,2048]{1,0:T(8,128)(2,1)S(1)} %slice.137), channel_id=1, source_target_pairs={{0,8},{4,12},{8,0},{12,4},{16,24},{20,28},{24,16},{28,20},{1,9},{5... | collective-permute-start | bytes 1572872 | tf_op jit(solution)/shard_map/ppermute | solution.py:425
  107.1 30.5 %collective-permute-start.21 = (bf16[256,2048]{1,0:T(8,128)(2,1)}, bf16[256,2048]{1,0:T(8,128)(2,1)}, u32[]{:S(2)}, u32[]{:S(2)}) collective-permute-start(bf16[256,2048]{1,0:T(8,128)(2,1)} %fusion.43), channel_id=1, source_target_pairs={{0,2},{1,3},{2,0},{3,1},{4,6},{5,7},{6,4},{7,5},{8,10},{9,11},{10,... | collective-permute-start | bytes 3145736 | tf_op jit(solution)/shard_map/ppermute | solution.py:422
  144.2 24.9 %collective-permute-start.27 = (bf16[256,2048]{1,0:T(8,128)(2,1)S(1)}, bf16[256,2048]{1,0:T(8,128)(2,1)}, u32[]{:S(2)}, u32[]{:S(2)}) collective-permute-start(bf16[256,2048]{1,0:T(8,128)(2,1)S(1)} %get-tuple-element.240), channel_id=1, source_target_pairs={{0,2},{1,3},{2,0},{3,1},{4,6},{5,7},{6,4},{7,5},{8,10},{9,11},{10,... | collective-permute-start | bytes 3145736 | tf_op jit(solution)/shard_map/ppermute | solution.py:418
  145.8 24.5 %collective-permute-start.28 = (bf16[256,2048]{1,0:T(8,128)(2,1)S(1)}, bf16[256,2048]{1,0:T(8,128)(2,1)S(1)}, u32[]{:S(2)}, u32[]{:S(2)}) collective-permute-start(bf16[256,2048]{1,0:T(8,128)(2,1)S(1)} %get-tuple-element.240), channel_id=1, source_target_pairs={{0,4},{4,0},{8,12},{12,8},{16,20},{20,16},{24,28},{28,24},{1,5},{5... | collective-permute-start | bytes 3145736 | tf_op jit(solution)/shard_map/ppermute | solution.py:425
  147.4 24.2 %collective-permute-start.29 = (bf16[256,2048]{1,0:T(8,128)(2,1)S(1)}, bf16[256,2048]{1,0:T(8,128)(2,1)S(1)}, u32[]{:S(2)}, u32[]{:S(2)}) collective-permute-start(bf16[256,2048]{1,0:T(8,128)(2,1)S(1)} %get-tuple-element.240), channel_id=1, source_target_pairs={{0,8},{4,12},{8,0},{12,4},{16,24},{20,28},{24,16},{28,20},{1,9},{5... | collective-permute-start | bytes 3145736 | tf_op jit(solution)/shard_map/ppermute | solution.py:425
  148.6 23.1 %collective-permute-start.30 = (bf16[256,2048]{1,0:T(8,128)(2,1)S(1)}, bf16[256,2048]{1,0:T(8,128)(2,1)S(1)}, u32[]{:S(2)}, u32[]{:S(2)}) collective-permute-start(bf16[256,2048]{1,0:T(8,128)(2,1)S(1)} %get-tuple-element.240), channel_id=1, source_target_pairs={{0,1},{1,0},{2,3},{3,2},{4,5},{5,4},{6,7},{7,6},{8,9},{9,8},{10,11... | collective-permute-start | bytes 3145736 | tf_op jit(solution)/shard_map/ppermute | solution.py:414
  171.8 27.4 %collective-permute-start.34 = (bf16[256,2048]{1,0:T(8,128)(2,1)}, bf16[256,2048]{1,0:T(8,128)(2,1)S(1)}, u32[]{:S(2)}, u32[]{:S(2)}) collective-permute-start(bf16[256,2048]{1,0:T(8,128)(2,1)} %collective-permute-done.27), channel_id=1, source_target_pairs={{0,8},{4,12},{8,0},{12,4},{16,24},{20,28},{24,16},{28,20},{1,9},{5... | collective-permute-start | bytes 3145736 | tf_op jit(solution)/shard_map/ppermute | solution.py:425
  173.0 26.2 %collective-permute-start.33 = (bf16[256,2048]{1,0:T(8,128)(2,1)S(1)}, bf16[256,2048]{1,0:T(8,128)(2,1)S(1)}, u32[]{:S(2)}, u32[]{:S(2)}) collective-permute-start(bf16[256,2048]{1,0:T(8,128)(2,1)S(1)} %collective-permute-done.28.refs_4_.refs_8_.refs_0_), channel_id=1, source_target_pairs={{0,2},{1,3},{2,0},{3,1},{4,6},{5,7},{6,4},{7,5},{8,10},{9,11},{10,... | collective-permute-start | bytes 3145736 | tf_op jit(solution)/shard_map/ppermute | solution.py:418
  173.5 26.5 %collective-permute-start.37 = (bf16[256,2048]{1,0:T(8,128)(2,1)S(1)}, bf16[256,2048]{1,0:T(8,128)(2,1)}, u32[]{:S(2)}, u32[]{:S(2)}) collective-permute-start(bf16[256,2048]{1,0:T(8,128)(2,1)S(1)} %collective-permute-done.28.refs_4_.refs_8_.refs_0_), channel_id=1, source_target_pairs={{0,1},{1,0},{2,3},{3,2},{4,5},{5,4},{6,7},{7,6},{8,9},{9,8},{10,11... | collective-permute-start | bytes 3145736 | tf_op jit(solution)/shard_map/ppermute | solution.py:414
  173.5 25.7 %collective-permute-start.32 = (bf16[256,2048]{1,0:T(8,128)(2,1)S(1)}, bf16[256,2048]{1,0:T(8,128)(2,1)}, u32[]{:S(2)}, u32[]{:S(2)}) collective-permute-start(bf16[256,2048]{1,0:T(8,128)(2,1)S(1)} %collective-permute-done.29.refs_8_.refs_12_.refs_4_), channel_id=1, source_target_pairs={{0,4},{4,0},{8,12},{12,8},{16,20},{20,16},{24,28},{28,24},{1,5},{5... | collective-permute-start | bytes 3145736 | tf_op jit(solution)/shard_map/ppermute | solution.py:425
  175.9 25.1 %collective-permute-start.39 = (bf16[256,2048]{1,0:T(8,128)(2,1)S(1)}, bf16[256,2048]{1,0:T(8,128)(2,1)}, u32[]{:S(2)}, u32[]{:S(2)}) collective-permute-start(bf16[256,2048]{1,0:T(8,128)(2,1)S(1)} %collective-permute-done.29.refs_8_.refs_12_.refs_4_), channel_id=1, source_target_pairs={{0,1},{1,0},{2,3},{3,2},{4,5},{5,4},{6,7},{7,6},{8,9},{9,8},{10,11... | collective-permute-start | bytes 3145736 | tf_op jit(solution)/shard_map/ppermute | solution.py:414
  199.2 15.9 %collective-permute-start.38 = (bf16[256,2048]{1,0:T(8,128)(2,1)S(1)}, bf16[256,2048]{1,0:T(8,128)(2,1)S(1)}, u32[]{:S(2)}, u32[]{:S(2)}) collective-permute-start(bf16[256,2048]{1,0:T(8,128)(2,1)S(1)} %collective-permute-done.33.refs_6_.refs_10_.refs_2_), channel_id=1, source_target_pairs={{0,1},{1,0},{2,3},{3,2},{4,5},{5,4},{6,7},{7,6},{8,9},{9,8},{10,11... | collective-permute-start | bytes 3145736 | tf_op jit(solution)/shard_map/ppermute | solution.py:414
  199.7 16.3 %collective-permute-start.41 = (bf16[256,2048]{1,0:T(8,128)(2,1)}, bf16[256,2048]{1,0:T(8,128)(2,1)S(1)}, u32[]{:S(2)}, u32[]{:S(2)}) collective-permute-start(bf16[256,2048]{1,0:T(8,128)(2,1)} %collective-permute-done.32.refs_12_.refs_16_.refs_8_), channel_id=1, source_target_pairs={{0,1},{1,0},{2,3},{3,2},{4,5},{5,4},{6,7},{7,6},{8,9},{9,8},{10,11... | collective-permute-start | bytes 3145736 | tf_op jit(solution)/shard_map/ppermute | solution.py:414
  231.7 31.2 %collective-permute-start.45 = (bf16[1024,384]{1,0:T(8,128)(2,1)S(1)}, bf16[1024,384]{1,0:T(8,128)(2,1)S(1)}, u32[]{:S(2)}, u32[]{:S(2)}) collective-permute-start(bf16[1024,384]{1,0:T(8,128)(2,1)S(1)} %get-tuple-element.405), channel_id=1, source_target_pairs={{0,4},{4,0},{8,12},{12,8},{16,20},{20,16},{24,28},{28,24},{1,5},{5... | collective-permute-start | bytes 2359304 | tf_op jit(solution)/shard_map/ppermute | solution.py:425
  232.7 37.0 %collective-permute-start.46 = (bf16[1024,384]{1,0:T(8,128)(2,1)S(1)}, bf16[1024,384]{1,0:T(8,128)(2,1)S(1)}, u32[]{:S(2)}, u32[]{:S(2)}) collective-permute-start(bf16[1024,384]{1,0:T(8,128)(2,1)S(1)} %get-tuple-element.404), channel_id=1, source_target_pairs={{0,8},{4,12},{8,0},{12,4},{16,24},{20,28},{24,16},{28,20},{1,9},{5... | collective-permute-start | bytes 2359304 | tf_op jit(solution)/shard_map/ppermute | solution.py:425
  233.6 29.3 %collective-permute-start.44 = (bf16[128,2048]{1,0:T(8,128)(2,1)}, bf16[128,2048]{1,0:T(8,128)(2,1)S(1)}, u32[]{:S(2)}, u32[]{:S(2)}) collective-permute-start(bf16[128,2048]{1,0:T(8,128)(2,1)} %get-tuple-element.263), channel_id=1, source_target_pairs={{0,16},{4,20},{8,24},{12,28},{16,0},{20,4},{24,8},{28,12},{1,17},{... | collective-permute-start | bytes 1572872 | tf_op jit(solution)/shard_map/ppermute | solution.py:425
  235.6 59.6 %collective-permute-start.43 = (bf16[128,2048]{1,0:T(8,128)(2,1)}, bf16[128,2048]{1,0:T(8,128)(2,1)}, u32[]{:S(2)}, u32[]{:S(2)}) collective-permute-start(bf16[128,2048]{1,0:T(8,128)(2,1)} %get-tuple-element.262), channel_id=1, source_target_pairs={{0,16},{4,20},{8,24},{12,28},{16,0},{20,4},{24,8},{28,12},{1,17},{... | collective-permute-start | bytes 1572872 | tf_op jit(solution)/shard_map/ppermute | solution.py:425
  236.5 67.7 %collective-permute-start.48 = (bf16[1024,384]{1,0:T(8,128)(2,1)}, bf16[1024,384]{1,0:T(8,128)(2,1)}, u32[]{:S(2)}, u32[]{:S(2)}) collective-permute-start(bf16[1024,384]{1,0:T(8,128)(2,1)} %get-tuple-element.403), channel_id=1, source_target_pairs={{0,12},{4,8},{8,4},{12,0},{16,28},{20,24},{24,20},{28,16},{1,13},{... | collective-permute-start | bytes 2359304 | tf_op jit(solution)/shard_map/ppermute | solution.py:425
  272.0 41.9 %collective-permute-start.47 = (bf16[128,2048]{1,0:T(8,128)(2,1)}, bf16[128,2048]{1,0:T(8,128)(2,1)}, u32[]{:S(2)}, u32[]{:S(2)}) collective-permute-start(bf16[128,2048]{1,0:T(8,128)(2,1)} %add_convert_fusion.10), channel_id=1, source_target_pairs={{0,8},{4,12},{8,0},{12,4},{16,24},{20,28},{24,16},{28,20},{1,9},{5... | collective-permute-start | bytes 1572872 | tf_op jit(solution)/shard_map/ppermute | solution.py:425
  275.6 58.1 %collective-permute-start.50 = (bf16[128,2048]{1,0:T(8,128)(2,1)}, bf16[128,2048]{1,0:T(8,128)(2,1)}, u32[]{:S(2)}, u32[]{:S(2)}) collective-permute-start(bf16[128,2048]{1,0:T(8,128)(2,1)} %get-tuple-element.277), channel_id=1, source_target_pairs={{0,16},{4,20},{8,24},{12,28},{16,0},{20,4},{24,8},{28,12},{1,17},{... | collective-permute-start | bytes 1572872 | tf_op jit(solution)/shard_map/ppermute | solution.py:425
  318.1 21.4 %collective-permute-start.51 = (bf16[128,2048]{1,0:T(8,128)(2,1)S(1)}, bf16[128,2048]{1,0:T(8,128)(2,1)}, u32[]{:S(2)}, u32[]{:S(2)}) collective-permute-start(bf16[128,2048]{1,0:T(8,128)(2,1)S(1)} %add_convert_fusion.9), channel_id=1, source_target_pairs={{0,8},{4,12},{8,0},{12,4},{16,24},{20,28},{24,16},{28,20},{1,9},{5... | collective-permute-start | bytes 1572872 | tf_op jit(solution)/shard_map/ppermute | solution.py:425
  319.7 24.1 %collective-permute-start.52 = (bf16[256,2048]{1,0:T(8,128)(2,1)S(1)}, bf16[256,2048]{1,0:T(8,128)(2,1)S(1)}, u32[]{:S(2)}, u32[]{:S(2)}) collective-permute-start(bf16[256,2048]{1,0:T(8,128)(2,1)S(1)} %pad_maximum_fusion.3.refs_0_.refs_2_), channel_id=1, source_target_pairs={{0,4},{4,0},{8,12},{12,8},{16,20},{20,16},{24,28},{28,24},{1,5},{5... | collective-permute-start | bytes 3145736 | tf_op jit(solution)/shard_map/ppermute | solution.py:425
  320.8 37.3 %collective-permute-start.49 = (bf16[128,2048]{1,0:T(8,128)(2,1)}, bf16[128,2048]{1,0:T(8,128)(2,1)}, u32[]{:S(2)}, u32[]{:S(2)}) collective-permute-start(bf16[128,2048]{1,0:T(8,128)(2,1)} %get-tuple-element.276), channel_id=1, source_target_pairs={{0,16},{4,20},{8,24},{12,28},{16,0},{20,4},{24,8},{28,12},{1,17},{... | collective-permute-start | bytes 1572872 | tf_op jit(solution)/shard_map/ppermute | solution.py:425
  345.5 44.7 %collective-permute-start.56 = (bf16[128,2048]{1,0:T(8,128)(2,1)}, bf16[128,2048]{1,0:T(8,128)(2,1)}, u32[]{:S(2)}, u32[]{:S(2)}) collective-permute-start(bf16[128,2048]{1,0:T(8,128)(2,1)} %get-tuple-element.289), channel_id=1, source_target_pairs={{0,16},{4,20},{8,24},{12,28},{16,0},{20,4},{24,8},{28,12},{1,17},{... | collective-permute-start | bytes 1572872 | tf_op jit(solution)/shard_map/ppermute | solution.py:425
  348.1 20.6 %collective-permute-start.53 = (bf16[128,2048]{1,0:T(8,128)(2,1)S(1)}, bf16[128,2048]{1,0:T(8,128)(2,1)S(1)}, u32[]{:S(2)}, u32[]{:S(2)}) collective-permute-start(bf16[128,2048]{1,0:T(8,128)(2,1)S(1)} %add_convert_fusion.8), channel_id=1, source_target_pairs={{0,8},{4,12},{8,0},{12,4},{16,24},{20,28},{24,16},{28,20},{1,9},{5... | collective-permute-start | bytes 1572872 | tf_op jit(solution)/shard_map/ppermute | solution.py:425
  349.6 22.7 %collective-permute-start.54 = (bf16[256,2048]{1,0:T(8,128)(2,1)S(1)}, bf16[256,2048]{1,0:T(8,128)(2,1)S(1)}, u32[]{:S(2)}, u32[]{:S(2)}) collective-permute-start(bf16[256,2048]{1,0:T(8,128)(2,1)S(1)} %pad_maximum_fusion.4.refs_1_.refs_3_), channel_id=1, source_target_pairs={{0,4},{4,0},{8,12},{12,8},{16,20},{20,16},{24,28},{28,24},{1,5},{5... | collective-permute-start | bytes 3145736 | tf_op jit(solution)/shard_map/ppermute | solution.py:425
  374.0 16.2 %collective-permute-start.57 = (bf16[128,2048]{1,0:T(8,128)(2,1)S(1)}, bf16[128,2048]{1,0:T(8,128)(2,1)S(1)}, u32[]{:S(2)}, u32[]{:S(2)}) collective-permute-start(bf16[128,2048]{1,0:T(8,128)(2,1)S(1)} %add_convert_fusion.7), channel_id=1, source_target_pairs={{0,8},{4,12},{8,0},{12,4},{16,24},{20,28},{24,16},{28,20},{1,9},{5... | collective-permute-start | bytes 1572872 | tf_op jit(solution)/shard_map/ppermute | solution.py:425
  375.5 21.1 %collective-permute-start.58 = (bf16[256,2048]{1,0:T(8,128)(2,1)S(1)}, bf16[256,2048]{1,0:T(8,128)(2,1)S(1)}, u32[]{:S(2)}, u32[]{:S(2)}) collective-permute-start(bf16[256,2048]{1,0:T(8,128)(2,1)S(1)} %pad_maximum_fusion.5.refs_1_.refs_3_), channel_id=1, source_target_pairs={{0,4},{4,0},{8,12},{12,8},{16,20},{20,16},{24,28},{28,24},{1,5},{5... | collective-permute-start | bytes 3145736 | tf_op jit(solution)/shard_map/ppermute | solution.py:425
  388.8 34.1 %collective-permute-start.55 = (bf16[512,512]{1,0:T(8,128)(2,1)}, bf16[512,512]{1,0:T(8,128)(2,1)}, u32[]{:S(2)}, u32[]{:S(2)}) collective-permute-start(bf16[512,512]{1,0:T(8,128)(2,1)} %get-tuple-element.288), channel_id=1, source_target_pairs={{0,16},{4,20},{8,24},{12,28},{16,0},{20,4},{24,8},{28,12},{1,17},{... | collective-permute-start | bytes 1572872 | tf_op jit(solution)/shard_map/ppermute | solution.py:425
  396.6 43.9 %collective-permute-start.61 = (bf16[512,512]{1,0:T(8,128)(2,1)}, bf16[512,512]{1,0:T(8,128)(2,1)}, u32[]{:S(2)}, u32[]{:S(2)}) collective-permute-start(bf16[512,512]{1,0:T(8,128)(2,1)} %get-tuple-element.303), channel_id=1, source_target_pairs={{0,16},{4,20},{8,24},{12,28},{16,0},{20,4},{24,8},{28,12},{1,17},{... | collective-permute-start | bytes 1572872 | tf_op jit(solution)/shard_map/ppermute | solution.py:425
  399.9 23.1 %collective-permute-start.59 = (bf16[128,2048]{1,0:T(8,128)(2,1)}, bf16[128,2048]{1,0:T(8,128)(2,1)}, u32[]{:S(2)}, u32[]{:S(2)}) collective-permute-start(bf16[128,2048]{1,0:T(8,128)(2,1)} %add_convert_fusion.6), channel_id=1, source_target_pairs={{0,8},{4,12},{8,0},{12,4},{16,24},{20,28},{24,16},{28,20},{1,9},{5... | collective-permute-start | bytes 1572872 | tf_op jit(solution)/shard_map/ppermute | solution.py:425
  402.0 20.9 %collective-permute-start.60 = (bf16[256,2048]{1,0:T(8,128)(2,1)}, bf16[256,2048]{1,0:T(8,128)(2,1)}, u32[]{:S(2)}, u32[]{:S(2)}) collective-permute-start(bf16[256,2048]{1,0:T(8,128)(2,1)} %pad_maximum_fusion.6.refs_1_.refs_3_), channel_id=1, source_target_pairs={{0,4},{4,0},{8,12},{12,8},{16,20},{20,16},{24,28},{28,24},{1,5},{5... | collective-permute-start | bytes 3145736 | tf_op jit(solution)/shard_map/ppermute | solution.py:425
  424.3 21.5 %collective-permute-start.62 = (bf16[512,512]{1,0:T(8,128)(2,1)S(1)}, bf16[512,512]{1,0:T(8,128)(2,1)S(1)}, u32[]{:S(2)}, u32[]{:S(2)}) collective-permute-start(bf16[512,512]{1,0:T(8,128)(2,1)S(1)} %add_convert_fusion.5), channel_id=1, source_target_pairs={{0,8},{4,12},{8,0},{12,4},{16,24},{20,28},{24,16},{28,20},{1,9},{5... | collective-permute-start | bytes 1572872 | tf_op jit(solution)/shard_map/ppermute | solution.py:425
  426.1 23.4 %collective-permute-start.63 = (bf16[256,2048]{1,0:T(8,128)(2,1)S(1)}, bf16[256,2048]{1,0:T(8,128)(2,1)S(1)}, u32[]{:S(2)}, u32[]{:S(2)}) collective-permute-start(bf16[256,2048]{1,0:T(8,128)(2,1)S(1)} %pad_maximum_fusion.7.refs_0_.refs_2_), channel_id=1, source_target_pairs={{0,4},{4,0},{8,12},{12,8},{16,20},{20,16},{24,28},{28,24},{1,5},{5... | collective-permute-start | bytes 3145736 | tf_op jit(solution)/shard_map/ppermute | solution.py:425
  437.4 29.4 %collective-permute-start.65 = (bf16[512,512]{1,0:T(8,128)(2,1)S(1)}, bf16[512,512]{1,0:T(8,128)(2,1)S(1)}, u32[]{:S(2)}, u32[]{:S(2)}) collective-permute-start(bf16[512,512]{1,0:T(8,128)(2,1)S(1)} %copy-done.61), channel_id=1, source_target_pairs={{0,16},{4,20},{8,24},{12,28},{16,0},{20,4},{24,8},{28,12},{1,17},{... | collective-permute-start | bytes 1572872 | tf_op jit(solution)/shard_map/ppermute | solution.py:425
  450.8 21.4 %collective-permute-start.66 = (bf16[512,512]{1,0:T(8,128)(2,1)S(1)}, bf16[512,512]{1,0:T(8,128)(2,1)S(1)}, u32[]{:S(2)}, u32[]{:S(2)}) collective-permute-start(bf16[512,512]{1,0:T(8,128)(2,1)S(1)} %add_convert_fusion.4), channel_id=1, source_target_pairs={{0,8},{4,12},{8,0},{12,4},{16,24},{20,28},{24,16},{28,20},{1,9},{5... | collective-permute-start | bytes 1572872 | tf_op jit(solution)/shard_map/ppermute | solution.py:425
  452.7 22.6 %collective-permute-start.67 = (bf16[1024,512]{1,0:T(8,128)(2,1)S(1)}, bf16[1024,512]{1,0:T(8,128)(2,1)S(1)}, u32[]{:S(2)}, u32[]{:S(2)}) collective-permute-start(bf16[1024,512]{1,0:T(8,128)(2,1)S(1)} %pad_maximum_fusion.8.refs_0_.refs_2_), channel_id=1, source_target_pairs={{0,4},{4,0},{8,12},{12,8},{16,20},{20,16},{24,28},{28,24},{1,5},{5... | collective-permute-start | bytes 3145736 | tf_op jit(solution)/shard_map/ppermute | solution.py:425
  454.1 21.3 %collective-permute-start.68 = (bf16[2,256,2048]{2,1,0:T(8,128)(2,1)S(1)}, bf16[2,256,2048]{2,1,0:T(8,128)(2,1)S(1)}, u32[]{:S(2)}, u32[]{:S(2)}) collective-permute-start(bf16[2,256,2048]{2,1,0:T(8,128)(2,1)S(1)} %fusion.31), channel_id=1, source_target_pairs={{0,1},{1,0},{2,3},{3,2},{4,5},{5,4},{6,7},{7,6},{8,9},{9,8},{10,11... | collective-permute-start | bytes 6291464 | tf_op jit(solution)/shard_map/ppermute | solution.py:414
  475.4 25.9 %collective-permute-start.70 = (bf16[1024,512]{1,0:T(8,128)(2,1)S(1)}, bf16[1024,512]{1,0:T(8,128)(2,1)S(1)}, u32[]{:S(2)}, u32[]{:S(2)}) collective-permute-start(bf16[1024,512]{1,0:T(8,128)(2,1)S(1)} %pad_maximum_fusion.9.refs_1_.refs_3_), channel_id=1, source_target_pairs={{0,4},{4,0},{8,12},{12,8},{16,20},{20,16},{24,28},{28,24},{1,5},{5... | collective-permute-start | bytes 3145736 | tf_op jit(solution)/shard_map/ppermute | solution.py:425
  477.1 24.2 %collective-permute-start.71 = (bf16[256,2048]{1,0:T(8,128)(2,1)S(1)}, bf16[256,2048]{1,0:T(8,128)(2,1)S(1)}, u32[]{:S(2)}, u32[]{:S(2)}) collective-permute-start(bf16[256,2048]{1,0:T(8,128)(2,1)S(1)} %fusion.45), channel_id=1, source_target_pairs={{0,2},{1,3},{2,0},{3,1},{4,6},{5,7},{6,4},{7,5},{8,10},{9,11},{10,... | collective-permute-start | bytes 3145736 | tf_op jit(solution)/shard_map/ppermute | solution.py:422
  478.7 22.2 %collective-permute-start.64 = (bf16[512,512]{1,0:T(8,128)(2,1)S(1)}, bf16[512,512]{1,0:T(8,128)(2,1)S(1)}, u32[]{:S(2)}, u32[]{:S(2)}) collective-permute-start(bf16[512,512]{1,0:T(8,128)(2,1)S(1)} %copy-done.60), channel_id=1, source_target_pairs={{0,16},{4,20},{8,24},{12,28},{16,0},{20,4},{24,8},{28,12},{1,17},{... | collective-permute-start | bytes 1572872 | tf_op jit(solution)/shard_map/ppermute | solution.py:425
  480.7 20.6 %collective-permute-start.69 = (bf16[512,512]{1,0:T(8,128)(2,1)S(1)}, bf16[512,512]{1,0:T(8,128)(2,1)S(1)}, u32[]{:S(2)}, u32[]{:S(2)}) collective-permute-start(bf16[512,512]{1,0:T(8,128)(2,1)S(1)} %add_convert_fusion.3), channel_id=1, source_target_pairs={{0,8},{4,12},{8,0},{12,4},{16,24},{20,28},{24,16},{28,20},{1,9},{5... | collective-permute-start | bytes 1572872 | tf_op jit(solution)/shard_map/ppermute | solution.py:425
  501.4 24.7 %collective-permute-start.73 = (bf16[1024,512]{1,0:T(8,128)(2,1)S(1)}, bf16[1024,512]{1,0:T(8,128)(2,1)S(1)}, u32[]{:S(2)}, u32[]{:S(2)}) collective-permute-start(bf16[1024,512]{1,0:T(8,128)(2,1)S(1)} %pad_maximum_fusion.10.refs_1_.refs_3_), channel_id=1, source_target_pairs={{0,4},{4,0},{8,12},{12,8},{16,20},{20,16},{24,28},{28,24},{1,5},{5... | collective-permute-start | bytes 3145736 | tf_op jit(solution)/shard_map/ppermute | solution.py:425
  501.9 21.6 %collective-permute-start.72 = (bf16[512,512]{1,0:T(8,128)(2,1)S(1)}, bf16[512,512]{1,0:T(8,128)(2,1)S(1)}, u32[]{:S(2)}, u32[]{:S(2)}) collective-permute-start(bf16[512,512]{1,0:T(8,128)(2,1)S(1)} %add_convert_fusion.2), channel_id=1, source_target_pairs={{0,8},{4,12},{8,0},{12,4},{16,24},{20,28},{24,16},{28,20},{1,9},{5... | collective-permute-start | bytes 1572872 | tf_op jit(solution)/shard_map/ppermute | solution.py:425
  502.0 19.4 %collective-permute-start.75 = (bf16[512,384]{1,0:T(8,128)(2,1)S(1)}, bf16[512,384]{1,0:T(8,128)(2,1)S(1)}, u32[]{:S(2)}, u32[]{:S(2)}) collective-permute-start(bf16[512,384]{1,0:T(8,128)(2,1)S(1)} %get-tuple-element.329), channel_id=1, source_target_pairs={{0,16},{4,20},{8,24},{12,28},{16,0},{20,4},{24,8},{28,12},{1,17},{... | collective-permute-start | bytes 1179656 | tf_op jit(solution)/shard_map/ppermute | solution.py:425
  526.2 23.8 %collective-permute-start.77 = (bf16[1024,512]{1,0:T(8,128)(2,1)S(1)}, bf16[1024,512]{1,0:T(8,128)(2,1)S(1)}, u32[]{:S(2)}, u32[]{:S(2)}) collective-permute-start(bf16[1024,512]{1,0:T(8,128)(2,1)S(1)} %pad_maximum_fusion.11.refs_1_.refs_3_), channel_id=1, source_target_pairs={{0,4},{4,0},{8,12},{12,8},{16,20},{20,16},{24,28},{28,24},{1,5},{5... | collective-permute-start | bytes 3145736 | tf_op jit(solution)/shard_map/ppermute | solution.py:425
  526.5 18.3 %collective-permute-start.76 = (bf16[512,384]{1,0:T(8,128)(2,1)S(1)}, bf16[512,384]{1,0:T(8,128)(2,1)S(1)}, u32[]{:S(2)}, u32[]{:S(2)}) collective-permute-start(bf16[512,384]{1,0:T(8,128)(2,1)S(1)} %get-tuple-element.334), channel_id=1, source_target_pairs={{0,16},{4,20},{8,24},{12,28},{16,0},{20,4},{24,8},{28,12},{1,17},{... | collective-permute-start | bytes 1179656 | tf_op jit(solution)/shard_map/ppermute | solution.py:425
  526.7 18.5 %collective-permute-start.79 = (bf16[512,384]{1,0:T(8,128)(2,1)S(1)}, bf16[512,384]{1,0:T(8,128)(2,1)S(1)}, u32[]{:S(2)}, u32[]{:S(2)}) collective-permute-start(bf16[512,384]{1,0:T(8,128)(2,1)S(1)} %add_convert_fusion.13), channel_id=1, source_target_pairs={{0,8},{4,12},{8,0},{12,4},{16,24},{20,28},{24,16},{28,20},{1,9},{5... | collective-permute-start | bytes 1179656 | tf_op jit(solution)/shard_map/ppermute | solution.py:425
  550.0 18.7 %collective-permute-start.83 = (bf16[1024,384]{1,0:T(8,128)(2,1)S(1)}, bf16[1024,384]{1,0:T(8,128)(2,1)S(1)}, u32[]{:S(2)}, u32[]{:S(2)}) collective-permute-start(bf16[1024,384]{1,0:T(8,128)(2,1)S(1)} %pad_maximum_fusion.12.refs_0_.refs_2_), channel_id=1, source_target_pairs={{0,4},{4,0},{8,12},{12,8},{16,20},{20,16},{24,28},{28,24},{1,5},{5... | collective-permute-start | bytes 2359304 | tf_op jit(solution)/shard_map/ppermute | solution.py:425
  550.4 17.4 %collective-permute-start.80 = (bf16[512,384]{1,0:T(8,128)(2,1)S(1)}, bf16[512,384]{1,0:T(8,128)(2,1)S(1)}, u32[]{:S(2)}, u32[]{:S(2)}) collective-permute-start(bf16[512,384]{1,0:T(8,128)(2,1)S(1)} %get-tuple-element.344), channel_id=1, source_target_pairs={{0,16},{4,20},{8,24},{12,28},{16,0},{20,4},{24,8},{28,12},{1,17},{... | collective-permute-start | bytes 1179656 | tf_op jit(solution)/shard_map/ppermute | solution.py:425
  550.6 18.1 %collective-permute-start.81 = (bf16[512,384]{1,0:T(8,128)(2,1)S(1)}, bf16[512,384]{1,0:T(8,128)(2,1)S(1)}, u32[]{:S(2)}, u32[]{:S(2)}) collective-permute-start(bf16[512,384]{1,0:T(8,128)(2,1)S(1)} %add_convert_fusion.12), channel_id=1, source_target_pairs={{0,8},{4,12},{8,0},{12,4},{16,24},{20,28},{24,16},{28,20},{1,9},{5... | collective-permute-start | bytes 1179656 | tf_op jit(solution)/shard_map/ppermute | solution.py:425
  568.8 18.6 %collective-permute-start.86 = (bf16[1024,384]{1,0:T(8,128)(2,1)S(1)}, bf16[1024,384]{1,0:T(8,128)(2,1)S(1)}, u32[]{:S(2)}, u32[]{:S(2)}) collective-permute-start(bf16[1024,384]{1,0:T(8,128)(2,1)S(1)} %pad_maximum_fusion.13.refs_1_.refs_3_), channel_id=1, source_target_pairs={{0,4},{4,0},{8,12},{12,8},{16,20},{20,16},{24,28},{28,24},{1,5},{5... | collective-permute-start | bytes 2359304 | tf_op jit(solution)/shard_map/ppermute | solution.py:425
  570.3 16.2 %collective-permute-start.85 = (bf16[512,384]{1,0:T(8,128)(2,1)S(1)}, bf16[512,384]{1,0:T(8,128)(2,1)S(1)}, u32[]{:S(2)}, u32[]{:S(2)}) collective-permute-start(bf16[512,384]{1,0:T(8,128)(2,1)S(1)} %add_convert_fusion.11), channel_id=1, source_target_pairs={{0,8},{4,12},{8,0},{12,4},{16,24},{20,28},{24,16},{28,20},{1,9},{5... | collective-permute-start | bytes 1179656 | tf_op jit(solution)/shard_map/ppermute | solution.py:425
  587.5 18.2 %collective-permute-start.90 = (bf16[1024,384]{1,0:T(8,128)(2,1)S(1)}, bf16[1024,384]{1,0:T(8,128)(2,1)S(1)}, u32[]{:S(2)}, u32[]{:S(2)}) collective-permute-start(bf16[1024,384]{1,0:T(8,128)(2,1)S(1)} %pad_maximum_fusion.14.refs_1_.refs_3_), channel_id=1, source_target_pairs={{0,4},{4,0},{8,12},{12,8},{16,20},{20,16},{24,28},{28,24},{1,5},{5... | collective-permute-start | bytes 2359304 | tf_op jit(solution)/shard_map/ppermute | solution.py:425
  (121 other events, 1318.7 us)

commit v8 on v7

--- a/solution.py
+++ b/solution.py
@@ -15,6 +15,7 @@
 EPSILON = 1e-05
 BF = jnp.bfloat16
 F32 = jnp.float32
+VMEM = 60 << 20
 SMALL = pl.CostEstimate(flops=1 << 20, bytes_accessed=1 << 16, transcendentals=0)
 
 
@@ -105,7 +106,7 @@
         out_specs=pl.BlockSpec((rows, HD), lambda j: (part, j)),
         out_shape=jax.ShapeDtypeStruct((length, columns), BF),
         input_output_aliases={6: 0} if part else {},
-        compiler_params=pltpu.CompilerParams(vmem_limit_bytes=40 << 20),
+        compiler_params=pltpu.CompilerParams(vmem_limit_bytes=VMEM),
         cost_estimate=SMALL,
         name="qkv_rotary",
     )(normed, weight, bias[None, :], table, table, table, *([whole] if part else []))
@@ -157,7 +158,7 @@
             jax.ShapeDtypeStruct((length, heads * HD), BF),
             jax.ShapeDtypeStruct((heads, length, 1), F32),
         ],
-        compiler_params=pltpu.CompilerParams(vmem_limit_bytes=32 << 20),
+        compiler_params=pltpu.CompilerParams(vmem_limit_bytes=VMEM),
         cost_estimate=SMALL,
         name="attend",
     )(prefix, qkv, qkv, qkv, spots[:, None], spots[None, :])
@@ -221,7 +222,7 @@
             scratch_shapes=[pltpu.VMEM((length, HD), F32), pltpu.VMEM((length, HD), F32)],
         ),
         out_shape=jax.ShapeDtypeStruct((length, heads * 3 * HD), BF),
-        compiler_params=pltpu.CompilerParams(vmem_limit_bytes=48 << 20),
+        compiler_params=pltpu.CompilerParams(vmem_limit_bytes=VMEM),
         cost_estimate=SMALL,
         name="attend_back",
     )(prefix, qkv, qkv, qkv, grad_context, log_total, spots[:, None], spots[None, :], table, table, table)
@@ -256,7 +257,7 @@
         ),
         out_shape=jax.ShapeDtypeStruct(shape, F32),
         input_output_aliases={} if first else {1: 0},
-        compiler_params=pltpu.CompilerParams(vmem_limit_bytes=24 << 20),
+        compiler_params=pltpu.CompilerParams(vmem_limit_bytes=VMEM),
         cost_estimate=SMALL,
         name="place_quarters",
     )(quarter.reshape(1), *operands)
@@ -293,7 +294,7 @@
         out_specs=[pl.BlockSpec((rows, width), lambda i: (i + skip, 0))] * 2,
         out_shape=[shape, shape],
         input_output_aliases={4 + count: 0, 5 + count: 1} if into else {},
-        compiler_params=pltpu.CompilerParams(vmem_limit_bytes=48 << 20),
+        compiler_params=pltpu.CompilerParams(vmem_limit_bytes=VMEM),
         cost_estimate=SMALL,
         name="both_norms",
     )(*gains, *blocks, *into)
@@ -345,7 +346,7 @@
             scratch_shapes=[pltpu.VMEM((left, tokens), BF), pltpu.VMEM((tokens, tile), BF)],
         ),
         out_shape=[jax.ShapeDtypeStruct((size, width), BF) for size in sizes],
-        compiler_params=pltpu.CompilerParams(vmem_limit_bytes=56 << 20),
+        compiler_params=pltpu.CompilerParams(vmem_limit_bytes=VMEM),
         cost_estimate=SMALL,
         name="outer_blocks",
     )(quarter.reshape(1), *[a for a, *_ in lefts], *rights)
@@ -374,7 +375,7 @@
         + [pl.BlockSpec((rows, width), lambda i: (0, 0))] * count,
         out_specs=pl.BlockSpec((rows, units), lambda i: (i, 0)),
         out_shape=jax.ShapeDtypeStruct((count * rows, units), BF),
-        compiler_params=pltpu.CompilerParams(vmem_limit_bytes=56 << 20),
+        compiler_params=pltpu.CompilerParams(vmem_limit_bytes=VMEM),
         cost_estimate=SMALL,
         name="back_blocks",
     )(weight, slope, *blocks)
@@ -594,19 +595,18 @@
     for block in grad_y:
         grad_blocks += [block, to_core(block)]
     grad_near = jnp.concatenate(grad_blocks, axis=0)
-    hidden_pre = jnp.concatenate([pre_own, pre_rest], axis=0)
-    grad_inner = (contract(grad_near, fc2_weight, 1, 1) * exact_gelu(hidden_pre)[1]).astype(BF)
     grad_context = contract(grad_near, out_weight, 1, 1).astype(BF)
-    grad_inner, grad_context, grad_near, grad_second = meet(
-        grad_inner, grad_context, grad_near, grad_second
-    )
+    grad_qkv = attend_back(qkv_low, grad_context, log_total, prefix_len, spots, table)
+    grad_qkv, grad_near, grad_second = meet(grad_qkv, grad_near, grad_second)
 
     grad_last = last_far(grad_second)
     corner, beside, across = grad_second
     ahead = [grad_first[0]] + beside + [grad_first[1]] + across + [corner]
     mates = [to_core(block) for block in ahead]
-    grad_qkv = attend_back(qkv_low, grad_context, log_total, prefix_len, spots, table)
-    grad_qkv, grad_last, mates = meet(grad_qkv, grad_last, mates)
+    swapped = [flip(quarter_of(grad_qkv, 1, quarter ^ m), m) for m in (1, 2)]
+    hidden_pre = jnp.concatenate([pre_own, pre_rest], axis=0)
+    grad_inner = (contract(grad_near, fc2_weight, 1, 1) * exact_gelu(hidden_pre)[1]).astype(BF)
+    grad_inner, grad_last, mates = meet(grad_inner, grad_last, mates)
 
     grad_last = [jnp.concatenate(pair, axis=0) for pair in grad_last]
     ahead += grad_last
@@ -638,9 +638,7 @@
         results.setdefault(name, []).append((near, far))
 
     def swap_walk(v, into):
-        got = yield [flipped(quarter_of(v, 1, quarter ^ m), m) for m in (1, 2)], 1
-        into.extend(got)
-        got = yield [flipped(quarter_of(v, 1, quarter ^ 3), 3)], 1
+        got = yield [flipped(quarter_of(v, 1, quarter ^ 3), 3)], 2
         into.extend(got)
 
     def last_walk(kept, mates, parts, others, into):
@@ -740,8 +738,7 @@
     chunk = half // 2
     kept_columns = context.shape[1] // 4
     enqueue("fc2", *outer_blocks(hidden_lefts(0), rights, [chunk] * 2, quarter))
-    turn()
-    grad_qkv_far = []
+    grad_qkv_far = list(turn(*swapped))
     walk(swap_walk(gate(grad_qkv), grad_qkv_far))
     lefts = hidden_lefts(1)
     for index, piece in enumerate([context_quarter] + context_far):

time: 641 us -> 674 us (1.051)
  waiting for transfers between devices: 179 us -> 130 us
  Pallas kernels: 138 us -> 171 us
  other arithmetic: 56 us -> 77.1 us
  starting transfers between devices: 94.2 us -> 106 us
  local copies, waits for them, and re-layouts: 46.2 us -> 57.2 us
    ppermute x69, waiting for transfers between devices: 175 us -> 127 us  [flip(): return lax.ppermute(v, 'dp', [(d, d ^ mask) for d in range(dp)])]
    pallas_call x15, Pallas kernels: 35 us -> 55 us  [place_quarters(): pl.pallas_call(place_kernel, grid_spec=pltpu.PrefetchScalarGridSpec(num_s...]
    ppermute x69, starting transfers between devices: 82.2 us -> 94 us  [flip(): return lax.ppermute(v, 'dp', [(d, d ^ mask) for d in range(dp)])]
    pallas_call x2, Pallas kernels: 10.8 us -> 17.7 us  [project_qkv(): pl.pallas_call(qkv_kernel, grid=(columns // HD,), in_specs=[pl.BlockSpec(...]
    unnamed x180 -> x184, local copies, waits for them, and re-layouts: 18.5 us -> 13 us
  transfers between devices with their start and end apart: 98 -> 98, of which waited for: 44 -> 34; matrix products, arithmetic and copies ran while one was open for 29% -> 33% of each run, Pallas kernels for 20% -> 25%
where the time goes in v8:
time: 674 us; the launch traced here: 663 us
  Pallas kernels  171 us (25%)
  waiting for transfers between devices  130 us (19%)
  matrix products  115 us (17%)
  starting transfers between devices  106 us (16%)
  other arithmetic  77.1 us (11%)
  local copies, waits for them, and re-layouts  57.2 us (8%)
    ppermute x69, waiting for transfers between devices, flip(): return lax.ppermute(v, 'dp', [(d, d ^ mask) for d in range(dp)])  127 us
    ppermute x69, starting transfers between devices, flip(): return lax.ppermute(v, 'dp', [(d, d ^ mask) for d in range(dp)])  94 us
    dot_general x10, matrix products, contract(): lax.dot_general(left_side, right_side, (((left_dim,), (right_dim,)), ((),...  69 us
    pallas_call x15, Pallas kernels, place_quarters(): pl.pallas_call(place_kernel, grid_spec=pltpu.PrefetchScalarGridSpec(num_s...  55 us
    pallas_call x4, Pallas kernels, both_norms(): pl.pallas_call(functools.partial(norms_kernel, count), grid=(count,), in_...  32.9 us
    pallas_call x2, Pallas kernels, outer_blocks(): pl.pallas_call(functools.partial(outer_kernel, len(lefts), pieces, len(si...  23.3 us
    dot_general x2, matrix products, units(): jnp.dot(normed, fc1_weight, preferred_element_type=F32)  19.6 us
    convert_element_type x15, other arithmetic, travel(): low = (low.astype(F32) + got.astype(F32)).astype(BF)  18.8 us
  transfers between devices with their start and end apart: 98, of which 34 were waited for; matrix products, arithmetic and copies ran while one was open for 33% of the time, Pallas kernels for 25%

profile of v8, /device:TPU:0, one launch (start us, length us, event | category | flops | bytes accessed | tf_op | source)
XLA Modules:
  0.0 663.1 jit_solution(18333508994423090887)
XLA Ops:
  15.3 5.1 both_norms.4
  26.1 9.6 %multiply_convert_fusion.2 = (bf16[512,2048]{1,0:T(8,128)(2,1)}, f32[512,2048]{1,0:T(8,128)}) fusion(f32[2048]{0:T(1024)S(1)} %convert_element_type.245, bf16[512,2048]{1,0:T(8,128)(2,1)} %get-tuple-element.200, bf16[2048,2048]{1,0:T(8,128)(2,1)} %param.32), kind=kOutput, calls=%fused_computation.38 | convolution fusion | flops 4301258752 | bytes 16785408 | tf_op jit(solution)/shard_map/dot_general | solution.py:473
  35.7 8.8 %qkv_rotary.2.refs_0_ = bf16[1024,1536]{1,0:T(8,128)(2,1)} custom-call(bf16[512,2048]{1,0:T(8,128)(2,1)} %get-tuple-element.202.x_ref, bf16[2048,1536]{1,0:T(8,128)(2,1)} %w_ref.3, bf16[1,1536]{1,0:T(2,128)(2,1)} %broadcast_in_dim.20.b_ref, f32[1024,384]{1,0:T(8,128)} %pad_maximum_fusion.2.keep_ref.up_ref.down_ref, ...), custom_call_target="tpu_custom_call" | custom-call | flops 1048576 | bytes 65536 | tf_op jit(solution)/shard_map/qkv_rotary/pallas_call | solution.py:96
  51.3 5.1 both_norms.5
  56.4 8.9 %qkv_rotary.3.q_ref.k_ref.v_ref = bf16[1024,1536]{1,0:T(8,128)(2,1)} custom-call(bf16[512,2048]{1,0:T(8,128)(2,1)} %get-tuple-element.207.x_ref, bf16[2048,1536]{1,0:T(8,128)(2,1)} %w_ref.3, bf16[1,1536]{1,0:T(2,128)(2,1)} %broadcast_in_dim.20.b_ref, f32[1024,384]{1,0:T(8,128)} %pad_maximum_fusion.2.keep_ref.up_ref.down_ref, ...), custom_call_target="tpu_custom_call", output_to_operand_aliasing={{}: (6, {})} | custom-call | flops 1048576 | bytes 65536 | tf_op jit(solution)/shard_map/qkv_rotary/pallas_call | solution.py:96
  65.3 11.3 %attend.1 = (bf16[1024,512]{1,0:T(8,128)(2,1)}, f32[2,1024,1]{2,1,0:T(8,128)}) custom-call(s32[1]{0:T(128)S(6)} %copy.79.prefix_ref, bf16[1024,1536]{1,0:T(8,128)(2,1)} %qkv_rotary.3.q_ref.k_ref.v_ref, bf16[1024,1536]{1,0:T(8,128)(2,1)} %qkv_rotary.3.q_ref.k_ref.v_ref, bf16[1024,1536]{1,0:T(8,128)(2,1)} %qkv_rotary.3.q_ref.k_ref.v_ref, ...), custom_call_target="tpu_custom_call" | custom-call | flops 1048576 | bytes 65536 | tf_op jit(solution)/shard_map/attend/pallas_call | solution.py:140
  81.6 9.9 %multiply_convert_fusion.1 = (bf16[512,2048]{1,0:T(8,128)(2,1)S(1)}, f32[512,2048]{1,0:T(8,128)}) fusion(f32[2048]{0:T(1024)S(1)} %convert_element_type.245, bf16[512,2048]{1,0:T(8,128)(2,1)} %get-tuple-element.210, bf16[2048,2048]{1,0:T(8,128)(2,1)} %param.32), kind=kOutput, calls=%fused_computation.37 | convolution fusion | flops 4301258752 | bytes 16785408 | tf_op jit(solution)/shard_map/dot_general | solution.py:473
  93.4 4.5 fusion.67
  100.5 4.5 fusion.68
  106.6 3.3 convolution_add_fusion.1
  116.6 17.2 %both_norms.6 = (bf16[3072,2048]{1,0:T(8,128)(2,1)}, bf16[3072,2048]{1,0:T(8,128)(2,1)}) custom-call(bf16[1,2048]{1,0:T(2,128)(2,1)} %broadcast_in_dim.16.refs_0_, bf16[1,2048]{1,0:T(2,128)(2,1)} %broadcast_in_dim.17.refs_1_, bf16[1,2048]{1,0:T(2,128)(2,1)} %broadcast_in_dim.18.refs_2_, bf16[1,2048]{1,0:T(2,128)(2,1)} %broadcast_in_dim.19.refs_3_, ...), custom_call_target="tpu_custom_call" | custom-call | flops 1048576 | bytes 65536 | tf_op jit(solution)/shard_map/both_norms/pallas_call | solution.py:288
  143.6 5.5 both_norms.7
  150.3 4.2 fusion.30
  154.5 4.3 fusion.62
  162.9 13.1 %fusion.21 = (f32[3072,512]{1,0:T(8,128)}, bf16[3072,512]{1,0:T(8,128)(2,1)}) fusion(f32[512]{0:T(512)S(1)} %dynamic-slice_convert_fusion, bf16[3072,2048]{1,0:T(8,128)(2,1)S(1)} %copy-done.16, bf16[2048,2048]{1,0:T(8,128)(2,1)} %param.32, s32[]{:T(128)S(6)} %select_n.81), kind=kOutput, calls=%fused_computation.28 | convolution fusion | flops 6459752448 | bytes 24119300 | tf_op jit(solution)/shard_map/dot_general | solution.py:584
  177.6 3.2 constant_dynamic-slice_fusion.6.weight_ref
  180.8 2.9 collective-permute-done.27
  190.6 3.4 convolution_convert_fusion.g_ref
  194.0 13.1 %attend_back.1 = bf16[1024,1536]{1,0:T(8,128)(2,1)} custom-call(s32[1]{0:T(128)S(6)} %copy.79.prefix_ref, bf16[1024,1536]{1,0:T(8,128)(2,1)} %qkv_rotary.3.q_ref.k_ref.v_ref, bf16[1024,1536]{1,0:T(8,128)(2,1)} %qkv_rotary.3.q_ref.k_ref.v_ref, bf16[1024,1536]{1,0:T(8,128)(2,1)} %qkv_rotary.3.q_ref.k_ref.v_ref, ...), custom_call_target="tpu_custom_call" | custom-call | flops 1048576 | bytes 65536 | tf_op jit(solution)/shard_map/attend_back/pallas_call | solution.py:206
  207.1 6.6 %collective-permute-done.32.refs_12_.refs_16_.refs_8_ = bf16[256,2048]{1,0:T(8,128)(2,1)} collective-permute-done((bf16[256,2048]{1,0:T(8,128)(2,1)}, bf16[256,2048]{1,0:T(8,128)(2,1)}, u32[]{:S(2)}, u32[]{:S(2)}) %collective-permute-start.32) | collective-permute-done | bytes 1048608 | tf_op jit(solution)/shard_map/ppermute | solution.py:426
  218.1 17.1 %fusion.17 = bf16[1024,2048]{1,0:T(8,128)(2,1)} fusion(f32[512,2048]{1,0:T(8,128)} %get-tuple-element.434, f32[512,2048]{1,0:T(8,128)} %get-tuple-element.432, bf16[1024,2048]{1,0:T(8,128)(2,1)} %copy-done.9, bf16[2048,2048]{1,0:T(8,128)(2,1)} %param.34), kind=kOutput, calls=%fused_computation.21 | convolution fusion | flops 8613003264 | bytes 25165824 | tf_op jit(solution)/shard_map/dot_general | solution.py:36
  237.8 3.1 constant_dynamic-slice_fusion
  243.5 10.7 %outer_blocks.2 = (bf16[128,2048]{1,0:T(8,128)(2,1)}, bf16[128,2048]{1,0:T(8,128)(2,1)}) custom-call(s32[1]{0:T(128)} %bitcast.9._.quarter_ref, bf16[512,2048]{1,0:T(8,128)(2,1)} %get-tuple-element.217.refs_0_, bf16[512,2048]{1,0:T(8,128)(2,1)} %copy-done.29, bf16[3072,512]{1,0:T(8,128)(2,1)} %get-tuple-element.245.refs_2_, bf16[1024,2048]{1,0:T(8,128)(2,1)} %copy-done.9, ...), custom_call_target="tpu_custom_call" | custom-call | flops 1048576 | bytes 65536 | tf_op jit(solution)/shard_map/outer_blocks/pallas_call | solution.py:338
  254.2 6.8 %collective-permute-done.43 = bf16[1024,384]{1,0:T(8,128)(2,1)} collective-permute-done((bf16[1024,384]{1,0:T(8,128)(2,1)}, bf16[1024,384]{1,0:T(8,128)(2,1)}, u32[]{:S(2)}, u32[]{:S(2)}) %collective-permute-start.43) | collective-permute-done | bytes 786464 | tf_op jit(solution)/shard_map/ppermute | solution.py:426
  268.4 12.5 %outer_blocks.3 = (bf16[128,2048]{1,0:T(8,128)(2,1)}, bf16[128,2048]{1,0:T(8,128)(2,1)}, bf16[128,2048]{1,0:T(8,128)(2,1)}) custom-call(s32[1]{0:T(128)} %bitcast.9._.quarter_ref, bf16[512,2048]{1,0:T(8,128)(2,1)} %get-tuple-element.217.refs_0_, bf16[512,2048]{1,0:T(8,128)(2,1)} %copy-done.29, bf16[3072,512]{1,0:T(8,128)(2,1)} %get-tuple-element.245.refs_2_, ...), custom_call_target="tpu_custom_call" | custom-call | flops 1048576 | bytes 65536 | tf_op jit(solution)/shard_map/outer_blocks/pallas_call | solution.py:338
  280.9 18.7 %collective-permute-done.47 = bf16[128,2048]{1,0:T(8,128)(2,1)} collective-permute-done((bf16[128,2048]{1,0:T(8,128)(2,1)}, bf16[128,2048]{1,0:T(8,128)(2,1)}, u32[]{:S(2)}, u32[]{:S(2)}) %collective-permute-start.47) | collective-permute-done | bytes 524320 | tf_op jit(solution)/shard_map/ppermute | solution.py:426
  304.4 17.5 %back_blocks.1 = bf16[3072,512]{1,0:T(8,128)(2,1)} custom-call(bf16[512,2048]{1,0:T(8,128)(2,1)} %constant_dynamic-slice_fusion.6.weight_ref, f32[3072,512]{1,0:T(8,128)} %get-tuple-element.403.slope_ref, bf16[256,2048]{1,0:T(8,128)(2,1)} %collective-permute-done.28.refs_4_.refs_8_.refs_0_, ...), custom_call_target="tpu_custom_call" | custom-call | flops 1048576 | bytes 65536 | tf_op jit(solution)/shard_map/back_blocks/pallas_call | solution.py:368
  322.0 5.7 collective-permute-done.48
  328.9 3.0 fusion.48
  336.8 11.0 %add_convert_fusion = bf16[2048,512]{1,0:T(8,128)(2,1)S(1)} fusion(f32[2048,512]{1,0:T(8,128)S(1)} %fusion.48, f32[2048,512]{1,0:T(8,128)S(1)} %fusion.46, bf16[3072,2048]{1,0:T(8,128)(2,1)} %get-tuple-element.242, bf16[3072,512]{1,0:T(8,128)(2,1)} %back_blocks.1), kind=kOutput, calls=%fused_computation.36 | convolution fusion | flops 6445596672 | bytes 26214400 | tf_op jit(solution)/shard_map/dot_general | solution.py:36
  347.8 6.7 %collective-permute-done.51 = bf16[128,2048]{1,0:T(8,128)(2,1)} collective-permute-done((bf16[128,2048]{1,0:T(8,128)(2,1)S(1)}, bf16[128,2048]{1,0:T(8,128)(2,1)}, u32[]{:S(2)}, u32[]{:S(2)}) %collective-permute-start.51) | collective-permute-done | bytes 524320 | tf_op jit(solution)/shard_map/ppermute | solution.py:426
  354.5 5.4 collective-permute-done.52.refs_1_.refs_3_
  365.4 6.7 %fusion.69 = f32[1024,2048]{1,0:T(8,128)S(1)} fusion(bf16[1024,1536]{1,0:T(8,128)(2,1)S(1)} %copy-done.3, bf16[2048,1536]{1,0:T(8,128)(2,1)S(1)} %bitcast.83), kind=kOutput, calls=%fused_computation.164 | convolution fusion | flops 6442450944 | bytes 17825792 | tf_op jit(solution)/shard_map/dot_general | solution.py:36
  373.4 11.0 %collective-permute-done.53 = bf16[128,2048]{1,0:T(8,128)(2,1)S(1)} collective-permute-done((bf16[128,2048]{1,0:T(8,128)(2,1)S(1)}, bf16[128,2048]{1,0:T(8,128)(2,1)S(1)}, u32[]{:S(2)}, u32[]{:S(2)}) %collective-permute-start.53) | collective-permute-done | bytes 524320 | tf_op jit(solution)/shard_map/ppermute | solution.py:426
  384.4 4.0 collective-permute-done.54.refs_2_.refs_4_
  391.9 12.6 %fusion.70 = f32[1024,2048]{1,0:T(8,128)S(1)} fusion(bf16[1024,2048]{1,0:T(8,128)(2,1)} %fusion.17, bf16[2048,2048]{1,0:T(8,128)(2,1)} %param.32), kind=kOutput, calls=%fused_computation.165 | convolution fusion | flops 8589934592 | bytes 20971520 | tf_op jit(solution)/shard_map/dot_general | solution.py:36
  406.9 6.6 collective-permute-done.58.refs_2_.refs_4_
  423.6 3.7 fusion.11
  427.3 10.5 %fusion.59 = (f32[2048]{0:T(1024)S(1)}, f32[2048]{0:T(1024)S(1)}, f32[1024]{0:T(1024)S(1)}, f32[1024]{0:T(1024)S(1)}, f32[1024,2048]{1,0:T(8,128)}, /*index=5*/f32[2048]{0:T(1024)S(1)}, f32[2048]{0:T(1024)S(1)}) fusion(f32[1024,2048]{1,0:T(8,128)S(1)} %fusion.70, f32[1024]{0:T(1024)S(1)} %add_rsqrt_fusion, f32[1024]{0:T(1024)S(1)} %broadcast_multiply_fusion.2, ...), kind=kLoop, calls=%fused_computation.155 | loop fusion | flops 46127104 | bytes 29425664 | tf_op jit(solution)/shard_map/reduce_sum | solution.py:780
  446.1 7.8 %fusion.10 = f32[1024,2048]{1,0:T(8,128)S(1)} fusion(f32[1024,2048]{1,0:T(8,128)} %get-tuple-element.400, f32[1024]{0:T(1024)S(1)} %broadcast_multiply_fusion, f32[1024]{0:T(1024)S(1)} %broadcast_multiply_fusion.1, f32[1024]{0:T(1024)S(1)} %add_rsqrt_fusion, f32[1024]{0:T(1024)S(1)} %broadcast_multiply_fusion.2, bf16[256,2048]{1,0:T(8,128)(2,1)S(1)} %copy-done.8, ...), kind=kLoop, calls=%fused_computation.14 | loop fusion | flops 29360128 | bytes 20987904 | tf_op jit(solution)/shard_map/mul | solution.py:786
  458.7 3.3 collective-permute-done.62
  462.0 4.2 collective-permute-done.63.refs_1_.refs_3_
  473.8 11.3 %add_convert_fusion.1 = bf16[2048,384]{1,0:T(8,128)(2,1)} fusion(f32[2048,384]{1,0:T(8,128)S(1)} %fusion.54, f32[2048,384]{1,0:T(8,128)S(1)} %fusion.52, bf16[3072,2048]{1,0:T(8,128)(2,1)} %get-tuple-element.318, bf16[1024,384]{1,0:T(8,128)(2,1)} %collective-permute-done.46, bf16[1024,384]{1,0:T(8,128)(2,1)} %collective-permute-done.44, ...), kind=kOutput, calls=%fused_computation.41 | convolution fusion | flops 4841275392 | bytes 22806528 | tf_op jit(solution)/shard_map/dot_general | solution.py:36
  485.1 3.4 collective-permute-done.66
  498.0 3.6 collective-permute-start.64
  502.8 4.0 place_quarters.15.refs_0_
  506.8 4.0 place_quarters.16
  513.0 7.7 %collective-permute-done.64 = bf16[512,512]{1,0:T(8,128)(2,1)S(1)} collective-permute-done((bf16[512,512]{1,0:T(8,128)(2,1)S(1)}, bf16[512,512]{1,0:T(8,128)(2,1)S(1)}, u32[]{:S(2)}, u32[]{:S(2)}) %collective-permute-start.64) | collective-permute-done | bytes 524320 | tf_op jit(solution)/shard_map/ppermute | solution.py:426
  528.1 4.0 place_quarters.18.refs_0_
  532.0 4.0 place_quarters.17.refs_0_
  536.0 8.1 %collective-permute-done.75 = bf16[512,384]{1,0:T(8,128)(2,1)} collective-permute-done((bf16[512,384]{1,0:T(8,128)(2,1)}, bf16[512,384]{1,0:T(8,128)(2,1)}, u32[]{:S(2)}, u32[]{:S(2)}) %collective-permute-start.75) | collective-permute-done | bytes 393248 | tf_op jit(solution)/shard_map/ppermute | solution.py:426
  552.3 2.9 collective-permute-start.79
  558.4 4.2 place_quarters.19.refs_0_
  562.6 4.0 place_quarters.20.refs_0_
  577.6 3.3 collective-permute-start.81
  584.0 4.0 place_quarters.21
  587.9 4.0 place_quarters.22.refs_0_
  595.8 3.0 collective-permute-start.84
  602.4 3.5 place_quarters.24.refs_0_
  605.9 4.1 place_quarters.23
  620.4 3.5 place_quarters.25.refs_0_
  626.4 4.3 collective-permute-done.90.refs_2_.refs_4_
  636.6 3.7 place_quarters.26.refs_0_
  643.9 3.8 fusion.33
  (469 shorter events, 225.2 us)
Async XLA Ops:
  1.2 43.3 %collective-permute-start.3 = (bf16[256,2048]{1,0:T(8,128)(2,1)}, bf16[256,2048]{1,0:T(8,128)(2,1)}, u32[]{:S(2)}, u32[]{:S(2)}) collective-permute-start(bf16[256,2048]{1,0:T(8,128)(2,1)} %refs_4_.1), channel_id=1, source_target_pairs={{0,4},{4,0},{8,12},{12,8},{16,20},{20,16},{24,28},{28,24},{1,5},{5... | collective-permute-start | bytes 3145736 | tf_op jit(solution)/shard_map/ppermute | solution.py:426
  3.8 40.7 %collective-permute-start.4 = (bf16[256,2048]{1,0:T(8,128)(2,1)}, bf16[256,2048]{1,0:T(8,128)(2,1)}, u32[]{:S(2)}, u32[]{:S(2)}) collective-permute-start(bf16[256,2048]{1,0:T(8,128)(2,1)} %refs_4_.1), channel_id=1, source_target_pairs={{0,8},{4,12},{8,0},{12,4},{16,24},{20,28},{24,16},{28,20},{1,9},{5... | collective-permute-start | bytes 3145736 | tf_op jit(solution)/shard_map/ppermute | solution.py:426
  5.3 39.2 %collective-permute-start.5 = (bf16[256,2048]{1,0:T(8,128)(2,1)}, bf16[256,2048]{1,0:T(8,128)(2,1)}, u32[]{:S(2)}, u32[]{:S(2)}) collective-permute-start(bf16[256,2048]{1,0:T(8,128)(2,1)} %refs_4_.1), channel_id=1, source_target_pairs={{0,2},{1,3},{2,0},{3,1},{4,6},{5,7},{6,4},{7,5},{8,10},{9,11},{10,... | collective-permute-start | bytes 3145736 | tf_op jit(solution)/shard_map/ppermute | solution.py:419
  25.5 19.0 %collective-permute-start.2 = (f32[8,128]{1,0:T(8,128)S(1)}, f32[8,128]{1,0:T(8,128)S(1)}, u32[]{:S(2)}, u32[]{:S(2)}) collective-permute-start(f32[8,128]{1,0:T(8,128)S(1)} %broadcast_add_fusion), channel_id=1, source_target_pairs={{0,4},{4,0},{8,12},{12,8},{16,20},{20,16},{24,28},{28,24},{1,5},{5... | collective-permute-start | bytes 12296 | tf_op jit(solution)/shard_map/ppermute | solution.py:426
  44.8 33.3 %collective-permute-start.8 = (bf16[256,2048]{1,0:T(8,128)(2,1)}, bf16[256,2048]{1,0:T(8,128)(2,1)}, u32[]{:S(2)}, u32[]{:S(2)}) collective-permute-start(bf16[256,2048]{1,0:T(8,128)(2,1)} %collective-permute-done.4.refs_8_), channel_id=1, source_target_pairs={{0,4},{4,0},{8,12},{12,8},{16,20},{20,16},{24,28},{28,24},{1,5},{5... | collective-permute-start | bytes 3145736 | tf_op jit(solution)/shard_map/ppermute | solution.py:426
  46.3 32.3 %collective-permute-start.9 = (bf16[256,2048]{1,0:T(8,128)(2,1)}, bf16[256,2048]{1,0:T(8,128)(2,1)}, u32[]{:S(2)}, u32[]{:S(2)}) collective-permute-start(bf16[256,2048]{1,0:T(8,128)(2,1)} %collective-permute-done.3.refs_4_), channel_id=1, source_target_pairs={{0,2},{1,3},{2,0},{3,1},{4,6},{5,7},{6,4},{7,5},{8,10},{9,11},{10,... | collective-permute-start | bytes 3145736 | tf_op jit(solution)/shard_map/ppermute | solution.py:419
  46.8 33.0 %collective-permute-start.10 = (bf16[256,2048]{1,0:T(8,128)(2,1)}, bf16[256,2048]{1,0:T(8,128)(2,1)}, u32[]{:S(2)}, u32[]{:S(2)}) collective-permute-start(bf16[256,2048]{1,0:T(8,128)(2,1)} %collective-permute-done.5.refs_4_), channel_id=1, source_target_pairs={{0,8},{4,12},{8,0},{12,4},{16,24},{20,28},{24,16},{28,20},{1,9},{5... | collective-permute-start | bytes 3145736 | tf_op jit(solution)/shard_map/ppermute | solution.py:426
  49.0 42.5 %collective-permute-start.14 = (bf16[256,2048]{1,0:T(8,128)(2,1)}, bf16[256,2048]{1,0:T(8,128)(2,1)}, u32[]{:S(2)}, u32[]{:S(2)}) collective-permute-start(bf16[256,2048]{1,0:T(8,128)(2,1)} %collective-permute-done.3.refs_4_), channel_id=1, source_target_pairs={{0,1},{1,0},{2,3},{3,2},{4,5},{5,4},{6,7},{7,6},{8,9},{9,8},{10,11... | collective-permute-start | bytes 3145736 | tf_op jit(solution)/shard_map/ppermute | solution.py:415
  49.6 28.1 %collective-permute-start.7 = (f32[8,128]{1,0:T(8,128)S(1)}, f32[8,128]{1,0:T(8,128)S(1)}, u32[]{:S(2)}, u32[]{:S(2)}) collective-permute-start(f32[8,128]{1,0:T(8,128)S(1)} %fusion.97), channel_id=1, source_target_pairs={{0,8},{4,12},{8,0},{12,4},{16,24},{20,28},{24,16},{28,20},{1,9},{5... | collective-permute-start | bytes 12296 | tf_op jit(solution)/shard_map/ppermute | solution.py:426
  112.8 21.0 %collective-permute-start.24 = (bf16[128,2048]{1,0:T(8,128)(2,1)}, bf16[128,2048]{1,0:T(8,128)(2,1)}, u32[]{:S(2)}, u32[]{:S(2)}) collective-permute-start(bf16[128,2048]{1,0:T(8,128)(2,1)} %slice.136), channel_id=1, source_target_pairs={{0,4},{4,0},{8,12},{12,8},{16,20},{20,16},{24,28},{28,24},{1,5},{5... | collective-permute-start | bytes 1572872 | tf_op jit(solution)/shard_map/ppermute | solution.py:426
  113.4 20.4 %collective-permute-start.25 = (bf16[128,2048]{1,0:T(8,128)(2,1)S(1)}, bf16[128,2048]{1,0:T(8,128)(2,1)}, u32[]{:S(2)}, u32[]{:S(2)}) collective-permute-start(bf16[128,2048]{1,0:T(8,128)(2,1)S(1)} %slice.137), channel_id=1, source_target_pairs={{0,8},{4,12},{8,0},{12,4},{16,24},{20,28},{24,16},{28,20},{1,9},{5... | collective-permute-start | bytes 1572872 | tf_op jit(solution)/shard_map/ppermute | solution.py:426
  116.1 32.9 %collective-permute-start.21 = (bf16[256,2048]{1,0:T(8,128)(2,1)}, bf16[256,2048]{1,0:T(8,128)(2,1)}, u32[]{:S(2)}, u32[]{:S(2)}) collective-permute-start(bf16[256,2048]{1,0:T(8,128)(2,1)} %fusion.43), channel_id=1, source_target_pairs={{0,2},{1,3},{2,0},{3,1},{4,6},{5,7},{6,4},{7,5},{8,10},{9,11},{10,... | collective-permute-start | bytes 3145736 | tf_op jit(solution)/shard_map/ppermute | solution.py:423
  158.8 24.9 %collective-permute-start.27 = (bf16[256,2048]{1,0:T(8,128)(2,1)S(1)}, bf16[256,2048]{1,0:T(8,128)(2,1)}, u32[]{:S(2)}, u32[]{:S(2)}) collective-permute-start(bf16[256,2048]{1,0:T(8,128)(2,1)S(1)} %get-tuple-element.241), channel_id=1, source_target_pairs={{0,2},{1,3},{2,0},{3,1},{4,6},{5,7},{6,4},{7,5},{8,10},{9,11},{10,... | collective-permute-start | bytes 3145736 | tf_op jit(solution)/shard_map/ppermute | solution.py:419
  160.3 24.6 %collective-permute-start.28 = (bf16[256,2048]{1,0:T(8,128)(2,1)S(1)}, bf16[256,2048]{1,0:T(8,128)(2,1)}, u32[]{:S(2)}, u32[]{:S(2)}) collective-permute-start(bf16[256,2048]{1,0:T(8,128)(2,1)S(1)} %get-tuple-element.241), channel_id=1, source_target_pairs={{0,4},{4,0},{8,12},{12,8},{16,20},{20,16},{24,28},{28,24},{1,5},{5... | collective-permute-start | bytes 3145736 | tf_op jit(solution)/shard_map/ppermute | solution.py:426
  161.8 24.3 %collective-permute-start.29 = (bf16[256,2048]{1,0:T(8,128)(2,1)S(1)}, bf16[256,2048]{1,0:T(8,128)(2,1)}, u32[]{:S(2)}, u32[]{:S(2)}) collective-permute-start(bf16[256,2048]{1,0:T(8,128)(2,1)S(1)} %get-tuple-element.241), channel_id=1, source_target_pairs={{0,8},{4,12},{8,0},{12,4},{16,24},{20,28},{24,16},{28,20},{1,9},{5... | collective-permute-start | bytes 3145736 | tf_op jit(solution)/shard_map/ppermute | solution.py:426
  162.9 23.3 %collective-permute-start.30 = (bf16[256,2048]{1,0:T(8,128)(2,1)S(1)}, bf16[256,2048]{1,0:T(8,128)(2,1)S(1)}, u32[]{:S(2)}, u32[]{:S(2)}) collective-permute-start(bf16[256,2048]{1,0:T(8,128)(2,1)S(1)} %get-tuple-element.241), channel_id=1, source_target_pairs={{0,1},{1,0},{2,3},{3,2},{4,5},{5,4},{6,7},{7,6},{8,9},{9,8},{10,11... | collective-permute-start | bytes 3145736 | tf_op jit(solution)/shard_map/ppermute | solution.py:415
  186.2 27.5 %collective-permute-start.34 = (bf16[256,2048]{1,0:T(8,128)(2,1)}, bf16[256,2048]{1,0:T(8,128)(2,1)}, u32[]{:S(2)}, u32[]{:S(2)}) collective-permute-start(bf16[256,2048]{1,0:T(8,128)(2,1)} %collective-permute-done.27), channel_id=1, source_target_pairs={{0,8},{4,12},{8,0},{12,4},{16,24},{20,28},{24,16},{28,20},{1,9},{5... | collective-permute-start | bytes 3145736 | tf_op jit(solution)/shard_map/ppermute | solution.py:426
  187.3 26.4 %collective-permute-start.33 = (bf16[256,2048]{1,0:T(8,128)(2,1)}, bf16[256,2048]{1,0:T(8,128)(2,1)}, u32[]{:S(2)}, u32[]{:S(2)}) collective-permute-start(bf16[256,2048]{1,0:T(8,128)(2,1)} %collective-permute-done.28.refs_4_.refs_8_.refs_0_), channel_id=1, source_target_pairs={{0,2},{1,3},{2,0},{3,1},{4,6},{5,7},{6,4},{7,5},{8,10},{9,11},{10,... | collective-permute-start | bytes 3145736 | tf_op jit(solution)/shard_map/ppermute | solution.py:419
  187.8 29.3 %collective-permute-start.37 = (bf16[256,2048]{1,0:T(8,128)(2,1)}, bf16[256,2048]{1,0:T(8,128)(2,1)}, u32[]{:S(2)}, u32[]{:S(2)}) collective-permute-start(bf16[256,2048]{1,0:T(8,128)(2,1)} %collective-permute-done.28.refs_4_.refs_8_.refs_0_), channel_id=1, source_target_pairs={{0,1},{1,0},{2,3},{3,2},{4,5},{5,4},{6,7},{7,6},{8,9},{9,8},{10,11... | collective-permute-start | bytes 3145736 | tf_op jit(solution)/shard_map/ppermute | solution.py:415
  187.8 25.9 %collective-permute-start.32 = (bf16[256,2048]{1,0:T(8,128)(2,1)}, bf16[256,2048]{1,0:T(8,128)(2,1)}, u32[]{:S(2)}, u32[]{:S(2)}) collective-permute-start(bf16[256,2048]{1,0:T(8,128)(2,1)} %collective-permute-done.29.refs_8_.refs_12_.refs_4_), channel_id=1, source_target_pairs={{0,4},{4,0},{8,12},{12,8},{16,20},{20,16},{24,28},{28,24},{1,5},{5... | collective-permute-start | bytes 3145736 | tf_op jit(solution)/shard_map/ppermute | solution.py:426
  189.0 29.1 %collective-permute-start.39 = (bf16[256,2048]{1,0:T(8,128)(2,1)}, bf16[256,2048]{1,0:T(8,128)(2,1)}, u32[]{:S(2)}, u32[]{:S(2)}) collective-permute-start(bf16[256,2048]{1,0:T(8,128)(2,1)} %collective-permute-done.29.refs_8_.refs_12_.refs_4_), channel_id=1, source_target_pairs={{0,1},{1,0},{2,3},{3,2},{4,5},{5,4},{6,7},{7,6},{8,9},{9,8},{10,11... | collective-permute-start | bytes 3145736 | tf_op jit(solution)/shard_map/ppermute | solution.py:415
  214.8 20.4 %collective-permute-start.38 = (bf16[256,2048]{1,0:T(8,128)(2,1)}, bf16[256,2048]{1,0:T(8,128)(2,1)S(1)}, u32[]{:S(2)}, u32[]{:S(2)}) collective-permute-start(bf16[256,2048]{1,0:T(8,128)(2,1)} %collective-permute-done.33.refs_6_.refs_10_.refs_2_), channel_id=1, source_target_pairs={{0,1},{1,0},{2,3},{3,2},{4,5},{5,4},{6,7},{7,6},{8,9},{9,8},{10,11... | collective-permute-start | bytes 3145736 | tf_op jit(solution)/shard_map/ppermute | solution.py:415
  216.0 19.2 %collective-permute-start.40 = (bf16[256,2048]{1,0:T(8,128)(2,1)}, bf16[256,2048]{1,0:T(8,128)(2,1)S(1)}, u32[]{:S(2)}, u32[]{:S(2)}) collective-permute-start(bf16[256,2048]{1,0:T(8,128)(2,1)} %collective-permute-done.34.refs_10_.refs_14_.refs_6_), channel_id=1, source_target_pairs={{0,1},{1,0},{2,3},{3,2},{4,5},{5,4},{6,7},{7,6},{8,9},{9,8},{10,11... | collective-permute-start | bytes 3145736 | tf_op jit(solution)/shard_map/ppermute | solution.py:415
  216.6 18.7 %collective-permute-start.35 = (bf16[128,2048]{1,0:T(8,128)(2,1)S(1)}, bf16[128,2048]{1,0:T(8,128)(2,1)S(1)}, u32[]{:S(2)}, u32[]{:S(2)}) collective-permute-start(bf16[128,2048]{1,0:T(8,128)(2,1)S(1)} %slice.139), channel_id=1, source_target_pairs={{0,4},{4,0},{8,12},{12,8},{16,20},{20,16},{24,28},{28,24},{1,5},{5... | collective-permute-start | bytes 1572872 | tf_op jit(solution)/shard_map/ppermute | solution.py:426
  217.1 18.1 %collective-permute-start.36 = (bf16[128,2048]{1,0:T(8,128)(2,1)S(1)}, bf16[128,2048]{1,0:T(8,128)(2,1)S(1)}, u32[]{:S(2)}, u32[]{:S(2)}) collective-permute-start(bf16[128,2048]{1,0:T(8,128)(2,1)S(1)} %slice.140), channel_id=1, source_target_pairs={{0,8},{4,12},{8,0},{12,4},{16,24},{20,28},{24,16},{28,20},{1,9},{5... | collective-permute-start | bytes 1572872 | tf_op jit(solution)/shard_map/ppermute | solution.py:426
  218.1 18.2 %collective-permute-start.41 = (bf16[256,2048]{1,0:T(8,128)(2,1)}, bf16[256,2048]{1,0:T(8,128)(2,1)S(1)}, u32[]{:S(2)}, u32[]{:S(2)}) collective-permute-start(bf16[256,2048]{1,0:T(8,128)(2,1)} %collective-permute-done.32.refs_12_.refs_16_.refs_8_), channel_id=1, source_target_pairs={{0,1},{1,0},{2,3},{3,2},{4,5},{5,4},{6,7},{7,6},{8,9},{9,8},{10,11... | collective-permute-start | bytes 3145736 | tf_op jit(solution)/shard_map/ppermute | solution.py:415
  240.9 20.2 %collective-permute-start.43 = (bf16[1024,384]{1,0:T(8,128)(2,1)}, bf16[1024,384]{1,0:T(8,128)(2,1)}, u32[]{:S(2)}, u32[]{:S(2)}) collective-permute-start(bf16[1024,384]{1,0:T(8,128)(2,1)} %get-tuple-element.407), channel_id=1, source_target_pairs={{0,4},{4,0},{8,12},{12,8},{16,20},{20,16},{24,28},{28,24},{1,5},{5... | collective-permute-start | bytes 2359304 | tf_op jit(solution)/shard_map/ppermute | solution.py:426
  242.4 19.8 %collective-permute-start.44 = (bf16[1024,384]{1,0:T(8,128)(2,1)}, bf16[1024,384]{1,0:T(8,128)(2,1)}, u32[]{:S(2)}, u32[]{:S(2)}) collective-permute-start(bf16[1024,384]{1,0:T(8,128)(2,1)} %get-tuple-element.406), channel_id=1, source_target_pairs={{0,8},{4,12},{8,0},{12,4},{16,24},{20,28},{24,16},{28,20},{1,9},{5... | collective-permute-start | bytes 2359304 | tf_op jit(solution)/shard_map/ppermute | solution.py:426
  262.3 37.4 %collective-permute-start.47 = (bf16[128,2048]{1,0:T(8,128)(2,1)}, bf16[128,2048]{1,0:T(8,128)(2,1)}, u32[]{:S(2)}, u32[]{:S(2)}) collective-permute-start(bf16[128,2048]{1,0:T(8,128)(2,1)} %get-tuple-element.266), channel_id=1, source_target_pairs={{0,16},{4,20},{8,24},{12,28},{16,0},{20,4},{24,8},{28,12},{1,17},{... | collective-permute-start | bytes 1572872 | tf_op jit(solution)/shard_map/ppermute | solution.py:426
  262.6 59.4 %collective-permute-start.45 = (bf16[128,2048]{1,0:T(8,128)(2,1)}, bf16[128,2048]{1,0:T(8,128)(2,1)}, u32[]{:S(2)}, u32[]{:S(2)}) collective-permute-start(bf16[128,2048]{1,0:T(8,128)(2,1)} %get-tuple-element.265), channel_id=1, source_target_pairs={{0,16},{4,20},{8,24},{12,28},{16,0},{20,4},{24,8},{28,12},{1,17},{... | collective-permute-start | bytes 1572872 | tf_op jit(solution)/shard_map/ppermute | solution.py:426
  267.3 54.6 %collective-permute-start.46 = (bf16[1024,384]{1,0:T(8,128)(2,1)}, bf16[1024,384]{1,0:T(8,128)(2,1)}, u32[]{:S(2)}, u32[]{:S(2)}) collective-permute-start(bf16[1024,384]{1,0:T(8,128)(2,1)} %constant_dynamic-slice_fusion.2), channel_id=1, source_target_pairs={{0,12},{4,8},{8,4},{12,0},{16,28},{20,24},{24,20},{28,16},{1,13},{... | collective-permute-start | bytes 2359304 | tf_op jit(solution)/shard_map/ppermute | solution.py:426
  301.6 26.1 %collective-permute-start.48 = (bf16[128,2048]{1,0:T(8,128)(2,1)}, bf16[128,2048]{1,0:T(8,128)(2,1)}, u32[]{:S(2)}, u32[]{:S(2)}) collective-permute-start(bf16[128,2048]{1,0:T(8,128)(2,1)} %add_convert_fusion.10), channel_id=1, source_target_pairs={{0,8},{4,12},{8,0},{12,4},{16,24},{20,28},{24,16},{28,20},{1,9},{5... | collective-permute-start | bytes 1572872 | tf_op jit(solution)/shard_map/ppermute | solution.py:426
  303.1 44.7 %collective-permute-start.50 = (bf16[128,2048]{1,0:T(8,128)(2,1)}, bf16[128,2048]{1,0:T(8,128)(2,1)}, u32[]{:S(2)}, u32[]{:S(2)}) collective-permute-start(bf16[128,2048]{1,0:T(8,128)(2,1)} %get-tuple-element.279), channel_id=1, source_target_pairs={{0,16},{4,20},{8,24},{12,28},{16,0},{20,4},{24,8},{28,12},{1,17},{... | collective-permute-start | bytes 1572872 | tf_op jit(solution)/shard_map/ppermute | solution.py:426
  333.2 21.3 %collective-permute-start.51 = (bf16[128,2048]{1,0:T(8,128)(2,1)S(1)}, bf16[128,2048]{1,0:T(8,128)(2,1)}, u32[]{:S(2)}, u32[]{:S(2)}) collective-permute-start(bf16[128,2048]{1,0:T(8,128)(2,1)S(1)} %add_convert_fusion.9), channel_id=1, source_target_pairs={{0,8},{4,12},{8,0},{12,4},{16,24},{20,28},{24,16},{28,20},{1,9},{5... | collective-permute-start | bytes 1572872 | tf_op jit(solution)/shard_map/ppermute | solution.py:426
  334.8 25.2 %collective-permute-start.52 = (bf16[256,2048]{1,0:T(8,128)(2,1)S(1)}, bf16[256,2048]{1,0:T(8,128)(2,1)S(1)}, u32[]{:S(2)}, u32[]{:S(2)}) collective-permute-start(bf16[256,2048]{1,0:T(8,128)(2,1)S(1)} %pad_maximum_fusion.3.refs_0_.refs_2_), channel_id=1, source_target_pairs={{0,4},{4,0},{8,12},{12,8},{16,20},{20,16},{24,28},{28,24},{1,5},{5... | collective-permute-start | bytes 3145736 | tf_op jit(solution)/shard_map/ppermute | solution.py:426
  335.5 37.9 %collective-permute-start.49 = (bf16[128,2048]{1,0:T(8,128)(2,1)}, bf16[128,2048]{1,0:T(8,128)(2,1)}, u32[]{:S(2)}, u32[]{:S(2)}) collective-permute-start(bf16[128,2048]{1,0:T(8,128)(2,1)} %get-tuple-element.278), channel_id=1, source_target_pairs={{0,16},{4,20},{8,24},{12,28},{16,0},{20,4},{24,8},{28,12},{1,17},{... | collective-permute-start | bytes 1572872 | tf_op jit(solution)/shard_map/ppermute | solution.py:426
  361.7 45.2 %collective-permute-start.56 = (bf16[128,2048]{1,0:T(8,128)(2,1)}, bf16[128,2048]{1,0:T(8,128)(2,1)}, u32[]{:S(2)}, u32[]{:S(2)}) collective-permute-start(bf16[128,2048]{1,0:T(8,128)(2,1)} %get-tuple-element.291), channel_id=1, source_target_pairs={{0,16},{4,20},{8,24},{12,28},{16,0},{20,4},{24,8},{28,12},{1,17},{... | collective-permute-start | bytes 1572872 | tf_op jit(solution)/shard_map/ppermute | solution.py:426
  362.7 21.7 %collective-permute-start.53 = (bf16[128,2048]{1,0:T(8,128)(2,1)S(1)}, bf16[128,2048]{1,0:T(8,128)(2,1)S(1)}, u32[]{:S(2)}, u32[]{:S(2)}) collective-permute-start(bf16[128,2048]{1,0:T(8,128)(2,1)S(1)} %add_convert_fusion.8), channel_id=1, source_target_pairs={{0,8},{4,12},{8,0},{12,4},{16,24},{20,28},{24,16},{28,20},{1,9},{5... | collective-permute-start | bytes 1572872 | tf_op jit(solution)/shard_map/ppermute | solution.py:426
  364.7 23.7 %collective-permute-start.54 = (bf16[256,2048]{1,0:T(8,128)(2,1)S(1)}, bf16[256,2048]{1,0:T(8,128)(2,1)S(1)}, u32[]{:S(2)}, u32[]{:S(2)}) collective-permute-start(bf16[256,2048]{1,0:T(8,128)(2,1)S(1)} %pad_maximum_fusion.4.refs_1_.refs_3_), channel_id=1, source_target_pairs={{0,4},{4,0},{8,12},{12,8},{16,20},{20,16},{24,28},{28,24},{1,5},{5... | collective-permute-start | bytes 3145736 | tf_op jit(solution)/shard_map/ppermute | solution.py:426
  391.2 22.2 %collective-permute-start.58 = (bf16[256,2048]{1,0:T(8,128)(2,1)S(1)}, bf16[256,2048]{1,0:T(8,128)(2,1)S(1)}, u32[]{:S(2)}, u32[]{:S(2)}) collective-permute-start(bf16[256,2048]{1,0:T(8,128)(2,1)S(1)} %pad_maximum_fusion.5.refs_1_.refs_3_), channel_id=1, source_target_pairs={{0,4},{4,0},{8,12},{12,8},{16,20},{20,16},{24,28},{28,24},{1,5},{5... | collective-permute-start | bytes 3145736 | tf_op jit(solution)/shard_map/ppermute | solution.py:426
  404.5 35.6 %collective-permute-start.55 = (bf16[512,512]{1,0:T(8,128)(2,1)}, bf16[512,512]{1,0:T(8,128)(2,1)}, u32[]{:S(2)}, u32[]{:S(2)}) collective-permute-start(bf16[512,512]{1,0:T(8,128)(2,1)} %get-tuple-element.290), channel_id=1, source_target_pairs={{0,16},{4,20},{8,24},{12,28},{16,0},{20,4},{24,8},{28,12},{1,17},{... | collective-permute-start | bytes 1572872 | tf_op jit(solution)/shard_map/ppermute | solution.py:426
  413.5 45.2 %collective-permute-start.61 = (bf16[512,512]{1,0:T(8,128)(2,1)}, bf16[512,512]{1,0:T(8,128)(2,1)}, u32[]{:S(2)}, u32[]{:S(2)}) collective-permute-start(bf16[512,512]{1,0:T(8,128)(2,1)} %get-tuple-element.305), channel_id=1, source_target_pairs={{0,16},{4,20},{8,24},{12,28},{16,0},{20,4},{24,8},{28,12},{1,17},{... | collective-permute-start | bytes 1572872 | tf_op jit(solution)/shard_map/ppermute | solution.py:426
  418.2 21.9 %collective-permute-start.59 = (bf16[128,2048]{1,0:T(8,128)(2,1)}, bf16[128,2048]{1,0:T(8,128)(2,1)}, u32[]{:S(2)}, u32[]{:S(2)}) collective-permute-start(bf16[128,2048]{1,0:T(8,128)(2,1)} %add_convert_fusion.6), channel_id=1, source_target_pairs={{0,8},{4,12},{8,0},{12,4},{16,24},{20,28},{24,16},{28,20},{1,9},{5... | collective-permute-start | bytes 1572872 | tf_op jit(solution)/shard_map/ppermute | solution.py:426
  420.2 21.0 %collective-permute-start.60 = (bf16[256,2048]{1,0:T(8,128)(2,1)}, bf16[256,2048]{1,0:T(8,128)(2,1)}, u32[]{:S(2)}, u32[]{:S(2)}) collective-permute-start(bf16[256,2048]{1,0:T(8,128)(2,1)} %pad_maximum_fusion.6.refs_1_.refs_3_), channel_id=1, source_target_pairs={{0,4},{4,0},{8,12},{12,8},{16,20},{20,16},{24,28},{28,24},{1,5},{5... | collective-permute-start | bytes 3145736 | tf_op jit(solution)/shard_map/ppermute | solution.py:426
  442.5 19.5 %collective-permute-start.62 = (bf16[512,512]{1,0:T(8,128)(2,1)S(1)}, bf16[512,512]{1,0:T(8,128)(2,1)S(1)}, u32[]{:S(2)}, u32[]{:S(2)}) collective-permute-start(bf16[512,512]{1,0:T(8,128)(2,1)S(1)} %add_convert_fusion.5), channel_id=1, source_target_pairs={{0,8},{4,12},{8,0},{12,4},{16,24},{20,28},{24,16},{28,20},{1,9},{5... | collective-permute-start | bytes 1572872 | tf_op jit(solution)/shard_map/ppermute | solution.py:426
  445.5 20.7 %collective-permute-start.63 = (bf16[256,2048]{1,0:T(8,128)(2,1)S(1)}, bf16[256,2048]{1,0:T(8,128)(2,1)S(1)}, u32[]{:S(2)}, u32[]{:S(2)}) collective-permute-start(bf16[256,2048]{1,0:T(8,128)(2,1)S(1)} %pad_maximum_fusion.7.refs_0_.refs_2_), channel_id=1, source_target_pairs={{0,4},{4,0},{8,12},{12,8},{16,20},{20,16},{24,28},{28,24},{1,5},{5... | collective-permute-start | bytes 3145736 | tf_op jit(solution)/shard_map/ppermute | solution.py:426
  456.3 28.8 %collective-permute-start.65 = (bf16[512,512]{1,0:T(8,128)(2,1)S(1)}, bf16[512,512]{1,0:T(8,128)(2,1)S(1)}, u32[]{:S(2)}, u32[]{:S(2)}) collective-permute-start(bf16[512,512]{1,0:T(8,128)(2,1)S(1)} %copy-done.51), channel_id=1, source_target_pairs={{0,16},{4,20},{8,24},{12,28},{16,0},{20,4},{24,8},{28,12},{1,17},{... | collective-permute-start | bytes 1572872 | tf_op jit(solution)/shard_map/ppermute | solution.py:426
  467.9 20.6 %collective-permute-start.66 = (bf16[512,512]{1,0:T(8,128)(2,1)S(1)}, bf16[512,512]{1,0:T(8,128)(2,1)S(1)}, u32[]{:S(2)}, u32[]{:S(2)}) collective-permute-start(bf16[512,512]{1,0:T(8,128)(2,1)S(1)} %add_convert_fusion.4), channel_id=1, source_target_pairs={{0,8},{4,12},{8,0},{12,4},{16,24},{20,28},{24,16},{28,20},{1,9},{5... | collective-permute-start | bytes 1572872 | tf_op jit(solution)/shard_map/ppermute | solution.py:426
  469.8 21.2 %collective-permute-start.67 = (bf16[1024,512]{1,0:T(8,128)(2,1)S(1)}, bf16[1024,512]{1,0:T(8,128)(2,1)S(1)}, u32[]{:S(2)}, u32[]{:S(2)}) collective-permute-start(bf16[1024,512]{1,0:T(8,128)(2,1)S(1)} %pad_maximum_fusion.8.refs_0_.refs_2_), channel_id=1, source_target_pairs={{0,4},{4,0},{8,12},{12,8},{16,20},{20,16},{24,28},{28,24},{1,5},{5... | collective-permute-start | bytes 3145736 | tf_op jit(solution)/shard_map/ppermute | solution.py:426
  471.1 19.8 %collective-permute-start.68 = (bf16[2,256,2048]{2,1,0:T(8,128)(2,1)S(1)}, bf16[2,256,2048]{2,1,0:T(8,128)(2,1)S(1)}, u32[]{:S(2)}, u32[]{:S(2)}) collective-permute-start(bf16[2,256,2048]{2,1,0:T(8,128)(2,1)S(1)} %fusion.31), channel_id=1, source_target_pairs={{0,1},{1,0},{2,3},{3,2},{4,5},{5,4},{6,7},{7,6},{8,9},{9,8},{10,11... | collective-permute-start | bytes 6291464 | tf_op jit(solution)/shard_map/ppermute | solution.py:415
  491.0 30.2 %collective-permute-start.70 = (bf16[1024,512]{1,0:T(8,128)(2,1)S(1)}, bf16[1024,512]{1,0:T(8,128)(2,1)S(1)}, u32[]{:S(2)}, u32[]{:S(2)}) collective-permute-start(bf16[1024,512]{1,0:T(8,128)(2,1)S(1)} %pad_maximum_fusion.9.refs_1_.refs_3_), channel_id=1, source_target_pairs={{0,4},{4,0},{8,12},{12,8},{16,20},{20,16},{24,28},{28,24},{1,5},{5... | collective-permute-start | bytes 3145736 | tf_op jit(solution)/shard_map/ppermute | solution.py:426
  496.6 24.6 %collective-permute-start.71 = (bf16[256,2048]{1,0:T(8,128)(2,1)}, bf16[256,2048]{1,0:T(8,128)(2,1)}, u32[]{:S(2)}, u32[]{:S(2)}) collective-permute-start(bf16[256,2048]{1,0:T(8,128)(2,1)} %fusion.45), channel_id=1, source_target_pairs={{0,2},{1,3},{2,0},{3,1},{4,6},{5,7},{6,4},{7,5},{8,10},{9,11},{10,... | collective-permute-start | bytes 3145736 | tf_op jit(solution)/shard_map/ppermute | solution.py:423
  498.0 22.7 %collective-permute-start.64 = (bf16[512,512]{1,0:T(8,128)(2,1)S(1)}, bf16[512,512]{1,0:T(8,128)(2,1)S(1)}, u32[]{:S(2)}, u32[]{:S(2)}) collective-permute-start(bf16[512,512]{1,0:T(8,128)(2,1)S(1)} %copy-done.49), channel_id=1, source_target_pairs={{0,16},{4,20},{8,24},{12,28},{16,0},{20,4},{24,8},{28,12},{1,17},{... | collective-permute-start | bytes 1572872 | tf_op jit(solution)/shard_map/ppermute | solution.py:426
  501.8 19.4 %collective-permute-start.69 = (bf16[512,512]{1,0:T(8,128)(2,1)S(1)}, bf16[512,512]{1,0:T(8,128)(2,1)}, u32[]{:S(2)}, u32[]{:S(2)}) collective-permute-start(bf16[512,512]{1,0:T(8,128)(2,1)S(1)} %add_convert_fusion.3), channel_id=1, source_target_pairs={{0,8},{4,12},{8,0},{12,4},{16,24},{20,28},{24,16},{28,20},{1,9},{5... | collective-permute-start | bytes 1572872 | tf_op jit(solution)/shard_map/ppermute | solution.py:426
  522.7 23.9 %collective-permute-start.73 = (bf16[1024,512]{1,0:T(8,128)(2,1)S(1)}, bf16[1024,512]{1,0:T(8,128)(2,1)S(1)}, u32[]{:S(2)}, u32[]{:S(2)}) collective-permute-start(bf16[1024,512]{1,0:T(8,128)(2,1)S(1)} %pad_maximum_fusion.10.refs_1_.refs_3_), channel_id=1, source_target_pairs={{0,4},{4,0},{8,12},{12,8},{16,20},{20,16},{24,28},{28,24},{1,5},{5... | collective-permute-start | bytes 3145736 | tf_op jit(solution)/shard_map/ppermute | solution.py:426
  524.8 21.0 %collective-permute-start.72 = (bf16[512,512]{1,0:T(8,128)(2,1)S(1)}, bf16[512,512]{1,0:T(8,128)(2,1)}, u32[]{:S(2)}, u32[]{:S(2)}) collective-permute-start(bf16[512,512]{1,0:T(8,128)(2,1)S(1)} %add_convert_fusion.2), channel_id=1, source_target_pairs={{0,8},{4,12},{8,0},{12,4},{16,24},{20,28},{24,16},{28,20},{1,9},{5... | collective-permute-start | bytes 1572872 | tf_op jit(solution)/shard_map/ppermute | solution.py:426
  525.4 18.8 %collective-permute-start.75 = (bf16[512,384]{1,0:T(8,128)(2,1)}, bf16[512,384]{1,0:T(8,128)(2,1)}, u32[]{:S(2)}, u32[]{:S(2)}) collective-permute-start(bf16[512,384]{1,0:T(8,128)(2,1)} %get-tuple-element.331), channel_id=1, source_target_pairs={{0,16},{4,20},{8,24},{12,28},{16,0},{20,4},{24,8},{28,12},{1,17},{... | collective-permute-start | bytes 1179656 | tf_op jit(solution)/shard_map/ppermute | solution.py:426
  548.1 23.1 %collective-permute-start.77 = (bf16[1024,512]{1,0:T(8,128)(2,1)S(1)}, bf16[1024,512]{1,0:T(8,128)(2,1)S(1)}, u32[]{:S(2)}, u32[]{:S(2)}) collective-permute-start(bf16[1024,512]{1,0:T(8,128)(2,1)S(1)} %pad_maximum_fusion.11.refs_1_.refs_3_), channel_id=1, source_target_pairs={{0,4},{4,0},{8,12},{12,8},{16,20},{20,16},{24,28},{28,24},{1,5},{5... | collective-permute-start | bytes 3145736 | tf_op jit(solution)/shard_map/ppermute | solution.py:426
  549.0 18.5 %collective-permute-start.76 = (bf16[512,384]{1,0:T(8,128)(2,1)}, bf16[512,384]{1,0:T(8,128)(2,1)}, u32[]{:S(2)}, u32[]{:S(2)}) collective-permute-start(bf16[512,384]{1,0:T(8,128)(2,1)} %get-tuple-element.336), channel_id=1, source_target_pairs={{0,16},{4,20},{8,24},{12,28},{16,0},{20,4},{24,8},{28,12},{1,17},{... | collective-permute-start | bytes 1179656 | tf_op jit(solution)/shard_map/ppermute | solution.py:426
  552.3 16.8 %collective-permute-start.79 = (bf16[512,384]{1,0:T(8,128)(2,1)}, bf16[512,384]{1,0:T(8,128)(2,1)}, u32[]{:S(2)}, u32[]{:S(2)}) collective-permute-start(bf16[512,384]{1,0:T(8,128)(2,1)} %add_convert_fusion.13), channel_id=1, source_target_pairs={{0,8},{4,12},{8,0},{12,4},{16,24},{20,28},{24,16},{28,20},{1,9},{5... | collective-permute-start | bytes 1179656 | tf_op jit(solution)/shard_map/ppermute | solution.py:426
  572.8 20.1 %collective-permute-start.83 = (bf16[1024,384]{1,0:T(8,128)(2,1)S(1)}, bf16[1024,384]{1,0:T(8,128)(2,1)S(1)}, u32[]{:S(2)}, u32[]{:S(2)}) collective-permute-start(bf16[1024,384]{1,0:T(8,128)(2,1)S(1)} %pad_maximum_fusion.12.refs_0_.refs_2_), channel_id=1, source_target_pairs={{0,4},{4,0},{8,12},{12,8},{16,20},{20,16},{24,28},{28,24},{1,5},{5... | collective-permute-start | bytes 2359304 | tf_op jit(solution)/shard_map/ppermute | solution.py:426
  573.8 18.2 %collective-permute-start.80 = (bf16[512,384]{1,0:T(8,128)(2,1)S(1)}, bf16[512,384]{1,0:T(8,128)(2,1)}, u32[]{:S(2)}, u32[]{:S(2)}) collective-permute-start(bf16[512,384]{1,0:T(8,128)(2,1)S(1)} %get-tuple-element.346), channel_id=1, source_target_pairs={{0,16},{4,20},{8,24},{12,28},{16,0},{20,4},{24,8},{28,12},{1,17},{... | collective-permute-start | bytes 1179656 | tf_op jit(solution)/shard_map/ppermute | solution.py:426
  594.2 17.9 %collective-permute-start.86 = (bf16[1024,384]{1,0:T(8,128)(2,1)S(1)}, bf16[1024,384]{1,0:T(8,128)(2,1)S(1)}, u32[]{:S(2)}, u32[]{:S(2)}) collective-permute-start(bf16[1024,384]{1,0:T(8,128)(2,1)S(1)} %pad_maximum_fusion.13.refs_1_.refs_3_), channel_id=1, source_target_pairs={{0,4},{4,0},{8,12},{12,8},{16,20},{20,16},{24,28},{28,24},{1,5},{5... | collective-permute-start | bytes 2359304 | tf_op jit(solution)/shard_map/ppermute | solution.py:426
  612.8 17.9 %collective-permute-start.90 = (bf16[1024,384]{1,0:T(8,128)(2,1)S(1)}, bf16[1024,384]{1,0:T(8,128)(2,1)S(1)}, u32[]{:S(2)}, u32[]{:S(2)}) collective-permute-start(bf16[1024,384]{1,0:T(8,128)(2,1)S(1)} %pad_maximum_fusion.14.refs_1_.refs_3_), channel_id=1, source_target_pairs={{0,4},{4,0},{8,12},{12,8},{16,20},{20,16},{24,28},{28,24},{1,5},{5... | collective-permute-start | bytes 2359304 | tf_op jit(solution)/shard_map/ppermute | solution.py:426
  (123 other events, 1322.2 us)

commit v9 on v8

--- a/solution.py
+++ b/solution.py
@@ -15,7 +15,6 @@
 EPSILON = 1e-05
 BF = jnp.bfloat16
 F32 = jnp.float32
-VMEM = 60 << 20
 SMALL = pl.CostEstimate(flops=1 << 20, bytes_accessed=1 << 16, transcendentals=0)
 
 
@@ -106,7 +105,7 @@
         out_specs=pl.BlockSpec((rows, HD), lambda j: (part, j)),
         out_shape=jax.ShapeDtypeStruct((length, columns), BF),
         input_output_aliases={6: 0} if part else {},
-        compiler_params=pltpu.CompilerParams(vmem_limit_bytes=VMEM),
+        compiler_params=pltpu.CompilerParams(vmem_limit_bytes=24 << 20),
         cost_estimate=SMALL,
         name="qkv_rotary",
     )(normed, weight, bias[None, :], table, table, table, *([whole] if part else []))
@@ -158,7 +157,7 @@
             jax.ShapeDtypeStruct((length, heads * HD), BF),
             jax.ShapeDtypeStruct((heads, length, 1), F32),
         ],
-        compiler_params=pltpu.CompilerParams(vmem_limit_bytes=VMEM),
+        compiler_params=pltpu.CompilerParams(vmem_limit_bytes=20 << 20),
         cost_estimate=SMALL,
         name="attend",
     )(prefix, qkv, qkv, qkv, spots[:, None], spots[None, :])
@@ -222,10 +221,49 @@
             scratch_shapes=[pltpu.VMEM((length, HD), F32), pltpu.VMEM((length, HD), F32)],
         ),
         out_shape=jax.ShapeDtypeStruct((length, heads * 3 * HD), BF),
-        compiler_params=pltpu.CompilerParams(vmem_limit_bytes=VMEM),
+        compiler_params=pltpu.CompilerParams(vmem_limit_bytes=32 << 20),
         cost_estimate=SMALL,
         name="attend_back",
     )(prefix, qkv, qkv, qkv, grad_context, log_total, spots[:, None], spots[None, :], table, table, table)
+
+
+def back_rows_kernel(now_ref, grad_ref, weight_ref, *refs):
+    o_ref = refs[-1]
+
+    @pl.when(now_ref[0] == 1)
+    def _():
+        o_ref[...] = contract(grad_ref[...], weight_ref[...], 1, 1)
+
+    if len(refs) == 2:
+
+        @pl.when(now_ref[0] == 0)
+        def _():
+            o_ref[...] = refs[0][...]
+
+
+def back_rows(grad, weight, now, before=None):
+    length, units = grad.shape
+    width = weight.shape[0]
+    tile = 256
+    kept = [] if before is None else [before]
+    return pl.pallas_call(
+        back_rows_kernel,
+        grid_spec=pltpu.PrefetchScalarGridSpec(
+            num_scalar_prefetch=1,
+            grid=(width // tile,),
+            in_specs=[
+                pl.BlockSpec((length, units), lambda j, n: (0, 0)),
+                pl.BlockSpec((tile, units), lambda j, n: (j * n[0], 0)),
+            ]
+            + [pl.BlockSpec((length, tile), lambda j, n: (0, 0))] * len(kept),
+            out_specs=pl.BlockSpec((length, tile), lambda j, n: (0, j * n[0])),
+        ),
+        out_shape=jax.ShapeDtypeStruct((length, width), F32),
+        input_output_aliases={3: 0} if kept else {},
+        compiler_params=pltpu.CompilerParams(vmem_limit_bytes=24 << 20),
+        cost_estimate=SMALL,
+        name="back_rows",
+    )(now.astype(jnp.int32).reshape(1), grad, weight, *kept)
 
 
 def place_kernel(quarter_ref, *refs):
@@ -257,7 +295,7 @@
         ),
         out_shape=jax.ShapeDtypeStruct(shape, F32),
         input_output_aliases={} if first else {1: 0},
-        compiler_params=pltpu.CompilerParams(vmem_limit_bytes=VMEM),
+        compiler_params=pltpu.CompilerParams(vmem_limit_bytes=12 << 20),
         cost_estimate=SMALL,
         name="place_quarters",
     )(quarter.reshape(1), *operands)
@@ -294,7 +332,7 @@
         out_specs=[pl.BlockSpec((rows, width), lambda i: (i + skip, 0))] * 2,
         out_shape=[shape, shape],
         input_output_aliases={4 + count: 0, 5 + count: 1} if into else {},
-        compiler_params=pltpu.CompilerParams(vmem_limit_bytes=VMEM),
+        compiler_params=pltpu.CompilerParams(vmem_limit_bytes=32 << 20),
         cost_estimate=SMALL,
         name="both_norms",
     )(*gains, *blocks, *into)
@@ -346,7 +384,7 @@
             scratch_shapes=[pltpu.VMEM((left, tokens), BF), pltpu.VMEM((tokens, tile), BF)],
         ),
         out_shape=[jax.ShapeDtypeStruct((size, width), BF) for size in sizes],
-        compiler_params=pltpu.CompilerParams(vmem_limit_bytes=VMEM),
+        compiler_params=pltpu.CompilerParams(vmem_limit_bytes=40 << 20),
         cost_estimate=SMALL,
         name="outer_blocks",
     )(quarter.reshape(1), *[a for a, *_ in lefts], *rights)
@@ -375,7 +413,7 @@
         + [pl.BlockSpec((rows, width), lambda i: (0, 0))] * count,
         out_specs=pl.BlockSpec((rows, units), lambda i: (i, 0)),
         out_shape=jax.ShapeDtypeStruct((count * rows, units), BF),
-        compiler_params=pltpu.CompilerParams(vmem_limit_bytes=VMEM),
+        compiler_params=pltpu.CompilerParams(vmem_limit_bytes=36 << 20),
         cost_estimate=SMALL,
         name="back_blocks",
     )(weight, slope, *blocks)
@@ -738,7 +776,9 @@
     chunk = half // 2
     kept_columns = context.shape[1] // 4
     enqueue("fc2", *outer_blocks(hidden_lefts(0), rights, [chunk] * 2, quarter))
-    grad_qkv_far = list(turn(*swapped))
+    grad_norm_attn = back_rows(after(grad_qkv, *queue[0][:1]), qkv_weight, core)
+    (grad_norm_attn,) = turn(grad_norm_attn)
+    grad_qkv_far = []
     walk(swap_walk(gate(grad_qkv), grad_qkv_far))
     lefts = hidden_lefts(1)
     for index, piece in enumerate([context_quarter] + context_far):
@@ -748,7 +788,7 @@
     )
     enqueue("fc2", *parts)
     enqueue("out", out_part)
-    turn()
+    swapped = turn(*swapped)
     grad_inner_far = back_blocks([gate(grad_far[0])] + grad_far[1:], fc2_quarter, slope_far)
     (grad_inner_far,) = turn(grad_inner_far)
     inner_quarter = gate(quarter_of(grad_inner, 1, quarter))
@@ -759,7 +799,7 @@
     )
     (fc1_part,) = turn(fc1_part.astype(BF))
     enqueue("fc1", *cut(fc1_part, [4, 4, 4, 4]))
-    grad_norm_attn = contract(gate(grad_qkv), qkv_weight, 1, 1)
+    grad_norm_attn = back_rows(gate(grad_qkv), qkv_weight, 1 - core, grad_norm_attn)
     (grad_norm_attn,) = turn(grad_norm_attn)
     grad_norm_mlp = contract(gate(grad_inner), fc1_weight, 1, 1)
     (grad_norm_mlp,) = turn(grad_norm_mlp)
@@ -797,7 +837,7 @@
     qkv_part = (
         contract(norm_attn_own, qkv_quarter[:close], 0, 0)
         + contract(norm_attn_rest, qkv_quarter[close:], 0, 0)
-        + contract(norm_attn_far, jnp.concatenate(grad_qkv_far, axis=0), 0, 0)
+        + contract(norm_attn_far, jnp.concatenate([*swapped, *grad_qkv_far], axis=0), 0, 0)
     )
     (qkv_part,) = turn(qkv_part.astype(BF))
     enqueue("qkv", *cut(qkv_part, [4, 4, 4, 2, 1, 1]))

time: 674 us -> 655 us (0.972)
  local copies, waits for them, and re-layouts: 57.2 us -> 102 us
  Pallas kernels: 171 us -> 136 us
  other arithmetic: 77.1 us -> 57.9 us
  matrix products: 115 us -> 107 us
    unnamed x184 -> x262, local copies, waits for them, and re-layouts: 13 us -> 68.9 us
    pallas_call x15, Pallas kernels: 55 us -> 36.6 us  [place_quarters(): pl.pallas_call(place_kernel, grid_spec=pltpu.PrefetchScalarGridSpec(num_s...]
    pallas_call x0 -> x2, Pallas kernels: none -> 9.32 us  [back_rows(): pl.pallas_call(back_rows_kernel, grid_spec=pltpu.PrefetchScalarGridSpec(n...]
    dot_general x10 -> x9, matrix products: 69 us -> 60.1 us  [contract(): lax.dot_general(left_side, right_side, (((left_dim,), (right_dim,)), ((),...]
    convert_element_type x15, other arithmetic: 18.8 us -> 10.3 us  [travel(): low = (low.astype(F32) + got.astype(F32)).astype(BF)]
    pallas_call x4, Pallas kernels: 32.9 us -> 26 us  [both_norms(): pl.pallas_call(functools.partial(norms_kernel, count), grid=(count,), in_...]
    pallas_call x2, Pallas kernels: 17.7 us -> 10.9 us  [project_qkv(): pl.pallas_call(qkv_kernel, grid=(columns // HD,), in_specs=[pl.BlockSpec(...]
  transfers between devices with their start and end apart: 98 -> 98, of which waited for: 34 -> 33; matrix products, arithmetic and copies ran while one was open for 33% -> 29% of each run, Pallas kernels for 25% -> 21%
where the time goes in v9:
time: 655 us; the launch traced here: 645 us
  Pallas kernels  136 us (21%)
  waiting for transfers between devices  126 us (19%)
  starting transfers between devices  109 us (17%)
  matrix products  107 us (16%)
  local copies, waits for them, and re-layouts  102 us (16%)
  other arithmetic  57.9 us (9%)
  between operations  6.74 us (1%)
    ppermute x69, waiting for transfers between devices, flip(): return lax.ppermute(v, 'dp', [(d, d ^ mask) for d in range(dp)])  122 us
    ppermute x69, starting transfers between devices, flip(): return lax.ppermute(v, 'dp', [(d, d ^ mask) for d in range(dp)])  96.8 us
    unnamed x262, local copies, waits for them, and re-layouts  68.9 us
    dot_general x9, matrix products, contract(): lax.dot_general(left_side, right_side, (((left_dim,), (right_dim,)), ((),...  60.1 us
    pallas_call x15, Pallas kernels, place_quarters(): pl.pallas_call(place_kernel, grid_spec=pltpu.PrefetchScalarGridSpec(num_s...  36.6 us
    pallas_call x4, Pallas kernels, both_norms(): pl.pallas_call(functools.partial(norms_kernel, count), grid=(count,), in_...  26 us
    pallas_call x2, Pallas kernels, outer_blocks(): pl.pallas_call(functools.partial(outer_kernel, len(lefts), pieces, len(si...  20.9 us
    dot_general x2, matrix products, units(): jnp.dot(normed, fc1_weight, preferred_element_type=F32)  20.8 us
  transfers between devices with their start and end apart: 98, of which 33 were waited for; matrix products, arithmetic and copies ran while one was open for 29% of the time, Pallas kernels for 21%

profile of v9, /device:TPU:0, one launch (start us, length us, event | category | flops | bytes accessed | tf_op | source)
XLA Modules:
  0.0 644.6 jit_solution(18162486002272109737)
XLA Ops:
  19.1 10.2 %multiply_convert_fusion.2 = (bf16[512,2048]{1,0:T(8,128)(2,1)}, f32[512,2048]{1,0:T(8,128)}) fusion(f32[2048]{0:T(1024)S(1)} %convert_element_type.245, bf16[512,2048]{1,0:T(8,128)(2,1)S(1)} %get-tuple-element.202, bf16[2048,2048]{1,0:T(8,128)(2,1)} %param.32), kind=kOutput, calls=%fused_computation.38 | convolution fusion | flops 4301258752 | bytes 16785408 | tf_op jit(solution)/shard_map/dot_general | solution.py:511
  29.3 5.5 qkv_rotary.2.refs_0_
  43.3 3.3 both_norms.5
  46.6 3.4 copy-done.3
  51.5 2.8 copy-done.9
  54.2 5.4 qkv_rotary.3.q_ref.k_ref.v_ref
  59.7 9.6 %attend.1 = (bf16[1024,512]{1,0:T(8,128)(2,1)S(1)}, f32[2,1024,1]{2,1,0:T(8,128)S(1)}) custom-call(s32[1]{0:T(128)S(6)} %copy.83.prefix_ref, bf16[1024,1536]{1,0:T(8,128)(2,1)S(1)} %qkv_rotary.3.q_ref.k_ref.v_ref, bf16[1024,1536]{1,0:T(8,128)(2,1)S(1)} %qkv_rotary.3.q_ref.k_ref.v_ref, bf16[1024,1536]{1,0:T(8,128)(2,1)S(1)} %qkv_rotary.3.q_ref.k_ref.v_ref, ...), custom_call_target="tpu_custom_call" | custom-call | flops 1048576 | bytes 65536 | tf_op jit(solution)/shard_map/attend/pallas_call | solution.py:139
  74.2 10.5 %multiply_convert_fusion.1 = (bf16[512,2048]{1,0:T(8,128)(2,1)S(1)}, f32[512,2048]{1,0:T(8,128)}) fusion(f32[2048]{0:T(1024)S(1)} %convert_element_type.245, bf16[512,2048]{1,0:T(8,128)(2,1)S(1)} %get-tuple-element.212, bf16[2048,2048]{1,0:T(8,128)(2,1)} %param.32), kind=kOutput, calls=%fused_computation.37 | convolution fusion | flops 4301258752 | bytes 16785408 | tf_op jit(solution)/shard_map/dot_general | solution.py:511
  86.1 4.5 fusion.67
  93.1 4.5 fusion.68
  106.7 15.8 %both_norms.6 = (bf16[3072,2048]{1,0:T(8,128)(2,1)}, bf16[3072,2048]{1,0:T(8,128)(2,1)}) custom-call(bf16[1,2048]{1,0:T(2,128)(2,1)S(1)} %broadcast_in_dim.16.refs_0_, bf16[1,2048]{1,0:T(2,128)(2,1)S(1)} %broadcast_in_dim.17.refs_1_, bf16[1,2048]{1,0:T(2,128)(2,1)S(1)} %broadcast_in_dim.18.refs_2_, bf16[1,2048]{1,0:T(2,128)(2,1)S(1)} %broadcast_in_dim.19.refs_3_, ...), custom_call_target="tpu_custom_call" | custom-call | flops 1048576 | bytes 65536 | tf_op jit(solution)/shard_map/both_norms/pallas_call | solution.py:326
  128.7 4.7 copy-done.36
  133.4 4.8 both_norms.7
  138.2 4.8 copy-done.37
  144.2 3.1 fusion.30
  153.8 14.7 %fusion.21 = (f32[3072,512]{1,0:T(8,128)}, bf16[3072,512]{1,0:T(8,128)(2,1)}) fusion(f32[512]{0:T(512)S(1)} %dynamic-slice_convert_fusion, bf16[3072,2048]{1,0:T(8,128)(2,1)} %get-tuple-element.244, bf16[2048,2048]{1,0:T(8,128)(2,1)} %param.32, s32[]{:T(128)S(6)} %select_n.81), kind=kOutput, calls=%fused_computation.28 | convolution fusion | flops 6459752448 | bytes 24119300 | tf_op jit(solution)/shard_map/dot_general | solution.py:622
  168.5 3.1 constant_dynamic-slice_fusion.6.weight_ref
  171.7 2.7 collective-permute-done.27
  184.8 9.9 %attend_back.1.grad_ref = bf16[1024,1536]{1,0:T(8,128)(2,1)S(1)} custom-call(s32[1]{0:T(128)S(6)} %copy.83.prefix_ref, bf16[1024,1536]{1,0:T(8,128)(2,1)S(1)} %copy-done.5, bf16[1024,1536]{1,0:T(8,128)(2,1)S(1)} %copy-done.5, bf16[1024,1536]{1,0:T(8,128)(2,1)S(1)} %copy-done.5, bf16[1024,512]{1,0:T(8,128)(2,1)S(1)} %convolution_convert_fusion.g_ref, ...), custom_call_target="tpu_custom_call" | custom-call | flops 1048576 | bytes 65536 | tf_op jit(solution)/shard_map/attend_back/pallas_call | solution.py:205
  194.7 9.6 %collective-permute-done.32.refs_12_.refs_16_.refs_8_ = bf16[256,2048]{1,0:T(8,128)(2,1)S(1)} collective-permute-done((bf16[256,2048]{1,0:T(8,128)(2,1)S(1)}, bf16[256,2048]{1,0:T(8,128)(2,1)S(1)}, u32[]{:S(2)}, u32[]{:S(2)}) %collective-permute-start.32) | collective-permute-done | bytes 1048608 | tf_op jit(solution)/shard_map/ppermute | solution.py:464
  208.1 17.5 %fusion.17 = bf16[1024,2048]{1,0:T(8,128)(2,1)} fusion(f32[512,2048]{1,0:T(8,128)} %get-tuple-element.438, f32[512,2048]{1,0:T(8,128)} %get-tuple-element.436, bf16[1024,2048]{1,0:T(8,128)(2,1)} %copy-done.99, bf16[2048,2048]{1,0:T(8,128)(2,1)} %param.34), kind=kOutput, calls=%fused_computation.21 | convolution fusion | flops 8613003264 | bytes 25165824 | tf_op jit(solution)/shard_map/dot_general | solution.py:35
  244.3 9.3 %outer_blocks.2 = (bf16[128,2048]{1,0:T(8,128)(2,1)}, bf16[128,2048]{1,0:T(8,128)(2,1)S(1)}) custom-call(s32[1]{0:T(128)} %bitcast.9._.quarter_ref, bf16[512,2048]{1,0:T(8,128)(2,1)} %get-tuple-element.219.refs_0_, bf16[512,2048]{1,0:T(8,128)(2,1)} %copy-done.102, bf16[3072,512]{1,0:T(8,128)(2,1)} %get-tuple-element.247.refs_2_, ...), custom_call_target="tpu_custom_call" | custom-call | flops 1048576 | bytes 65536 | tf_op jit(solution)/shard_map/outer_blocks/pallas_call | solution.py:376
  254.4 3.4 copy-done.11
  277.7 11.6 %outer_blocks.3 = (bf16[128,2048]{1,0:T(8,128)(2,1)S(1)}, bf16[128,2048]{1,0:T(8,128)(2,1)}, bf16[128,2048]{1,0:T(8,128)(2,1)S(1)}) custom-call(s32[1]{0:T(128)} %bitcast.9._.quarter_ref, bf16[512,2048]{1,0:T(8,128)(2,1)} %get-tuple-element.219.refs_0_, bf16[512,2048]{1,0:T(8,128)(2,1)} %copy-done.102, bf16[3072,512]{1,0:T(8,128)(2,1)} %get-tuple-element.247.refs_2_, ...), custom_call_target="tpu_custom_call" | custom-call | flops 1048576 | bytes 65536 | tf_op jit(solution)/shard_map/outer_blocks/pallas_call | solution.py:376
  289.3 6.4 collective-permute-done.45
  302.5 13.2 %back_blocks.1 = bf16[3072,512]{1,0:T(8,128)(2,1)S(1)} custom-call(bf16[512,2048]{1,0:T(8,128)(2,1)S(1)} %copy-done.74, f32[3072,512]{1,0:T(8,128)} %get-tuple-element.407.slope_ref, bf16[256,2048]{1,0:T(8,128)(2,1)S(1)} %copy-done.45, bf16[256,2048]{1,0:T(8,128)(2,1)S(1)} %copy-done.53, bf16[256,2048]{1,0:T(8,128)(2,1)S(1)} %copy-done.35, ...), custom_call_target="tpu_custom_call" | custom-call | flops 1048576 | bytes 65536 | tf_op jit(solution)/shard_map/back_blocks/pallas_call | solution.py:406
  315.7 9.0 %collective-permute-done.48 = bf16[128,2048]{1,0:T(8,128)(2,1)S(1)} collective-permute-done((bf16[128,2048]{1,0:T(8,128)(2,1)S(1)}, bf16[128,2048]{1,0:T(8,128)(2,1)S(1)}, u32[]{:S(2)}, u32[]{:S(2)}) %collective-permute-start.48) | collective-permute-done | bytes 524320 | tf_op jit(solution)/shard_map/ppermute | solution.py:464
  329.5 10.8 %add_convert_fusion = bf16[2048,512]{1,0:T(8,128)(2,1)} fusion(f32[2048,512]{1,0:T(8,128)S(1)} %fusion.48, f32[2048,512]{1,0:T(8,128)S(1)} %fusion.46, bf16[3072,2048]{1,0:T(8,128)(2,1)} %get-tuple-element.244, bf16[3072,512]{1,0:T(8,128)(2,1)S(1)} %back_blocks.1), kind=kOutput, calls=%fused_computation.36 | convolution fusion | flops 6445596672 | bytes 26214400 | tf_op jit(solution)/shard_map/dot_general | solution.py:35
  342.9 11.5 %collective-permute-done.52.refs_1_.refs_3_ = bf16[256,2048]{1,0:T(8,128)(2,1)S(1)} collective-permute-done((bf16[256,2048]{1,0:T(8,128)(2,1)S(1)}, bf16[256,2048]{1,0:T(8,128)(2,1)S(1)}, u32[]{:S(2)}, u32[]{:S(2)}) %collective-permute-start.52) | collective-permute-done | bytes 1048608 | tf_op jit(solution)/shard_map/ppermute | solution.py:464
  356.9 2.9 collective-permute-start.49
  364.3 2.8 copy-done.10
  367.1 3.4 copy-done.12
  370.4 9.0 %back_rows.3 = f32[1024,2048]{1,0:T(8,128)S(1)} custom-call(s32[1]{0:T(128)} %bitcast.12.now_ref, bf16[1024,1536]{1,0:T(8,128)(2,1)S(1)} %attend_back.1.grad_ref, bf16[2048,1536]{1,0:T(8,128)(2,1)S(1)} %copy-done.10, f32[1024,2048]{1,0:T(8,128)S(1)} %copy-done.12), custom_call_target="tpu_custom_call", output_to_operand_aliasing={{}: (3, {})} | custom-call | flops 1048576 | bytes 65536 | tf_op jit(solution)/shard_map/back_rows/pallas_call | solution.py:249
  379.5 3.4 copy-done.13
  384.2 8.1 %collective-permute-done.49 = bf16[128,2048]{1,0:T(8,128)(2,1)} collective-permute-done((bf16[128,2048]{1,0:T(8,128)(2,1)}, bf16[128,2048]{1,0:T(8,128)(2,1)}, u32[]{:S(2)}, u32[]{:S(2)}) %collective-permute-start.49) | collective-permute-done | bytes 524320 | tf_op jit(solution)/shard_map/ppermute | solution.py:464
  396.9 12.7 %fusion.69 = f32[1024,2048]{1,0:T(8,128)S(1)} fusion(bf16[1024,2048]{1,0:T(8,128)(2,1)} %fusion.17, bf16[2048,2048]{1,0:T(8,128)(2,1)} %param.32), kind=kOutput, calls=%fused_computation.164 | convolution fusion | flops 8589934592 | bytes 20971520 | tf_op jit(solution)/shard_map/dot_general | solution.py:35
  412.3 5.7 collective-permute-done.56
  419.1 3.8 collective-permute-start.59
  424.5 2.9 convert_reduce_fusion
  427.4 3.7 fusion.11
  431.2 10.3 %fusion.59 = (f32[2048]{0:T(1024)S(1)}, f32[2048]{0:T(1024)S(1)}, f32[1024]{0:T(1024)S(1)}, f32[1024]{0:T(1024)S(1)}, f32[1024,2048]{1,0:T(8,128)}, /*index=5*/f32[2048]{0:T(1024)S(1)}, f32[2048]{0:T(1024)S(1)}) fusion(f32[1024,2048]{1,0:T(8,128)S(1)} %fusion.69, f32[1024]{0:T(1024)S(1)} %add_rsqrt_fusion, f32[1024]{0:T(1024)S(1)} %broadcast_multiply_fusion.2, ...), kind=kLoop, calls=%fused_computation.155 | loop fusion | flops 46127104 | bytes 29425664 | tf_op jit(solution)/shard_map/reduce_sum | solution.py:820
  446.6 8.7 %fusion.10 = f32[1024,2048]{1,0:T(8,128)} fusion(f32[1024,2048]{1,0:T(8,128)} %get-tuple-element.404, f32[1024]{0:T(1024)S(1)} %broadcast_multiply_fusion, f32[1024]{0:T(1024)S(1)} %broadcast_multiply_fusion.1, f32[1024]{0:T(1024)S(1)} %add_rsqrt_fusion, f32[1024]{0:T(1024)S(1)} %broadcast_multiply_fusion.2, bf16[256,2048]{1,0:T(8,128)(2,1)S(1)} %copy-done.23, ...), kind=kLoop, calls=%fused_computation.14 | loop fusion | flops 29360128 | bytes 20987904 | tf_op jit(solution)/shard_map/mul | solution.py:826
  460.6 4.0 fusion.31
  471.6 3.0 fusion.52
  474.6 10.0 %add_convert_fusion.1 = bf16[2048,384]{1,0:T(8,128)(2,1)} fusion(f32[2048,384]{1,0:T(8,128)S(1)} %fusion.54, f32[2048,384]{1,0:T(8,128)} %fusion.52, bf16[3072,2048]{1,0:T(8,128)(2,1)S(1)} %bitcast.87, bf16[1024,384]{1,0:T(8,128)(2,1)} %collective-permute-done.44, bf16[1024,384]{1,0:T(8,128)(2,1)} %collective-permute-done.47, ...), kind=kOutput, calls=%fused_computation.41 | convolution fusion | flops 4841275392 | bytes 22806528 | tf_op jit(solution)/shard_map/dot_general | solution.py:35
  486.8 2.8 collective-permute-done.67.refs_1_.refs_3_
  504.7 10.8 %collective-permute-done.64 = bf16[512,512]{1,0:T(8,128)(2,1)S(1)} collective-permute-done((bf16[512,512]{1,0:T(8,128)(2,1)S(1)}, bf16[512,512]{1,0:T(8,128)(2,1)S(1)}, u32[]{:S(2)}, u32[]{:S(2)}) %collective-permute-start.64) | collective-permute-done | bytes 524320 | tf_op jit(solution)/shard_map/ppermute | solution.py:464
  523.0 4.0 place_quarters.17.refs_0_
  527.0 9.0 %collective-permute-done.75 = bf16[512,384]{1,0:T(8,128)(2,1)S(1)} collective-permute-done((bf16[512,384]{1,0:T(8,128)(2,1)S(1)}, bf16[512,384]{1,0:T(8,128)(2,1)S(1)}, u32[]{:S(2)}, u32[]{:S(2)}) %collective-permute-start.75) | collective-permute-done | bytes 393248 | tf_op jit(solution)/shard_map/ppermute | solution.py:464
  542.1 3.0 collective-permute-start.79
  545.6 2.7 place_quarters.19.refs_0_
  550.7 6.6 %collective-permute-done.76 = bf16[512,384]{1,0:T(8,128)(2,1)S(1)} collective-permute-done((bf16[512,384]{1,0:T(8,128)(2,1)S(1)}, bf16[512,384]{1,0:T(8,128)(2,1)S(1)}, u32[]{:S(2)}, u32[]{:S(2)}) %collective-permute-start.76) | collective-permute-done | bytes 393248 | tf_op jit(solution)/shard_map/ppermute | solution.py:464
  557.5 5.6 collective-permute-done.77.refs_2_.refs_4_
  565.4 3.3 collective-permute-start.81
  569.1 4.0 place_quarters.21
  575.5 4.1 collective-permute-done.80
  584.1 3.1 collective-permute-start.85
  591.9 6.0 collective-permute-done.87
  598.9 2.9 collective-permute-start.89
  601.9 3.4 collective-permute-start.88
  608.5 2.8 collective-permute-done.91
  611.3 4.4 collective-permute-done.90.refs_2_.refs_4_
  616.1 2.8 collective-permute-start.92
  618.9 4.0 collective-permute-start.93
  (551 shorter events, 233.1 us)
Async XLA Ops:
  1.2 35.3 %collective-permute-start.3 = (bf16[256,2048]{1,0:T(8,128)(2,1)}, bf16[256,2048]{1,0:T(8,128)(2,1)}, u32[]{:S(2)}, u32[]{:S(2)}) collective-permute-start(bf16[256,2048]{1,0:T(8,128)(2,1)} %refs_4_.1), channel_id=1, source_target_pairs={{0,4},{4,0},{8,12},{12,8},{16,20},{20,16},{24,28},{28,24},{1,5},{5... | collective-permute-start | bytes 3145736 | tf_op jit(solution)/shard_map/ppermute | solution.py:464
  3.8 32.8 %collective-permute-start.4 = (bf16[256,2048]{1,0:T(8,128)(2,1)}, bf16[256,2048]{1,0:T(8,128)(2,1)}, u32[]{:S(2)}, u32[]{:S(2)}) collective-permute-start(bf16[256,2048]{1,0:T(8,128)(2,1)} %refs_4_.1), channel_id=1, source_target_pairs={{0,8},{4,12},{8,0},{12,4},{16,24},{20,28},{24,16},{28,20},{1,9},{5... | collective-permute-start | bytes 3145736 | tf_op jit(solution)/shard_map/ppermute | solution.py:464
  5.3 31.2 %collective-permute-start.5 = (bf16[256,2048]{1,0:T(8,128)(2,1)}, bf16[256,2048]{1,0:T(8,128)(2,1)}, u32[]{:S(2)}, u32[]{:S(2)}) collective-permute-start(bf16[256,2048]{1,0:T(8,128)(2,1)} %refs_4_.1), channel_id=1, source_target_pairs={{0,2},{1,3},{2,0},{3,1},{4,6},{5,7},{6,4},{7,5},{8,10},{9,11},{10,... | collective-permute-start | bytes 3145736 | tf_op jit(solution)/shard_map/ppermute | solution.py:457
  18.5 18.1 %collective-permute-start.2 = (f32[8,128]{1,0:T(8,128)S(1)}, f32[8,128]{1,0:T(8,128)S(1)}, u32[]{:S(2)}, u32[]{:S(2)}) collective-permute-start(f32[8,128]{1,0:T(8,128)S(1)} %broadcast_add_fusion), channel_id=1, source_target_pairs={{0,4},{4,0},{8,12},{12,8},{16,20},{20,16},{24,28},{28,24},{1,5},{5... | collective-permute-start | bytes 12296 | tf_op jit(solution)/shard_map/ppermute | solution.py:464
  36.9 33.8 %collective-permute-start.8 = (bf16[256,2048]{1,0:T(8,128)(2,1)}, bf16[256,2048]{1,0:T(8,128)(2,1)}, u32[]{:S(2)}, u32[]{:S(2)}) collective-permute-start(bf16[256,2048]{1,0:T(8,128)(2,1)} %collective-permute-done.4.refs_8_), channel_id=1, source_target_pairs={{0,4},{4,0},{8,12},{12,8},{16,20},{20,16},{24,28},{28,24},{1,5},{5... | collective-permute-start | bytes 3145736 | tf_op jit(solution)/shard_map/ppermute | solution.py:464
  38.3 33.1 %collective-permute-start.9 = (bf16[256,2048]{1,0:T(8,128)(2,1)}, bf16[256,2048]{1,0:T(8,128)(2,1)}, u32[]{:S(2)}, u32[]{:S(2)}) collective-permute-start(bf16[256,2048]{1,0:T(8,128)(2,1)} %collective-permute-done.3.refs_4_), channel_id=1, source_target_pairs={{0,2},{1,3},{2,0},{3,1},{4,6},{5,7},{6,4},{7,5},{8,10},{9,11},{10,... | collective-permute-start | bytes 3145736 | tf_op jit(solution)/shard_map/ppermute | solution.py:457
  38.8 33.3 %collective-permute-start.10 = (bf16[256,2048]{1,0:T(8,128)(2,1)}, bf16[256,2048]{1,0:T(8,128)(2,1)}, u32[]{:S(2)}, u32[]{:S(2)}) collective-permute-start(bf16[256,2048]{1,0:T(8,128)(2,1)} %collective-permute-done.5.refs_4_), channel_id=1, source_target_pairs={{0,8},{4,12},{8,0},{12,4},{16,24},{20,28},{24,16},{28,20},{1,9},{5... | collective-permute-start | bytes 3145736 | tf_op jit(solution)/shard_map/ppermute | solution.py:464
  41.0 43.8 %collective-permute-start.14 = (bf16[256,2048]{1,0:T(8,128)(2,1)}, bf16[256,2048]{1,0:T(8,128)(2,1)S(1)}, u32[]{:S(2)}, u32[]{:S(2)}) collective-permute-start(bf16[256,2048]{1,0:T(8,128)(2,1)} %collective-permute-done.3.refs_4_), channel_id=1, source_target_pairs={{0,1},{1,0},{2,3},{3,2},{4,5},{5,4},{6,7},{7,6},{8,9},{9,8},{10,11... | collective-permute-start | bytes 3145736 | tf_op jit(solution)/shard_map/ppermute | solution.py:453
  41.6 28.8 %collective-permute-start.7 = (f32[8,128]{1,0:T(8,128)S(1)}, f32[8,128]{1,0:T(8,128)S(1)}, u32[]{:S(2)}, u32[]{:S(2)}) collective-permute-start(f32[8,128]{1,0:T(8,128)S(1)} %fusion.94), channel_id=1, source_target_pairs={{0,8},{4,12},{8,0},{12,4},{16,24},{20,28},{24,16},{28,20},{1,9},{5... | collective-permute-start | bytes 12296 | tf_op jit(solution)/shard_map/ppermute | solution.py:464
  103.4 19.0 %collective-permute-start.24 = (bf16[128,2048]{1,0:T(8,128)(2,1)S(1)}, bf16[128,2048]{1,0:T(8,128)(2,1)S(1)}, u32[]{:S(2)}, u32[]{:S(2)}) collective-permute-start(bf16[128,2048]{1,0:T(8,128)(2,1)S(1)} %slice.136), channel_id=1, source_target_pairs={{0,4},{4,0},{8,12},{12,8},{16,20},{20,16},{24,28},{28,24},{1,5},{5... | collective-permute-start | bytes 1572872 | tf_op jit(solution)/shard_map/ppermute | solution.py:464
  104.7 17.8 %collective-permute-start.25 = (bf16[128,2048]{1,0:T(8,128)(2,1)S(1)}, bf16[128,2048]{1,0:T(8,128)(2,1)S(1)}, u32[]{:S(2)}, u32[]{:S(2)}) collective-permute-start(bf16[128,2048]{1,0:T(8,128)(2,1)S(1)} %slice.137), channel_id=1, source_target_pairs={{0,8},{4,12},{8,0},{12,4},{16,24},{20,28},{24,16},{28,20},{1,9},{5... | collective-permute-start | bytes 1572872 | tf_op jit(solution)/shard_map/ppermute | solution.py:464
  106.1 36.8 %collective-permute-start.21 = (bf16[256,2048]{1,0:T(8,128)(2,1)}, bf16[256,2048]{1,0:T(8,128)(2,1)}, u32[]{:S(2)}, u32[]{:S(2)}) collective-permute-start(bf16[256,2048]{1,0:T(8,128)(2,1)} %fusion.43), channel_id=1, source_target_pairs={{0,2},{1,3},{2,0},{3,1},{4,6},{5,7},{6,4},{7,5},{8,10},{9,11},{10,... | collective-permute-start | bytes 3145736 | tf_op jit(solution)/shard_map/ppermute | solution.py:461
  125.5 17.4 %collective-permute-start.22 = (bf16[256,2048]{1,0:T(8,128)(2,1)}, bf16[256,2048]{1,0:T(8,128)(2,1)}, u32[]{:S(2)}, u32[]{:S(2)}) collective-permute-start(bf16[256,2048]{1,0:T(8,128)(2,1)} %fusion.44), channel_id=1, source_target_pairs={{0,1},{1,0},{2,3},{3,2},{4,5},{5,4},{6,7},{7,6},{8,9},{9,8},{10,11... | collective-permute-start | bytes 3145736 | tf_op jit(solution)/shard_map/ppermute | solution.py:453
  126.0 16.9 %collective-permute-start.23 = (f32[8,128]{1,0:T(8,128)S(1)}, f32[8,128]{1,0:T(8,128)S(1)}, u32[]{:S(2)}, u32[]{:S(2)}) collective-permute-start(f32[8,128]{1,0:T(8,128)S(1)} %add.317), channel_id=1, source_target_pairs={{0,16},{4,20},{8,24},{12,28},{16,0},{20,4},{24,8},{28,12},{1,17},{... | collective-permute-start | bytes 12296 | tf_op jit(solution)/shard_map/ppermute | solution.py:464
  149.6 24.8 %collective-permute-start.27 = (bf16[256,2048]{1,0:T(8,128)(2,1)S(1)}, bf16[256,2048]{1,0:T(8,128)(2,1)S(1)}, u32[]{:S(2)}, u32[]{:S(2)}) collective-permute-start(bf16[256,2048]{1,0:T(8,128)(2,1)S(1)} %get-tuple-element.243), channel_id=1, source_target_pairs={{0,2},{1,3},{2,0},{3,1},{4,6},{5,7},{6,4},{7,5},{8,10},{9,11},{10,... | collective-permute-start | bytes 3145736 | tf_op jit(solution)/shard_map/ppermute | solution.py:457
  151.1 24.5 %collective-permute-start.28 = (bf16[256,2048]{1,0:T(8,128)(2,1)S(1)}, bf16[256,2048]{1,0:T(8,128)(2,1)S(1)}, u32[]{:S(2)}, u32[]{:S(2)}) collective-permute-start(bf16[256,2048]{1,0:T(8,128)(2,1)S(1)} %get-tuple-element.243), channel_id=1, source_target_pairs={{0,4},{4,0},{8,12},{12,8},{16,20},{20,16},{24,28},{28,24},{1,5},{5... | collective-permute-start | bytes 3145736 | tf_op jit(solution)/shard_map/ppermute | solution.py:464
  152.7 24.2 %collective-permute-start.29 = (bf16[256,2048]{1,0:T(8,128)(2,1)S(1)}, bf16[256,2048]{1,0:T(8,128)(2,1)S(1)}, u32[]{:S(2)}, u32[]{:S(2)}) collective-permute-start(bf16[256,2048]{1,0:T(8,128)(2,1)S(1)} %get-tuple-element.243), channel_id=1, source_target_pairs={{0,8},{4,12},{8,0},{12,4},{16,24},{20,28},{24,16},{28,20},{1,9},{5... | collective-permute-start | bytes 3145736 | tf_op jit(solution)/shard_map/ppermute | solution.py:464
  153.8 23.2 %collective-permute-start.30 = (bf16[256,2048]{1,0:T(8,128)(2,1)S(1)}, bf16[256,2048]{1,0:T(8,128)(2,1)S(1)}, u32[]{:S(2)}, u32[]{:S(2)}) collective-permute-start(bf16[256,2048]{1,0:T(8,128)(2,1)S(1)} %get-tuple-element.243), channel_id=1, source_target_pairs={{0,1},{1,0},{2,3},{3,2},{4,5},{5,4},{6,7},{7,6},{8,9},{9,8},{10,11... | collective-permute-start | bytes 3145736 | tf_op jit(solution)/shard_map/ppermute | solution.py:453
  177.1 27.2 %collective-permute-start.34 = (bf16[256,2048]{1,0:T(8,128)(2,1)S(1)}, bf16[256,2048]{1,0:T(8,128)(2,1)S(1)}, u32[]{:S(2)}, u32[]{:S(2)}) collective-permute-start(bf16[256,2048]{1,0:T(8,128)(2,1)S(1)} %collective-permute-done.27), channel_id=1, source_target_pairs={{0,8},{4,12},{8,0},{12,4},{16,24},{20,28},{24,16},{28,20},{1,9},{5... | collective-permute-start | bytes 3145736 | tf_op jit(solution)/shard_map/ppermute | solution.py:464
  178.2 26.1 %collective-permute-start.33 = (bf16[256,2048]{1,0:T(8,128)(2,1)S(1)}, bf16[256,2048]{1,0:T(8,128)(2,1)S(1)}, u32[]{:S(2)}, u32[]{:S(2)}) collective-permute-start(bf16[256,2048]{1,0:T(8,128)(2,1)S(1)} %collective-permute-done.28.refs_4_.refs_8_.refs_0_), channel_id=1, source_target_pairs={{0,2},{1,3},{2,0},{3,1},{4,6},{5,7},{6,4},{7,5},{8,10},{9,11},{10,... | collective-permute-start | bytes 3145736 | tf_op jit(solution)/shard_map/ppermute | solution.py:457
  178.7 29.1 %collective-permute-start.37 = (bf16[256,2048]{1,0:T(8,128)(2,1)S(1)}, bf16[256,2048]{1,0:T(8,128)(2,1)S(1)}, u32[]{:S(2)}, u32[]{:S(2)}) collective-permute-start(bf16[256,2048]{1,0:T(8,128)(2,1)S(1)} %collective-permute-done.28.refs_4_.refs_8_.refs_0_), channel_id=1, source_target_pairs={{0,1},{1,0},{2,3},{3,2},{4,5},{5,4},{6,7},{7,6},{8,9},{9,8},{10,11... | collective-permute-start | bytes 3145736 | tf_op jit(solution)/shard_map/ppermute | solution.py:453
  178.7 25.6 %collective-permute-start.32 = (bf16[256,2048]{1,0:T(8,128)(2,1)S(1)}, bf16[256,2048]{1,0:T(8,128)(2,1)S(1)}, u32[]{:S(2)}, u32[]{:S(2)}) collective-permute-start(bf16[256,2048]{1,0:T(8,128)(2,1)S(1)} %collective-permute-done.29.refs_8_.refs_12_.refs_4_), channel_id=1, source_target_pairs={{0,4},{4,0},{8,12},{12,8},{16,20},{20,16},{24,28},{28,24},{1,5},{5... | collective-permute-start | bytes 3145736 | tf_op jit(solution)/shard_map/ppermute | solution.py:464
  180.0 28.1 %collective-permute-start.39 = (bf16[256,2048]{1,0:T(8,128)(2,1)S(1)}, bf16[256,2048]{1,0:T(8,128)(2,1)S(1)}, u32[]{:S(2)}, u32[]{:S(2)}) collective-permute-start(bf16[256,2048]{1,0:T(8,128)(2,1)S(1)} %collective-permute-done.29.refs_8_.refs_12_.refs_4_), channel_id=1, source_target_pairs={{0,1},{1,0},{2,3},{3,2},{4,5},{5,4},{6,7},{7,6},{8,9},{9,8},{10,11... | collective-permute-start | bytes 3145736 | tf_op jit(solution)/shard_map/ppermute | solution.py:453
  205.3 20.4 %collective-permute-start.38 = (bf16[256,2048]{1,0:T(8,128)(2,1)S(1)}, bf16[256,2048]{1,0:T(8,128)(2,1)S(1)}, u32[]{:S(2)}, u32[]{:S(2)}) collective-permute-start(bf16[256,2048]{1,0:T(8,128)(2,1)S(1)} %collective-permute-done.33.refs_6_.refs_10_.refs_2_), channel_id=1, source_target_pairs={{0,1},{1,0},{2,3},{3,2},{4,5},{5,4},{6,7},{7,6},{8,9},{9,8},{10,11... | collective-permute-start | bytes 3145736 | tf_op jit(solution)/shard_map/ppermute | solution.py:453
  206.2 20.4 %collective-permute-start.40 = (bf16[256,2048]{1,0:T(8,128)(2,1)S(1)}, bf16[256,2048]{1,0:T(8,128)(2,1)S(1)}, u32[]{:S(2)}, u32[]{:S(2)}) collective-permute-start(bf16[256,2048]{1,0:T(8,128)(2,1)S(1)} %collective-permute-done.34.refs_10_.refs_14_.refs_6_), channel_id=1, source_target_pairs={{0,1},{1,0},{2,3},{3,2},{4,5},{5,4},{6,7},{7,6},{8,9},{9,8},{10,11... | collective-permute-start | bytes 3145736 | tf_op jit(solution)/shard_map/ppermute | solution.py:453
  206.6 19.0 %collective-permute-start.35 = (bf16[128,2048]{1,0:T(8,128)(2,1)}, bf16[128,2048]{1,0:T(8,128)(2,1)}, u32[]{:S(2)}, u32[]{:S(2)}) collective-permute-start(bf16[128,2048]{1,0:T(8,128)(2,1)} %slice.139), channel_id=1, source_target_pairs={{0,4},{4,0},{8,12},{12,8},{16,20},{20,16},{24,28},{28,24},{1,5},{5... | collective-permute-start | bytes 1572872 | tf_op jit(solution)/shard_map/ppermute | solution.py:464
  207.8 17.8 %collective-permute-start.36 = (bf16[128,2048]{1,0:T(8,128)(2,1)}, bf16[128,2048]{1,0:T(8,128)(2,1)}, u32[]{:S(2)}, u32[]{:S(2)}) collective-permute-start(bf16[128,2048]{1,0:T(8,128)(2,1)} %slice.140), channel_id=1, source_target_pairs={{0,8},{4,12},{8,0},{12,4},{16,24},{20,28},{24,16},{28,20},{1,9},{5... | collective-permute-start | bytes 1572872 | tf_op jit(solution)/shard_map/ppermute | solution.py:464
  208.1 19.6 %collective-permute-start.41 = (bf16[256,2048]{1,0:T(8,128)(2,1)S(1)}, bf16[256,2048]{1,0:T(8,128)(2,1)S(1)}, u32[]{:S(2)}, u32[]{:S(2)}) collective-permute-start(bf16[256,2048]{1,0:T(8,128)(2,1)S(1)} %collective-permute-done.32.refs_12_.refs_16_.refs_8_), channel_id=1, source_target_pairs={{0,1},{1,0},{2,3},{3,2},{4,5},{5,4},{6,7},{7,6},{8,9},{9,8},{10,11... | collective-permute-start | bytes 3145736 | tf_op jit(solution)/shard_map/ppermute | solution.py:453
  234.0 55.3 %collective-permute-start.46 = (bf16[1024,384]{1,0:T(8,128)(2,1)}, bf16[1024,384]{1,0:T(8,128)(2,1)}, u32[]{:S(2)}, u32[]{:S(2)}) collective-permute-start(bf16[1024,384]{1,0:T(8,128)(2,1)} %get-tuple-element.411), channel_id=1, source_target_pairs={{0,4},{4,0},{8,12},{12,8},{16,20},{20,16},{24,28},{28,24},{1,5},{5... | collective-permute-start | bytes 2359304 | tf_op jit(solution)/shard_map/ppermute | solution.py:464
  235.6 53.8 %collective-permute-start.47 = (bf16[1024,384]{1,0:T(8,128)(2,1)}, bf16[1024,384]{1,0:T(8,128)(2,1)}, u32[]{:S(2)}, u32[]{:S(2)}) collective-permute-start(bf16[1024,384]{1,0:T(8,128)(2,1)} %get-tuple-element.410), channel_id=1, source_target_pairs={{0,8},{4,12},{8,0},{12,4},{16,24},{20,28},{24,16},{28,20},{1,9},{5... | collective-permute-start | bytes 2359304 | tf_op jit(solution)/shard_map/ppermute | solution.py:464
  257.8 37.9 %collective-permute-start.45 = (bf16[128,2048]{1,0:T(8,128)(2,1)}, bf16[128,2048]{1,0:T(8,128)(2,1)}, u32[]{:S(2)}, u32[]{:S(2)}) collective-permute-start(bf16[128,2048]{1,0:T(8,128)(2,1)} %get-tuple-element.269), channel_id=1, source_target_pairs={{0,16},{4,20},{8,24},{12,28},{16,0},{20,4},{24,8},{28,12},{1,17},{... | collective-permute-start | bytes 1572872 | tf_op jit(solution)/shard_map/ppermute | solution.py:464
  259.2 56.5 %collective-permute-start.43 = (bf16[128,2048]{1,0:T(8,128)(2,1)}, bf16[128,2048]{1,0:T(8,128)(2,1)}, u32[]{:S(2)}, u32[]{:S(2)}) collective-permute-start(bf16[128,2048]{1,0:T(8,128)(2,1)} %copy-done.89), channel_id=1, source_target_pairs={{0,16},{4,20},{8,24},{12,28},{16,0},{20,4},{24,8},{28,12},{1,17},{... | collective-permute-start | bytes 1572872 | tf_op jit(solution)/shard_map/ppermute | solution.py:464
  261.7 54.0 %collective-permute-start.44 = (bf16[1024,384]{1,0:T(8,128)(2,1)}, bf16[1024,384]{1,0:T(8,128)(2,1)}, u32[]{:S(2)}, u32[]{:S(2)}) collective-permute-start(bf16[1024,384]{1,0:T(8,128)(2,1)} %constant_dynamic-slice_fusion.4), channel_id=1, source_target_pairs={{0,12},{4,8},{8,4},{12,0},{16,28},{20,24},{24,20},{28,16},{1,13},{... | collective-permute-start | bytes 2359304 | tf_op jit(solution)/shard_map/ppermute | solution.py:464
  297.0 27.7 %collective-permute-start.48 = (bf16[128,2048]{1,0:T(8,128)(2,1)S(1)}, bf16[128,2048]{1,0:T(8,128)(2,1)S(1)}, u32[]{:S(2)}, u32[]{:S(2)}) collective-permute-start(bf16[128,2048]{1,0:T(8,128)(2,1)S(1)} %add_convert_fusion.10), channel_id=1, source_target_pairs={{0,8},{4,12},{8,0},{12,4},{16,24},{20,28},{24,16},{28,20},{1,9},{5... | collective-permute-start | bytes 1572872 | tf_op jit(solution)/shard_map/ppermute | solution.py:464
  298.4 41.9 %collective-permute-start.50 = (bf16[128,2048]{1,0:T(8,128)(2,1)S(1)}, bf16[128,2048]{1,0:T(8,128)(2,1)S(1)}, u32[]{:S(2)}, u32[]{:S(2)}) collective-permute-start(bf16[128,2048]{1,0:T(8,128)(2,1)S(1)} %get-tuple-element.282), channel_id=1, source_target_pairs={{0,16},{4,20},{8,24},{12,28},{16,0},{20,4},{24,8},{28,12},{1,17},{... | collective-permute-start | bytes 1572872 | tf_op jit(solution)/shard_map/ppermute | solution.py:464
  329.0 25.3 %collective-permute-start.52 = (bf16[256,2048]{1,0:T(8,128)(2,1)S(1)}, bf16[256,2048]{1,0:T(8,128)(2,1)S(1)}, u32[]{:S(2)}, u32[]{:S(2)}) collective-permute-start(bf16[256,2048]{1,0:T(8,128)(2,1)S(1)} %pad_maximum_fusion.3.refs_0_.refs_2_), channel_id=1, source_target_pairs={{0,4},{4,0},{8,12},{12,8},{16,20},{20,16},{24,28},{28,24},{1,5},{5... | collective-permute-start | bytes 3145736 | tf_op jit(solution)/shard_map/ppermute | solution.py:464
  356.5 35.9 %collective-permute-start.54 = (bf16[256,2048]{1,0:T(8,128)(2,1)}, bf16[256,2048]{1,0:T(8,128)(2,1)}, u32[]{:S(2)}, u32[]{:S(2)}) collective-permute-start(bf16[256,2048]{1,0:T(8,128)(2,1)} %pad_maximum_fusion.4.refs_1_.refs_3_), channel_id=1, source_target_pairs={{0,4},{4,0},{8,12},{12,8},{16,20},{20,16},{24,28},{28,24},{1,5},{5... | collective-permute-start | bytes 3145736 | tf_op jit(solution)/shard_map/ppermute | solution.py:464
  356.9 35.4 %collective-permute-start.49 = (bf16[128,2048]{1,0:T(8,128)(2,1)}, bf16[128,2048]{1,0:T(8,128)(2,1)}, u32[]{:S(2)}, u32[]{:S(2)}) collective-permute-start(bf16[128,2048]{1,0:T(8,128)(2,1)} %get-tuple-element.281), channel_id=1, source_target_pairs={{0,16},{4,20},{8,24},{12,28},{16,0},{20,4},{24,8},{28,12},{1,17},{... | collective-permute-start | bytes 1572872 | tf_op jit(solution)/shard_map/ppermute | solution.py:464
  360.7 31.6 %collective-permute-start.53 = (bf16[128,2048]{1,0:T(8,128)(2,1)}, bf16[128,2048]{1,0:T(8,128)(2,1)}, u32[]{:S(2)}, u32[]{:S(2)}) collective-permute-start(bf16[128,2048]{1,0:T(8,128)(2,1)} %add_convert_fusion.8), channel_id=1, source_target_pairs={{0,8},{4,12},{8,0},{12,4},{16,24},{20,28},{24,16},{28,20},{1,9},{5... | collective-permute-start | bytes 1572872 | tf_op jit(solution)/shard_map/ppermute | solution.py:464
  362.8 55.1 %collective-permute-start.56 = (bf16[128,2048]{1,0:T(8,128)(2,1)}, bf16[128,2048]{1,0:T(8,128)(2,1)S(1)}, u32[]{:S(2)}, u32[]{:S(2)}) collective-permute-start(bf16[128,2048]{1,0:T(8,128)(2,1)} %copy-done.87), channel_id=1, source_target_pairs={{0,16},{4,20},{8,24},{12,28},{16,0},{20,4},{24,8},{28,12},{1,17},{... | collective-permute-start | bytes 1572872 | tf_op jit(solution)/shard_map/ppermute | solution.py:464
  393.7 24.3 %collective-permute-start.57 = (bf16[128,2048]{1,0:T(8,128)(2,1)S(1)}, bf16[128,2048]{1,0:T(8,128)(2,1)S(1)}, u32[]{:S(2)}, u32[]{:S(2)}) collective-permute-start(bf16[128,2048]{1,0:T(8,128)(2,1)S(1)} %add_convert_fusion.7), channel_id=1, source_target_pairs={{0,8},{4,12},{8,0},{12,4},{16,24},{20,28},{24,16},{28,20},{1,9},{5... | collective-permute-start | bytes 1572872 | tf_op jit(solution)/shard_map/ppermute | solution.py:464
  395.2 22.7 %collective-permute-start.58 = (bf16[256,2048]{1,0:T(8,128)(2,1)S(1)}, bf16[256,2048]{1,0:T(8,128)(2,1)S(1)}, u32[]{:S(2)}, u32[]{:S(2)}) collective-permute-start(bf16[256,2048]{1,0:T(8,128)(2,1)S(1)} %pad_maximum_fusion.5.refs_1_.refs_3_), channel_id=1, source_target_pairs={{0,4},{4,0},{8,12},{12,8},{16,20},{20,16},{24,28},{28,24},{1,5},{5... | collective-permute-start | bytes 3145736 | tf_op jit(solution)/shard_map/ppermute | solution.py:464
  409.6 32.6 %collective-permute-start.55 = (bf16[512,512]{1,0:T(8,128)(2,1)}, bf16[512,512]{1,0:T(8,128)(2,1)}, u32[]{:S(2)}, u32[]{:S(2)}) collective-permute-start(bf16[512,512]{1,0:T(8,128)(2,1)} %get-tuple-element.294), channel_id=1, source_target_pairs={{0,16},{4,20},{8,24},{12,28},{16,0},{20,4},{24,8},{28,12},{1,17},{... | collective-permute-start | bytes 1572872 | tf_op jit(solution)/shard_map/ppermute | solution.py:464
  417.9 46.7 %collective-permute-start.61 = (bf16[512,512]{1,0:T(8,128)(2,1)}, bf16[512,512]{1,0:T(8,128)(2,1)}, u32[]{:S(2)}, u32[]{:S(2)}) collective-permute-start(bf16[512,512]{1,0:T(8,128)(2,1)} %get-tuple-element.309), channel_id=1, source_target_pairs={{0,16},{4,20},{8,24},{12,28},{16,0},{20,4},{24,8},{28,12},{1,17},{... | collective-permute-start | bytes 1572872 | tf_op jit(solution)/shard_map/ppermute | solution.py:464
  419.1 23.2 %collective-permute-start.59 = (bf16[128,2048]{1,0:T(8,128)(2,1)}, bf16[128,2048]{1,0:T(8,128)(2,1)}, u32[]{:S(2)}, u32[]{:S(2)}) collective-permute-start(bf16[128,2048]{1,0:T(8,128)(2,1)} %add_convert_fusion.6), channel_id=1, source_target_pairs={{0,8},{4,12},{8,0},{12,4},{16,24},{20,28},{24,16},{28,20},{1,9},{5... | collective-permute-start | bytes 1572872 | tf_op jit(solution)/shard_map/ppermute | solution.py:464
  423.9 18.4 %collective-permute-start.60 = (bf16[256,2048]{1,0:T(8,128)(2,1)}, bf16[256,2048]{1,0:T(8,128)(2,1)}, u32[]{:S(2)}, u32[]{:S(2)}) collective-permute-start(bf16[256,2048]{1,0:T(8,128)(2,1)} %pad_maximum_fusion.6.refs_1_.refs_3_), channel_id=1, source_target_pairs={{0,4},{4,0},{8,12},{12,8},{16,20},{20,16},{24,28},{28,24},{1,5},{5... | collective-permute-start | bytes 3145736 | tf_op jit(solution)/shard_map/ppermute | solution.py:464
  443.8 20.8 %collective-permute-start.62 = (bf16[512,512]{1,0:T(8,128)(2,1)S(1)}, bf16[512,512]{1,0:T(8,128)(2,1)S(1)}, u32[]{:S(2)}, u32[]{:S(2)}) collective-permute-start(bf16[512,512]{1,0:T(8,128)(2,1)S(1)} %add_convert_fusion.5), channel_id=1, source_target_pairs={{0,8},{4,12},{8,0},{12,4},{16,24},{20,28},{24,16},{28,20},{1,9},{5... | collective-permute-start | bytes 1572872 | tf_op jit(solution)/shard_map/ppermute | solution.py:464
  445.2 20.3 %collective-permute-start.63 = (bf16[256,2048]{1,0:T(8,128)(2,1)S(1)}, bf16[256,2048]{1,0:T(8,128)(2,1)S(1)}, u32[]{:S(2)}, u32[]{:S(2)}) collective-permute-start(bf16[256,2048]{1,0:T(8,128)(2,1)S(1)} %pad_maximum_fusion.7.refs_0_.refs_2_), channel_id=1, source_target_pairs={{0,4},{4,0},{8,12},{12,8},{16,20},{20,16},{24,28},{28,24},{1,5},{5... | collective-permute-start | bytes 3145736 | tf_op jit(solution)/shard_map/ppermute | solution.py:464
  458.4 26.2 %collective-permute-start.65 = (bf16[512,512]{1,0:T(8,128)(2,1)}, bf16[512,512]{1,0:T(8,128)(2,1)S(1)}, u32[]{:S(2)}, u32[]{:S(2)}) collective-permute-start(bf16[512,512]{1,0:T(8,128)(2,1)} %get-tuple-element.317), channel_id=1, source_target_pairs={{0,16},{4,20},{8,24},{12,28},{16,0},{20,4},{24,8},{28,12},{1,17},{... | collective-permute-start | bytes 1572872 | tf_op jit(solution)/shard_map/ppermute | solution.py:464
  466.8 20.0 %collective-permute-start.66 = (bf16[512,512]{1,0:T(8,128)(2,1)S(1)}, bf16[512,512]{1,0:T(8,128)(2,1)S(1)}, u32[]{:S(2)}, u32[]{:S(2)}) collective-permute-start(bf16[512,512]{1,0:T(8,128)(2,1)S(1)} %add_convert_fusion.4), channel_id=1, source_target_pairs={{0,8},{4,12},{8,0},{12,4},{16,24},{20,28},{24,16},{28,20},{1,9},{5... | collective-permute-start | bytes 1572872 | tf_op jit(solution)/shard_map/ppermute | solution.py:464
  468.7 20.9 %collective-permute-start.67 = (bf16[1024,512]{1,0:T(8,128)(2,1)S(1)}, bf16[1024,512]{1,0:T(8,128)(2,1)S(1)}, u32[]{:S(2)}, u32[]{:S(2)}) collective-permute-start(bf16[1024,512]{1,0:T(8,128)(2,1)S(1)} %pad_maximum_fusion.8.refs_0_.refs_2_), channel_id=1, source_target_pairs={{0,4},{4,0},{8,12},{12,8},{16,20},{20,16},{24,28},{28,24},{1,5},{5... | collective-permute-start | bytes 3145736 | tf_op jit(solution)/shard_map/ppermute | solution.py:464
  470.3 19.3 %collective-permute-start.68 = (bf16[2,256,2048]{2,1,0:T(8,128)(2,1)}, bf16[2,256,2048]{2,1,0:T(8,128)(2,1)}, u32[]{:S(2)}, u32[]{:S(2)}) collective-permute-start(bf16[2,256,2048]{2,1,0:T(8,128)(2,1)} %fusion.31), channel_id=1, source_target_pairs={{0,1},{1,0},{2,3},{3,2},{4,5},{5,4},{6,7},{7,6},{8,9},{9,8},{10,11... | collective-permute-start | bytes 6291464 | tf_op jit(solution)/shard_map/ppermute | solution.py:453
  489.7 27.0 %collective-permute-start.70 = (bf16[1024,512]{1,0:T(8,128)(2,1)S(1)}, bf16[1024,512]{1,0:T(8,128)(2,1)S(1)}, u32[]{:S(2)}, u32[]{:S(2)}) collective-permute-start(bf16[1024,512]{1,0:T(8,128)(2,1)S(1)} %pad_maximum_fusion.9.refs_1_.refs_3_), channel_id=1, source_target_pairs={{0,4},{4,0},{8,12},{12,8},{16,20},{20,16},{24,28},{28,24},{1,5},{5... | collective-permute-start | bytes 3145736 | tf_op jit(solution)/shard_map/ppermute | solution.py:464
  494.2 22.5 %collective-permute-start.71 = (bf16[256,2048]{1,0:T(8,128)(2,1)S(1)}, bf16[256,2048]{1,0:T(8,128)(2,1)S(1)}, u32[]{:S(2)}, u32[]{:S(2)}) collective-permute-start(bf16[256,2048]{1,0:T(8,128)(2,1)S(1)} %fusion.45), channel_id=1, source_target_pairs={{0,2},{1,3},{2,0},{3,1},{4,6},{5,7},{6,4},{7,5},{8,10},{9,11},{10,... | collective-permute-start | bytes 3145736 | tf_op jit(solution)/shard_map/ppermute | solution.py:461
  495.8 19.7 %collective-permute-start.64 = (bf16[512,512]{1,0:T(8,128)(2,1)S(1)}, bf16[512,512]{1,0:T(8,128)(2,1)S(1)}, u32[]{:S(2)}, u32[]{:S(2)}) collective-permute-start(bf16[512,512]{1,0:T(8,128)(2,1)S(1)} %copy-done.107), channel_id=1, source_target_pairs={{0,16},{4,20},{8,24},{12,28},{16,0},{20,4},{24,8},{28,12},{1,17},{... | collective-permute-start | bytes 1572872 | tf_op jit(solution)/shard_map/ppermute | solution.py:464
  499.6 17.1 %collective-permute-start.69 = (bf16[512,512]{1,0:T(8,128)(2,1)S(1)}, bf16[512,512]{1,0:T(8,128)(2,1)S(1)}, u32[]{:S(2)}, u32[]{:S(2)}) collective-permute-start(bf16[512,512]{1,0:T(8,128)(2,1)S(1)} %add_convert_fusion.3), channel_id=1, source_target_pairs={{0,8},{4,12},{8,0},{12,4},{16,24},{20,28},{24,16},{28,20},{1,9},{5... | collective-permute-start | bytes 1572872 | tf_op jit(solution)/shard_map/ppermute | solution.py:464
  516.8 22.6 %collective-permute-start.73 = (bf16[1024,512]{1,0:T(8,128)(2,1)S(1)}, bf16[1024,512]{1,0:T(8,128)(2,1)S(1)}, u32[]{:S(2)}, u32[]{:S(2)}) collective-permute-start(bf16[1024,512]{1,0:T(8,128)(2,1)S(1)} %pad_maximum_fusion.10.refs_1_.refs_3_), channel_id=1, source_target_pairs={{0,4},{4,0},{8,12},{12,8},{16,20},{20,16},{24,28},{28,24},{1,5},{5... | collective-permute-start | bytes 3145736 | tf_op jit(solution)/shard_map/ppermute | solution.py:464
  518.8 19.2 %collective-permute-start.72 = (bf16[512,512]{1,0:T(8,128)(2,1)S(1)}, bf16[512,512]{1,0:T(8,128)(2,1)S(1)}, u32[]{:S(2)}, u32[]{:S(2)}) collective-permute-start(bf16[512,512]{1,0:T(8,128)(2,1)S(1)} %add_convert_fusion.2), channel_id=1, source_target_pairs={{0,8},{4,12},{8,0},{12,4},{16,24},{20,28},{24,16},{28,20},{1,9},{5... | collective-permute-start | bytes 1572872 | tf_op jit(solution)/shard_map/ppermute | solution.py:464
  518.8 17.2 %collective-permute-start.75 = (bf16[512,384]{1,0:T(8,128)(2,1)S(1)}, bf16[512,384]{1,0:T(8,128)(2,1)S(1)}, u32[]{:S(2)}, u32[]{:S(2)}) collective-permute-start(bf16[512,384]{1,0:T(8,128)(2,1)S(1)} %get-tuple-element.335), channel_id=1, source_target_pairs={{0,16},{4,20},{8,24},{12,28},{16,0},{20,4},{24,8},{28,12},{1,17},{... | collective-permute-start | bytes 1179656 | tf_op jit(solution)/shard_map/ppermute | solution.py:464
  539.4 23.7 %collective-permute-start.77 = (bf16[1024,512]{1,0:T(8,128)(2,1)S(1)}, bf16[1024,512]{1,0:T(8,128)(2,1)S(1)}, u32[]{:S(2)}, u32[]{:S(2)}) collective-permute-start(bf16[1024,512]{1,0:T(8,128)(2,1)S(1)} %pad_maximum_fusion.11.refs_1_.refs_3_), channel_id=1, source_target_pairs={{0,4},{4,0},{8,12},{12,8},{16,20},{20,16},{24,28},{28,24},{1,5},{5... | collective-permute-start | bytes 3145736 | tf_op jit(solution)/shard_map/ppermute | solution.py:464
  542.1 15.5 %collective-permute-start.79 = (bf16[512,384]{1,0:T(8,128)(2,1)S(1)}, bf16[512,384]{1,0:T(8,128)(2,1)S(1)}, u32[]{:S(2)}, u32[]{:S(2)}) collective-permute-start(bf16[512,384]{1,0:T(8,128)(2,1)S(1)} %add_convert_fusion.13), channel_id=1, source_target_pairs={{0,8},{4,12},{8,0},{12,4},{16,24},{20,28},{24,16},{28,20},{1,9},{5... | collective-permute-start | bytes 1179656 | tf_op jit(solution)/shard_map/ppermute | solution.py:464
  563.2 16.7 %collective-permute-start.83 = (bf16[1024,384]{1,0:T(8,128)(2,1)S(1)}, bf16[1024,384]{1,0:T(8,128)(2,1)S(1)}, u32[]{:S(2)}, u32[]{:S(2)}) collective-permute-start(bf16[1024,384]{1,0:T(8,128)(2,1)S(1)} %pad_maximum_fusion.12.refs_0_.refs_2_), channel_id=1, source_target_pairs={{0,4},{4,0},{8,12},{12,8},{16,20},{20,16},{24,28},{28,24},{1,5},{5... | collective-permute-start | bytes 2359304 | tf_op jit(solution)/shard_map/ppermute | solution.py:464
  580.0 18.0 %collective-permute-start.86 = (bf16[1024,384]{1,0:T(8,128)(2,1)S(1)}, bf16[1024,384]{1,0:T(8,128)(2,1)S(1)}, u32[]{:S(2)}, u32[]{:S(2)}) collective-permute-start(bf16[1024,384]{1,0:T(8,128)(2,1)S(1)} %pad_maximum_fusion.13.refs_1_.refs_3_), channel_id=1, source_target_pairs={{0,4},{4,0},{8,12},{12,8},{16,20},{20,16},{24,28},{28,24},{1,5},{5... | collective-permute-start | bytes 2359304 | tf_op jit(solution)/shard_map/ppermute | solution.py:464
  598.0 17.7 %collective-permute-start.90 = (bf16[1024,384]{1,0:T(8,128)(2,1)S(1)}, bf16[1024,384]{1,0:T(8,128)(2,1)S(1)}, u32[]{:S(2)}, u32[]{:S(2)}) collective-permute-start(bf16[1024,384]{1,0:T(8,128)(2,1)S(1)} %pad_maximum_fusion.14.refs_1_.refs_3_), channel_id=1, source_target_pairs={{0,4},{4,0},{8,12},{12,8},{16,20},{20,16},{24,28},{28,24},{1,5},{5... | collective-permute-start | bytes 2359304 | tf_op jit(solution)/shard_map/ppermute | solution.py:464
  (162 other events, 1635.8 us)

commit v10 on v7

--- a/solution.py
+++ b/solution.py
@@ -227,6 +227,72 @@
     )(prefix, qkv, qkv, qkv, grad_context, log_total, spots[:, None], spots[None, :], table, table, table)
 
 
+def norm_back_kernel(
+    count, grad_qkv_ref, grad_inner_ref, qkv_ref, fc1_ref, gain_a_ref, gain_m_ref, *refs
+):
+    blocks, (o_ref, sums_ref, qkv_sum_ref, inner_sum_ref, rows_ref) = refs[:count], refs[count:]
+    step = pl.program_id(0)
+    for index, block in enumerate(blocks):
+
+        @pl.when(step == index)
+        def _(block=block):
+            rows_ref[...] = block[...]
+
+    features = rows_ref[...].astype(F32)
+    centered = features - jnp.mean(features, axis=-1, keepdims=True)
+    inverse = lax.rsqrt(jnp.mean(centered * centered, axis=-1, keepdims=True) + EPSILON)
+    xhat = centered * inverse
+    grad_attn = contract(grad_qkv_ref[...], qkv_ref[...], 1, 1)
+    grad_mlp = contract(grad_inner_ref[...], fc1_ref[...], 1, 1)
+    gained = grad_attn * gain_a_ref[...].astype(F32) + grad_mlp * gain_m_ref[...].astype(F32)
+    o_ref[...] = inverse * (
+        gained
+        - jnp.mean(gained, axis=-1, keepdims=True)
+        - xhat * jnp.mean(gained * xhat, axis=-1, keepdims=True)
+    )
+    pairs = (
+        (sums_ref, 0, grad_attn * xhat),
+        (sums_ref, 1, grad_attn),
+        (sums_ref, 2, grad_mlp * xhat),
+        (sums_ref, 3, grad_mlp),
+        (qkv_sum_ref, 0, grad_qkv_ref[...].astype(F32)),
+        (inner_sum_ref, 0, grad_inner_ref[...].astype(F32)),
+    )
+    for ref, row, values in pairs:
+        total = jnp.sum(values, axis=0, keepdims=True)
+
+        @pl.when(step == 0)
+        def _(ref=ref, row=row, total=total):
+            ref[row : row + 1, :] = total
+
+        @pl.when(step > 0)
+        def _(ref=ref, row=row, total=total):
+            ref[row : row + 1, :] += total
+
+
+def norm_back(grad_qkv, grad_inner, qkv_weight, fc1_weight, gains, blocks):
+    count = len(blocks)
+    rows, width = blocks[0].shape
+    each = lambda a: pl.BlockSpec((rows, a.shape[1]), lambda i: (i, 0))
+    full = lambda a: pl.BlockSpec(a.shape, lambda i: (0, 0), pipeline_mode=pl.Buffered(1))
+    sums = [(8, width), (8, grad_qkv.shape[1]), (8, grad_inner.shape[1])]
+    return pl.pallas_call(
+        functools.partial(norm_back_kernel, count),
+        grid=(count,),
+        in_specs=[each(grad_qkv), each(grad_inner), full(qkv_weight), full(fc1_weight)]
+        + [full(gains[0]), full(gains[2])]
+        + [full(b) for b in blocks],
+        out_specs=[pl.BlockSpec((rows, width), lambda i: (i, 0))]
+        + [pl.BlockSpec(shape, lambda i: (0, 0)) for shape in sums],
+        out_shape=[jax.ShapeDtypeStruct((count * rows, width), F32)]
+        + [jax.ShapeDtypeStruct(shape, F32) for shape in sums],
+        scratch_shapes=[pltpu.VMEM((rows, width), BF)],
+        compiler_params=pltpu.CompilerParams(vmem_limit_bytes=56 << 20),
+        cost_estimate=SMALL,
+        name="norm_back",
+    )(grad_qkv, grad_inner, qkv_weight, fc1_weight, gains[0], gains[2], *blocks)
+
+
 def place_kernel(quarter_ref, *refs):
     pieces, out_ref = refs[-5:-1], refs[-1]
     for index, piece in enumerate(pieces):
@@ -554,11 +620,7 @@
     )
     far_blocks = [block for pair in zip(ahead, mates) for block in pair]
     norms_far = both_norms(far_blocks, gains, 6 * ways)
-    last, norms_far = meet(last, norms_far)
-    last = [jnp.concatenate(pair, axis=0) for pair in last]
-    far_blocks = [block for v in last for block in (v, to_core(v))]
-    norm_attn_far, norm_mlp_far = both_norms(far_blocks, gains, 6 * ways, norms_far)
-    came, mates_own, counted, norm_mlp_far = meet(came, mates_own, counted, norm_mlp_far)
+    came, mates_own, counted, norms_far, last = meet(came, mates_own, counted, norms_far, last)
     count = count + counted
     mask = 8
     while mask < dp:
@@ -572,11 +634,14 @@
     error_part = jnp.sum(mask_f[:, None] * mismatch * mismatch)
     grad_out = mask_f[:, None] * mismatch * (2.0 * total_tokens / count[0, 0])
     grad_low = grad_out.astype(BF)
-    grad_out, grad_low, norm_mlp_far = meet(grad_out, grad_low, norm_mlp_far)
+    grad_out, grad_low, last = meet(grad_out, grad_low, last)
 
     grad_y = [from_y(grad_low, step) for step in range(1, ways)]
     grad_first = first_far(grad_low)
     grad_mate = to_core(grad_low)
+    last = [jnp.concatenate([after(v, grad_mate), u], axis=0) for v, u in last]
+    far_blocks = [block for v in last for block in (v, to_core(v))]
+    norm_attn_far, norm_mlp_far = both_norms(far_blocks, gains, 6 * ways, norms_far)
     fc1_quarter = quarter_of(fc1_weight, 1, quarter)
     fc2_quarter = quarter_of(after(fc2_weight, norm_mlp_far), 0, quarter)
     context_quarter = quarter_of(after(context, norm_mlp_far), 1, quarter)
@@ -608,11 +673,10 @@
     grad_qkv = attend_back(qkv_low, grad_context, log_total, prefix_len, spots, table)
     grad_qkv, grad_last, mates = meet(grad_qkv, grad_last, mates)
 
-    grad_last = [jnp.concatenate(pair, axis=0) for pair in grad_last]
-    ahead += grad_last
-    mates += [to_core(block) for block in grad_last]
+    last_mates = [tuple(to_core(v) for v in pair) for pair in grad_last]
+    swapped = [flip(quarter_of(grad_qkv, 1, quarter ^ m), m) for m in (1, 2)]
     grad_far = [block for pair in zip(ahead, mates) for block in pair]
-    bias_part = jnp.sum(grad_out, axis=0)
+    halves = [v for pair, mate in zip(grad_last, last_mates) for v in pair + mate]
 
     queue = []
     due = {}
@@ -638,9 +702,7 @@
         results.setdefault(name, []).append((near, far))
 
     def swap_walk(v, into):
-        got = yield [flipped(quarter_of(v, 1, quarter ^ m), m) for m in (1, 2)], 1
-        into.extend(got)
-        got = yield [flipped(quarter_of(v, 1, quarter ^ 3), 3)], 1
+        got = yield [flipped(quarter_of(v, 1, quarter ^ 3), 3)], 2
         into.extend(got)
 
     def last_walk(kept, mates, parts, others, into):
@@ -728,7 +790,7 @@
         return whole
 
     half = active_far.shape[1] // 2
-    rights = [grad_near] + grad_far
+    rights = [grad_near] + grad_far + halves
 
     def hidden_lefts(part):
         return [
@@ -747,11 +809,13 @@
     for index, piece in enumerate([context_quarter] + context_far):
         lefts.append((piece, kept_columns, 0, 0, half, index * LEN))
     *parts, out_part = outer_blocks(
-        lefts, [gate(grad_near)] + grad_far, [chunk] * 2 + [kept_columns], quarter
+        lefts, [gate(grad_near)] + rights[1:], [chunk] * 2 + [kept_columns], quarter
     )
     enqueue("fc2", *parts)
     enqueue("out", out_part)
-    turn()
+    swapped = turn(*swapped)
+    halves = lax.optimization_barrier((token[0], *halves))[1:]
+    grad_far += [jnp.concatenate(halves[i : i + 2], axis=0) for i in range(0, len(halves), 2)]
     grad_inner_far = back_blocks([gate(grad_far[0])] + grad_far[1:], fc2_quarter, slope_far)
     (grad_inner_far,) = turn(grad_inner_far)
     inner_quarter = gate(quarter_of(grad_inner, 1, quarter))
@@ -762,47 +826,27 @@
     )
     (fc1_part,) = turn(fc1_part.astype(BF))
     enqueue("fc1", *cut(fc1_part, [4, 4, 4, 4]))
-    grad_norm_attn = contract(gate(grad_qkv), qkv_weight, 1, 1)
-    (grad_norm_attn,) = turn(grad_norm_attn)
-    grad_norm_mlp = contract(gate(grad_inner), fc1_weight, 1, 1)
-    (grad_norm_mlp,) = turn(grad_norm_mlp)
-
-    near_blocks = lax.optimization_barrier((token[0], *near_blocks))[1:]
-    features = jnp.concatenate(near_blocks, axis=0).astype(F32)
-    centered = features - jnp.mean(features, axis=-1, keepdims=True)
-    inverse = lax.rsqrt(jnp.mean(centered * centered, axis=-1, keepdims=True) + EPSILON)
-    xhat = centered * inverse
-    gained = grad_norm_attn * gain_attn + grad_norm_mlp * gain_mlp
-    lift = jnp.mean(gained, axis=-1, keepdims=True)
-    pull = jnp.mean(gained * xhat, axis=-1, keepdims=True)
-    tensor_parts = jnp.stack(
-        [
-            jnp.sum(grad_norm_attn * xhat, axis=0),
-            jnp.sum(grad_norm_attn, axis=0),
-            jnp.sum(grad_norm_mlp * xhat, axis=0),
-            jnp.sum(grad_norm_mlp, axis=0),
-            bias_part,
-            jnp.full((D,), error_part, F32),
-        ]
-    ).reshape(-1)
-    tensor_parts, lift, pull = turn(tensor_parts, lift, pull)
-    grad_hidden = inverse * (gained - lift - xhat * pull)
+    grad_hidden, sums, qkv_sum, inner_sum = norm_back(
+        gate(grad_qkv), grad_inner, qkv_weight, fc1_weight, gains, near_blocks
+    )
+    grad_hidden, sums = turn(grad_hidden, sums)
     blocks = grad_hidden.reshape(ways, 2, rows, D)
-    fc1_bias_part = jnp.sum(gate(grad_inner), axis=0, dtype=F32)
-    qkv_bias_part = jnp.sum(gate(grad_qkv), axis=0, dtype=F32)
-    kept, mates, fc1_bias_part, qkv_bias_part = turn(
-        blocks[:, 0], blocks[:, 1].astype(BF), fc1_bias_part, qkv_bias_part
-    )
+    kept, mates = blocks[:, 0], blocks[:, 1].astype(BF)
+    bias_part = jnp.sum(gate(grad_out), axis=0)
+    tensor_parts = jnp.concatenate(
+        [sums[:4].reshape(-1), bias_part, jnp.full((D,), error_part, F32)]
+    )
+    fc1_bias_part, qkv_bias_part = inner_sum[0], qkv_sum[0]
+    others = jnp.concatenate([fc1_bias_part, qkv_bias_part])
     outcome = {}
-    others = jnp.concatenate([fc1_bias_part, qkv_bias_part])
-    walk(last_walk(kept, mates, tensor_parts, others, outcome))
     qkv_quarter = gate(quarter_of(grad_qkv, 1, quarter))
     qkv_part = (
         contract(norm_attn_own, qkv_quarter[:close], 0, 0)
         + contract(norm_attn_rest, qkv_quarter[close:], 0, 0)
-        + contract(norm_attn_far, jnp.concatenate(grad_qkv_far, axis=0), 0, 0)
-    )
-    (qkv_part,) = turn(qkv_part.astype(BF))
+        + contract(norm_attn_far, jnp.concatenate([*swapped, *grad_qkv_far], axis=0), 0, 0)
+    )
+    qkv_part, mates, tensor_parts = turn(qkv_part.astype(BF), mates, tensor_parts)
+    walk(last_walk(kept, mates, tensor_parts, others, outcome))
     enqueue("qkv", *cut(qkv_part, [4, 4, 4, 2, 1, 1]))
     axes = {"fc2": 0, "out": 0, "fc1": 1, "qkv": 1}
     placed = {name: (None, 0, 0) for name in axes}

time: 641 us -> 651 us (1.016)
  waiting for transfers between devices: 179 us -> 213 us
  other arithmetic: 56 us -> 24.3 us
  Pallas kernels: 138 us -> 168 us
  matrix products: 111 us -> 92.3 us
    pallas_call x0 -> x1, Pallas kernels: none -> 31.3 us  [norm_back(): pl.pallas_call(functools.partial(norm_back_kernel, count), grid=(count,),...]
    ppermute x69, waiting for transfers between devices: 175 us -> 197 us  [flip(): return lax.ppermute(v, 'dp', [(d, d ^ mask) for d in range(dp)])]
    dot_general x10 -> x8, matrix products: 64.9 us -> 45.8 us  [contract(): lax.dot_general(left_side, right_side, (((left_dim,), (right_dim,)), ((),...]
    reduce_sum x6 -> x1, other arithmetic: 18.2 us -> 1.71 us  [on_device(): bias_part = jnp.sum(gate(grad_out), axis=0)]
    ppermute x4, waiting for transfers between devices: 1.02 us -> 10.6 us  [from_y(): return lax.ppermute(v, 'tensor', pairs)]
    convert_element_type x15, other arithmetic: 12.3 us -> 3.74 us  [travel(): low = (low.astype(F32) + got.astype(F32)).astype(BF)]
    mul x1 -> x0, other arithmetic: 7.79 us -> none  [on_device(): grad_hidden = inverse * (gained - lift - xhat * pull)]
    unnamed x180 -> x173, local copies, waits for them, and re-layouts: 18.5 us -> 17.2 us
  transfers between devices with their start and end apart: 98 -> 99, of which waited for: 44 -> 38; matrix products, arithmetic and copies ran while one was open for 29% -> 21% of each run, Pallas kernels for 20% -> 26%
where the time goes in v10:
time: 651 us; the launch traced here: 641 us
  waiting for transfers between devices  213 us (33%)
  Pallas kernels  168 us (26%)
  matrix products  92.3 us (14%)
  starting transfers between devices  90.1 us (14%)
  local copies, waits for them, and re-layouts  46.4 us (7%)
  other arithmetic  24.3 us (4%)
  between operations  6.55 us (1%)
    ppermute x69, waiting for transfers between devices, flip(): return lax.ppermute(v, 'dp', [(d, d ^ mask) for d in range(dp)])  197 us
    ppermute x69, starting transfers between devices, flip(): return lax.ppermute(v, 'dp', [(d, d ^ mask) for d in range(dp)])  76.8 us
    dot_general x8, matrix products, contract(): lax.dot_general(left_side, right_side, (((left_dim,), (right_dim,)), ((),...  45.8 us
    pallas_call x15, Pallas kernels, place_quarters(): pl.pallas_call(place_kernel, grid_spec=pltpu.PrefetchScalarGridSpec(num_s...  34.7 us
    pallas_call x1, Pallas kernels, norm_back(): pl.pallas_call(functools.partial(norm_back_kernel, count), grid=(count,),...  31.3 us
    pallas_call x4, Pallas kernels, both_norms(): pl.pallas_call(functools.partial(norms_kernel, count), grid=(count,), in_...  29.1 us
    pallas_call x2, Pallas kernels, outer_blocks(): pl.pallas_call(functools.partial(outer_kernel, len(lefts), pieces, len(si...  23.1 us
    dot_general x2, matrix products, units(): jnp.dot(normed, fc1_weight, preferred_element_type=F32)  19.9 us
  transfers between devices with their start and end apart: 99, of which 38 were waited for; matrix products, arithmetic and copies ran while one was open for 21% of the time, Pallas kernels for 26%

profile of v10, /device:TPU:0, one launch (start us, length us, event | category | flops | bytes accessed | tf_op | source)
XLA Modules:
  0.0 641.2 jit_solution(2354831300710467436)
XLA Ops:
  1.2 2.6 collective-permute-start.3
  12.4 3.2 both_norms.4
  20.1 9.6 %multiply_convert_fusion.2 = (bf16[512,2048]{1,0:T(8,128)(2,1)}, f32[512,2048]{1,0:T(8,128)}) fusion(f32[2048]{0:T(1024)S(1)} %convert_element_type.230, bf16[512,2048]{1,0:T(8,128)(2,1)} %get-tuple-element.197, bf16[2048,2048]{1,0:T(8,128)(2,1)} %fc1_ref.1), kind=kOutput, calls=%fused_computation.20 | convolution fusion | flops 4301258752 | bytes 16785408 | tf_op jit(solution)/shard_map/dot_general | solution.py:538
  29.8 5.4 qkv_rotary.2.refs_0_
  42.8 4.6 both_norms.5
  47.4 2.6 copy-done.3
  51.5 2.8 copy-done.8
  54.2 5.4 qkv_rotary.3.q_ref.k_ref.v_ref
  59.7 9.6 %attend.1 = (bf16[1024,512]{1,0:T(8,128)(2,1)S(1)}, f32[2,1024,1]{2,1,0:T(8,128)S(1)}) custom-call(s32[1]{0:T(128)S(6)} %copy.83.prefix_ref, bf16[1024,1536]{1,0:T(8,128)(2,1)S(1)} %qkv_rotary.3.q_ref.k_ref.v_ref, bf16[1024,1536]{1,0:T(8,128)(2,1)S(1)} %qkv_rotary.3.q_ref.k_ref.v_ref, bf16[1024,1536]{1,0:T(8,128)(2,1)S(1)} %qkv_rotary.3.q_ref.k_ref.v_ref, ...), custom_call_target="tpu_custom_call" | custom-call | flops 1048576 | bytes 65536 | tf_op jit(solution)/shard_map/attend/pallas_call | solution.py:139
  71.0 2.6 collective-permute-start.13
  73.6 10.3 %multiply_convert_fusion.1 = (bf16[512,2048]{1,0:T(8,128)(2,1)S(1)}, f32[512,2048]{1,0:T(8,128)}) fusion(f32[2048]{0:T(1024)S(1)} %convert_element_type.230, bf16[512,2048]{1,0:T(8,128)(2,1)S(1)} %copy-done.46, bf16[2048,2048]{1,0:T(8,128)(2,1)} %fc1_ref.1), kind=kOutput, calls=%fused_computation.19 | convolution fusion | flops 4301258752 | bytes 16785408 | tf_op jit(solution)/shard_map/dot_general | solution.py:538
  83.9 10.6 %collective-permute-done.9.refs_6_ = bf16[256,2048]{1,0:T(8,128)(2,1)S(1)} collective-permute-done((bf16[256,2048]{1,0:T(8,128)(2,1)}, bf16[256,2048]{1,0:T(8,128)(2,1)S(1)}, u32[]{:S(2)}, u32[]{:S(2)}) %collective-permute-start.9) | collective-permute-done | bytes 1048608 | tf_op jit(solution)/shard_map/ppermute | solution.py:484
  94.6 4.5 fusion.54
  101.6 4.5 fusion.55
  116.7 2.6 collective-permute-start.23
  119.4 16.6 %both_norms.6 = (bf16[3072,2048]{1,0:T(8,128)(2,1)}, bf16[3072,2048]{1,0:T(8,128)(2,1)}) custom-call(bf16[1,2048]{1,0:T(2,128)(2,1)S(1)} %broadcast_in_dim.18.refs_0_.gain_a_ref, bf16[1,2048]{1,0:T(2,128)(2,1)S(1)} %broadcast_in_dim.38.refs_1_, bf16[1,2048]{1,0:T(2,128)(2,1)S(1)} %broadcast_in_dim.39.refs_2_.gain_m_ref, ...), custom_call_target="tpu_custom_call" | custom-call | flops 1048576 | bytes 65536 | tf_op jit(solution)/shard_map/both_norms/pallas_call | solution.py:353
  137.4 2.8 fusion.19
  142.4 2.8 collective-permute-done.29
  150.2 4.7 both_norms.7
  154.9 14.7 %fusion.9 = (f32[3072,512]{1,0:T(8,128)}, bf16[3072,512]{1,0:T(8,128)(2,1)}) fusion(f32[512]{0:T(512)S(1)} %dynamic-slice_convert_fusion, bf16[3072,2048]{1,0:T(8,128)(2,1)} %get-tuple-element.240, bf16[2048,2048]{1,0:T(8,128)(2,1)} %fc1_ref.1, s32[]{:T(128)S(6)} %select_n.81), kind=kOutput, calls=%fused_computation.12 | convolution fusion | flops 6459752448 | bytes 24119300 | tf_op jit(solution)/shard_map/dot_general | solution.py:648
  171.3 3.2 constant_dynamic-slice_fusion.6.weight_ref
  180.5 17.4 %fusion.5.grad_inner_ref = bf16[1024,2048]{1,0:T(8,128)(2,1)} fusion(f32[512,2048]{1,0:T(8,128)} %get-tuple-element.414, f32[512,2048]{1,0:T(8,128)} %get-tuple-element.412, bf16[1024,2048]{1,0:T(8,128)(2,1)S(1)} %constant_dynamic-update-slice_fusion.2.refs_3_.refs_7_, bf16[2048,2048]{1,0:T(8,128)(2,1)} %param.34), kind=kOutput, calls=%fused_computation.7 | convolution fusion | flops 8613003264 | bytes 25165824 | tf_op jit(solution)/shard_map/dot_general | solution.py:35
  204.4 12.0 %attend_back.1.grad_qkv_ref = bf16[1024,1536]{1,0:T(8,128)(2,1)} custom-call(s32[1]{0:T(128)S(6)} %copy.83.prefix_ref, bf16[1024,1536]{1,0:T(8,128)(2,1)} %copy-done.4, bf16[1024,1536]{1,0:T(8,128)(2,1)} %copy-done.4, bf16[1024,1536]{1,0:T(8,128)(2,1)} %copy-done.4, bf16[1024,512]{1,0:T(8,128)(2,1)S(1)} %convolution_convert_fusion.g_ref, ...), custom_call_target="tpu_custom_call" | custom-call | flops 1048576 | bytes 65536 | tf_op jit(solution)/shard_map/attend_back/pallas_call | solution.py:205
  218.7 3.3 constant_dynamic-slice_fusion
  224.8 10.6 %outer_blocks.2 = (bf16[128,2048]{1,0:T(8,128)(2,1)}, bf16[128,2048]{1,0:T(8,128)(2,1)}) custom-call(s32[1]{0:T(128)} %bitcast.9._.quarter_ref, bf16[512,2048]{1,0:T(8,128)(2,1)} %get-tuple-element.214.refs_0_, bf16[512,2048]{1,0:T(8,128)(2,1)} %copy-done.37, bf16[3072,512]{1,0:T(8,128)(2,1)} %get-tuple-element.243.refs_2_, bf16[1024,2048]{1,0:T(8,128)(2,1)} %copy-done.27, ...), custom_call_target="tpu_custom_call" | custom-call | flops 1048576 | bytes 65536 | tf_op jit(solution)/shard_map/outer_blocks/pallas_call | solution.py:403
  241.2 12.5 %outer_blocks.3 = (bf16[128,2048]{1,0:T(8,128)(2,1)}, bf16[128,2048]{1,0:T(8,128)(2,1)}, bf16[128,2048]{1,0:T(8,128)(2,1)}) custom-call(s32[1]{0:T(128)} %bitcast.9._.quarter_ref, bf16[512,2048]{1,0:T(8,128)(2,1)} %get-tuple-element.214.refs_0_, bf16[512,2048]{1,0:T(8,128)(2,1)} %copy-done.37, bf16[3072,512]{1,0:T(8,128)(2,1)} %get-tuple-element.243.refs_2_, ...), custom_call_target="tpu_custom_call" | custom-call | flops 1048576 | bytes 65536 | tf_op jit(solution)/shard_map/outer_blocks/pallas_call | solution.py:403
  253.8 8.9 %collective-permute-done.44 = bf16[128,2048]{1,0:T(8,128)(2,1)S(1)} collective-permute-done((bf16[128,2048]{1,0:T(8,128)(2,1)}, bf16[128,2048]{1,0:T(8,128)(2,1)S(1)}, u32[]{:S(2)}, u32[]{:S(2)}) %collective-permute-start.44) | collective-permute-done | bytes 524320 | tf_op jit(solution)/shard_map/ppermute | solution.py:491
  269.2 17.8 %back_blocks.1 = bf16[3072,512]{1,0:T(8,128)(2,1)} custom-call(bf16[512,2048]{1,0:T(8,128)(2,1)} %constant_dynamic-slice_fusion.6.weight_ref, f32[3072,512]{1,0:T(8,128)} %get-tuple-element.383.slope_ref, bf16[256,2048]{1,0:T(8,128)(2,1)} %copy-done.31, bf16[256,2048]{1,0:T(8,128)(2,1)} %copy-done.33, bf16[256,2048]{1,0:T(8,128)(2,1)} %copy-done.30, ...), custom_call_target="tpu_custom_call" | custom-call | flops 1048576 | bytes 65536 | tf_op jit(solution)/shard_map/back_blocks/pallas_call | solution.py:433
  287.0 14.6 %collective-permute-done.50 = bf16[128,2048]{1,0:T(8,128)(2,1)S(1)} collective-permute-done((bf16[128,2048]{1,0:T(8,128)(2,1)S(1)}, bf16[128,2048]{1,0:T(8,128)(2,1)S(1)}, u32[]{:S(2)}, u32[]{:S(2)}) %collective-permute-start.50) | collective-permute-done | bytes 524320 | tf_op jit(solution)/shard_map/ppermute | solution.py:491
  306.0 2.5 collective-permute-start.52
  308.5 9.8 %add_convert_fusion = bf16[2048,512]{1,0:T(8,128)(2,1)S(1)} fusion(f32[2048,512]{1,0:T(8,128)S(1)} %fusion.37, f32[2048,512]{1,0:T(8,128)S(1)} %fusion.35, bf16[3072,2048]{1,0:T(8,128)(2,1)} %get-tuple-element.240, bf16[3072,512]{1,0:T(8,128)(2,1)S(1)} %copy-done.49), kind=kOutput, calls=%fused_computation.18 | convolution fusion | flops 6445596672 | bytes 26214400 | tf_op jit(solution)/shard_map/dot_general | solution.py:35
  318.3 2.5 collective-permute-done.51
  320.8 9.8 %collective-permute-done.52.refs_1_.refs_3_ = bf16[256,2048]{1,0:T(8,128)(2,1)S(1)} collective-permute-done((bf16[256,2048]{1,0:T(8,128)(2,1)S(1)}, bf16[256,2048]{1,0:T(8,128)(2,1)S(1)}, u32[]{:S(2)}, u32[]{:S(2)}) %collective-permute-start.52) | collective-permute-done | bytes 1048608 | tf_op jit(solution)/shard_map/ppermute | solution.py:491
  336.7 31.3 %norm_back.1 = (f32[1024,2048]{1,0:T(8,128)}, f32[8,2048]{1,0:T(8,128)}, f32[8,1536]{1,0:T(8,128)}, f32[8,2048]{1,0:T(8,128)}) custom-call(bf16[1024,1536]{1,0:T(8,128)(2,1)} %attend_back.1.grad_qkv_ref, bf16[1024,2048]{1,0:T(8,128)(2,1)} %fusion.5.grad_inner_ref, bf16[2048,1536]{1,0:T(8,128)(2,1)} %qkv_ref.1, bf16[2048,2048]{1,0:T(8,128)(2,1)} %fc1_ref.1, ...), custom_call_target="tpu_custom_call" | custom-call | flops 1048576 | bytes 65536 | tf_op jit(solution)/shard_map/norm_back/pallas_call | solution.py:279
  376.9 11.1 %add_convert_fusion.1 = bf16[2048,384]{1,0:T(8,128)(2,1)} fusion(f32[2048,384]{1,0:T(8,128)S(1)} %fusion.43, f32[2048,384]{1,0:T(8,128)S(1)} %fusion.41, bf16[3072,2048]{1,0:T(8,128)(2,1)} %get-tuple-element.297, bf16[1024,384]{1,0:T(8,128)(2,1)S(1)} %copy-done.76, bf16[1024,384]{1,0:T(8,128)(2,1)} %collective-permute-done.46, ...), kind=kOutput, calls=%fused_computation.23 | convolution fusion | flops 4841275392 | bytes 22806528 | tf_op jit(solution)/shard_map/dot_general | solution.py:35
  390.5 2.5 fusion.20
  393.0 3.8 collective-permute-done.58.refs_2_.refs_4_
  398.8 2.6 collective-permute-start.59
  403.3 2.4 place_quarters.15.refs_0_
  405.7 19.3 %collective-permute-done.59 = bf16[512,512]{1,0:T(8,128)(2,1)S(1)} collective-permute-done((bf16[512,512]{1,0:T(8,128)(2,1)S(1)}, bf16[512,512]{1,0:T(8,128)(2,1)S(1)}, u32[]{:S(2)}, u32[]{:S(2)}) %collective-permute-start.59) | collective-permute-done | bytes 524320 | tf_op jit(solution)/shard_map/ppermute | solution.py:491
  427.8 2.5 collective-permute-start.67
  431.8 2.4 place_quarters.16.refs_0_
  434.3 20.1 %collective-permute-done.64 = bf16[512,512]{1,0:T(8,128)(2,1)S(1)} collective-permute-done((bf16[512,512]{1,0:T(8,128)(2,1)S(1)}, bf16[512,512]{1,0:T(8,128)(2,1)S(1)}, u32[]{:S(2)}, u32[]{:S(2)}) %collective-permute-start.64) | collective-permute-done | bytes 524320 | tf_op jit(solution)/shard_map/ppermute | solution.py:491
  458.3 2.5 place_quarters.18
  460.8 3.7 place_quarters.17.refs_0_
  464.5 15.3 %collective-permute-done.63 = bf16[512,512]{1,0:T(8,128)(2,1)S(1)} collective-permute-done((bf16[512,512]{1,0:T(8,128)(2,1)S(1)}, bf16[512,512]{1,0:T(8,128)(2,1)S(1)}, u32[]{:S(2)}, u32[]{:S(2)}) %collective-permute-start.63) | collective-permute-done | bytes 524320 | tf_op jit(solution)/shard_map/ppermute | solution.py:491
  485.7 2.4 place_quarters.20.refs_0_
  488.1 2.7 place_quarters.19
  490.8 15.0 %collective-permute-done.71 = bf16[512,512]{1,0:T(8,128)(2,1)S(1)} collective-permute-done((bf16[512,512]{1,0:T(8,128)(2,1)S(1)}, bf16[512,512]{1,0:T(8,128)(2,1)S(1)}, u32[]{:S(2)}, u32[]{:S(2)}) %collective-permute-start.71) | collective-permute-done | bytes 524320 | tf_op jit(solution)/shard_map/ppermute | solution.py:491
  508.4 2.5 collective-permute-start.75
  512.6 2.4 place_quarters.21.refs_0_
  515.1 12.3 %collective-permute-done.75 = bf16[512,384]{1,0:T(8,128)(2,1)S(1)} collective-permute-done((bf16[512,384]{1,0:T(8,128)(2,1)S(1)}, bf16[512,384]{1,0:T(8,128)(2,1)S(1)}, u32[]{:S(2)}, u32[]{:S(2)}) %collective-permute-start.75) | collective-permute-done | bytes 393248 | tf_op jit(solution)/shard_map/ppermute | solution.py:491
  527.4 5.1 collective-permute-done.78
  536.4 2.5 place_quarters.22.refs_0_
  538.9 13.0 %collective-permute-done.79 = bf16[512,384]{1,0:T(8,128)(2,1)S(1)} collective-permute-done((bf16[512,384]{1,0:T(8,128)(2,1)S(1)}, bf16[512,384]{1,0:T(8,128)(2,1)S(1)}, u32[]{:S(2)}, u32[]{:S(2)}) %collective-permute-start.79) | collective-permute-done | bytes 393248 | tf_op jit(solution)/shard_map/ppermute | solution.py:491
  553.9 2.6 collective-permute-done.81.refs_2_.refs_4_
  561.6 2.5 place_quarters.23
  564.1 11.7 %collective-permute-done.83 = bf16[512,384]{1,0:T(8,128)(2,1)S(1)} collective-permute-done((bf16[512,384]{1,0:T(8,128)(2,1)S(1)}, bf16[512,384]{1,0:T(8,128)(2,1)S(1)}, u32[]{:S(2)}, u32[]{:S(2)}) %collective-permute-start.83) | collective-permute-done | bytes 393248 | tf_op jit(solution)/shard_map/ppermute | solution.py:491
  578.6 3.2 collective-permute-start.87
  583.9 7.4 %collective-permute-done.87 = bf16[256,384]{1,0:T(8,128)(2,1)S(1)} collective-permute-done((bf16[256,384]{1,0:T(8,128)(2,1)S(1)}, bf16[256,384]{1,0:T(8,128)(2,1)S(1)}, u32[]{:S(2)}, u32[]{:S(2)}) %collective-permute-start.87) | collective-permute-done | bytes 196640 | tf_op jit(solution)/shard_map/ppermute | solution.py:491
  593.5 3.8 collective-permute-done.89.refs_2_.refs_4_
  598.1 3.0 collective-permute-start.91
  605.9 10.2 %collective-permute-done.93.refs_2_.refs_4_ = bf16[1024,384]{1,0:T(8,128)(2,1)S(1)} collective-permute-done((bf16[1024,384]{1,0:T(8,128)(2,1)S(1)}, bf16[1024,384]{1,0:T(8,128)(2,1)S(1)}, u32[]{:S(2)}, u32[]{:S(2)}) %collective-permute-start.93) | collective-permute-done | bytes 786464 | tf_op jit(solution)/shard_map/ppermute | solution.py:491
  616.7 2.8 collective-permute-start.94
  (449 shorter events, 162.9 us)
Async XLA Ops:
  1.2 35.7 %collective-permute-start.3 = (bf16[256,2048]{1,0:T(8,128)(2,1)}, bf16[256,2048]{1,0:T(8,128)(2,1)}, u32[]{:S(2)}, u32[]{:S(2)}) collective-permute-start(bf16[256,2048]{1,0:T(8,128)(2,1)} %refs_0_.1), channel_id=1, source_target_pairs={{0,4},{4,0},{8,12},{12,8},{16,20},{20,16},{24,28},{28,24},{1,5},{5... | collective-permute-start | bytes 3145736 | tf_op jit(solution)/shard_map/ppermute | solution.py:491
  3.8 33.1 %collective-permute-start.4 = (bf16[256,2048]{1,0:T(8,128)(2,1)}, bf16[256,2048]{1,0:T(8,128)(2,1)}, u32[]{:S(2)}, u32[]{:S(2)}) collective-permute-start(bf16[256,2048]{1,0:T(8,128)(2,1)} %refs_0_.1), channel_id=1, source_target_pairs={{0,8},{4,12},{8,0},{12,4},{16,24},{20,28},{24,16},{28,20},{1,9},{5... | collective-permute-start | bytes 3145736 | tf_op jit(solution)/shard_map/ppermute | solution.py:491
  5.3 31.5 %collective-permute-start.5 = (bf16[256,2048]{1,0:T(8,128)(2,1)}, bf16[256,2048]{1,0:T(8,128)(2,1)}, u32[]{:S(2)}, u32[]{:S(2)}) collective-permute-start(bf16[256,2048]{1,0:T(8,128)(2,1)} %refs_0_.1), channel_id=1, source_target_pairs={{0,2},{1,3},{2,0},{3,1},{4,6},{5,7},{6,4},{7,5},{8,10},{9,11},{10,... | collective-permute-start | bytes 3145736 | tf_op jit(solution)/shard_map/ppermute | solution.py:484
  37.2 33.0 %collective-permute-start.10 = (bf16[256,2048]{1,0:T(8,128)(2,1)}, bf16[256,2048]{1,0:T(8,128)(2,1)}, u32[]{:S(2)}, u32[]{:S(2)}) collective-permute-start(bf16[256,2048]{1,0:T(8,128)(2,1)} %collective-permute-done.5.refs_4_.refs_2_), channel_id=1, source_target_pairs={{0,8},{4,12},{8,0},{12,4},{16,24},{20,28},{24,16},{28,20},{1,9},{5... | collective-permute-start | bytes 3145736 | tf_op jit(solution)/shard_map/ppermute | solution.py:491
  37.6 33.2 %collective-permute-start.14 = (bf16[256,2048]{1,0:T(8,128)(2,1)}, bf16[256,2048]{1,0:T(8,128)(2,1)}, u32[]{:S(2)}, u32[]{:S(2)}) collective-permute-start(bf16[256,2048]{1,0:T(8,128)(2,1)} %collective-permute-done.3.refs_4_), channel_id=1, source_target_pairs={{0,1},{1,0},{2,3},{3,2},{4,5},{5,4},{6,7},{7,6},{8,9},{9,8},{10,11... | collective-permute-start | bytes 3145736 | tf_op jit(solution)/shard_map/ppermute | solution.py:480
  37.6 33.3 %collective-permute-start.15 = (bf16[256,2048]{1,0:T(8,128)(2,1)}, bf16[256,2048]{1,0:T(8,128)(2,1)}, u32[]{:S(2)}, u32[]{:S(2)}) collective-permute-start(bf16[256,2048]{1,0:T(8,128)(2,1)} %collective-permute-done.4.refs_8_), channel_id=1, source_target_pairs={{0,1},{1,0},{2,3},{3,2},{4,5},{5,4},{6,7},{7,6},{8,9},{9,8},{10,11... | collective-permute-start | bytes 3145736 | tf_op jit(solution)/shard_map/ppermute | solution.py:480
  39.0 44.9 %collective-permute-start.8 = (bf16[256,2048]{1,0:T(8,128)(2,1)}, bf16[256,2048]{1,0:T(8,128)(2,1)S(1)}, u32[]{:S(2)}, u32[]{:S(2)}) collective-permute-start(bf16[256,2048]{1,0:T(8,128)(2,1)} %collective-permute-done.4.refs_8_), channel_id=1, source_target_pairs={{0,4},{4,0},{8,12},{12,8},{16,20},{20,16},{24,28},{28,24},{1,5},{5... | collective-permute-start | bytes 3145736 | tf_op jit(solution)/shard_map/ppermute | solution.py:491
  41.2 28.4 %collective-permute-start.7 = (f32[8,128]{1,0:T(8,128)S(1)}, f32[8,128]{1,0:T(8,128)S(1)}, u32[]{:S(2)}, u32[]{:S(2)}) collective-permute-start(f32[8,128]{1,0:T(8,128)S(1)} %fusion.78), channel_id=1, source_target_pairs={{0,8},{4,12},{8,0},{12,4},{16,24},{20,28},{24,16},{28,20},{1,9},{5... | collective-permute-start | bytes 12296 | tf_op jit(solution)/shard_map/ppermute | solution.py:491
  69.5 24.9 %collective-permute-start.9 = (bf16[256,2048]{1,0:T(8,128)(2,1)}, bf16[256,2048]{1,0:T(8,128)(2,1)S(1)}, u32[]{:S(2)}, u32[]{:S(2)}) collective-permute-start(bf16[256,2048]{1,0:T(8,128)(2,1)} %collective-permute-done.3.refs_4_), channel_id=1, source_target_pairs={{0,2},{1,3},{2,0},{3,1},{4,6},{5,7},{6,4},{7,5},{8,10},{9,11},{10,... | collective-permute-start | bytes 3145736 | tf_op jit(solution)/shard_map/ppermute | solution.py:484
  70.1 24.4 %collective-permute-start.11 = (bf16[1024,128]{1,0:T(8,128)(2,1)S(1)}, bf16[1024,128]{1,0:T(8,128)(2,1)S(1)}, u32[]{:S(2)}, u32[]{:S(2)}) collective-permute-start(bf16[1024,128]{1,0:T(8,128)(2,1)S(1)} %get-tuple-element.404), channel_id=1, source_target_pairs={{0,4},{4,0},{8,12},{12,8},{16,20},{20,16},{24,28},{28,24},{1,5},{5... | collective-permute-start | bytes 786440 | tf_op jit(solution)/shard_map/ppermute | solution.py:491
  70.8 23.7 %collective-permute-start.12 = (bf16[1024,128]{1,0:T(8,128)(2,1)S(1)}, bf16[1024,128]{1,0:T(8,128)(2,1)S(1)}, u32[]{:S(2)}, u32[]{:S(2)}) collective-permute-start(bf16[1024,128]{1,0:T(8,128)(2,1)S(1)} %get-tuple-element.403), channel_id=1, source_target_pairs={{0,8},{4,12},{8,0},{12,4},{16,24},{20,28},{24,16},{28,20},{1,9},{5... | collective-permute-start | bytes 786440 | tf_op jit(solution)/shard_map/ppermute | solution.py:491
  71.0 23.5 %collective-permute-start.13 = (bf16[1024,128]{1,0:T(8,128)(2,1)S(1)}, bf16[1024,128]{1,0:T(8,128)(2,1)S(1)}, u32[]{:S(2)}, u32[]{:S(2)}) collective-permute-start(bf16[1024,128]{1,0:T(8,128)(2,1)S(1)} %get-tuple-element.402), channel_id=1, source_target_pairs={{0,12},{4,8},{8,4},{12,0},{16,28},{20,24},{24,20},{28,16},{1,13},{... | collective-permute-start | bytes 786440 | tf_op jit(solution)/shard_map/ppermute | solution.py:491
  111.3 24.7 %collective-permute-start.21 = (bf16[256,2048]{1,0:T(8,128)(2,1)}, bf16[256,2048]{1,0:T(8,128)(2,1)S(1)}, u32[]{:S(2)}, u32[]{:S(2)}) collective-permute-start(bf16[256,2048]{1,0:T(8,128)(2,1)} %fusion.32), channel_id=1, source_target_pairs={{0,2},{1,3},{2,0},{3,1},{4,6},{5,7},{6,4},{7,5},{8,10},{9,11},{10,... | collective-permute-start | bytes 3145736 | tf_op jit(solution)/shard_map/ppermute | solution.py:488
  113.0 23.1 %collective-permute-start.22 = (bf16[256,2048]{1,0:T(8,128)(2,1)}, bf16[256,2048]{1,0:T(8,128)(2,1)}, u32[]{:S(2)}, u32[]{:S(2)}) collective-permute-start(bf16[256,2048]{1,0:T(8,128)(2,1)} %fusion.33), channel_id=1, source_target_pairs={{0,1},{1,0},{2,3},{3,2},{4,5},{5,4},{6,7},{7,6},{8,9},{9,8},{10,11... | collective-permute-start | bytes 3145736 | tf_op jit(solution)/shard_map/ppermute | solution.py:480
  115.8 20.2 %collective-permute-start.24 = (bf16[128,2048]{1,0:T(8,128)(2,1)}, bf16[128,2048]{1,0:T(8,128)(2,1)S(1)}, u32[]{:S(2)}, u32[]{:S(2)}) collective-permute-start(bf16[128,2048]{1,0:T(8,128)(2,1)} %slice.145), channel_id=1, source_target_pairs={{0,4},{4,0},{8,12},{12,8},{16,20},{20,16},{24,28},{28,24},{1,5},{5... | collective-permute-start | bytes 1572872 | tf_op jit(solution)/shard_map/ppermute | solution.py:491
  116.3 19.7 %collective-permute-start.25 = (bf16[128,2048]{1,0:T(8,128)(2,1)}, bf16[128,2048]{1,0:T(8,128)(2,1)S(1)}, u32[]{:S(2)}, u32[]{:S(2)}) collective-permute-start(bf16[128,2048]{1,0:T(8,128)(2,1)} %slice.146), channel_id=1, source_target_pairs={{0,8},{4,12},{8,0},{12,4},{16,24},{20,28},{24,16},{28,20},{1,9},{5... | collective-permute-start | bytes 1572872 | tf_op jit(solution)/shard_map/ppermute | solution.py:491
  116.7 19.3 %collective-permute-start.23 = (f32[8,128]{1,0:T(8,128)S(1)}, f32[8,128]{1,0:T(8,128)S(1)}, u32[]{:S(2)}, u32[]{:S(2)}) collective-permute-start(f32[8,128]{1,0:T(8,128)S(1)} %add.303), channel_id=1, source_target_pairs={{0,16},{4,20},{8,24},{12,28},{16,0},{20,4},{24,8},{28,12},{1,17},{... | collective-permute-start | bytes 12296 | tf_op jit(solution)/shard_map/ppermute | solution.py:491
  145.6 28.9 %collective-permute-start.26 = (bf16[256,2048]{1,0:T(8,128)(2,1)}, bf16[256,2048]{1,0:T(8,128)(2,1)}, u32[]{:S(2)}, u32[]{:S(2)}) collective-permute-start(bf16[256,2048]{1,0:T(8,128)(2,1)} %copy-done.43), channel_id=1, source_target_pairs={{0,2},{1,3},{2,0},{3,1},{4,6},{5,7},{6,4},{7,5},{8,10},{9,11},{10,... | collective-permute-start | bytes 3145736 | tf_op jit(solution)/shard_map/ppermute | solution.py:484
  147.1 27.4 %collective-permute-start.27 = (bf16[256,2048]{1,0:T(8,128)(2,1)}, bf16[256,2048]{1,0:T(8,128)(2,1)S(1)}, u32[]{:S(2)}, u32[]{:S(2)}) collective-permute-start(bf16[256,2048]{1,0:T(8,128)(2,1)} %copy-done.43), channel_id=1, source_target_pairs={{0,4},{4,0},{8,12},{12,8},{16,20},{20,16},{24,28},{28,24},{1,5},{5... | collective-permute-start | bytes 3145736 | tf_op jit(solution)/shard_map/ppermute | solution.py:491
  148.6 25.9 %collective-permute-start.28 = (bf16[256,2048]{1,0:T(8,128)(2,1)}, bf16[256,2048]{1,0:T(8,128)(2,1)S(1)}, u32[]{:S(2)}, u32[]{:S(2)}) collective-permute-start(bf16[256,2048]{1,0:T(8,128)(2,1)} %copy-done.43), channel_id=1, source_target_pairs={{0,8},{4,12},{8,0},{12,4},{16,24},{20,28},{24,16},{28,20},{1,9},{5... | collective-permute-start | bytes 3145736 | tf_op jit(solution)/shard_map/ppermute | solution.py:491
  174.7 26.9 %collective-permute-start.34 = (bf16[256,2048]{1,0:T(8,128)(2,1)}, bf16[256,2048]{1,0:T(8,128)(2,1)S(1)}, u32[]{:S(2)}, u32[]{:S(2)}) collective-permute-start(bf16[256,2048]{1,0:T(8,128)(2,1)} %collective-permute-done.26), channel_id=1, source_target_pairs={{0,8},{4,12},{8,0},{12,4},{16,24},{20,28},{24,16},{28,20},{1,9},{5... | collective-permute-start | bytes 3145736 | tf_op jit(solution)/shard_map/ppermute | solution.py:491
  175.4 26.2 %collective-permute-start.33 = (bf16[256,2048]{1,0:T(8,128)(2,1)S(1)}, bf16[256,2048]{1,0:T(8,128)(2,1)S(1)}, u32[]{:S(2)}, u32[]{:S(2)}) collective-permute-start(bf16[256,2048]{1,0:T(8,128)(2,1)S(1)} %collective-permute-done.27.refs_4_.refs_8_.refs_0_), channel_id=1, source_target_pairs={{0,2},{1,3},{2,0},{3,1},{4,6},{5,7},{6,4},{7,5},{8,10},{9,11},{10,... | collective-permute-start | bytes 3145736 | tf_op jit(solution)/shard_map/ppermute | solution.py:484
  175.9 26.5 %collective-permute-start.37 = (bf16[256,2048]{1,0:T(8,128)(2,1)S(1)}, bf16[256,2048]{1,0:T(8,128)(2,1)S(1)}, u32[]{:S(2)}, u32[]{:S(2)}) collective-permute-start(bf16[256,2048]{1,0:T(8,128)(2,1)S(1)} %collective-permute-done.27.refs_4_.refs_8_.refs_0_), channel_id=1, source_target_pairs={{0,1},{1,0},{2,3},{3,2},{4,5},{5,4},{6,7},{7,6},{8,9},{9,8},{10,11... | collective-permute-start | bytes 3145736 | tf_op jit(solution)/shard_map/ppermute | solution.py:480
  175.9 25.7 %collective-permute-start.32 = (bf16[256,2048]{1,0:T(8,128)(2,1)S(1)}, bf16[256,2048]{1,0:T(8,128)(2,1)}, u32[]{:S(2)}, u32[]{:S(2)}) collective-permute-start(bf16[256,2048]{1,0:T(8,128)(2,1)S(1)} %collective-permute-done.28.refs_8_.refs_12_.refs_4_), channel_id=1, source_target_pairs={{0,4},{4,0},{8,12},{12,8},{16,20},{20,16},{24,28},{28,24},{1,5},{5... | collective-permute-start | bytes 3145736 | tf_op jit(solution)/shard_map/ppermute | solution.py:491
  180.1 23.9 %collective-permute-start.39 = (bf16[256,2048]{1,0:T(8,128)(2,1)S(1)}, bf16[256,2048]{1,0:T(8,128)(2,1)}, u32[]{:S(2)}, u32[]{:S(2)}) collective-permute-start(bf16[256,2048]{1,0:T(8,128)(2,1)S(1)} %collective-permute-done.28.refs_8_.refs_12_.refs_4_), channel_id=1, source_target_pairs={{0,1},{1,0},{2,3},{3,2},{4,5},{5,4},{6,7},{7,6},{8,9},{9,8},{10,11... | collective-permute-start | bytes 3145736 | tf_op jit(solution)/shard_map/ppermute | solution.py:480
  221.9 31.8 %collective-permute-start.45 = (bf16[1024,384]{1,0:T(8,128)(2,1)}, bf16[1024,384]{1,0:T(8,128)(2,1)}, u32[]{:S(2)}, u32[]{:S(2)}) collective-permute-start(bf16[1024,384]{1,0:T(8,128)(2,1)} %get-tuple-element.387), channel_id=1, source_target_pairs={{0,4},{4,0},{8,12},{12,8},{16,20},{20,16},{24,28},{28,24},{1,5},{5... | collective-permute-start | bytes 2359304 | tf_op jit(solution)/shard_map/ppermute | solution.py:491
  222.5 31.3 %collective-permute-start.46 = (bf16[1024,384]{1,0:T(8,128)(2,1)}, bf16[1024,384]{1,0:T(8,128)(2,1)}, u32[]{:S(2)}, u32[]{:S(2)}) collective-permute-start(bf16[1024,384]{1,0:T(8,128)(2,1)} %get-tuple-element.386), channel_id=1, source_target_pairs={{0,8},{4,12},{8,0},{12,4},{16,24},{20,28},{24,16},{28,20},{1,9},{5... | collective-permute-start | bytes 2359304 | tf_op jit(solution)/shard_map/ppermute | solution.py:491
  235.4 27.4 %collective-permute-start.44 = (bf16[128,2048]{1,0:T(8,128)(2,1)}, bf16[128,2048]{1,0:T(8,128)(2,1)S(1)}, u32[]{:S(2)}, u32[]{:S(2)}) collective-permute-start(bf16[128,2048]{1,0:T(8,128)(2,1)} %get-tuple-element.261), channel_id=1, source_target_pairs={{0,16},{4,20},{8,24},{12,28},{16,0},{20,4},{24,8},{28,12},{1,17},{... | collective-permute-start | bytes 1572872 | tf_op jit(solution)/shard_map/ppermute | solution.py:491
  237.2 49.7 %collective-permute-start.49 = (bf16[1024,384]{1,0:T(8,128)(2,1)S(1)}, bf16[1024,384]{1,0:T(8,128)(2,1)S(1)}, u32[]{:S(2)}, u32[]{:S(2)}) collective-permute-start(bf16[1024,384]{1,0:T(8,128)(2,1)S(1)} %constant_dynamic-slice_fusion.2), channel_id=1, source_target_pairs={{0,12},{4,8},{8,4},{12,0},{16,28},{20,24},{24,20},{28,16},{1,13},{... | collective-permute-start | bytes 2359304 | tf_op jit(solution)/shard_map/ppermute | solution.py:491
  239.1 47.8 %collective-permute-start.48 = (bf16[128,2048]{1,0:T(8,128)(2,1)}, bf16[128,2048]{1,0:T(8,128)(2,1)S(1)}, u32[]{:S(2)}, u32[]{:S(2)}) collective-permute-start(bf16[128,2048]{1,0:T(8,128)(2,1)} %get-tuple-element.270), channel_id=1, source_target_pairs={{0,16},{4,20},{8,24},{12,28},{16,0},{20,4},{24,8},{28,12},{1,17},{... | collective-permute-start | bytes 1572872 | tf_op jit(solution)/shard_map/ppermute | solution.py:491
  262.9 38.7 %collective-permute-start.50 = (bf16[128,2048]{1,0:T(8,128)(2,1)S(1)}, bf16[128,2048]{1,0:T(8,128)(2,1)S(1)}, u32[]{:S(2)}, u32[]{:S(2)}) collective-permute-start(bf16[128,2048]{1,0:T(8,128)(2,1)S(1)} %add_convert_fusion.10), channel_id=1, source_target_pairs={{0,8},{4,12},{8,0},{12,4},{16,24},{20,28},{24,16},{28,20},{1,9},{5... | collective-permute-start | bytes 1572872 | tf_op jit(solution)/shard_map/ppermute | solution.py:491
  264.2 54.0 %collective-permute-start.47 = (bf16[128,2048]{1,0:T(8,128)(2,1)}, bf16[128,2048]{1,0:T(8,128)(2,1)S(1)}, u32[]{:S(2)}, u32[]{:S(2)}) collective-permute-start(bf16[128,2048]{1,0:T(8,128)(2,1)} %get-tuple-element.269), channel_id=1, source_target_pairs={{0,16},{4,20},{8,24},{12,28},{16,0},{20,4},{24,8},{28,12},{1,17},{... | collective-permute-start | bytes 1572872 | tf_op jit(solution)/shard_map/ppermute | solution.py:491
  306.0 24.6 %collective-permute-start.52 = (bf16[256,2048]{1,0:T(8,128)(2,1)S(1)}, bf16[256,2048]{1,0:T(8,128)(2,1)S(1)}, u32[]{:S(2)}, u32[]{:S(2)}) collective-permute-start(bf16[256,2048]{1,0:T(8,128)(2,1)S(1)} %pad_maximum_fusion.4.refs_0_.refs_2_), channel_id=1, source_target_pairs={{0,4},{4,0},{8,12},{12,8},{16,20},{20,16},{24,28},{28,24},{1,5},{5... | collective-permute-start | bytes 3145736 | tf_op jit(solution)/shard_map/ppermute | solution.py:491
  331.6 37.7 %collective-permute-start.56 = (bf16[256,2048]{1,0:T(8,128)(2,1)S(1)}, bf16[256,2048]{1,0:T(8,128)(2,1)S(1)}, u32[]{:S(2)}, u32[]{:S(2)}) collective-permute-start(bf16[256,2048]{1,0:T(8,128)(2,1)S(1)} %pad_maximum_fusion.5.refs_1_.refs_3_), channel_id=1, source_target_pairs={{0,4},{4,0},{8,12},{12,8},{16,20},{20,16},{24,28},{28,24},{1,5},{5... | collective-permute-start | bytes 3145736 | tf_op jit(solution)/shard_map/ppermute | solution.py:491
  333.5 35.9 %collective-permute-start.54 = (bf16[128,2048]{1,0:T(8,128)(2,1)S(1)}, bf16[128,2048]{1,0:T(8,128)(2,1)S(1)}, u32[]{:S(2)}, u32[]{:S(2)}) collective-permute-start(bf16[128,2048]{1,0:T(8,128)(2,1)S(1)} %copy-done.58), channel_id=1, source_target_pairs={{0,16},{4,20},{8,24},{12,28},{16,0},{20,4},{24,8},{28,12},{1,17},{... | collective-permute-start | bytes 1572872 | tf_op jit(solution)/shard_map/ppermute | solution.py:491
  333.6 35.8 %collective-permute-start.55 = (bf16[128,2048]{1,0:T(8,128)(2,1)S(1)}, bf16[128,2048]{1,0:T(8,128)(2,1)S(1)}, u32[]{:S(2)}, u32[]{:S(2)}) collective-permute-start(bf16[128,2048]{1,0:T(8,128)(2,1)S(1)} %add_convert_fusion.8), channel_id=1, source_target_pairs={{0,8},{4,12},{8,0},{12,4},{16,24},{20,28},{24,16},{28,20},{1,9},{5... | collective-permute-start | bytes 1572872 | tf_op jit(solution)/shard_map/ppermute | solution.py:491
  335.4 57.6 %collective-permute-start.53 = (bf16[128,2048]{1,0:T(8,128)(2,1)}, bf16[128,2048]{1,0:T(8,128)(2,1)}, u32[]{:S(2)}, u32[]{:S(2)}) collective-permute-start(bf16[128,2048]{1,0:T(8,128)(2,1)} %get-tuple-element.286), channel_id=1, source_target_pairs={{0,16},{4,20},{8,24},{12,28},{16,0},{20,4},{24,8},{28,12},{1,17},{... | collective-permute-start | bytes 1572872 | tf_op jit(solution)/shard_map/ppermute | solution.py:491
  374.6 22.3 %collective-permute-start.58 = (bf16[256,2048]{1,0:T(8,128)(2,1)S(1)}, bf16[256,2048]{1,0:T(8,128)(2,1)}, u32[]{:S(2)}, u32[]{:S(2)}) collective-permute-start(bf16[256,2048]{1,0:T(8,128)(2,1)S(1)} %pad_maximum_fusion.6.refs_1_.refs_3_), channel_id=1, source_target_pairs={{0,4},{4,0},{8,12},{12,8},{16,20},{20,16},{24,28},{28,24},{1,5},{5... | collective-permute-start | bytes 3145736 | tf_op jit(solution)/shard_map/ppermute | solution.py:491
  396.8 29.9 %collective-permute-start.62 = (bf16[2,256,2048]{2,1,0:T(8,128)(2,1)S(1)}, bf16[2,256,2048]{2,1,0:T(8,128)(2,1)S(1)}, u32[]{:S(2)}, u32[]{:S(2)}) collective-permute-start(bf16[2,256,2048]{2,1,0:T(8,128)(2,1)S(1)} %fusion.20), channel_id=1, source_target_pairs={{0,1},{1,0},{2,3},{3,2},{4,5},{5,4},{6,7},{7,6},{8,9},{9,8},{10,11... | collective-permute-start | bytes 6291464 | tf_op jit(solution)/shard_map/ppermute | solution.py:480
  398.1 28.6 %collective-permute-start.61 = (bf16[256,2048]{1,0:T(8,128)(2,1)S(1)}, bf16[256,2048]{1,0:T(8,128)(2,1)S(1)}, u32[]{:S(2)}, u32[]{:S(2)}) collective-permute-start(bf16[256,2048]{1,0:T(8,128)(2,1)S(1)} %pad_maximum_fusion.7.refs_1_.refs_3_), channel_id=1, source_target_pairs={{0,4},{4,0},{8,12},{12,8},{16,20},{20,16},{24,28},{28,24},{1,5},{5... | collective-permute-start | bytes 3145736 | tf_op jit(solution)/shard_map/ppermute | solution.py:491
  398.8 26.3 %collective-permute-start.59 = (bf16[512,512]{1,0:T(8,128)(2,1)S(1)}, bf16[512,512]{1,0:T(8,128)(2,1)S(1)}, u32[]{:S(2)}, u32[]{:S(2)}) collective-permute-start(bf16[512,512]{1,0:T(8,128)(2,1)S(1)} %copy-done.53), channel_id=1, source_target_pairs={{0,16},{4,20},{8,24},{12,28},{16,0},{20,4},{24,8},{28,12},{1,17},{... | collective-permute-start | bytes 1572872 | tf_op jit(solution)/shard_map/ppermute | solution.py:491
  402.9 23.9 %collective-permute-start.60 = (bf16[128,2048]{1,0:T(8,128)(2,1)S(1)}, bf16[128,2048]{1,0:T(8,128)(2,1)S(1)}, u32[]{:S(2)}, u32[]{:S(2)}) collective-permute-start(bf16[128,2048]{1,0:T(8,128)(2,1)S(1)} %add_convert_fusion.6), channel_id=1, source_target_pairs={{0,8},{4,12},{8,0},{12,4},{16,24},{20,28},{24,16},{28,20},{1,9},{5... | collective-permute-start | bytes 1572872 | tf_op jit(solution)/shard_map/ppermute | solution.py:491
  427.8 26.9 %collective-permute-start.67 = (bf16[256,2048]{1,0:T(8,128)(2,1)S(1)}, bf16[256,2048]{1,0:T(8,128)(2,1)S(1)}, u32[]{:S(2)}, u32[]{:S(2)}) collective-permute-start(bf16[256,2048]{1,0:T(8,128)(2,1)S(1)} %fusion.34), channel_id=1, source_target_pairs={{0,2},{1,3},{2,0},{3,1},{4,6},{5,7},{6,4},{7,5},{8,10},{9,11},{10,... | collective-permute-start | bytes 3145736 | tf_op jit(solution)/shard_map/ppermute | solution.py:488
  430.4 24.3 %collective-permute-start.66 = (bf16[256,2048]{1,0:T(8,128)(2,1)S(1)}, bf16[256,2048]{1,0:T(8,128)(2,1)S(1)}, u32[]{:S(2)}, u32[]{:S(2)}) collective-permute-start(bf16[256,2048]{1,0:T(8,128)(2,1)S(1)} %pad_maximum_fusion.8.refs_0_.refs_2_), channel_id=1, source_target_pairs={{0,4},{4,0},{8,12},{12,8},{16,20},{20,16},{24,28},{28,24},{1,5},{5... | collective-permute-start | bytes 3145736 | tf_op jit(solution)/shard_map/ppermute | solution.py:491
  430.5 23.9 %collective-permute-start.64 = (bf16[512,512]{1,0:T(8,128)(2,1)S(1)}, bf16[512,512]{1,0:T(8,128)(2,1)S(1)}, u32[]{:S(2)}, u32[]{:S(2)}) collective-permute-start(bf16[512,512]{1,0:T(8,128)(2,1)S(1)} %copy-done.52), channel_id=1, source_target_pairs={{0,16},{4,20},{8,24},{12,28},{16,0},{20,4},{24,8},{28,12},{1,17},{... | collective-permute-start | bytes 1572872 | tf_op jit(solution)/shard_map/ppermute | solution.py:491
  430.7 23.9 %collective-permute-start.65 = (bf16[512,512]{1,0:T(8,128)(2,1)S(1)}, bf16[512,512]{1,0:T(8,128)(2,1)S(1)}, u32[]{:S(2)}, u32[]{:S(2)}) collective-permute-start(bf16[512,512]{1,0:T(8,128)(2,1)S(1)} %add_convert_fusion.5), channel_id=1, source_target_pairs={{0,8},{4,12},{8,0},{12,4},{16,24},{20,28},{24,16},{28,20},{1,9},{5... | collective-permute-start | bytes 1572872 | tf_op jit(solution)/shard_map/ppermute | solution.py:491
  454.8 26.4 %collective-permute-start.69 = (bf16[1024,512]{1,0:T(8,128)(2,1)S(1)}, bf16[1024,512]{1,0:T(8,128)(2,1)S(1)}, u32[]{:S(2)}, u32[]{:S(2)}) collective-permute-start(bf16[1024,512]{1,0:T(8,128)(2,1)S(1)} %pad_maximum_fusion.9.refs_0_.refs_2_), channel_id=1, source_target_pairs={{0,4},{4,0},{8,12},{12,8},{16,20},{20,16},{24,28},{28,24},{1,5},{5... | collective-permute-start | bytes 3145736 | tf_op jit(solution)/shard_map/ppermute | solution.py:491
  456.5 23.3 %collective-permute-start.63 = (bf16[512,512]{1,0:T(8,128)(2,1)S(1)}, bf16[512,512]{1,0:T(8,128)(2,1)S(1)}, u32[]{:S(2)}, u32[]{:S(2)}) collective-permute-start(bf16[512,512]{1,0:T(8,128)(2,1)S(1)} %copy-done.51), channel_id=1, source_target_pairs={{0,16},{4,20},{8,24},{12,28},{16,0},{20,4},{24,8},{28,12},{1,17},{... | collective-permute-start | bytes 1572872 | tf_op jit(solution)/shard_map/ppermute | solution.py:491
  456.9 24.3 %collective-permute-start.68 = (bf16[512,512]{1,0:T(8,128)(2,1)S(1)}, bf16[512,512]{1,0:T(8,128)(2,1)S(1)}, u32[]{:S(2)}, u32[]{:S(2)}) collective-permute-start(bf16[512,512]{1,0:T(8,128)(2,1)S(1)} %add_convert_fusion.4), channel_id=1, source_target_pairs={{0,8},{4,12},{8,0},{12,4},{16,24},{20,28},{24,16},{28,20},{1,9},{5... | collective-permute-start | bytes 1572872 | tf_op jit(solution)/shard_map/ppermute | solution.py:491
  481.3 24.9 %collective-permute-start.73 = (bf16[1024,512]{1,0:T(8,128)(2,1)S(1)}, bf16[1024,512]{1,0:T(8,128)(2,1)S(1)}, u32[]{:S(2)}, u32[]{:S(2)}) collective-permute-start(bf16[1024,512]{1,0:T(8,128)(2,1)S(1)} %pad_maximum_fusion.10.refs_1_.refs_3_), channel_id=1, source_target_pairs={{0,4},{4,0},{8,12},{12,8},{16,20},{20,16},{24,28},{28,24},{1,5},{5... | collective-permute-start | bytes 3145736 | tf_op jit(solution)/shard_map/ppermute | solution.py:491
  481.7 24.1 %collective-permute-start.71 = (bf16[512,512]{1,0:T(8,128)(2,1)S(1)}, bf16[512,512]{1,0:T(8,128)(2,1)S(1)}, u32[]{:S(2)}, u32[]{:S(2)}) collective-permute-start(bf16[512,512]{1,0:T(8,128)(2,1)S(1)} %copy-done.50), channel_id=1, source_target_pairs={{0,16},{4,20},{8,24},{12,28},{16,0},{20,4},{24,8},{28,12},{1,17},{... | collective-permute-start | bytes 1572872 | tf_op jit(solution)/shard_map/ppermute | solution.py:491
  481.9 24.4 %collective-permute-start.72 = (bf16[512,512]{1,0:T(8,128)(2,1)S(1)}, bf16[512,512]{1,0:T(8,128)(2,1)S(1)}, u32[]{:S(2)}, u32[]{:S(2)}) collective-permute-start(bf16[512,512]{1,0:T(8,128)(2,1)S(1)} %add_convert_fusion.3), channel_id=1, source_target_pairs={{0,8},{4,12},{8,0},{12,4},{16,24},{20,28},{24,16},{28,20},{1,9},{5... | collective-permute-start | bytes 1572872 | tf_op jit(solution)/shard_map/ppermute | solution.py:491
  484.3 21.5 %collective-permute-start.74 = (f32[12288]{0:T(1024)S(1)}, f32[12288]{0:T(1024)S(1)}, u32[]{:S(2)}, u32[]{:S(2)}) collective-permute-start(f32[12288]{0:T(1024)S(1)} %add.336), channel_id=1, source_target_pairs={{0,2},{1,3},{2,0},{3,1},{4,6},{5,7},{6,4},{7,5},{8,10},{9,11},{10,... | collective-permute-start | bytes 147464 | tf_op jit(solution)/shard_map/ppermute | solution.py:719
  506.3 26.1 %collective-permute-start.77 = (bf16[1024,512]{1,0:T(8,128)(2,1)S(1)}, bf16[1024,512]{1,0:T(8,128)(2,1)S(1)}, u32[]{:S(2)}, u32[]{:S(2)}) collective-permute-start(bf16[1024,512]{1,0:T(8,128)(2,1)S(1)} %pad_maximum_fusion.11.refs_1_.refs_3_), channel_id=1, source_target_pairs={{0,4},{4,0},{8,12},{12,8},{16,20},{20,16},{24,28},{28,24},{1,5},{5... | collective-permute-start | bytes 3145736 | tf_op jit(solution)/shard_map/ppermute | solution.py:491
  507.5 24.9 %collective-permute-start.76 = (bf16[512,512]{1,0:T(8,128)(2,1)S(1)}, bf16[512,512]{1,0:T(8,128)(2,1)S(1)}, u32[]{:S(2)}, u32[]{:S(2)}) collective-permute-start(bf16[512,512]{1,0:T(8,128)(2,1)S(1)} %add_convert_fusion.2), channel_id=1, source_target_pairs={{0,8},{4,12},{8,0},{12,4},{16,24},{20,28},{24,16},{28,20},{1,9},{5... | collective-permute-start | bytes 1572872 | tf_op jit(solution)/shard_map/ppermute | solution.py:491
  508.4 18.9 %collective-permute-start.75 = (bf16[512,384]{1,0:T(8,128)(2,1)S(1)}, bf16[512,384]{1,0:T(8,128)(2,1)S(1)}, u32[]{:S(2)}, u32[]{:S(2)}) collective-permute-start(bf16[512,384]{1,0:T(8,128)(2,1)S(1)} %get-tuple-element.334), channel_id=1, source_target_pairs={{0,16},{4,20},{8,24},{12,28},{16,0},{20,4},{24,8},{28,12},{1,17},{... | collective-permute-start | bytes 1179656 | tf_op jit(solution)/shard_map/ppermute | solution.py:491
  511.7 20.7 %collective-permute-start.78 = (f32[15872]{0:T(1024)S(1)}, f32[15872]{0:T(1024)S(1)}, u32[]{:S(2)}, u32[]{:S(2)}) collective-permute-start(f32[15872]{0:T(1024)S(1)} %pad_maximum_fusion.19), channel_id=1, source_target_pairs={{0,4},{4,0},{8,12},{12,8},{16,20},{20,16},{24,28},{28,24},{1,5},{5... | collective-permute-start | bytes 190472 | tf_op jit(solution)/shard_map/ppermute | solution.py:491
  532.5 24.0 %collective-permute-start.81 = (bf16[1024,512]{1,0:T(8,128)(2,1)S(1)}, bf16[1024,512]{1,0:T(8,128)(2,1)S(1)}, u32[]{:S(2)}, u32[]{:S(2)}) collective-permute-start(bf16[1024,512]{1,0:T(8,128)(2,1)S(1)} %pad_maximum_fusion.12.refs_1_.refs_3_), channel_id=1, source_target_pairs={{0,4},{4,0},{8,12},{12,8},{16,20},{20,16},{24,28},{28,24},{1,5},{5... | collective-permute-start | bytes 3145736 | tf_op jit(solution)/shard_map/ppermute | solution.py:491
  534.0 17.9 %collective-permute-start.79 = (bf16[512,384]{1,0:T(8,128)(2,1)S(1)}, bf16[512,384]{1,0:T(8,128)(2,1)S(1)}, u32[]{:S(2)}, u32[]{:S(2)}) collective-permute-start(bf16[512,384]{1,0:T(8,128)(2,1)S(1)} %get-tuple-element.340), channel_id=1, source_target_pairs={{0,16},{4,20},{8,24},{12,28},{16,0},{20,4},{24,8},{28,12},{1,17},{... | collective-permute-start | bytes 1179656 | tf_op jit(solution)/shard_map/ppermute | solution.py:491
  534.1 19.8 %collective-permute-start.80 = (bf16[512,384]{1,0:T(8,128)(2,1)S(1)}, bf16[512,384]{1,0:T(8,128)(2,1)S(1)}, u32[]{:S(2)}, u32[]{:S(2)}) collective-permute-start(bf16[512,384]{1,0:T(8,128)(2,1)S(1)} %add_convert_fusion.13), channel_id=1, source_target_pairs={{0,8},{4,12},{8,0},{12,4},{16,24},{20,28},{24,16},{28,20},{1,9},{5... | collective-permute-start | bytes 1179656 | tf_op jit(solution)/shard_map/ppermute | solution.py:491
  556.6 21.1 %collective-permute-start.85 = (bf16[1024,384]{1,0:T(8,128)(2,1)S(1)}, bf16[1024,384]{1,0:T(8,128)(2,1)S(1)}, u32[]{:S(2)}, u32[]{:S(2)}) collective-permute-start(bf16[1024,384]{1,0:T(8,128)(2,1)S(1)} %pad_maximum_fusion.13.refs_0_.refs_2_), channel_id=1, source_target_pairs={{0,4},{4,0},{8,12},{12,8},{16,20},{20,16},{24,28},{28,24},{1,5},{5... | collective-permute-start | bytes 2359304 | tf_op jit(solution)/shard_map/ppermute | solution.py:491
  558.5 19.2 %collective-permute-start.84 = (bf16[512,384]{1,0:T(8,128)(2,1)S(1)}, bf16[512,384]{1,0:T(8,128)(2,1)S(1)}, u32[]{:S(2)}, u32[]{:S(2)}) collective-permute-start(bf16[512,384]{1,0:T(8,128)(2,1)S(1)} %add_convert_fusion.12), channel_id=1, source_target_pairs={{0,8},{4,12},{8,0},{12,4},{16,24},{20,28},{24,16},{28,20},{1,9},{5... | collective-permute-start | bytes 1179656 | tf_op jit(solution)/shard_map/ppermute | solution.py:491
  577.8 19.5 %collective-permute-start.89 = (bf16[1024,384]{1,0:T(8,128)(2,1)S(1)}, bf16[1024,384]{1,0:T(8,128)(2,1)S(1)}, u32[]{:S(2)}, u32[]{:S(2)}) collective-permute-start(bf16[1024,384]{1,0:T(8,128)(2,1)S(1)} %pad_maximum_fusion.14.refs_1_.refs_3_), channel_id=1, source_target_pairs={{0,4},{4,0},{8,12},{12,8},{16,20},{20,16},{24,28},{28,24},{1,5},{5... | collective-permute-start | bytes 2359304 | tf_op jit(solution)/shard_map/ppermute | solution.py:491
  597.4 18.7 %collective-permute-start.93 = (bf16[1024,384]{1,0:T(8,128)(2,1)S(1)}, bf16[1024,384]{1,0:T(8,128)(2,1)S(1)}, u32[]{:S(2)}, u32[]{:S(2)}) collective-permute-start(bf16[1024,384]{1,0:T(8,128)(2,1)S(1)} %pad_maximum_fusion.15.refs_1_.refs_3_), channel_id=1, source_target_pairs={{0,4},{4,0},{8,12},{12,8},{16,20},{20,16},{24,28},{28,24},{1,5},{5... | collective-permute-start | bytes 2359304 | tf_op jit(solution)/shard_map/ppermute | solution.py:491
  (118 other events, 1606.0 us)

commit v11 on v10

--- a/solution.py
+++ b/solution.py
@@ -293,39 +293,68 @@
     )(grad_qkv, grad_inner, qkv_weight, fc1_weight, gains[0], gains[2], *blocks)
 
 
-def place_kernel(quarter_ref, *refs):
-    pieces, out_ref = refs[-5:-1], refs[-1]
-    for index, piece in enumerate(pieces):
-
-        @pl.when(pl.program_id(0) == index)
-        def _(piece=piece):
-            out_ref[...] = piece[...].astype(F32)
-
-
-def place_quarters(whole, near, far, shape, axis, offset, quarter):
-    rows, columns = near.shape[0] // 2, near.shape[1]
-    if axis == 0:
-        each, first_row = shape[0] // 4 // rows, offset // rows
-        spot = lambda k, q: ((q[0] ^ k) * each + first_row, 0)
-    else:
-        spot = lambda k, q: (offset // rows, q[0] ^ k)
+def place_kernel(axis, offsets, joins, where_ref, *refs):
+    chunks = len(offsets)
+    pair_refs, refs = refs[: 2 * joins], refs[2 * joins :]
+    sources, (*outs, wide_ref, sems) = refs[: 2 * chunks], refs[2 * chunks :]
+    out_ref = outs[-1 - joins]
+    rows, columns = wide_ref.shape[1:]
+
+    @pl.when(where_ref[1] == 1)
+    def _():
+        for index, offset in enumerate(offsets):
+            copies = []
+            for k in range(4):
+                source = sources[2 * index + k % 2]
+                wide_ref[k] = source[pl.ds(k // 2 * rows, rows), :].astype(F32)
+                place = where_ref[0] ^ k
+                if axis == 0:
+                    row = place * (out_ref.shape[0] // 4) + offset
+                    target = out_ref.at[pl.ds(pl.multiple_of(row, 8), rows), :]
+                else:
+                    column = pl.multiple_of(place * columns, 128)
+                    target = out_ref.at[pl.ds(offset, rows), pl.ds(column, columns)]
+                copies.append(pltpu.make_async_copy(wide_ref.at[k], target, sems.at[k]))
+                copies[-1].start()
+            for copy in copies:
+                copy.wait()
+
+    if joins:
+        half = pair_refs[0].shape[0]
+        outs[-1][:half, :] = pair_refs[0][...]
+        outs[-1][half:, :] = pair_refs[1][...]
+
+
+def place_quarters(whole, items, shape, axis, quarter, now, pair=()):
+    rows, columns = items[0][0].shape[0] // 2, items[0][0].shape[1]
+    blocks = list(pair) + [a for near, far, _ in items for a in (near, far)]
     first = whole is None
-    operands = ([] if first else [whole]) + [near, far, near, far]
-    return pl.pallas_call(
-        place_kernel,
+    out_specs = [pl.BlockSpec(memory_space=pl.ANY)]
+    out_shape = [jax.ShapeDtypeStruct(shape, F32)]
+    if pair:
+        joined = (2 * pair[0].shape[0], pair[0].shape[1])
+        out_specs.append(pl.BlockSpec(joined, lambda i, w: (0, 0)))
+        out_shape.append(jax.ShapeDtypeStruct(joined, BF))
+    out = pl.pallas_call(
+        functools.partial(place_kernel, axis, [o for *_, o in items], 1 if pair else 0),
         grid_spec=pltpu.PrefetchScalarGridSpec(
             num_scalar_prefetch=1,
-            grid=(4,),
-            in_specs=([] if first else [pl.BlockSpec(memory_space=pl.ANY)])
-            + [pl.BlockSpec((rows, columns), lambda k, q, h=h: (h, 0)) for h in (0, 0, 1, 1)],
-            out_specs=pl.BlockSpec((rows, columns), spot),
+            grid=(1,),
+            in_specs=[pl.BlockSpec(a.shape, lambda i, w: (0, 0)) for a in blocks]
+            + ([] if first else [pl.BlockSpec(memory_space=pl.ANY)]),
+            out_specs=out_specs,
+            scratch_shapes=[
+                pltpu.VMEM((4, rows, columns), F32),
+                pltpu.SemaphoreType.DMA((4,)),
+            ],
         ),
-        out_shape=jax.ShapeDtypeStruct(shape, F32),
-        input_output_aliases={} if first else {1: 0},
-        compiler_params=pltpu.CompilerParams(vmem_limit_bytes=24 << 20),
+        out_shape=out_shape,
+        input_output_aliases={} if first else {1 + len(blocks): 0},
+        compiler_params=pltpu.CompilerParams(vmem_limit_bytes=32 << 20 if pair else 20 << 20),
         cost_estimate=SMALL,
         name="place_quarters",
-    )(quarter.reshape(1), *operands)
+    )(jnp.stack([quarter, now]), *blocks, *([] if first else [whole]))
+    return out if pair else out[0]
 
 
 def norms_kernel(count, *refs):
@@ -621,6 +650,7 @@
     far_blocks = [block for pair in zip(ahead, mates) for block in pair]
     norms_far = both_norms(far_blocks, gains, 6 * ways)
     came, mates_own, counted, norms_far, last = meet(came, mates_own, counted, norms_far, last)
+    last_mates = [tuple(to_core(v) for v in pair) for pair in last]
     count = count + counted
     mask = 8
     while mask < dp:
@@ -634,14 +664,13 @@
     error_part = jnp.sum(mask_f[:, None] * mismatch * mismatch)
     grad_out = mask_f[:, None] * mismatch * (2.0 * total_tokens / count[0, 0])
     grad_low = grad_out.astype(BF)
-    grad_out, grad_low, last = meet(grad_out, grad_low, last)
+    grad_out, grad_low, last, last_mates = meet(grad_out, grad_low, last, last_mates)
 
     grad_y = [from_y(grad_low, step) for step in range(1, ways)]
     grad_first = first_far(grad_low)
     grad_mate = to_core(grad_low)
-    last = [jnp.concatenate([after(v, grad_mate), u], axis=0) for v, u in last]
-    far_blocks = [block for v in last for block in (v, to_core(v))]
-    norm_attn_far, norm_mlp_far = both_norms(far_blocks, gains, 6 * ways, norms_far)
+    far_blocks = [v for pair, mate in zip(last, last_mates) for v in pair + mate]
+    norm_attn_far, norm_mlp_far = both_norms(far_blocks, gains, 12 * ways, norms_far)
     fc1_quarter = quarter_of(fc1_weight, 1, quarter)
     fc2_quarter = quarter_of(after(fc2_weight, norm_mlp_far), 0, quarter)
     context_quarter = quarter_of(after(context, norm_mlp_far), 1, quarter)
@@ -681,6 +710,7 @@
     queue = []
     due = {}
     clock, launched = [0], [0]
+    join = [lambda low, across: jnp.concatenate([low, across], axis=0)]
     results = {}
     token = [grad_near]
 
@@ -697,7 +727,7 @@
             low = (low.astype(F32) + got.astype(F32)).astype(BF)
             mask, wait = mask * 2, 1
         (across,) = yield [flipped(low, 2)], 1
-        near = jnp.concatenate([low, across], axis=0)
+        near = join[0](low, across)
         (far,) = yield [flipped(near, 1)], 1
         results.setdefault(name, []).append((near, far))
 
@@ -706,14 +736,14 @@
         into.extend(got)
 
     def last_walk(kept, mates, parts, others, into):
-        (got,) = yield [(mates, to_core)], 1
-        sums = kept + got.astype(F32)
+        got, more = yield [(mates, to_core), (parts, to_core)], 1
+        sums, parts = kept + got.astype(F32), parts + more
         total = sums[0]
         for step in range(1, ways):
             (got,) = yield [(sums[step].astype(BF), lambda v, s=step: to_y(v, s))], 1
             total = total + got.astype(F32)
         into["input"] = grad_out + total
-        bit = 1
+        bit = 2
         while bit < tp:
             pairs = [(t, t ^ bit) for t in range(tp)]
             (got,) = yield [(parts, lambda v, p=pairs: lax.ppermute(v, "tensor", p))], 1
@@ -774,10 +804,12 @@
             start(walker, request, now)
         return tied
 
-    def place_one(whole, near, far, shape, axis, offset):
+    always = jnp.ones((), jnp.int32)
+
+    def place_one(whole, near, far, shape, axis, offset, now):
         rows_here, columns = near.shape[0] // 2, near.shape[1]
         if columns % 128 == 0:
-            return place_quarters(whole, near, far, shape, axis, offset, quarter)
+            return place_quarters(whole, [(near, far, offset)], shape, axis, quarter, now)
         if whole is None:
             whole = jnp.zeros(shape, F32)
         pieces = (near[:rows_here], far[:rows_here], near[rows_here:], far[rows_here:])
@@ -849,28 +881,50 @@
     walk(last_walk(kept, mates, tensor_parts, others, outcome))
     enqueue("qkv", *cut(qkv_part, [4, 4, 4, 2, 1, 1]))
     axes = {"fc2": 0, "out": 0, "fc1": 1, "qkv": 1}
-    placed = {name: (None, 0, 0) for name in axes}
-
-    def place(name):
-        whole, done, offset = placed[name]
-        pieces = results[name][done]
+    placed = {name: (None, 0) for name in axes}
+
+    def place_at(name, index, now):
+        near, far = results[name][index]
         lengths, columns = parts_of[name]
         shape = (4 * lengths, columns) if axes[name] == 0 else (lengths, 4 * columns)
-        whole = place_one(whole, *pieces, shape, axes[name], offset)
-        placed[name] = (whole, done + 1, offset + pieces[0].shape[0] // 2)
-
+        offset = sum(n.shape[0] // 2 for n, _ in results[name][:index])
+        return place_one(placed[name][0], near, far, shape, axes[name], offset, now)
+
+    def place(name):
+        placed[name] = (place_at(name, placed[name][1], always), placed[name][1] + 1)
+
+    shared = 3
+
+    def place_and_join(low, across):
+        lengths, columns = parts_of["fc2"]
+        items, offset = [], 0
+        for near, far in results["fc2"][:shared]:
+            items.append((near, far, offset))
+            offset += near.shape[0] // 2
+        whole, near = place_quarters(
+            None, items, (4 * lengths, columns), 0, quarter, core, (low, across)
+        )
+        placed["fc2"] = (whole, shared)
+        return near
+
+    simple_join = join[0]
+    turns_here = 0
     while queue or due:
         ready = []
-        for name in axes:
+        join[0] = place_and_join if turns_here == 1 else simple_join
+        for name in axes if turns_here > 1 else ():
             if len(ready) < 2 and len(results.get(name, [])) > placed[name][1]:
                 place(name)
                 ready.append(name)
         wholes = turn(*[placed[name][0] for name in ready])
         for name, whole in zip(ready, wholes):
             placed[name] = (whole,) + placed[name][1:]
+        turns_here += 1
     for name in axes:
         while len(results[name]) > placed[name][1]:
             place(name)
+    for index in range(shared):
+        placed["fc2"] = (place_at("fc2", index, 1 - core), placed["fc2"][1])
     input_grad = outcome["input"]
     small = outcome["small"]
     vectors = small[: 6 * D].reshape(6, D)

time: 651 us -> 673 us (1.034)
    pallas_call x15 -> x16, Pallas kernels: 34.7 us -> 39.3 us  [place_quarters(): pl.pallas_call(functools.partial(place_kernel, axis, [o for *_, o in item...]
    unnamed x173 -> x186, local copies, waits for them, and re-layouts: 17.2 us -> 16.8 us
  transfers between devices with their start and end apart: 99 -> 100, of which waited for: 38 -> 37; matrix products, arithmetic and copies ran while one was open for 21% -> 23% of each run, Pallas kernels for 26% -> 26%
where the time goes in v11:
time: 673 us; the launch traced here: 663 us
  waiting for transfers between devices  216 us (32%)
  Pallas kernels  173 us (26%)
  matrix products  97.2 us (14%)
  starting transfers between devices  92.9 us (14%)
  local copies, waits for them, and re-layouts  47 us (7%)
  other arithmetic  30.3 us (5%)
  between operations  6.76 us (1%)
    ppermute x69, waiting for transfers between devices, flip(): return lax.ppermute(v, 'dp', [(d, d ^ mask) for d in range(dp)])  203 us
    ppermute x69, starting transfers between devices, flip(): return lax.ppermute(v, 'dp', [(d, d ^ mask) for d in range(dp)])  80.2 us
    dot_general x8, matrix products, contract(): lax.dot_general(left_side, right_side, (((left_dim,), (right_dim,)), ((),...  50.3 us
    pallas_call x16, Pallas kernels, place_quarters(): pl.pallas_call(functools.partial(place_kernel, axis, [o for *_, o in item...  39.3 us
    pallas_call x1, Pallas kernels, norm_back(): pl.pallas_call(functools.partial(norm_back_kernel, count), grid=(count,),...  31.3 us
    pallas_call x4, Pallas kernels, both_norms(): pl.pallas_call(functools.partial(norms_kernel, count), grid=(count,), in_...  29.2 us
    pallas_call x2, Pallas kernels, outer_blocks(): pl.pallas_call(functools.partial(outer_kernel, len(lefts), pieces, len(si...  23.1 us
    dot_general x2, matrix products, units(): jnp.dot(normed, fc1_weight, preferred_element_type=F32)  20 us
  transfers between devices with their start and end apart: 100, of which 37 were waited for; matrix products, arithmetic and copies ran while one was open for 23% of the time, Pallas kernels for 26%

profile of v11, /device:TPU:0, one launch (start us, length us, event | category | flops | bytes accessed | tf_op | source)
XLA Modules:
  0.0 663.3 jit_solution(720131680365840722)
XLA Ops:
  1.2 2.6 collective-permute-start.3
  12.4 3.1 both_norms.4
  20.1 9.7 %multiply_convert_fusion.2 = (bf16[512,2048]{1,0:T(8,128)(2,1)}, f32[512,2048]{1,0:T(8,128)}) fusion(f32[2048]{0:T(1024)S(1)} %convert_element_type.230, bf16[512,2048]{1,0:T(8,128)(2,1)} %get-tuple-element.197, bf16[2048,2048]{1,0:T(8,128)(2,1)} %fc1_ref.1), kind=kOutput, calls=%fused_computation.20 | convolution fusion | flops 4301258752 | bytes 16785408 | tf_op jit(solution)/shard_map/dot_general | solution.py:567
  29.8 5.5 qkv_rotary.2.refs_0_
  42.9 4.6 both_norms.5
  47.5 2.6 copy-done.3
  51.6 2.8 copy-done.8
  54.4 5.5 qkv_rotary.3.q_ref.k_ref.v_ref
  59.9 9.6 %attend.1 = (bf16[1024,512]{1,0:T(8,128)(2,1)S(1)}, f32[2,1024,1]{2,1,0:T(8,128)S(1)}) custom-call(s32[1]{0:T(128)S(6)} %copy.84.prefix_ref, bf16[1024,1536]{1,0:T(8,128)(2,1)S(1)} %qkv_rotary.3.q_ref.k_ref.v_ref, bf16[1024,1536]{1,0:T(8,128)(2,1)S(1)} %qkv_rotary.3.q_ref.k_ref.v_ref, bf16[1024,1536]{1,0:T(8,128)(2,1)S(1)} %qkv_rotary.3.q_ref.k_ref.v_ref, ...), custom_call_target="tpu_custom_call" | custom-call | flops 1048576 | bytes 65536 | tf_op jit(solution)/shard_map/attend/pallas_call | solution.py:139
  71.2 2.6 collective-permute-start.13
  73.8 10.3 %multiply_convert_fusion.1 = (bf16[512,2048]{1,0:T(8,128)(2,1)S(1)}, f32[512,2048]{1,0:T(8,128)}) fusion(f32[2048]{0:T(1024)S(1)} %convert_element_type.230, bf16[512,2048]{1,0:T(8,128)(2,1)S(1)} %copy-done.52, bf16[2048,2048]{1,0:T(8,128)(2,1)} %fc1_ref.1), kind=kOutput, calls=%fused_computation.19 | convolution fusion | flops 4301258752 | bytes 16785408 | tf_op jit(solution)/shard_map/dot_general | solution.py:567
  84.1 10.5 %collective-permute-done.9.refs_6_ = bf16[256,2048]{1,0:T(8,128)(2,1)S(1)} collective-permute-done((bf16[256,2048]{1,0:T(8,128)(2,1)}, bf16[256,2048]{1,0:T(8,128)(2,1)S(1)}, u32[]{:S(2)}, u32[]{:S(2)}) %collective-permute-start.9) | collective-permute-done | bytes 1048608 | tf_op jit(solution)/shard_map/ppermute | solution.py:513
  94.7 4.6 fusion.51
  102.0 4.6 fusion.52
  117.6 2.6 collective-permute-start.23
  122.8 16.6 %both_norms.6 = (bf16[3072,2048]{1,0:T(8,128)(2,1)}, bf16[3072,2048]{1,0:T(8,128)(2,1)}) custom-call(bf16[1,2048]{1,0:T(2,128)(2,1)S(1)} %broadcast_in_dim.18.refs_0_.gain_a_ref, bf16[1,2048]{1,0:T(2,128)(2,1)S(1)} %broadcast_in_dim.38.refs_1_, bf16[1,2048]{1,0:T(2,128)(2,1)S(1)} %broadcast_in_dim.39.refs_2_.gain_m_ref, ...), custom_call_target="tpu_custom_call" | custom-call | flops 1048576 | bytes 65536 | tf_op jit(solution)/shard_map/both_norms/pallas_call | solution.py:382
  141.2 3.0 fusion.17
  151.0 4.9 both_norms.7
  155.9 14.7 %fusion.9 = (f32[3072,512]{1,0:T(8,128)}, bf16[3072,512]{1,0:T(8,128)(2,1)}) fusion(f32[512]{0:T(512)S(1)} %dynamic-slice_convert_fusion, bf16[3072,2048]{1,0:T(8,128)(2,1)} %get-tuple-element.241, bf16[2048,2048]{1,0:T(8,128)(2,1)} %fc1_ref.1, s32[]{:T(128)S(6)} %select_n.81), kind=kOutput, calls=%fused_computation.12 | convolution fusion | flops 6459752448 | bytes 24119300 | tf_op jit(solution)/shard_map/dot_general | solution.py:677
  172.2 3.1 constant_dynamic-slice_fusion.6.weight_ref
  179.7 17.5 %fusion.5.grad_inner_ref = bf16[1024,2048]{1,0:T(8,128)(2,1)} fusion(f32[512,2048]{1,0:T(8,128)} %get-tuple-element.414, f32[512,2048]{1,0:T(8,128)} %get-tuple-element.412, bf16[1024,2048]{1,0:T(8,128)(2,1)S(1)} %constant_dynamic-update-slice_fusion.refs_3_.refs_7_, bf16[2048,2048]{1,0:T(8,128)(2,1)} %param.34), kind=kOutput, calls=%fused_computation.7 | convolution fusion | flops 8613003264 | bytes 25165824 | tf_op jit(solution)/shard_map/dot_general | solution.py:35
  199.6 3.3 collective-permute-done.33.refs_12_.refs_16_.refs_8_
  206.0 12.0 %attend_back.1.grad_qkv_ref = bf16[1024,1536]{1,0:T(8,128)(2,1)} custom-call(s32[1]{0:T(128)S(6)} %copy.84.prefix_ref, bf16[1024,1536]{1,0:T(8,128)(2,1)} %copy-done.4, bf16[1024,1536]{1,0:T(8,128)(2,1)} %copy-done.4, bf16[1024,1536]{1,0:T(8,128)(2,1)} %copy-done.4, bf16[1024,512]{1,0:T(8,128)(2,1)S(1)} %convolution_convert_fusion.g_ref, ...), custom_call_target="tpu_custom_call" | custom-call | flops 1048576 | bytes 65536 | tf_op jit(solution)/shard_map/attend_back/pallas_call | solution.py:205
  219.1 3.3 constant_dynamic-slice_fusion
  226.5 10.6 %outer_blocks.2 = (bf16[128,2048]{1,0:T(8,128)(2,1)}, bf16[128,2048]{1,0:T(8,128)(2,1)}) custom-call(s32[1]{0:T(128)} %bitcast.9._, bf16[512,2048]{1,0:T(8,128)(2,1)} %get-tuple-element.214.refs_0_, bf16[512,2048]{1,0:T(8,128)(2,1)} %copy-done.45, bf16[3072,512]{1,0:T(8,128)(2,1)} %get-tuple-element.244.refs_2_, bf16[1024,2048]{1,0:T(8,128)(2,1)} %copy-done.35, ...), custom_call_target="tpu_custom_call" | custom-call | flops 1048576 | bytes 65536 | tf_op jit(solution)/shard_map/outer_blocks/pallas_call | solution.py:432
  239.2 2.6 collective-permute-start.49
  241.8 12.5 %outer_blocks.3 = (bf16[128,2048]{1,0:T(8,128)(2,1)}, bf16[128,2048]{1,0:T(8,128)(2,1)}, bf16[128,2048]{1,0:T(8,128)(2,1)}) custom-call(s32[1]{0:T(128)} %bitcast.9._, bf16[512,2048]{1,0:T(8,128)(2,1)} %get-tuple-element.214.refs_0_, bf16[512,2048]{1,0:T(8,128)(2,1)} %copy-done.45, bf16[3072,512]{1,0:T(8,128)(2,1)} %get-tuple-element.244.refs_2_, ...), custom_call_target="tpu_custom_call" | custom-call | flops 1048576 | bytes 65536 | tf_op jit(solution)/shard_map/outer_blocks/pallas_call | solution.py:432
  254.3 10.1 %collective-permute-done.45 = bf16[128,2048]{1,0:T(8,128)(2,1)S(1)} collective-permute-done((bf16[128,2048]{1,0:T(8,128)(2,1)}, bf16[128,2048]{1,0:T(8,128)(2,1)S(1)}, u32[]{:S(2)}, u32[]{:S(2)}) %collective-permute-start.45) | collective-permute-done | bytes 524320 | tf_op jit(solution)/shard_map/ppermute | solution.py:520
  270.2 17.8 %back_blocks.1 = bf16[3072,512]{1,0:T(8,128)(2,1)} custom-call(bf16[512,2048]{1,0:T(8,128)(2,1)} %constant_dynamic-slice_fusion.6.weight_ref, f32[3072,512]{1,0:T(8,128)} %get-tuple-element.383.slope_ref, bf16[256,2048]{1,0:T(8,128)(2,1)} %copy-done.39, bf16[256,2048]{1,0:T(8,128)(2,1)} %copy-done.41, bf16[256,2048]{1,0:T(8,128)(2,1)} %copy-done.38, ...), custom_call_target="tpu_custom_call" | custom-call | flops 1048576 | bytes 65536 | tf_op jit(solution)/shard_map/back_blocks/pallas_call | solution.py:462
  288.1 14.2 %collective-permute-done.51 = bf16[128,2048]{1,0:T(8,128)(2,1)S(1)} collective-permute-done((bf16[128,2048]{1,0:T(8,128)(2,1)S(1)}, bf16[128,2048]{1,0:T(8,128)(2,1)S(1)}, u32[]{:S(2)}, u32[]{:S(2)}) %collective-permute-start.51) | collective-permute-done | bytes 524320 | tf_op jit(solution)/shard_map/ppermute | solution.py:520
  306.7 4.8 collective-permute-start.55
  311.5 11.6 %add_convert_fusion = bf16[2048,512]{1,0:T(8,128)(2,1)} fusion(f32[2048,512]{1,0:T(8,128)S(1)} %fusion.35, f32[2048,512]{1,0:T(8,128)S(1)} %fusion.33, bf16[3072,2048]{1,0:T(8,128)(2,1)} %get-tuple-element.241, bf16[3072,512]{1,0:T(8,128)(2,1)} %back_blocks.1), kind=kOutput, calls=%fused_computation.18 | convolution fusion | flops 6445596672 | bytes 26214400 | tf_op jit(solution)/shard_map/dot_general | solution.py:35
  323.1 7.0 %collective-permute-done.52 = bf16[128,2048]{1,0:T(8,128)(2,1)} collective-permute-done((bf16[128,2048]{1,0:T(8,128)(2,1)S(1)}, bf16[128,2048]{1,0:T(8,128)(2,1)}, u32[]{:S(2)}, u32[]{:S(2)}) %collective-permute-start.52) | collective-permute-done | bytes 524320 | tf_op jit(solution)/shard_map/ppermute | solution.py:520
  334.7 10.3 %fusion.11 = f32[2048,384]{1,0:T(8,128)} fusion(bf16[3072,2048]{1,0:T(8,128)(2,1)S(1)} %bitcast.85, bf16[1024,384]{1,0:T(8,128)(2,1)} %collective-permute-done.50, bf16[1024,384]{1,0:T(8,128)(2,1)} %collective-permute-done.47, bf16[1024,384]{1,0:T(8,128)(2,1)} %collective-permute-done.46), kind=kOutput, calls=%fused_computation.28 | convolution fusion | flops 4838916096 | bytes 18087936 | tf_op jit(solution)/shard_map/dot_general | solution.py:35
  345.0 3.8 collective-permute-start.54
  348.7 31.3 %norm_back.1 = (f32[1024,2048]{1,0:T(8,128)}, f32[8,2048]{1,0:T(8,128)}, f32[8,1536]{1,0:T(8,128)}, f32[8,2048]{1,0:T(8,128)}) custom-call(bf16[1024,1536]{1,0:T(8,128)(2,1)} %attend_back.1.grad_qkv_ref, bf16[1024,2048]{1,0:T(8,128)(2,1)} %fusion.5.grad_inner_ref, bf16[2048,1536]{1,0:T(8,128)(2,1)} %qkv_ref.1, bf16[2048,2048]{1,0:T(8,128)(2,1)} %fc1_ref.1, ...), custom_call_target="tpu_custom_call" | custom-call | flops 1048576 | bytes 65536 | tf_op jit(solution)/shard_map/norm_back/pallas_call | solution.py:279
  381.5 2.7 add_convert_fusion.7
  388.0 3.8 fusion.18
  396.8 3.5 add_convert_fusion.1
  400.3 2.5 collective-permute-done.58
  402.8 6.2 collective-permute-done.59.refs_7_.refs_1_
  414.2 23.8 %collective-permute-done.60 = bf16[512,512]{1,0:T(8,128)(2,1)S(1)} collective-permute-done((bf16[512,512]{1,0:T(8,128)(2,1)S(1)}, bf16[512,512]{1,0:T(8,128)(2,1)S(1)}, u32[]{:S(2)}, u32[]{:S(2)}) %collective-permute-start.60) | collective-permute-done | bytes 524320 | tf_op jit(solution)/shard_map/ppermute | solution.py:520
  444.0 21.3 %collective-permute-done.66 = bf16[512,512]{1,0:T(8,128)(2,1)S(1)} collective-permute-done((bf16[512,512]{1,0:T(8,128)(2,1)S(1)}, bf16[512,512]{1,0:T(8,128)(2,1)S(1)}, u32[]{:S(2)}, u32[]{:S(2)}) %collective-permute-start.66) | collective-permute-done | bytes 524320 | tf_op jit(solution)/shard_map/ppermute | solution.py:520
  470.1 2.5 collective-permute-start.70
  473.7 2.7 place_quarters.18
  476.3 2.7 place_quarters.17.refs_2_
  479.0 17.4 %collective-permute-done.65 = bf16[512,512]{1,0:T(8,128)(2,1)S(1)} collective-permute-done((bf16[512,512]{1,0:T(8,128)(2,1)S(1)}, bf16[512,512]{1,0:T(8,128)(2,1)S(1)}, u32[]{:S(2)}, u32[]{:S(2)}) %collective-permute-start.65) | collective-permute-done | bytes 524320 | tf_op jit(solution)/shard_map/ppermute | solution.py:520
  502.5 2.6 place_quarters.19.refs_2_
  505.2 17.2 %collective-permute-done.73 = bf16[512,512]{1,0:T(8,128)(2,1)S(1)} collective-permute-done((bf16[512,512]{1,0:T(8,128)(2,1)S(1)}, bf16[512,512]{1,0:T(8,128)(2,1)S(1)}, u32[]{:S(2)}, u32[]{:S(2)}) %collective-permute-start.73) | collective-permute-done | bytes 524320 | tf_op jit(solution)/shard_map/ppermute | solution.py:520
  527.1 2.6 place_quarters.20.refs_2_
  529.7 14.8 %collective-permute-done.77 = bf16[512,384]{1,0:T(8,128)(2,1)S(1)} collective-permute-done((bf16[512,384]{1,0:T(8,128)(2,1)S(1)}, bf16[512,384]{1,0:T(8,128)(2,1)S(1)}, u32[]{:S(2)}, u32[]{:S(2)}) %collective-permute-start.77) | collective-permute-done | bytes 393248 | tf_op jit(solution)/shard_map/ppermute | solution.py:520
  544.5 2.9 collective-permute-done.80
  552.3 2.7 place_quarters.21.refs_2_
  554.9 13.1 %collective-permute-done.81 = bf16[512,384]{1,0:T(8,128)(2,1)S(1)} collective-permute-done((bf16[512,384]{1,0:T(8,128)(2,1)S(1)}, bf16[512,384]{1,0:T(8,128)(2,1)S(1)}, u32[]{:S(2)}, u32[]{:S(2)}) %collective-permute-start.81) | collective-permute-done | bytes 393248 | tf_op jit(solution)/shard_map/ppermute | solution.py:520
  575.8 2.7 place_quarters.22
  578.4 13.2 %collective-permute-done.86 = bf16[512,384]{1,0:T(8,128)(2,1)S(1)} collective-permute-done((bf16[512,384]{1,0:T(8,128)(2,1)S(1)}, bf16[512,384]{1,0:T(8,128)(2,1)S(1)}, u32[]{:S(2)}, u32[]{:S(2)}) %collective-permute-start.86) | collective-permute-done | bytes 393248 | tf_op jit(solution)/shard_map/ppermute | solution.py:520
  597.8 7.5 %collective-permute-done.85 = bf16[256,384]{1,0:T(8,128)(2,1)S(1)} collective-permute-done((bf16[256,384]{1,0:T(8,128)(2,1)S(1)}, bf16[256,384]{1,0:T(8,128)(2,1)S(1)}, u32[]{:S(2)}, u32[]{:S(2)}) %collective-permute-start.85) | collective-permute-done | bytes 196640 | tf_op jit(solution)/shard_map/ppermute | solution.py:520
  607.5 3.6 collective-permute-done.90.refs_1_
  612.1 2.9 collective-permute-start.92
  619.4 10.0 %collective-permute-done.94.refs_1_ = bf16[1024,384]{1,0:T(8,128)(2,1)S(1)} collective-permute-done((bf16[1024,384]{1,0:T(8,128)(2,1)S(1)}, bf16[1024,384]{1,0:T(8,128)(2,1)S(1)}, u32[]{:S(2)}, u32[]{:S(2)}) %collective-permute-start.94) | collective-permute-done | bytes 786464 | tf_op jit(solution)/shard_map/ppermute | solution.py:520
  630.3 3.5 collective-permute-start.95
  641.4 2.6 place_quarters.29.refs_2_
  644.1 2.7 place_quarters.30.refs_2_
  646.7 4.2 place_quarters.31
  (467 shorter events, 162.2 us)
Async XLA Ops:
  1.2 35.8 %collective-permute-start.3 = (bf16[256,2048]{1,0:T(8,128)(2,1)}, bf16[256,2048]{1,0:T(8,128)(2,1)}, u32[]{:S(2)}, u32[]{:S(2)}) collective-permute-start(bf16[256,2048]{1,0:T(8,128)(2,1)} %refs_0_.1), channel_id=1, source_target_pairs={{0,4},{4,0},{8,12},{12,8},{16,20},{20,16},{24,28},{28,24},{1,5},{5... | collective-permute-start | bytes 3145736 | tf_op jit(solution)/shard_map/ppermute | solution.py:520
  3.8 33.2 %collective-permute-start.4 = (bf16[256,2048]{1,0:T(8,128)(2,1)}, bf16[256,2048]{1,0:T(8,128)(2,1)}, u32[]{:S(2)}, u32[]{:S(2)}) collective-permute-start(bf16[256,2048]{1,0:T(8,128)(2,1)} %refs_0_.1), channel_id=1, source_target_pairs={{0,8},{4,12},{8,0},{12,4},{16,24},{20,28},{24,16},{28,20},{1,9},{5... | collective-permute-start | bytes 3145736 | tf_op jit(solution)/shard_map/ppermute | solution.py:520
  5.3 31.6 %collective-permute-start.5 = (bf16[256,2048]{1,0:T(8,128)(2,1)}, bf16[256,2048]{1,0:T(8,128)(2,1)}, u32[]{:S(2)}, u32[]{:S(2)}) collective-permute-start(bf16[256,2048]{1,0:T(8,128)(2,1)} %refs_0_.1), channel_id=1, source_target_pairs={{0,2},{1,3},{2,0},{3,1},{4,6},{5,7},{6,4},{7,5},{8,10},{9,11},{10,... | collective-permute-start | bytes 3145736 | tf_op jit(solution)/shard_map/ppermute | solution.py:513
  37.3 33.0 %collective-permute-start.10 = (bf16[256,2048]{1,0:T(8,128)(2,1)}, bf16[256,2048]{1,0:T(8,128)(2,1)}, u32[]{:S(2)}, u32[]{:S(2)}) collective-permute-start(bf16[256,2048]{1,0:T(8,128)(2,1)} %collective-permute-done.5.refs_4_.refs_2_), channel_id=1, source_target_pairs={{0,8},{4,12},{8,0},{12,4},{16,24},{20,28},{24,16},{28,20},{1,9},{5... | collective-permute-start | bytes 3145736 | tf_op jit(solution)/shard_map/ppermute | solution.py:520
  37.7 33.2 %collective-permute-start.14 = (bf16[256,2048]{1,0:T(8,128)(2,1)}, bf16[256,2048]{1,0:T(8,128)(2,1)}, u32[]{:S(2)}, u32[]{:S(2)}) collective-permute-start(bf16[256,2048]{1,0:T(8,128)(2,1)} %collective-permute-done.3.refs_4_), channel_id=1, source_target_pairs={{0,1},{1,0},{2,3},{3,2},{4,5},{5,4},{6,7},{7,6},{8,9},{9,8},{10,11... | collective-permute-start | bytes 3145736 | tf_op jit(solution)/shard_map/ppermute | solution.py:509
  37.7 33.4 %collective-permute-start.15 = (bf16[256,2048]{1,0:T(8,128)(2,1)}, bf16[256,2048]{1,0:T(8,128)(2,1)}, u32[]{:S(2)}, u32[]{:S(2)}) collective-permute-start(bf16[256,2048]{1,0:T(8,128)(2,1)} %collective-permute-done.4.refs_8_), channel_id=1, source_target_pairs={{0,1},{1,0},{2,3},{3,2},{4,5},{5,4},{6,7},{7,6},{8,9},{9,8},{10,11... | collective-permute-start | bytes 3145736 | tf_op jit(solution)/shard_map/ppermute | solution.py:509
  39.2 45.0 %collective-permute-start.8 = (bf16[256,2048]{1,0:T(8,128)(2,1)}, bf16[256,2048]{1,0:T(8,128)(2,1)S(1)}, u32[]{:S(2)}, u32[]{:S(2)}) collective-permute-start(bf16[256,2048]{1,0:T(8,128)(2,1)} %collective-permute-done.4.refs_8_), channel_id=1, source_target_pairs={{0,4},{4,0},{8,12},{12,8},{16,20},{20,16},{24,28},{28,24},{1,5},{5... | collective-permute-start | bytes 3145736 | tf_op jit(solution)/shard_map/ppermute | solution.py:520
  41.3 28.5 %collective-permute-start.7 = (f32[8,128]{1,0:T(8,128)S(1)}, f32[8,128]{1,0:T(8,128)S(1)}, u32[]{:S(2)}, u32[]{:S(2)}) collective-permute-start(f32[8,128]{1,0:T(8,128)S(1)} %fusion.75), channel_id=1, source_target_pairs={{0,8},{4,12},{8,0},{12,4},{16,24},{20,28},{24,16},{28,20},{1,9},{5... | collective-permute-start | bytes 12296 | tf_op jit(solution)/shard_map/ppermute | solution.py:520
  69.7 24.9 %collective-permute-start.9 = (bf16[256,2048]{1,0:T(8,128)(2,1)}, bf16[256,2048]{1,0:T(8,128)(2,1)S(1)}, u32[]{:S(2)}, u32[]{:S(2)}) collective-permute-start(bf16[256,2048]{1,0:T(8,128)(2,1)} %collective-permute-done.3.refs_4_), channel_id=1, source_target_pairs={{0,2},{1,3},{2,0},{3,1},{4,6},{5,7},{6,4},{7,5},{8,10},{9,11},{10,... | collective-permute-start | bytes 3145736 | tf_op jit(solution)/shard_map/ppermute | solution.py:513
  70.3 24.4 %collective-permute-start.11 = (bf16[1024,128]{1,0:T(8,128)(2,1)S(1)}, bf16[1024,128]{1,0:T(8,128)(2,1)S(1)}, u32[]{:S(2)}, u32[]{:S(2)}) collective-permute-start(bf16[1024,128]{1,0:T(8,128)(2,1)S(1)} %get-tuple-element.404), channel_id=1, source_target_pairs={{0,4},{4,0},{8,12},{12,8},{16,20},{20,16},{24,28},{28,24},{1,5},{5... | collective-permute-start | bytes 786440 | tf_op jit(solution)/shard_map/ppermute | solution.py:520
  70.9 23.7 %collective-permute-start.12 = (bf16[1024,128]{1,0:T(8,128)(2,1)S(1)}, bf16[1024,128]{1,0:T(8,128)(2,1)S(1)}, u32[]{:S(2)}, u32[]{:S(2)}) collective-permute-start(bf16[1024,128]{1,0:T(8,128)(2,1)S(1)} %get-tuple-element.403), channel_id=1, source_target_pairs={{0,8},{4,12},{8,0},{12,4},{16,24},{20,28},{24,16},{28,20},{1,9},{5... | collective-permute-start | bytes 786440 | tf_op jit(solution)/shard_map/ppermute | solution.py:520
  71.2 23.5 %collective-permute-start.13 = (bf16[1024,128]{1,0:T(8,128)(2,1)S(1)}, bf16[1024,128]{1,0:T(8,128)(2,1)S(1)}, u32[]{:S(2)}, u32[]{:S(2)}) collective-permute-start(bf16[1024,128]{1,0:T(8,128)(2,1)S(1)} %get-tuple-element.402), channel_id=1, source_target_pairs={{0,12},{4,8},{8,4},{12,0},{16,28},{20,24},{24,20},{28,16},{1,13},{... | collective-permute-start | bytes 786440 | tf_op jit(solution)/shard_map/ppermute | solution.py:520
  111.9 27.5 %collective-permute-start.21 = (bf16[256,2048]{1,0:T(8,128)(2,1)}, bf16[256,2048]{1,0:T(8,128)(2,1)}, u32[]{:S(2)}, u32[]{:S(2)}) collective-permute-start(bf16[256,2048]{1,0:T(8,128)(2,1)} %fusion.30), channel_id=1, source_target_pairs={{0,2},{1,3},{2,0},{3,1},{4,6},{5,7},{6,4},{7,5},{8,10},{9,11},{10,... | collective-permute-start | bytes 3145736 | tf_op jit(solution)/shard_map/ppermute | solution.py:517
  113.8 25.6 %collective-permute-start.22 = (bf16[256,2048]{1,0:T(8,128)(2,1)}, bf16[256,2048]{1,0:T(8,128)(2,1)}, u32[]{:S(2)}, u32[]{:S(2)}) collective-permute-start(bf16[256,2048]{1,0:T(8,128)(2,1)} %fusion.31), channel_id=1, source_target_pairs={{0,1},{1,0},{2,3},{3,2},{4,5},{5,4},{6,7},{7,6},{8,9},{9,8},{10,11... | collective-permute-start | bytes 3145736 | tf_op jit(solution)/shard_map/ppermute | solution.py:509
  116.6 22.8 %collective-permute-start.24 = (bf16[128,2048]{1,0:T(8,128)(2,1)}, bf16[128,2048]{1,0:T(8,128)(2,1)}, u32[]{:S(2)}, u32[]{:S(2)}) collective-permute-start(bf16[128,2048]{1,0:T(8,128)(2,1)} %slice.145), channel_id=1, source_target_pairs={{0,4},{4,0},{8,12},{12,8},{16,20},{20,16},{24,28},{28,24},{1,5},{5... | collective-permute-start | bytes 1572872 | tf_op jit(solution)/shard_map/ppermute | solution.py:520
  117.2 22.2 %collective-permute-start.25 = (bf16[128,2048]{1,0:T(8,128)(2,1)}, bf16[128,2048]{1,0:T(8,128)(2,1)}, u32[]{:S(2)}, u32[]{:S(2)}) collective-permute-start(bf16[128,2048]{1,0:T(8,128)(2,1)} %slice.146), channel_id=1, source_target_pairs={{0,8},{4,12},{8,0},{12,4},{16,24},{20,28},{24,16},{28,20},{1,9},{5... | collective-permute-start | bytes 1572872 | tf_op jit(solution)/shard_map/ppermute | solution.py:520
  117.6 21.8 %collective-permute-start.23 = (f32[8,128]{1,0:T(8,128)S(1)}, f32[8,128]{1,0:T(8,128)S(1)}, u32[]{:S(2)}, u32[]{:S(2)}) collective-permute-start(f32[8,128]{1,0:T(8,128)S(1)} %add.303), channel_id=1, source_target_pairs={{0,16},{4,20},{8,24},{12,28},{16,0},{20,4},{24,8},{28,12},{1,17},{... | collective-permute-start | bytes 12296 | tf_op jit(solution)/shard_map/ppermute | solution.py:520
  146.6 28.8 %collective-permute-start.28 = (bf16[256,2048]{1,0:T(8,128)(2,1)S(1)}, bf16[256,2048]{1,0:T(8,128)(2,1)}, u32[]{:S(2)}, u32[]{:S(2)}) collective-permute-start(bf16[256,2048]{1,0:T(8,128)(2,1)S(1)} %get-tuple-element.234), channel_id=1, source_target_pairs={{0,2},{1,3},{2,0},{3,1},{4,6},{5,7},{6,4},{7,5},{8,10},{9,11},{10,... | collective-permute-start | bytes 3145736 | tf_op jit(solution)/shard_map/ppermute | solution.py:513
  147.9 27.4 %collective-permute-start.29 = (bf16[256,2048]{1,0:T(8,128)(2,1)S(1)}, bf16[256,2048]{1,0:T(8,128)(2,1)S(1)}, u32[]{:S(2)}, u32[]{:S(2)}) collective-permute-start(bf16[256,2048]{1,0:T(8,128)(2,1)S(1)} %get-tuple-element.234), channel_id=1, source_target_pairs={{0,4},{4,0},{8,12},{12,8},{16,20},{20,16},{24,28},{28,24},{1,5},{5... | collective-permute-start | bytes 3145736 | tf_op jit(solution)/shard_map/ppermute | solution.py:520
  149.4 25.9 %collective-permute-start.30 = (bf16[256,2048]{1,0:T(8,128)(2,1)S(1)}, bf16[256,2048]{1,0:T(8,128)(2,1)S(1)}, u32[]{:S(2)}, u32[]{:S(2)}) collective-permute-start(bf16[256,2048]{1,0:T(8,128)(2,1)S(1)} %get-tuple-element.234), channel_id=1, source_target_pairs={{0,8},{4,12},{8,0},{12,4},{16,24},{20,28},{24,16},{28,20},{1,9},{5... | collective-permute-start | bytes 3145736 | tf_op jit(solution)/shard_map/ppermute | solution.py:520
  151.0 24.4 %collective-permute-start.31 = (bf16[256,2048]{1,0:T(8,128)(2,1)S(1)}, bf16[256,2048]{1,0:T(8,128)(2,1)S(1)}, u32[]{:S(2)}, u32[]{:S(2)}) collective-permute-start(bf16[256,2048]{1,0:T(8,128)(2,1)S(1)} %get-tuple-element.234), channel_id=1, source_target_pairs={{0,1},{1,0},{2,3},{3,2},{4,5},{5,4},{6,7},{7,6},{8,9},{9,8},{10,11... | collective-permute-start | bytes 3145736 | tf_op jit(solution)/shard_map/ppermute | solution.py:509
  176.1 26.9 %collective-permute-start.35 = (bf16[256,2048]{1,0:T(8,128)(2,1)}, bf16[256,2048]{1,0:T(8,128)(2,1)S(1)}, u32[]{:S(2)}, u32[]{:S(2)}) collective-permute-start(bf16[256,2048]{1,0:T(8,128)(2,1)} %collective-permute-done.28), channel_id=1, source_target_pairs={{0,8},{4,12},{8,0},{12,4},{16,24},{20,28},{24,16},{28,20},{1,9},{5... | collective-permute-start | bytes 3145736 | tf_op jit(solution)/shard_map/ppermute | solution.py:520
  176.6 26.4 %collective-permute-start.34 = (bf16[256,2048]{1,0:T(8,128)(2,1)S(1)}, bf16[256,2048]{1,0:T(8,128)(2,1)S(1)}, u32[]{:S(2)}, u32[]{:S(2)}) collective-permute-start(bf16[256,2048]{1,0:T(8,128)(2,1)S(1)} %collective-permute-done.29.refs_4_.refs_8_.refs_0_), channel_id=1, source_target_pairs={{0,2},{1,3},{2,0},{3,1},{4,6},{5,7},{6,4},{7,5},{8,10},{9,11},{10,... | collective-permute-start | bytes 3145736 | tf_op jit(solution)/shard_map/ppermute | solution.py:513
  177.3 26.4 %collective-permute-start.38 = (bf16[256,2048]{1,0:T(8,128)(2,1)S(1)}, bf16[256,2048]{1,0:T(8,128)(2,1)S(1)}, u32[]{:S(2)}, u32[]{:S(2)}) collective-permute-start(bf16[256,2048]{1,0:T(8,128)(2,1)S(1)} %collective-permute-done.29.refs_4_.refs_8_.refs_0_), channel_id=1, source_target_pairs={{0,1},{1,0},{2,3},{3,2},{4,5},{5,4},{6,7},{7,6},{8,9},{9,8},{10,11... | collective-permute-start | bytes 3145736 | tf_op jit(solution)/shard_map/ppermute | solution.py:509
  177.3 25.7 %collective-permute-start.33 = (bf16[256,2048]{1,0:T(8,128)(2,1)S(1)}, bf16[256,2048]{1,0:T(8,128)(2,1)}, u32[]{:S(2)}, u32[]{:S(2)}) collective-permute-start(bf16[256,2048]{1,0:T(8,128)(2,1)S(1)} %collective-permute-done.30.refs_8_.refs_12_.refs_4_), channel_id=1, source_target_pairs={{0,4},{4,0},{8,12},{12,8},{16,20},{20,16},{24,28},{28,24},{1,5},{5... | collective-permute-start | bytes 3145736 | tf_op jit(solution)/shard_map/ppermute | solution.py:520
  179.3 25.1 %collective-permute-start.40 = (bf16[256,2048]{1,0:T(8,128)(2,1)S(1)}, bf16[256,2048]{1,0:T(8,128)(2,1)}, u32[]{:S(2)}, u32[]{:S(2)}) collective-permute-start(bf16[256,2048]{1,0:T(8,128)(2,1)S(1)} %collective-permute-done.30.refs_8_.refs_12_.refs_4_), channel_id=1, source_target_pairs={{0,1},{1,0},{2,3},{3,2},{4,5},{5,4},{6,7},{7,6},{8,9},{9,8},{10,11... | collective-permute-start | bytes 3145736 | tf_op jit(solution)/shard_map/ppermute | solution.py:509
  222.4 31.9 %collective-permute-start.46 = (bf16[1024,384]{1,0:T(8,128)(2,1)}, bf16[1024,384]{1,0:T(8,128)(2,1)}, u32[]{:S(2)}, u32[]{:S(2)}) collective-permute-start(bf16[1024,384]{1,0:T(8,128)(2,1)} %get-tuple-element.387), channel_id=1, source_target_pairs={{0,4},{4,0},{8,12},{12,8},{16,20},{20,16},{24,28},{28,24},{1,5},{5... | collective-permute-start | bytes 2359304 | tf_op jit(solution)/shard_map/ppermute | solution.py:520
  223.9 30.5 %collective-permute-start.47 = (bf16[1024,384]{1,0:T(8,128)(2,1)}, bf16[1024,384]{1,0:T(8,128)(2,1)}, u32[]{:S(2)}, u32[]{:S(2)}) collective-permute-start(bf16[1024,384]{1,0:T(8,128)(2,1)} %get-tuple-element.386), channel_id=1, source_target_pairs={{0,8},{4,12},{8,0},{12,4},{16,24},{20,28},{24,16},{28,20},{1,9},{5... | collective-permute-start | bytes 2359304 | tf_op jit(solution)/shard_map/ppermute | solution.py:520
  237.1 27.3 %collective-permute-start.45 = (bf16[128,2048]{1,0:T(8,128)(2,1)}, bf16[128,2048]{1,0:T(8,128)(2,1)S(1)}, u32[]{:S(2)}, u32[]{:S(2)}) collective-permute-start(bf16[128,2048]{1,0:T(8,128)(2,1)} %get-tuple-element.262), channel_id=1, source_target_pairs={{0,16},{4,20},{8,24},{12,28},{16,0},{20,4},{24,8},{28,12},{1,17},{... | collective-permute-start | bytes 1572872 | tf_op jit(solution)/shard_map/ppermute | solution.py:520
  238.7 49.3 %collective-permute-start.50 = (bf16[1024,384]{1,0:T(8,128)(2,1)S(1)}, bf16[1024,384]{1,0:T(8,128)(2,1)}, u32[]{:S(2)}, u32[]{:S(2)}) collective-permute-start(bf16[1024,384]{1,0:T(8,128)(2,1)S(1)} %constant_dynamic-slice_fusion.2), channel_id=1, source_target_pairs={{0,12},{4,8},{8,4},{12,0},{16,28},{20,24},{24,20},{28,16},{1,13},{... | collective-permute-start | bytes 2359304 | tf_op jit(solution)/shard_map/ppermute | solution.py:520
  239.2 48.9 %collective-permute-start.49 = (bf16[128,2048]{1,0:T(8,128)(2,1)}, bf16[128,2048]{1,0:T(8,128)(2,1)S(1)}, u32[]{:S(2)}, u32[]{:S(2)}) collective-permute-start(bf16[128,2048]{1,0:T(8,128)(2,1)} %get-tuple-element.271), channel_id=1, source_target_pairs={{0,16},{4,20},{8,24},{12,28},{16,0},{20,4},{24,8},{28,12},{1,17},{... | collective-permute-start | bytes 1572872 | tf_op jit(solution)/shard_map/ppermute | solution.py:520
  264.6 37.7 %collective-permute-start.51 = (bf16[128,2048]{1,0:T(8,128)(2,1)S(1)}, bf16[128,2048]{1,0:T(8,128)(2,1)S(1)}, u32[]{:S(2)}, u32[]{:S(2)}) collective-permute-start(bf16[128,2048]{1,0:T(8,128)(2,1)S(1)} %add_convert_fusion.10), channel_id=1, source_target_pairs={{0,8},{4,12},{8,0},{12,4},{16,24},{20,28},{24,16},{28,20},{1,9},{5... | collective-permute-start | bytes 1572872 | tf_op jit(solution)/shard_map/ppermute | solution.py:520
  266.1 57.0 %collective-permute-start.48 = (bf16[128,2048]{1,0:T(8,128)(2,1)}, bf16[128,2048]{1,0:T(8,128)(2,1)}, u32[]{:S(2)}, u32[]{:S(2)}) collective-permute-start(bf16[128,2048]{1,0:T(8,128)(2,1)} %get-tuple-element.270), channel_id=1, source_target_pairs={{0,16},{4,20},{8,24},{12,28},{16,0},{20,4},{24,8},{28,12},{1,17},{... | collective-permute-start | bytes 1572872 | tf_op jit(solution)/shard_map/ppermute | solution.py:520
  306.2 24.0 %collective-permute-start.53 = (bf16[256,2048]{1,0:T(8,128)(2,1)S(1)}, bf16[256,2048]{1,0:T(8,128)(2,1)S(1)}, u32[]{:S(2)}, u32[]{:S(2)}) collective-permute-start(bf16[256,2048]{1,0:T(8,128)(2,1)S(1)} %pad_maximum_fusion.4.refs_2_.refs_0_), channel_id=1, source_target_pairs={{0,4},{4,0},{8,12},{12,8},{16,20},{20,16},{24,28},{28,24},{1,5},{5... | collective-permute-start | bytes 3145736 | tf_op jit(solution)/shard_map/ppermute | solution.py:520
  306.7 23.3 %collective-permute-start.52 = (bf16[128,2048]{1,0:T(8,128)(2,1)S(1)}, bf16[128,2048]{1,0:T(8,128)(2,1)}, u32[]{:S(2)}, u32[]{:S(2)}) collective-permute-start(bf16[128,2048]{1,0:T(8,128)(2,1)S(1)} %add_convert_fusion.9), channel_id=1, source_target_pairs={{0,8},{4,12},{8,0},{12,4},{16,24},{20,28},{24,16},{28,20},{1,9},{5... | collective-permute-start | bytes 1572872 | tf_op jit(solution)/shard_map/ppermute | solution.py:520
  306.7 74.7 %collective-permute-start.55 = (bf16[128,2048]{1,0:T(8,128)(2,1)}, bf16[128,2048]{1,0:T(8,128)(2,1)}, u32[]{:S(2)}, u32[]{:S(2)}) collective-permute-start(bf16[128,2048]{1,0:T(8,128)(2,1)} %get-tuple-element.288), channel_id=1, source_target_pairs={{0,16},{4,20},{8,24},{12,28},{16,0},{20,4},{24,8},{28,12},{1,17},{... | collective-permute-start | bytes 1572872 | tf_op jit(solution)/shard_map/ppermute | solution.py:520
  331.7 49.7 %collective-permute-start.57 = (bf16[256,2048]{1,0:T(8,128)(2,1)S(1)}, bf16[256,2048]{1,0:T(8,128)(2,1)S(1)}, u32[]{:S(2)}, u32[]{:S(2)}) collective-permute-start(bf16[256,2048]{1,0:T(8,128)(2,1)S(1)} %pad_maximum_fusion.5.refs_4_.refs_0_), channel_id=1, source_target_pairs={{0,4},{4,0},{8,12},{12,8},{16,20},{20,16},{24,28},{28,24},{1,5},{5... | collective-permute-start | bytes 3145736 | tf_op jit(solution)/shard_map/ppermute | solution.py:520
  334.5 46.9 %collective-permute-start.56 = (bf16[128,2048]{1,0:T(8,128)(2,1)S(1)}, bf16[128,2048]{1,0:T(8,128)(2,1)S(1)}, u32[]{:S(2)}, u32[]{:S(2)}) collective-permute-start(bf16[128,2048]{1,0:T(8,128)(2,1)S(1)} %add_convert_fusion.8), channel_id=1, source_target_pairs={{0,8},{4,12},{8,0},{12,4},{16,24},{20,28},{24,16},{28,20},{1,9},{5... | collective-permute-start | bytes 1572872 | tf_op jit(solution)/shard_map/ppermute | solution.py:520
  345.0 55.3 %collective-permute-start.54 = (bf16[128,2048]{1,0:T(8,128)(2,1)}, bf16[128,2048]{1,0:T(8,128)(2,1)}, u32[]{:S(2)}, u32[]{:S(2)}) collective-permute-start(bf16[128,2048]{1,0:T(8,128)(2,1)} %get-tuple-element.287), channel_id=1, source_target_pairs={{0,16},{4,20},{8,24},{12,28},{16,0},{20,4},{24,8},{28,12},{1,17},{... | collective-permute-start | bytes 1572872 | tf_op jit(solution)/shard_map/ppermute | solution.py:520
  386.5 22.6 %collective-permute-start.59 = (bf16[256,2048]{1,0:T(8,128)(2,1)}, bf16[256,2048]{1,0:T(8,128)(2,1)}, u32[]{:S(2)}, u32[]{:S(2)}) collective-permute-start(bf16[256,2048]{1,0:T(8,128)(2,1)} %pad_maximum_fusion.6.refs_6_.refs_0_), channel_id=1, source_target_pairs={{0,4},{4,0},{8,12},{12,8},{16,20},{20,16},{24,28},{28,24},{1,5},{5... | collective-permute-start | bytes 3145736 | tf_op jit(solution)/shard_map/ppermute | solution.py:520
  409.1 29.7 %collective-permute-start.63 = (bf16[2,256,2048]{2,1,0:T(8,128)(2,1)S(1)}, bf16[2,256,2048]{2,1,0:T(8,128)(2,1)S(1)}, u32[]{:S(2)}, u32[]{:S(2)}) collective-permute-start(bf16[2,256,2048]{2,1,0:T(8,128)(2,1)S(1)} %copy-done.55), channel_id=1, source_target_pairs={{0,1},{1,0},{2,3},{3,2},{4,5},{5,4},{6,7},{7,6},{8,9},{9,8},{10,11... | collective-permute-start | bytes 6291464 | tf_op jit(solution)/shard_map/ppermute | solution.py:509
  410.4 28.4 %collective-permute-start.62 = (bf16[256,2048]{1,0:T(8,128)(2,1)S(1)}, bf16[256,2048]{1,0:T(8,128)(2,1)S(1)}, u32[]{:S(2)}, u32[]{:S(2)}) collective-permute-start(bf16[256,2048]{1,0:T(8,128)(2,1)S(1)} %pad_maximum_fusion.7.refs_0_), channel_id=1, source_target_pairs={{0,4},{4,0},{8,12},{12,8},{16,20},{20,16},{24,28},{28,24},{1,5},{5... | collective-permute-start | bytes 3145736 | tf_op jit(solution)/shard_map/ppermute | solution.py:520
  411.9 26.1 %collective-permute-start.60 = (bf16[512,512]{1,0:T(8,128)(2,1)S(1)}, bf16[512,512]{1,0:T(8,128)(2,1)S(1)}, u32[]{:S(2)}, u32[]{:S(2)}) collective-permute-start(bf16[512,512]{1,0:T(8,128)(2,1)S(1)} %copy-done.62), channel_id=1, source_target_pairs={{0,16},{4,20},{8,24},{12,28},{16,0},{20,4},{24,8},{28,12},{1,17},{... | collective-permute-start | bytes 1572872 | tf_op jit(solution)/shard_map/ppermute | solution.py:520
  413.8 25.0 %collective-permute-start.61 = (bf16[128,2048]{1,0:T(8,128)(2,1)S(1)}, bf16[128,2048]{1,0:T(8,128)(2,1)S(1)}, u32[]{:S(2)}, u32[]{:S(2)}) collective-permute-start(bf16[128,2048]{1,0:T(8,128)(2,1)S(1)} %add_convert_fusion.6), channel_id=1, source_target_pairs={{0,8},{4,12},{8,0},{12,4},{16,24},{20,28},{24,16},{28,20},{1,9},{5... | collective-permute-start | bytes 1572872 | tf_op jit(solution)/shard_map/ppermute | solution.py:520
  414.2 23.8 %collective-permute-start.64 = (f32[12288]{0:T(1024)S(1)}, f32[12288]{0:T(1024)S(1)}, u32[]{:S(2)}, u32[]{:S(2)}) collective-permute-start(f32[12288]{0:T(1024)S(1)} %pad_maximum_fusion.19), channel_id=1, source_target_pairs={{0,1},{1,0},{2,3},{3,2},{4,5},{5,4},{6,7},{7,6},{8,9},{9,8},{10,11... | collective-permute-start | bytes 147464 | tf_op jit(solution)/shard_map/ppermute | solution.py:509
  439.9 26.0 %collective-permute-start.69 = (bf16[256,2048]{1,0:T(8,128)(2,1)S(1)}, bf16[256,2048]{1,0:T(8,128)(2,1)S(1)}, u32[]{:S(2)}, u32[]{:S(2)}) collective-permute-start(bf16[256,2048]{1,0:T(8,128)(2,1)S(1)} %fusion.32), channel_id=1, source_target_pairs={{0,2},{1,3},{2,0},{3,1},{4,6},{5,7},{6,4},{7,5},{8,10},{9,11},{10,... | collective-permute-start | bytes 3145736 | tf_op jit(solution)/shard_map/ppermute | solution.py:517
  441.3 24.6 %collective-permute-start.68 = (bf16[256,2048]{1,0:T(8,128)(2,1)S(1)}, bf16[256,2048]{1,0:T(8,128)(2,1)S(1)}, u32[]{:S(2)}, u32[]{:S(2)}) collective-permute-start(bf16[256,2048]{1,0:T(8,128)(2,1)S(1)} %pad_maximum_fusion.8.refs_0_), channel_id=1, source_target_pairs={{0,4},{4,0},{8,12},{12,8},{16,20},{20,16},{24,28},{28,24},{1,5},{5... | collective-permute-start | bytes 3145736 | tf_op jit(solution)/shard_map/ppermute | solution.py:520
  442.0 23.3 %collective-permute-start.66 = (bf16[512,512]{1,0:T(8,128)(2,1)S(1)}, bf16[512,512]{1,0:T(8,128)(2,1)S(1)}, u32[]{:S(2)}, u32[]{:S(2)}) collective-permute-start(bf16[512,512]{1,0:T(8,128)(2,1)S(1)} %copy-done.61), channel_id=1, source_target_pairs={{0,16},{4,20},{8,24},{12,28},{16,0},{20,4},{24,8},{28,12},{1,17},{... | collective-permute-start | bytes 1572872 | tf_op jit(solution)/shard_map/ppermute | solution.py:520
  442.1 23.8 %collective-permute-start.67 = (bf16[512,512]{1,0:T(8,128)(2,1)S(1)}, bf16[512,512]{1,0:T(8,128)(2,1)S(1)}, u32[]{:S(2)}, u32[]{:S(2)}) collective-permute-start(bf16[512,512]{1,0:T(8,128)(2,1)S(1)} %add_convert_fusion.5.refs_0_), channel_id=1, source_target_pairs={{0,8},{4,12},{8,0},{12,4},{16,24},{20,28},{24,16},{28,20},{1,9},{5... | collective-permute-start | bytes 1572872 | tf_op jit(solution)/shard_map/ppermute | solution.py:520
  468.4 28.0 %collective-permute-start.71 = (bf16[1024,512]{1,0:T(8,128)(2,1)S(1)}, bf16[1024,512]{1,0:T(8,128)(2,1)S(1)}, u32[]{:S(2)}, u32[]{:S(2)}) collective-permute-start(bf16[1024,512]{1,0:T(8,128)(2,1)S(1)} %get-tuple-element.322.refs_0_), channel_id=1, source_target_pairs={{0,4},{4,0},{8,12},{12,8},{16,20},{20,16},{24,28},{28,24},{1,5},{5... | collective-permute-start | bytes 3145736 | tf_op jit(solution)/shard_map/ppermute | solution.py:520
  469.9 26.5 %collective-permute-start.65 = (bf16[512,512]{1,0:T(8,128)(2,1)S(1)}, bf16[512,512]{1,0:T(8,128)(2,1)S(1)}, u32[]{:S(2)}, u32[]{:S(2)}) collective-permute-start(bf16[512,512]{1,0:T(8,128)(2,1)S(1)} %copy-done.60), channel_id=1, source_target_pairs={{0,16},{4,20},{8,24},{12,28},{16,0},{20,4},{24,8},{28,12},{1,17},{... | collective-permute-start | bytes 1572872 | tf_op jit(solution)/shard_map/ppermute | solution.py:520
  470.1 26.3 %collective-permute-start.70 = (bf16[512,512]{1,0:T(8,128)(2,1)S(1)}, bf16[512,512]{1,0:T(8,128)(2,1)S(1)}, u32[]{:S(2)}, u32[]{:S(2)}) collective-permute-start(bf16[512,512]{1,0:T(8,128)(2,1)S(1)} %add_convert_fusion.4), channel_id=1, source_target_pairs={{0,8},{4,12},{8,0},{12,4},{16,24},{20,28},{24,16},{28,20},{1,9},{5... | collective-permute-start | bytes 1572872 | tf_op jit(solution)/shard_map/ppermute | solution.py:520
  496.4 26.6 %collective-permute-start.75 = (bf16[1024,512]{1,0:T(8,128)(2,1)S(1)}, bf16[1024,512]{1,0:T(8,128)(2,1)S(1)}, u32[]{:S(2)}, u32[]{:S(2)}) collective-permute-start(bf16[1024,512]{1,0:T(8,128)(2,1)S(1)} %pad_maximum_fusion.9.refs_0_), channel_id=1, source_target_pairs={{0,4},{4,0},{8,12},{12,8},{16,20},{20,16},{24,28},{28,24},{1,5},{5... | collective-permute-start | bytes 3145736 | tf_op jit(solution)/shard_map/ppermute | solution.py:520
  497.1 25.3 %collective-permute-start.73 = (bf16[512,512]{1,0:T(8,128)(2,1)S(1)}, bf16[512,512]{1,0:T(8,128)(2,1)S(1)}, u32[]{:S(2)}, u32[]{:S(2)}) collective-permute-start(bf16[512,512]{1,0:T(8,128)(2,1)S(1)} %copy-done.59), channel_id=1, source_target_pairs={{0,16},{4,20},{8,24},{12,28},{16,0},{20,4},{24,8},{28,12},{1,17},{... | collective-permute-start | bytes 1572872 | tf_op jit(solution)/shard_map/ppermute | solution.py:520
  497.2 25.8 %collective-permute-start.74 = (bf16[512,512]{1,0:T(8,128)(2,1)S(1)}, bf16[512,512]{1,0:T(8,128)(2,1)S(1)}, u32[]{:S(2)}, u32[]{:S(2)}) collective-permute-start(bf16[512,512]{1,0:T(8,128)(2,1)S(1)} %add_convert_fusion.3), channel_id=1, source_target_pairs={{0,8},{4,12},{8,0},{12,4},{16,24},{20,28},{24,16},{28,20},{1,9},{5... | collective-permute-start | bytes 1572872 | tf_op jit(solution)/shard_map/ppermute | solution.py:520
  501.1 21.9 %collective-permute-start.76 = (f32[15872]{0:T(1024)S(1)}, f32[15872]{0:T(1024)S(1)}, u32[]{:S(2)}, u32[]{:S(2)}) collective-permute-start(f32[15872]{0:T(1024)S(1)} %pad_maximum_fusion.18), channel_id=1, source_target_pairs={{0,4},{4,0},{8,12},{12,8},{16,20},{20,16},{24,28},{28,24},{1,5},{5... | collective-permute-start | bytes 190472 | tf_op jit(solution)/shard_map/ppermute | solution.py:520
  523.1 24.4 %collective-permute-start.79 = (bf16[1024,512]{1,0:T(8,128)(2,1)S(1)}, bf16[1024,512]{1,0:T(8,128)(2,1)S(1)}, u32[]{:S(2)}, u32[]{:S(2)}) collective-permute-start(bf16[1024,512]{1,0:T(8,128)(2,1)S(1)} %pad_maximum_fusion.10.refs_0_), channel_id=1, source_target_pairs={{0,4},{4,0},{8,12},{12,8},{16,20},{20,16},{24,28},{28,24},{1,5},{5... | collective-permute-start | bytes 3145736 | tf_op jit(solution)/shard_map/ppermute | solution.py:520
  524.4 23.0 %collective-permute-start.78 = (bf16[512,512]{1,0:T(8,128)(2,1)S(1)}, bf16[512,512]{1,0:T(8,128)(2,1)S(1)}, u32[]{:S(2)}, u32[]{:S(2)}) collective-permute-start(bf16[512,512]{1,0:T(8,128)(2,1)S(1)} %add_convert_fusion.2), channel_id=1, source_target_pairs={{0,8},{4,12},{8,0},{12,4},{16,24},{20,28},{24,16},{28,20},{1,9},{5... | collective-permute-start | bytes 1572872 | tf_op jit(solution)/shard_map/ppermute | solution.py:520
  524.5 20.1 %collective-permute-start.77 = (bf16[512,384]{1,0:T(8,128)(2,1)S(1)}, bf16[512,384]{1,0:T(8,128)(2,1)S(1)}, u32[]{:S(2)}, u32[]{:S(2)}) collective-permute-start(bf16[512,384]{1,0:T(8,128)(2,1)S(1)} %get-tuple-element.335), channel_id=1, source_target_pairs={{0,16},{4,20},{8,24},{12,28},{16,0},{20,4},{24,8},{28,12},{1,17},{... | collective-permute-start | bytes 1179656 | tf_op jit(solution)/shard_map/ppermute | solution.py:520
  526.9 20.5 %collective-permute-start.80 = (f32[15872]{0:T(1024)S(1)}, f32[15872]{0:T(1024)S(1)}, u32[]{:S(2)}, u32[]{:S(2)}) collective-permute-start(f32[15872]{0:T(1024)S(1)} %fusion.44), channel_id=1, source_target_pairs={{0,8},{4,12},{8,0},{12,4},{16,24},{20,28},{24,16},{28,20},{1,9},{5... | collective-permute-start | bytes 190472 | tf_op jit(solution)/shard_map/ppermute | solution.py:520
  547.6 24.0 %collective-permute-start.83 = (bf16[1024,512]{1,0:T(8,128)(2,1)S(1)}, bf16[1024,512]{1,0:T(8,128)(2,1)S(1)}, u32[]{:S(2)}, u32[]{:S(2)}) collective-permute-start(bf16[1024,512]{1,0:T(8,128)(2,1)S(1)} %pad_maximum_fusion.11.refs_0_), channel_id=1, source_target_pairs={{0,4},{4,0},{8,12},{12,8},{16,20},{20,16},{24,28},{28,24},{1,5},{5... | collective-permute-start | bytes 3145736 | tf_op jit(solution)/shard_map/ppermute | solution.py:520
  549.7 20.4 %collective-permute-start.82 = (bf16[512,384]{1,0:T(8,128)(2,1)S(1)}, bf16[512,384]{1,0:T(8,128)(2,1)S(1)}, u32[]{:S(2)}, u32[]{:S(2)}) collective-permute-start(bf16[512,384]{1,0:T(8,128)(2,1)S(1)} %add_convert_fusion.13), channel_id=1, source_target_pairs={{0,8},{4,12},{8,0},{12,4},{16,24},{20,28},{24,16},{28,20},{1,9},{5... | collective-permute-start | bytes 1179656 | tf_op jit(solution)/shard_map/ppermute | solution.py:520
  571.7 20.2 %collective-permute-start.88 = (bf16[1024,384]{1,0:T(8,128)(2,1)S(1)}, bf16[1024,384]{1,0:T(8,128)(2,1)S(1)}, u32[]{:S(2)}, u32[]{:S(2)}) collective-permute-start(bf16[1024,384]{1,0:T(8,128)(2,1)S(1)} %pad_maximum_fusion.12.refs_0_), channel_id=1, source_target_pairs={{0,4},{4,0},{8,12},{12,8},{16,20},{20,16},{24,28},{28,24},{1,5},{5... | collective-permute-start | bytes 2359304 | tf_op jit(solution)/shard_map/ppermute | solution.py:520
  592.0 19.1 %collective-permute-start.90 = (bf16[1024,384]{1,0:T(8,128)(2,1)S(1)}, bf16[1024,384]{1,0:T(8,128)(2,1)S(1)}, u32[]{:S(2)}, u32[]{:S(2)}) collective-permute-start(bf16[1024,384]{1,0:T(8,128)(2,1)S(1)} %pad_maximum_fusion.13.refs_0_), channel_id=1, source_target_pairs={{0,4},{4,0},{8,12},{12,8},{16,20},{20,16},{24,28},{28,24},{1,5},{5... | collective-permute-start | bytes 2359304 | tf_op jit(solution)/shard_map/ppermute | solution.py:520
  (126 other events, 1892.1 us)

commit v12 on v10

--- a/solution.py
+++ b/solution.py
@@ -59,56 +59,54 @@
     return jnp.concatenate([moved, block[:, 128:]], axis=1)
 
 
-def qkv_kernel(x_ref, w_ref, b_ref, keep_ref, up_ref, down_ref, *refs):
-    o_ref = refs[-1]
+def qkv_kernel(own_ref, rest_ref, w_ref, b_ref, keep_ref, up_ref, down_ref, o_ref):
     kind = pl.program_id(0) % 3
-    rows = x_ref.shape[0]
-    tile = min(rows, 512)
-
-    def project(at):
-        return (
-            jnp.dot(x_ref[at, :], w_ref[...], preferred_element_type=F32)
-            + b_ref[...].astype(F32)
-        )
-
-    for start in range(0, rows, tile):
-        at = pl.ds(start, min(tile, rows - start))
-
-        @pl.when(kind == 2)
-        def _(at=at):
-            o_ref[at, :] = project(at).astype(BF)
-
-        @pl.when(kind != 2)
-        def _(at=at):
-            o_ref[at, :] = turned(
-                project(at), keep_ref[at, :], up_ref[at, :], down_ref[at, :], 1.0
-            ).astype(BF)
-
-
-def project_qkv(normed, weight, bias, table, length, whole=None):
-    rows, width = normed.shape
+    row = 0
+    for x_ref in (own_ref, rest_ref):
+        rows = x_ref.shape[0]
+        tile = min(rows, 512)
+        for start in range(0, rows, tile):
+            here = pl.ds(start, min(tile, rows - start))
+            at = pl.ds(row + start, min(tile, rows - start))
+
+            def project(x_ref=x_ref, here=here):
+                return (
+                    jnp.dot(x_ref[here, :], w_ref[...], preferred_element_type=F32)
+                    + b_ref[...].astype(F32)
+                )
+
+            @pl.when(kind == 2)
+            def _(at=at, project=project):
+                o_ref[at, :] = project().astype(BF)
+
+            @pl.when(kind != 2)
+            def _(at=at, project=project):
+                o_ref[at, :] = turned(
+                    project(), keep_ref[at, :], up_ref[at, :], down_ref[at, :], 1.0
+                ).astype(BF)
+
+        row += rows
+
+
+def project_qkv(own, rest, weight, bias, table):
+    length, width = own.shape[0] + rest.shape[0], own.shape[1]
     columns = weight.shape[1]
-    part = 0 if whole is None else 1
-    if part and rows * 2 != length:
-        rest = project_qkv(normed, weight, bias, table[length - rows :], rows)
-        return jnp.concatenate([whole[: length - rows], rest], axis=0)
     return pl.pallas_call(
         qkv_kernel,
         grid=(columns // HD,),
         in_specs=[
-            pl.BlockSpec((rows, width), lambda j: (0, 0)),
+            pl.BlockSpec(own.shape, lambda j: (0, 0)),
+            pl.BlockSpec(rest.shape, lambda j: (0, 0)),
             pl.BlockSpec((width, HD), lambda j: (0, j)),
             pl.BlockSpec((1, HD), lambda j: (0, j)),
         ]
-        + [pl.BlockSpec((rows, 128), lambda j, k=k: (part, k)) for k in range(3)]
-        + [pl.BlockSpec(memory_space=pl.ANY)] * part,
-        out_specs=pl.BlockSpec((rows, HD), lambda j: (part, j)),
+        + [pl.BlockSpec((length, 128), lambda j, k=k: (0, k)) for k in range(3)],
+        out_specs=pl.BlockSpec((length, HD), lambda j: (0, j)),
         out_shape=jax.ShapeDtypeStruct((length, columns), BF),
-        input_output_aliases={6: 0} if part else {},
         compiler_params=pltpu.CompilerParams(vmem_limit_bytes=40 << 20),
         cost_estimate=SMALL,
         name="qkv_rotary",
-    )(normed, weight, bias[None, :], table, table, table, *([whole] if part else []))
+    )(own, rest, weight, bias[None, :], table, table, table)
 
 
 def visible_scores(queries, keys, row_spots, key_spots, prefix):
@@ -228,7 +226,7 @@
 
 
 def norm_back_kernel(
-    count, grad_qkv_ref, grad_inner_ref, qkv_ref, fc1_ref, gain_a_ref, gain_m_ref, *refs
+    count, grad_qkv_ref, grad_inner_ref, qkv_ref, fc1_ref, gains_ref, *refs
 ):
     blocks, (o_ref, sums_ref, qkv_sum_ref, inner_sum_ref, rows_ref) = refs[:count], refs[count:]
     step = pl.program_id(0)
@@ -244,7 +242,8 @@
     xhat = centered * inverse
     grad_attn = contract(grad_qkv_ref[...], qkv_ref[...], 1, 1)
     grad_mlp = contract(grad_inner_ref[...], fc1_ref[...], 1, 1)
-    gained = grad_attn * gain_a_ref[...].astype(F32) + grad_mlp * gain_m_ref[...].astype(F32)
+    gain_a, gain_m = gains_ref[0:1, :].astype(F32), gains_ref[2:3, :].astype(F32)
+    gained = grad_attn * gain_a + grad_mlp * gain_m
     o_ref[...] = inverse * (
         gained
         - jnp.mean(gained, axis=-1, keepdims=True)
@@ -280,7 +279,7 @@
         functools.partial(norm_back_kernel, count),
         grid=(count,),
         in_specs=[each(grad_qkv), each(grad_inner), full(qkv_weight), full(fc1_weight)]
-        + [full(gains[0]), full(gains[2])]
+        + [full(gains)]
         + [full(b) for b in blocks],
         out_specs=[pl.BlockSpec((rows, width), lambda i: (i, 0))]
         + [pl.BlockSpec(shape, lambda i: (0, 0)) for shape in sums],
@@ -290,7 +289,7 @@
         compiler_params=pltpu.CompilerParams(vmem_limit_bytes=56 << 20),
         cost_estimate=SMALL,
         name="norm_back",
-    )(grad_qkv, grad_inner, qkv_weight, fc1_weight, gains[0], gains[2], *blocks)
+    )(grad_qkv, grad_inner, qkv_weight, fc1_weight, gains, *blocks)
 
 
 def place_kernel(quarter_ref, *refs):
@@ -329,7 +328,7 @@
 
 
 def norms_kernel(count, *refs):
-    gains, blocks, (attn_ref, mlp_ref) = refs[:4], refs[4 : 4 + count], refs[-2:]
+    gains_ref, blocks, (attn_ref, mlp_ref) = refs[0], refs[1 : 1 + count], refs[-2:]
     for index, block in enumerate(blocks):
 
         @pl.when(pl.program_id(0) == index)
@@ -339,7 +338,9 @@
             centered = features - average
             spread = jnp.mean(centered * centered, axis=-1, keepdims=True)
             xhat = centered * lax.rsqrt(spread + EPSILON)
-            gain_a, shift_a, gain_m, shift_m = (ref[...].astype(F32) for ref in gains)
+            gain_a, shift_a, gain_m, shift_m = (
+                gains_ref[i : i + 1, :].astype(F32) for i in range(4)
+            )
             attn_ref[...] = (xhat * gain_a + shift_a).astype(BF)
             mlp_ref[...] = (xhat * gain_m + shift_m).astype(BF)
 
@@ -353,16 +354,16 @@
     return pl.pallas_call(
         functools.partial(norms_kernel, count),
         grid=(count,),
-        in_specs=[pl.BlockSpec((1, width), lambda i: (0, 0))] * 4
+        in_specs=[pl.BlockSpec(gains.shape, lambda i: (0, 0))]
         + [pl.BlockSpec((rows, width), lambda i: (0, 0))] * count
         + [pl.BlockSpec(memory_space=pl.ANY)] * len(into),
         out_specs=[pl.BlockSpec((rows, width), lambda i: (i + skip, 0))] * 2,
         out_shape=[shape, shape],
-        input_output_aliases={4 + count: 0, 5 + count: 1} if into else {},
+        input_output_aliases={1 + count: 0, 2 + count: 1} if into else {},
         compiler_params=pltpu.CompilerParams(vmem_limit_bytes=48 << 20),
         cost_estimate=SMALL,
         name="both_norms",
-    )(*gains, *blocks, *into)
+    )(gains, *blocks, *into)
 
 
 def outer_kernel(lefts, pieces, outs, _, *refs):
@@ -531,7 +532,7 @@
     shift_attn = ln1_bias.astype(F32)
     gain_mlp = ln2_gain.astype(F32)
     shift_mlp = ln2_bias.astype(F32)
-    gains = [v[None, :] for v in (ln1_gain, ln1_bias, ln2_gain, ln2_bias)]
+    gains = jnp.stack([ln1_gain, ln1_bias, ln2_gain, ln2_bias])
     close = 2 * rows
 
     def units(normed):
@@ -540,12 +541,11 @@
     near_blocks, hidden_y = gather_near(hidden)
     first = first_far(hidden)
     norm_attn_own, norm_mlp_own = both_norms(near_blocks[:2], gains)
-    mask_f = after(valid_mask, norm_mlp_own).astype(F32)
-    count = jnp.full((8, 128), jnp.sum(mask_f), F32)
-    count = count + to_core(count)
-    counted = flip(count, 1)
     pre_own = units(norm_mlp_own)
     active_own = exact_gelu(pre_own)[0].astype(BF)
+    mask_f = after(valid_mask, active_own).astype(F32)
+    count = jnp.full((8, 128), jnp.sum(mask_f), F32)
+    counted = to_core(count)
     table = jnp.concatenate(
         [
             lax.dynamic_slice_in_dim(jnp.asarray(rotary_table(LEN)), b * rows, rows, 0)
@@ -554,10 +554,8 @@
         axis=0,
     )
     spots = jnp.concatenate([b * rows + jnp.arange(rows, dtype=jnp.int32) for b in block_ids])
-    active_own, table = after(active_own, table), after(table, active_own)
-    qkv_own = project_qkv(norm_attn_own, qkv_weight, qkv_bias, table, LEN)
-    active_own, qkv_own, counted, first, hidden_y = meet(
-        active_own, qkv_own, counted, first, hidden_y
+    active_own, table, spots, counted, first, hidden_y, norm_attn_own = meet(
+        active_own, table, spots, counted, first, hidden_y, norm_attn_own
     )
     count = count + counted
 
@@ -565,17 +563,16 @@
     for block in hidden_y:
         near_blocks += [block, to_core(block)]
     second = second_far(first, hidden_y)
-    first_mates = [to_core(block) for block in first]
-    counted = flip(count, 2)
+    counted = flip(count, 1)
     norm_attn_rest, norm_mlp_rest = both_norms(near_blocks[2:], gains)
-    qkv_low = project_qkv(norm_attn_rest, qkv_weight, qkv_bias, table, LEN, qkv_own)
+    qkv_low = project_qkv(norm_attn_own, norm_attn_rest, qkv_weight, qkv_bias, table)
     context, log_total = attend(qkv_low, prefix_len, spots)
     norm_mlp_rest = after(norm_mlp_rest, context)
     context_far = swap_quarters(context)
     pre_rest = units(norm_mlp_rest)
     active_rest = exact_gelu(pre_rest)[0].astype(BF)
-    active_rest, context, counted, second, context_far, first_mates = meet(
-        active_rest, context, counted, second, context_far, first_mates
+    active_rest, context, counted, second, context_far = meet(
+        active_rest, context, counted, second, context_far
     )
     count = count + counted
 
@@ -589,7 +586,9 @@
         return blocks[:, 0] + to_core(blocks[:, 1].astype(BF)).astype(F32)
 
     corner, beside, across = second
+    first_mates = [to_core(block) for block in first]
     second_mates = [to_core(block) for block in [corner] + beside + across]
+    count = count + flip(count, 2)
     counted = jnp.zeros_like(count)
     bit = 2
     while bit < tp:
@@ -600,8 +599,8 @@
     part_rest = branch_rows(context[close:], active_rest).reshape(-1, 2, rows, D)
     mates_rest = to_core(part_rest[:, 1].astype(BF))
     part_own = branch_rows(context[:close], after(active_own, part_rest)).reshape(2, rows, D)
-    part_own, mates_rest, counted, second_mates = meet(
-        part_own, mates_rest, counted, second_mates
+    part_own, mates_rest, counted, first_mates, second_mates = meet(
+        part_own, mates_rest, counted, first_mates, second_mates
     )
     count = count + counted
 
@@ -609,7 +608,7 @@
     came = [to_y(sums[step - 1].astype(BF), step) for step in range(1, ways)]
     mates_own = to_core(part_own[1].astype(BF))
     counted = flip(count, 4) if dp > 4 else jnp.zeros_like(count)
-    last = last_far(second)
+    last = [flip(block, 1) for block in across]
     ahead = [first[0]] + beside + [first[1]] + across + [corner]
     mates = (
         [first_mates[0]]
@@ -631,15 +630,14 @@
         branch = branch + got.astype(F32)
     output_f = hidden.astype(F32) + branch + out_bias.astype(F32) + fc2_bias.astype(F32)
     mismatch = output_f - teacher.astype(F32)
-    error_part = jnp.sum(mask_f[:, None] * mismatch * mismatch)
-    grad_out = mask_f[:, None] * mismatch * (2.0 * total_tokens / count[0, 0])
+    scale = 2.0 * total_tokens / count[0, 0]
+    grad_out = mask_f[:, None] * mismatch * scale
     grad_low = grad_out.astype(BF)
     grad_out, grad_low, last = meet(grad_out, grad_low, last)
 
     grad_y = [from_y(grad_low, step) for step in range(1, ways)]
     grad_first = first_far(grad_low)
     grad_mate = to_core(grad_low)
-    last = [jnp.concatenate([after(v, grad_mate), u], axis=0) for v, u in last]
     far_blocks = [block for v in last for block in (v, to_core(v))]
     norm_attn_far, norm_mlp_far = both_norms(far_blocks, gains, 6 * ways, norms_far)
     fc1_quarter = quarter_of(fc1_weight, 1, quarter)
@@ -659,22 +657,20 @@
     for block in grad_y:
         grad_blocks += [block, to_core(block)]
     grad_near = jnp.concatenate(grad_blocks, axis=0)
-    hidden_pre = jnp.concatenate([pre_own, pre_rest], axis=0)
-    grad_inner = (contract(grad_near, fc2_weight, 1, 1) * exact_gelu(hidden_pre)[1]).astype(BF)
     grad_context = contract(grad_near, out_weight, 1, 1).astype(BF)
-    grad_inner, grad_context, grad_near, grad_second = meet(
-        grad_inner, grad_context, grad_near, grad_second
-    )
+    grad_qkv = attend_back(qkv_low, grad_context, log_total, prefix_len, spots, table)
+    grad_qkv, grad_near, grad_second = meet(grad_qkv, grad_near, grad_second)
 
     grad_last = last_far(grad_second)
     corner, beside, across = grad_second
     ahead = [grad_first[0]] + beside + [grad_first[1]] + across + [corner]
     mates = [to_core(block) for block in ahead]
-    grad_qkv = attend_back(qkv_low, grad_context, log_total, prefix_len, spots, table)
-    grad_qkv, grad_last, mates = meet(grad_qkv, grad_last, mates)
+    swapped = [flip(quarter_of(grad_qkv, 1, quarter ^ m), m) for m in (1, 2)]
+    hidden_pre = jnp.concatenate([pre_own, pre_rest], axis=0)
+    grad_inner = (contract(grad_near, fc2_weight, 1, 1) * exact_gelu(hidden_pre)[1]).astype(BF)
+    grad_inner, grad_last, mates = meet(grad_inner, grad_last, mates)
 
     last_mates = [tuple(to_core(v) for v in pair) for pair in grad_last]
-    swapped = [flip(quarter_of(grad_qkv, 1, quarter ^ m), m) for m in (1, 2)]
     grad_far = [block for pair in zip(ahead, mates) for block in pair]
     halves = [v for pair, mate in zip(grad_last, last_mates) for v in pair + mate]
 
@@ -832,7 +828,9 @@
     grad_hidden, sums = turn(grad_hidden, sums)
     blocks = grad_hidden.reshape(ways, 2, rows, D)
     kept, mates = blocks[:, 0], blocks[:, 1].astype(BF)
-    bias_part = jnp.sum(gate(grad_out), axis=0)
+    grad_later = gate(grad_out)
+    bias_part = jnp.sum(grad_later, axis=0)
+    error_part = jnp.sum(grad_later * grad_later) / (scale * scale)
     tensor_parts = jnp.concatenate(
         [sums[:4].reshape(-1), bias_part, jnp.full((D,), error_part, F32)]
     )

time: 651 us -> 643 us (0.988)
  local copies, waits for them, and re-layouts: 46.4 us -> 33.5 us
    ppermute x69 -> x68, waiting for transfers between devices: 197 us -> 207 us  [flip(): return lax.ppermute(v, 'dp', [(d, d ^ mask) for d in range(dp)])]
    ppermute x4, waiting for transfers between devices: 10.6 us -> 1.3 us  [from_y(): return lax.ppermute(v, 'tensor', pairs)]
    unnamed x173 -> x140, local copies, waits for them, and re-layouts: 17.2 us -> 11.1 us
    ppermute x69 -> x68, starting transfers between devices: 76.8 us -> 76.6 us  [flip(): return lax.ppermute(v, 'dp', [(d, d ^ mask) for d in range(dp)])]
  transfers between devices with their start and end apart: 99 -> 98, of which waited for: 38 -> 36; matrix products, arithmetic and copies ran while one was open for 21% -> 22% of each run, Pallas kernels for 26% -> 26%
where the time goes in v12:
time: 643 us; the launch traced here: 634 us
  waiting for transfers between devices  211 us (33%)
  Pallas kernels  169 us (26%)
  matrix products  94.4 us (15%)
  starting transfers between devices  89.1 us (14%)
  local copies, waits for them, and re-layouts  33.5 us (5%)
  other arithmetic  29.3 us (5%)
  between operations  6.85 us (1%)
    ppermute x68, waiting for transfers between devices, flip(): return lax.ppermute(v, 'dp', [(d, d ^ mask) for d in range(dp)])  207 us
    ppermute x68, starting transfers between devices, flip(): return lax.ppermute(v, 'dp', [(d, d ^ mask) for d in range(dp)])  76.6 us
    dot_general x8, matrix products, contract(): lax.dot_general(left_side, right_side, (((left_dim,), (right_dim,)), ((),...  46.1 us
    pallas_call x15, Pallas kernels, place_quarters(): pl.pallas_call(place_kernel, grid_spec=pltpu.PrefetchScalarGridSpec(num_s...  34.7 us
    pallas_call x1, Pallas kernels, norm_back(): pl.pallas_call(functools.partial(norm_back_kernel, count), grid=(count,),...  31.2 us
    pallas_call x4, Pallas kernels, both_norms(): pl.pallas_call(functools.partial(norms_kernel, count), grid=(count,), in_...  29.8 us
    pallas_call x2, Pallas kernels, outer_blocks(): pl.pallas_call(functools.partial(outer_kernel, len(lefts), pieces, len(si...  23.5 us
    dot_general x2, matrix products, units(): jnp.dot(normed, fc1_weight, preferred_element_type=F32)  21.3 us
  transfers between devices with their start and end apart: 98, of which 36 were waited for; matrix products, arithmetic and copies ran while one was open for 22% of the time, Pallas kernels for 26%

profile of v12, /device:TPU:0, one launch (start us, length us, event | category | flops | bytes accessed | tf_op | source)
XLA Modules:
  0.0 633.9 jit_solution(11219886738066002729)
XLA Ops:
  1.2 2.6 collective-permute-start.2
  13.1 4.4 both_norms.4
  17.5 10.4 %multiply_convert_fusion.2 = (bf16[512,2048]{1,0:T(8,128)(2,1)}, f32[512,2048]{1,0:T(8,128)}) fusion(f32[2048]{0:T(1024)S(1)} %convert_element_type.230, bf16[512,2048]{1,0:T(8,128)(2,1)} %get-tuple-element.193, bf16[2048,2048]{1,0:T(8,128)(2,1)} %fc1_ref.1), kind=kOutput, calls=%fused_computation.20 | convolution fusion | flops 4301258752 | bytes 16785408 | tf_op jit(solution)/shard_map/dot_general | solution.py:539
  37.1 4.6 both_norms.5
  45.5 10.9 %qkv_rotary.1.q_ref.k_ref.v_ref = bf16[1024,1536]{1,0:T(8,128)(2,1)S(1)} custom-call(bf16[512,2048]{1,0:T(8,128)(2,1)S(1)} %copy-done.6, bf16[512,2048]{1,0:T(8,128)(2,1)S(1)} %get-tuple-element.199.rest_ref, bf16[2048,1536]{1,0:T(8,128)(2,1)} %qkv_ref.1, bf16[1,1536]{1,0:T(2,128)(2,1)S(1)} %broadcast_in_dim.11.b_ref, f32[1024,384]{1,0:T(8,128)S(1)} %copy-done.3, ...), custom_call_target="tpu_custom_call" | custom-call | flops 1048576 | bytes 65536 | tf_op jit(solution)/shard_map/qkv_rotary/pallas_call | solution.py:94
  56.4 9.6 %attend.1 = (bf16[1024,512]{1,0:T(8,128)(2,1)S(1)}, f32[2,1024,1]{2,1,0:T(8,128)S(1)}) custom-call(s32[1]{0:T(128)S(6)} %copy.80.prefix_ref, bf16[1024,1536]{1,0:T(8,128)(2,1)S(1)} %qkv_rotary.1.q_ref.k_ref.v_ref, bf16[1024,1536]{1,0:T(8,128)(2,1)S(1)} %qkv_rotary.1.q_ref.k_ref.v_ref, bf16[1024,1536]{1,0:T(8,128)(2,1)S(1)} %qkv_rotary.1.q_ref.k_ref.v_ref, ...), custom_call_target="tpu_custom_call" | custom-call | flops 1048576 | bytes 65536 | tf_op jit(solution)/shard_map/attend/pallas_call | solution.py:137
  69.8 10.9 %multiply_convert_fusion.1 = (bf16[512,2048]{1,0:T(8,128)(2,1)S(1)}, f32[512,2048]{1,0:T(8,128)}) fusion(f32[2048]{0:T(1024)S(1)} %convert_element_type.230, bf16[512,2048]{1,0:T(8,128)(2,1)S(1)} %copy-done.34, bf16[2048,2048]{1,0:T(8,128)(2,1)} %fc1_ref.1), kind=kOutput, calls=%fused_computation.19 | convolution fusion | flops 4301258752 | bytes 16785408 | tf_op jit(solution)/shard_map/dot_general | solution.py:539
  83.1 4.6 fusion.54
  90.4 4.6 fusion.55
  101.7 2.7 collective-permute-start.23
  104.4 16.2 %both_norms.6 = (bf16[3072,2048]{1,0:T(8,128)(2,1)}, bf16[3072,2048]{1,0:T(8,128)(2,1)}) custom-call(bf16[4,2048]{1,0:T(4,128)(2,1)S(1)} %pad_maximum_fusion.21.refs_0_.gains_ref, bf16[256,2048]{1,0:T(8,128)(2,1)} %collective-permute-done.2.refs_1_, bf16[256,2048]{1,0:T(8,128)(2,1)S(1)} %collective-permute-done.16.refs_2_, ...), custom_call_target="tpu_custom_call" | custom-call | flops 1048576 | bytes 65536 | tf_op jit(solution)/shard_map/both_norms/pallas_call | solution.py:354
  120.5 2.4 collective-permute-done.24.refs_1_
  126.0 4.8 fusion.49
  134.6 4.7 both_norms.7
  139.3 14.7 %fusion.9 = (f32[3072,512]{1,0:T(8,128)}, bf16[3072,512]{1,0:T(8,128)(2,1)}) fusion(f32[512]{0:T(512)S(1)} %dynamic-slice_convert_fusion, bf16[3072,2048]{1,0:T(8,128)(2,1)} %get-tuple-element.233, bf16[2048,2048]{1,0:T(8,128)(2,1)} %fc1_ref.1, s32[]{:T(128)S(6)} %select_n.81), kind=kOutput, calls=%fused_computation.12 | convolution fusion | flops 6459752448 | bytes 24119300 | tf_op jit(solution)/shard_map/dot_general | solution.py:646
  155.7 3.2 constant_dynamic-slice_fusion.6.weight_ref
  164.5 2.4 convolution_convert_fusion.g_ref
  167.9 11.9 %attend_back.1.grad_qkv_ref = bf16[1024,1536]{1,0:T(8,128)(2,1)} custom-call(s32[1]{0:T(128)S(6)} %copy.80.prefix_ref, bf16[1024,1536]{1,0:T(8,128)(2,1)} %copy-done.2, bf16[1024,1536]{1,0:T(8,128)(2,1)} %copy-done.2, bf16[1024,1536]{1,0:T(8,128)(2,1)} %copy-done.2, bf16[1024,512]{1,0:T(8,128)(2,1)S(1)} %convolution_convert_fusion.g_ref, ...), custom_call_target="tpu_custom_call" | custom-call | flops 1048576 | bytes 65536 | tf_op jit(solution)/shard_map/attend_back/pallas_call | solution.py:203
  179.8 7.4 %collective-permute-done.31.refs_12_.refs_16_.refs_8_ = bf16[256,2048]{1,0:T(8,128)(2,1)} collective-permute-done((bf16[256,2048]{1,0:T(8,128)(2,1)S(1)}, bf16[256,2048]{1,0:T(8,128)(2,1)}, u32[]{:S(2)}, u32[]{:S(2)}) %collective-permute-start.31) | collective-permute-done | bytes 1048608 | tf_op jit(solution)/shard_map/ppermute | solution.py:492
  190.1 16.2 %fusion.5.grad_inner_ref = bf16[1024,2048]{1,0:T(8,128)(2,1)} fusion(f32[512,2048]{1,0:T(8,128)} %get-tuple-element.406, f32[512,2048]{1,0:T(8,128)} %get-tuple-element.404, bf16[1024,2048]{1,0:T(8,128)(2,1)S(1)} %constant_dynamic-update-slice_fusion.refs_3_.refs_7_, bf16[2048,2048]{1,0:T(8,128)(2,1)} %param.34), kind=kOutput, calls=%fused_computation.7 | convolution fusion | flops 8613003264 | bytes 25165824 | tf_op jit(solution)/shard_map/dot_general | solution.py:35
  210.4 11.0 %outer_blocks.2 = (bf16[128,2048]{1,0:T(8,128)(2,1)}, bf16[128,2048]{1,0:T(8,128)(2,1)}) custom-call(s32[1]{0:T(128)} %bitcast.9._.quarter_ref, bf16[512,2048]{1,0:T(8,128)(2,1)} %get-tuple-element.210.refs_0_, bf16[512,2048]{1,0:T(8,128)(2,1)} %copy-done.31, bf16[3072,512]{1,0:T(8,128)(2,1)} %get-tuple-element.236.refs_2_, bf16[1024,2048]{1,0:T(8,128)(2,1)} %copy-done.22, ...), custom_call_target="tpu_custom_call" | custom-call | flops 1048576 | bytes 65536 | tf_op jit(solution)/shard_map/outer_blocks/pallas_call | solution.py:404
  221.3 2.7 collective-permute-start.43
  226.0 12.5 %outer_blocks.3 = (bf16[128,2048]{1,0:T(8,128)(2,1)}, bf16[128,2048]{1,0:T(8,128)(2,1)}, bf16[128,2048]{1,0:T(8,128)(2,1)}) custom-call(s32[1]{0:T(128)} %bitcast.9._.quarter_ref, bf16[512,2048]{1,0:T(8,128)(2,1)} %get-tuple-element.210.refs_0_, bf16[512,2048]{1,0:T(8,128)(2,1)} %copy-done.31, bf16[3072,512]{1,0:T(8,128)(2,1)} %get-tuple-element.236.refs_2_, ...), custom_call_target="tpu_custom_call" | custom-call | flops 1048576 | bytes 65536 | tf_op jit(solution)/shard_map/outer_blocks/pallas_call | solution.py:404
  238.6 10.2 %collective-permute-done.43 = bf16[128,2048]{1,0:T(8,128)(2,1)} collective-permute-done((bf16[128,2048]{1,0:T(8,128)(2,1)}, bf16[128,2048]{1,0:T(8,128)(2,1)}, u32[]{:S(2)}, u32[]{:S(2)}) %collective-permute-start.43) | collective-permute-done | bytes 524320 | tf_op jit(solution)/shard_map/ppermute | solution.py:492
  251.5 3.5 collective-permute-start.46
  259.6 17.6 %back_blocks.1 = bf16[3072,512]{1,0:T(8,128)(2,1)} custom-call(bf16[512,2048]{1,0:T(8,128)(2,1)} %constant_dynamic-slice_fusion.6.weight_ref, f32[3072,512]{1,0:T(8,128)} %get-tuple-element.376.slope_ref, bf16[256,2048]{1,0:T(8,128)(2,1)} %copy-done.27, bf16[256,2048]{1,0:T(8,128)(2,1)} %copy-done.29, bf16[256,2048]{1,0:T(8,128)(2,1)} %copy-done.26, ...), custom_call_target="tpu_custom_call" | custom-call | flops 1048576 | bytes 65536 | tf_op jit(solution)/shard_map/back_blocks/pallas_call | solution.py:434
  277.2 13.8 %collective-permute-done.49 = bf16[128,2048]{1,0:T(8,128)(2,1)S(1)} collective-permute-done((bf16[128,2048]{1,0:T(8,128)(2,1)S(1)}, bf16[128,2048]{1,0:T(8,128)(2,1)S(1)}, u32[]{:S(2)}, u32[]{:S(2)}) %collective-permute-start.49) | collective-permute-done | bytes 524320 | tf_op jit(solution)/shard_map/ppermute | solution.py:492
  294.9 10.9 %add_convert_fusion = bf16[2048,512]{1,0:T(8,128)(2,1)} fusion(f32[2048,512]{1,0:T(8,128)S(1)} %fusion.36, f32[2048,512]{1,0:T(8,128)S(1)} %fusion.34, bf16[3072,2048]{1,0:T(8,128)(2,1)} %get-tuple-element.233, bf16[3072,512]{1,0:T(8,128)(2,1)S(1)} %copy-done.37), kind=kOutput, calls=%fused_computation.18 | convolution fusion | flops 6445596672 | bytes 26214400 | tf_op jit(solution)/shard_map/dot_general | solution.py:35
  307.5 11.2 %collective-permute-done.51.refs_1_.refs_3_ = bf16[256,2048]{1,0:T(8,128)(2,1)S(1)} collective-permute-done((bf16[256,2048]{1,0:T(8,128)(2,1)S(1)}, bf16[256,2048]{1,0:T(8,128)(2,1)S(1)}, u32[]{:S(2)}, u32[]{:S(2)}) %collective-permute-start.51) | collective-permute-done | bytes 1048608 | tf_op jit(solution)/shard_map/ppermute | solution.py:492
  322.9 2.5 collective-permute-start.54
  325.4 31.2 %norm_back.1 = (f32[1024,2048]{1,0:T(8,128)}, f32[8,2048]{1,0:T(8,128)}, f32[8,1536]{1,0:T(8,128)}, f32[8,2048]{1,0:T(8,128)}) custom-call(bf16[1024,1536]{1,0:T(8,128)(2,1)} %attend_back.1.grad_qkv_ref, bf16[1024,2048]{1,0:T(8,128)(2,1)} %fusion.5.grad_inner_ref, bf16[2048,1536]{1,0:T(8,128)(2,1)} %qkv_ref.1, bf16[2048,2048]{1,0:T(8,128)(2,1)} %fc1_ref.1, ...), custom_call_target="tpu_custom_call" | custom-call | flops 1048576 | bytes 65536 | tf_op jit(solution)/shard_map/norm_back/pallas_call | solution.py:278
  368.8 11.4 %add_convert_fusion.1 = bf16[2048,384]{1,0:T(8,128)(2,1)} fusion(f32[2048,384]{1,0:T(8,128)S(1)} %fusion.42, f32[2048,384]{1,0:T(8,128)S(1)} %fusion.40, bf16[3072,2048]{1,0:T(8,128)(2,1)} %get-tuple-element.289, bf16[1024,384]{1,0:T(8,128)(2,1)S(1)} %copy-done.62, bf16[1024,384]{1,0:T(8,128)(2,1)} %collective-permute-done.45, ...), kind=kOutput, calls=%fused_computation.23 | convolution fusion | flops 4841275392 | bytes 22806528 | tf_op jit(solution)/shard_map/dot_general | solution.py:35
  382.1 2.6 fusion.19
  384.8 3.6 collective-permute-done.57.refs_2_.refs_4_
  394.4 2.4 place_quarters.15.refs_0_
  396.9 20.3 %collective-permute-done.58 = bf16[512,512]{1,0:T(8,128)(2,1)S(1)} collective-permute-done((bf16[512,512]{1,0:T(8,128)(2,1)S(1)}, bf16[512,512]{1,0:T(8,128)(2,1)S(1)}, u32[]{:S(2)}, u32[]{:S(2)}) %collective-permute-start.58) | collective-permute-done | bytes 524320 | tf_op jit(solution)/shard_map/ppermute | solution.py:492
  423.8 2.4 place_quarters.16.refs_0_
  426.2 20.1 %collective-permute-done.63 = bf16[512,512]{1,0:T(8,128)(2,1)S(1)} collective-permute-done((bf16[512,512]{1,0:T(8,128)(2,1)S(1)}, bf16[512,512]{1,0:T(8,128)(2,1)S(1)}, u32[]{:S(2)}, u32[]{:S(2)}) %collective-permute-start.63) | collective-permute-done | bytes 524320 | tf_op jit(solution)/shard_map/ppermute | solution.py:492
  447.6 2.4 collective-permute-start.67
  450.2 2.5 place_quarters.18
  452.6 3.7 place_quarters.17.refs_0_
  456.4 16.1 %collective-permute-done.62 = bf16[512,512]{1,0:T(8,128)(2,1)S(1)} collective-permute-done((bf16[512,512]{1,0:T(8,128)(2,1)S(1)}, bf16[512,512]{1,0:T(8,128)(2,1)S(1)}, u32[]{:S(2)}, u32[]{:S(2)}) %collective-permute-start.62) | collective-permute-done | bytes 524320 | tf_op jit(solution)/shard_map/ppermute | solution.py:492
  474.1 2.5 collective-permute-start.71
  477.5 2.4 place_quarters.20.refs_0_
  479.9 2.4 place_quarters.19
  482.4 16.3 %collective-permute-done.70 = bf16[512,512]{1,0:T(8,128)(2,1)S(1)} collective-permute-done((bf16[512,512]{1,0:T(8,128)(2,1)S(1)}, bf16[512,512]{1,0:T(8,128)(2,1)S(1)}, u32[]{:S(2)}, u32[]{:S(2)}) %collective-permute-start.70) | collective-permute-done | bytes 524320 | tf_op jit(solution)/shard_map/ppermute | solution.py:492
  500.9 2.8 collective-permute-start.74
  505.2 2.4 place_quarters.21.refs_0_
  507.6 11.7 %collective-permute-done.74 = bf16[512,384]{1,0:T(8,128)(2,1)S(1)} collective-permute-done((bf16[512,384]{1,0:T(8,128)(2,1)S(1)}, bf16[512,384]{1,0:T(8,128)(2,1)S(1)}, u32[]{:S(2)}, u32[]{:S(2)}) %collective-permute-start.74) | collective-permute-done | bytes 393248 | tf_op jit(solution)/shard_map/ppermute | solution.py:492
  519.3 5.9 collective-permute-done.77
  526.0 3.0 collective-permute-start.79
  529.1 2.5 place_quarters.22.refs_0_
  531.6 12.9 %collective-permute-done.78 = bf16[512,384]{1,0:T(8,128)(2,1)S(1)} collective-permute-done((bf16[512,384]{1,0:T(8,128)(2,1)S(1)}, bf16[512,384]{1,0:T(8,128)(2,1)S(1)}, u32[]{:S(2)}, u32[]{:S(2)}) %collective-permute-start.78) | collective-permute-done | bytes 393248 | tf_op jit(solution)/shard_map/ppermute | solution.py:492
  546.2 2.9 collective-permute-done.80.refs_2_.refs_4_
  549.9 3.0 collective-permute-start.83
  553.0 2.7 place_quarters.23
  555.7 12.5 %collective-permute-done.82 = bf16[512,384]{1,0:T(8,128)(2,1)S(1)} collective-permute-done((bf16[512,384]{1,0:T(8,128)(2,1)S(1)}, bf16[512,384]{1,0:T(8,128)(2,1)S(1)}, u32[]{:S(2)}, u32[]{:S(2)}) %collective-permute-start.82) | collective-permute-done | bytes 393248 | tf_op jit(solution)/shard_map/ppermute | solution.py:492
  570.9 3.2 collective-permute-start.86
  576.2 7.4 %collective-permute-done.86 = bf16[256,384]{1,0:T(8,128)(2,1)S(1)} collective-permute-done((bf16[256,384]{1,0:T(8,128)(2,1)S(1)}, bf16[256,384]{1,0:T(8,128)(2,1)S(1)}, u32[]{:S(2)}, u32[]{:S(2)}) %collective-permute-start.86) | collective-permute-done | bytes 196640 | tf_op jit(solution)/shard_map/ppermute | solution.py:492
  585.9 4.0 collective-permute-done.88.refs_2_.refs_4_
  590.5 3.2 collective-permute-start.90
  598.3 10.3 %collective-permute-done.92.refs_2_.refs_4_ = bf16[1024,384]{1,0:T(8,128)(2,1)S(1)} collective-permute-done((bf16[1024,384]{1,0:T(8,128)(2,1)S(1)}, bf16[1024,384]{1,0:T(8,128)(2,1)S(1)}, u32[]{:S(2)}, u32[]{:S(2)}) %collective-permute-start.92) | collective-permute-done | bytes 786464 | tf_op jit(solution)/shard_map/ppermute | solution.py:492
  609.1 3.2 collective-permute-start.93
  627.8 2.5 collective-permute-done.97.refs_2_.refs_4_
  (409 shorter events, 143.7 us)
Async XLA Ops:
  1.2 28.0 %collective-permute-start.2 = (bf16[256,2048]{1,0:T(8,128)(2,1)}, bf16[256,2048]{1,0:T(8,128)(2,1)}, u32[]{:S(2)}, u32[]{:S(2)}) collective-permute-start(bf16[256,2048]{1,0:T(8,128)(2,1)} %refs_0_.1), channel_id=1, source_target_pairs={{0,4},{4,0},{8,12},{12,8},{16,20},{20,16},{24,28},{28,24},{1,5},{5... | collective-permute-start | bytes 3145736 | tf_op jit(solution)/shard_map/ppermute | solution.py:492
  3.8 25.5 %collective-permute-start.3 = (bf16[256,2048]{1,0:T(8,128)(2,1)}, bf16[256,2048]{1,0:T(8,128)(2,1)}, u32[]{:S(2)}, u32[]{:S(2)}) collective-permute-start(bf16[256,2048]{1,0:T(8,128)(2,1)} %refs_0_.1), channel_id=1, source_target_pairs={{0,8},{4,12},{8,0},{12,4},{16,24},{20,28},{24,16},{28,20},{1,9},{5... | collective-permute-start | bytes 3145736 | tf_op jit(solution)/shard_map/ppermute | solution.py:492
  5.3 25.3 %collective-permute-start.4 = (bf16[256,2048]{1,0:T(8,128)(2,1)}, bf16[256,2048]{1,0:T(8,128)(2,1)}, u32[]{:S(2)}, u32[]{:S(2)}) collective-permute-start(bf16[256,2048]{1,0:T(8,128)(2,1)} %refs_0_.1), channel_id=1, source_target_pairs={{0,2},{1,3},{2,0},{3,1},{4,6},{5,7},{6,4},{7,5},{8,10},{9,11},{10,... | collective-permute-start | bytes 3145736 | tf_op jit(solution)/shard_map/ppermute | solution.py:485
  30.6 37.8 %collective-permute-start.7 = (bf16[256,2048]{1,0:T(8,128)(2,1)}, bf16[256,2048]{1,0:T(8,128)(2,1)}, u32[]{:S(2)}, u32[]{:S(2)}) collective-permute-start(bf16[256,2048]{1,0:T(8,128)(2,1)} %collective-permute-done.3.refs_5_), channel_id=1, source_target_pairs={{0,4},{4,0},{8,12},{12,8},{16,20},{20,16},{24,28},{28,24},{1,5},{5... | collective-permute-start | bytes 3145736 | tf_op jit(solution)/shard_map/ppermute | solution.py:492
  31.8 49.0 %collective-permute-start.9 = (bf16[256,2048]{1,0:T(8,128)(2,1)}, bf16[256,2048]{1,0:T(8,128)(2,1)}, u32[]{:S(2)}, u32[]{:S(2)}) collective-permute-start(bf16[256,2048]{1,0:T(8,128)(2,1)} %collective-permute-done.4.refs_1_.refs_2_), channel_id=1, source_target_pairs={{0,8},{4,12},{8,0},{12,4},{16,24},{20,28},{24,16},{28,20},{1,9},{5... | collective-permute-start | bytes 3145736 | tf_op jit(solution)/shard_map/ppermute | solution.py:492
  33.9 32.9 %collective-permute-start.6 = (f32[8,128]{1,0:T(8,128)S(1)}, f32[8,128]{1,0:T(8,128)S(1)}, u32[]{:S(2)}, u32[]{:S(2)}) collective-permute-start(f32[8,128]{1,0:T(8,128)S(1)} %broadcast_add_fusion), channel_id=1, source_target_pairs={{0,4},{4,0},{8,12},{12,8},{16,20},{20,16},{24,28},{28,24},{1,5},{5... | collective-permute-start | bytes 12296 | tf_op jit(solution)/shard_map/ppermute | solution.py:492
  35.6 45.2 %collective-permute-start.8 = (bf16[256,2048]{1,0:T(8,128)(2,1)}, bf16[256,2048]{1,0:T(8,128)(2,1)S(1)}, u32[]{:S(2)}, u32[]{:S(2)}) collective-permute-start(bf16[256,2048]{1,0:T(8,128)(2,1)} %collective-permute-done.2.refs_1_), channel_id=1, source_target_pairs={{0,2},{1,3},{2,0},{3,1},{4,6},{5,7},{6,4},{7,5},{8,10},{9,11},{10,... | collective-permute-start | bytes 3145736 | tf_op jit(solution)/shard_map/ppermute | solution.py:485
  98.7 24.3 %collective-permute-start.24 = (bf16[256,2048]{1,0:T(8,128)(2,1)}, bf16[256,2048]{1,0:T(8,128)(2,1)}, u32[]{:S(2)}, u32[]{:S(2)}) collective-permute-start(bf16[256,2048]{1,0:T(8,128)(2,1)} %collective-permute-done.9.refs_7_), channel_id=1, source_target_pairs={{0,4},{4,0},{8,12},{12,8},{16,20},{20,16},{24,28},{28,24},{1,5},{5... | collective-permute-start | bytes 3145736 | tf_op jit(solution)/shard_map/ppermute | solution.py:492
  100.9 23.8 %collective-permute-start.21 = (bf16[256,2048]{1,0:T(8,128)(2,1)S(1)}, bf16[256,2048]{1,0:T(8,128)(2,1)}, u32[]{:S(2)}, u32[]{:S(2)}) collective-permute-start(bf16[256,2048]{1,0:T(8,128)(2,1)S(1)} %fusion.31), channel_id=1, source_target_pairs={{0,2},{1,3},{2,0},{3,1},{4,6},{5,7},{6,4},{7,5},{8,10},{9,11},{10,... | collective-permute-start | bytes 3145736 | tf_op jit(solution)/shard_map/ppermute | solution.py:489
  101.6 23.2 %collective-permute-start.22 = (bf16[256,2048]{1,0:T(8,128)(2,1)S(1)}, bf16[256,2048]{1,0:T(8,128)(2,1)}, u32[]{:S(2)}, u32[]{:S(2)}) collective-permute-start(bf16[256,2048]{1,0:T(8,128)(2,1)S(1)} %fusion.32), channel_id=1, source_target_pairs={{0,1},{1,0},{2,3},{3,2},{4,5},{5,4},{6,7},{7,6},{8,9},{9,8},{10,11... | collective-permute-start | bytes 3145736 | tf_op jit(solution)/shard_map/ppermute | solution.py:481
  101.7 21.3 %collective-permute-start.23 = (f32[8,128]{1,0:T(8,128)S(1)}, f32[8,128]{1,0:T(8,128)S(1)}, u32[]{:S(2)}, u32[]{:S(2)}) collective-permute-start(f32[8,128]{1,0:T(8,128)S(1)} %add.303), channel_id=1, source_target_pairs={{0,16},{4,20},{8,24},{12,28},{16,0},{20,4},{24,8},{28,12},{1,17},{... | collective-permute-start | bytes 12296 | tf_op jit(solution)/shard_map/ppermute | solution.py:492
  131.6 27.4 %collective-permute-start.25 = (bf16[256,2048]{1,0:T(8,128)(2,1)}, bf16[256,2048]{1,0:T(8,128)(2,1)}, u32[]{:S(2)}, u32[]{:S(2)}) collective-permute-start(bf16[256,2048]{1,0:T(8,128)(2,1)} %get-tuple-element.229), channel_id=1, source_target_pairs={{0,2},{1,3},{2,0},{3,1},{4,6},{5,7},{6,4},{7,5},{8,10},{9,11},{10,... | collective-permute-start | bytes 3145736 | tf_op jit(solution)/shard_map/ppermute | solution.py:485
  132.7 26.2 %collective-permute-start.26 = (bf16[256,2048]{1,0:T(8,128)(2,1)}, bf16[256,2048]{1,0:T(8,128)(2,1)S(1)}, u32[]{:S(2)}, u32[]{:S(2)}) collective-permute-start(bf16[256,2048]{1,0:T(8,128)(2,1)} %get-tuple-element.229), channel_id=1, source_target_pairs={{0,4},{4,0},{8,12},{12,8},{16,20},{20,16},{24,28},{28,24},{1,5},{5... | collective-permute-start | bytes 3145736 | tf_op jit(solution)/shard_map/ppermute | solution.py:492
  133.5 25.4 %collective-permute-start.27 = (bf16[256,2048]{1,0:T(8,128)(2,1)}, bf16[256,2048]{1,0:T(8,128)(2,1)S(1)}, u32[]{:S(2)}, u32[]{:S(2)}) collective-permute-start(bf16[256,2048]{1,0:T(8,128)(2,1)} %get-tuple-element.229), channel_id=1, source_target_pairs={{0,8},{4,12},{8,0},{12,4},{16,24},{20,28},{24,16},{28,20},{1,9},{5... | collective-permute-start | bytes 3145736 | tf_op jit(solution)/shard_map/ppermute | solution.py:492
  134.6 24.3 %collective-permute-start.29 = (bf16[256,2048]{1,0:T(8,128)(2,1)}, bf16[256,2048]{1,0:T(8,128)(2,1)S(1)}, u32[]{:S(2)}, u32[]{:S(2)}) collective-permute-start(bf16[256,2048]{1,0:T(8,128)(2,1)} %get-tuple-element.229), channel_id=1, source_target_pairs={{0,1},{1,0},{2,3},{3,2},{4,5},{5,4},{6,7},{7,6},{8,9},{9,8},{10,11... | collective-permute-start | bytes 3145736 | tf_op jit(solution)/shard_map/ppermute | solution.py:481
  159.6 27.5 %collective-permute-start.33 = (bf16[256,2048]{1,0:T(8,128)(2,1)}, bf16[256,2048]{1,0:T(8,128)(2,1)S(1)}, u32[]{:S(2)}, u32[]{:S(2)}) collective-permute-start(bf16[256,2048]{1,0:T(8,128)(2,1)} %collective-permute-done.25), channel_id=1, source_target_pairs={{0,8},{4,12},{8,0},{12,4},{16,24},{20,28},{24,16},{28,20},{1,9},{5... | collective-permute-start | bytes 3145736 | tf_op jit(solution)/shard_map/ppermute | solution.py:492
  160.6 26.5 %collective-permute-start.32 = (bf16[256,2048]{1,0:T(8,128)(2,1)S(1)}, bf16[256,2048]{1,0:T(8,128)(2,1)S(1)}, u32[]{:S(2)}, u32[]{:S(2)}) collective-permute-start(bf16[256,2048]{1,0:T(8,128)(2,1)S(1)} %collective-permute-done.26.refs_4_.refs_8_.refs_0_), channel_id=1, source_target_pairs={{0,2},{1,3},{2,0},{3,1},{4,6},{5,7},{6,4},{7,5},{8,10},{9,11},{10,... | collective-permute-start | bytes 3145736 | tf_op jit(solution)/shard_map/ppermute | solution.py:485
  161.4 27.7 %collective-permute-start.36 = (bf16[256,2048]{1,0:T(8,128)(2,1)S(1)}, bf16[256,2048]{1,0:T(8,128)(2,1)S(1)}, u32[]{:S(2)}, u32[]{:S(2)}) collective-permute-start(bf16[256,2048]{1,0:T(8,128)(2,1)S(1)} %collective-permute-done.26.refs_4_.refs_8_.refs_0_), channel_id=1, source_target_pairs={{0,1},{1,0},{2,3},{3,2},{4,5},{5,4},{6,7},{7,6},{8,9},{9,8},{10,11... | collective-permute-start | bytes 3145736 | tf_op jit(solution)/shard_map/ppermute | solution.py:481
  161.4 25.7 %collective-permute-start.31 = (bf16[256,2048]{1,0:T(8,128)(2,1)S(1)}, bf16[256,2048]{1,0:T(8,128)(2,1)}, u32[]{:S(2)}, u32[]{:S(2)}) collective-permute-start(bf16[256,2048]{1,0:T(8,128)(2,1)S(1)} %collective-permute-done.27.refs_8_.refs_12_.refs_4_), channel_id=1, source_target_pairs={{0,4},{4,0},{8,12},{12,8},{16,20},{20,16},{24,28},{28,24},{1,5},{5... | collective-permute-start | bytes 3145736 | tf_op jit(solution)/shard_map/ppermute | solution.py:492
  162.8 26.7 %collective-permute-start.38 = (bf16[256,2048]{1,0:T(8,128)(2,1)S(1)}, bf16[256,2048]{1,0:T(8,128)(2,1)}, u32[]{:S(2)}, u32[]{:S(2)}) collective-permute-start(bf16[256,2048]{1,0:T(8,128)(2,1)S(1)} %collective-permute-done.27.refs_8_.refs_12_.refs_4_), channel_id=1, source_target_pairs={{0,1},{1,0},{2,3},{3,2},{4,5},{5,4},{6,7},{7,6},{8,9},{9,8},{10,11... | collective-permute-start | bytes 3145736 | tf_op jit(solution)/shard_map/ppermute | solution.py:481
  187.2 19.1 %collective-permute-start.37 = (bf16[256,2048]{1,0:T(8,128)(2,1)S(1)}, bf16[256,2048]{1,0:T(8,128)(2,1)}, u32[]{:S(2)}, u32[]{:S(2)}) collective-permute-start(bf16[256,2048]{1,0:T(8,128)(2,1)S(1)} %collective-permute-done.32.refs_6_.refs_10_.refs_2_), channel_id=1, source_target_pairs={{0,1},{1,0},{2,3},{3,2},{4,5},{5,4},{6,7},{7,6},{8,9},{9,8},{10,11... | collective-permute-start | bytes 3145736 | tf_op jit(solution)/shard_map/ppermute | solution.py:481
  187.3 19.0 %collective-permute-start.39 = (bf16[256,2048]{1,0:T(8,128)(2,1)S(1)}, bf16[256,2048]{1,0:T(8,128)(2,1)}, u32[]{:S(2)}, u32[]{:S(2)}) collective-permute-start(bf16[256,2048]{1,0:T(8,128)(2,1)S(1)} %collective-permute-done.33.refs_10_.refs_14_.refs_6_), channel_id=1, source_target_pairs={{0,1},{1,0},{2,3},{3,2},{4,5},{5,4},{6,7},{7,6},{8,9},{9,8},{10,11... | collective-permute-start | bytes 3145736 | tf_op jit(solution)/shard_map/ppermute | solution.py:481
  187.9 18.4 %collective-permute-start.34 = (bf16[128,2048]{1,0:T(8,128)(2,1)S(1)}, bf16[128,2048]{1,0:T(8,128)(2,1)}, u32[]{:S(2)}, u32[]{:S(2)}) collective-permute-start(bf16[128,2048]{1,0:T(8,128)(2,1)S(1)} %slice.140), channel_id=1, source_target_pairs={{0,4},{4,0},{8,12},{12,8},{16,20},{20,16},{24,28},{28,24},{1,5},{5... | collective-permute-start | bytes 1572872 | tf_op jit(solution)/shard_map/ppermute | solution.py:492
  208.4 30.1 %collective-permute-start.44 = (bf16[1024,384]{1,0:T(8,128)(2,1)}, bf16[1024,384]{1,0:T(8,128)(2,1)}, u32[]{:S(2)}, u32[]{:S(2)}) collective-permute-start(bf16[1024,384]{1,0:T(8,128)(2,1)} %get-tuple-element.380), channel_id=1, source_target_pairs={{0,4},{4,0},{8,12},{12,8},{16,20},{20,16},{24,28},{28,24},{1,5},{5... | collective-permute-start | bytes 2359304 | tf_op jit(solution)/shard_map/ppermute | solution.py:492
  209.4 29.1 %collective-permute-start.45 = (bf16[1024,384]{1,0:T(8,128)(2,1)}, bf16[1024,384]{1,0:T(8,128)(2,1)}, u32[]{:S(2)}, u32[]{:S(2)}) collective-permute-start(bf16[1024,384]{1,0:T(8,128)(2,1)} %get-tuple-element.379), channel_id=1, source_target_pairs={{0,8},{4,12},{8,0},{12,4},{16,24},{20,28},{24,16},{28,20},{1,9},{5... | collective-permute-start | bytes 2359304 | tf_op jit(solution)/shard_map/ppermute | solution.py:492
  221.3 27.4 %collective-permute-start.43 = (bf16[128,2048]{1,0:T(8,128)(2,1)}, bf16[128,2048]{1,0:T(8,128)(2,1)}, u32[]{:S(2)}, u32[]{:S(2)}) collective-permute-start(bf16[128,2048]{1,0:T(8,128)(2,1)} %get-tuple-element.253), channel_id=1, source_target_pairs={{0,16},{4,20},{8,24},{12,28},{16,0},{20,4},{24,8},{28,12},{1,17},{... | collective-permute-start | bytes 1572872 | tf_op jit(solution)/shard_map/ppermute | solution.py:492
  224.1 53.1 %collective-permute-start.48 = (bf16[1024,384]{1,0:T(8,128)(2,1)S(1)}, bf16[1024,384]{1,0:T(8,128)(2,1)S(1)}, u32[]{:S(2)}, u32[]{:S(2)}) collective-permute-start(bf16[1024,384]{1,0:T(8,128)(2,1)S(1)} %constant_dynamic-slice_fusion.2), channel_id=1, source_target_pairs={{0,12},{4,8},{8,4},{12,0},{16,28},{20,24},{24,20},{28,16},{1,13},{... | collective-permute-start | bytes 2359304 | tf_op jit(solution)/shard_map/ppermute | solution.py:492
  225.7 51.5 %collective-permute-start.47 = (bf16[128,2048]{1,0:T(8,128)(2,1)}, bf16[128,2048]{1,0:T(8,128)(2,1)S(1)}, u32[]{:S(2)}, u32[]{:S(2)}) collective-permute-start(bf16[128,2048]{1,0:T(8,128)(2,1)} %get-tuple-element.262), channel_id=1, source_target_pairs={{0,16},{4,20},{8,24},{12,28},{16,0},{20,4},{24,8},{28,12},{1,17},{... | collective-permute-start | bytes 1572872 | tf_op jit(solution)/shard_map/ppermute | solution.py:492
  249.9 41.1 %collective-permute-start.49 = (bf16[128,2048]{1,0:T(8,128)(2,1)S(1)}, bf16[128,2048]{1,0:T(8,128)(2,1)S(1)}, u32[]{:S(2)}, u32[]{:S(2)}) collective-permute-start(bf16[128,2048]{1,0:T(8,128)(2,1)S(1)} %add_convert_fusion.10), channel_id=1, source_target_pairs={{0,8},{4,12},{8,0},{12,4},{16,24},{20,28},{24,16},{28,20},{1,9},{5... | collective-permute-start | bytes 1572872 | tf_op jit(solution)/shard_map/ppermute | solution.py:492
  251.5 54.3 %collective-permute-start.46 = (bf16[128,2048]{1,0:T(8,128)(2,1)}, bf16[128,2048]{1,0:T(8,128)(2,1)S(1)}, u32[]{:S(2)}, u32[]{:S(2)}) collective-permute-start(bf16[128,2048]{1,0:T(8,128)(2,1)} %get-tuple-element.261), channel_id=1, source_target_pairs={{0,16},{4,20},{8,24},{12,28},{16,0},{20,4},{24,8},{28,12},{1,17},{... | collective-permute-start | bytes 1572872 | tf_op jit(solution)/shard_map/ppermute | solution.py:492
  294.2 24.5 %collective-permute-start.51 = (bf16[256,2048]{1,0:T(8,128)(2,1)S(1)}, bf16[256,2048]{1,0:T(8,128)(2,1)S(1)}, u32[]{:S(2)}, u32[]{:S(2)}) collective-permute-start(bf16[256,2048]{1,0:T(8,128)(2,1)S(1)} %pad_maximum_fusion.4.refs_0_.refs_2_), channel_id=1, source_target_pairs={{0,4},{4,0},{8,12},{12,8},{16,20},{20,16},{24,28},{28,24},{1,5},{5... | collective-permute-start | bytes 3145736 | tf_op jit(solution)/shard_map/ppermute | solution.py:492
  319.7 38.3 %collective-permute-start.55 = (bf16[256,2048]{1,0:T(8,128)(2,1)S(1)}, bf16[256,2048]{1,0:T(8,128)(2,1)S(1)}, u32[]{:S(2)}, u32[]{:S(2)}) collective-permute-start(bf16[256,2048]{1,0:T(8,128)(2,1)S(1)} %pad_maximum_fusion.5.refs_1_.refs_3_), channel_id=1, source_target_pairs={{0,4},{4,0},{8,12},{12,8},{16,20},{20,16},{24,28},{28,24},{1,5},{5... | collective-permute-start | bytes 3145736 | tf_op jit(solution)/shard_map/ppermute | solution.py:492
  320.0 37.9 %collective-permute-start.53 = (bf16[128,2048]{1,0:T(8,128)(2,1)}, bf16[128,2048]{1,0:T(8,128)(2,1)}, u32[]{:S(2)}, u32[]{:S(2)}) collective-permute-start(bf16[128,2048]{1,0:T(8,128)(2,1)} %get-tuple-element.279), channel_id=1, source_target_pairs={{0,16},{4,20},{8,24},{12,28},{16,0},{20,4},{24,8},{28,12},{1,17},{... | collective-permute-start | bytes 1572872 | tf_op jit(solution)/shard_map/ppermute | solution.py:492
  322.9 35.0 %collective-permute-start.54 = (bf16[128,2048]{1,0:T(8,128)(2,1)}, bf16[128,2048]{1,0:T(8,128)(2,1)}, u32[]{:S(2)}, u32[]{:S(2)}) collective-permute-start(bf16[128,2048]{1,0:T(8,128)(2,1)} %add_convert_fusion.8), channel_id=1, source_target_pairs={{0,8},{4,12},{8,0},{12,4},{16,24},{20,28},{24,16},{28,20},{1,9},{5... | collective-permute-start | bytes 1572872 | tf_op jit(solution)/shard_map/ppermute | solution.py:492
  325.4 59.4 %collective-permute-start.52 = (bf16[128,2048]{1,0:T(8,128)(2,1)}, bf16[128,2048]{1,0:T(8,128)(2,1)}, u32[]{:S(2)}, u32[]{:S(2)}) collective-permute-start(bf16[128,2048]{1,0:T(8,128)(2,1)} %get-tuple-element.278), channel_id=1, source_target_pairs={{0,16},{4,20},{8,24},{12,28},{16,0},{20,4},{24,8},{28,12},{1,17},{... | collective-permute-start | bytes 1572872 | tf_op jit(solution)/shard_map/ppermute | solution.py:492
  365.5 22.8 %collective-permute-start.57 = (bf16[256,2048]{1,0:T(8,128)(2,1)S(1)}, bf16[256,2048]{1,0:T(8,128)(2,1)}, u32[]{:S(2)}, u32[]{:S(2)}) collective-permute-start(bf16[256,2048]{1,0:T(8,128)(2,1)S(1)} %pad_maximum_fusion.6.refs_1_.refs_3_), channel_id=1, source_target_pairs={{0,4},{4,0},{8,12},{12,8},{16,20},{20,16},{24,28},{28,24},{1,5},{5... | collective-permute-start | bytes 3145736 | tf_op jit(solution)/shard_map/ppermute | solution.py:492
  366.8 18.0 %collective-permute-start.56 = (bf16[128,2048]{1,0:T(8,128)(2,1)}, bf16[128,2048]{1,0:T(8,128)(2,1)}, u32[]{:S(2)}, u32[]{:S(2)}) collective-permute-start(bf16[128,2048]{1,0:T(8,128)(2,1)} %add_convert_fusion.7), channel_id=1, source_target_pairs={{0,8},{4,12},{8,0},{12,4},{16,24},{20,28},{24,16},{28,20},{1,9},{5... | collective-permute-start | bytes 1572872 | tf_op jit(solution)/shard_map/ppermute | solution.py:492
  388.3 29.4 %collective-permute-start.61 = (bf16[2,256,2048]{2,1,0:T(8,128)(2,1)S(1)}, bf16[2,256,2048]{2,1,0:T(8,128)(2,1)S(1)}, u32[]{:S(2)}, u32[]{:S(2)}) collective-permute-start(bf16[2,256,2048]{2,1,0:T(8,128)(2,1)S(1)} %fusion.19), channel_id=1, source_target_pairs={{0,1},{1,0},{2,3},{3,2},{4,5},{5,4},{6,7},{7,6},{8,9},{9,8},{10,11... | collective-permute-start | bytes 6291464 | tf_op jit(solution)/shard_map/ppermute | solution.py:481
  389.7 28.1 %collective-permute-start.60 = (bf16[256,2048]{1,0:T(8,128)(2,1)S(1)}, bf16[256,2048]{1,0:T(8,128)(2,1)S(1)}, u32[]{:S(2)}, u32[]{:S(2)}) collective-permute-start(bf16[256,2048]{1,0:T(8,128)(2,1)S(1)} %pad_maximum_fusion.7.refs_1_.refs_3_), channel_id=1, source_target_pairs={{0,4},{4,0},{8,12},{12,8},{16,20},{20,16},{24,28},{28,24},{1,5},{5... | collective-permute-start | bytes 3145736 | tf_op jit(solution)/shard_map/ppermute | solution.py:492
  390.9 26.3 %collective-permute-start.58 = (bf16[512,512]{1,0:T(8,128)(2,1)S(1)}, bf16[512,512]{1,0:T(8,128)(2,1)S(1)}, u32[]{:S(2)}, u32[]{:S(2)}) collective-permute-start(bf16[512,512]{1,0:T(8,128)(2,1)S(1)} %copy-done.42), channel_id=1, source_target_pairs={{0,16},{4,20},{8,24},{12,28},{16,0},{20,4},{24,8},{28,12},{1,17},{... | collective-permute-start | bytes 1572872 | tf_op jit(solution)/shard_map/ppermute | solution.py:492
  394.0 23.8 %collective-permute-start.59 = (bf16[128,2048]{1,0:T(8,128)(2,1)S(1)}, bf16[128,2048]{1,0:T(8,128)(2,1)S(1)}, u32[]{:S(2)}, u32[]{:S(2)}) collective-permute-start(bf16[128,2048]{1,0:T(8,128)(2,1)S(1)} %add_convert_fusion.6), channel_id=1, source_target_pairs={{0,8},{4,12},{8,0},{12,4},{16,24},{20,28},{24,16},{28,20},{1,9},{5... | collective-permute-start | bytes 1572872 | tf_op jit(solution)/shard_map/ppermute | solution.py:492
  418.9 27.5 %collective-permute-start.66 = (bf16[256,2048]{1,0:T(8,128)(2,1)S(1)}, bf16[256,2048]{1,0:T(8,128)(2,1)S(1)}, u32[]{:S(2)}, u32[]{:S(2)}) collective-permute-start(bf16[256,2048]{1,0:T(8,128)(2,1)S(1)} %fusion.33), channel_id=1, source_target_pairs={{0,2},{1,3},{2,0},{3,1},{4,6},{5,7},{6,4},{7,5},{8,10},{9,11},{10,... | collective-permute-start | bytes 3145736 | tf_op jit(solution)/shard_map/ppermute | solution.py:489
  420.2 26.2 %collective-permute-start.65 = (bf16[256,2048]{1,0:T(8,128)(2,1)S(1)}, bf16[256,2048]{1,0:T(8,128)(2,1)S(1)}, u32[]{:S(2)}, u32[]{:S(2)}) collective-permute-start(bf16[256,2048]{1,0:T(8,128)(2,1)S(1)} %pad_maximum_fusion.8.refs_0_.refs_2_), channel_id=1, source_target_pairs={{0,4},{4,0},{8,12},{12,8},{16,20},{20,16},{24,28},{28,24},{1,5},{5... | collective-permute-start | bytes 3145736 | tf_op jit(solution)/shard_map/ppermute | solution.py:492
  422.3 24.0 %collective-permute-start.63 = (bf16[512,512]{1,0:T(8,128)(2,1)S(1)}, bf16[512,512]{1,0:T(8,128)(2,1)S(1)}, u32[]{:S(2)}, u32[]{:S(2)}) collective-permute-start(bf16[512,512]{1,0:T(8,128)(2,1)S(1)} %copy-done.41), channel_id=1, source_target_pairs={{0,16},{4,20},{8,24},{12,28},{16,0},{20,4},{24,8},{28,12},{1,17},{... | collective-permute-start | bytes 1572872 | tf_op jit(solution)/shard_map/ppermute | solution.py:492
  422.5 23.8 %collective-permute-start.64 = (bf16[512,512]{1,0:T(8,128)(2,1)S(1)}, bf16[512,512]{1,0:T(8,128)(2,1)S(1)}, u32[]{:S(2)}, u32[]{:S(2)}) collective-permute-start(bf16[512,512]{1,0:T(8,128)(2,1)S(1)} %add_convert_fusion.5), channel_id=1, source_target_pairs={{0,8},{4,12},{8,0},{12,4},{16,24},{20,28},{24,16},{28,20},{1,9},{5... | collective-permute-start | bytes 1572872 | tf_op jit(solution)/shard_map/ppermute | solution.py:492
  446.4 26.4 %collective-permute-start.68 = (bf16[1024,512]{1,0:T(8,128)(2,1)S(1)}, bf16[1024,512]{1,0:T(8,128)(2,1)S(1)}, u32[]{:S(2)}, u32[]{:S(2)}) collective-permute-start(bf16[1024,512]{1,0:T(8,128)(2,1)S(1)} %pad_maximum_fusion.9.refs_0_.refs_2_), channel_id=1, source_target_pairs={{0,4},{4,0},{8,12},{12,8},{16,20},{20,16},{24,28},{28,24},{1,5},{5... | collective-permute-start | bytes 3145736 | tf_op jit(solution)/shard_map/ppermute | solution.py:492
  447.4 25.0 %collective-permute-start.62 = (bf16[512,512]{1,0:T(8,128)(2,1)S(1)}, bf16[512,512]{1,0:T(8,128)(2,1)S(1)}, u32[]{:S(2)}, u32[]{:S(2)}) collective-permute-start(bf16[512,512]{1,0:T(8,128)(2,1)S(1)} %copy-done.40), channel_id=1, source_target_pairs={{0,16},{4,20},{8,24},{12,28},{16,0},{20,4},{24,8},{28,12},{1,17},{... | collective-permute-start | bytes 1572872 | tf_op jit(solution)/shard_map/ppermute | solution.py:492
  447.6 25.2 %collective-permute-start.67 = (bf16[512,512]{1,0:T(8,128)(2,1)S(1)}, bf16[512,512]{1,0:T(8,128)(2,1)S(1)}, u32[]{:S(2)}, u32[]{:S(2)}) collective-permute-start(bf16[512,512]{1,0:T(8,128)(2,1)S(1)} %add_convert_fusion.4), channel_id=1, source_target_pairs={{0,8},{4,12},{8,0},{12,4},{16,24},{20,28},{24,16},{28,20},{1,9},{5... | collective-permute-start | bytes 1572872 | tf_op jit(solution)/shard_map/ppermute | solution.py:492
  472.9 26.1 %collective-permute-start.72 = (bf16[1024,512]{1,0:T(8,128)(2,1)S(1)}, bf16[1024,512]{1,0:T(8,128)(2,1)S(1)}, u32[]{:S(2)}, u32[]{:S(2)}) collective-permute-start(bf16[1024,512]{1,0:T(8,128)(2,1)S(1)} %pad_maximum_fusion.10.refs_1_.refs_3_), channel_id=1, source_target_pairs={{0,4},{4,0},{8,12},{12,8},{16,20},{20,16},{24,28},{28,24},{1,5},{5... | collective-permute-start | bytes 3145736 | tf_op jit(solution)/shard_map/ppermute | solution.py:492
  473.7 24.9 %collective-permute-start.70 = (bf16[512,512]{1,0:T(8,128)(2,1)S(1)}, bf16[512,512]{1,0:T(8,128)(2,1)S(1)}, u32[]{:S(2)}, u32[]{:S(2)}) collective-permute-start(bf16[512,512]{1,0:T(8,128)(2,1)S(1)} %copy-done.39), channel_id=1, source_target_pairs={{0,16},{4,20},{8,24},{12,28},{16,0},{20,4},{24,8},{28,12},{1,17},{... | collective-permute-start | bytes 1572872 | tf_op jit(solution)/shard_map/ppermute | solution.py:492
  474.1 24.8 %collective-permute-start.71 = (bf16[512,512]{1,0:T(8,128)(2,1)S(1)}, bf16[512,512]{1,0:T(8,128)(2,1)S(1)}, u32[]{:S(2)}, u32[]{:S(2)}) collective-permute-start(bf16[512,512]{1,0:T(8,128)(2,1)S(1)} %add_convert_fusion.3), channel_id=1, source_target_pairs={{0,8},{4,12},{8,0},{12,4},{16,24},{20,28},{24,16},{28,20},{1,9},{5... | collective-permute-start | bytes 1572872 | tf_op jit(solution)/shard_map/ppermute | solution.py:492
  476.7 22.0 %collective-permute-start.73 = (f32[12288]{0:T(1024)S(1)}, f32[12288]{0:T(1024)S(1)}, u32[]{:S(2)}, u32[]{:S(2)}) collective-permute-start(f32[12288]{0:T(1024)S(1)} %add.336), channel_id=1, source_target_pairs={{0,2},{1,3},{2,0},{3,1},{4,6},{5,7},{6,4},{7,5},{8,10},{9,11},{10,... | collective-permute-start | bytes 147464 | tf_op jit(solution)/shard_map/ppermute | solution.py:715
  499.0 26.2 %collective-permute-start.76 = (bf16[1024,512]{1,0:T(8,128)(2,1)S(1)}, bf16[1024,512]{1,0:T(8,128)(2,1)S(1)}, u32[]{:S(2)}, u32[]{:S(2)}) collective-permute-start(bf16[1024,512]{1,0:T(8,128)(2,1)S(1)} %pad_maximum_fusion.11.refs_1_.refs_3_), channel_id=1, source_target_pairs={{0,4},{4,0},{8,12},{12,8},{16,20},{20,16},{24,28},{28,24},{1,5},{5... | collective-permute-start | bytes 3145736 | tf_op jit(solution)/shard_map/ppermute | solution.py:492
  499.9 25.3 %collective-permute-start.75 = (bf16[512,512]{1,0:T(8,128)(2,1)S(1)}, bf16[512,512]{1,0:T(8,128)(2,1)S(1)}, u32[]{:S(2)}, u32[]{:S(2)}) collective-permute-start(bf16[512,512]{1,0:T(8,128)(2,1)S(1)} %add_convert_fusion.2), channel_id=1, source_target_pairs={{0,8},{4,12},{8,0},{12,4},{16,24},{20,28},{24,16},{28,20},{1,9},{5... | collective-permute-start | bytes 1572872 | tf_op jit(solution)/shard_map/ppermute | solution.py:492
  500.9 18.4 %collective-permute-start.74 = (bf16[512,384]{1,0:T(8,128)(2,1)S(1)}, bf16[512,384]{1,0:T(8,128)(2,1)S(1)}, u32[]{:S(2)}, u32[]{:S(2)}) collective-permute-start(bf16[512,384]{1,0:T(8,128)(2,1)S(1)} %get-tuple-element.326), channel_id=1, source_target_pairs={{0,16},{4,20},{8,24},{12,28},{16,0},{20,4},{24,8},{28,12},{1,17},{... | collective-permute-start | bytes 1179656 | tf_op jit(solution)/shard_map/ppermute | solution.py:492
  504.5 20.7 %collective-permute-start.77 = (f32[15872]{0:T(1024)S(1)}, f32[15872]{0:T(1024)S(1)}, u32[]{:S(2)}, u32[]{:S(2)}) collective-permute-start(f32[15872]{0:T(1024)S(1)} %pad_maximum_fusion.19), channel_id=1, source_target_pairs={{0,4},{4,0},{8,12},{12,8},{16,20},{20,16},{24,28},{28,24},{1,5},{5... | collective-permute-start | bytes 190472 | tf_op jit(solution)/shard_map/ppermute | solution.py:492
  525.3 23.9 %collective-permute-start.80 = (bf16[1024,512]{1,0:T(8,128)(2,1)S(1)}, bf16[1024,512]{1,0:T(8,128)(2,1)S(1)}, u32[]{:S(2)}, u32[]{:S(2)}) collective-permute-start(bf16[1024,512]{1,0:T(8,128)(2,1)S(1)} %pad_maximum_fusion.12.refs_1_.refs_3_), channel_id=1, source_target_pairs={{0,4},{4,0},{8,12},{12,8},{16,20},{20,16},{24,28},{28,24},{1,5},{5... | collective-permute-start | bytes 3145736 | tf_op jit(solution)/shard_map/ppermute | solution.py:492
  525.9 18.6 %collective-permute-start.78 = (bf16[512,384]{1,0:T(8,128)(2,1)S(1)}, bf16[512,384]{1,0:T(8,128)(2,1)S(1)}, u32[]{:S(2)}, u32[]{:S(2)}) collective-permute-start(bf16[512,384]{1,0:T(8,128)(2,1)S(1)} %get-tuple-element.332), channel_id=1, source_target_pairs={{0,16},{4,20},{8,24},{12,28},{16,0},{20,4},{24,8},{28,12},{1,17},{... | collective-permute-start | bytes 1179656 | tf_op jit(solution)/shard_map/ppermute | solution.py:492
  526.0 20.2 %collective-permute-start.79 = (bf16[512,384]{1,0:T(8,128)(2,1)S(1)}, bf16[512,384]{1,0:T(8,128)(2,1)S(1)}, u32[]{:S(2)}, u32[]{:S(2)}) collective-permute-start(bf16[512,384]{1,0:T(8,128)(2,1)S(1)} %add_convert_fusion.13), channel_id=1, source_target_pairs={{0,8},{4,12},{8,0},{12,4},{16,24},{20,28},{24,16},{28,20},{1,9},{5... | collective-permute-start | bytes 1179656 | tf_op jit(solution)/shard_map/ppermute | solution.py:492
  549.2 21.0 %collective-permute-start.84 = (bf16[1024,384]{1,0:T(8,128)(2,1)S(1)}, bf16[1024,384]{1,0:T(8,128)(2,1)S(1)}, u32[]{:S(2)}, u32[]{:S(2)}) collective-permute-start(bf16[1024,384]{1,0:T(8,128)(2,1)S(1)} %pad_maximum_fusion.13.refs_0_.refs_2_), channel_id=1, source_target_pairs={{0,4},{4,0},{8,12},{12,8},{16,20},{20,16},{24,28},{28,24},{1,5},{5... | collective-permute-start | bytes 2359304 | tf_op jit(solution)/shard_map/ppermute | solution.py:492
  549.8 18.4 %collective-permute-start.82 = (bf16[512,384]{1,0:T(8,128)(2,1)S(1)}, bf16[512,384]{1,0:T(8,128)(2,1)S(1)}, u32[]{:S(2)}, u32[]{:S(2)}) collective-permute-start(bf16[512,384]{1,0:T(8,128)(2,1)S(1)} %get-tuple-element.338), channel_id=1, source_target_pairs={{0,16},{4,20},{8,24},{12,28},{16,0},{20,4},{24,8},{28,12},{1,17},{... | collective-permute-start | bytes 1179656 | tf_op jit(solution)/shard_map/ppermute | solution.py:492
  549.9 20.3 %collective-permute-start.83 = (bf16[512,384]{1,0:T(8,128)(2,1)S(1)}, bf16[512,384]{1,0:T(8,128)(2,1)S(1)}, u32[]{:S(2)}, u32[]{:S(2)}) collective-permute-start(bf16[512,384]{1,0:T(8,128)(2,1)S(1)} %add_convert_fusion.12), channel_id=1, source_target_pairs={{0,8},{4,12},{8,0},{12,4},{16,24},{20,28},{24,16},{28,20},{1,9},{5... | collective-permute-start | bytes 1179656 | tf_op jit(solution)/shard_map/ppermute | solution.py:492
  570.3 19.5 %collective-permute-start.88 = (bf16[1024,384]{1,0:T(8,128)(2,1)S(1)}, bf16[1024,384]{1,0:T(8,128)(2,1)S(1)}, u32[]{:S(2)}, u32[]{:S(2)}) collective-permute-start(bf16[1024,384]{1,0:T(8,128)(2,1)S(1)} %pad_maximum_fusion.14.refs_1_.refs_3_), channel_id=1, source_target_pairs={{0,4},{4,0},{8,12},{12,8},{16,20},{20,16},{24,28},{28,24},{1,5},{5... | collective-permute-start | bytes 2359304 | tf_op jit(solution)/shard_map/ppermute | solution.py:492
  589.9 18.7 %collective-permute-start.92 = (bf16[1024,384]{1,0:T(8,128)(2,1)S(1)}, bf16[1024,384]{1,0:T(8,128)(2,1)S(1)}, u32[]{:S(2)}, u32[]{:S(2)}) collective-permute-start(bf16[1024,384]{1,0:T(8,128)(2,1)S(1)} %pad_maximum_fusion.15.refs_1_.refs_3_), channel_id=1, source_target_pairs={{0,4},{4,0},{8,12},{12,8},{16,20},{20,16},{24,28},{28,24},{1,5},{5... | collective-permute-start | bytes 2359304 | tf_op jit(solution)/shard_map/ppermute | solution.py:492
  (101 other events, 1222.2 us)

commit v13 on v12

--- a/solution.py
+++ b/solution.py
@@ -269,10 +269,10 @@
             ref[row : row + 1, :] += total
 
 
-def norm_back(grad_qkv, grad_inner, qkv_weight, fc1_weight, gains, blocks):
+def norm_back(grad_qkv, grad_inner, qkv_weight, fc1_weight, gains, blocks, skip):
     count = len(blocks)
     rows, width = blocks[0].shape
-    each = lambda a: pl.BlockSpec((rows, a.shape[1]), lambda i: (i, 0))
+    each = lambda a: pl.BlockSpec((rows, a.shape[1]), lambda i: (i + skip, 0))
     full = lambda a: pl.BlockSpec(a.shape, lambda i: (0, 0), pipeline_mode=pl.Buffered(1))
     sums = [(8, width), (8, grad_qkv.shape[1]), (8, grad_inner.shape[1])]
     return pl.pallas_call(
@@ -822,12 +822,23 @@
     )
     (fc1_part,) = turn(fc1_part.astype(BF))
     enqueue("fc1", *cut(fc1_part, [4, 4, 4, 4]))
-    grad_hidden, sums, qkv_sum, inner_sum = norm_back(
-        gate(grad_qkv), grad_inner, qkv_weight, fc1_weight, gains, near_blocks
-    )
-    grad_hidden, sums = turn(grad_hidden, sums)
-    blocks = grad_hidden.reshape(ways, 2, rows, D)
-    kept, mates = blocks[:, 0], blocks[:, 1].astype(BF)
+    def norm_back_part(part):
+        made = norm_back(
+            gate(grad_qkv),
+            grad_inner,
+            qkv_weight,
+            fc1_weight,
+            gains,
+            near_blocks[part * ways : (part + 1) * ways],
+            part * ways,
+        )
+        return turn(*made)
+
+    first_part, second_part = norm_back_part(0), norm_back_part(1)
+    sums, qkv_sum, inner_sum = (a + b for a, b in zip(first_part[1:], second_part[1:]))
+    blocks = [v.reshape(-1, 2, rows, D) for v in (first_part[0], second_part[0])]
+    kept = jnp.concatenate([v[:, 0] for v in blocks], axis=0)
+    mates = jnp.concatenate([v[:, 1].astype(BF) for v in blocks], axis=0)
     grad_later = gate(grad_out)
     bias_part = jnp.sum(grad_later, axis=0)
     error_part = jnp.sum(grad_later * grad_later) / (scale * scale)

time: 643 us -> 631 us (0.981)
  waiting for transfers between devices: 211 us -> 189 us
  Pallas kernels: 169 us -> 176 us
    ppermute x68, waiting for transfers between devices: 207 us -> 185 us  [flip(): return lax.ppermute(v, 'dp', [(d, d ^ mask) for d in range(dp)])]
    pallas_call x1 -> x2, Pallas kernels: 31.2 us -> 38.2 us  [norm_back(): pl.pallas_call(functools.partial(norm_back_kernel, count), grid=(count,),...]
  transfers between devices with their start and end apart: 98 -> 98, of which waited for: 36 -> 38; matrix products, arithmetic and copies ran while one was open for 22% -> 23% of each run, Pallas kernels for 26% -> 28%
where the time goes in v13:
time: 631 us; the launch traced here: 621 us
  waiting for transfers between devices  189 us (30%)
  Pallas kernels  176 us (28%)
  matrix products  93.5 us (15%)
  starting transfers between devices  90.5 us (14%)
  local copies, waits for them, and re-layouts  35.4 us (6%)
  other arithmetic  30.1 us (5%)
  between operations  6.95 us (1%)
    ppermute x68, waiting for transfers between devices, flip(): return lax.ppermute(v, 'dp', [(d, d ^ mask) for d in range(dp)])  185 us
    ppermute x68, starting transfers between devices, flip(): return lax.ppermute(v, 'dp', [(d, d ^ mask) for d in range(dp)])  77.9 us
    dot_general x8, matrix products, contract(): lax.dot_general(left_side, right_side, (((left_dim,), (right_dim,)), ((),...  45.2 us
    pallas_call x2, Pallas kernels, norm_back(): pl.pallas_call(functools.partial(norm_back_kernel, count), grid=(count,),...  38.2 us
    pallas_call x15, Pallas kernels, place_quarters(): pl.pallas_call(place_kernel, grid_spec=pltpu.PrefetchScalarGridSpec(num_s...  34.4 us
    pallas_call x4, Pallas kernels, both_norms(): pl.pallas_call(functools.partial(norms_kernel, count), grid=(count,), in_...  29.8 us
    pallas_call x2, Pallas kernels, outer_blocks(): pl.pallas_call(functools.partial(outer_kernel, len(lefts), pieces, len(si...  23.5 us
    dot_general x2, matrix products, units(): jnp.dot(normed, fc1_weight, preferred_element_type=F32)  21.4 us
  transfers between devices with their start and end apart: 98, of which 38 were waited for; matrix products, arithmetic and copies ran while one was open for 23% of the time, Pallas kernels for 28%

profile of v13, /device:TPU:0, one launch (start us, length us, event | category | flops | bytes accessed | tf_op | source)
XLA Modules:
  0.0 621.5 jit_solution(1122893357135217898)
XLA Ops:
  1.2 2.6 collective-permute-start.2
  13.1 4.4 both_norms.4
  17.5 10.4 %multiply_convert_fusion.2 = (bf16[512,2048]{1,0:T(8,128)(2,1)}, f32[512,2048]{1,0:T(8,128)}) fusion(f32[2048]{0:T(1024)S(1)} %convert_element_type.250, bf16[512,2048]{1,0:T(8,128)(2,1)} %get-tuple-element.204, bf16[2048,2048]{1,0:T(8,128)(2,1)} %fc1_ref.3), kind=kOutput, calls=%fused_computation.18 | convolution fusion | flops 4301258752 | bytes 16785408 | tf_op jit(solution)/shard_map/dot_general | solution.py:539
  37.1 4.6 both_norms.5
  45.5 10.9 %qkv_rotary.1.q_ref.k_ref.v_ref = bf16[1024,1536]{1,0:T(8,128)(2,1)S(1)} custom-call(bf16[512,2048]{1,0:T(8,128)(2,1)S(1)} %copy-done.6, bf16[512,2048]{1,0:T(8,128)(2,1)S(1)} %get-tuple-element.210.rest_ref, bf16[2048,1536]{1,0:T(8,128)(2,1)} %qkv_ref.3, bf16[1,1536]{1,0:T(2,128)(2,1)S(1)} %broadcast_in_dim.11.b_ref, f32[1024,384]{1,0:T(8,128)S(1)} %copy-done.3, ...), custom_call_target="tpu_custom_call" | custom-call | flops 1048576 | bytes 65536 | tf_op jit(solution)/shard_map/qkv_rotary/pallas_call | solution.py:94
  56.4 9.6 %attend.1 = (bf16[1024,512]{1,0:T(8,128)(2,1)S(1)}, f32[2,1024,1]{2,1,0:T(8,128)S(1)}) custom-call(s32[1]{0:T(128)S(6)} %copy.68.prefix_ref, bf16[1024,1536]{1,0:T(8,128)(2,1)S(1)} %qkv_rotary.1.q_ref.k_ref.v_ref, bf16[1024,1536]{1,0:T(8,128)(2,1)S(1)} %qkv_rotary.1.q_ref.k_ref.v_ref, bf16[1024,1536]{1,0:T(8,128)(2,1)S(1)} %qkv_rotary.1.q_ref.k_ref.v_ref, ...), custom_call_target="tpu_custom_call" | custom-call | flops 1048576 | bytes 65536 | tf_op jit(solution)/shard_map/attend/pallas_call | solution.py:137
  69.8 10.9 %multiply_convert_fusion.1 = (bf16[512,2048]{1,0:T(8,128)(2,1)S(1)}, f32[512,2048]{1,0:T(8,128)}) fusion(f32[2048]{0:T(1024)S(1)} %convert_element_type.250, bf16[512,2048]{1,0:T(8,128)(2,1)S(1)} %copy-done.38, bf16[2048,2048]{1,0:T(8,128)(2,1)} %fc1_ref.3), kind=kOutput, calls=%fused_computation.17 | convolution fusion | flops 4301258752 | bytes 16785408 | tf_op jit(solution)/shard_map/dot_general | solution.py:539
  83.1 4.6 fusion.56
  90.4 4.6 fusion.57
  101.7 2.7 collective-permute-start.23
  104.4 16.2 %both_norms.6 = (bf16[3072,2048]{1,0:T(8,128)(2,1)}, bf16[3072,2048]{1,0:T(8,128)(2,1)}) custom-call(bf16[4,2048]{1,0:T(4,128)(2,1)S(1)} %pad_maximum_fusion.22.refs_0_.gains_ref, bf16[256,2048]{1,0:T(8,128)(2,1)} %collective-permute-done.2.refs_1_, bf16[256,2048]{1,0:T(8,128)(2,1)S(1)} %collective-permute-done.16.refs_2_, ...), custom_call_target="tpu_custom_call" | custom-call | flops 1048576 | bytes 65536 | tf_op jit(solution)/shard_map/both_norms/pallas_call | solution.py:354
  120.5 2.4 collective-permute-done.24.refs_1_
  126.0 4.8 fusion.51
  134.6 4.7 both_norms.7
  139.3 14.7 %fusion.9 = (f32[3072,512]{1,0:T(8,128)}, bf16[3072,512]{1,0:T(8,128)(2,1)}) fusion(f32[512]{0:T(512)S(1)} %dynamic-slice_convert_fusion, bf16[3072,2048]{1,0:T(8,128)(2,1)} %get-tuple-element.244, bf16[2048,2048]{1,0:T(8,128)(2,1)} %fc1_ref.3, s32[]{:T(128)S(6)} %select_n.81), kind=kOutput, calls=%fused_computation.12 | convolution fusion | flops 6459752448 | bytes 24119300 | tf_op jit(solution)/shard_map/dot_general | solution.py:646
  155.7 3.2 constant_dynamic-slice_fusion.6.weight_ref
  164.5 2.4 convolution_convert_fusion.g_ref
  167.8 11.9 %attend_back.1.grad_qkv_ref = bf16[1024,1536]{1,0:T(8,128)(2,1)} custom-call(s32[1]{0:T(128)S(6)} %copy.68.prefix_ref, bf16[1024,1536]{1,0:T(8,128)(2,1)} %copy-done.2, bf16[1024,1536]{1,0:T(8,128)(2,1)} %copy-done.2, bf16[1024,1536]{1,0:T(8,128)(2,1)} %copy-done.2, bf16[1024,512]{1,0:T(8,128)(2,1)S(1)} %convolution_convert_fusion.g_ref, ...), custom_call_target="tpu_custom_call" | custom-call | flops 1048576 | bytes 65536 | tf_op jit(solution)/shard_map/attend_back/pallas_call | solution.py:203
  179.7 7.4 %collective-permute-done.31.refs_12_.refs_16_.refs_8_ = bf16[256,2048]{1,0:T(8,128)(2,1)} collective-permute-done((bf16[256,2048]{1,0:T(8,128)(2,1)S(1)}, bf16[256,2048]{1,0:T(8,128)(2,1)}, u32[]{:S(2)}, u32[]{:S(2)}) %collective-permute-start.31) | collective-permute-done | bytes 1048608 | tf_op jit(solution)/shard_map/ppermute | solution.py:492
  190.1 16.2 %fusion.5.grad_inner_ref = bf16[1024,2048]{1,0:T(8,128)(2,1)} fusion(f32[512,2048]{1,0:T(8,128)} %get-tuple-element.428, f32[512,2048]{1,0:T(8,128)} %get-tuple-element.426, bf16[1024,2048]{1,0:T(8,128)(2,1)S(1)} %constant_dynamic-update-slice_fusion.refs_3_.refs_7_, bf16[2048,2048]{1,0:T(8,128)(2,1)} %param.34), kind=kOutput, calls=%fused_computation.7 | convolution fusion | flops 8613003264 | bytes 25165824 | tf_op jit(solution)/shard_map/dot_general | solution.py:35
  210.3 10.9 %outer_blocks.2 = (bf16[128,2048]{1,0:T(8,128)(2,1)}, bf16[128,2048]{1,0:T(8,128)(2,1)}) custom-call(s32[1]{0:T(128)} %bitcast.9._.quarter_ref, bf16[512,2048]{1,0:T(8,128)(2,1)} %get-tuple-element.221.refs_0_, bf16[512,2048]{1,0:T(8,128)(2,1)} %copy-done.35, bf16[3072,512]{1,0:T(8,128)(2,1)} %get-tuple-element.247.refs_2_, bf16[1024,2048]{1,0:T(8,128)(2,1)} %copy-done.26, ...), custom_call_target="tpu_custom_call" | custom-call | flops 1048576 | bytes 65536 | tf_op jit(solution)/shard_map/outer_blocks/pallas_call | solution.py:404
  221.3 2.7 collective-permute-start.45
  226.0 12.5 %outer_blocks.3 = (bf16[128,2048]{1,0:T(8,128)(2,1)}, bf16[128,2048]{1,0:T(8,128)(2,1)}, bf16[128,2048]{1,0:T(8,128)(2,1)}) custom-call(s32[1]{0:T(128)} %bitcast.9._.quarter_ref, bf16[512,2048]{1,0:T(8,128)(2,1)} %get-tuple-element.221.refs_0_, bf16[512,2048]{1,0:T(8,128)(2,1)} %copy-done.35, bf16[3072,512]{1,0:T(8,128)(2,1)} %get-tuple-element.247.refs_2_, ...), custom_call_target="tpu_custom_call" | custom-call | flops 1048576 | bytes 65536 | tf_op jit(solution)/shard_map/outer_blocks/pallas_call | solution.py:404
  238.6 10.2 %collective-permute-done.45 = bf16[128,2048]{1,0:T(8,128)(2,1)} collective-permute-done((bf16[128,2048]{1,0:T(8,128)(2,1)}, bf16[128,2048]{1,0:T(8,128)(2,1)}, u32[]{:S(2)}, u32[]{:S(2)}) %collective-permute-start.45) | collective-permute-done | bytes 524320 | tf_op jit(solution)/shard_map/ppermute | solution.py:492
  251.5 3.5 collective-permute-start.50
  259.6 17.6 %back_blocks.1 = bf16[3072,512]{1,0:T(8,128)(2,1)} custom-call(bf16[512,2048]{1,0:T(8,128)(2,1)} %constant_dynamic-slice_fusion.6.weight_ref, f32[3072,512]{1,0:T(8,128)} %get-tuple-element.398.slope_ref, bf16[256,2048]{1,0:T(8,128)(2,1)} %copy-done.31, bf16[256,2048]{1,0:T(8,128)(2,1)} %copy-done.33, bf16[256,2048]{1,0:T(8,128)(2,1)} %copy-done.30, ...), custom_call_target="tpu_custom_call" | custom-call | flops 1048576 | bytes 65536 | tf_op jit(solution)/shard_map/back_blocks/pallas_call | solution.py:434
  277.2 13.8 %collective-permute-done.48 = bf16[128,2048]{1,0:T(8,128)(2,1)S(1)} collective-permute-done((bf16[128,2048]{1,0:T(8,128)(2,1)S(1)}, bf16[128,2048]{1,0:T(8,128)(2,1)S(1)}, u32[]{:S(2)}, u32[]{:S(2)}) %collective-permute-start.48) | collective-permute-done | bytes 524320 | tf_op jit(solution)/shard_map/ppermute | solution.py:492
  294.9 9.9 %add_convert_fusion = bf16[2048,512]{1,0:T(8,128)(2,1)S(1)} fusion(f32[2048,512]{1,0:T(8,128)S(1)} %fusion.36, f32[2048,512]{1,0:T(8,128)S(1)} %fusion.34, bf16[3072,2048]{1,0:T(8,128)(2,1)} %get-tuple-element.244, bf16[3072,512]{1,0:T(8,128)(2,1)S(1)} %copy-done.41), kind=kOutput, calls=%fused_computation.16 | convolution fusion | flops 6445596672 | bytes 26214400 | tf_op jit(solution)/shard_map/dot_general | solution.py:35
  304.9 2.6 collective-permute-done.51
  307.5 11.2 %collective-permute-done.52.refs_1_.refs_3_ = bf16[256,2048]{1,0:T(8,128)(2,1)S(1)} collective-permute-done((bf16[256,2048]{1,0:T(8,128)(2,1)S(1)}, bf16[256,2048]{1,0:T(8,128)(2,1)S(1)}, u32[]{:S(2)}, u32[]{:S(2)}) %collective-permute-start.52) | collective-permute-done | bytes 1048608 | tf_op jit(solution)/shard_map/ppermute | solution.py:492
  321.1 2.5 collective-permute-start.53
  323.6 19.0 %norm_back.2 = (f32[512,2048]{1,0:T(8,128)}, f32[8,2048]{1,0:T(8,128)}, f32[8,1536]{1,0:T(8,128)}, f32[8,2048]{1,0:T(8,128)}) custom-call(bf16[1024,1536]{1,0:T(8,128)(2,1)} %attend_back.1.grad_qkv_ref, bf16[1024,2048]{1,0:T(8,128)(2,1)} %fusion.5.grad_inner_ref, bf16[2048,1536]{1,0:T(8,128)(2,1)} %qkv_ref.3, bf16[2048,2048]{1,0:T(8,128)(2,1)} %fc1_ref.3, ...), custom_call_target="tpu_custom_call" | custom-call | flops 1048576 | bytes 65536 | tf_op jit(solution)/shard_map/norm_back/pallas_call | solution.py:278
  348.1 2.5 collective-permute-start.57
  350.8 19.3 %norm_back.3 = (f32[512,2048]{1,0:T(8,128)}, f32[8,2048]{1,0:T(8,128)}, f32[8,1536]{1,0:T(8,128)}, f32[8,2048]{1,0:T(8,128)}) custom-call(bf16[1024,1536]{1,0:T(8,128)(2,1)} %attend_back.1.grad_qkv_ref, bf16[1024,2048]{1,0:T(8,128)(2,1)} %fusion.5.grad_inner_ref, bf16[2048,1536]{1,0:T(8,128)(2,1)} %qkv_ref.3, bf16[2048,2048]{1,0:T(8,128)(2,1)} %fc1_ref.3, ...), custom_call_target="tpu_custom_call" | custom-call | flops 1048576 | bytes 65536 | tf_op jit(solution)/shard_map/norm_back/pallas_call | solution.py:278
  370.1 2.7 fusion.31
  380.8 11.4 %add_convert_fusion.1 = bf16[2048,384]{1,0:T(8,128)(2,1)} fusion(f32[2048,384]{1,0:T(8,128)S(1)} %fusion.42, f32[2048,384]{1,0:T(8,128)S(1)} %fusion.40, bf16[3072,2048]{1,0:T(8,128)(2,1)} %get-tuple-element.310, bf16[1024,384]{1,0:T(8,128)(2,1)S(1)} %copy-done.71, bf16[1024,384]{1,0:T(8,128)(2,1)} %collective-permute-done.47, ...), kind=kOutput, calls=%fused_computation.21 | convolution fusion | flops 4841275392 | bytes 22806528 | tf_op jit(solution)/shard_map/dot_general | solution.py:35
  392.2 2.7 fusion.32
  398.7 4.9 collective-permute-done.59
  403.7 2.5 place_quarters.15.refs_0_
  412.9 21.7 %collective-permute-done.61 = bf16[512,512]{1,0:T(8,128)(2,1)S(1)} collective-permute-done((bf16[512,512]{1,0:T(8,128)(2,1)S(1)}, bf16[512,512]{1,0:T(8,128)(2,1)S(1)}, u32[]{:S(2)}, u32[]{:S(2)}) %collective-permute-start.61) | collective-permute-done | bytes 524320 | tf_op jit(solution)/shard_map/ppermute | solution.py:492
  439.7 2.4 collective-permute-start.67
  442.2 2.5 place_quarters.17
  444.6 2.4 place_quarters.16.refs_0_
  447.1 16.3 %collective-permute-done.66 = bf16[512,512]{1,0:T(8,128)(2,1)S(1)} collective-permute-done((bf16[512,512]{1,0:T(8,128)(2,1)S(1)}, bf16[512,512]{1,0:T(8,128)(2,1)S(1)}, u32[]{:S(2)}, u32[]{:S(2)}) %collective-permute-start.66) | collective-permute-done | bytes 524320 | tf_op jit(solution)/shard_map/ppermute | solution.py:492
  465.1 2.4 collective-permute-start.70
  467.5 2.4 place_quarters.19.refs_0_
  470.0 2.4 place_quarters.18.refs_0_
  472.4 17.1 %collective-permute-done.65 = bf16[512,512]{1,0:T(8,128)(2,1)S(1)} collective-permute-done((bf16[512,512]{1,0:T(8,128)(2,1)S(1)}, bf16[512,512]{1,0:T(8,128)(2,1)S(1)}, u32[]{:S(2)}, u32[]{:S(2)}) %collective-permute-start.65) | collective-permute-done | bytes 524320 | tf_op jit(solution)/shard_map/ppermute | solution.py:492
  491.5 2.3 collective-permute-start.73
  494.6 2.4 place_quarters.21.refs_0_
  497.1 3.6 place_quarters.20
  500.7 10.1 %collective-permute-done.73 = bf16[512,384]{1,0:T(8,128)(2,1)S(1)} collective-permute-done((bf16[512,384]{1,0:T(8,128)(2,1)S(1)}, bf16[512,384]{1,0:T(8,128)(2,1)S(1)}, u32[]{:S(2)}, u32[]{:S(2)}) %collective-permute-start.73) | collective-permute-done | bytes 393248 | tf_op jit(solution)/shard_map/ppermute | solution.py:492
  517.1 2.4 collective-permute-start.78
  521.9 2.4 place_quarters.22.refs_0_
  524.3 13.0 %collective-permute-done.77 = bf16[512,384]{1,0:T(8,128)(2,1)S(1)} collective-permute-done((bf16[512,384]{1,0:T(8,128)(2,1)S(1)}, bf16[512,384]{1,0:T(8,128)(2,1)S(1)}, u32[]{:S(2)}, u32[]{:S(2)}) %collective-permute-start.77) | collective-permute-done | bytes 393248 | tf_op jit(solution)/shard_map/ppermute | solution.py:492
  537.3 2.5 collective-permute-done.80
  543.6 2.5 place_quarters.23
  546.1 5.8 collective-permute-done.81
  551.8 7.8 %collective-permute-done.84 = f32[15872]{0:T(1024)S(1)} collective-permute-done((f32[15872]{0:T(1024)S(1)}, f32[15872]{0:T(1024)S(1)}, u32[]{:S(2)}, u32[]{:S(2)}) %collective-permute-start.84) | collective-permute-done | bytes 63520 | tf_op jit(solution)/shard_map/ppermute | solution.py:492
  560.8 2.5 collective-permute-start.85
  566.0 6.3 %collective-permute-done.85 = bf16[256,384]{1,0:T(8,128)(2,1)S(1)} collective-permute-done((bf16[256,384]{1,0:T(8,128)(2,1)S(1)}, bf16[256,384]{1,0:T(8,128)(2,1)S(1)}, u32[]{:S(2)}, u32[]{:S(2)}) %collective-permute-start.85) | collective-permute-done | bytes 196640 | tf_op jit(solution)/shard_map/ppermute | solution.py:492
  578.4 2.6 collective-permute-start.90
  585.1 10.1 %collective-permute-done.92.refs_2_.refs_4_ = bf16[1024,384]{1,0:T(8,128)(2,1)S(1)} collective-permute-done((bf16[1024,384]{1,0:T(8,128)(2,1)S(1)}, bf16[1024,384]{1,0:T(8,128)(2,1)S(1)}, u32[]{:S(2)}, u32[]{:S(2)}) %collective-permute-start.92) | collective-permute-done | bytes 786464 | tf_op jit(solution)/shard_map/ppermute | solution.py:492
  596.1 2.5 collective-permute-start.93
  (427 shorter events, 154.5 us)
Async XLA Ops:
  1.2 28.1 %collective-permute-start.2 = (bf16[256,2048]{1,0:T(8,128)(2,1)}, bf16[256,2048]{1,0:T(8,128)(2,1)}, u32[]{:S(2)}, u32[]{:S(2)}) collective-permute-start(bf16[256,2048]{1,0:T(8,128)(2,1)} %refs_0_.1), channel_id=1, source_target_pairs={{0,4},{4,0},{8,12},{12,8},{16,20},{20,16},{24,28},{28,24},{1,5},{5... | collective-permute-start | bytes 3145736 | tf_op jit(solution)/shard_map/ppermute | solution.py:492
  3.8 25.5 %collective-permute-start.3 = (bf16[256,2048]{1,0:T(8,128)(2,1)}, bf16[256,2048]{1,0:T(8,128)(2,1)}, u32[]{:S(2)}, u32[]{:S(2)}) collective-permute-start(bf16[256,2048]{1,0:T(8,128)(2,1)} %refs_0_.1), channel_id=1, source_target_pairs={{0,8},{4,12},{8,0},{12,4},{16,24},{20,28},{24,16},{28,20},{1,9},{5... | collective-permute-start | bytes 3145736 | tf_op jit(solution)/shard_map/ppermute | solution.py:492
  5.3 25.3 %collective-permute-start.4 = (bf16[256,2048]{1,0:T(8,128)(2,1)}, bf16[256,2048]{1,0:T(8,128)(2,1)}, u32[]{:S(2)}, u32[]{:S(2)}) collective-permute-start(bf16[256,2048]{1,0:T(8,128)(2,1)} %refs_0_.1), channel_id=1, source_target_pairs={{0,2},{1,3},{2,0},{3,1},{4,6},{5,7},{6,4},{7,5},{8,10},{9,11},{10,... | collective-permute-start | bytes 3145736 | tf_op jit(solution)/shard_map/ppermute | solution.py:485
  30.6 37.8 %collective-permute-start.7 = (bf16[256,2048]{1,0:T(8,128)(2,1)}, bf16[256,2048]{1,0:T(8,128)(2,1)}, u32[]{:S(2)}, u32[]{:S(2)}) collective-permute-start(bf16[256,2048]{1,0:T(8,128)(2,1)} %collective-permute-done.3.refs_5_), channel_id=1, source_target_pairs={{0,4},{4,0},{8,12},{12,8},{16,20},{20,16},{24,28},{28,24},{1,5},{5... | collective-permute-start | bytes 3145736 | tf_op jit(solution)/shard_map/ppermute | solution.py:492
  31.8 49.0 %collective-permute-start.9 = (bf16[256,2048]{1,0:T(8,128)(2,1)}, bf16[256,2048]{1,0:T(8,128)(2,1)}, u32[]{:S(2)}, u32[]{:S(2)}) collective-permute-start(bf16[256,2048]{1,0:T(8,128)(2,1)} %collective-permute-done.4.refs_1_.refs_0_), channel_id=1, source_target_pairs={{0,8},{4,12},{8,0},{12,4},{16,24},{20,28},{24,16},{28,20},{1,9},{5... | collective-permute-start | bytes 3145736 | tf_op jit(solution)/shard_map/ppermute | solution.py:492
  34.0 32.8 %collective-permute-start.6 = (f32[8,128]{1,0:T(8,128)S(1)}, f32[8,128]{1,0:T(8,128)S(1)}, u32[]{:S(2)}, u32[]{:S(2)}) collective-permute-start(f32[8,128]{1,0:T(8,128)S(1)} %broadcast_add_fusion), channel_id=1, source_target_pairs={{0,4},{4,0},{8,12},{12,8},{16,20},{20,16},{24,28},{28,24},{1,5},{5... | collective-permute-start | bytes 12296 | tf_op jit(solution)/shard_map/ppermute | solution.py:492
  35.6 45.2 %collective-permute-start.8 = (bf16[256,2048]{1,0:T(8,128)(2,1)}, bf16[256,2048]{1,0:T(8,128)(2,1)S(1)}, u32[]{:S(2)}, u32[]{:S(2)}) collective-permute-start(bf16[256,2048]{1,0:T(8,128)(2,1)} %collective-permute-done.2.refs_1_), channel_id=1, source_target_pairs={{0,2},{1,3},{2,0},{3,1},{4,6},{5,7},{6,4},{7,5},{8,10},{9,11},{10,... | collective-permute-start | bytes 3145736 | tf_op jit(solution)/shard_map/ppermute | solution.py:485
  98.6 24.3 %collective-permute-start.24 = (bf16[256,2048]{1,0:T(8,128)(2,1)}, bf16[256,2048]{1,0:T(8,128)(2,1)}, u32[]{:S(2)}, u32[]{:S(2)}) collective-permute-start(bf16[256,2048]{1,0:T(8,128)(2,1)} %collective-permute-done.9.refs_7_), channel_id=1, source_target_pairs={{0,4},{4,0},{8,12},{12,8},{16,20},{20,16},{24,28},{28,24},{1,5},{5... | collective-permute-start | bytes 3145736 | tf_op jit(solution)/shard_map/ppermute | solution.py:492
  100.9 23.8 %collective-permute-start.21 = (bf16[256,2048]{1,0:T(8,128)(2,1)S(1)}, bf16[256,2048]{1,0:T(8,128)(2,1)}, u32[]{:S(2)}, u32[]{:S(2)}) collective-permute-start(bf16[256,2048]{1,0:T(8,128)(2,1)S(1)} %fusion.29), channel_id=1, source_target_pairs={{0,2},{1,3},{2,0},{3,1},{4,6},{5,7},{6,4},{7,5},{8,10},{9,11},{10,... | collective-permute-start | bytes 3145736 | tf_op jit(solution)/shard_map/ppermute | solution.py:489
  101.6 23.2 %collective-permute-start.22 = (bf16[256,2048]{1,0:T(8,128)(2,1)S(1)}, bf16[256,2048]{1,0:T(8,128)(2,1)}, u32[]{:S(2)}, u32[]{:S(2)}) collective-permute-start(bf16[256,2048]{1,0:T(8,128)(2,1)S(1)} %fusion.30), channel_id=1, source_target_pairs={{0,1},{1,0},{2,3},{3,2},{4,5},{5,4},{6,7},{7,6},{8,9},{9,8},{10,11... | collective-permute-start | bytes 3145736 | tf_op jit(solution)/shard_map/ppermute | solution.py:481
  101.7 21.3 %collective-permute-start.23 = (f32[8,128]{1,0:T(8,128)S(1)}, f32[8,128]{1,0:T(8,128)S(1)}, u32[]{:S(2)}, u32[]{:S(2)}) collective-permute-start(f32[8,128]{1,0:T(8,128)S(1)} %add.312), channel_id=1, source_target_pairs={{0,16},{4,20},{8,24},{12,28},{16,0},{20,4},{24,8},{28,12},{1,17},{... | collective-permute-start | bytes 12296 | tf_op jit(solution)/shard_map/ppermute | solution.py:492
  131.5 27.3 %collective-permute-start.25 = (bf16[256,2048]{1,0:T(8,128)(2,1)}, bf16[256,2048]{1,0:T(8,128)(2,1)}, u32[]{:S(2)}, u32[]{:S(2)}) collective-permute-start(bf16[256,2048]{1,0:T(8,128)(2,1)} %get-tuple-element.240), channel_id=1, source_target_pairs={{0,2},{1,3},{2,0},{3,1},{4,6},{5,7},{6,4},{7,5},{8,10},{9,11},{10,... | collective-permute-start | bytes 3145736 | tf_op jit(solution)/shard_map/ppermute | solution.py:485
  132.7 26.2 %collective-permute-start.26 = (bf16[256,2048]{1,0:T(8,128)(2,1)}, bf16[256,2048]{1,0:T(8,128)(2,1)S(1)}, u32[]{:S(2)}, u32[]{:S(2)}) collective-permute-start(bf16[256,2048]{1,0:T(8,128)(2,1)} %get-tuple-element.240), channel_id=1, source_target_pairs={{0,4},{4,0},{8,12},{12,8},{16,20},{20,16},{24,28},{28,24},{1,5},{5... | collective-permute-start | bytes 3145736 | tf_op jit(solution)/shard_map/ppermute | solution.py:492
  133.5 25.4 %collective-permute-start.27 = (bf16[256,2048]{1,0:T(8,128)(2,1)}, bf16[256,2048]{1,0:T(8,128)(2,1)S(1)}, u32[]{:S(2)}, u32[]{:S(2)}) collective-permute-start(bf16[256,2048]{1,0:T(8,128)(2,1)} %get-tuple-element.240), channel_id=1, source_target_pairs={{0,8},{4,12},{8,0},{12,4},{16,24},{20,28},{24,16},{28,20},{1,9},{5... | collective-permute-start | bytes 3145736 | tf_op jit(solution)/shard_map/ppermute | solution.py:492
  134.6 24.3 %collective-permute-start.29 = (bf16[256,2048]{1,0:T(8,128)(2,1)}, bf16[256,2048]{1,0:T(8,128)(2,1)S(1)}, u32[]{:S(2)}, u32[]{:S(2)}) collective-permute-start(bf16[256,2048]{1,0:T(8,128)(2,1)} %get-tuple-element.240), channel_id=1, source_target_pairs={{0,1},{1,0},{2,3},{3,2},{4,5},{5,4},{6,7},{7,6},{8,9},{9,8},{10,11... | collective-permute-start | bytes 3145736 | tf_op jit(solution)/shard_map/ppermute | solution.py:481
  159.6 27.6 %collective-permute-start.33 = (bf16[256,2048]{1,0:T(8,128)(2,1)}, bf16[256,2048]{1,0:T(8,128)(2,1)S(1)}, u32[]{:S(2)}, u32[]{:S(2)}) collective-permute-start(bf16[256,2048]{1,0:T(8,128)(2,1)} %collective-permute-done.25), channel_id=1, source_target_pairs={{0,8},{4,12},{8,0},{12,4},{16,24},{20,28},{24,16},{28,20},{1,9},{5... | collective-permute-start | bytes 3145736 | tf_op jit(solution)/shard_map/ppermute | solution.py:492
  160.6 26.5 %collective-permute-start.32 = (bf16[256,2048]{1,0:T(8,128)(2,1)S(1)}, bf16[256,2048]{1,0:T(8,128)(2,1)S(1)}, u32[]{:S(2)}, u32[]{:S(2)}) collective-permute-start(bf16[256,2048]{1,0:T(8,128)(2,1)S(1)} %collective-permute-done.26.refs_4_.refs_8_.refs_0_), channel_id=1, source_target_pairs={{0,2},{1,3},{2,0},{3,1},{4,6},{5,7},{6,4},{7,5},{8,10},{9,11},{10,... | collective-permute-start | bytes 3145736 | tf_op jit(solution)/shard_map/ppermute | solution.py:485
  161.4 27.7 %collective-permute-start.36 = (bf16[256,2048]{1,0:T(8,128)(2,1)S(1)}, bf16[256,2048]{1,0:T(8,128)(2,1)S(1)}, u32[]{:S(2)}, u32[]{:S(2)}) collective-permute-start(bf16[256,2048]{1,0:T(8,128)(2,1)S(1)} %collective-permute-done.26.refs_4_.refs_8_.refs_0_), channel_id=1, source_target_pairs={{0,1},{1,0},{2,3},{3,2},{4,5},{5,4},{6,7},{7,6},{8,9},{9,8},{10,11... | collective-permute-start | bytes 3145736 | tf_op jit(solution)/shard_map/ppermute | solution.py:481
  161.4 25.7 %collective-permute-start.31 = (bf16[256,2048]{1,0:T(8,128)(2,1)S(1)}, bf16[256,2048]{1,0:T(8,128)(2,1)}, u32[]{:S(2)}, u32[]{:S(2)}) collective-permute-start(bf16[256,2048]{1,0:T(8,128)(2,1)S(1)} %collective-permute-done.27.refs_8_.refs_12_.refs_4_), channel_id=1, source_target_pairs={{0,4},{4,0},{8,12},{12,8},{16,20},{20,16},{24,28},{28,24},{1,5},{5... | collective-permute-start | bytes 3145736 | tf_op jit(solution)/shard_map/ppermute | solution.py:492
  162.7 26.7 %collective-permute-start.38 = (bf16[256,2048]{1,0:T(8,128)(2,1)S(1)}, bf16[256,2048]{1,0:T(8,128)(2,1)}, u32[]{:S(2)}, u32[]{:S(2)}) collective-permute-start(bf16[256,2048]{1,0:T(8,128)(2,1)S(1)} %collective-permute-done.27.refs_8_.refs_12_.refs_4_), channel_id=1, source_target_pairs={{0,1},{1,0},{2,3},{3,2},{4,5},{5,4},{6,7},{7,6},{8,9},{9,8},{10,11... | collective-permute-start | bytes 3145736 | tf_op jit(solution)/shard_map/ppermute | solution.py:481
  187.2 19.2 %collective-permute-start.37 = (bf16[256,2048]{1,0:T(8,128)(2,1)S(1)}, bf16[256,2048]{1,0:T(8,128)(2,1)}, u32[]{:S(2)}, u32[]{:S(2)}) collective-permute-start(bf16[256,2048]{1,0:T(8,128)(2,1)S(1)} %collective-permute-done.32.refs_6_.refs_10_.refs_2_), channel_id=1, source_target_pairs={{0,1},{1,0},{2,3},{3,2},{4,5},{5,4},{6,7},{7,6},{8,9},{9,8},{10,11... | collective-permute-start | bytes 3145736 | tf_op jit(solution)/shard_map/ppermute | solution.py:481
  187.3 19.0 %collective-permute-start.39 = (bf16[256,2048]{1,0:T(8,128)(2,1)S(1)}, bf16[256,2048]{1,0:T(8,128)(2,1)}, u32[]{:S(2)}, u32[]{:S(2)}) collective-permute-start(bf16[256,2048]{1,0:T(8,128)(2,1)S(1)} %collective-permute-done.33.refs_10_.refs_14_.refs_6_), channel_id=1, source_target_pairs={{0,1},{1,0},{2,3},{3,2},{4,5},{5,4},{6,7},{7,6},{8,9},{9,8},{10,11... | collective-permute-start | bytes 3145736 | tf_op jit(solution)/shard_map/ppermute | solution.py:481
  187.9 18.5 %collective-permute-start.34 = (bf16[128,2048]{1,0:T(8,128)(2,1)S(1)}, bf16[128,2048]{1,0:T(8,128)(2,1)}, u32[]{:S(2)}, u32[]{:S(2)}) collective-permute-start(bf16[128,2048]{1,0:T(8,128)(2,1)S(1)} %slice.147), channel_id=1, source_target_pairs={{0,4},{4,0},{8,12},{12,8},{16,20},{20,16},{24,28},{28,24},{1,5},{5... | collective-permute-start | bytes 1572872 | tf_op jit(solution)/shard_map/ppermute | solution.py:492
  208.4 30.1 %collective-permute-start.46 = (bf16[1024,384]{1,0:T(8,128)(2,1)}, bf16[1024,384]{1,0:T(8,128)(2,1)}, u32[]{:S(2)}, u32[]{:S(2)}) collective-permute-start(bf16[1024,384]{1,0:T(8,128)(2,1)} %get-tuple-element.402), channel_id=1, source_target_pairs={{0,4},{4,0},{8,12},{12,8},{16,20},{20,16},{24,28},{28,24},{1,5},{5... | collective-permute-start | bytes 2359304 | tf_op jit(solution)/shard_map/ppermute | solution.py:492
  209.4 29.2 %collective-permute-start.47 = (bf16[1024,384]{1,0:T(8,128)(2,1)}, bf16[1024,384]{1,0:T(8,128)(2,1)}, u32[]{:S(2)}, u32[]{:S(2)}) collective-permute-start(bf16[1024,384]{1,0:T(8,128)(2,1)} %get-tuple-element.401), channel_id=1, source_target_pairs={{0,8},{4,12},{8,0},{12,4},{16,24},{20,28},{24,16},{28,20},{1,9},{5... | collective-permute-start | bytes 2359304 | tf_op jit(solution)/shard_map/ppermute | solution.py:492
  221.3 27.4 %collective-permute-start.45 = (bf16[128,2048]{1,0:T(8,128)(2,1)}, bf16[128,2048]{1,0:T(8,128)(2,1)}, u32[]{:S(2)}, u32[]{:S(2)}) collective-permute-start(bf16[128,2048]{1,0:T(8,128)(2,1)} %get-tuple-element.266), channel_id=1, source_target_pairs={{0,16},{4,20},{8,24},{12,28},{16,0},{20,4},{24,8},{28,12},{1,17},{... | collective-permute-start | bytes 1572872 | tf_op jit(solution)/shard_map/ppermute | solution.py:492
  224.0 53.2 %collective-permute-start.44 = (bf16[1024,384]{1,0:T(8,128)(2,1)S(1)}, bf16[1024,384]{1,0:T(8,128)(2,1)S(1)}, u32[]{:S(2)}, u32[]{:S(2)}) collective-permute-start(bf16[1024,384]{1,0:T(8,128)(2,1)S(1)} %constant_dynamic-slice_fusion.4), channel_id=1, source_target_pairs={{0,12},{4,8},{8,4},{12,0},{16,28},{20,24},{24,20},{28,16},{1,13},{... | collective-permute-start | bytes 2359304 | tf_op jit(solution)/shard_map/ppermute | solution.py:492
  225.7 51.5 %collective-permute-start.43 = (bf16[128,2048]{1,0:T(8,128)(2,1)}, bf16[128,2048]{1,0:T(8,128)(2,1)S(1)}, u32[]{:S(2)}, u32[]{:S(2)}) collective-permute-start(bf16[128,2048]{1,0:T(8,128)(2,1)} %get-tuple-element.264), channel_id=1, source_target_pairs={{0,16},{4,20},{8,24},{12,28},{16,0},{20,4},{24,8},{28,12},{1,17},{... | collective-permute-start | bytes 1572872 | tf_op jit(solution)/shard_map/ppermute | solution.py:492
  249.9 41.1 %collective-permute-start.48 = (bf16[128,2048]{1,0:T(8,128)(2,1)S(1)}, bf16[128,2048]{1,0:T(8,128)(2,1)S(1)}, u32[]{:S(2)}, u32[]{:S(2)}) collective-permute-start(bf16[128,2048]{1,0:T(8,128)(2,1)S(1)} %add_convert_fusion.10), channel_id=1, source_target_pairs={{0,8},{4,12},{8,0},{12,4},{16,24},{20,28},{24,16},{28,20},{1,9},{5... | collective-permute-start | bytes 1572872 | tf_op jit(solution)/shard_map/ppermute | solution.py:492
  251.5 53.4 %collective-permute-start.50 = (bf16[128,2048]{1,0:T(8,128)(2,1)}, bf16[128,2048]{1,0:T(8,128)(2,1)S(1)}, u32[]{:S(2)}, u32[]{:S(2)}) collective-permute-start(bf16[128,2048]{1,0:T(8,128)(2,1)} %get-tuple-element.283), channel_id=1, source_target_pairs={{0,16},{4,20},{8,24},{12,28},{16,0},{20,4},{24,8},{28,12},{1,17},{... | collective-permute-start | bytes 1572872 | tf_op jit(solution)/shard_map/ppermute | solution.py:492
  294.2 24.5 %collective-permute-start.52 = (bf16[256,2048]{1,0:T(8,128)(2,1)S(1)}, bf16[256,2048]{1,0:T(8,128)(2,1)S(1)}, u32[]{:S(2)}, u32[]{:S(2)}) collective-permute-start(bf16[256,2048]{1,0:T(8,128)(2,1)S(1)} %pad_maximum_fusion.5.refs_0_.refs_2_), channel_id=1, source_target_pairs={{0,4},{4,0},{8,12},{12,8},{16,20},{20,16},{24,28},{28,24},{1,5},{5... | collective-permute-start | bytes 3145736 | tf_op jit(solution)/shard_map/ppermute | solution.py:492
  319.7 24.9 %collective-permute-start.54 = (bf16[256,2048]{1,0:T(8,128)(2,1)S(1)}, bf16[256,2048]{1,0:T(8,128)(2,1)S(1)}, u32[]{:S(2)}, u32[]{:S(2)}) collective-permute-start(bf16[256,2048]{1,0:T(8,128)(2,1)S(1)} %pad_maximum_fusion.6.refs_1_.refs_3_), channel_id=1, source_target_pairs={{0,4},{4,0},{8,12},{12,8},{16,20},{20,16},{24,28},{28,24},{1,5},{5... | collective-permute-start | bytes 3145736 | tf_op jit(solution)/shard_map/ppermute | solution.py:492
  320.1 24.3 %collective-permute-start.49 = (bf16[128,2048]{1,0:T(8,128)(2,1)S(1)}, bf16[128,2048]{1,0:T(8,128)(2,1)S(1)}, u32[]{:S(2)}, u32[]{:S(2)}) collective-permute-start(bf16[128,2048]{1,0:T(8,128)(2,1)S(1)} %copy-done.53), channel_id=1, source_target_pairs={{0,16},{4,20},{8,24},{12,28},{16,0},{20,4},{24,8},{28,12},{1,17},{... | collective-permute-start | bytes 1572872 | tf_op jit(solution)/shard_map/ppermute | solution.py:492
  321.1 23.5 %collective-permute-start.53 = (bf16[128,2048]{1,0:T(8,128)(2,1)S(1)}, bf16[128,2048]{1,0:T(8,128)(2,1)S(1)}, u32[]{:S(2)}, u32[]{:S(2)}) collective-permute-start(bf16[128,2048]{1,0:T(8,128)(2,1)S(1)} %add_convert_fusion.8), channel_id=1, source_target_pairs={{0,8},{4,12},{8,0},{12,4},{16,24},{20,28},{24,16},{28,20},{1,9},{5... | collective-permute-start | bytes 1572872 | tf_op jit(solution)/shard_map/ppermute | solution.py:492
  345.7 27.6 %collective-permute-start.58 = (bf16[256,2048]{1,0:T(8,128)(2,1)S(1)}, bf16[256,2048]{1,0:T(8,128)(2,1)S(1)}, u32[]{:S(2)}, u32[]{:S(2)}) collective-permute-start(bf16[256,2048]{1,0:T(8,128)(2,1)S(1)} %pad_maximum_fusion.7.refs_1_.refs_3_), channel_id=1, source_target_pairs={{0,4},{4,0},{8,12},{12,8},{16,20},{20,16},{24,28},{28,24},{1,5},{5... | collective-permute-start | bytes 3145736 | tf_op jit(solution)/shard_map/ppermute | solution.py:492
  346.3 26.9 %collective-permute-start.56 = (bf16[128,2048]{1,0:T(8,128)(2,1)}, bf16[128,2048]{1,0:T(8,128)(2,1)S(1)}, u32[]{:S(2)}, u32[]{:S(2)}) collective-permute-start(bf16[128,2048]{1,0:T(8,128)(2,1)} %get-tuple-element.299), channel_id=1, source_target_pairs={{0,16},{4,20},{8,24},{12,28},{16,0},{20,4},{24,8},{28,12},{1,17},{... | collective-permute-start | bytes 1572872 | tf_op jit(solution)/shard_map/ppermute | solution.py:492
  348.1 25.1 %collective-permute-start.57 = (bf16[128,2048]{1,0:T(8,128)(2,1)S(1)}, bf16[128,2048]{1,0:T(8,128)(2,1)S(1)}, u32[]{:S(2)}, u32[]{:S(2)}) collective-permute-start(bf16[128,2048]{1,0:T(8,128)(2,1)S(1)} %add_convert_fusion.7), channel_id=1, source_target_pairs={{0,8},{4,12},{8,0},{12,4},{16,24},{20,28},{24,16},{28,20},{1,9},{5... | collective-permute-start | bytes 1572872 | tf_op jit(solution)/shard_map/ppermute | solution.py:492
  350.6 48.0 %collective-permute-start.55 = (bf16[512,512]{1,0:T(8,128)(2,1)}, bf16[512,512]{1,0:T(8,128)(2,1)}, u32[]{:S(2)}, u32[]{:S(2)}) collective-permute-start(bf16[512,512]{1,0:T(8,128)(2,1)} %get-tuple-element.298), channel_id=1, source_target_pairs={{0,16},{4,20},{8,24},{12,28},{16,0},{20,4},{24,8},{28,12},{1,17},{... | collective-permute-start | bytes 1572872 | tf_op jit(solution)/shard_map/ppermute | solution.py:492
  377.7 25.9 %collective-permute-start.60 = (bf16[256,2048]{1,0:T(8,128)(2,1)S(1)}, bf16[256,2048]{1,0:T(8,128)(2,1)}, u32[]{:S(2)}, u32[]{:S(2)}) collective-permute-start(bf16[256,2048]{1,0:T(8,128)(2,1)S(1)} %pad_maximum_fusion.8.refs_1_.refs_3_), channel_id=1, source_target_pairs={{0,4},{4,0},{8,12},{12,8},{16,20},{20,16},{24,28},{28,24},{1,5},{5... | collective-permute-start | bytes 3145736 | tf_op jit(solution)/shard_map/ppermute | solution.py:492
  378.8 24.8 %collective-permute-start.59 = (bf16[128,2048]{1,0:T(8,128)(2,1)}, bf16[128,2048]{1,0:T(8,128)(2,1)}, u32[]{:S(2)}, u32[]{:S(2)}) collective-permute-start(bf16[128,2048]{1,0:T(8,128)(2,1)} %add_convert_fusion.6), channel_id=1, source_target_pairs={{0,8},{4,12},{8,0},{12,4},{16,24},{20,28},{24,16},{28,20},{1,9},{5... | collective-permute-start | bytes 1572872 | tf_op jit(solution)/shard_map/ppermute | solution.py:492
  403.6 32.1 %collective-permute-start.64 = (bf16[2,256,2048]{2,1,0:T(8,128)(2,1)S(1)}, bf16[2,256,2048]{2,1,0:T(8,128)(2,1)S(1)}, u32[]{:S(2)}, u32[]{:S(2)}) collective-permute-start(bf16[2,256,2048]{2,1,0:T(8,128)(2,1)S(1)} %pad_maximum_fusion.1), channel_id=1, source_target_pairs={{0,1},{1,0},{2,3},{3,2},{4,5},{5,4},{6,7},{7,6},{8,9},{9,8},{10,11... | collective-permute-start | bytes 6291464 | tf_op jit(solution)/shard_map/ppermute | solution.py:481
  407.7 28.0 %collective-permute-start.63 = (bf16[256,2048]{1,0:T(8,128)(2,1)S(1)}, bf16[256,2048]{1,0:T(8,128)(2,1)S(1)}, u32[]{:S(2)}, u32[]{:S(2)}) collective-permute-start(bf16[256,2048]{1,0:T(8,128)(2,1)S(1)} %pad_maximum_fusion.9.refs_0_.refs_2_), channel_id=1, source_target_pairs={{0,4},{4,0},{8,12},{12,8},{16,20},{20,16},{24,28},{28,24},{1,5},{5... | collective-permute-start | bytes 3145736 | tf_op jit(solution)/shard_map/ppermute | solution.py:492
  409.0 25.5 %collective-permute-start.61 = (bf16[512,512]{1,0:T(8,128)(2,1)S(1)}, bf16[512,512]{1,0:T(8,128)(2,1)S(1)}, u32[]{:S(2)}, u32[]{:S(2)}) collective-permute-start(bf16[512,512]{1,0:T(8,128)(2,1)S(1)} %copy-done.46), channel_id=1, source_target_pairs={{0,16},{4,20},{8,24},{12,28},{16,0},{20,4},{24,8},{28,12},{1,17},{... | collective-permute-start | bytes 1572872 | tf_op jit(solution)/shard_map/ppermute | solution.py:492
  410.5 25.2 %collective-permute-start.62 = (bf16[512,512]{1,0:T(8,128)(2,1)S(1)}, bf16[512,512]{1,0:T(8,128)(2,1)S(1)}, u32[]{:S(2)}, u32[]{:S(2)}) collective-permute-start(bf16[512,512]{1,0:T(8,128)(2,1)S(1)} %add_convert_fusion.5), channel_id=1, source_target_pairs={{0,8},{4,12},{8,0},{12,4},{16,24},{20,28},{24,16},{28,20},{1,9},{5... | collective-permute-start | bytes 1572872 | tf_op jit(solution)/shard_map/ppermute | solution.py:492
  436.8 26.9 %collective-permute-start.69 = (bf16[256,2048]{1,0:T(8,128)(2,1)S(1)}, bf16[256,2048]{1,0:T(8,128)(2,1)S(1)}, u32[]{:S(2)}, u32[]{:S(2)}) collective-permute-start(bf16[256,2048]{1,0:T(8,128)(2,1)S(1)} %fusion.33), channel_id=1, source_target_pairs={{0,2},{1,3},{2,0},{3,1},{4,6},{5,7},{6,4},{7,5},{8,10},{9,11},{10,... | collective-permute-start | bytes 3145736 | tf_op jit(solution)/shard_map/ppermute | solution.py:489
  438.2 25.6 %collective-permute-start.68 = (bf16[1024,512]{1,0:T(8,128)(2,1)S(1)}, bf16[1024,512]{1,0:T(8,128)(2,1)S(1)}, u32[]{:S(2)}, u32[]{:S(2)}) collective-permute-start(bf16[1024,512]{1,0:T(8,128)(2,1)S(1)} %pad_maximum_fusion.10.refs_0_.refs_2_), channel_id=1, source_target_pairs={{0,4},{4,0},{8,12},{12,8},{16,20},{20,16},{24,28},{28,24},{1,5},{5... | collective-permute-start | bytes 3145736 | tf_op jit(solution)/shard_map/ppermute | solution.py:492
  439.5 23.9 %collective-permute-start.66 = (bf16[512,512]{1,0:T(8,128)(2,1)S(1)}, bf16[512,512]{1,0:T(8,128)(2,1)S(1)}, u32[]{:S(2)}, u32[]{:S(2)}) collective-permute-start(bf16[512,512]{1,0:T(8,128)(2,1)S(1)} %copy-done.45), channel_id=1, source_target_pairs={{0,16},{4,20},{8,24},{12,28},{16,0},{20,4},{24,8},{28,12},{1,17},{... | collective-permute-start | bytes 1572872 | tf_op jit(solution)/shard_map/ppermute | solution.py:492
  439.7 24.1 %collective-permute-start.67 = (bf16[512,512]{1,0:T(8,128)(2,1)S(1)}, bf16[512,512]{1,0:T(8,128)(2,1)S(1)}, u32[]{:S(2)}, u32[]{:S(2)}) collective-permute-start(bf16[512,512]{1,0:T(8,128)(2,1)S(1)} %add_convert_fusion.4), channel_id=1, source_target_pairs={{0,8},{4,12},{8,0},{12,4},{16,24},{20,28},{24,16},{28,20},{1,9},{5... | collective-permute-start | bytes 1572872 | tf_op jit(solution)/shard_map/ppermute | solution.py:492
  463.8 26.0 %collective-permute-start.71 = (bf16[1024,512]{1,0:T(8,128)(2,1)S(1)}, bf16[1024,512]{1,0:T(8,128)(2,1)S(1)}, u32[]{:S(2)}, u32[]{:S(2)}) collective-permute-start(bf16[1024,512]{1,0:T(8,128)(2,1)S(1)} %pad_maximum_fusion.11.refs_1_.refs_3_), channel_id=1, source_target_pairs={{0,4},{4,0},{8,12},{12,8},{16,20},{20,16},{24,28},{28,24},{1,5},{5... | collective-permute-start | bytes 3145736 | tf_op jit(solution)/shard_map/ppermute | solution.py:492
  464.9 24.6 %collective-permute-start.65 = (bf16[512,512]{1,0:T(8,128)(2,1)S(1)}, bf16[512,512]{1,0:T(8,128)(2,1)S(1)}, u32[]{:S(2)}, u32[]{:S(2)}) collective-permute-start(bf16[512,512]{1,0:T(8,128)(2,1)S(1)} %copy-done.44), channel_id=1, source_target_pairs={{0,16},{4,20},{8,24},{12,28},{16,0},{20,4},{24,8},{28,12},{1,17},{... | collective-permute-start | bytes 1572872 | tf_op jit(solution)/shard_map/ppermute | solution.py:492
  465.1 24.7 %collective-permute-start.70 = (bf16[512,512]{1,0:T(8,128)(2,1)S(1)}, bf16[512,512]{1,0:T(8,128)(2,1)S(1)}, u32[]{:S(2)}, u32[]{:S(2)}) collective-permute-start(bf16[512,512]{1,0:T(8,128)(2,1)S(1)} %add_convert_fusion.3), channel_id=1, source_target_pairs={{0,8},{4,12},{8,0},{12,4},{16,24},{20,28},{24,16},{28,20},{1,9},{5... | collective-permute-start | bytes 1572872 | tf_op jit(solution)/shard_map/ppermute | solution.py:492
  489.9 24.7 %collective-permute-start.75 = (bf16[1024,512]{1,0:T(8,128)(2,1)S(1)}, bf16[1024,512]{1,0:T(8,128)(2,1)S(1)}, u32[]{:S(2)}, u32[]{:S(2)}) collective-permute-start(bf16[1024,512]{1,0:T(8,128)(2,1)S(1)} %pad_maximum_fusion.12.refs_1_.refs_3_), channel_id=1, source_target_pairs={{0,4},{4,0},{8,12},{12,8},{16,20},{20,16},{24,28},{28,24},{1,5},{5... | collective-permute-start | bytes 3145736 | tf_op jit(solution)/shard_map/ppermute | solution.py:492
  491.4 21.6 %collective-permute-start.74 = (bf16[512,512]{1,0:T(8,128)(2,1)S(1)}, bf16[512,512]{1,0:T(8,128)(2,1)S(1)}, u32[]{:S(2)}, u32[]{:S(2)}) collective-permute-start(bf16[512,512]{1,0:T(8,128)(2,1)S(1)} %add_convert_fusion.2), channel_id=1, source_target_pairs={{0,8},{4,12},{8,0},{12,4},{16,24},{20,28},{24,16},{28,20},{1,9},{5... | collective-permute-start | bytes 1572872 | tf_op jit(solution)/shard_map/ppermute | solution.py:492
  491.5 19.3 %collective-permute-start.73 = (bf16[512,384]{1,0:T(8,128)(2,1)S(1)}, bf16[512,384]{1,0:T(8,128)(2,1)S(1)}, u32[]{:S(2)}, u32[]{:S(2)}) collective-permute-start(bf16[512,384]{1,0:T(8,128)(2,1)S(1)} %get-tuple-element.341), channel_id=1, source_target_pairs={{0,16},{4,20},{8,24},{12,28},{16,0},{20,4},{24,8},{28,12},{1,17},{... | collective-permute-start | bytes 1179656 | tf_op jit(solution)/shard_map/ppermute | solution.py:492
  514.7 25.2 %collective-permute-start.79 = (bf16[1024,512]{1,0:T(8,128)(2,1)S(1)}, bf16[1024,512]{1,0:T(8,128)(2,1)S(1)}, u32[]{:S(2)}, u32[]{:S(2)}) collective-permute-start(bf16[1024,512]{1,0:T(8,128)(2,1)S(1)} %pad_maximum_fusion.13.refs_1_.refs_3_), channel_id=1, source_target_pairs={{0,4},{4,0},{8,12},{12,8},{16,20},{20,16},{24,28},{28,24},{1,5},{5... | collective-permute-start | bytes 3145736 | tf_op jit(solution)/shard_map/ppermute | solution.py:492
  516.9 20.5 %collective-permute-start.77 = (bf16[512,384]{1,0:T(8,128)(2,1)S(1)}, bf16[512,384]{1,0:T(8,128)(2,1)S(1)}, u32[]{:S(2)}, u32[]{:S(2)}) collective-permute-start(bf16[512,384]{1,0:T(8,128)(2,1)S(1)} %get-tuple-element.353), channel_id=1, source_target_pairs={{0,16},{4,20},{8,24},{12,28},{16,0},{20,4},{24,8},{28,12},{1,17},{... | collective-permute-start | bytes 1179656 | tf_op jit(solution)/shard_map/ppermute | solution.py:492
  517.1 22.8 %collective-permute-start.78 = (bf16[512,384]{1,0:T(8,128)(2,1)S(1)}, bf16[512,384]{1,0:T(8,128)(2,1)S(1)}, u32[]{:S(2)}, u32[]{:S(2)}) collective-permute-start(bf16[512,384]{1,0:T(8,128)(2,1)S(1)} %add_convert_fusion.13), channel_id=1, source_target_pairs={{0,8},{4,12},{8,0},{12,4},{16,24},{20,28},{24,16},{28,20},{1,9},{5... | collective-permute-start | bytes 1179656 | tf_op jit(solution)/shard_map/ppermute | solution.py:492
  520.4 19.5 %collective-permute-start.80 = (f32[15872]{0:T(1024)S(1)}, f32[15872]{0:T(1024)S(1)}, u32[]{:S(2)}, u32[]{:S(2)}) collective-permute-start(f32[15872]{0:T(1024)S(1)} %pad_maximum_fusion.20), channel_id=1, source_target_pairs={{0,4},{4,0},{8,12},{12,8},{16,20},{20,16},{24,28},{28,24},{1,5},{5... | collective-permute-start | bytes 190472 | tf_op jit(solution)/shard_map/ppermute | solution.py:492
  521.4 30.4 %collective-permute-start.81 = (bf16[512,384]{1,0:T(8,128)(2,1)S(1)}, bf16[512,384]{1,0:T(8,128)(2,1)S(1)}, u32[]{:S(2)}, u32[]{:S(2)}) collective-permute-start(bf16[512,384]{1,0:T(8,128)(2,1)S(1)} %get-tuple-element.359), channel_id=1, source_target_pairs={{0,16},{4,20},{8,24},{12,28},{16,0},{20,4},{24,8},{28,12},{1,17},{... | collective-permute-start | bytes 1179656 | tf_op jit(solution)/shard_map/ppermute | solution.py:492
  540.0 19.7 %collective-permute-start.83 = (bf16[1024,384]{1,0:T(8,128)(2,1)S(1)}, bf16[1024,384]{1,0:T(8,128)(2,1)S(1)}, u32[]{:S(2)}, u32[]{:S(2)}) collective-permute-start(bf16[1024,384]{1,0:T(8,128)(2,1)S(1)} %pad_maximum_fusion.14.refs_0_.refs_2_), channel_id=1, source_target_pairs={{0,4},{4,0},{8,12},{12,8},{16,20},{20,16},{24,28},{28,24},{1,5},{5... | collective-permute-start | bytes 2359304 | tf_op jit(solution)/shard_map/ppermute | solution.py:492
  541.4 18.3 %collective-permute-start.82 = (bf16[512,384]{1,0:T(8,128)(2,1)S(1)}, bf16[512,384]{1,0:T(8,128)(2,1)S(1)}, u32[]{:S(2)}, u32[]{:S(2)}) collective-permute-start(bf16[512,384]{1,0:T(8,128)(2,1)S(1)} %add_convert_fusion.12), channel_id=1, source_target_pairs={{0,8},{4,12},{8,0},{12,4},{16,24},{20,28},{24,16},{28,20},{1,9},{5... | collective-permute-start | bytes 1179656 | tf_op jit(solution)/shard_map/ppermute | solution.py:492
  541.5 18.2 %collective-permute-start.84 = (f32[15872]{0:T(1024)S(1)}, f32[15872]{0:T(1024)S(1)}, u32[]{:S(2)}, u32[]{:S(2)}) collective-permute-start(f32[15872]{0:T(1024)S(1)} %fusion.48), channel_id=1, source_target_pairs={{0,8},{4,12},{8,0},{12,4},{16,24},{20,28},{24,16},{28,20},{1,9},{5... | collective-permute-start | bytes 190472 | tf_op jit(solution)/shard_map/ppermute | solution.py:492
  559.7 17.7 %collective-permute-start.87 = (bf16[1024,384]{1,0:T(8,128)(2,1)S(1)}, bf16[1024,384]{1,0:T(8,128)(2,1)S(1)}, u32[]{:S(2)}, u32[]{:S(2)}) collective-permute-start(bf16[1024,384]{1,0:T(8,128)(2,1)S(1)} %pad_maximum_fusion.15.refs_1_.refs_3_), channel_id=1, source_target_pairs={{0,4},{4,0},{8,12},{12,8},{16,20},{20,16},{24,28},{28,24},{1,5},{5... | collective-permute-start | bytes 2359304 | tf_op jit(solution)/shard_map/ppermute | solution.py:492
  577.5 17.7 %collective-permute-start.92 = (bf16[1024,384]{1,0:T(8,128)(2,1)S(1)}, bf16[1024,384]{1,0:T(8,128)(2,1)S(1)}, u32[]{:S(2)}, u32[]{:S(2)}) collective-permute-start(bf16[1024,384]{1,0:T(8,128)(2,1)S(1)} %pad_maximum_fusion.16.refs_1_.refs_3_), channel_id=1, source_target_pairs={{0,4},{4,0},{8,12},{12,8},{16,20},{20,16},{24,28},{28,24},{1,5},{5... | collective-permute-start | bytes 2359304 | tf_op jit(solution)/shard_map/ppermute | solution.py:492
  (108 other events, 1179.1 us)

commit v14 on v13

--- a/solution.py
+++ b/solution.py
@@ -513,10 +513,6 @@
         across = [flip(block, 2) for block in over_y]
         return corner, beside, across
 
-    def last_far(second):
-        half = rows // 2
-        return [(flip(v[:half], 1), flip(u[half:], 2)) for u, v in zip(second[1], second[2])]
-
     def meet(*trees):
         leaves, shape = jax.tree.flatten(trees)
         return jax.tree.unflatten(shape, lax.optimization_barrier(tuple(leaves)))
@@ -661,18 +657,19 @@
     grad_qkv = attend_back(qkv_low, grad_context, log_total, prefix_len, spots, table)
     grad_qkv, grad_near, grad_second = meet(grad_qkv, grad_near, grad_second)
 
-    grad_last = last_far(grad_second)
     corner, beside, across = grad_second
+    grad_last = [flip(block, 1) for block in across]
     ahead = [grad_first[0]] + beside + [grad_first[1]] + across + [corner]
     mates = [to_core(block) for block in ahead]
-    swapped = [flip(quarter_of(grad_qkv, 1, quarter ^ m), m) for m in (1, 2)]
+    swapped_z = flip(quarter_of(grad_qkv, 1, quarter ^ 2), 2)
     hidden_pre = jnp.concatenate([pre_own, pre_rest], axis=0)
     grad_inner = (contract(grad_near, fc2_weight, 1, 1) * exact_gelu(hidden_pre)[1]).astype(BF)
-    grad_inner, grad_last, mates = meet(grad_inner, grad_last, mates)
-
-    last_mates = [tuple(to_core(v) for v in pair) for pair in grad_last]
+    grad_inner, grad_last, mates, swapped_z = meet(grad_inner, grad_last, mates, swapped_z)
+
+    swapped_x = flip(quarter_of(grad_qkv, 1, quarter ^ 1), 1)
+    ahead += grad_last
+    mates += [to_core(block) for block in grad_last]
     grad_far = [block for pair in zip(ahead, mates) for block in pair]
-    halves = [v for pair, mate in zip(grad_last, last_mates) for v in pair + mate]
 
     queue = []
     due = {}
@@ -786,7 +783,7 @@
         return whole
 
     half = active_far.shape[1] // 2
-    rights = [grad_near] + grad_far + halves
+    rights = [grad_near] + grad_far
 
     def hidden_lefts(part):
         return [
@@ -809,9 +806,7 @@
     )
     enqueue("fc2", *parts)
     enqueue("out", out_part)
-    swapped = turn(*swapped)
-    halves = lax.optimization_barrier((token[0], *halves))[1:]
-    grad_far += [jnp.concatenate(halves[i : i + 2], axis=0) for i in range(0, len(halves), 2)]
+    (swapped_x,) = turn(swapped_x)
     grad_inner_far = back_blocks([gate(grad_far[0])] + grad_far[1:], fc2_quarter, slope_far)
     (grad_inner_far,) = turn(grad_inner_far)
     inner_quarter = gate(quarter_of(grad_inner, 1, quarter))
@@ -852,11 +847,11 @@
     qkv_part = (
         contract(norm_attn_own, qkv_quarter[:close], 0, 0)
         + contract(norm_attn_rest, qkv_quarter[close:], 0, 0)
-        + contract(norm_attn_far, jnp.concatenate([*swapped, *grad_qkv_far], axis=0), 0, 0)
+        + contract(norm_attn_far, jnp.concatenate([swapped_x, swapped_z, *grad_qkv_far], axis=0), 0, 0)
     )
     qkv_part, mates, tensor_parts = turn(qkv_part.astype(BF), mates, tensor_parts)
     walk(last_walk(kept, mates, tensor_parts, others, outcome))
-    enqueue("qkv", *cut(qkv_part, [4, 4, 4, 2, 1, 1]))
+    enqueue("qkv", *cut(qkv_part, [4, 4, 4, 4]))
     axes = {"fc2": 0, "out": 0, "fc1": 1, "qkv": 1}
     placed = {name: (None, 0, 0) for name in axes}
 

time: 631 us -> 636 us (level)
  waiting for transfers between devices: 189 us -> 200 us
  starting transfers between devices: 90.5 us -> 82.3 us
    ppermute x68 -> x61, waiting for transfers between devices: 185 us -> 193 us  [flip(): return lax.ppermute(v, 'dp', [(d, d ^ mask) for d in range(dp)])]
    ppermute x68 -> x61, starting transfers between devices: 77.9 us -> 70.3 us  [flip(): return lax.ppermute(v, 'dp', [(d, d ^ mask) for d in range(dp)])]
    pallas_call x15 -> x13, Pallas kernels: 34.4 us -> 33.2 us  [place_quarters(): pl.pallas_call(place_kernel, grid_spec=pltpu.PrefetchScalarGridSpec(num_s...]
  transfers between devices with their start and end apart: 98 -> 90, of which waited for: 38 -> 35; matrix products, arithmetic and copies ran while one was open for 23% -> 23% of each run, Pallas kernels for 28% -> 27%
where the time goes in v14:
time: 636 us; the launch traced here: 626 us
  waiting for transfers between devices  200 us (31%)
  Pallas kernels  175 us (28%)
  matrix products  94.6 us (15%)
  starting transfers between devices  82.3 us (13%)
  local copies, waits for them, and re-layouts  40.3 us (6%)
  other arithmetic  27.2 us (4%)
  between operations  6.84 us (1%)
    ppermute x61, waiting for transfers between devices, flip(): return lax.ppermute(v, 'dp', [(d, d ^ mask) for d in range(dp)])  193 us
    ppermute x61, starting transfers between devices, flip(): return lax.ppermute(v, 'dp', [(d, d ^ mask) for d in range(dp)])  70.3 us
    dot_general x8, matrix products, contract(): lax.dot_general(left_side, right_side, (((left_dim,), (right_dim,)), ((),...  46.6 us
    pallas_call x2, Pallas kernels, norm_back(): pl.pallas_call(functools.partial(norm_back_kernel, count), grid=(count,),...  38.3 us
    pallas_call x13, Pallas kernels, place_quarters(): pl.pallas_call(place_kernel, grid_spec=pltpu.PrefetchScalarGridSpec(num_s...  33.2 us
    pallas_call x4, Pallas kernels, both_norms(): pl.pallas_call(functools.partial(norms_kernel, count), grid=(count,), in_...  29.9 us
    pallas_call x2, Pallas kernels, outer_blocks(): pl.pallas_call(functools.partial(outer_kernel, len(lefts), pieces, len(si...  23.5 us
    dot_general x2, matrix products, units(): jnp.dot(normed, fc1_weight, preferred_element_type=F32)  21.3 us
  transfers between devices with their start and end apart: 90, of which 35 were waited for; matrix products, arithmetic and copies ran while one was open for 23% of the time, Pallas kernels for 27%

profile of v14, /device:TPU:0, one launch (start us, length us, event | category | flops | bytes accessed | tf_op | source)
XLA Modules:
  0.0 626.0 jit_solution(16941424922014907014)
XLA Ops:
  1.2 2.6 collective-permute-start.2
  13.1 4.4 both_norms.4
  17.5 10.4 %multiply_convert_fusion.2 = (bf16[512,2048]{1,0:T(8,128)(2,1)}, f32[512,2048]{1,0:T(8,128)}) fusion(f32[2048]{0:T(1024)S(1)} %convert_element_type.232, bf16[512,2048]{1,0:T(8,128)(2,1)} %get-tuple-element.189, bf16[2048,2048]{1,0:T(8,128)(2,1)} %fc1_ref.3), kind=kOutput, calls=%fused_computation.18 | convolution fusion | flops 4301258752 | bytes 16785408 | tf_op jit(solution)/shard_map/dot_general | solution.py:535
  37.1 4.6 both_norms.5
  45.5 10.9 %qkv_rotary.1.q_ref.k_ref.v_ref = bf16[1024,1536]{1,0:T(8,128)(2,1)S(1)} custom-call(bf16[512,2048]{1,0:T(8,128)(2,1)S(1)} %copy-done.6, bf16[512,2048]{1,0:T(8,128)(2,1)S(1)} %get-tuple-element.195.rest_ref, bf16[2048,1536]{1,0:T(8,128)(2,1)} %qkv_ref.3, bf16[1,1536]{1,0:T(2,128)(2,1)S(1)} %broadcast_in_dim.11.b_ref, f32[1024,384]{1,0:T(8,128)S(1)} %copy-done.3, ...), custom_call_target="tpu_custom_call" | custom-call | flops 1048576 | bytes 65536 | tf_op jit(solution)/shard_map/qkv_rotary/pallas_call | solution.py:94
  56.4 9.6 %attend.1 = (bf16[1024,512]{1,0:T(8,128)(2,1)S(1)}, f32[2,1024,1]{2,1,0:T(8,128)S(1)}) custom-call(s32[1]{0:T(128)S(6)} %copy.64.prefix_ref, bf16[1024,1536]{1,0:T(8,128)(2,1)S(1)} %qkv_rotary.1.q_ref.k_ref.v_ref, bf16[1024,1536]{1,0:T(8,128)(2,1)S(1)} %qkv_rotary.1.q_ref.k_ref.v_ref, bf16[1024,1536]{1,0:T(8,128)(2,1)S(1)} %qkv_rotary.1.q_ref.k_ref.v_ref, ...), custom_call_target="tpu_custom_call" | custom-call | flops 1048576 | bytes 65536 | tf_op jit(solution)/shard_map/attend/pallas_call | solution.py:137
  69.8 10.9 %multiply_convert_fusion.1 = (bf16[512,2048]{1,0:T(8,128)(2,1)S(1)}, f32[512,2048]{1,0:T(8,128)}) fusion(f32[2048]{0:T(1024)S(1)} %convert_element_type.232, bf16[512,2048]{1,0:T(8,128)(2,1)S(1)} %copy-done.41, bf16[2048,2048]{1,0:T(8,128)(2,1)} %fc1_ref.3), kind=kOutput, calls=%fused_computation.17 | convolution fusion | flops 4301258752 | bytes 16785408 | tf_op jit(solution)/shard_map/dot_general | solution.py:535
  83.1 4.5 fusion.55
  90.2 4.5 fusion.56
  102.8 2.6 collective-permute-start.23
  105.5 16.2 %both_norms.6 = (bf16[3072,2048]{1,0:T(8,128)(2,1)}, bf16[3072,2048]{1,0:T(8,128)(2,1)}) custom-call(bf16[4,2048]{1,0:T(4,128)(2,1)S(1)} %pad_maximum_fusion.18.refs_0_.gains_ref, bf16[256,2048]{1,0:T(8,128)(2,1)} %collective-permute-done.2.refs_1_, bf16[256,2048]{1,0:T(8,128)(2,1)S(1)} %collective-permute-done.16.refs_2_, ...), custom_call_target="tpu_custom_call" | custom-call | flops 1048576 | bytes 65536 | tf_op jit(solution)/shard_map/both_norms/pallas_call | solution.py:354
  123.6 2.4 collective-permute-done.21
  127.2 4.2 fusion.51
  135.1 4.7 both_norms.7
  139.8 14.7 %fusion.9 = (f32[3072,512]{1,0:T(8,128)}, bf16[3072,512]{1,0:T(8,128)(2,1)}) fusion(f32[512]{0:T(512)S(1)} %dynamic-slice_convert_fusion, bf16[3072,2048]{1,0:T(8,128)(2,1)} %get-tuple-element.229, bf16[2048,2048]{1,0:T(8,128)(2,1)} %fc1_ref.3, s32[]{:T(128)S(6)} %select_n.81), kind=kOutput, calls=%fused_computation.12 | convolution fusion | flops 6459752448 | bytes 24119300 | tf_op jit(solution)/shard_map/dot_general | solution.py:642
  156.2 3.2 constant_dynamic-slice_fusion.6.weight_ref
  167.6 2.4 convolution_convert_fusion.g_ref
  170.9 11.8 %attend_back.1.grad_qkv_ref = bf16[1024,1536]{1,0:T(8,128)(2,1)} custom-call(s32[1]{0:T(128)S(6)} %copy.64.prefix_ref, bf16[1024,1536]{1,0:T(8,128)(2,1)} %copy-done.2, bf16[1024,1536]{1,0:T(8,128)(2,1)} %copy-done.2, bf16[1024,1536]{1,0:T(8,128)(2,1)} %copy-done.2, bf16[1024,512]{1,0:T(8,128)(2,1)S(1)} %convolution_convert_fusion.g_ref, ...), custom_call_target="tpu_custom_call" | custom-call | flops 1048576 | bytes 65536 | tf_op jit(solution)/shard_map/attend_back/pallas_call | solution.py:203
  182.7 5.0 collective-permute-done.31.refs_12_.refs_16_.refs_8_
  189.1 3.1 constant_dynamic-slice_fusion
  193.6 16.1 %fusion.5.grad_inner_ref = bf16[1024,2048]{1,0:T(8,128)(2,1)} fusion(f32[512,2048]{1,0:T(8,128)} %get-tuple-element.397, f32[512,2048]{1,0:T(8,128)} %get-tuple-element.395, bf16[1024,2048]{1,0:T(8,128)(2,1)S(1)} %constant_dynamic-update-slice_fusion.refs_3_.refs_7_, bf16[2048,2048]{1,0:T(8,128)(2,1)} %param.34), kind=kOutput, calls=%fused_computation.7 | convolution fusion | flops 8613003264 | bytes 25165824 | tf_op jit(solution)/shard_map/dot_general | solution.py:35
  209.7 2.8 collective-permute-done.40
  216.4 10.9 %outer_blocks.2 = (bf16[128,2048]{1,0:T(8,128)(2,1)}, bf16[128,2048]{1,0:T(8,128)(2,1)}) custom-call(s32[1]{0:T(128)} %bitcast.9._.quarter_ref, bf16[512,2048]{1,0:T(8,128)(2,1)} %get-tuple-element.206.refs_0_, bf16[512,2048]{1,0:T(8,128)(2,1)} %copy-done.38, bf16[3072,512]{1,0:T(8,128)(2,1)} %get-tuple-element.232.refs_2_, bf16[1024,2048]{1,0:T(8,128)(2,1)} %copy-done.25, ...), custom_call_target="tpu_custom_call" | custom-call | flops 1048576 | bytes 65536 | tf_op jit(solution)/shard_map/outer_blocks/pallas_call | solution.py:404
  227.3 2.7 collective-permute-start.44
  232.8 12.5 %outer_blocks.3 = (bf16[128,2048]{1,0:T(8,128)(2,1)}, bf16[128,2048]{1,0:T(8,128)(2,1)}, bf16[128,2048]{1,0:T(8,128)(2,1)}) custom-call(s32[1]{0:T(128)} %bitcast.9._.quarter_ref, bf16[512,2048]{1,0:T(8,128)(2,1)} %get-tuple-element.206.refs_0_, bf16[512,2048]{1,0:T(8,128)(2,1)} %copy-done.38, bf16[3072,512]{1,0:T(8,128)(2,1)} %get-tuple-element.232.refs_2_, ...), custom_call_target="tpu_custom_call" | custom-call | flops 1048576 | bytes 65536 | tf_op jit(solution)/shard_map/outer_blocks/pallas_call | solution.py:404
  245.3 9.1 %collective-permute-done.44 = bf16[128,2048]{1,0:T(8,128)(2,1)S(1)} collective-permute-done((bf16[128,2048]{1,0:T(8,128)(2,1)}, bf16[128,2048]{1,0:T(8,128)(2,1)S(1)}, u32[]{:S(2)}, u32[]{:S(2)}) %collective-permute-start.44) | collective-permute-done | bytes 524320 | tf_op jit(solution)/shard_map/ppermute | solution.py:492
  256.1 3.4 collective-permute-start.48
  259.5 17.6 %back_blocks.1 = bf16[3072,512]{1,0:T(8,128)(2,1)} custom-call(bf16[512,2048]{1,0:T(8,128)(2,1)} %constant_dynamic-slice_fusion.6.weight_ref, f32[3072,512]{1,0:T(8,128)} %get-tuple-element.368.slope_ref, bf16[256,2048]{1,0:T(8,128)(2,1)} %collective-permute-done.26.refs_4_.refs_8_.refs_0_, bf16[256,2048]{1,0:T(8,128)(2,1)} %copy-done.30, ...), custom_call_target="tpu_custom_call" | custom-call | flops 1048576 | bytes 65536 | tf_op jit(solution)/shard_map/back_blocks/pallas_call | solution.py:434
  277.1 13.4 %collective-permute-done.46 = bf16[128,2048]{1,0:T(8,128)(2,1)S(1)} collective-permute-done((bf16[128,2048]{1,0:T(8,128)(2,1)S(1)}, bf16[128,2048]{1,0:T(8,128)(2,1)S(1)}, u32[]{:S(2)}, u32[]{:S(2)}) %collective-permute-start.46) | collective-permute-done | bytes 524320 | tf_op jit(solution)/shard_map/ppermute | solution.py:492
  294.6 9.9 %add_convert_fusion = bf16[2048,512]{1,0:T(8,128)(2,1)S(1)} fusion(f32[2048,512]{1,0:T(8,128)S(1)} %fusion.36, f32[2048,512]{1,0:T(8,128)S(1)} %fusion.34, bf16[3072,2048]{1,0:T(8,128)(2,1)} %get-tuple-element.229, bf16[3072,512]{1,0:T(8,128)(2,1)S(1)} %copy-done.44), kind=kOutput, calls=%fused_computation.16 | convolution fusion | flops 6445596672 | bytes 26214400 | tf_op jit(solution)/shard_map/dot_general | solution.py:35
  304.6 5.4 collective-permute-done.49
  310.0 7.9 %collective-permute-done.50.refs_1_.refs_3_ = bf16[256,2048]{1,0:T(8,128)(2,1)S(1)} collective-permute-done((bf16[256,2048]{1,0:T(8,128)(2,1)S(1)}, bf16[256,2048]{1,0:T(8,128)(2,1)S(1)}, u32[]{:S(2)}, u32[]{:S(2)}) %collective-permute-start.50) | collective-permute-done | bytes 1048608 | tf_op jit(solution)/shard_map/ppermute | solution.py:492
  321.6 19.0 %norm_back.2 = (f32[512,2048]{1,0:T(8,128)}, f32[8,2048]{1,0:T(8,128)}, f32[8,1536]{1,0:T(8,128)}, f32[8,2048]{1,0:T(8,128)}) custom-call(bf16[1024,1536]{1,0:T(8,128)(2,1)} %attend_back.1.grad_qkv_ref, bf16[1024,2048]{1,0:T(8,128)(2,1)} %fusion.5.grad_inner_ref, bf16[2048,1536]{1,0:T(8,128)(2,1)} %qkv_ref.3, bf16[2048,2048]{1,0:T(8,128)(2,1)} %fc1_ref.3, ...), custom_call_target="tpu_custom_call" | custom-call | flops 1048576 | bytes 65536 | tf_op jit(solution)/shard_map/norm_back/pallas_call | solution.py:278
  349.7 19.3 %norm_back.3 = (f32[512,2048]{1,0:T(8,128)}, f32[8,2048]{1,0:T(8,128)}, f32[8,1536]{1,0:T(8,128)}, f32[8,2048]{1,0:T(8,128)}) custom-call(bf16[1024,1536]{1,0:T(8,128)(2,1)} %attend_back.1.grad_qkv_ref, bf16[1024,2048]{1,0:T(8,128)(2,1)} %fusion.5.grad_inner_ref, bf16[2048,1536]{1,0:T(8,128)(2,1)} %qkv_ref.3, bf16[2048,2048]{1,0:T(8,128)(2,1)} %fc1_ref.3, ...), custom_call_target="tpu_custom_call" | custom-call | flops 1048576 | bytes 65536 | tf_op jit(solution)/shard_map/norm_back/pallas_call | solution.py:278
  369.0 2.7 fusion.31
  372.3 2.9 fusion.40
  381.8 11.4 %add_convert_fusion.1 = bf16[2048,384]{1,0:T(8,128)(2,1)} fusion(f32[2048,384]{1,0:T(8,128)S(1)} %fusion.42, f32[2048,384]{1,0:T(8,128)S(1)} %fusion.40, bf16[3072,2048]{1,0:T(8,128)(2,1)} %get-tuple-element.290, bf16[1024,384]{1,0:T(8,128)(2,1)S(1)} %copy-done.73, bf16[1024,384]{1,0:T(8,128)(2,1)} %collective-permute-done.40, ...), kind=kOutput, calls=%fused_computation.21 | convolution fusion | flops 4841275392 | bytes 22806528 | tf_op jit(solution)/shard_map/dot_general | solution.py:35
  393.2 2.7 fusion.32
  399.7 4.0 collective-permute-done.57
  404.4 2.5 place_quarters.13.refs_0_
  413.4 22.1 %collective-permute-done.59 = bf16[512,512]{1,0:T(8,128)(2,1)S(1)} collective-permute-done((bf16[512,512]{1,0:T(8,128)(2,1)S(1)}, bf16[512,512]{1,0:T(8,128)(2,1)S(1)}, u32[]{:S(2)}, u32[]{:S(2)}) %collective-permute-start.59) | collective-permute-done | bytes 524320 | tf_op jit(solution)/shard_map/ppermute | solution.py:492
  440.2 2.5 collective-permute-start.65
  442.9 2.5 place_quarters.15
  445.4 2.4 place_quarters.14.refs_0_
  447.8 15.9 %collective-permute-done.64 = bf16[512,512]{1,0:T(8,128)(2,1)S(1)} collective-permute-done((bf16[512,512]{1,0:T(8,128)(2,1)S(1)}, bf16[512,512]{1,0:T(8,128)(2,1)S(1)}, u32[]{:S(2)}, u32[]{:S(2)}) %collective-permute-start.64) | collective-permute-done | bytes 524320 | tf_op jit(solution)/shard_map/ppermute | solution.py:492
  465.6 2.3 collective-permute-start.68
  467.9 2.4 place_quarters.17.refs_0_
  470.4 2.4 place_quarters.16.refs_0_
  472.8 17.1 %collective-permute-done.63 = bf16[512,512]{1,0:T(8,128)(2,1)S(1)} collective-permute-done((bf16[512,512]{1,0:T(8,128)(2,1)S(1)}, bf16[512,512]{1,0:T(8,128)(2,1)S(1)}, u32[]{:S(2)}, u32[]{:S(2)}) %collective-permute-start.63) | collective-permute-done | bytes 524320 | tf_op jit(solution)/shard_map/ppermute | solution.py:492
  495.1 2.4 place_quarters.19.refs_0_
  497.5 3.6 place_quarters.18
  501.1 10.1 %collective-permute-done.71 = bf16[512,384]{1,0:T(8,128)(2,1)S(1)} collective-permute-done((bf16[512,384]{1,0:T(8,128)(2,1)S(1)}, bf16[512,384]{1,0:T(8,128)(2,1)S(1)}, u32[]{:S(2)}, u32[]{:S(2)}) %collective-permute-start.71) | collective-permute-done | bytes 393248 | tf_op jit(solution)/shard_map/ppermute | solution.py:492
  517.5 2.3 collective-permute-start.76
  521.9 2.4 place_quarters.20.refs_0_
  524.3 10.9 %collective-permute-done.75 = bf16[512,384]{1,0:T(8,128)(2,1)S(1)} collective-permute-done((bf16[512,384]{1,0:T(8,128)(2,1)S(1)}, bf16[512,384]{1,0:T(8,128)(2,1)S(1)}, u32[]{:S(2)}, u32[]{:S(2)}) %collective-permute-start.75) | collective-permute-done | bytes 393248 | tf_op jit(solution)/shard_map/ppermute | solution.py:492
  535.3 5.0 collective-permute-done.78
  541.8 2.4 collective-permute-start.80
  544.2 2.5 place_quarters.21
  546.7 12.0 %collective-permute-done.79 = bf16[512,384]{1,0:T(8,128)(2,1)S(1)} collective-permute-done((bf16[512,384]{1,0:T(8,128)(2,1)S(1)}, bf16[512,384]{1,0:T(8,128)(2,1)S(1)}, u32[]{:S(2)}, u32[]{:S(2)}) %collective-permute-start.79) | collective-permute-done | bytes 393248 | tf_op jit(solution)/shard_map/ppermute | solution.py:492
  567.0 12.9 %collective-permute-done.83 = bf16[512,384]{1,0:T(8,128)(2,1)S(1)} collective-permute-done((bf16[512,384]{1,0:T(8,128)(2,1)S(1)}, bf16[512,384]{1,0:T(8,128)(2,1)S(1)}, u32[]{:S(2)}, u32[]{:S(2)}) %collective-permute-start.83) | collective-permute-done | bytes 393248 | tf_op jit(solution)/shard_map/ppermute | solution.py:492
  586.4 7.9 %collective-permute-done.87 = bf16[512,384]{1,0:T(8,128)(2,1)S(1)} collective-permute-done((bf16[512,384]{1,0:T(8,128)(2,1)S(1)}, bf16[512,384]{1,0:T(8,128)(2,1)S(1)}, u32[]{:S(2)}, u32[]{:S(2)}) %collective-permute-start.87) | collective-permute-done | bytes 393248 | tf_op jit(solution)/shard_map/ppermute | solution.py:492
  594.3 7.3 %collective-permute-done.88.refs_2_.refs_4_ = bf16[1024,384]{1,0:T(8,128)(2,1)S(1)} collective-permute-done((bf16[1024,384]{1,0:T(8,128)(2,1)S(1)}, bf16[1024,384]{1,0:T(8,128)(2,1)S(1)}, u32[]{:S(2)}, u32[]{:S(2)}) %collective-permute-start.88) | collective-permute-done | bytes 786464 | tf_op jit(solution)/shard_map/ppermute | solution.py:492
  609.4 11.0 %collective-permute-done.89.refs_2_.refs_4_ = bf16[1024,384]{1,0:T(8,128)(2,1)} collective-permute-done((bf16[1024,384]{1,0:T(8,128)(2,1)S(1)}, bf16[1024,384]{1,0:T(8,128)(2,1)}, u32[]{:S(2)}, u32[]{:S(2)}) %collective-permute-start.89) | collective-permute-done | bytes 786464 | tf_op jit(solution)/shard_map/ppermute | solution.py:492
  620.5 3.4 place_quarters.25
  (403 shorter events, 144.3 us)
Async XLA Ops:
  1.2 28.1 %collective-permute-start.2 = (bf16[256,2048]{1,0:T(8,128)(2,1)}, bf16[256,2048]{1,0:T(8,128)(2,1)}, u32[]{:S(2)}, u32[]{:S(2)}) collective-permute-start(bf16[256,2048]{1,0:T(8,128)(2,1)} %refs_0_.1), channel_id=1, source_target_pairs={{0,4},{4,0},{8,12},{12,8},{16,20},{20,16},{24,28},{28,24},{1,5},{5... | collective-permute-start | bytes 3145736 | tf_op jit(solution)/shard_map/ppermute | solution.py:492
  3.8 25.5 %collective-permute-start.3 = (bf16[256,2048]{1,0:T(8,128)(2,1)}, bf16[256,2048]{1,0:T(8,128)(2,1)}, u32[]{:S(2)}, u32[]{:S(2)}) collective-permute-start(bf16[256,2048]{1,0:T(8,128)(2,1)} %refs_0_.1), channel_id=1, source_target_pairs={{0,8},{4,12},{8,0},{12,4},{16,24},{20,28},{24,16},{28,20},{1,9},{5... | collective-permute-start | bytes 3145736 | tf_op jit(solution)/shard_map/ppermute | solution.py:492
  5.3 25.3 %collective-permute-start.4 = (bf16[256,2048]{1,0:T(8,128)(2,1)}, bf16[256,2048]{1,0:T(8,128)(2,1)}, u32[]{:S(2)}, u32[]{:S(2)}) collective-permute-start(bf16[256,2048]{1,0:T(8,128)(2,1)} %refs_0_.1), channel_id=1, source_target_pairs={{0,2},{1,3},{2,0},{3,1},{4,6},{5,7},{6,4},{7,5},{8,10},{9,11},{10,... | collective-permute-start | bytes 3145736 | tf_op jit(solution)/shard_map/ppermute | solution.py:485
  30.6 37.8 %collective-permute-start.7 = (bf16[256,2048]{1,0:T(8,128)(2,1)}, bf16[256,2048]{1,0:T(8,128)(2,1)}, u32[]{:S(2)}, u32[]{:S(2)}) collective-permute-start(bf16[256,2048]{1,0:T(8,128)(2,1)} %collective-permute-done.3.refs_5_), channel_id=1, source_target_pairs={{0,4},{4,0},{8,12},{12,8},{16,20},{20,16},{24,28},{28,24},{1,5},{5... | collective-permute-start | bytes 3145736 | tf_op jit(solution)/shard_map/ppermute | solution.py:492
  31.8 49.0 %collective-permute-start.9 = (bf16[256,2048]{1,0:T(8,128)(2,1)}, bf16[256,2048]{1,0:T(8,128)(2,1)}, u32[]{:S(2)}, u32[]{:S(2)}) collective-permute-start(bf16[256,2048]{1,0:T(8,128)(2,1)} %collective-permute-done.4.refs_1_.refs_0_), channel_id=1, source_target_pairs={{0,8},{4,12},{8,0},{12,4},{16,24},{20,28},{24,16},{28,20},{1,9},{5... | collective-permute-start | bytes 3145736 | tf_op jit(solution)/shard_map/ppermute | solution.py:492
  34.0 32.8 %collective-permute-start.6 = (f32[8,128]{1,0:T(8,128)S(1)}, f32[8,128]{1,0:T(8,128)S(1)}, u32[]{:S(2)}, u32[]{:S(2)}) collective-permute-start(f32[8,128]{1,0:T(8,128)S(1)} %broadcast_add_fusion), channel_id=1, source_target_pairs={{0,4},{4,0},{8,12},{12,8},{16,20},{20,16},{24,28},{28,24},{1,5},{5... | collective-permute-start | bytes 12296 | tf_op jit(solution)/shard_map/ppermute | solution.py:492
  35.6 45.1 %collective-permute-start.8 = (bf16[256,2048]{1,0:T(8,128)(2,1)}, bf16[256,2048]{1,0:T(8,128)(2,1)S(1)}, u32[]{:S(2)}, u32[]{:S(2)}) collective-permute-start(bf16[256,2048]{1,0:T(8,128)(2,1)} %collective-permute-done.2.refs_1_), channel_id=1, source_target_pairs={{0,2},{1,3},{2,0},{3,1},{4,6},{5,7},{6,4},{7,5},{8,10},{9,11},{10,... | collective-permute-start | bytes 3145736 | tf_op jit(solution)/shard_map/ppermute | solution.py:485
  99.2 24.3 %collective-permute-start.24 = (bf16[256,2048]{1,0:T(8,128)(2,1)}, bf16[256,2048]{1,0:T(8,128)(2,1)}, u32[]{:S(2)}, u32[]{:S(2)}) collective-permute-start(bf16[256,2048]{1,0:T(8,128)(2,1)} %collective-permute-done.9.refs_7_), channel_id=1, source_target_pairs={{0,4},{4,0},{8,12},{12,8},{16,20},{20,16},{24,28},{28,24},{1,5},{5... | collective-permute-start | bytes 3145736 | tf_op jit(solution)/shard_map/ppermute | solution.py:492
  102.0 23.9 %collective-permute-start.21 = (bf16[256,2048]{1,0:T(8,128)(2,1)}, bf16[256,2048]{1,0:T(8,128)(2,1)S(1)}, u32[]{:S(2)}, u32[]{:S(2)}) collective-permute-start(bf16[256,2048]{1,0:T(8,128)(2,1)} %fusion.29), channel_id=1, source_target_pairs={{0,2},{1,3},{2,0},{3,1},{4,6},{5,7},{6,4},{7,5},{8,10},{9,11},{10,... | collective-permute-start | bytes 3145736 | tf_op jit(solution)/shard_map/ppermute | solution.py:489
  102.7 23.3 %collective-permute-start.22 = (bf16[256,2048]{1,0:T(8,128)(2,1)S(1)}, bf16[256,2048]{1,0:T(8,128)(2,1)}, u32[]{:S(2)}, u32[]{:S(2)}) collective-permute-start(bf16[256,2048]{1,0:T(8,128)(2,1)S(1)} %fusion.30), channel_id=1, source_target_pairs={{0,1},{1,0},{2,3},{3,2},{4,5},{5,4},{6,7},{7,6},{8,9},{9,8},{10,11... | collective-permute-start | bytes 3145736 | tf_op jit(solution)/shard_map/ppermute | solution.py:481
  102.8 20.8 %collective-permute-start.23 = (f32[8,128]{1,0:T(8,128)S(1)}, f32[8,128]{1,0:T(8,128)S(1)}, u32[]{:S(2)}, u32[]{:S(2)}) collective-permute-start(f32[8,128]{1,0:T(8,128)S(1)} %add.306), channel_id=1, source_target_pairs={{0,16},{4,20},{8,24},{12,28},{16,0},{20,4},{24,8},{28,12},{1,17},{... | collective-permute-start | bytes 12296 | tf_op jit(solution)/shard_map/ppermute | solution.py:492
  132.1 27.3 %collective-permute-start.25 = (bf16[256,2048]{1,0:T(8,128)(2,1)}, bf16[256,2048]{1,0:T(8,128)(2,1)}, u32[]{:S(2)}, u32[]{:S(2)}) collective-permute-start(bf16[256,2048]{1,0:T(8,128)(2,1)} %get-tuple-element.225), channel_id=1, source_target_pairs={{0,2},{1,3},{2,0},{3,1},{4,6},{5,7},{6,4},{7,5},{8,10},{9,11},{10,... | collective-permute-start | bytes 3145736 | tf_op jit(solution)/shard_map/ppermute | solution.py:485
  133.2 26.2 %collective-permute-start.26 = (bf16[256,2048]{1,0:T(8,128)(2,1)}, bf16[256,2048]{1,0:T(8,128)(2,1)}, u32[]{:S(2)}, u32[]{:S(2)}) collective-permute-start(bf16[256,2048]{1,0:T(8,128)(2,1)} %get-tuple-element.225), channel_id=1, source_target_pairs={{0,4},{4,0},{8,12},{12,8},{16,20},{20,16},{24,28},{28,24},{1,5},{5... | collective-permute-start | bytes 3145736 | tf_op jit(solution)/shard_map/ppermute | solution.py:492
  134.0 25.4 %collective-permute-start.27 = (bf16[256,2048]{1,0:T(8,128)(2,1)}, bf16[256,2048]{1,0:T(8,128)(2,1)}, u32[]{:S(2)}, u32[]{:S(2)}) collective-permute-start(bf16[256,2048]{1,0:T(8,128)(2,1)} %get-tuple-element.225), channel_id=1, source_target_pairs={{0,8},{4,12},{8,0},{12,4},{16,24},{20,28},{24,16},{28,20},{1,9},{5... | collective-permute-start | bytes 3145736 | tf_op jit(solution)/shard_map/ppermute | solution.py:492
  135.1 24.3 %collective-permute-start.29 = (bf16[256,2048]{1,0:T(8,128)(2,1)}, bf16[256,2048]{1,0:T(8,128)(2,1)}, u32[]{:S(2)}, u32[]{:S(2)}) collective-permute-start(bf16[256,2048]{1,0:T(8,128)(2,1)} %get-tuple-element.225), channel_id=1, source_target_pairs={{0,1},{1,0},{2,3},{3,2},{4,5},{5,4},{6,7},{7,6},{8,9},{9,8},{10,11... | collective-permute-start | bytes 3145736 | tf_op jit(solution)/shard_map/ppermute | solution.py:481
  160.0 27.7 %collective-permute-start.33 = (bf16[256,2048]{1,0:T(8,128)(2,1)}, bf16[256,2048]{1,0:T(8,128)(2,1)S(1)}, u32[]{:S(2)}, u32[]{:S(2)}) collective-permute-start(bf16[256,2048]{1,0:T(8,128)(2,1)} %collective-permute-done.25), channel_id=1, source_target_pairs={{0,8},{4,12},{8,0},{12,4},{16,24},{20,28},{24,16},{28,20},{1,9},{5... | collective-permute-start | bytes 3145736 | tf_op jit(solution)/shard_map/ppermute | solution.py:492
  161.1 26.7 %collective-permute-start.32 = (bf16[256,2048]{1,0:T(8,128)(2,1)}, bf16[256,2048]{1,0:T(8,128)(2,1)S(1)}, u32[]{:S(2)}, u32[]{:S(2)}) collective-permute-start(bf16[256,2048]{1,0:T(8,128)(2,1)} %collective-permute-done.26.refs_4_.refs_8_.refs_0_), channel_id=1, source_target_pairs={{0,2},{1,3},{2,0},{3,1},{4,6},{5,7},{6,4},{7,5},{8,10},{9,11},{10,... | collective-permute-start | bytes 3145736 | tf_op jit(solution)/shard_map/ppermute | solution.py:485
  162.0 31.1 %collective-permute-start.35 = (bf16[256,2048]{1,0:T(8,128)(2,1)}, bf16[256,2048]{1,0:T(8,128)(2,1)S(1)}, u32[]{:S(2)}, u32[]{:S(2)}) collective-permute-start(bf16[256,2048]{1,0:T(8,128)(2,1)} %collective-permute-done.26.refs_4_.refs_8_.refs_0_), channel_id=1, source_target_pairs={{0,1},{1,0},{2,3},{3,2},{4,5},{5,4},{6,7},{7,6},{8,9},{9,8},{10,11... | collective-permute-start | bytes 3145736 | tf_op jit(solution)/shard_map/ppermute | solution.py:481
  162.0 25.8 %collective-permute-start.31 = (bf16[256,2048]{1,0:T(8,128)(2,1)}, bf16[256,2048]{1,0:T(8,128)(2,1)S(1)}, u32[]{:S(2)}, u32[]{:S(2)}) collective-permute-start(bf16[256,2048]{1,0:T(8,128)(2,1)} %collective-permute-done.27.refs_8_.refs_12_.refs_4_), channel_id=1, source_target_pairs={{0,4},{4,0},{8,12},{12,8},{16,20},{20,16},{24,28},{28,24},{1,5},{5... | collective-permute-start | bytes 3145736 | tf_op jit(solution)/shard_map/ppermute | solution.py:492
  165.9 27.2 %collective-permute-start.37 = (bf16[256,2048]{1,0:T(8,128)(2,1)}, bf16[256,2048]{1,0:T(8,128)(2,1)S(1)}, u32[]{:S(2)}, u32[]{:S(2)}) collective-permute-start(bf16[256,2048]{1,0:T(8,128)(2,1)} %collective-permute-done.27.refs_8_.refs_12_.refs_4_), channel_id=1, source_target_pairs={{0,1},{1,0},{2,3},{3,2},{4,5},{5,4},{6,7},{7,6},{8,9},{9,8},{10,11... | collective-permute-start | bytes 3145736 | tf_op jit(solution)/shard_map/ppermute | solution.py:481
  187.8 24.9 %collective-permute-start.34 = (bf16[256,2048]{1,0:T(8,128)(2,1)S(1)}, bf16[256,2048]{1,0:T(8,128)(2,1)S(1)}, u32[]{:S(2)}, u32[]{:S(2)}) collective-permute-start(bf16[256,2048]{1,0:T(8,128)(2,1)S(1)} %collective-permute-done.33.refs_10_.refs_14_.refs_6_), channel_id=1, source_target_pairs={{0,4},{4,0},{8,12},{12,8},{16,20},{20,16},{24,28},{28,24},{1,5},{5... | collective-permute-start | bytes 3145736 | tf_op jit(solution)/shard_map/ppermute | solution.py:492
  189.1 23.6 %collective-permute-start.38 = (bf16[256,2048]{1,0:T(8,128)(2,1)S(1)}, bf16[256,2048]{1,0:T(8,128)(2,1)S(1)}, u32[]{:S(2)}, u32[]{:S(2)}) collective-permute-start(bf16[256,2048]{1,0:T(8,128)(2,1)S(1)} %collective-permute-done.33.refs_10_.refs_14_.refs_6_), channel_id=1, source_target_pairs={{0,1},{1,0},{2,3},{3,2},{4,5},{5,4},{6,7},{7,6},{8,9},{9,8},{10,11... | collective-permute-start | bytes 3145736 | tf_op jit(solution)/shard_map/ppermute | solution.py:481
  192.2 20.3 %collective-permute-start.40 = (bf16[1024,384]{1,0:T(8,128)(2,1)}, bf16[1024,384]{1,0:T(8,128)(2,1)}, u32[]{:S(2)}, u32[]{:S(2)}) collective-permute-start(bf16[1024,384]{1,0:T(8,128)(2,1)} %get-tuple-element.372), channel_id=1, source_target_pairs={{0,8},{4,12},{8,0},{12,4},{16,24},{20,28},{24,16},{28,20},{1,9},{5... | collective-permute-start | bytes 2359304 | tf_op jit(solution)/shard_map/ppermute | solution.py:492
  193.1 19.6 %collective-permute-start.36 = (bf16[256,2048]{1,0:T(8,128)(2,1)S(1)}, bf16[256,2048]{1,0:T(8,128)(2,1)S(1)}, u32[]{:S(2)}, u32[]{:S(2)}) collective-permute-start(bf16[256,2048]{1,0:T(8,128)(2,1)S(1)} %collective-permute-done.32.refs_6_.refs_10_.refs_2_), channel_id=1, source_target_pairs={{0,1},{1,0},{2,3},{3,2},{4,5},{5,4},{6,7},{7,6},{8,9},{9,8},{10,11... | collective-permute-start | bytes 3145736 | tf_op jit(solution)/shard_map/ppermute | solution.py:481
  193.1 19.6 %collective-permute-start.39 = (bf16[256,2048]{1,0:T(8,128)(2,1)S(1)}, bf16[256,2048]{1,0:T(8,128)(2,1)}, u32[]{:S(2)}, u32[]{:S(2)}) collective-permute-start(bf16[256,2048]{1,0:T(8,128)(2,1)S(1)} %collective-permute-done.31.refs_12_.refs_16_.refs_8_), channel_id=1, source_target_pairs={{0,1},{1,0},{2,3},{3,2},{4,5},{5,4},{6,7},{7,6},{8,9},{9,8},{10,11... | collective-permute-start | bytes 3145736 | tf_op jit(solution)/shard_map/ppermute | solution.py:481
  212.8 32.5 %collective-permute-start.45 = (bf16[1024,384]{1,0:T(8,128)(2,1)}, bf16[1024,384]{1,0:T(8,128)(2,1)}, u32[]{:S(2)}, u32[]{:S(2)}) collective-permute-start(bf16[1024,384]{1,0:T(8,128)(2,1)} %get-tuple-element.371), channel_id=1, source_target_pairs={{0,4},{4,0},{8,12},{12,8},{16,20},{20,16},{24,28},{28,24},{1,5},{5... | collective-permute-start | bytes 2359304 | tf_op jit(solution)/shard_map/ppermute | solution.py:492
  227.3 27.1 %collective-permute-start.44 = (bf16[128,2048]{1,0:T(8,128)(2,1)}, bf16[128,2048]{1,0:T(8,128)(2,1)S(1)}, u32[]{:S(2)}, u32[]{:S(2)}) collective-permute-start(bf16[128,2048]{1,0:T(8,128)(2,1)} %get-tuple-element.250), channel_id=1, source_target_pairs={{0,16},{4,20},{8,24},{12,28},{16,0},{20,4},{24,8},{28,12},{1,17},{... | collective-permute-start | bytes 1572872 | tf_op jit(solution)/shard_map/ppermute | solution.py:492
  231.2 45.9 %collective-permute-start.43 = (bf16[1024,384]{1,0:T(8,128)(2,1)S(1)}, bf16[1024,384]{1,0:T(8,128)(2,1)S(1)}, u32[]{:S(2)}, u32[]{:S(2)}) collective-permute-start(bf16[1024,384]{1,0:T(8,128)(2,1)S(1)} %constant_dynamic-slice_fusion.3), channel_id=1, source_target_pairs={{0,12},{4,8},{8,4},{12,0},{16,28},{20,24},{24,20},{28,16},{1,13},{... | collective-permute-start | bytes 2359304 | tf_op jit(solution)/shard_map/ppermute | solution.py:492
  232.4 44.7 %collective-permute-start.42 = (bf16[128,2048]{1,0:T(8,128)(2,1)}, bf16[128,2048]{1,0:T(8,128)(2,1)S(1)}, u32[]{:S(2)}, u32[]{:S(2)}) collective-permute-start(bf16[128,2048]{1,0:T(8,128)(2,1)} %get-tuple-element.249), channel_id=1, source_target_pairs={{0,16},{4,20},{8,24},{12,28},{16,0},{20,4},{24,8},{28,12},{1,17},{... | collective-permute-start | bytes 1572872 | tf_op jit(solution)/shard_map/ppermute | solution.py:492
  254.5 36.0 %collective-permute-start.46 = (bf16[128,2048]{1,0:T(8,128)(2,1)S(1)}, bf16[128,2048]{1,0:T(8,128)(2,1)S(1)}, u32[]{:S(2)}, u32[]{:S(2)}) collective-permute-start(bf16[128,2048]{1,0:T(8,128)(2,1)S(1)} %add_convert_fusion.10), channel_id=1, source_target_pairs={{0,8},{4,12},{8,0},{12,4},{16,24},{20,28},{24,16},{28,20},{1,9},{5... | collective-permute-start | bytes 1572872 | tf_op jit(solution)/shard_map/ppermute | solution.py:492
  256.1 48.5 %collective-permute-start.48 = (bf16[128,2048]{1,0:T(8,128)(2,1)}, bf16[128,2048]{1,0:T(8,128)(2,1)S(1)}, u32[]{:S(2)}, u32[]{:S(2)}) collective-permute-start(bf16[128,2048]{1,0:T(8,128)(2,1)} %get-tuple-element.263), channel_id=1, source_target_pairs={{0,16},{4,20},{8,24},{12,28},{16,0},{20,4},{24,8},{28,12},{1,17},{... | collective-permute-start | bytes 1572872 | tf_op jit(solution)/shard_map/ppermute | solution.py:492
  293.8 24.1 %collective-permute-start.50 = (bf16[256,2048]{1,0:T(8,128)(2,1)S(1)}, bf16[256,2048]{1,0:T(8,128)(2,1)S(1)}, u32[]{:S(2)}, u32[]{:S(2)}) collective-permute-start(bf16[256,2048]{1,0:T(8,128)(2,1)S(1)} %pad_maximum_fusion.3.refs_0_.refs_2_), channel_id=1, source_target_pairs={{0,4},{4,0},{8,12},{12,8},{16,20},{20,16},{24,28},{28,24},{1,5},{5... | collective-permute-start | bytes 3145736 | tf_op jit(solution)/shard_map/ppermute | solution.py:492
  319.0 23.9 %collective-permute-start.52 = (bf16[256,2048]{1,0:T(8,128)(2,1)S(1)}, bf16[256,2048]{1,0:T(8,128)(2,1)S(1)}, u32[]{:S(2)}, u32[]{:S(2)}) collective-permute-start(bf16[256,2048]{1,0:T(8,128)(2,1)S(1)} %pad_maximum_fusion.4.refs_1_.refs_3_), channel_id=1, source_target_pairs={{0,4},{4,0},{8,12},{12,8},{16,20},{20,16},{24,28},{28,24},{1,5},{5... | collective-permute-start | bytes 3145736 | tf_op jit(solution)/shard_map/ppermute | solution.py:492
  319.8 22.8 %collective-permute-start.47 = (bf16[128,2048]{1,0:T(8,128)(2,1)S(1)}, bf16[128,2048]{1,0:T(8,128)(2,1)S(1)}, u32[]{:S(2)}, u32[]{:S(2)}) collective-permute-start(bf16[128,2048]{1,0:T(8,128)(2,1)S(1)} %copy-done.57), channel_id=1, source_target_pairs={{0,16},{4,20},{8,24},{12,28},{16,0},{20,4},{24,8},{28,12},{1,17},{... | collective-permute-start | bytes 1572872 | tf_op jit(solution)/shard_map/ppermute | solution.py:492
  320.0 22.9 %collective-permute-start.51 = (bf16[128,2048]{1,0:T(8,128)(2,1)S(1)}, bf16[128,2048]{1,0:T(8,128)(2,1)S(1)}, u32[]{:S(2)}, u32[]{:S(2)}) collective-permute-start(bf16[128,2048]{1,0:T(8,128)(2,1)S(1)} %add_convert_fusion.8), channel_id=1, source_target_pairs={{0,8},{4,12},{8,0},{12,4},{16,24},{20,28},{24,16},{28,20},{1,9},{5... | collective-permute-start | bytes 1572872 | tf_op jit(solution)/shard_map/ppermute | solution.py:492
  344.0 28.3 %collective-permute-start.56 = (bf16[256,2048]{1,0:T(8,128)(2,1)S(1)}, bf16[256,2048]{1,0:T(8,128)(2,1)S(1)}, u32[]{:S(2)}, u32[]{:S(2)}) collective-permute-start(bf16[256,2048]{1,0:T(8,128)(2,1)S(1)} %pad_maximum_fusion.5.refs_1_.refs_3_), channel_id=1, source_target_pairs={{0,4},{4,0},{8,12},{12,8},{16,20},{20,16},{24,28},{28,24},{1,5},{5... | collective-permute-start | bytes 3145736 | tf_op jit(solution)/shard_map/ppermute | solution.py:492
  345.3 27.0 %collective-permute-start.54 = (bf16[128,2048]{1,0:T(8,128)(2,1)}, bf16[128,2048]{1,0:T(8,128)(2,1)}, u32[]{:S(2)}, u32[]{:S(2)}) collective-permute-start(bf16[128,2048]{1,0:T(8,128)(2,1)} %get-tuple-element.279), channel_id=1, source_target_pairs={{0,16},{4,20},{8,24},{12,28},{16,0},{20,4},{24,8},{28,12},{1,17},{... | collective-permute-start | bytes 1572872 | tf_op jit(solution)/shard_map/ppermute | solution.py:492
  347.2 25.1 %collective-permute-start.55 = (bf16[128,2048]{1,0:T(8,128)(2,1)S(1)}, bf16[128,2048]{1,0:T(8,128)(2,1)}, u32[]{:S(2)}, u32[]{:S(2)}) collective-permute-start(bf16[128,2048]{1,0:T(8,128)(2,1)S(1)} %add_convert_fusion.7), channel_id=1, source_target_pairs={{0,8},{4,12},{8,0},{12,4},{16,24},{20,28},{24,16},{28,20},{1,9},{5... | collective-permute-start | bytes 1572872 | tf_op jit(solution)/shard_map/ppermute | solution.py:492
  349.3 50.4 %collective-permute-start.53 = (bf16[512,512]{1,0:T(8,128)(2,1)}, bf16[512,512]{1,0:T(8,128)(2,1)}, u32[]{:S(2)}, u32[]{:S(2)}) collective-permute-start(bf16[512,512]{1,0:T(8,128)(2,1)} %get-tuple-element.278), channel_id=1, source_target_pairs={{0,16},{4,20},{8,24},{12,28},{16,0},{20,4},{24,8},{28,12},{1,17},{... | collective-permute-start | bytes 1572872 | tf_op jit(solution)/shard_map/ppermute | solution.py:492
  379.7 24.7 %collective-permute-start.58 = (bf16[256,2048]{1,0:T(8,128)(2,1)S(1)}, bf16[256,2048]{1,0:T(8,128)(2,1)}, u32[]{:S(2)}, u32[]{:S(2)}) collective-permute-start(bf16[256,2048]{1,0:T(8,128)(2,1)S(1)} %pad_maximum_fusion.6.refs_1_.refs_3_), channel_id=1, source_target_pairs={{0,4},{4,0},{8,12},{12,8},{16,20},{20,16},{24,28},{28,24},{1,5},{5... | collective-permute-start | bytes 3145736 | tf_op jit(solution)/shard_map/ppermute | solution.py:492
  380.6 23.1 %collective-permute-start.57 = (bf16[128,2048]{1,0:T(8,128)(2,1)}, bf16[128,2048]{1,0:T(8,128)(2,1)}, u32[]{:S(2)}, u32[]{:S(2)}) collective-permute-start(bf16[128,2048]{1,0:T(8,128)(2,1)} %add_convert_fusion.6), channel_id=1, source_target_pairs={{0,8},{4,12},{8,0},{12,4},{16,24},{20,28},{24,16},{28,20},{1,9},{5... | collective-permute-start | bytes 1572872 | tf_op jit(solution)/shard_map/ppermute | solution.py:492
  404.4 32.1 %collective-permute-start.62 = (bf16[2,256,2048]{2,1,0:T(8,128)(2,1)S(1)}, bf16[2,256,2048]{2,1,0:T(8,128)(2,1)S(1)}, u32[]{:S(2)}, u32[]{:S(2)}) collective-permute-start(bf16[2,256,2048]{2,1,0:T(8,128)(2,1)S(1)} %pad_maximum_fusion.1), channel_id=1, source_target_pairs={{0,1},{1,0},{2,3},{3,2},{4,5},{5,4},{6,7},{7,6},{8,9},{9,8},{10,11... | collective-permute-start | bytes 6291464 | tf_op jit(solution)/shard_map/ppermute | solution.py:481
  408.5 28.0 %collective-permute-start.61 = (bf16[256,2048]{1,0:T(8,128)(2,1)S(1)}, bf16[256,2048]{1,0:T(8,128)(2,1)S(1)}, u32[]{:S(2)}, u32[]{:S(2)}) collective-permute-start(bf16[256,2048]{1,0:T(8,128)(2,1)S(1)} %pad_maximum_fusion.7.refs_0_.refs_2_), channel_id=1, source_target_pairs={{0,4},{4,0},{8,12},{12,8},{16,20},{20,16},{24,28},{28,24},{1,5},{5... | collective-permute-start | bytes 3145736 | tf_op jit(solution)/shard_map/ppermute | solution.py:492
  409.5 26.0 %collective-permute-start.59 = (bf16[512,512]{1,0:T(8,128)(2,1)S(1)}, bf16[512,512]{1,0:T(8,128)(2,1)S(1)}, u32[]{:S(2)}, u32[]{:S(2)}) collective-permute-start(bf16[512,512]{1,0:T(8,128)(2,1)S(1)} %copy-done.49), channel_id=1, source_target_pairs={{0,16},{4,20},{8,24},{12,28},{16,0},{20,4},{24,8},{28,12},{1,17},{... | collective-permute-start | bytes 1572872 | tf_op jit(solution)/shard_map/ppermute | solution.py:492
  411.7 24.8 %collective-permute-start.60 = (bf16[512,512]{1,0:T(8,128)(2,1)S(1)}, bf16[512,512]{1,0:T(8,128)(2,1)S(1)}, u32[]{:S(2)}, u32[]{:S(2)}) collective-permute-start(bf16[512,512]{1,0:T(8,128)(2,1)S(1)} %add_convert_fusion.5), channel_id=1, source_target_pairs={{0,8},{4,12},{8,0},{12,4},{16,24},{20,28},{24,16},{28,20},{1,9},{5... | collective-permute-start | bytes 1572872 | tf_op jit(solution)/shard_map/ppermute | solution.py:492
  437.6 26.5 %collective-permute-start.67 = (bf16[256,2048]{1,0:T(8,128)(2,1)S(1)}, bf16[256,2048]{1,0:T(8,128)(2,1)S(1)}, u32[]{:S(2)}, u32[]{:S(2)}) collective-permute-start(bf16[256,2048]{1,0:T(8,128)(2,1)S(1)} %fusion.33), channel_id=1, source_target_pairs={{0,2},{1,3},{2,0},{3,1},{4,6},{5,7},{6,4},{7,5},{8,10},{9,11},{10,... | collective-permute-start | bytes 3145736 | tf_op jit(solution)/shard_map/ppermute | solution.py:489
  438.9 25.2 %collective-permute-start.66 = (bf16[1024,512]{1,0:T(8,128)(2,1)S(1)}, bf16[1024,512]{1,0:T(8,128)(2,1)S(1)}, u32[]{:S(2)}, u32[]{:S(2)}) collective-permute-start(bf16[1024,512]{1,0:T(8,128)(2,1)S(1)} %pad_maximum_fusion.8.refs_0_.refs_2_), channel_id=1, source_target_pairs={{0,4},{4,0},{8,12},{12,8},{16,20},{20,16},{24,28},{28,24},{1,5},{5... | collective-permute-start | bytes 3145736 | tf_op jit(solution)/shard_map/ppermute | solution.py:492
  439.9 23.8 %collective-permute-start.64 = (bf16[512,512]{1,0:T(8,128)(2,1)S(1)}, bf16[512,512]{1,0:T(8,128)(2,1)S(1)}, u32[]{:S(2)}, u32[]{:S(2)}) collective-permute-start(bf16[512,512]{1,0:T(8,128)(2,1)S(1)} %copy-done.48), channel_id=1, source_target_pairs={{0,16},{4,20},{8,24},{12,28},{16,0},{20,4},{24,8},{28,12},{1,17},{... | collective-permute-start | bytes 1572872 | tf_op jit(solution)/shard_map/ppermute | solution.py:492
  440.2 23.9 %collective-permute-start.65 = (bf16[512,512]{1,0:T(8,128)(2,1)S(1)}, bf16[512,512]{1,0:T(8,128)(2,1)S(1)}, u32[]{:S(2)}, u32[]{:S(2)}) collective-permute-start(bf16[512,512]{1,0:T(8,128)(2,1)S(1)} %add_convert_fusion.4), channel_id=1, source_target_pairs={{0,8},{4,12},{8,0},{12,4},{16,24},{20,28},{24,16},{28,20},{1,9},{5... | collective-permute-start | bytes 1572872 | tf_op jit(solution)/shard_map/ppermute | solution.py:492
  464.2 26.1 %collective-permute-start.69 = (bf16[1024,512]{1,0:T(8,128)(2,1)S(1)}, bf16[1024,512]{1,0:T(8,128)(2,1)S(1)}, u32[]{:S(2)}, u32[]{:S(2)}) collective-permute-start(bf16[1024,512]{1,0:T(8,128)(2,1)S(1)} %pad_maximum_fusion.9.refs_1_.refs_3_), channel_id=1, source_target_pairs={{0,4},{4,0},{8,12},{12,8},{16,20},{20,16},{24,28},{28,24},{1,5},{5... | collective-permute-start | bytes 3145736 | tf_op jit(solution)/shard_map/ppermute | solution.py:492
  465.4 24.5 %collective-permute-start.63 = (bf16[512,512]{1,0:T(8,128)(2,1)S(1)}, bf16[512,512]{1,0:T(8,128)(2,1)S(1)}, u32[]{:S(2)}, u32[]{:S(2)}) collective-permute-start(bf16[512,512]{1,0:T(8,128)(2,1)S(1)} %copy-done.47), channel_id=1, source_target_pairs={{0,16},{4,20},{8,24},{12,28},{16,0},{20,4},{24,8},{28,12},{1,17},{... | collective-permute-start | bytes 1572872 | tf_op jit(solution)/shard_map/ppermute | solution.py:492
  465.6 24.6 %collective-permute-start.68 = (bf16[512,512]{1,0:T(8,128)(2,1)S(1)}, bf16[512,512]{1,0:T(8,128)(2,1)S(1)}, u32[]{:S(2)}, u32[]{:S(2)}) collective-permute-start(bf16[512,512]{1,0:T(8,128)(2,1)S(1)} %add_convert_fusion.3), channel_id=1, source_target_pairs={{0,8},{4,12},{8,0},{12,4},{16,24},{20,28},{24,16},{28,20},{1,9},{5... | collective-permute-start | bytes 1572872 | tf_op jit(solution)/shard_map/ppermute | solution.py:492
  490.3 24.7 %collective-permute-start.73 = (bf16[1024,512]{1,0:T(8,128)(2,1)S(1)}, bf16[1024,512]{1,0:T(8,128)(2,1)S(1)}, u32[]{:S(2)}, u32[]{:S(2)}) collective-permute-start(bf16[1024,512]{1,0:T(8,128)(2,1)S(1)} %pad_maximum_fusion.10.refs_1_.refs_3_), channel_id=1, source_target_pairs={{0,4},{4,0},{8,12},{12,8},{16,20},{20,16},{24,28},{28,24},{1,5},{5... | collective-permute-start | bytes 3145736 | tf_op jit(solution)/shard_map/ppermute | solution.py:492
  491.8 21.6 %collective-permute-start.72 = (bf16[512,512]{1,0:T(8,128)(2,1)S(1)}, bf16[512,512]{1,0:T(8,128)(2,1)S(1)}, u32[]{:S(2)}, u32[]{:S(2)}) collective-permute-start(bf16[512,512]{1,0:T(8,128)(2,1)S(1)} %add_convert_fusion.2), channel_id=1, source_target_pairs={{0,8},{4,12},{8,0},{12,4},{16,24},{20,28},{24,16},{28,20},{1,9},{5... | collective-permute-start | bytes 1572872 | tf_op jit(solution)/shard_map/ppermute | solution.py:492
  491.9 19.3 %collective-permute-start.71 = (bf16[512,384]{1,0:T(8,128)(2,1)S(1)}, bf16[512,384]{1,0:T(8,128)(2,1)S(1)}, u32[]{:S(2)}, u32[]{:S(2)}) collective-permute-start(bf16[512,384]{1,0:T(8,128)(2,1)S(1)} %get-tuple-element.321), channel_id=1, source_target_pairs={{0,16},{4,20},{8,24},{12,28},{16,0},{20,4},{24,8},{28,12},{1,17},{... | collective-permute-start | bytes 1179656 | tf_op jit(solution)/shard_map/ppermute | solution.py:492
  515.1 25.2 %collective-permute-start.77 = (bf16[1024,512]{1,0:T(8,128)(2,1)S(1)}, bf16[1024,512]{1,0:T(8,128)(2,1)S(1)}, u32[]{:S(2)}, u32[]{:S(2)}) collective-permute-start(bf16[1024,512]{1,0:T(8,128)(2,1)S(1)} %pad_maximum_fusion.11.refs_1_.refs_3_), channel_id=1, source_target_pairs={{0,4},{4,0},{8,12},{12,8},{16,20},{20,16},{24,28},{28,24},{1,5},{5... | collective-permute-start | bytes 3145736 | tf_op jit(solution)/shard_map/ppermute | solution.py:492
  517.5 22.8 %collective-permute-start.76 = (bf16[512,384]{1,0:T(8,128)(2,1)S(1)}, bf16[512,384]{1,0:T(8,128)(2,1)S(1)}, u32[]{:S(2)}, u32[]{:S(2)}) collective-permute-start(bf16[512,384]{1,0:T(8,128)(2,1)S(1)} %add_convert_fusion.14), channel_id=1, source_target_pairs={{0,8},{4,12},{8,0},{12,4},{16,24},{20,28},{24,16},{28,20},{1,9},{5... | collective-permute-start | bytes 1179656 | tf_op jit(solution)/shard_map/ppermute | solution.py:492
  520.7 19.6 %collective-permute-start.78 = (f32[15872]{0:T(1024)S(1)}, f32[15872]{0:T(1024)S(1)}, u32[]{:S(2)}, u32[]{:S(2)}) collective-permute-start(f32[15872]{0:T(1024)S(1)} %pad_maximum_fusion.16), channel_id=1, source_target_pairs={{0,4},{4,0},{8,12},{12,8},{16,20},{20,16},{24,28},{28,24},{1,5},{5... | collective-permute-start | bytes 190472 | tf_op jit(solution)/shard_map/ppermute | solution.py:492
  540.4 20.0 %collective-permute-start.81 = (bf16[1024,384]{1,0:T(8,128)(2,1)S(1)}, bf16[1024,384]{1,0:T(8,128)(2,1)S(1)}, u32[]{:S(2)}, u32[]{:S(2)}) collective-permute-start(bf16[1024,384]{1,0:T(8,128)(2,1)S(1)} %pad_maximum_fusion.12.refs_0_.refs_2_), channel_id=1, source_target_pairs={{0,4},{4,0},{8,12},{12,8},{16,20},{20,16},{24,28},{28,24},{1,5},{5... | collective-permute-start | bytes 2359304 | tf_op jit(solution)/shard_map/ppermute | solution.py:492
  541.8 18.6 %collective-permute-start.80 = (bf16[512,384]{1,0:T(8,128)(2,1)S(1)}, bf16[512,384]{1,0:T(8,128)(2,1)S(1)}, u32[]{:S(2)}, u32[]{:S(2)}) collective-permute-start(bf16[512,384]{1,0:T(8,128)(2,1)S(1)} %add_convert_fusion.13), channel_id=1, source_target_pairs={{0,8},{4,12},{8,0},{12,4},{16,24},{20,28},{24,16},{28,20},{1,9},{5... | collective-permute-start | bytes 1179656 | tf_op jit(solution)/shard_map/ppermute | solution.py:492
  560.5 21.5 %collective-permute-start.85 = (bf16[1024,384]{1,0:T(8,128)(2,1)S(1)}, bf16[1024,384]{1,0:T(8,128)(2,1)S(1)}, u32[]{:S(2)}, u32[]{:S(2)}) collective-permute-start(bf16[1024,384]{1,0:T(8,128)(2,1)S(1)} %pad_maximum_fusion.13.refs_1_.refs_3_), channel_id=1, source_target_pairs={{0,4},{4,0},{8,12},{12,8},{16,20},{20,16},{24,28},{28,24},{1,5},{5... | collective-permute-start | bytes 2359304 | tf_op jit(solution)/shard_map/ppermute | solution.py:492
  562.0 20.0 %collective-permute-start.84 = (bf16[512,384]{1,0:T(8,128)(2,1)S(1)}, bf16[512,384]{1,0:T(8,128)(2,1)S(1)}, u32[]{:S(2)}, u32[]{:S(2)}) collective-permute-start(bf16[512,384]{1,0:T(8,128)(2,1)S(1)} %add_convert_fusion.12), channel_id=1, source_target_pairs={{0,8},{4,12},{8,0},{12,4},{16,24},{20,28},{24,16},{28,20},{1,9},{5... | collective-permute-start | bytes 1179656 | tf_op jit(solution)/shard_map/ppermute | solution.py:492
  582.1 19.5 %collective-permute-start.88 = (bf16[1024,384]{1,0:T(8,128)(2,1)S(1)}, bf16[1024,384]{1,0:T(8,128)(2,1)S(1)}, u32[]{:S(2)}, u32[]{:S(2)}) collective-permute-start(bf16[1024,384]{1,0:T(8,128)(2,1)S(1)} %pad_maximum_fusion.14.refs_1_.refs_3_), channel_id=1, source_target_pairs={{0,4},{4,0},{8,12},{12,8},{16,20},{20,16},{24,28},{28,24},{1,5},{5... | collective-permute-start | bytes 2359304 | tf_op jit(solution)/shard_map/ppermute | solution.py:492
  601.7 18.8 %collective-permute-start.89 = (bf16[1024,384]{1,0:T(8,128)(2,1)S(1)}, bf16[1024,384]{1,0:T(8,128)(2,1)}, u32[]{:S(2)}, u32[]{:S(2)}) collective-permute-start(bf16[1024,384]{1,0:T(8,128)(2,1)S(1)} %pad_maximum_fusion.15.refs_1_.refs_3_), channel_id=1, source_target_pairs={{0,4},{4,0},{8,12},{12,8},{16,20},{20,16},{24,28},{28,24},{1,5},{5... | collective-permute-start | bytes 2359304 | tf_op jit(solution)/shard_map/ppermute | solution.py:492
  (102 other events, 1217.6 us)

commit v15 on v14

--- a/solution.py
+++ b/solution.py
@@ -615,7 +615,11 @@
     )
     far_blocks = [block for pair in zip(ahead, mates) for block in pair]
     norms_far = both_norms(far_blocks, gains, 6 * ways)
-    came, mates_own, counted, norms_far, last = meet(came, mates_own, counted, norms_far, last)
+    fc2_quarter = quarter_of(after(fc2_weight, norms_far[0]), 0, quarter)
+    context_quarter = quarter_of(after(context, norms_far[0]), 1, quarter)
+    came, mates_own, counted, norms_far, last, fc2_quarter, context_quarter = meet(
+        came, mates_own, counted, norms_far, last, fc2_quarter, context_quarter
+    )
     count = count + counted
     mask = 8
     while mask < dp:
@@ -637,16 +641,12 @@
     far_blocks = [block for v in last for block in (v, to_core(v))]
     norm_attn_far, norm_mlp_far = both_norms(far_blocks, gains, 6 * ways, norms_far)
     fc1_quarter = quarter_of(fc1_weight, 1, quarter)
-    fc2_quarter = quarter_of(after(fc2_weight, norm_mlp_far), 0, quarter)
-    context_quarter = quarter_of(after(context, norm_mlp_far), 1, quarter)
     pre_far = jnp.dot(norm_mlp_far, fc1_quarter, preferred_element_type=F32) + quarter_of(
         fc1_bias, 0, quarter
     ).astype(F32)
     active_far, slope_far = exact_gelu(pre_far)
     active_far = active_far.astype(BF)
-    grad_y, grad_first, active_far, grad_mate, fc2_quarter, context_quarter = meet(
-        grad_y, grad_first, active_far, grad_mate, fc2_quarter, context_quarter
-    )
+    grad_y, grad_first, active_far, grad_mate = meet(grad_y, grad_first, active_far, grad_mate)
 
     grad_second = second_far(grad_first, grad_y)
     grad_blocks = [grad_low, grad_mate]
@@ -851,7 +851,7 @@
     )
     qkv_part, mates, tensor_parts = turn(qkv_part.astype(BF), mates, tensor_parts)
     walk(last_walk(kept, mates, tensor_parts, others, outcome))
-    enqueue("qkv", *cut(qkv_part, [4, 4, 4, 4]))
+    enqueue("qkv", *cut(qkv_part, [4, 4, 4, 2, 1, 1]))
     axes = {"fc2": 0, "out": 0, "fc1": 1, "qkv": 1}
     placed = {name: (None, 0, 0) for name in axes}
 

time: 636 us -> 638 us (level)
  waiting for transfers between devices: 200 us -> 186 us
  local copies, waits for them, and re-layouts: 40.3 us -> 48.3 us
  starting transfers between devices: 82.3 us -> 89.5 us
    ppermute x61 -> x67, waiting for transfers between devices: 193 us -> 179 us  [flip(): return lax.ppermute(v, 'dp', [(d, d ^ mask) for d in range(dp)])]
    ppermute x61 -> x67, starting transfers between devices: 70.3 us -> 78.3 us  [flip(): return lax.ppermute(v, 'dp', [(d, d ^ mask) for d in range(dp)])]
    unnamed x157 -> x177, local copies, waits for them, and re-layouts: 12.5 us -> 19.6 us
    pallas_call x13 -> x15, Pallas kernels: 33.2 us -> 34.4 us  [place_quarters(): pl.pallas_call(place_kernel, grid_spec=pltpu.PrefetchScalarGridSpec(num_s...]
  transfers between devices with their start and end apart: 90 -> 96, of which waited for: 35 -> 44; matrix products, arithmetic and copies ran while one was open for 23% -> 23% of each run, Pallas kernels for 27% -> 28%
where the time goes in v15:
time: 638 us; the launch traced here: 629 us
  waiting for transfers between devices  186 us (29%)
  Pallas kernels  176 us (28%)
  matrix products  94.3 us (15%)
  starting transfers between devices  89.5 us (14%)
  local copies, waits for them, and re-layouts  48.3 us (8%)
  other arithmetic  27.1 us (4%)
  between operations  6.97 us (1%)
    ppermute x67, waiting for transfers between devices, flip(): return lax.ppermute(v, 'dp', [(d, d ^ mask) for d in range(dp)])  179 us
    ppermute x67, starting transfers between devices, flip(): return lax.ppermute(v, 'dp', [(d, d ^ mask) for d in range(dp)])  78.3 us
    dot_general x8, matrix products, contract(): lax.dot_general(left_side, right_side, (((left_dim,), (right_dim,)), ((),...  46.4 us
    pallas_call x2, Pallas kernels, norm_back(): pl.pallas_call(functools.partial(norm_back_kernel, count), grid=(count,),...  38.2 us
    pallas_call x15, Pallas kernels, place_quarters(): pl.pallas_call(place_kernel, grid_spec=pltpu.PrefetchScalarGridSpec(num_s...  34.4 us
    pallas_call x4, Pallas kernels, both_norms(): pl.pallas_call(functools.partial(norms_kernel, count), grid=(count,), in_...  29.9 us
    pallas_call x2, Pallas kernels, outer_blocks(): pl.pallas_call(functools.partial(outer_kernel, len(lefts), pieces, len(si...  23.4 us
    dot_general x2, matrix products, units(): jnp.dot(normed, fc1_weight, preferred_element_type=F32)  21.3 us
  transfers between devices with their start and end apart: 96, of which 44 were waited for; matrix products, arithmetic and copies ran while one was open for 23% of the time, Pallas kernels for 28%

profile of v15, /device:TPU:0, one launch (start us, length us, event | category | flops | bytes accessed | tf_op | source)
XLA Modules:
  0.0 628.6 jit_solution(7823020178107798327)
XLA Ops:
  1.2 2.6 collective-permute-start.2
  13.1 4.4 both_norms.4
  17.5 10.4 %multiply_convert_fusion.2 = (bf16[512,2048]{1,0:T(8,128)(2,1)}, f32[512,2048]{1,0:T(8,128)}) fusion(f32[2048]{0:T(1024)S(1)} %convert_element_type.250, bf16[512,2048]{1,0:T(8,128)(2,1)} %get-tuple-element.199, bf16[2048,2048]{1,0:T(8,128)(2,1)} %fc1_ref.3), kind=kOutput, calls=%fused_computation.18 | convolution fusion | flops 4301258752 | bytes 16785408 | tf_op jit(solution)/shard_map/dot_general | solution.py:535
  37.1 4.6 both_norms.5
  45.5 10.9 %qkv_rotary.1.q_ref.k_ref.v_ref = bf16[1024,1536]{1,0:T(8,128)(2,1)S(1)} custom-call(bf16[512,2048]{1,0:T(8,128)(2,1)S(1)} %copy-done.6, bf16[512,2048]{1,0:T(8,128)(2,1)S(1)} %get-tuple-element.205.rest_ref, bf16[2048,1536]{1,0:T(8,128)(2,1)} %qkv_ref.3, bf16[1,1536]{1,0:T(2,128)(2,1)S(1)} %broadcast_in_dim.11.b_ref, f32[1024,384]{1,0:T(8,128)S(1)} %copy-done.3, ...), custom_call_target="tpu_custom_call" | custom-call | flops 1048576 | bytes 65536 | tf_op jit(solution)/shard_map/qkv_rotary/pallas_call | solution.py:94
  56.4 9.6 %attend.1 = (bf16[1024,512]{1,0:T(8,128)(2,1)S(1)}, f32[2,1024,1]{2,1,0:T(8,128)S(1)}) custom-call(s32[1]{0:T(128)S(6)} %copy.68.prefix_ref, bf16[1024,1536]{1,0:T(8,128)(2,1)S(1)} %qkv_rotary.1.q_ref.k_ref.v_ref, bf16[1024,1536]{1,0:T(8,128)(2,1)S(1)} %qkv_rotary.1.q_ref.k_ref.v_ref, bf16[1024,1536]{1,0:T(8,128)(2,1)S(1)} %qkv_rotary.1.q_ref.k_ref.v_ref, ...), custom_call_target="tpu_custom_call" | custom-call | flops 1048576 | bytes 65536 | tf_op jit(solution)/shard_map/attend/pallas_call | solution.py:137
  69.8 10.9 %multiply_convert_fusion.1 = (bf16[512,2048]{1,0:T(8,128)(2,1)S(1)}, f32[512,2048]{1,0:T(8,128)}) fusion(f32[2048]{0:T(1024)S(1)} %convert_element_type.250, bf16[512,2048]{1,0:T(8,128)(2,1)S(1)} %copy-done.50, bf16[2048,2048]{1,0:T(8,128)(2,1)} %fc1_ref.3), kind=kOutput, calls=%fused_computation.17 | convolution fusion | flops 4301258752 | bytes 16785408 | tf_op jit(solution)/shard_map/dot_general | solution.py:535
  83.1 4.5 fusion.56
  90.2 4.5 fusion.57
  108.4 16.2 %both_norms.6 = (bf16[3072,2048]{1,0:T(8,128)(2,1)}, bf16[3072,2048]{1,0:T(8,128)(2,1)}) custom-call(bf16[4,2048]{1,0:T(4,128)(2,1)S(1)} %pad_maximum_fusion.20.refs_0_.gains_ref, bf16[256,2048]{1,0:T(8,128)(2,1)} %collective-permute-done.2.refs_1_, bf16[256,2048]{1,0:T(8,128)(2,1)S(1)} %copy-done.27, bf16[256,2048]{1,0:T(8,128)(2,1)S(1)} %copy-done.25, ...), custom_call_target="tpu_custom_call" | custom-call | flops 1048576 | bytes 65536 | tf_op jit(solution)/shard_map/both_norms/pallas_call | solution.py:354
  124.6 2.7 collective-permute-start.23
  127.2 3.1 constant_dynamic-slice_fusion.6.weight_ref
  133.3 4.3 fusion.51
  142.0 4.7 both_norms.7
  146.7 14.7 %fusion.9 = (f32[3072,512]{1,0:T(8,128)}, bf16[3072,512]{1,0:T(8,128)(2,1)}) fusion(f32[512]{0:T(512)S(1)} %dynamic-slice_convert_fusion, bf16[3072,2048]{1,0:T(8,128)(2,1)} %get-tuple-element.241, bf16[2048,2048]{1,0:T(8,128)(2,1)} %fc1_ref.3, s32[]{:T(128)S(6)} %select_n.81), kind=kOutput, calls=%fused_computation.12 | convolution fusion | flops 6459752448 | bytes 24119300 | tf_op jit(solution)/shard_map/dot_general | solution.py:644
  161.3 2.7 collective-permute-done.25
  175.2 2.4 convolution_convert_fusion.g_ref
  178.5 11.8 %attend_back.1.grad_qkv_ref = bf16[1024,1536]{1,0:T(8,128)(2,1)} custom-call(s32[1]{0:T(128)S(6)} %copy.68.prefix_ref, bf16[1024,1536]{1,0:T(8,128)(2,1)} %copy-done.2, bf16[1024,1536]{1,0:T(8,128)(2,1)} %copy-done.2, bf16[1024,1536]{1,0:T(8,128)(2,1)} %copy-done.2, bf16[1024,512]{1,0:T(8,128)(2,1)S(1)} %convolution_convert_fusion.g_ref, ...), custom_call_target="tpu_custom_call" | custom-call | flops 1048576 | bytes 65536 | tf_op jit(solution)/shard_map/attend_back/pallas_call | solution.py:203
  190.3 5.3 collective-permute-done.31.refs_12_.refs_16_.refs_8_
  196.7 3.1 constant_dynamic-slice_fusion
  201.6 15.9 %fusion.5.grad_inner_ref = bf16[1024,2048]{1,0:T(8,128)(2,1)} fusion(f32[512,2048]{1,0:T(8,128)} %get-tuple-element.418, f32[512,2048]{1,0:T(8,128)} %get-tuple-element.416, bf16[1024,2048]{1,0:T(8,128)(2,1)S(1)} %constant_dynamic-update-slice_fusion.refs_3_.refs_7_, bf16[2048,2048]{1,0:T(8,128)(2,1)} %param.34), kind=kOutput, calls=%fused_computation.7 | convolution fusion | flops 8613003264 | bytes 25165824 | tf_op jit(solution)/shard_map/dot_general | solution.py:35
  217.5 2.6 collective-permute-done.40
  224.3 10.9 %outer_blocks.2 = (bf16[128,2048]{1,0:T(8,128)(2,1)}, bf16[128,2048]{1,0:T(8,128)(2,1)}) custom-call(s32[1]{0:T(128)} %bitcast.9._.quarter_ref, bf16[512,2048]{1,0:T(8,128)(2,1)} %get-tuple-element.216.refs_0_, bf16[512,2048]{1,0:T(8,128)(2,1)} %copy-done.47, bf16[3072,512]{1,0:T(8,128)(2,1)} %get-tuple-element.242.refs_2_, bf16[1024,2048]{1,0:T(8,128)(2,1)} %copy-done.33, ...), custom_call_target="tpu_custom_call" | custom-call | flops 1048576 | bytes 65536 | tf_op jit(solution)/shard_map/outer_blocks/pallas_call | solution.py:404
  238.7 2.4 collective-permute-start.42
  241.1 12.5 %outer_blocks.3 = (bf16[128,2048]{1,0:T(8,128)(2,1)}, bf16[128,2048]{1,0:T(8,128)(2,1)}, bf16[128,2048]{1,0:T(8,128)(2,1)}) custom-call(s32[1]{0:T(128)} %bitcast.9._.quarter_ref, bf16[512,2048]{1,0:T(8,128)(2,1)} %get-tuple-element.216.refs_0_, bf16[512,2048]{1,0:T(8,128)(2,1)} %copy-done.47, bf16[3072,512]{1,0:T(8,128)(2,1)} %get-tuple-element.242.refs_2_, ...), custom_call_target="tpu_custom_call" | custom-call | flops 1048576 | bytes 65536 | tf_op jit(solution)/shard_map/outer_blocks/pallas_call | solution.py:404
  253.7 8.7 %collective-permute-done.44 = bf16[128,2048]{1,0:T(8,128)(2,1)S(1)} collective-permute-done((bf16[128,2048]{1,0:T(8,128)(2,1)}, bf16[128,2048]{1,0:T(8,128)(2,1)S(1)}, u32[]{:S(2)}, u32[]{:S(2)}) %collective-permute-start.44) | collective-permute-done | bytes 524320 | tf_op jit(solution)/shard_map/ppermute | solution.py:492
  265.3 17.6 %back_blocks.1 = bf16[3072,512]{1,0:T(8,128)(2,1)} custom-call(bf16[512,2048]{1,0:T(8,128)(2,1)} %constant_dynamic-slice_fusion.6.weight_ref, f32[3072,512]{1,0:T(8,128)} %get-tuple-element.388.slope_ref, bf16[256,2048]{1,0:T(8,128)(2,1)} %copy-done.36, bf16[256,2048]{1,0:T(8,128)(2,1)} %copy-done.39, bf16[256,2048]{1,0:T(8,128)(2,1)} %copy-done.38, ...), custom_call_target="tpu_custom_call" | custom-call | flops 1048576 | bytes 65536 | tf_op jit(solution)/shard_map/back_blocks/pallas_call | solution.py:434
  284.8 11.3 %collective-permute-done.46 = bf16[128,2048]{1,0:T(8,128)(2,1)S(1)} collective-permute-done((bf16[128,2048]{1,0:T(8,128)(2,1)S(1)}, bf16[128,2048]{1,0:T(8,128)(2,1)S(1)}, u32[]{:S(2)}, u32[]{:S(2)}) %collective-permute-start.46) | collective-permute-done | bytes 524320 | tf_op jit(solution)/shard_map/ppermute | solution.py:492
  300.5 9.9 %add_convert_fusion = bf16[2048,512]{1,0:T(8,128)(2,1)S(1)} fusion(f32[2048,512]{1,0:T(8,128)S(1)} %fusion.36, f32[2048,512]{1,0:T(8,128)S(1)} %fusion.34, bf16[3072,2048]{1,0:T(8,128)(2,1)} %get-tuple-element.241, bf16[3072,512]{1,0:T(8,128)(2,1)S(1)} %copy-done.53), kind=kOutput, calls=%fused_computation.16 | convolution fusion | flops 6445596672 | bytes 26214400 | tf_op jit(solution)/shard_map/dot_general | solution.py:35
  310.4 7.4 %collective-permute-done.49 = bf16[128,2048]{1,0:T(8,128)(2,1)S(1)} collective-permute-done((bf16[128,2048]{1,0:T(8,128)(2,1)S(1)}, bf16[128,2048]{1,0:T(8,128)(2,1)S(1)}, u32[]{:S(2)}, u32[]{:S(2)}) %collective-permute-start.49) | collective-permute-done | bytes 524320 | tf_op jit(solution)/shard_map/ppermute | solution.py:492
  317.9 5.7 collective-permute-done.50.refs_1_.refs_3_
  326.8 2.5 collective-permute-start.51
  329.4 19.0 %norm_back.2 = (f32[512,2048]{1,0:T(8,128)}, f32[8,2048]{1,0:T(8,128)}, f32[8,1536]{1,0:T(8,128)}, f32[8,2048]{1,0:T(8,128)}) custom-call(bf16[1024,1536]{1,0:T(8,128)(2,1)} %attend_back.1.grad_qkv_ref, bf16[1024,2048]{1,0:T(8,128)(2,1)} %fusion.5.grad_inner_ref, bf16[2048,1536]{1,0:T(8,128)(2,1)} %qkv_ref.3, bf16[2048,2048]{1,0:T(8,128)(2,1)} %fc1_ref.3, ...), custom_call_target="tpu_custom_call" | custom-call | flops 1048576 | bytes 65536 | tf_op jit(solution)/shard_map/norm_back/pallas_call | solution.py:278
  356.5 19.3 %norm_back.3 = (f32[512,2048]{1,0:T(8,128)}, f32[8,2048]{1,0:T(8,128)}, f32[8,1536]{1,0:T(8,128)}, f32[8,2048]{1,0:T(8,128)}) custom-call(bf16[1024,1536]{1,0:T(8,128)(2,1)} %attend_back.1.grad_qkv_ref, bf16[1024,2048]{1,0:T(8,128)(2,1)} %fusion.5.grad_inner_ref, bf16[2048,1536]{1,0:T(8,128)(2,1)} %qkv_ref.3, bf16[2048,2048]{1,0:T(8,128)(2,1)} %fc1_ref.3, ...), custom_call_target="tpu_custom_call" | custom-call | flops 1048576 | bytes 65536 | tf_op jit(solution)/shard_map/norm_back/pallas_call | solution.py:278
  375.8 2.7 fusion.31
  379.0 2.9 fusion.40
  388.7 11.4 %add_convert_fusion.1 = bf16[2048,384]{1,0:T(8,128)(2,1)} fusion(f32[2048,384]{1,0:T(8,128)S(1)} %fusion.42, f32[2048,384]{1,0:T(8,128)S(1)} %fusion.40, bf16[3072,2048]{1,0:T(8,128)(2,1)} %get-tuple-element.300, bf16[1024,384]{1,0:T(8,128)(2,1)S(1)} %copy-done.83, bf16[1024,384]{1,0:T(8,128)(2,1)} %collective-permute-done.40, ...), kind=kOutput, calls=%fused_computation.21 | convolution fusion | flops 4841275392 | bytes 22806528 | tf_op jit(solution)/shard_map/dot_general | solution.py:35
  400.2 2.7 fusion.32
  406.7 4.1 collective-permute-done.57
  411.1 2.5 place_quarters.15.refs_0_
  420.3 21.9 %collective-permute-done.59 = bf16[512,512]{1,0:T(8,128)(2,1)S(1)} collective-permute-done((bf16[512,512]{1,0:T(8,128)(2,1)S(1)}, bf16[512,512]{1,0:T(8,128)(2,1)S(1)}, u32[]{:S(2)}, u32[]{:S(2)}) %collective-permute-start.59) | collective-permute-done | bytes 524320 | tf_op jit(solution)/shard_map/ppermute | solution.py:492
  447.2 2.5 collective-permute-start.65
  449.8 2.5 place_quarters.17
  452.3 2.4 place_quarters.16.refs_0_
  454.7 16.2 %collective-permute-done.64 = bf16[512,512]{1,0:T(8,128)(2,1)S(1)} collective-permute-done((bf16[512,512]{1,0:T(8,128)(2,1)S(1)}, bf16[512,512]{1,0:T(8,128)(2,1)S(1)}, u32[]{:S(2)}, u32[]{:S(2)}) %collective-permute-start.64) | collective-permute-done | bytes 524320 | tf_op jit(solution)/shard_map/ppermute | solution.py:492
  472.5 2.5 collective-permute-start.68
  475.1 2.4 place_quarters.19.refs_0_
  477.5 2.4 place_quarters.18.refs_0_
  480.0 17.1 %collective-permute-done.63 = bf16[512,512]{1,0:T(8,128)(2,1)S(1)} collective-permute-done((bf16[512,512]{1,0:T(8,128)(2,1)S(1)}, bf16[512,512]{1,0:T(8,128)(2,1)S(1)}, u32[]{:S(2)}, u32[]{:S(2)}) %collective-permute-start.63) | collective-permute-done | bytes 524320 | tf_op jit(solution)/shard_map/ppermute | solution.py:492
  498.7 2.7 collective-permute-start.71
  501.9 2.4 place_quarters.21.refs_0_
  504.3 3.6 place_quarters.20
  508.0 10.1 %collective-permute-done.71 = bf16[512,384]{1,0:T(8,128)(2,1)S(1)} collective-permute-done((bf16[512,384]{1,0:T(8,128)(2,1)S(1)}, bf16[512,384]{1,0:T(8,128)(2,1)S(1)}, u32[]{:S(2)}, u32[]{:S(2)}) %collective-permute-start.71) | collective-permute-done | bytes 393248 | tf_op jit(solution)/shard_map/ppermute | solution.py:492
  524.3 2.7 collective-permute-start.76
  529.4 2.4 place_quarters.22.refs_0_
  531.9 13.0 %collective-permute-done.75 = bf16[512,384]{1,0:T(8,128)(2,1)S(1)} collective-permute-done((bf16[512,384]{1,0:T(8,128)(2,1)S(1)}, bf16[512,384]{1,0:T(8,128)(2,1)S(1)}, u32[]{:S(2)}, u32[]{:S(2)}) %collective-permute-start.75) | collective-permute-done | bytes 393248 | tf_op jit(solution)/shard_map/ppermute | solution.py:492
  544.9 2.5 collective-permute-done.78
  550.8 2.5 place_quarters.23
  553.3 6.1 collective-permute-done.79
  559.4 7.5 %collective-permute-done.82 = f32[15872]{0:T(1024)S(1)} collective-permute-done((f32[15872]{0:T(1024)S(1)}, f32[15872]{0:T(1024)S(1)}, u32[]{:S(2)}, u32[]{:S(2)}) %collective-permute-start.82) | collective-permute-done | bytes 63520 | tf_op jit(solution)/shard_map/ppermute | solution.py:492
  568.3 2.4 collective-permute-start.83
  573.5 6.4 %collective-permute-done.83 = bf16[256,384]{1,0:T(8,128)(2,1)S(1)} collective-permute-done((bf16[256,384]{1,0:T(8,128)(2,1)S(1)}, bf16[256,384]{1,0:T(8,128)(2,1)S(1)}, u32[]{:S(2)}, u32[]{:S(2)}) %collective-permute-start.83) | collective-permute-done | bytes 196640 | tf_op jit(solution)/shard_map/ppermute | solution.py:492
  592.7 9.5 %collective-permute-done.90.refs_2_.refs_4_ = bf16[1024,384]{1,0:T(8,128)(2,1)S(1)} collective-permute-done((bf16[1024,384]{1,0:T(8,128)(2,1)S(1)}, bf16[1024,384]{1,0:T(8,128)(2,1)S(1)}, u32[]{:S(2)}, u32[]{:S(2)}) %collective-permute-start.90) | collective-permute-done | bytes 786464 | tf_op jit(solution)/shard_map/ppermute | solution.py:492
  603.6 2.3 collective-permute-start.91
  (443 shorter events, 169.9 us)
Async XLA Ops:
  1.2 28.0 %collective-permute-start.2 = (bf16[256,2048]{1,0:T(8,128)(2,1)}, bf16[256,2048]{1,0:T(8,128)(2,1)}, u32[]{:S(2)}, u32[]{:S(2)}) collective-permute-start(bf16[256,2048]{1,0:T(8,128)(2,1)} %refs_0_.1), channel_id=1, source_target_pairs={{0,4},{4,0},{8,12},{12,8},{16,20},{20,16},{24,28},{28,24},{1,5},{5... | collective-permute-start | bytes 3145736 | tf_op jit(solution)/shard_map/ppermute | solution.py:492
  3.8 25.5 %collective-permute-start.3 = (bf16[256,2048]{1,0:T(8,128)(2,1)}, bf16[256,2048]{1,0:T(8,128)(2,1)}, u32[]{:S(2)}, u32[]{:S(2)}) collective-permute-start(bf16[256,2048]{1,0:T(8,128)(2,1)} %refs_0_.1), channel_id=1, source_target_pairs={{0,8},{4,12},{8,0},{12,4},{16,24},{20,28},{24,16},{28,20},{1,9},{5... | collective-permute-start | bytes 3145736 | tf_op jit(solution)/shard_map/ppermute | solution.py:492
  5.3 25.3 %collective-permute-start.4 = (bf16[256,2048]{1,0:T(8,128)(2,1)}, bf16[256,2048]{1,0:T(8,128)(2,1)}, u32[]{:S(2)}, u32[]{:S(2)}) collective-permute-start(bf16[256,2048]{1,0:T(8,128)(2,1)} %refs_0_.1), channel_id=1, source_target_pairs={{0,2},{1,3},{2,0},{3,1},{4,6},{5,7},{6,4},{7,5},{8,10},{9,11},{10,... | collective-permute-start | bytes 3145736 | tf_op jit(solution)/shard_map/ppermute | solution.py:485
  30.6 37.8 %collective-permute-start.7 = (bf16[256,2048]{1,0:T(8,128)(2,1)}, bf16[256,2048]{1,0:T(8,128)(2,1)}, u32[]{:S(2)}, u32[]{:S(2)}) collective-permute-start(bf16[256,2048]{1,0:T(8,128)(2,1)} %collective-permute-done.3.refs_5_), channel_id=1, source_target_pairs={{0,4},{4,0},{8,12},{12,8},{16,20},{20,16},{24,28},{28,24},{1,5},{5... | collective-permute-start | bytes 3145736 | tf_op jit(solution)/shard_map/ppermute | solution.py:492
  31.8 49.0 %collective-permute-start.9 = (bf16[256,2048]{1,0:T(8,128)(2,1)}, bf16[256,2048]{1,0:T(8,128)(2,1)}, u32[]{:S(2)}, u32[]{:S(2)}) collective-permute-start(bf16[256,2048]{1,0:T(8,128)(2,1)} %collective-permute-done.4.refs_1_.refs_0_), channel_id=1, source_target_pairs={{0,8},{4,12},{8,0},{12,4},{16,24},{20,28},{24,16},{28,20},{1,9},{5... | collective-permute-start | bytes 3145736 | tf_op jit(solution)/shard_map/ppermute | solution.py:492
  34.0 32.9 %collective-permute-start.6 = (f32[8,128]{1,0:T(8,128)S(1)}, f32[8,128]{1,0:T(8,128)S(1)}, u32[]{:S(2)}, u32[]{:S(2)}) collective-permute-start(f32[8,128]{1,0:T(8,128)S(1)} %broadcast_add_fusion), channel_id=1, source_target_pairs={{0,4},{4,0},{8,12},{12,8},{16,20},{20,16},{24,28},{28,24},{1,5},{5... | collective-permute-start | bytes 12296 | tf_op jit(solution)/shard_map/ppermute | solution.py:492
  35.6 45.2 %collective-permute-start.8 = (bf16[256,2048]{1,0:T(8,128)(2,1)}, bf16[256,2048]{1,0:T(8,128)(2,1)S(1)}, u32[]{:S(2)}, u32[]{:S(2)}) collective-permute-start(bf16[256,2048]{1,0:T(8,128)(2,1)} %collective-permute-done.2.refs_1_), channel_id=1, source_target_pairs={{0,2},{1,3},{2,0},{3,1},{4,6},{5,7},{6,4},{7,5},{8,10},{9,11},{10,... | collective-permute-start | bytes 3145736 | tf_op jit(solution)/shard_map/ppermute | solution.py:485
  99.3 32.8 %collective-permute-start.24 = (bf16[256,2048]{1,0:T(8,128)(2,1)}, bf16[256,2048]{1,0:T(8,128)(2,1)}, u32[]{:S(2)}, u32[]{:S(2)}) collective-permute-start(bf16[256,2048]{1,0:T(8,128)(2,1)} %collective-permute-done.9.refs_7_), channel_id=1, source_target_pairs={{0,4},{4,0},{8,12},{12,8},{16,20},{20,16},{24,28},{28,24},{1,5},{5... | collective-permute-start | bytes 3145736 | tf_op jit(solution)/shard_map/ppermute | solution.py:492
  102.9 29.1 %collective-permute-start.21 = (bf16[256,2048]{1,0:T(8,128)(2,1)}, bf16[256,2048]{1,0:T(8,128)(2,1)}, u32[]{:S(2)}, u32[]{:S(2)}) collective-permute-start(bf16[256,2048]{1,0:T(8,128)(2,1)} %fusion.29), channel_id=1, source_target_pairs={{0,2},{1,3},{2,0},{3,1},{4,6},{5,7},{6,4},{7,5},{8,10},{9,11},{10,... | collective-permute-start | bytes 3145736 | tf_op jit(solution)/shard_map/ppermute | solution.py:489
  104.6 27.5 %collective-permute-start.22 = (bf16[256,2048]{1,0:T(8,128)(2,1)}, bf16[256,2048]{1,0:T(8,128)(2,1)}, u32[]{:S(2)}, u32[]{:S(2)}) collective-permute-start(bf16[256,2048]{1,0:T(8,128)(2,1)} %fusion.30), channel_id=1, source_target_pairs={{0,1},{1,0},{2,3},{3,2},{4,5},{5,4},{6,7},{7,6},{8,9},{9,8},{10,11... | collective-permute-start | bytes 3145736 | tf_op jit(solution)/shard_map/ppermute | solution.py:481
  138.6 25.5 %collective-permute-start.25 = (bf16[256,2048]{1,0:T(8,128)(2,1)S(1)}, bf16[256,2048]{1,0:T(8,128)(2,1)}, u32[]{:S(2)}, u32[]{:S(2)}) collective-permute-start(bf16[256,2048]{1,0:T(8,128)(2,1)S(1)} %get-tuple-element.237), channel_id=1, source_target_pairs={{0,2},{1,3},{2,0},{3,1},{4,6},{5,7},{6,4},{7,5},{8,10},{9,11},{10,... | collective-permute-start | bytes 3145736 | tf_op jit(solution)/shard_map/ppermute | solution.py:485
  140.1 25.1 %collective-permute-start.26 = (bf16[256,2048]{1,0:T(8,128)(2,1)S(1)}, bf16[256,2048]{1,0:T(8,128)(2,1)S(1)}, u32[]{:S(2)}, u32[]{:S(2)}) collective-permute-start(bf16[256,2048]{1,0:T(8,128)(2,1)S(1)} %get-tuple-element.237), channel_id=1, source_target_pairs={{0,4},{4,0},{8,12},{12,8},{16,20},{20,16},{24,28},{28,24},{1,5},{5... | collective-permute-start | bytes 3145736 | tf_op jit(solution)/shard_map/ppermute | solution.py:492
  140.9 24.9 %collective-permute-start.27 = (bf16[256,2048]{1,0:T(8,128)(2,1)S(1)}, bf16[256,2048]{1,0:T(8,128)(2,1)}, u32[]{:S(2)}, u32[]{:S(2)}) collective-permute-start(bf16[256,2048]{1,0:T(8,128)(2,1)S(1)} %get-tuple-element.237), channel_id=1, source_target_pairs={{0,8},{4,12},{8,0},{12,4},{16,24},{20,28},{24,16},{28,20},{1,9},{5... | collective-permute-start | bytes 3145736 | tf_op jit(solution)/shard_map/ppermute | solution.py:492
  142.0 23.9 %collective-permute-start.29 = (bf16[256,2048]{1,0:T(8,128)(2,1)S(1)}, bf16[256,2048]{1,0:T(8,128)(2,1)S(1)}, u32[]{:S(2)}, u32[]{:S(2)}) collective-permute-start(bf16[256,2048]{1,0:T(8,128)(2,1)S(1)} %get-tuple-element.237), channel_id=1, source_target_pairs={{0,1},{1,0},{2,3},{3,2},{4,5},{5,4},{6,7},{7,6},{8,9},{9,8},{10,11... | collective-permute-start | bytes 3145736 | tf_op jit(solution)/shard_map/ppermute | solution.py:481
  168.2 27.4 %collective-permute-start.33 = (bf16[256,2048]{1,0:T(8,128)(2,1)}, bf16[256,2048]{1,0:T(8,128)(2,1)S(1)}, u32[]{:S(2)}, u32[]{:S(2)}) collective-permute-start(bf16[256,2048]{1,0:T(8,128)(2,1)} %collective-permute-done.25), channel_id=1, source_target_pairs={{0,8},{4,12},{8,0},{12,4},{16,24},{20,28},{24,16},{28,20},{1,9},{5... | collective-permute-start | bytes 3145736 | tf_op jit(solution)/shard_map/ppermute | solution.py:492
  169.3 26.3 %collective-permute-start.32 = (bf16[256,2048]{1,0:T(8,128)(2,1)S(1)}, bf16[256,2048]{1,0:T(8,128)(2,1)S(1)}, u32[]{:S(2)}, u32[]{:S(2)}) collective-permute-start(bf16[256,2048]{1,0:T(8,128)(2,1)S(1)} %collective-permute-done.26.refs_4_.refs_8_.refs_0_), channel_id=1, source_target_pairs={{0,2},{1,3},{2,0},{3,1},{4,6},{5,7},{6,4},{7,5},{8,10},{9,11},{10,... | collective-permute-start | bytes 3145736 | tf_op jit(solution)/shard_map/ppermute | solution.py:485
  169.9 31.2 %collective-permute-start.35 = (bf16[256,2048]{1,0:T(8,128)(2,1)S(1)}, bf16[256,2048]{1,0:T(8,128)(2,1)S(1)}, u32[]{:S(2)}, u32[]{:S(2)}) collective-permute-start(bf16[256,2048]{1,0:T(8,128)(2,1)S(1)} %collective-permute-done.26.refs_4_.refs_8_.refs_0_), channel_id=1, source_target_pairs={{0,1},{1,0},{2,3},{3,2},{4,5},{5,4},{6,7},{7,6},{8,9},{9,8},{10,11... | collective-permute-start | bytes 3145736 | tf_op jit(solution)/shard_map/ppermute | solution.py:481
  169.9 25.8 %collective-permute-start.31 = (bf16[256,2048]{1,0:T(8,128)(2,1)}, bf16[256,2048]{1,0:T(8,128)(2,1)S(1)}, u32[]{:S(2)}, u32[]{:S(2)}) collective-permute-start(bf16[256,2048]{1,0:T(8,128)(2,1)} %collective-permute-done.27.refs_8_.refs_12_.refs_4_), channel_id=1, source_target_pairs={{0,4},{4,0},{8,12},{12,8},{16,20},{20,16},{24,28},{28,24},{1,5},{5... | collective-permute-start | bytes 3145736 | tf_op jit(solution)/shard_map/ppermute | solution.py:492
  173.5 27.8 %collective-permute-start.37 = (bf16[256,2048]{1,0:T(8,128)(2,1)}, bf16[256,2048]{1,0:T(8,128)(2,1)}, u32[]{:S(2)}, u32[]{:S(2)}) collective-permute-start(bf16[256,2048]{1,0:T(8,128)(2,1)} %collective-permute-done.27.refs_8_.refs_12_.refs_4_), channel_id=1, source_target_pairs={{0,1},{1,0},{2,3},{3,2},{4,5},{5,4},{6,7},{7,6},{8,9},{9,8},{10,11... | collective-permute-start | bytes 3145736 | tf_op jit(solution)/shard_map/ppermute | solution.py:481
  195.7 24.9 %collective-permute-start.34 = (bf16[256,2048]{1,0:T(8,128)(2,1)S(1)}, bf16[256,2048]{1,0:T(8,128)(2,1)S(1)}, u32[]{:S(2)}, u32[]{:S(2)}) collective-permute-start(bf16[256,2048]{1,0:T(8,128)(2,1)S(1)} %collective-permute-done.33.refs_10_.refs_14_.refs_6_), channel_id=1, source_target_pairs={{0,4},{4,0},{8,12},{12,8},{16,20},{20,16},{24,28},{28,24},{1,5},{5... | collective-permute-start | bytes 3145736 | tf_op jit(solution)/shard_map/ppermute | solution.py:492
  196.7 23.8 %collective-permute-start.38 = (bf16[256,2048]{1,0:T(8,128)(2,1)S(1)}, bf16[256,2048]{1,0:T(8,128)(2,1)S(1)}, u32[]{:S(2)}, u32[]{:S(2)}) collective-permute-start(bf16[256,2048]{1,0:T(8,128)(2,1)S(1)} %collective-permute-done.33.refs_10_.refs_14_.refs_6_), channel_id=1, source_target_pairs={{0,1},{1,0},{2,3},{3,2},{4,5},{5,4},{6,7},{7,6},{8,9},{9,8},{10,11... | collective-permute-start | bytes 3145736 | tf_op jit(solution)/shard_map/ppermute | solution.py:481
  199.8 20.3 %collective-permute-start.40 = (bf16[1024,384]{1,0:T(8,128)(2,1)}, bf16[1024,384]{1,0:T(8,128)(2,1)}, u32[]{:S(2)}, u32[]{:S(2)}) collective-permute-start(bf16[1024,384]{1,0:T(8,128)(2,1)} %get-tuple-element.392), channel_id=1, source_target_pairs={{0,8},{4,12},{8,0},{12,4},{16,24},{20,28},{24,16},{28,20},{1,9},{5... | collective-permute-start | bytes 2359304 | tf_op jit(solution)/shard_map/ppermute | solution.py:492
  201.0 19.5 %collective-permute-start.36 = (bf16[256,2048]{1,0:T(8,128)(2,1)S(1)}, bf16[256,2048]{1,0:T(8,128)(2,1)S(1)}, u32[]{:S(2)}, u32[]{:S(2)}) collective-permute-start(bf16[256,2048]{1,0:T(8,128)(2,1)S(1)} %collective-permute-done.32.refs_6_.refs_10_.refs_2_), channel_id=1, source_target_pairs={{0,1},{1,0},{2,3},{3,2},{4,5},{5,4},{6,7},{7,6},{8,9},{9,8},{10,11... | collective-permute-start | bytes 3145736 | tf_op jit(solution)/shard_map/ppermute | solution.py:481
  201.3 19.3 %collective-permute-start.39 = (bf16[256,2048]{1,0:T(8,128)(2,1)S(1)}, bf16[256,2048]{1,0:T(8,128)(2,1)S(1)}, u32[]{:S(2)}, u32[]{:S(2)}) collective-permute-start(bf16[256,2048]{1,0:T(8,128)(2,1)S(1)} %collective-permute-done.31.refs_12_.refs_16_.refs_8_), channel_id=1, source_target_pairs={{0,1},{1,0},{2,3},{3,2},{4,5},{5,4},{6,7},{7,6},{8,9},{9,8},{10,11... | collective-permute-start | bytes 3145736 | tf_op jit(solution)/shard_map/ppermute | solution.py:481
  220.6 33.0 %collective-permute-start.45 = (bf16[1024,384]{1,0:T(8,128)(2,1)}, bf16[1024,384]{1,0:T(8,128)(2,1)}, u32[]{:S(2)}, u32[]{:S(2)}) collective-permute-start(bf16[1024,384]{1,0:T(8,128)(2,1)} %get-tuple-element.391), channel_id=1, source_target_pairs={{0,4},{4,0},{8,12},{12,8},{16,20},{20,16},{24,28},{28,24},{1,5},{5... | collective-permute-start | bytes 2359304 | tf_op jit(solution)/shard_map/ppermute | solution.py:492
  235.2 27.1 %collective-permute-start.44 = (bf16[128,2048]{1,0:T(8,128)(2,1)}, bf16[128,2048]{1,0:T(8,128)(2,1)S(1)}, u32[]{:S(2)}, u32[]{:S(2)}) collective-permute-start(bf16[128,2048]{1,0:T(8,128)(2,1)} %get-tuple-element.260), channel_id=1, source_target_pairs={{0,16},{4,20},{8,24},{12,28},{16,0},{20,4},{24,8},{28,12},{1,17},{... | collective-permute-start | bytes 1572872 | tf_op jit(solution)/shard_map/ppermute | solution.py:492
  237.0 47.8 %collective-permute-start.43 = (bf16[1024,384]{1,0:T(8,128)(2,1)S(1)}, bf16[1024,384]{1,0:T(8,128)(2,1)S(1)}, u32[]{:S(2)}, u32[]{:S(2)}) collective-permute-start(bf16[1024,384]{1,0:T(8,128)(2,1)S(1)} %constant_dynamic-slice_fusion.3), channel_id=1, source_target_pairs={{0,12},{4,8},{8,4},{12,0},{16,28},{20,24},{24,20},{28,16},{1,13},{... | collective-permute-start | bytes 2359304 | tf_op jit(solution)/shard_map/ppermute | solution.py:492
  238.7 46.2 %collective-permute-start.42 = (bf16[128,2048]{1,0:T(8,128)(2,1)}, bf16[128,2048]{1,0:T(8,128)(2,1)S(1)}, u32[]{:S(2)}, u32[]{:S(2)}) collective-permute-start(bf16[128,2048]{1,0:T(8,128)(2,1)} %get-tuple-element.259), channel_id=1, source_target_pairs={{0,16},{4,20},{8,24},{12,28},{16,0},{20,4},{24,8},{28,12},{1,17},{... | collective-permute-start | bytes 1572872 | tf_op jit(solution)/shard_map/ppermute | solution.py:492
  262.5 33.7 %collective-permute-start.46 = (bf16[128,2048]{1,0:T(8,128)(2,1)S(1)}, bf16[128,2048]{1,0:T(8,128)(2,1)S(1)}, u32[]{:S(2)}, u32[]{:S(2)}) collective-permute-start(bf16[128,2048]{1,0:T(8,128)(2,1)S(1)} %add_convert_fusion.10), channel_id=1, source_target_pairs={{0,8},{4,12},{8,0},{12,4},{16,24},{20,28},{24,16},{28,20},{1,9},{5... | collective-permute-start | bytes 1572872 | tf_op jit(solution)/shard_map/ppermute | solution.py:492
  263.8 46.6 %collective-permute-start.48 = (bf16[128,2048]{1,0:T(8,128)(2,1)}, bf16[128,2048]{1,0:T(8,128)(2,1)S(1)}, u32[]{:S(2)}, u32[]{:S(2)}) collective-permute-start(bf16[128,2048]{1,0:T(8,128)(2,1)} %get-tuple-element.273), channel_id=1, source_target_pairs={{0,16},{4,20},{8,24},{12,28},{16,0},{20,4},{24,8},{28,12},{1,17},{... | collective-permute-start | bytes 1572872 | tf_op jit(solution)/shard_map/ppermute | solution.py:492
  299.3 24.2 %collective-permute-start.50 = (bf16[256,2048]{1,0:T(8,128)(2,1)S(1)}, bf16[256,2048]{1,0:T(8,128)(2,1)S(1)}, u32[]{:S(2)}, u32[]{:S(2)}) collective-permute-start(bf16[256,2048]{1,0:T(8,128)(2,1)S(1)} %pad_maximum_fusion.3.refs_0_.refs_2_), channel_id=1, source_target_pairs={{0,4},{4,0},{8,12},{12,8},{16,20},{20,16},{24,28},{28,24},{1,5},{5... | collective-permute-start | bytes 3145736 | tf_op jit(solution)/shard_map/ppermute | solution.py:492
  324.6 25.3 %collective-permute-start.52 = (bf16[256,2048]{1,0:T(8,128)(2,1)S(1)}, bf16[256,2048]{1,0:T(8,128)(2,1)S(1)}, u32[]{:S(2)}, u32[]{:S(2)}) collective-permute-start(bf16[256,2048]{1,0:T(8,128)(2,1)S(1)} %pad_maximum_fusion.4.refs_1_.refs_3_), channel_id=1, source_target_pairs={{0,4},{4,0},{8,12},{12,8},{16,20},{20,16},{24,28},{28,24},{1,5},{5... | collective-permute-start | bytes 3145736 | tf_op jit(solution)/shard_map/ppermute | solution.py:492
  325.7 24.0 %collective-permute-start.47 = (bf16[128,2048]{1,0:T(8,128)(2,1)S(1)}, bf16[128,2048]{1,0:T(8,128)(2,1)S(1)}, u32[]{:S(2)}, u32[]{:S(2)}) collective-permute-start(bf16[128,2048]{1,0:T(8,128)(2,1)S(1)} %copy-done.67), channel_id=1, source_target_pairs={{0,16},{4,20},{8,24},{12,28},{16,0},{20,4},{24,8},{28,12},{1,17},{... | collective-permute-start | bytes 1572872 | tf_op jit(solution)/shard_map/ppermute | solution.py:492
  326.8 23.1 %collective-permute-start.51 = (bf16[128,2048]{1,0:T(8,128)(2,1)S(1)}, bf16[128,2048]{1,0:T(8,128)(2,1)S(1)}, u32[]{:S(2)}, u32[]{:S(2)}) collective-permute-start(bf16[128,2048]{1,0:T(8,128)(2,1)S(1)} %add_convert_fusion.8), channel_id=1, source_target_pairs={{0,8},{4,12},{8,0},{12,4},{16,24},{20,28},{24,16},{28,20},{1,9},{5... | collective-permute-start | bytes 1572872 | tf_op jit(solution)/shard_map/ppermute | solution.py:492
  351.0 28.0 %collective-permute-start.56 = (bf16[256,2048]{1,0:T(8,128)(2,1)S(1)}, bf16[256,2048]{1,0:T(8,128)(2,1)S(1)}, u32[]{:S(2)}, u32[]{:S(2)}) collective-permute-start(bf16[256,2048]{1,0:T(8,128)(2,1)S(1)} %pad_maximum_fusion.5.refs_1_.refs_3_), channel_id=1, source_target_pairs={{0,4},{4,0},{8,12},{12,8},{16,20},{20,16},{24,28},{28,24},{1,5},{5... | collective-permute-start | bytes 3145736 | tf_op jit(solution)/shard_map/ppermute | solution.py:492
  352.1 26.8 %collective-permute-start.54 = (bf16[128,2048]{1,0:T(8,128)(2,1)}, bf16[128,2048]{1,0:T(8,128)(2,1)}, u32[]{:S(2)}, u32[]{:S(2)}) collective-permute-start(bf16[128,2048]{1,0:T(8,128)(2,1)} %get-tuple-element.289), channel_id=1, source_target_pairs={{0,16},{4,20},{8,24},{12,28},{16,0},{20,4},{24,8},{28,12},{1,17},{... | collective-permute-start | bytes 1572872 | tf_op jit(solution)/shard_map/ppermute | solution.py:492
  353.9 25.1 %collective-permute-start.55 = (bf16[128,2048]{1,0:T(8,128)(2,1)S(1)}, bf16[128,2048]{1,0:T(8,128)(2,1)}, u32[]{:S(2)}, u32[]{:S(2)}) collective-permute-start(bf16[128,2048]{1,0:T(8,128)(2,1)S(1)} %add_convert_fusion.7), channel_id=1, source_target_pairs={{0,8},{4,12},{8,0},{12,4},{16,24},{20,28},{24,16},{28,20},{1,9},{5... | collective-permute-start | bytes 1572872 | tf_op jit(solution)/shard_map/ppermute | solution.py:492
  355.9 50.8 %collective-permute-start.53 = (bf16[512,512]{1,0:T(8,128)(2,1)}, bf16[512,512]{1,0:T(8,128)(2,1)}, u32[]{:S(2)}, u32[]{:S(2)}) collective-permute-start(bf16[512,512]{1,0:T(8,128)(2,1)} %get-tuple-element.288), channel_id=1, source_target_pairs={{0,16},{4,20},{8,24},{12,28},{16,0},{20,4},{24,8},{28,12},{1,17},{... | collective-permute-start | bytes 1572872 | tf_op jit(solution)/shard_map/ppermute | solution.py:492
  386.3 24.7 %collective-permute-start.58 = (bf16[256,2048]{1,0:T(8,128)(2,1)S(1)}, bf16[256,2048]{1,0:T(8,128)(2,1)}, u32[]{:S(2)}, u32[]{:S(2)}) collective-permute-start(bf16[256,2048]{1,0:T(8,128)(2,1)S(1)} %pad_maximum_fusion.6.refs_1_.refs_3_), channel_id=1, source_target_pairs={{0,4},{4,0},{8,12},{12,8},{16,20},{20,16},{24,28},{28,24},{1,5},{5... | collective-permute-start | bytes 3145736 | tf_op jit(solution)/shard_map/ppermute | solution.py:492
  387.3 23.4 %collective-permute-start.57 = (bf16[128,2048]{1,0:T(8,128)(2,1)}, bf16[128,2048]{1,0:T(8,128)(2,1)}, u32[]{:S(2)}, u32[]{:S(2)}) collective-permute-start(bf16[128,2048]{1,0:T(8,128)(2,1)} %add_convert_fusion.6), channel_id=1, source_target_pairs={{0,8},{4,12},{8,0},{12,4},{16,24},{20,28},{24,16},{28,20},{1,9},{5... | collective-permute-start | bytes 1572872 | tf_op jit(solution)/shard_map/ppermute | solution.py:492
  411.0 32.2 %collective-permute-start.62 = (bf16[2,256,2048]{2,1,0:T(8,128)(2,1)S(1)}, bf16[2,256,2048]{2,1,0:T(8,128)(2,1)S(1)}, u32[]{:S(2)}, u32[]{:S(2)}) collective-permute-start(bf16[2,256,2048]{2,1,0:T(8,128)(2,1)S(1)} %pad_maximum_fusion.1), channel_id=1, source_target_pairs={{0,1},{1,0},{2,3},{3,2},{4,5},{5,4},{6,7},{7,6},{8,9},{9,8},{10,11... | collective-permute-start | bytes 6291464 | tf_op jit(solution)/shard_map/ppermute | solution.py:481
  415.1 28.1 %collective-permute-start.61 = (bf16[256,2048]{1,0:T(8,128)(2,1)S(1)}, bf16[256,2048]{1,0:T(8,128)(2,1)S(1)}, u32[]{:S(2)}, u32[]{:S(2)}) collective-permute-start(bf16[256,2048]{1,0:T(8,128)(2,1)S(1)} %pad_maximum_fusion.7.refs_0_.refs_2_), channel_id=1, source_target_pairs={{0,4},{4,0},{8,12},{12,8},{16,20},{20,16},{24,28},{28,24},{1,5},{5... | collective-permute-start | bytes 3145736 | tf_op jit(solution)/shard_map/ppermute | solution.py:492
  416.3 25.9 %collective-permute-start.59 = (bf16[512,512]{1,0:T(8,128)(2,1)S(1)}, bf16[512,512]{1,0:T(8,128)(2,1)S(1)}, u32[]{:S(2)}, u32[]{:S(2)}) collective-permute-start(bf16[512,512]{1,0:T(8,128)(2,1)S(1)} %copy-done.58), channel_id=1, source_target_pairs={{0,16},{4,20},{8,24},{12,28},{16,0},{20,4},{24,8},{28,12},{1,17},{... | collective-permute-start | bytes 1572872 | tf_op jit(solution)/shard_map/ppermute | solution.py:492
  418.4 24.8 %collective-permute-start.60 = (bf16[512,512]{1,0:T(8,128)(2,1)S(1)}, bf16[512,512]{1,0:T(8,128)(2,1)S(1)}, u32[]{:S(2)}, u32[]{:S(2)}) collective-permute-start(bf16[512,512]{1,0:T(8,128)(2,1)S(1)} %add_convert_fusion.5), channel_id=1, source_target_pairs={{0,8},{4,12},{8,0},{12,4},{16,24},{20,28},{24,16},{28,20},{1,9},{5... | collective-permute-start | bytes 1572872 | tf_op jit(solution)/shard_map/ppermute | solution.py:492
  444.3 27.0 %collective-permute-start.67 = (bf16[256,2048]{1,0:T(8,128)(2,1)S(1)}, bf16[256,2048]{1,0:T(8,128)(2,1)S(1)}, u32[]{:S(2)}, u32[]{:S(2)}) collective-permute-start(bf16[256,2048]{1,0:T(8,128)(2,1)S(1)} %fusion.33), channel_id=1, source_target_pairs={{0,2},{1,3},{2,0},{3,1},{4,6},{5,7},{6,4},{7,5},{8,10},{9,11},{10,... | collective-permute-start | bytes 3145736 | tf_op jit(solution)/shard_map/ppermute | solution.py:489
  445.7 25.7 %collective-permute-start.66 = (bf16[1024,512]{1,0:T(8,128)(2,1)S(1)}, bf16[1024,512]{1,0:T(8,128)(2,1)S(1)}, u32[]{:S(2)}, u32[]{:S(2)}) collective-permute-start(bf16[1024,512]{1,0:T(8,128)(2,1)S(1)} %pad_maximum_fusion.8.refs_0_.refs_2_), channel_id=1, source_target_pairs={{0,4},{4,0},{8,12},{12,8},{16,20},{20,16},{24,28},{28,24},{1,5},{5... | collective-permute-start | bytes 3145736 | tf_op jit(solution)/shard_map/ppermute | solution.py:492
  447.1 23.9 %collective-permute-start.64 = (bf16[512,512]{1,0:T(8,128)(2,1)S(1)}, bf16[512,512]{1,0:T(8,128)(2,1)S(1)}, u32[]{:S(2)}, u32[]{:S(2)}) collective-permute-start(bf16[512,512]{1,0:T(8,128)(2,1)S(1)} %copy-done.57), channel_id=1, source_target_pairs={{0,16},{4,20},{8,24},{12,28},{16,0},{20,4},{24,8},{28,12},{1,17},{... | collective-permute-start | bytes 1572872 | tf_op jit(solution)/shard_map/ppermute | solution.py:492
  447.2 24.1 %collective-permute-start.65 = (bf16[512,512]{1,0:T(8,128)(2,1)S(1)}, bf16[512,512]{1,0:T(8,128)(2,1)S(1)}, u32[]{:S(2)}, u32[]{:S(2)}) collective-permute-start(bf16[512,512]{1,0:T(8,128)(2,1)S(1)} %add_convert_fusion.4), channel_id=1, source_target_pairs={{0,8},{4,12},{8,0},{12,4},{16,24},{20,28},{24,16},{28,20},{1,9},{5... | collective-permute-start | bytes 1572872 | tf_op jit(solution)/shard_map/ppermute | solution.py:492
  471.4 26.0 %collective-permute-start.69 = (bf16[1024,512]{1,0:T(8,128)(2,1)S(1)}, bf16[1024,512]{1,0:T(8,128)(2,1)S(1)}, u32[]{:S(2)}, u32[]{:S(2)}) collective-permute-start(bf16[1024,512]{1,0:T(8,128)(2,1)S(1)} %pad_maximum_fusion.9.refs_1_.refs_3_), channel_id=1, source_target_pairs={{0,4},{4,0},{8,12},{12,8},{16,20},{20,16},{24,28},{28,24},{1,5},{5... | collective-permute-start | bytes 3145736 | tf_op jit(solution)/shard_map/ppermute | solution.py:492
  472.3 24.8 %collective-permute-start.63 = (bf16[512,512]{1,0:T(8,128)(2,1)S(1)}, bf16[512,512]{1,0:T(8,128)(2,1)S(1)}, u32[]{:S(2)}, u32[]{:S(2)}) collective-permute-start(bf16[512,512]{1,0:T(8,128)(2,1)S(1)} %copy-done.56), channel_id=1, source_target_pairs={{0,16},{4,20},{8,24},{12,28},{16,0},{20,4},{24,8},{28,12},{1,17},{... | collective-permute-start | bytes 1572872 | tf_op jit(solution)/shard_map/ppermute | solution.py:492
  472.5 24.9 %collective-permute-start.68 = (bf16[512,512]{1,0:T(8,128)(2,1)S(1)}, bf16[512,512]{1,0:T(8,128)(2,1)S(1)}, u32[]{:S(2)}, u32[]{:S(2)}) collective-permute-start(bf16[512,512]{1,0:T(8,128)(2,1)S(1)} %add_convert_fusion.3), channel_id=1, source_target_pairs={{0,8},{4,12},{8,0},{12,4},{16,24},{20,28},{24,16},{28,20},{1,9},{5... | collective-permute-start | bytes 1572872 | tf_op jit(solution)/shard_map/ppermute | solution.py:492
  497.5 24.7 %collective-permute-start.73 = (bf16[1024,512]{1,0:T(8,128)(2,1)S(1)}, bf16[1024,512]{1,0:T(8,128)(2,1)S(1)}, u32[]{:S(2)}, u32[]{:S(2)}) collective-permute-start(bf16[1024,512]{1,0:T(8,128)(2,1)S(1)} %pad_maximum_fusion.10.refs_1_.refs_3_), channel_id=1, source_target_pairs={{0,4},{4,0},{8,12},{12,8},{16,20},{20,16},{24,28},{28,24},{1,5},{5... | collective-permute-start | bytes 3145736 | tf_op jit(solution)/shard_map/ppermute | solution.py:492
  498.6 21.6 %collective-permute-start.72 = (bf16[512,512]{1,0:T(8,128)(2,1)S(1)}, bf16[512,512]{1,0:T(8,128)(2,1)S(1)}, u32[]{:S(2)}, u32[]{:S(2)}) collective-permute-start(bf16[512,512]{1,0:T(8,128)(2,1)S(1)} %add_convert_fusion.2), channel_id=1, source_target_pairs={{0,8},{4,12},{8,0},{12,4},{16,24},{20,28},{24,16},{28,20},{1,9},{5... | collective-permute-start | bytes 1572872 | tf_op jit(solution)/shard_map/ppermute | solution.py:492
  498.7 19.3 %collective-permute-start.71 = (bf16[512,384]{1,0:T(8,128)(2,1)S(1)}, bf16[512,384]{1,0:T(8,128)(2,1)S(1)}, u32[]{:S(2)}, u32[]{:S(2)}) collective-permute-start(bf16[512,384]{1,0:T(8,128)(2,1)S(1)} %get-tuple-element.331), channel_id=1, source_target_pairs={{0,16},{4,20},{8,24},{12,28},{16,0},{20,4},{24,8},{28,12},{1,17},{... | collective-permute-start | bytes 1179656 | tf_op jit(solution)/shard_map/ppermute | solution.py:492
  522.2 25.2 %collective-permute-start.77 = (bf16[1024,512]{1,0:T(8,128)(2,1)S(1)}, bf16[1024,512]{1,0:T(8,128)(2,1)S(1)}, u32[]{:S(2)}, u32[]{:S(2)}) collective-permute-start(bf16[1024,512]{1,0:T(8,128)(2,1)S(1)} %pad_maximum_fusion.11.refs_1_.refs_3_), channel_id=1, source_target_pairs={{0,4},{4,0},{8,12},{12,8},{16,20},{20,16},{24,28},{28,24},{1,5},{5... | collective-permute-start | bytes 3145736 | tf_op jit(solution)/shard_map/ppermute | solution.py:492
  524.1 20.7 %collective-permute-start.75 = (bf16[512,384]{1,0:T(8,128)(2,1)S(1)}, bf16[512,384]{1,0:T(8,128)(2,1)S(1)}, u32[]{:S(2)}, u32[]{:S(2)}) collective-permute-start(bf16[512,384]{1,0:T(8,128)(2,1)S(1)} %get-tuple-element.343), channel_id=1, source_target_pairs={{0,16},{4,20},{8,24},{12,28},{16,0},{20,4},{24,8},{28,12},{1,17},{... | collective-permute-start | bytes 1179656 | tf_op jit(solution)/shard_map/ppermute | solution.py:492
  524.3 23.1 %collective-permute-start.76 = (bf16[512,384]{1,0:T(8,128)(2,1)S(1)}, bf16[512,384]{1,0:T(8,128)(2,1)S(1)}, u32[]{:S(2)}, u32[]{:S(2)}) collective-permute-start(bf16[512,384]{1,0:T(8,128)(2,1)S(1)} %add_convert_fusion.13), channel_id=1, source_target_pairs={{0,8},{4,12},{8,0},{12,4},{16,24},{20,28},{24,16},{28,20},{1,9},{5... | collective-permute-start | bytes 1179656 | tf_op jit(solution)/shard_map/ppermute | solution.py:492
  527.9 19.5 %collective-permute-start.78 = (f32[15872]{0:T(1024)S(1)}, f32[15872]{0:T(1024)S(1)}, u32[]{:S(2)}, u32[]{:S(2)}) collective-permute-start(f32[15872]{0:T(1024)S(1)} %pad_maximum_fusion.18), channel_id=1, source_target_pairs={{0,4},{4,0},{8,12},{12,8},{16,20},{20,16},{24,28},{28,24},{1,5},{5... | collective-permute-start | bytes 190472 | tf_op jit(solution)/shard_map/ppermute | solution.py:492
  528.8 30.6 %collective-permute-start.79 = (bf16[512,384]{1,0:T(8,128)(2,1)S(1)}, bf16[512,384]{1,0:T(8,128)(2,1)S(1)}, u32[]{:S(2)}, u32[]{:S(2)}) collective-permute-start(bf16[512,384]{1,0:T(8,128)(2,1)S(1)} %get-tuple-element.349), channel_id=1, source_target_pairs={{0,16},{4,20},{8,24},{12,28},{16,0},{20,4},{24,8},{28,12},{1,17},{... | collective-permute-start | bytes 1179656 | tf_op jit(solution)/shard_map/ppermute | solution.py:492
  547.5 19.4 %collective-permute-start.81 = (bf16[1024,384]{1,0:T(8,128)(2,1)S(1)}, bf16[1024,384]{1,0:T(8,128)(2,1)S(1)}, u32[]{:S(2)}, u32[]{:S(2)}) collective-permute-start(bf16[1024,384]{1,0:T(8,128)(2,1)S(1)} %pad_maximum_fusion.12.refs_0_.refs_2_), channel_id=1, source_target_pairs={{0,4},{4,0},{8,12},{12,8},{16,20},{20,16},{24,28},{28,24},{1,5},{5... | collective-permute-start | bytes 2359304 | tf_op jit(solution)/shard_map/ppermute | solution.py:492
  548.6 18.3 %collective-permute-start.80 = (bf16[512,384]{1,0:T(8,128)(2,1)S(1)}, bf16[512,384]{1,0:T(8,128)(2,1)S(1)}, u32[]{:S(2)}, u32[]{:S(2)}) collective-permute-start(bf16[512,384]{1,0:T(8,128)(2,1)S(1)} %add_convert_fusion.12), channel_id=1, source_target_pairs={{0,8},{4,12},{8,0},{12,4},{16,24},{20,28},{24,16},{28,20},{1,9},{5... | collective-permute-start | bytes 1179656 | tf_op jit(solution)/shard_map/ppermute | solution.py:492
  548.7 18.2 %collective-permute-start.82 = (f32[15872]{0:T(1024)S(1)}, f32[15872]{0:T(1024)S(1)}, u32[]{:S(2)}, u32[]{:S(2)}) collective-permute-start(f32[15872]{0:T(1024)S(1)} %fusion.48), channel_id=1, source_target_pairs={{0,8},{4,12},{8,0},{12,4},{16,24},{20,28},{24,16},{28,20},{1,9},{5... | collective-permute-start | bytes 190472 | tf_op jit(solution)/shard_map/ppermute | solution.py:492
  567.0 17.5 %collective-permute-start.85 = (bf16[1024,384]{1,0:T(8,128)(2,1)S(1)}, bf16[1024,384]{1,0:T(8,128)(2,1)S(1)}, u32[]{:S(2)}, u32[]{:S(2)}) collective-permute-start(bf16[1024,384]{1,0:T(8,128)(2,1)S(1)} %pad_maximum_fusion.13.refs_1_.refs_3_), channel_id=1, source_target_pairs={{0,4},{4,0},{8,12},{12,8},{16,20},{20,16},{24,28},{28,24},{1,5},{5... | collective-permute-start | bytes 2359304 | tf_op jit(solution)/shard_map/ppermute | solution.py:492
  584.6 17.7 %collective-permute-start.90 = (bf16[1024,384]{1,0:T(8,128)(2,1)S(1)}, bf16[1024,384]{1,0:T(8,128)(2,1)S(1)}, u32[]{:S(2)}, u32[]{:S(2)}) collective-permute-start(bf16[1024,384]{1,0:T(8,128)(2,1)S(1)} %pad_maximum_fusion.14.refs_1_.refs_3_), channel_id=1, source_target_pairs={{0,4},{4,0},{8,12},{12,8},{16,20},{20,16},{24,28},{28,24},{1,5},{5... | collective-permute-start | bytes 2359304 | tf_op jit(solution)/shard_map/ppermute | solution.py:492
  (118 other events, 1231.8 us)
